TPU v7x, 32 devices: a whole 2x2x4 slice. The times are simulated.
32 devices in a mesh: tm: 2 (over x), segment: 4 (over z), band: 4 (over y, core).
Axes of the slice: x: 2, y: 2, z: 4, core: 2. Of those that a mesh axis runs over, the one named last changes fastest.
Arguments:
- features: bfloat16 [4, 4, 16, 16, 384], P(None, 'tm', 'band'), may hold values from -6 to 6
- conv_weight: bfloat16 [4, 27, 384, 384], P('segment'), may hold values from -0.0625 to 0.0625
- conv_bias: float32 [4, 384], P('segment'), may hold values from -3 to 3
- norm_gain: float32 [4, 384], P('segment'), may hold values from 0.5 to 2
Outputs:
- decoded: bfloat16 [4, 4, 16, 16, 384], P('segment', 'tm', 'band')
All inputs are finite; a program needn't handle non-finite values.
Results may differ from a plain program's by a relative error of at most 0.007.
Values may be sent and summed in bfloat16 or wider, within the bound.
No kernel may reach another device: no remote copies, remote signals or barrier semaphores. Data moves between devices by JAX's collectives and lax.ppermute only.
A program may use at most 64 MiB of HBM per device.

v0:
```python
import jax
import jax.numpy as jnp
from jax import lax
from jax.sharding import PartitionSpec as P


def from_behind(value, axis, by):
    length = lax.axis_size(axis)
    pairs = [(i, i + by) for i in range(length) if 0 <= i + by < length]
    return lax.ppermute(value, axis, pairs)


def padded(cells, sides, width):
    for axis, dim in sides:
        count = lax.axis_size(axis)
        ends = count - 1
        head = lax.slice_in_dim(cells, 0, width, axis=dim)
        tail = lax.slice_in_dim(cells, cells.shape[dim] - width, cells.shape[dim], axis=dim)
        cells = jnp.concatenate(
            [
                lax.ppermute(tail, axis, [(i, (i + 1) % count) for i in range(ends)]),
                cells,
                lax.ppermute(head, axis, [((i + 1) % count, i) for i in range(ends)]),
            ],
            axis=dim,
        )
    return cells


def spread(value, axis, source):
    kept = jnp.where(lax.axis_index(axis) == source, value, 0).astype(value.dtype)
    return lax.psum(kept, axis)


def prepare(field, scale_gain):
    wide = field.astype(jnp.float32)
    meansq = jnp.mean(wide * wide, axis=-1, keepdims=True)
    return jax.nn.silu(wide * lax.rsqrt(meansq + 1e-06) * scale_gain).astype(jnp.bfloat16)


def convolve(extended, incoming, kernel, shift_bias, scale_gain):
    frame_count = incoming.shape[0]
    row_count = incoming.shape[1]
    col_count = incoming.shape[2]
    channel_count = incoming.shape[3]
    ready = prepare(extended, scale_gain)
    ready = jnp.pad(ready, ((0, 0), (0, 0), (1, 1), (0, 0)))
    columns = []
    for offset_time in range(3):
        for offset_row in range(3):
            for offset_col in range(3):
                piece = ready[
                    offset_time : offset_time + frame_count,
                    offset_row : offset_row + row_count,
                    offset_col : offset_col + col_count,
                ]
                columns.append(piece.reshape(-1, channel_count))
    stacked = jnp.concatenate(columns, axis=1)
    mixed = jnp.dot(stacked, kernel, preferred_element_type=jnp.float32)
    summed = incoming.astype(jnp.float32) + mixed.reshape(incoming.shape) + shift_bias
    return summed.astype(jnp.bfloat16)


def local(features, conv_weight, conv_bias, norm_gain):
    segment_count = lax.axis_size("segment")
    position = lax.axis_index("segment")
    clip_count = features.shape[0]
    channel_count = features.shape[4]
    kernel = conv_weight[0].reshape(27 * channel_count, channel_count)
    shift_bias = conv_bias[0]
    scale_gain = norm_gain[0]
    entry_cache = from_behind(features, "tm", 1)
    current = jnp.zeros_like(features[0])
    history = jnp.zeros_like(features[0, -2:])
    finished = jnp.zeros_like(features)
    total_steps = clip_count + segment_count - 1
    leading = position == 0
    trailing = position == segment_count - 1
    for step_number in range(total_steps):
        item_index = step_number - position
        active = jnp.logical_and(item_index >= 0, item_index < clip_count)
        safe_index = jnp.clip(item_index, 0, clip_count - 1)
        fresh = lax.dynamic_index_in_dim(features, safe_index, 0, keepdims=False)
        incoming = jnp.where(leading, fresh, current)
        fresh_cache = lax.dynamic_index_in_dim(entry_cache, safe_index, 0, keepdims=False)
        cached = jnp.where(leading, fresh_cache, history)
        joined = jnp.concatenate([cached, incoming], axis=0)
        extended = padded(joined, (("band", 1),), 1)

        def run_unit():
            return convolve(extended, incoming, kernel, shift_bias, scale_gain)

        def pass_through():
            return incoming

        result = lax.cond(active, run_unit, pass_through)
        keep_result = jnp.logical_and(active, trailing)
        finished = jnp.where(
            keep_result, lax.dynamic_update_index_in_dim(finished, result, safe_index, 0), finished
        )
        if step_number + 1 < total_steps:
            current = from_behind(result, "segment", 1)
            history = from_behind(current, "tm", 1)
    collected = spread(finished, "segment", segment_count - 1)
    per_device = clip_count // segment_count
    return lax.dynamic_slice_in_dim(collected, position * per_device, per_device, 0)


def solution(mesh):
    return jax.shard_map(
        local,
        mesh=mesh,
        in_specs=(
            P(None, "tm", "band", None, None),
            P("segment", None, None, None),
            P("segment", None),
            P("segment", None),
        ),
        out_specs=P("segment", "tm", "band", None, None),
        check_vma=False,
    )
```

profile of v0, /device:TPU:18, one launch (start us, length us, event | category | flops | bytes accessed | tf_op | source)
XLA Modules:
  0.0 233.9 jit_solution(18045206745259716363)
XLA Ops:
  8.7 10.7 %collective-permute-done = bf16[4,2,4,16,384]{4,3,2,1,0:T(8,128)(2,1)S(1)} collective-permute-done((bf16[4,2,4,16,384]{4,3,2,1,0:T(8,128)(2,1)}, bf16[4,2,4,16,384]{4,3,2,1,0:T(8,128)(2,1)S(1)}, u32[]{:S(2)}, u32[]{:S(2)}) %collective-permute-start) | collective-permute-done | bytes 393248 | tf_op jit(solution)/shard_map/ppermute | solution.py:10
  20.8 3.0 %collective-permute-start.1 = (bf16[4,1,16,384]{3,2,1,0:T(8,128)(2,1)S(1)}, bf16[4,1,16,384]{3,2,1,0:T(8,128)(2,1)S(1)}, u32[]{:S(2)}, u32[]{:S(2)}) collective-permute-start(bf16[4,1,16,384]{3,2,1,0:T(8,128)(2,1)S(1)} %get-tuple-element.379), channel_id=1, source_target_pairs={{0,1},{1,2},{2,3},{4,5},{5,6},{6,7},{8,9},{9,10},{10,11},{12,13},{... | collective-permute-start | bytes 147464 | tf_op jit(solution)/shard_map/ppermute | solution.py:21
  24.8 3.6 %collective-permute-start.3 = (bf16[2,4,16,384]{3,2,1,0:T(8,128)(2,1)S(1)}, bf16[2,4,16,384]{3,2,1,0:T(8,128)(2,1)S(1)}, u32[]{:S(2)}, u32[]{:S(2)}) collective-permute-start(bf16[2,4,16,384]{3,2,1,0:T(8,128)(2,1)S(1)} %get-tuple-element.388), channel_id=1, source_target_pairs={{0,4},{4,8},{8,12},{1,5},{5,9},{9,13},{2,6},{6,10},{10,14},{3,7},{... | collective-permute-start | bytes 294920 | tf_op jit(solution)/shard_map/ppermute | solution.py:10
  28.4 3.7 %collective-permute-done.3 = bf16[2,4,16,384]{3,2,1,0:T(8,128)(2,1)S(1)} collective-permute-done((bf16[2,4,16,384]{3,2,1,0:T(8,128)(2,1)S(1)}, bf16[2,4,16,384]{3,2,1,0:T(8,128)(2,1)S(1)}, u32[]{:S(2)}, u32[]{:S(2)}) %collective-permute-start.3) | collective-permute-done | bytes 98336 | tf_op jit(solution)/shard_map/ppermute | solution.py:10
  33.5 5.5 %collective-permute-done.4 = bf16[2,4,16,384]{3,2,1,0:T(8,128)(2,1)S(1)} collective-permute-done((bf16[2,4,16,384]{3,2,1,0:T(8,128)(2,1)S(1)}, bf16[2,4,16,384]{3,2,1,0:T(8,128)(2,1)S(1)}, u32[]{:S(2)}, u32[]{:S(2)}) %collective-permute-start.4) | collective-permute-done | bytes 98336 | tf_op jit(solution)/shard_map/ppermute | solution.py:10
  40.3 3.0 %collective-permute-start.5 = (bf16[4,1,16,384]{3,2,1,0:T(8,128)(2,1)S(1)}, bf16[4,1,16,384]{3,2,1,0:T(8,128)(2,1)S(1)}, u32[]{:S(2)}, u32[]{:S(2)}) collective-permute-start(bf16[4,1,16,384]{3,2,1,0:T(8,128)(2,1)S(1)} %get-tuple-element.377), channel_id=1, source_target_pairs={{0,1},{1,2},{2,3},{4,5},{5,6},{6,7},{8,9},{9,10},{10,11},{12,13},{... | collective-permute-start | bytes 147464 | tf_op jit(solution)/shard_map/ppermute | solution.py:21
  44.2 3.5 %collective-permute-start.7 = (bf16[2,4,16,384]{3,2,1,0:T(8,128)(2,1)S(1)}, bf16[2,4,16,384]{3,2,1,0:T(8,128)(2,1)S(1)}, u32[]{:S(2)}, u32[]{:S(2)}) collective-permute-start(bf16[2,4,16,384]{3,2,1,0:T(8,128)(2,1)S(1)} %get-tuple-element.389), channel_id=1, source_target_pairs={{0,4},{4,8},{8,12},{1,5},{5,9},{9,13},{2,6},{6,10},{10,14},{3,7},{... | collective-permute-start | bytes 294920 | tf_op jit(solution)/shard_map/ppermute | solution.py:10
  47.7 11.2 %collective-permute-done.7 = bf16[2,4,16,384]{3,2,1,0:T(8,128)(2,1)S(1)} collective-permute-done((bf16[2,4,16,384]{3,2,1,0:T(8,128)(2,1)S(1)}, bf16[2,4,16,384]{3,2,1,0:T(8,128)(2,1)S(1)}, u32[]{:S(2)}, u32[]{:S(2)}) %collective-permute-start.7) | collective-permute-done | bytes 98336 | tf_op jit(solution)/shard_map/ppermute | solution.py:10
  60.3 5.5 %collective-permute-done.8 = bf16[2,4,16,384]{3,2,1,0:T(8,128)(2,1)S(1)} collective-permute-done((bf16[2,4,16,384]{3,2,1,0:T(8,128)(2,1)S(1)}, bf16[2,4,16,384]{3,2,1,0:T(8,128)(2,1)S(1)}, u32[]{:S(2)}, u32[]{:S(2)}) %collective-permute-start.8) | collective-permute-done | bytes 98336 | tf_op jit(solution)/shard_map/ppermute | solution.py:10
  67.1 3.1 %collective-permute-start.9 = (bf16[4,1,16,384]{3,2,1,0:T(8,128)(2,1)S(1)}, bf16[4,1,16,384]{3,2,1,0:T(8,128)(2,1)S(1)}, u32[]{:S(2)}, u32[]{:S(2)}) collective-permute-start(bf16[4,1,16,384]{3,2,1,0:T(8,128)(2,1)S(1)} %get-tuple-element.375), channel_id=1, source_target_pairs={{0,1},{1,2},{2,3},{4,5},{5,6},{6,7},{8,9},{9,10},{10,11},{12,13},{... | collective-permute-start | bytes 147464 | tf_op jit(solution)/shard_map/ppermute | solution.py:21
  71.1 6.0 %conditional.9 = (bf16[2,4,16,384]{3,2,1,0:T(8,128)(2,1)S(1)}) conditional(s32[]{:T(128)} %convert_element_type.117, bf16[2,4,16,384]{3,2,1,0:T(8,128)(2,1)S(1)} %bitcast_select_fusion.13, (bf16[2,4,16,384]{3,2,1,0:T(8,128)(2,1)S(1)}, bf16[4,6,16,384]{3,2,1,0:T(8,128)(2,1)S(1)}, f32[1,384]{1,0:T(1,128)}, bf16[10368,384]{1,0:T(8,128)(2,1)}, ...), branch_computations={%region_6.7_spmd, %region_7.9_spmd} | conditional | flops 1021034880 | bytes 53400648 | solution.py:96
  73.3 2.2 copy-done.2
  79.1 4.8 %collective-permute-done.11 = bf16[2,4,16,384]{3,2,1,0:T(8,128)(2,1)S(1)} collective-permute-done((bf16[2,4,16,384]{3,2,1,0:T(8,128)(2,1)S(1)}, bf16[2,4,16,384]{3,2,1,0:T(8,128)(2,1)S(1)}, u32[]{:S(2)}, u32[]{:S(2)}) %collective-permute-start.11) | collective-permute-done | bytes 98336 | tf_op jit(solution)/shard_map/ppermute | solution.py:10
  85.3 5.2 %collective-permute-done.12 = bf16[2,4,16,384]{3,2,1,0:T(8,128)(2,1)S(1)} collective-permute-done((bf16[2,4,16,384]{3,2,1,0:T(8,128)(2,1)S(1)}, bf16[2,4,16,384]{3,2,1,0:T(8,128)(2,1)S(1)}, u32[]{:S(2)}, u32[]{:S(2)}) %collective-permute-start.12) | collective-permute-done | bytes 98336 | tf_op jit(solution)/shard_map/ppermute | solution.py:10
  91.8 4.8 %collective-permute-start.13 = (bf16[4,1,16,384]{3,2,1,0:T(8,128)(2,1)S(1)}, bf16[4,1,16,384]{3,2,1,0:T(8,128)(2,1)S(1)}, u32[]{:S(2)}, u32[]{:S(2)}) collective-permute-start(bf16[4,1,16,384]{3,2,1,0:T(8,128)(2,1)S(1)} %get-tuple-element.373), channel_id=1, source_target_pairs={{0,1},{1,2},{2,3},{4,5},{5,6},{6,7},{8,9},{9,10},{10,11},{12,13},{... | collective-permute-start | bytes 147464 | tf_op jit(solution)/shard_map/ppermute | solution.py:21
  97.3 6.0 %conditional.10 = (bf16[2,4,16,384]{3,2,1,0:T(8,128)(2,1)S(1)}) conditional(s32[]{:T(128)} %convert_element_type.118, bf16[2,4,16,384]{3,2,1,0:T(8,128)(2,1)S(1)} %bitcast_select_fusion.10, (bf16[2,4,16,384]{3,2,1,0:T(8,128)(2,1)S(1)}, bf16[4,6,16,384]{3,2,1,0:T(8,128)(2,1)S(1)}, f32[1,384]{1,0:T(1,128)}, bf16[10368,384]{1,0:T(8,128)(2,1)}, ...), branch_computations={%region_9.10_spmd, %region_10.12_spmd} | conditional | flops 1021034880 | bytes 53400648 | solution.py:96
  99.5 2.2 copy-done.3
  105.4 4.5 %collective-permute-done.15 = bf16[2,4,16,384]{3,2,1,0:T(8,128)(2,1)S(1)} collective-permute-done((bf16[2,4,16,384]{3,2,1,0:T(8,128)(2,1)S(1)}, bf16[2,4,16,384]{3,2,1,0:T(8,128)(2,1)S(1)}, u32[]{:S(2)}, u32[]{:S(2)}) %collective-permute-start.15) | collective-permute-done | bytes 98336 | tf_op jit(solution)/shard_map/ppermute | solution.py:10
  111.2 5.2 %collective-permute-done.16 = bf16[2,4,16,384]{3,2,1,0:T(8,128)(2,1)S(1)} collective-permute-done((bf16[2,4,16,384]{3,2,1,0:T(8,128)(2,1)S(1)}, bf16[2,4,16,384]{3,2,1,0:T(8,128)(2,1)S(1)}, u32[]{:S(2)}, u32[]{:S(2)}) %collective-permute-start.16) | collective-permute-done | bytes 98336 | tf_op jit(solution)/shard_map/ppermute | solution.py:10
  117.7 5.2 %collective-permute-start.17 = (bf16[4,1,16,384]{3,2,1,0:T(8,128)(2,1)S(1)}, bf16[4,1,16,384]{3,2,1,0:T(8,128)(2,1)S(1)}, u32[]{:S(2)}, u32[]{:S(2)}) collective-permute-start(bf16[4,1,16,384]{3,2,1,0:T(8,128)(2,1)S(1)} %get-tuple-element.371), channel_id=1, source_target_pairs={{0,1},{1,2},{2,3},{4,5},{5,6},{6,7},{8,9},{9,10},{10,11},{12,13},{... | collective-permute-start | bytes 147464 | tf_op jit(solution)/shard_map/ppermute | solution.py:21
  123.8 6.0 %conditional.11 = (bf16[2,4,16,384]{3,2,1,0:T(8,128)(2,1)S(1)}) conditional(s32[]{:T(128)} %convert_element_type.119, bf16[2,4,16,384]{3,2,1,0:T(8,128)(2,1)S(1)} %bitcast_select_fusion.7, (bf16[2,4,16,384]{3,2,1,0:T(8,128)(2,1)S(1)}, bf16[4,6,16,384]{3,2,1,0:T(8,128)(2,1)S(1)}, f32[1,384]{1,0:T(1,128)}, bf16[10368,384]{1,0:T(8,128)(2,1)}, ...), branch_computations={%region_12.13_spmd, %region_13.15_spmd} | conditional | flops 1021034880 | bytes 53400648 | solution.py:96
  126.0 2.2 copy-done.4
  131.8 4.5 %collective-permute-done.19 = bf16[2,4,16,384]{3,2,1,0:T(8,128)(2,1)S(1)} collective-permute-done((bf16[2,4,16,384]{3,2,1,0:T(8,128)(2,1)S(1)}, bf16[2,4,16,384]{3,2,1,0:T(8,128)(2,1)S(1)}, u32[]{:S(2)}, u32[]{:S(2)}) %collective-permute-start.19) | collective-permute-done | bytes 98336 | tf_op jit(solution)/shard_map/ppermute | solution.py:10
  137.7 5.2 %collective-permute-done.20 = bf16[2,4,16,384]{3,2,1,0:T(8,128)(2,1)S(1)} collective-permute-done((bf16[2,4,16,384]{3,2,1,0:T(8,128)(2,1)S(1)}, bf16[2,4,16,384]{3,2,1,0:T(8,128)(2,1)S(1)}, u32[]{:S(2)}, u32[]{:S(2)}) %collective-permute-start.20) | collective-permute-done | bytes 98336 | tf_op jit(solution)/shard_map/ppermute | solution.py:10
  144.2 5.2 %collective-permute-start.21 = (bf16[4,1,16,384]{3,2,1,0:T(8,128)(2,1)S(1)}, bf16[4,1,16,384]{3,2,1,0:T(8,128)(2,1)S(1)}, u32[]{:S(2)}, u32[]{:S(2)}) collective-permute-start(bf16[4,1,16,384]{3,2,1,0:T(8,128)(2,1)S(1)} %get-tuple-element.369), channel_id=1, source_target_pairs={{0,1},{1,2},{2,3},{4,5},{5,6},{6,7},{8,9},{9,10},{10,11},{12,13},{... | collective-permute-start | bytes 147464 | tf_op jit(solution)/shard_map/ppermute | solution.py:21
  150.3 6.0 %conditional.12 = (bf16[2,4,16,384]{3,2,1,0:T(8,128)(2,1)S(1)}) conditional(s32[]{:T(128)} %convert_element_type.120, bf16[2,4,16,384]{3,2,1,0:T(8,128)(2,1)S(1)} %bitcast_select_fusion.4, (bf16[2,4,16,384]{3,2,1,0:T(8,128)(2,1)S(1)}, bf16[4,6,16,384]{3,2,1,0:T(8,128)(2,1)S(1)}, f32[1,384]{1,0:T(1,128)}, bf16[10368,384]{1,0:T(8,128)(2,1)}, ...), branch_computations={%region_15.16_spmd, %region_16.18_spmd} | conditional | flops 1021034880 | bytes 53400648 | solution.py:96
  152.5 2.2 copy-done.5
  156.4 1.9 collective-permute-start.23
  158.3 4.5 %collective-permute-done.23 = bf16[2,4,16,384]{3,2,1,0:T(8,128)(2,1)S(1)} collective-permute-done((bf16[2,4,16,384]{3,2,1,0:T(8,128)(2,1)S(1)}, bf16[2,4,16,384]{3,2,1,0:T(8,128)(2,1)S(1)}, u32[]{:S(2)}, u32[]{:S(2)}) %collective-permute-start.23) | collective-permute-done | bytes 98336 | tf_op jit(solution)/shard_map/ppermute | solution.py:10
  164.2 5.2 %collective-permute-done.24 = bf16[2,4,16,384]{3,2,1,0:T(8,128)(2,1)S(1)} collective-permute-done((bf16[2,4,16,384]{3,2,1,0:T(8,128)(2,1)S(1)}, bf16[2,4,16,384]{3,2,1,0:T(8,128)(2,1)S(1)}, u32[]{:S(2)}, u32[]{:S(2)}) %collective-permute-start.24) | collective-permute-done | bytes 98336 | tf_op jit(solution)/shard_map/ppermute | solution.py:10
  170.7 4.9 %collective-permute-start.25 = (bf16[4,1,16,384]{3,2,1,0:T(8,128)(2,1)S(1)}, bf16[4,1,16,384]{3,2,1,0:T(8,128)(2,1)S(1)}, u32[]{:S(2)}, u32[]{:S(2)}) collective-permute-start(bf16[4,1,16,384]{3,2,1,0:T(8,128)(2,1)S(1)} %get-tuple-element.367), channel_id=1, source_target_pairs={{0,1},{1,2},{2,3},{4,5},{5,6},{6,7},{8,9},{9,10},{10,11},{12,13},{... | collective-permute-start | bytes 147464 | tf_op jit(solution)/shard_map/ppermute | solution.py:21
  177.6 47.8 %all-reduce.9.cloned.1.call-done = bf16[4,2,4,16,384]{4,3,2,1,0:T(8,128)(2,1)} async-done(((bf16[4,2,4,16,384]{4,3,2,1,0:T(8,128)(2,1)}), bf16[4,2,4,16,384]{4,3,2,1,0:T(8,128)(2,1)}) %all-reduce.9.cloned.1.call-update) | async-done | bytes 393232 | tf_op jit(solution)/shard_map/psum | solution.py:32
  (232 shorter events, 48.3 us)
Async XLA Ops:
  6.5 218.9 %all-reduce.9.cloned.1.call-start = ((), (), s32[]{:S(2)}) async-start(), calls=%async_computation | async-start | bytes 786432 | tf_op jit(solution)/shard_map/psum | solution.py:32
  6.5 12.9 %collective-permute-start = (bf16[4,2,4,16,384]{4,3,2,1,0:T(8,128)(2,1)}, bf16[4,2,4,16,384]{4,3,2,1,0:T(8,128)(2,1)S(1)}, u32[]{:S(2)}, u32[]{:S(2)}) collective-permute-start(bf16[4,2,4,16,384]{4,3,2,1,0:T(8,128)(2,1)} %param.18), channel_id=1, source_target_pairs={{0,16},{1,17},{2,18},{3,19},{4,20},{5,21},{6,22},{7,23},{8,24},{9,... | collective-permute-start | bytes 1179656 | tf_op jit(solution)/shard_map/ppermute | solution.py:10
  19.5 4.3 %collective-permute-start.2 = (bf16[4,1,16,384]{3,2,1,0:T(8,128)(2,1)S(1)}, bf16[4,1,16,384]{3,2,1,0:T(8,128)(2,1)S(1)}, u32[]{:S(2)}, u32[]{:S(2)}) collective-permute-start(bf16[4,1,16,384]{3,2,1,0:T(8,128)(2,1)S(1)} %get-tuple-element.380), channel_id=1, source_target_pairs={{1,0},{2,1},{3,2},{5,4},{6,5},{7,6},{9,8},{10,9},{11,10},{13,12},{... | collective-permute-start | bytes 147464 | tf_op jit(solution)/shard_map/ppermute | solution.py:23
  20.8 3.9 %collective-permute-start.1 = (bf16[4,1,16,384]{3,2,1,0:T(8,128)(2,1)S(1)}, bf16[4,1,16,384]{3,2,1,0:T(8,128)(2,1)S(1)}, u32[]{:S(2)}, u32[]{:S(2)}) collective-permute-start(bf16[4,1,16,384]{3,2,1,0:T(8,128)(2,1)S(1)} %get-tuple-element.379), channel_id=1, source_target_pairs={{0,1},{1,2},{2,3},{4,5},{5,6},{6,7},{8,9},{9,10},{10,11},{12,13},{... | collective-permute-start | bytes 147464 | tf_op jit(solution)/shard_map/ppermute | solution.py:21
  24.8 8.6 %copy-start.7 = (bf16[4,2,4,16,384]{4,3,2,1,0:T(8,128)(2,1)S(1)}, bf16[4,2,4,16,384]{4,3,2,1,0:T(8,128)(2,1)}, u32[]{:S(2)}) copy-start(bf16[4,2,4,16,384]{4,3,2,1,0:T(8,128)(2,1)} %param.18) | copy-start | bytes 1179652
  24.8 7.3 %collective-permute-start.3 = (bf16[2,4,16,384]{3,2,1,0:T(8,128)(2,1)S(1)}, bf16[2,4,16,384]{3,2,1,0:T(8,128)(2,1)S(1)}, u32[]{:S(2)}, u32[]{:S(2)}) collective-permute-start(bf16[2,4,16,384]{3,2,1,0:T(8,128)(2,1)S(1)} %get-tuple-element.388), channel_id=1, source_target_pairs={{0,4},{4,8},{8,12},{1,5},{5,9},{9,13},{2,6},{6,10},{10,14},{3,7},{... | collective-permute-start | bytes 294920 | tf_op jit(solution)/shard_map/ppermute | solution.py:10
  32.1 6.8 %collective-permute-start.4 = (bf16[2,4,16,384]{3,2,1,0:T(8,128)(2,1)S(1)}, bf16[2,4,16,384]{3,2,1,0:T(8,128)(2,1)S(1)}, u32[]{:S(2)}, u32[]{:S(2)}) collective-permute-start(bf16[2,4,16,384]{3,2,1,0:T(8,128)(2,1)S(1)} %collective-permute-done.3), channel_id=1, source_target_pairs={{0,16},{1,17},{2,18},{3,19},{4,20},{5,21},{6,22},{7,23},{8,24},{9,... | collective-permute-start | bytes 294920 | tf_op jit(solution)/shard_map/ppermute | solution.py:10
  39.0 4.3 %collective-permute-start.6 = (bf16[4,1,16,384]{3,2,1,0:T(8,128)(2,1)S(1)}, bf16[4,1,16,384]{3,2,1,0:T(8,128)(2,1)S(1)}, u32[]{:S(2)}, u32[]{:S(2)}) collective-permute-start(bf16[4,1,16,384]{3,2,1,0:T(8,128)(2,1)S(1)} %get-tuple-element.378), channel_id=1, source_target_pairs={{1,0},{2,1},{3,2},{5,4},{6,5},{7,6},{9,8},{10,9},{11,10},{13,12},{... | collective-permute-start | bytes 147464 | tf_op jit(solution)/shard_map/ppermute | solution.py:23
  40.3 3.9 %collective-permute-start.5 = (bf16[4,1,16,384]{3,2,1,0:T(8,128)(2,1)S(1)}, bf16[4,1,16,384]{3,2,1,0:T(8,128)(2,1)S(1)}, u32[]{:S(2)}, u32[]{:S(2)}) collective-permute-start(bf16[4,1,16,384]{3,2,1,0:T(8,128)(2,1)S(1)} %get-tuple-element.377), channel_id=1, source_target_pairs={{0,1},{1,2},{2,3},{4,5},{5,6},{6,7},{8,9},{9,10},{10,11},{12,13},{... | collective-permute-start | bytes 147464 | tf_op jit(solution)/shard_map/ppermute | solution.py:21
  44.2 14.7 %collective-permute-start.7 = (bf16[2,4,16,384]{3,2,1,0:T(8,128)(2,1)S(1)}, bf16[2,4,16,384]{3,2,1,0:T(8,128)(2,1)S(1)}, u32[]{:S(2)}, u32[]{:S(2)}) collective-permute-start(bf16[2,4,16,384]{3,2,1,0:T(8,128)(2,1)S(1)} %get-tuple-element.389), channel_id=1, source_target_pairs={{0,4},{4,8},{8,12},{1,5},{5,9},{9,13},{2,6},{6,10},{10,14},{3,7},{... | collective-permute-start | bytes 294920 | tf_op jit(solution)/shard_map/ppermute | solution.py:10
  59.0 6.8 %collective-permute-start.8 = (bf16[2,4,16,384]{3,2,1,0:T(8,128)(2,1)S(1)}, bf16[2,4,16,384]{3,2,1,0:T(8,128)(2,1)S(1)}, u32[]{:S(2)}, u32[]{:S(2)}) collective-permute-start(bf16[2,4,16,384]{3,2,1,0:T(8,128)(2,1)S(1)} %collective-permute-done.7), channel_id=1, source_target_pairs={{0,16},{1,17},{2,18},{3,19},{4,20},{5,21},{6,22},{7,23},{8,24},{9,... | collective-permute-start | bytes 294920 | tf_op jit(solution)/shard_map/ppermute | solution.py:10
  65.8 4.4 %collective-permute-start.10 = (bf16[4,1,16,384]{3,2,1,0:T(8,128)(2,1)S(1)}, bf16[4,1,16,384]{3,2,1,0:T(8,128)(2,1)S(1)}, u32[]{:S(2)}, u32[]{:S(2)}) collective-permute-start(bf16[4,1,16,384]{3,2,1,0:T(8,128)(2,1)S(1)} %get-tuple-element.376), channel_id=1, source_target_pairs={{1,0},{2,1},{3,2},{5,4},{6,5},{7,6},{9,8},{10,9},{11,10},{13,12},{... | collective-permute-start | bytes 147464 | tf_op jit(solution)/shard_map/ppermute | solution.py:23
  67.1 4.0 %collective-permute-start.9 = (bf16[4,1,16,384]{3,2,1,0:T(8,128)(2,1)S(1)}, bf16[4,1,16,384]{3,2,1,0:T(8,128)(2,1)S(1)}, u32[]{:S(2)}, u32[]{:S(2)}) collective-permute-start(bf16[4,1,16,384]{3,2,1,0:T(8,128)(2,1)S(1)} %get-tuple-element.375), channel_id=1, source_target_pairs={{0,1},{1,2},{2,3},{4,5},{5,6},{6,7},{8,9},{9,10},{10,11},{12,13},{... | collective-permute-start | bytes 147464 | tf_op jit(solution)/shard_map/ppermute | solution.py:21
  72.3 3.3 %copy-start.2 = (bf16[10368,384]{1,0:T(8,128)(2,1)S(1)}, bf16[10368,384]{1,0:T(8,128)(2,1)}, u32[]{:S(2)}) copy-start(bf16[10368,384]{1,0:T(8,128)(2,1)} %get-tuple-element.155) | copy-start | bytes 23887876 | tf_op jit(solution)/shard_map/cond
  77.2 6.8 %collective-permute-start.11 = (bf16[2,4,16,384]{3,2,1,0:T(8,128)(2,1)S(1)}, bf16[2,4,16,384]{3,2,1,0:T(8,128)(2,1)S(1)}, u32[]{:S(2)}, u32[]{:S(2)}) collective-permute-start(bf16[2,4,16,384]{3,2,1,0:T(8,128)(2,1)S(1)} %get-tuple-element.390), channel_id=1, source_target_pairs={{0,4},{4,8},{8,12},{1,5},{5,9},{9,13},{2,6},{6,10},{10,14},{3,7},{... | collective-permute-start | bytes 294920 | tf_op jit(solution)/shard_map/ppermute | solution.py:10
  83.9 6.5 %collective-permute-start.12 = (bf16[2,4,16,384]{3,2,1,0:T(8,128)(2,1)S(1)}, bf16[2,4,16,384]{3,2,1,0:T(8,128)(2,1)S(1)}, u32[]{:S(2)}, u32[]{:S(2)}) collective-permute-start(bf16[2,4,16,384]{3,2,1,0:T(8,128)(2,1)S(1)} %collective-permute-done.11), channel_id=1, source_target_pairs={{0,16},{1,17},{2,18},{3,19},{4,20},{5,21},{6,22},{7,23},{8,24},{9,... | collective-permute-start | bytes 294920 | tf_op jit(solution)/shard_map/ppermute | solution.py:10
  90.5 6.2 %collective-permute-start.14 = (bf16[4,1,16,384]{3,2,1,0:T(8,128)(2,1)S(1)}, bf16[4,1,16,384]{3,2,1,0:T(8,128)(2,1)S(1)}, u32[]{:S(2)}, u32[]{:S(2)}) collective-permute-start(bf16[4,1,16,384]{3,2,1,0:T(8,128)(2,1)S(1)} %get-tuple-element.374), channel_id=1, source_target_pairs={{1,0},{2,1},{3,2},{5,4},{6,5},{7,6},{9,8},{10,9},{11,10},{13,12},{... | collective-permute-start | bytes 147464 | tf_op jit(solution)/shard_map/ppermute | solution.py:23
  91.8 5.5 %collective-permute-start.13 = (bf16[4,1,16,384]{3,2,1,0:T(8,128)(2,1)S(1)}, bf16[4,1,16,384]{3,2,1,0:T(8,128)(2,1)S(1)}, u32[]{:S(2)}, u32[]{:S(2)}) collective-permute-start(bf16[4,1,16,384]{3,2,1,0:T(8,128)(2,1)S(1)} %get-tuple-element.373), channel_id=1, source_target_pairs={{0,1},{1,2},{2,3},{4,5},{5,6},{6,7},{8,9},{9,10},{10,11},{12,13},{... | collective-permute-start | bytes 147464 | tf_op jit(solution)/shard_map/ppermute | solution.py:21
  98.5 3.3 %copy-start.3 = (bf16[10368,384]{1,0:T(8,128)(2,1)S(1)}, bf16[10368,384]{1,0:T(8,128)(2,1)}, u32[]{:S(2)}) copy-start(bf16[10368,384]{1,0:T(8,128)(2,1)} %get-tuple-element.160) | copy-start | bytes 23887876 | tf_op jit(solution)/shard_map/cond
  103.4 6.5 %collective-permute-start.15 = (bf16[2,4,16,384]{3,2,1,0:T(8,128)(2,1)S(1)}, bf16[2,4,16,384]{3,2,1,0:T(8,128)(2,1)S(1)}, u32[]{:S(2)}, u32[]{:S(2)}) collective-permute-start(bf16[2,4,16,384]{3,2,1,0:T(8,128)(2,1)S(1)} %get-tuple-element.391), channel_id=1, source_target_pairs={{0,4},{4,8},{8,12},{1,5},{5,9},{9,13},{2,6},{6,10},{10,14},{3,7},{... | collective-permute-start | bytes 294920 | tf_op jit(solution)/shard_map/ppermute | solution.py:10
  109.9 6.5 %collective-permute-start.16 = (bf16[2,4,16,384]{3,2,1,0:T(8,128)(2,1)S(1)}, bf16[2,4,16,384]{3,2,1,0:T(8,128)(2,1)S(1)}, u32[]{:S(2)}, u32[]{:S(2)}) collective-permute-start(bf16[2,4,16,384]{3,2,1,0:T(8,128)(2,1)S(1)} %collective-permute-done.15), channel_id=1, source_target_pairs={{0,16},{1,17},{2,18},{3,19},{4,20},{5,21},{6,22},{7,23},{8,24},{9,... | collective-permute-start | bytes 294920 | tf_op jit(solution)/shard_map/ppermute | solution.py:10
  116.4 6.5 %collective-permute-start.18 = (bf16[4,1,16,384]{3,2,1,0:T(8,128)(2,1)S(1)}, bf16[4,1,16,384]{3,2,1,0:T(8,128)(2,1)S(1)}, u32[]{:S(2)}, u32[]{:S(2)}) collective-permute-start(bf16[4,1,16,384]{3,2,1,0:T(8,128)(2,1)S(1)} %get-tuple-element.372), channel_id=1, source_target_pairs={{1,0},{2,1},{3,2},{5,4},{6,5},{7,6},{9,8},{10,9},{11,10},{13,12},{... | collective-permute-start | bytes 147464 | tf_op jit(solution)/shard_map/ppermute | solution.py:23
  117.7 6.0 %collective-permute-start.17 = (bf16[4,1,16,384]{3,2,1,0:T(8,128)(2,1)S(1)}, bf16[4,1,16,384]{3,2,1,0:T(8,128)(2,1)S(1)}, u32[]{:S(2)}, u32[]{:S(2)}) collective-permute-start(bf16[4,1,16,384]{3,2,1,0:T(8,128)(2,1)S(1)} %get-tuple-element.371), channel_id=1, source_target_pairs={{0,1},{1,2},{2,3},{4,5},{5,6},{6,7},{8,9},{9,10},{10,11},{12,13},{... | collective-permute-start | bytes 147464 | tf_op jit(solution)/shard_map/ppermute | solution.py:21
  124.9 3.3 %copy-start.4 = (bf16[10368,384]{1,0:T(8,128)(2,1)S(1)}, bf16[10368,384]{1,0:T(8,128)(2,1)}, u32[]{:S(2)}) copy-start(bf16[10368,384]{1,0:T(8,128)(2,1)} %get-tuple-element.165) | copy-start | bytes 23887876 | tf_op jit(solution)/shard_map/cond
  129.9 6.5 %collective-permute-start.19 = (bf16[2,4,16,384]{3,2,1,0:T(8,128)(2,1)S(1)}, bf16[2,4,16,384]{3,2,1,0:T(8,128)(2,1)S(1)}, u32[]{:S(2)}, u32[]{:S(2)}) collective-permute-start(bf16[2,4,16,384]{3,2,1,0:T(8,128)(2,1)S(1)} %get-tuple-element.392), channel_id=1, source_target_pairs={{0,4},{4,8},{8,12},{1,5},{5,9},{9,13},{2,6},{6,10},{10,14},{3,7},{... | collective-permute-start | bytes 294920 | tf_op jit(solution)/shard_map/ppermute | solution.py:10
  136.4 6.5 %collective-permute-start.20 = (bf16[2,4,16,384]{3,2,1,0:T(8,128)(2,1)S(1)}, bf16[2,4,16,384]{3,2,1,0:T(8,128)(2,1)S(1)}, u32[]{:S(2)}, u32[]{:S(2)}) collective-permute-start(bf16[2,4,16,384]{3,2,1,0:T(8,128)(2,1)S(1)} %collective-permute-done.19), channel_id=1, source_target_pairs={{0,16},{1,17},{2,18},{3,19},{4,20},{5,21},{6,22},{7,23},{8,24},{9,... | collective-permute-start | bytes 294920 | tf_op jit(solution)/shard_map/ppermute | solution.py:10
  142.9 6.5 %collective-permute-start.22 = (bf16[4,1,16,384]{3,2,1,0:T(8,128)(2,1)S(1)}, bf16[4,1,16,384]{3,2,1,0:T(8,128)(2,1)S(1)}, u32[]{:S(2)}, u32[]{:S(2)}) collective-permute-start(bf16[4,1,16,384]{3,2,1,0:T(8,128)(2,1)S(1)} %get-tuple-element.370), channel_id=1, source_target_pairs={{1,0},{2,1},{3,2},{5,4},{6,5},{7,6},{9,8},{10,9},{11,10},{13,12},{... | collective-permute-start | bytes 147464 | tf_op jit(solution)/shard_map/ppermute | solution.py:23
  144.2 6.0 %collective-permute-start.21 = (bf16[4,1,16,384]{3,2,1,0:T(8,128)(2,1)S(1)}, bf16[4,1,16,384]{3,2,1,0:T(8,128)(2,1)S(1)}, u32[]{:S(2)}, u32[]{:S(2)}) collective-permute-start(bf16[4,1,16,384]{3,2,1,0:T(8,128)(2,1)S(1)} %get-tuple-element.369), channel_id=1, source_target_pairs={{0,1},{1,2},{2,3},{4,5},{5,6},{6,7},{8,9},{9,10},{10,11},{12,13},{... | collective-permute-start | bytes 147464 | tf_op jit(solution)/shard_map/ppermute | solution.py:21
  156.4 6.5 %collective-permute-start.23 = (bf16[2,4,16,384]{3,2,1,0:T(8,128)(2,1)S(1)}, bf16[2,4,16,384]{3,2,1,0:T(8,128)(2,1)S(1)}, u32[]{:S(2)}, u32[]{:S(2)}) collective-permute-start(bf16[2,4,16,384]{3,2,1,0:T(8,128)(2,1)S(1)} %get-tuple-element.393), channel_id=1, source_target_pairs={{0,4},{4,8},{8,12},{1,5},{5,9},{9,13},{2,6},{6,10},{10,14},{3,7},{... | collective-permute-start | bytes 294920 | tf_op jit(solution)/shard_map/ppermute | solution.py:10
  162.9 6.5 %collective-permute-start.24 = (bf16[2,4,16,384]{3,2,1,0:T(8,128)(2,1)S(1)}, bf16[2,4,16,384]{3,2,1,0:T(8,128)(2,1)S(1)}, u32[]{:S(2)}, u32[]{:S(2)}) collective-permute-start(bf16[2,4,16,384]{3,2,1,0:T(8,128)(2,1)S(1)} %collective-permute-done.23), channel_id=1, source_target_pairs={{0,16},{1,17},{2,18},{3,19},{4,20},{5,21},{6,22},{7,23},{8,24},{9,... | collective-permute-start | bytes 294920 | tf_op jit(solution)/shard_map/ppermute | solution.py:10
  169.4 6.3 %collective-permute-start.26 = (bf16[4,1,16,384]{3,2,1,0:T(8,128)(2,1)S(1)}, bf16[4,1,16,384]{3,2,1,0:T(8,128)(2,1)S(1)}, u32[]{:S(2)}, u32[]{:S(2)}) collective-permute-start(bf16[4,1,16,384]{3,2,1,0:T(8,128)(2,1)S(1)} %get-tuple-element.368), channel_id=1, source_target_pairs={{1,0},{2,1},{3,2},{5,4},{6,5},{7,6},{9,8},{10,9},{11,10},{13,12},{... | collective-permute-start | bytes 147464 | tf_op jit(solution)/shard_map/ppermute | solution.py:23
  170.7 5.8 %collective-permute-start.25 = (bf16[4,1,16,384]{3,2,1,0:T(8,128)(2,1)S(1)}, bf16[4,1,16,384]{3,2,1,0:T(8,128)(2,1)S(1)}, u32[]{:S(2)}, u32[]{:S(2)}) collective-permute-start(bf16[4,1,16,384]{3,2,1,0:T(8,128)(2,1)S(1)} %get-tuple-element.367), channel_id=1, source_target_pairs={{0,1},{1,2},{2,3},{4,5},{5,6},{6,7},{8,9},{9,10},{10,11},{12,13},{... | collective-permute-start | bytes 147464 | tf_op jit(solution)/shard_map/ppermute | solution.py:21
  (5 other events, 9.5 us)
Sparse Core Ops, SparseCore 0:
  177.8 47.6 all-reduce.8
where the time goes:
time: 237 us; the launch traced here: 234 us
  waiting for transfers between devices  129 us (54%)
  starting transfers between devices  62 us (26%)
  between operations  14 us (6%)
  local copies, waits for them, and re-layouts  13.8 us (6%)
  other arithmetic  7.45 us (3%)
  matrix products  6.19 us (3%)
    ppermute x13, waiting for transfers between devices, from_behind(): return lax.ppermute(value, axis, pairs)  75.7 us
    psum x1, waiting for transfers between devices, spread(): return lax.psum(kept, axis)  47.8 us
    ppermute x7, starting transfers between devices, padded(): lax.ppermute(tail, axis, [(i, (i + 1) % count) for i in range(ends)])  29.2 us
    ppermute x13, starting transfers between devices, from_behind(): return lax.ppermute(value, axis, pairs)  23.7 us
    cond x120, local copies, waits for them, and re-layouts  10.8 us
    ppermute x7, starting transfers between devices, padded(): lax.ppermute(head, axis, [((i + 1) % count, i) for i in range(ends)])  9.04 us
    dot_general x4, matrix products, convolve(): mixed = jnp.dot(stacked, kernel, preferred_element_type=jnp.float32)  6.19 us
    ppermute x7, waiting for transfers between devices, padded(): lax.ppermute(tail, axis, [(i, (i + 1) % count) for i in range(ends)])  5.57 us
  transfers between devices with their start and end apart: 28, of which 21 were waited for; matrix products, arithmetic and copies ran while one was open for 1% of the time, Pallas kernels for 0%

commit v1 on v0

v1 whole, which is shorter than its diff:
```python
import functools

import jax
import jax.numpy as jnp
from jax import lax
from jax.experimental import pallas as pl
from jax.experimental.pallas import tpu as pltpu
from jax.sharding import PartitionSpec as P

HALVES = 2
LAG = 2
VMEM = pltpu.VMEM
MESH_AXES = ("tm", "segment", "band")


def whole(space=VMEM):
    return pl.BlockSpec(memory_space=space)


def resident(value):
    return pltpu.with_memory_space_constraint(value, pltpu.VMEM)


def is_active(place, slot, frames):
    number = slot - LAG * place[0]
    return jnp.logical_and(place[2] > 0, jnp.logical_and(number >= 0, number < frames))


def frame_kernel(slot, frames, has_pieces, has_received, finals, half_pos, cols, *refs):
    refs = list(refs)
    place = refs.pop(0)
    pieces = [refs.pop(0) for _ in range(has_pieces)]
    received = refs.pop(0) if has_received else None
    partial, weight, bias, gain = refs[:4]
    refs = refs[4:]
    if finals and half_pos:
        refs = refs[finals:]
    out, spread = refs[:2]
    refs = refs[2:]
    tails = refs[:finals]
    entry = refs[finals]
    size, channels = out.shape

    @pl.when(is_active(place, slot, frames))
    def _():
        if has_pieces:
            step = size // has_pieces

            @pl.when(place[0] == 0)
            def _():
                for number, piece in enumerate(pieces):
                    entry[pl.ds(number * step, step), :] = piece[...]

        if has_received:

            @pl.when(place[0] > 0)
            def _():
                entry[...] = received[...]

        wide = entry[...].astype(jnp.float32)
        meansq = jnp.sum(wide * wide, axis=-1, keepdims=True) * (1.0 / channels)
        normed = wide * lax.rsqrt(meansq + 1e-06) * gain[...]
        ready = normed / (1.0 + jnp.exp(-normed))
        column = lax.broadcasted_iota(jnp.int32, ready.shape, 0) & (cols - 1)
        before = jnp.where(column == 0, 0.0, pltpu.roll(ready, 1, 0))
        after = jnp.where(column == cols - 1, 0.0, pltpu.roll(ready, size - 1, 0))
        edge = jnp.zeros((cols, 3 * channels), jnp.bfloat16)
        spread[pl.ds(0, cols), :] = edge
        spread[pl.ds(size + cols, cols), :] = edge
        for number, value in enumerate((before, ready, after)):
            spread[pl.ds(cols, size), pl.ds(number * channels, channels)] = value.astype(jnp.bfloat16)
        total = partial[...] + wide + bias[...]
        for row in range(3):
            total += jnp.dot(
                spread[pl.ds(row * cols, size), :], weight[2, row], preferred_element_type=jnp.float32
            )
        out[...] = total.astype(jnp.bfloat16)
        if finals:
            length = tails[0].shape[1]
            for number, tail in enumerate(tails):
                start = pl.multiple_of((place[1] + number) * length, length)
                tail[half_pos] = out[pl.ds(start, length), :]


def history_kernel(slot, frames, cols, place, spread, near, far, weight, near_out, far_out):
    size = near.shape[0]

    @pl.when(is_active(place, slot, frames))
    def _():
        total = far[...]
        later = jnp.zeros(far.shape, jnp.float32)
        for row in range(3):
            ready = spread[pl.ds(row * cols, size), :]
            total += jnp.dot(ready, weight[1, row], preferred_element_type=jnp.float32)
            later += jnp.dot(ready, weight[0, row], preferred_element_type=jnp.float32)
        near_out[...] = total
        far_out[...] = later


def local(features, conv_weight, conv_bias, norm_gain):
    times, segments, bands = (lax.axis_size(name) for name in MESH_AXES)
    time, position, band = (lax.axis_index(name) for name in MESH_AXES)
    clips, own_frames, own_rows, cols, channels = features.shape
    frames = own_frames * times
    rows = own_rows * bands
    per_half = bands // HALVES
    half_rows = rows // HALVES
    window = half_rows + segments
    pieces = window // own_rows
    assert clips == segments and window % own_rows == 0 and pieces - per_half == bands - pieces
    assert clips % per_half == 0 and clips // per_half <= times
    size = window * cols
    piece = own_rows * cols

    def stream(clip, half):
        return clip // per_half, half * per_half + clip % per_half

    def flat(t, s, b):
        return (t * segments + s) * bands + b

    half = band // per_half
    holds = time < clips // per_half
    place = jnp.stack([position, half, holds.astype(jnp.int32)]).astype(jnp.int32)
    weight = conv_weight[0].reshape(3, 3, 3 * channels, channels)
    weight = resident(weight)
    bias = resident(conv_bias)
    gain = resident(norm_gain)

    mine = lax.dynamic_index_in_dim(features, position, 0, keepdims=False)
    mine = mine.reshape(own_frames, piece, channels)
    entries = []
    for t in range(times):
        group = []
        for number in range(pieces):
            pairs = []
            for clip in range(clips):
                for h in range(HALVES):
                    source = h * (bands - pieces) + number
                    there, at = stream(clip, h)
                    pairs.append((flat(t, clip, source), flat(there, 0, at)))
            group.append(lax.ppermute(mine, MESH_AXES, pairs))
        entries.append(group)

    near = jnp.zeros((size, channels), jnp.float32)
    far = jnp.zeros((size, channels), jnp.float32)
    slots = frames + LAG * (segments - 1)
    moving = {}
    tails = None
    landed = []
    small = 24 << 20
    frame_bytes = size * channels
    frame_cost = pl.CostEstimate(
        flops=2 * size * channels * 9 * channels, transcendentals=size * channels, bytes_accessed=12 * frame_bytes
    )
    past_cost = pl.CostEstimate(
        flops=2 * size * channels * 18 * channels, transcendentals=0, bytes_accessed=12 * frame_bytes
    )
    for slot in range(slots):
        given = []
        if slot < frames:
            given = [resident(value[slot % own_frames]) for value in entries[slot // own_frames]]
        came = [resident(moving.pop(slot - LAG))] if slot >= LAG else []
        last = slot - LAG * (segments - 1)
        finals = per_half if last >= 0 else 0
        half_pos = last % own_frames if last >= 0 else 0
        operands = [place, *given, *came, resident(near), weight, bias, gain]
        aliases = {}
        if finals and half_pos:
            for index, value in enumerate(tails):
                aliases[len(operands)] = 2 + index
                operands.append(resident(value))
        results = pl.pallas_call(
            functools.partial(frame_kernel, slot, frames, len(given), len(came), finals, half_pos, cols),
            out_shape=[
                pltpu.VMEM((size, channels), jnp.bfloat16),
                pltpu.VMEM((size + 2 * cols, 3 * channels), jnp.bfloat16),
            ]
            + [pltpu.VMEM((own_frames, piece, channels), jnp.bfloat16)] * finals,
            in_specs=[whole(pltpu.SMEM)] + [whole()] * (len(operands) - 1),
            out_specs=[whole()] * (2 + finals),
            scratch_shapes=[pltpu.VMEM((size, channels), jnp.bfloat16)],
            input_output_aliases=aliases,
            compiler_params=pltpu.CompilerParams(vmem_limit_bytes=small),
            cost_estimate=frame_cost,
            name="frame",
        )(*operands)
        out, spread = results[:2]
        tails = results[2:]
        pairs = [
            (s, s + 1) for s in range(segments - 1) if 0 <= slot - LAG * s < frames
        ]
        if pairs:
            moving[slot] = lax.ppermute(out, "segment", pairs)
        if finals and half_pos == own_frames - 1:
            there = last // own_frames
            for index in range(per_half):
                pairs = []
                for clip in range(clips):
                    for h in range(HALVES):
                        t, b = stream(clip, h)
                        pairs.append((flat(t, segments - 1, b), flat(there, clip, h * per_half + index)))
                landed.append((there, index, lax.ppermute(tails[index], MESH_AXES, pairs)))
        if slot + 1 < slots:
            near, far = pl.pallas_call(
                functools.partial(history_kernel, slot, frames, cols),
                out_shape=[pltpu.VMEM((size, channels), jnp.float32)] * 2,
                in_specs=[whole(pltpu.SMEM)] + [whole()] * 4,
                out_specs=[whole()] * 2,
                input_output_aliases={2: 0, 3: 1},
                compiler_params=pltpu.CompilerParams(vmem_limit_bytes=small),
                cost_estimate=past_cost,
                name="history",
            )(place, resident(spread), resident(near), resident(far), weight)

    result = landed[0][2]
    for there, index, value in landed[1:]:
        here = jnp.logical_and(time == there, band % per_half == index)
        result = jnp.where(here, value, result)
    return result.reshape(1, own_frames, own_rows, cols, channels)


def solution(mesh):
    return jax.shard_map(
        local,
        mesh=mesh,
        in_specs=(
            P(None, "tm", "band", None, None),
            P("segment", None, None, None),
            P("segment", None),
            P("segment", None),
        ),
        out_specs=P("segment", "tm", "band", None, None),
        check_vma=False,
    )
```

time: 237 us -> 77 us (0.32); the launches traced: 234 us -> 76.5 us
  waiting for transfers between devices: 129 us -> 14.9 us
  starting transfers between devices: 62 us -> 29.2 us
  Pallas kernels: 0 us -> 23.5 us
  between operations: 14 us -> 0.54 us
  other arithmetic: 7.45 us -> 0.74 us
  matrix products: 6.19 us -> 0 us
  local copies, waits for them, and re-layouts: 13.8 us -> 7.61 us
    ppermute x27 -> x18, waiting for transfers between devices: 81.3 us -> 14.9 us  [the longest x4 12.1 us: local(): landed.append((there, index, lax.ppermute(tails[index], MESH_AXES, pairs)))]
    psum x1 -> x0, waiting for transfers between devices: 47.8 us -> none  [spread(): return lax.psum(kept, axis)]
    ppermute x27 -> x18, starting transfers between devices: 62 us -> 29.2 us  [the longest x6 15.4 us: local(): group.append(lax.ppermute(mine, MESH_AXES, pairs))]
    pallas_call x0 -> x19, Pallas kernels: none -> 23.5 us  [the longest x9 11.8 us: local(): pl.pallas_call(functools.partial(history_kernel, slot, frames, cols), out...]
    cond x120 -> x0, local copies, waits for them, and re-layouts: 10.8 us -> none
    unnamed x2 -> x14, local copies, waits for them, and re-layouts: 0.01 us -> 7.49 us
    dot_general x4 -> x0, matrix products: 6.19 us -> none  [convolve(): mixed = jnp.dot(stacked, kernel, preferred_element_type=jnp.float32)]
    another operation x8 -> x1, other arithmetic: 2.88 us -> 0.08 us  [local(): jnp.stack([position, half, holds.astype(jnp.int32)]).astype(jnp.int32)]
  transfers between devices with their start and end apart: 28 -> 18, of which waited for: 21 -> 2; matrix products, arithmetic and copies ran while one was open for 1% -> 0% of each run, Pallas kernels for 0% -> 31%
where the time goes in v1:
time: 77 us; the launch traced here: 76.5 us
  starting transfers between devices  29.2 us (38%)
  Pallas kernels  23.5 us (31%)
  waiting for transfers between devices  14.9 us (19%)
  local copies, waits for them, and re-layouts  7.61 us (10%)
    ppermute x6, starting transfers between devices, local(): group.append(lax.ppermute(mine, MESH_AXES, pairs))  15.4 us
    ppermute x4, waiting for transfers between devices, local(): landed.append((there, index, lax.ppermute(tails[index], MESH_AXES, pairs)))  12.1 us
    pallas_call x9, Pallas kernels, local(): pl.pallas_call(functools.partial(history_kernel, slot, frames, cols), out...  11.8 us
    pallas_call x10, Pallas kernels, local(): pl.pallas_call(functools.partial(frame_kernel, slot, frames, len(given),...  11.7 us
    ppermute x8, starting transfers between devices, local(): moving[slot] = lax.ppermute(out, 'segment', pairs)  10.5 us
    unnamed x14, local copies, waits for them, and re-layouts  7.49 us
    ppermute x4, starting transfers between devices, local(): landed.append((there, index, lax.ppermute(tails[index], MESH_AXES, pairs)))  3.28 us
    ppermute x8, waiting for transfers between devices, local(): moving[slot] = lax.ppermute(out, 'segment', pairs)  2.88 us
  transfers between devices with their start and end apart: 18, of which 2 were waited for; matrix products, arithmetic and copies ran while one was open for 0% of the time, Pallas kernels for 31%

profile of v1, /device:TPU:18, one launch (start us, length us, event | category | flops | bytes accessed | tf_op | source)
XLA Modules:
  0.0 76.5 jit_solution(4211331268166250376)
XLA Ops:
  0.0 1.0 %copy-done = bf16[4,2,4,16,384]{4,3,2,1,0:T(8,128)(2,1)S(1)} copy-done((bf16[4,2,4,16,384]{4,3,2,1,0:T(8,128)(2,1)S(1)}, bf16[4,2,4,16,384]{4,3,2,1,0:T(8,128)(2,1)}, u32[]{:S(2)}) %copy-start) | copy-done | bytes 393240
  1.0 0.7 collective-permute-start.5
  1.7 0.7 collective-permute-start.4
  2.4 0.7 collective-permute-start.3
  3.0 0.7 collective-permute-start.2
  4.5 12.1 %collective-permute-start = (bf16[2,64,384]{2,1,0:T(8,128)(2,1)S(1)}, bf16[2,64,384]{2,1,0:T(8,128)(2,1)S(1)}, u32[]{:S(2)}, u32[]{:S(2)}) collective-permute-start(bf16[2,64,384]{2,1,0:T(8,128)(2,1)S(1)} %bitcast.54), channel_id=1, source_target_pairs={{16,0},{17,2},{20,1},{21,3},{24,16},{25,18},{28,17},{29,19}} | collective-permute-start | bytes 294920 | tf_op jit(solution)/shard_map/ppermute | solution.py:141
  16.7 3.3 %copy-done.1 = bf16[1,27,384,384]{3,2,1,0:T(8,128)(2,1)S(1)} copy-done((bf16[1,27,384,384]{3,2,1,0:T(8,128)(2,1)S(1)}, bf16[1,27,384,384]{3,2,1,0:T(8,128)(2,1)}, u32[]{:S(2)}) %copy-start.1) | copy-done | bytes 7962648
  20.0 0.7 copy-done.3
  20.6 0.7 copy-done.5
  21.9 0.8 %collective-permute-start.7 = (bf16[192,384]{1,0:T(8,128)(2,1)S(1)}, bf16[192,384]{1,0:T(8,128)(2,1)S(1)}, u32[]{:S(2)}, u32[]{:S(2)}) collective-permute-start(bf16[192,384]{1,0:T(8,128)(2,1)S(1)} %get-tuple-element.50), channel_id=1, source_target_pairs={{0,4},{1,5},{2,6},{3,7},{16,20},{17,21},{18,22},{19,23}} | collective-permute-start | bytes 442376 | tf_op jit(solution)/shard_map/ppermute | solution.py:193
  22.7 1.9 %copy-done.2 = bf16[1,27,384,384]{3,2,1,0:T(8,128)(2,1)S(1)} copy-done((bf16[1,27,384,384]{3,2,1,0:T(8,128)(2,1)S(1)}, bf16[1,27,384,384]{3,2,1,0:T(8,128)(2,1)}, u32[]{:S(2)}) %copy-start.2) | copy-done | bytes 7962648
  25.7 0.7 collective-permute-start.6
  27.6 1.3 %collective-permute-start.9 = (bf16[192,384]{1,0:T(8,128)(2,1)S(1)}, bf16[192,384]{1,0:T(8,128)(2,1)S(1)}, u32[]{:S(2)}, u32[]{:S(2)}) collective-permute-start(bf16[192,384]{1,0:T(8,128)(2,1)S(1)} %get-tuple-element.58), channel_id=1, source_target_pairs={{0,4},{4,8},{1,5},{5,9},{2,6},{6,10},{3,7},{7,11},{16,20},{20,24},... | collective-permute-start | bytes 442376 | tf_op jit(solution)/shard_map/ppermute | solution.py:193
  30.1 1.3 %collective-permute-start.8 = (bf16[192,384]{1,0:T(8,128)(2,1)S(1)}, bf16[192,384]{1,0:T(8,128)(2,1)S(1)}, u32[]{:S(2)}, u32[]{:S(2)}) collective-permute-start(bf16[192,384]{1,0:T(8,128)(2,1)S(1)} %get-tuple-element.57), channel_id=1, source_target_pairs={{0,4},{4,8},{1,5},{5,9},{2,6},{6,10},{3,7},{7,11},{16,20},{20,24},... | collective-permute-start | bytes 442376 | tf_op jit(solution)/shard_map/ppermute | solution.py:193
  31.9 2.9 %collective-permute-done.9.refs_1_ = bf16[192,384]{1,0:T(8,128)(2,1)S(1)} collective-permute-done((bf16[192,384]{1,0:T(8,128)(2,1)S(1)}, bf16[192,384]{1,0:T(8,128)(2,1)S(1)}, u32[]{:S(2)}, u32[]{:S(2)}) %collective-permute-start.9) | collective-permute-done | bytes 147488 | tf_op jit(solution)/shard_map/ppermute | solution.py:193
  34.8 1.8 %frame.14 = (bf16[192,384]{1,0:T(8,128)(2,1)S(1)}, bf16[224,1152]{1,0:T(8,128)(2,1)S(1)}) custom-call(s32[3]{0:T(128)S(1)} %pad_add_fusion.refs_0_.place, bf16[192,384]{1,0:T(8,128)(2,1)S(1)} %collective-permute-done.9.refs_1_, f32[192,384]{1,0:T(8,128)S(1)} %get-tuple-element.61.refs_2_.near, bf16[3,3,1152,384]{3,2,1,0:T(8,128)(2,1)S(1)} %bitcast.38, ...), custom_call_target="tpu_custom_call" | custom-call | flops 509607936 | bytes 884736 | tf_op jit(solution)/shard_map/frame/pallas_call | solution.py:172
  36.6 1.9 %collective-permute-start.11 = (bf16[192,384]{1,0:T(8,128)(2,1)S(1)}, bf16[192,384]{1,0:T(8,128)(2,1)S(1)}, u32[]{:S(2)}, u32[]{:S(2)}) collective-permute-start(bf16[192,384]{1,0:T(8,128)(2,1)S(1)} %get-tuple-element.66), channel_id=1, source_target_pairs={{4,8},{8,12},{5,9},{9,13},{6,10},{10,14},{7,11},{11,15},{20,24},{2... | collective-permute-start | bytes 442376 | tf_op jit(solution)/shard_map/ppermute | solution.py:193
  38.6 2.2 %history.13 = (f32[192,384]{1,0:T(8,128)S(1)}, f32[192,384]{1,0:T(8,128)S(1)}) custom-call(s32[3]{0:T(128)S(1)} %pad_add_fusion.refs_0_.place, bf16[224,1152]{1,0:T(8,128)(2,1)S(1)} %get-tuple-element.62.spread, f32[192,384]{1,0:T(8,128)S(1)} %get-tuple-element.61.refs_2_.near, ...), custom_call_target="tpu_custom_call", output_to_operand_aliasing={{0}: (2, {}), {1}: (3, {})} | custom-call | flops 1019215872 | bytes 884736 | tf_op jit(solution)/shard_map/history/pallas_call | solution.py:204
  40.8 1.7 %frame.15 = (bf16[192,384]{1,0:T(8,128)(2,1)S(1)}, bf16[224,1152]{1,0:T(8,128)(2,1)S(1)}) custom-call(s32[3]{0:T(128)S(1)} %pad_add_fusion.refs_0_.place, bf16[192,384]{1,0:T(8,128)(2,1)S(1)} %collective-permute-done.8.refs_1_, f32[192,384]{1,0:T(8,128)S(1)} %get-tuple-element.64.refs_2_.near, bf16[3,3,1152,384]{3,2,1,0:T(8,128)(2,1)S(1)} %bitcast.40, ...), custom_call_target="tpu_custom_call" | custom-call | flops 509607936 | bytes 884736 | tf_op jit(solution)/shard_map/frame/pallas_call | solution.py:172
  42.5 1.9 %collective-permute-start.10 = (bf16[192,384]{1,0:T(8,128)(2,1)S(1)}, bf16[192,384]{1,0:T(8,128)(2,1)S(1)}, u32[]{:S(2)}, u32[]{:S(2)}) collective-permute-start(bf16[192,384]{1,0:T(8,128)(2,1)S(1)} %get-tuple-element.65), channel_id=1, source_target_pairs={{4,8},{8,12},{5,9},{9,13},{6,10},{10,14},{7,11},{11,15},{20,24},{2... | collective-permute-start | bytes 442376 | tf_op jit(solution)/shard_map/ppermute | solution.py:193
  44.4 2.2 %history.14 = (f32[192,384]{1,0:T(8,128)S(1)}, f32[192,384]{1,0:T(8,128)S(1)}) custom-call(s32[3]{0:T(128)S(1)} %pad_add_fusion.refs_0_.place, bf16[224,1152]{1,0:T(8,128)(2,1)S(1)} %get-tuple-element.67.spread, f32[192,384]{1,0:T(8,128)S(1)} %get-tuple-element.64.refs_2_.near, ...), custom_call_target="tpu_custom_call", output_to_operand_aliasing={{0}: (2, {}), {1}: (3, {})} | custom-call | flops 1019215872 | bytes 884736 | tf_op jit(solution)/shard_map/history/pallas_call | solution.py:204
  46.6 1.7 %frame.16 = (bf16[192,384]{1,0:T(8,128)(2,1)S(1)}, bf16[224,1152]{1,0:T(8,128)(2,1)S(1)}, bf16[2,64,384]{2,1,0:T(8,128)(2,1)S(1)}, bf16[2,64,384]{2,1,0:T(8,128)(2,1)S(1)}) custom-call(s32[3]{0:T(128)S(1)} %pad_add_fusion.refs_0_.place, bf16[192,384]{1,0:T(8,128)(2,1)S(1)} %collective-permute-done.11.refs_1_, f32[192,384]{1,0:T(8,128)S(1)} %get-tuple-element.69.refs_2_.near, ...), custom_call_target="tpu_custom_call" | custom-call | flops 509607936 | bytes 884736 | tf_op jit(solution)/shard_map/frame/pallas_call | solution.py:172
  48.3 1.3 %collective-permute-start.13 = (bf16[192,384]{1,0:T(8,128)(2,1)S(1)}, bf16[192,384]{1,0:T(8,128)(2,1)S(1)}, u32[]{:S(2)}, u32[]{:S(2)}) collective-permute-start(bf16[192,384]{1,0:T(8,128)(2,1)S(1)} %get-tuple-element.76), channel_id=1, source_target_pairs={{8,12},{9,13},{10,14},{11,15},{24,28},{25,29},{26,30},{27,31}} | collective-permute-start | bytes 442376 | tf_op jit(solution)/shard_map/ppermute | solution.py:193
  49.6 2.2 %history.15 = (f32[192,384]{1,0:T(8,128)S(1)}, f32[192,384]{1,0:T(8,128)S(1)}) custom-call(s32[3]{0:T(128)S(1)} %pad_add_fusion.refs_0_.place, bf16[224,1152]{1,0:T(8,128)(2,1)S(1)} %get-tuple-element.70.spread, f32[192,384]{1,0:T(8,128)S(1)} %get-tuple-element.69.refs_2_.near, ...), custom_call_target="tpu_custom_call", output_to_operand_aliasing={{0}: (2, {}), {1}: (3, {})} | custom-call | flops 1019215872 | bytes 884736 | tf_op jit(solution)/shard_map/history/pallas_call | solution.py:204
  51.8 1.7 %frame.17 = (bf16[192,384]{1,0:T(8,128)(2,1)S(1)}, bf16[224,1152]{1,0:T(8,128)(2,1)S(1)}, bf16[2,64,384]{2,1,0:T(8,128)(2,1)S(1)}, bf16[2,64,384]{2,1,0:T(8,128)(2,1)S(1)}) custom-call(s32[3]{0:T(128)S(1)} %pad_add_fusion.refs_0_.place, bf16[192,384]{1,0:T(8,128)(2,1)S(1)} %collective-permute-done.10.refs_1_, ...), custom_call_target="tpu_custom_call", output_to_operand_aliasing={{2}: (6, {}), {3}: (7, {})} | custom-call | flops 509607936 | bytes 884736 | tf_op jit(solution)/shard_map/frame/pallas_call | solution.py:172
  53.5 1.3 %collective-permute-start.12 = (bf16[192,384]{1,0:T(8,128)(2,1)S(1)}, bf16[192,384]{1,0:T(8,128)(2,1)S(1)}, u32[]{:S(2)}, u32[]{:S(2)}) collective-permute-start(bf16[192,384]{1,0:T(8,128)(2,1)S(1)} %get-tuple-element.75), channel_id=1, source_target_pairs={{8,12},{9,13},{10,14},{11,15},{24,28},{25,29},{26,30},{27,31}} | collective-permute-start | bytes 442376 | tf_op jit(solution)/shard_map/ppermute | solution.py:193
  56.2 2.2 %history.16 = (f32[192,384]{1,0:T(8,128)S(1)}, f32[192,384]{1,0:T(8,128)S(1)}) custom-call(s32[3]{0:T(128)S(1)} %pad_add_fusion.refs_0_.place, bf16[224,1152]{1,0:T(8,128)(2,1)S(1)} %get-tuple-element.77.spread, f32[192,384]{1,0:T(8,128)S(1)} %get-tuple-element.72.refs_2_.near, ...), custom_call_target="tpu_custom_call", output_to_operand_aliasing={{0}: (2, {}), {1}: (3, {})} | custom-call | flops 1019215872 | bytes 884736 | tf_op jit(solution)/shard_map/history/pallas_call | solution.py:204
  58.4 1.2 %frame.18 = (bf16[192,384]{1,0:T(8,128)(2,1)}, bf16[224,1152]{1,0:T(8,128)(2,1)S(1)}, bf16[2,64,384]{2,1,0:T(8,128)(2,1)S(1)}, bf16[2,64,384]{2,1,0:T(8,128)(2,1)S(1)}) custom-call(s32[3]{0:T(128)S(1)} %pad_add_fusion.refs_0_.place, bf16[192,384]{1,0:T(8,128)(2,1)S(1)} %collective-permute-done.13.refs_1_, f32[192,384]{1,0:T(8,128)S(1)} %get-tuple-element.79.refs_2_.near, ...), custom_call_target="tpu_custom_call" | custom-call | flops 509607936 | bytes 884736 | tf_op jit(solution)/shard_map/frame/pallas_call | solution.py:172
  59.6 0.8 %history.17 = (f32[192,384]{1,0:T(8,128)S(1)}, f32[192,384]{1,0:T(8,128)S(1)}) custom-call(s32[3]{0:T(128)S(1)} %pad_add_fusion.refs_0_.place, bf16[224,1152]{1,0:T(8,128)(2,1)S(1)} %get-tuple-element.80.spread, f32[192,384]{1,0:T(8,128)S(1)} %get-tuple-element.79.refs_2_.near, ...), custom_call_target="tpu_custom_call", output_to_operand_aliasing={{0}: (2, {}), {1}: (3, {})} | custom-call | flops 1019215872 | bytes 884736 | tf_op jit(solution)/shard_map/history/pallas_call | solution.py:204
  60.4 1.4 %frame.19 = (bf16[192,384]{1,0:T(8,128)(2,1)}, bf16[224,1152]{1,0:T(8,128)(2,1)}, bf16[2,64,384]{2,1,0:T(8,128)(2,1)S(1)}, bf16[2,64,384]{2,1,0:T(8,128)(2,1)S(1)}) custom-call(s32[3]{0:T(128)S(1)} %pad_add_fusion.refs_0_.place, bf16[192,384]{1,0:T(8,128)(2,1)S(1)} %collective-permute-done.12.refs_1_, ...), custom_call_target="tpu_custom_call", output_to_operand_aliasing={{2}: (6, {}), {3}: (7, {})} | custom-call | flops 509607936 | bytes 884736 | tf_op jit(solution)/shard_map/frame/pallas_call | solution.py:172
  62.5 1.3 %collective-permute-start.15 = (bf16[2,64,384]{2,1,0:T(8,128)(2,1)S(1)}, bf16[2,64,384]{2,1,0:T(8,128)(2,1)S(1)}, u32[]{:S(2)}, u32[]{:S(2)}) collective-permute-start(bf16[2,64,384]{2,1,0:T(8,128)(2,1)S(1)} %get-tuple-element.86), channel_id=1, source_target_pairs={{12,16},{14,18},{13,20},{15,22},{28,24},{30,26},{29,28},{31,30}} | collective-permute-start | bytes 294920 | tf_op jit(solution)/shard_map/ppermute | solution.py:202
  63.8 12.0 %collective-permute-done.15 = bf16[2,64,384]{2,1,0:T(8,128)(2,1)S(1)} collective-permute-done((bf16[2,64,384]{2,1,0:T(8,128)(2,1)S(1)}, bf16[2,64,384]{2,1,0:T(8,128)(2,1)S(1)}, u32[]{:S(2)}, u32[]{:S(2)}) %collective-permute-start.15) | collective-permute-done | bytes 98336 | tf_op jit(solution)/shard_map/ppermute | solution.py:202
  (48 shorter events, 8.0 us)
Async XLA Ops:
  0.0 1.0 %copy-start = (bf16[4,2,4,16,384]{4,3,2,1,0:T(8,128)(2,1)S(1)}, bf16[4,2,4,16,384]{4,3,2,1,0:T(8,128)(2,1)}, u32[]{:S(2)}) copy-start(bf16[4,2,4,16,384]{4,3,2,1,0:T(8,128)(2,1)} %param.4) | copy-start | bytes 1179652
  1.0 3.5 %collective-permute-start.5 = (bf16[2,64,384]{2,1,0:T(8,128)(2,1)S(1)}, bf16[2,64,384]{2,1,0:T(8,128)(2,1)S(1)}, u32[]{:S(2)}, u32[]{:S(2)}) collective-permute-start(bf16[2,64,384]{2,1,0:T(8,128)(2,1)S(1)} %bitcast.49), channel_id=1, source_target_pairs={{2,0},{3,2},{6,1},{7,3},{10,16},{11,18},{14,17},{15,19}} | collective-permute-start | bytes 294920 | tf_op jit(solution)/shard_map/ppermute | solution.py:141
  1.7 14.9 %collective-permute-start.4 = (bf16[2,64,384]{2,1,0:T(8,128)(2,1)S(1)}, bf16[2,64,384]{2,1,0:T(8,128)(2,1)S(1)}, u32[]{:S(2)}, u32[]{:S(2)}) collective-permute-start(bf16[2,64,384]{2,1,0:T(8,128)(2,1)S(1)} %bitcast.50), channel_id=1, source_target_pairs={{1,0},{2,2},{5,1},{6,3},{9,16},{10,18},{13,17},{14,19}} | collective-permute-start | bytes 294920 | tf_op jit(solution)/shard_map/ppermute | solution.py:141
  2.4 14.3 %collective-permute-start.3 = (bf16[2,64,384]{2,1,0:T(8,128)(2,1)S(1)}, bf16[2,64,384]{2,1,0:T(8,128)(2,1)S(1)}, u32[]{:S(2)}, u32[]{:S(2)}) collective-permute-start(bf16[2,64,384]{2,1,0:T(8,128)(2,1)S(1)} %bitcast.51), channel_id=1, source_target_pairs={{0,0},{1,2},{4,1},{5,3},{8,16},{9,18},{12,17},{13,19}} | collective-permute-start | bytes 294920 | tf_op jit(solution)/shard_map/ppermute | solution.py:141
  3.0 23.4 %collective-permute-start.2 = (bf16[2,64,384]{2,1,0:T(8,128)(2,1)S(1)}, bf16[2,64,384]{2,1,0:T(8,128)(2,1)S(1)}, u32[]{:S(2)}, u32[]{:S(2)}) collective-permute-start(bf16[2,64,384]{2,1,0:T(8,128)(2,1)S(1)} %bitcast.52), channel_id=1, source_target_pairs={{18,0},{19,2},{22,1},{23,3},{26,16},{27,18},{30,17},{31,19}} | collective-permute-start | bytes 294920 | tf_op jit(solution)/shard_map/ppermute | solution.py:141
  3.7 22.7 %collective-permute-start.1 = (bf16[2,64,384]{2,1,0:T(8,128)(2,1)S(1)}, bf16[2,64,384]{2,1,0:T(8,128)(2,1)S(1)}, u32[]{:S(2)}, u32[]{:S(2)}) collective-permute-start(bf16[2,64,384]{2,1,0:T(8,128)(2,1)S(1)} %bitcast.53), channel_id=1, source_target_pairs={{17,0},{18,2},{21,1},{22,3},{25,16},{26,18},{29,17},{30,19}} | collective-permute-start | bytes 294920 | tf_op jit(solution)/shard_map/ppermute | solution.py:141
  4.5 22.0 %collective-permute-start = (bf16[2,64,384]{2,1,0:T(8,128)(2,1)S(1)}, bf16[2,64,384]{2,1,0:T(8,128)(2,1)S(1)}, u32[]{:S(2)}, u32[]{:S(2)}) collective-permute-start(bf16[2,64,384]{2,1,0:T(8,128)(2,1)S(1)} %bitcast.54), channel_id=1, source_target_pairs={{16,0},{17,2},{20,1},{21,3},{24,16},{25,18},{28,17},{29,19}} | collective-permute-start | bytes 294920 | tf_op jit(solution)/shard_map/ppermute | solution.py:141
  16.7 3.3 %copy-start.1 = (bf16[1,27,384,384]{3,2,1,0:T(8,128)(2,1)S(1)}, bf16[1,27,384,384]{3,2,1,0:T(8,128)(2,1)}, u32[]{:S(2)}) copy-start(bf16[1,27,384,384]{3,2,1,0:T(8,128)(2,1)} %param.5) | copy-start | bytes 23887876
  20.0 0.7 copy-start.3
  20.6 0.7 copy-start.5
  21.3 3.3 %copy-start.2 = (bf16[1,27,384,384]{3,2,1,0:T(8,128)(2,1)S(1)}, bf16[1,27,384,384]{3,2,1,0:T(8,128)(2,1)}, u32[]{:S(2)}) copy-start(bf16[1,27,384,384]{3,2,1,0:T(8,128)(2,1)} %param.5) | copy-start | bytes 23887876
  21.9 5.2 %collective-permute-start.7 = (bf16[192,384]{1,0:T(8,128)(2,1)S(1)}, bf16[192,384]{1,0:T(8,128)(2,1)S(1)}, u32[]{:S(2)}, u32[]{:S(2)}) collective-permute-start(bf16[192,384]{1,0:T(8,128)(2,1)S(1)} %get-tuple-element.50), channel_id=1, source_target_pairs={{0,4},{1,5},{2,6},{3,7},{16,20},{17,21},{18,22},{19,23}} | collective-permute-start | bytes 442376 | tf_op jit(solution)/shard_map/ppermute | solution.py:193
  25.1 1.9 %copy-start.4 = (f32[1,384]{1,0:T(1,128)S(1)}, f32[1,384]{1,0:T(1,128)}, u32[]{:S(2)}) copy-start(f32[1,384]{1,0:T(1,128)} %refs_4_.11) | copy-start | bytes 4612
  25.1 1.9 %copy-start.6 = (f32[1,384]{1,0:T(1,128)S(1)}, f32[1,384]{1,0:T(1,128)}, u32[]{:S(2)}) copy-start(f32[1,384]{1,0:T(1,128)} %refs_5_.11) | copy-start | bytes 4612
  25.7 3.8 %collective-permute-start.6 = (bf16[192,384]{1,0:T(8,128)(2,1)S(1)}, bf16[192,384]{1,0:T(8,128)(2,1)S(1)}, u32[]{:S(2)}, u32[]{:S(2)}) collective-permute-start(bf16[192,384]{1,0:T(8,128)(2,1)S(1)} %get-tuple-element.49), channel_id=1, source_target_pairs={{0,4},{1,5},{2,6},{3,7},{16,20},{17,21},{18,22},{19,23}} | collective-permute-start | bytes 442376 | tf_op jit(solution)/shard_map/ppermute | solution.py:193
  27.6 7.2 %collective-permute-start.9 = (bf16[192,384]{1,0:T(8,128)(2,1)S(1)}, bf16[192,384]{1,0:T(8,128)(2,1)S(1)}, u32[]{:S(2)}, u32[]{:S(2)}) collective-permute-start(bf16[192,384]{1,0:T(8,128)(2,1)S(1)} %get-tuple-element.58), channel_id=1, source_target_pairs={{0,4},{4,8},{1,5},{5,9},{2,6},{6,10},{3,7},{7,11},{16,20},{20,24},... | collective-permute-start | bytes 442376 | tf_op jit(solution)/shard_map/ppermute | solution.py:193
  30.1 10.7 %collective-permute-start.8 = (bf16[192,384]{1,0:T(8,128)(2,1)S(1)}, bf16[192,384]{1,0:T(8,128)(2,1)S(1)}, u32[]{:S(2)}, u32[]{:S(2)}) collective-permute-start(bf16[192,384]{1,0:T(8,128)(2,1)S(1)} %get-tuple-element.57), channel_id=1, source_target_pairs={{0,4},{4,8},{1,5},{5,9},{2,6},{6,10},{3,7},{7,11},{16,20},{20,24},... | collective-permute-start | bytes 442376 | tf_op jit(solution)/shard_map/ppermute | solution.py:193
  36.6 10.0 %collective-permute-start.11 = (bf16[192,384]{1,0:T(8,128)(2,1)S(1)}, bf16[192,384]{1,0:T(8,128)(2,1)S(1)}, u32[]{:S(2)}, u32[]{:S(2)}) collective-permute-start(bf16[192,384]{1,0:T(8,128)(2,1)S(1)} %get-tuple-element.66), channel_id=1, source_target_pairs={{4,8},{8,12},{5,9},{9,13},{6,10},{10,14},{7,11},{11,15},{20,24},{2... | collective-permute-start | bytes 442376 | tf_op jit(solution)/shard_map/ppermute | solution.py:193
  42.5 9.3 %collective-permute-start.10 = (bf16[192,384]{1,0:T(8,128)(2,1)S(1)}, bf16[192,384]{1,0:T(8,128)(2,1)S(1)}, u32[]{:S(2)}, u32[]{:S(2)}) collective-permute-start(bf16[192,384]{1,0:T(8,128)(2,1)S(1)} %get-tuple-element.65), channel_id=1, source_target_pairs={{4,8},{8,12},{5,9},{9,13},{6,10},{10,14},{7,11},{11,15},{20,24},{2... | collective-permute-start | bytes 442376 | tf_op jit(solution)/shard_map/ppermute | solution.py:193
  48.3 10.1 %collective-permute-start.13 = (bf16[192,384]{1,0:T(8,128)(2,1)S(1)}, bf16[192,384]{1,0:T(8,128)(2,1)S(1)}, u32[]{:S(2)}, u32[]{:S(2)}) collective-permute-start(bf16[192,384]{1,0:T(8,128)(2,1)S(1)} %get-tuple-element.76), channel_id=1, source_target_pairs={{8,12},{9,13},{10,14},{11,15},{24,28},{25,29},{26,30},{27,31}} | collective-permute-start | bytes 442376 | tf_op jit(solution)/shard_map/ppermute | solution.py:193
  53.5 6.9 %collective-permute-start.12 = (bf16[192,384]{1,0:T(8,128)(2,1)S(1)}, bf16[192,384]{1,0:T(8,128)(2,1)S(1)}, u32[]{:S(2)}, u32[]{:S(2)}) collective-permute-start(bf16[192,384]{1,0:T(8,128)(2,1)S(1)} %get-tuple-element.75), channel_id=1, source_target_pairs={{8,12},{9,13},{10,14},{11,15},{24,28},{25,29},{26,30},{27,31}} | collective-permute-start | bytes 442376 | tf_op jit(solution)/shard_map/ppermute | solution.py:193
  54.8 9.0 %collective-permute-start.16 = (bf16[2,64,384]{2,1,0:T(8,128)(2,1)S(1)}, bf16[2,64,384]{2,1,0:T(8,128)(2,1)S(1)}, u32[]{:S(2)}, u32[]{:S(2)}) collective-permute-start(bf16[2,64,384]{2,1,0:T(8,128)(2,1)S(1)} %get-tuple-element.87), channel_id=1, source_target_pairs={{12,1},{14,3},{13,5},{15,7},{28,9},{30,11},{29,13},{31,15}} | collective-permute-start | bytes 294920 | tf_op jit(solution)/shard_map/ppermute | solution.py:202
  55.5 8.3 %collective-permute-start.17 = (bf16[2,64,384]{2,1,0:T(8,128)(2,1)S(1)}, bf16[2,64,384]{2,1,0:T(8,128)(2,1)S(1)}, u32[]{:S(2)}, u32[]{:S(2)}) collective-permute-start(bf16[2,64,384]{2,1,0:T(8,128)(2,1)S(1)} %get-tuple-element.88), channel_id=1, source_target_pairs={{12,0},{14,2},{13,4},{15,6},{28,8},{30,10},{29,12},{31,14}} | collective-permute-start | bytes 294920 | tf_op jit(solution)/shard_map/ppermute | solution.py:202
  61.8 2.0 %collective-permute-start.14 = (bf16[2,64,384]{2,1,0:T(8,128)(2,1)S(1)}, bf16[2,64,384]{2,1,0:T(8,128)(2,1)S(1)}, u32[]{:S(2)}, u32[]{:S(2)}) collective-permute-start(bf16[2,64,384]{2,1,0:T(8,128)(2,1)S(1)} %get-tuple-element.85), channel_id=1, source_target_pairs={{12,17},{14,19},{13,21},{15,23},{28,25},{30,27},{29,29},{31,31}} | collective-permute-start | bytes 294920 | tf_op jit(solution)/shard_map/ppermute | solution.py:202
  62.5 13.4 %collective-permute-start.15 = (bf16[2,64,384]{2,1,0:T(8,128)(2,1)S(1)}, bf16[2,64,384]{2,1,0:T(8,128)(2,1)S(1)}, u32[]{:S(2)}, u32[]{:S(2)}) collective-permute-start(bf16[2,64,384]{2,1,0:T(8,128)(2,1)S(1)} %get-tuple-element.86), channel_id=1, source_target_pairs={{12,16},{14,18},{13,20},{15,22},{28,24},{30,26},{29,28},{31,30}} | collective-permute-start | bytes 294920 | tf_op jit(solution)/shard_map/ppermute | solution.py:202

commit v2 on v1

--- a/solution.py
+++ b/solution.py
@@ -21,39 +21,57 @@
     return pltpu.with_memory_space_constraint(value, pltpu.VMEM)
 
 
-def is_active(place, slot, frames):
-    number = slot - LAG * place[0]
-    return jnp.logical_and(place[2] > 0, jnp.logical_and(number >= 0, number < frames))
-
-
-def frame_kernel(slot, frames, has_pieces, has_received, finals, half_pos, cols, *refs):
+def is_active(slot, frames, holders):
+    number = slot - LAG * lax.axis_index("segment")
+    here = jnp.logical_and(number >= 0, number < frames)
+    if holders < lax.axis_size("tm"):
+        here = jnp.logical_and(here, lax.axis_index("tm") < holders)
+    return here
+
+
+def loader_kernel(*refs):
+    count = len(refs) // 2
+    sources, targets, sems = refs[:count], refs[count : 2 * count], refs[-1]
+    copies = [
+        pltpu.make_async_copy(source, target, sems.at[number])
+        for number, (source, target) in enumerate(zip(sources, targets))
+    ]
+    for copy in copies:
+        copy.start()
+    for copy in copies:
+        copy.wait()
+
+
+def frame_kernel(slot, frames, holders, has_pieces, has_received, finals, half_pos, keep, cols, *refs):
     refs = list(refs)
-    place = refs.pop(0)
+    leading = lax.axis_index("segment") == 0
     pieces = [refs.pop(0) for _ in range(has_pieces)]
     received = refs.pop(0) if has_received else None
     partial, weight, bias, gain = refs[:4]
     refs = refs[4:]
     if finals and half_pos:
         refs = refs[finals:]
-    out, spread = refs[:2]
-    refs = refs[2:]
-    tails = refs[:finals]
-    entry = refs[finals]
+    out = refs.pop(0) if keep[0] else None
+    spread = refs.pop(0) if keep[1] else None
+    tails = [refs.pop(0) for _ in range(finals)]
+    entry = refs.pop(0)
+    out = refs.pop(0) if out is None else out
+    spread = refs.pop(0) if spread is None else spread
     size, channels = out.shape
 
-    @pl.when(is_active(place, slot, frames))
+    @pl.when(is_active(slot, frames, holders))
     def _():
         if has_pieces:
             step = size // has_pieces
 
-            @pl.when(place[0] == 0)
+            @pl.when(leading)
             def _():
                 for number, piece in enumerate(pieces):
                     entry[pl.ds(number * step, step), :] = piece[...]
 
         if has_received:
 
-            @pl.when(place[0] > 0)
+            @pl.when(jnp.logical_not(leading))
             def _():
                 entry[...] = received[...]
 
@@ -77,15 +95,16 @@
         out[...] = total.astype(jnp.bfloat16)
         if finals:
             length = tails[0].shape[1]
+            half = lax.axis_index("band") // finals
             for number, tail in enumerate(tails):
-                start = pl.multiple_of((place[1] + number) * length, length)
+                start = pl.multiple_of((half + number) * length, length)
                 tail[half_pos] = out[pl.ds(start, length), :]
 
 
-def history_kernel(slot, frames, cols, place, spread, near, far, weight, near_out, far_out):
+def history_kernel(slot, frames, holders, cols, spread, near, far, weight, near_out, far_out):
     size = near.shape[0]
 
-    @pl.when(is_active(place, slot, frames))
+    @pl.when(is_active(slot, frames - 1, holders))
     def _():
         total = far[...]
         later = jnp.zeros(far.shape, jnp.float32)
@@ -118,13 +137,19 @@
     def flat(t, s, b):
         return (t * segments + s) * bands + b
 
-    half = band // per_half
-    holds = time < clips // per_half
-    place = jnp.stack([position, half, holds.astype(jnp.int32)]).astype(jnp.int32)
-    weight = conv_weight[0].reshape(3, 3, 3 * channels, channels)
-    weight = resident(weight)
-    bias = resident(conv_bias)
-    gain = resident(norm_gain)
+    holders = clips // per_half
+    stored = [conv_weight[0].reshape(3, 3, 3 * channels, channels), conv_bias, norm_gain]
+    weight, bias, gain = pl.pallas_call(
+        loader_kernel,
+        out_shape=[pltpu.VMEM(value.shape, value.dtype) for value in stored],
+        in_specs=[whole(pltpu.HBM)] * 3,
+        out_specs=[whole()] * 3,
+        scratch_shapes=[pltpu.SemaphoreType.DMA((3,))],
+        compiler_params=pltpu.CompilerParams(vmem_limit_bytes=1 << 20),
+        cost_estimate=pl.CostEstimate(flops=0, transcendentals=0, bytes_accessed=2 * stored[0].size),
+        name="loader",
+    )(*[pltpu.with_memory_space_constraint(value, pltpu.HBM) for value in stored])
+    weight, bias, gain = resident(weight), resident(bias), resident(gain)
 
     mine = lax.dynamic_index_in_dim(features, position, 0, keepdims=False)
     mine = mine.reshape(own_frames, piece, channels)
@@ -163,32 +188,36 @@
         last = slot - LAG * (segments - 1)
         finals = per_half if last >= 0 else 0
         half_pos = last % own_frames if last >= 0 else 0
-        operands = [place, *given, *came, resident(near), weight, bias, gain]
+        operands = [*given, *came, resident(near), weight, bias, gain]
         aliases = {}
         if finals and half_pos:
             for index, value in enumerate(tails):
-                aliases[len(operands)] = 2 + index
+                aliases[len(operands)] = index
                 operands.append(resident(value))
+        pairs = [(s, s + 1) for s in range(segments - 1) if 0 <= slot - LAG * s < frames]
+        keep = (bool(pairs), slot + 1 < slots)
+        shapes = [((size, channels), jnp.bfloat16), ((size + 2 * cols, 3 * channels), jnp.bfloat16)]
+        kept = [pltpu.VMEM(*shape) for shape, wanted in zip(shapes, keep) if wanted]
+        spare = [pltpu.VMEM(*shape) for shape, wanted in zip(shapes, keep) if not wanted]
+        if finals and half_pos:
+            aliases = {index: len(kept) + value for index, value in aliases.items()}
         results = pl.pallas_call(
-            functools.partial(frame_kernel, slot, frames, len(given), len(came), finals, half_pos, cols),
-            out_shape=[
-                pltpu.VMEM((size, channels), jnp.bfloat16),
-                pltpu.VMEM((size + 2 * cols, 3 * channels), jnp.bfloat16),
-            ]
-            + [pltpu.VMEM((own_frames, piece, channels), jnp.bfloat16)] * finals,
-            in_specs=[whole(pltpu.SMEM)] + [whole()] * (len(operands) - 1),
-            out_specs=[whole()] * (2 + finals),
-            scratch_shapes=[pltpu.VMEM((size, channels), jnp.bfloat16)],
+            functools.partial(
+                frame_kernel, slot, frames, holders, len(given), len(came), finals, half_pos, keep, cols
+            ),
+            out_shape=kept + [pltpu.VMEM((own_frames, piece, channels), jnp.bfloat16)] * finals,
+            in_specs=[whole()] * len(operands),
+            out_specs=[whole()] * (len(kept) + finals),
+            scratch_shapes=[pltpu.VMEM((size, channels), jnp.bfloat16)] + spare,
             input_output_aliases=aliases,
             compiler_params=pltpu.CompilerParams(vmem_limit_bytes=small),
             cost_estimate=frame_cost,
             name="frame",
         )(*operands)
-        out, spread = results[:2]
-        tails = results[2:]
-        pairs = [
-            (s, s + 1) for s in range(segments - 1) if 0 <= slot - LAG * s < frames
-        ]
+        results = list(results)
+        out = results.pop(0) if keep[0] else None
+        spread = results.pop(0) if keep[1] else None
+        tails = results
         if pairs:
             moving[slot] = lax.ppermute(out, "segment", pairs)
         if finals and half_pos == own_frames - 1:
@@ -202,15 +231,15 @@
                 landed.append((there, index, lax.ppermute(tails[index], MESH_AXES, pairs)))
         if slot + 1 < slots:
             near, far = pl.pallas_call(
-                functools.partial(history_kernel, slot, frames, cols),
+                functools.partial(history_kernel, slot, frames, holders, cols),
                 out_shape=[pltpu.VMEM((size, channels), jnp.float32)] * 2,
-                in_specs=[whole(pltpu.SMEM)] + [whole()] * 4,
+                in_specs=[whole()] * 4,
                 out_specs=[whole()] * 2,
-                input_output_aliases={2: 0, 3: 1},
+                input_output_aliases={1: 0, 2: 1},
                 compiler_params=pltpu.CompilerParams(vmem_limit_bytes=small),
                 cost_estimate=past_cost,
                 name="history",
-            )(place, resident(spread), resident(near), resident(far), weight)
+            )(resident(spread), resident(near), resident(far), weight)
 
     result = landed[0][2]
     for there, index, value in landed[1:]:

time: 77 us -> 63.7 us (0.83)
  Pallas kernels: 23.5 us -> 13.4 us
  waiting for transfers between devices: 14.9 us -> 21.8 us
  local copies, waits for them, and re-layouts: 7.61 us -> 1.12 us
  starting transfers between devices: 29.2 us -> 25.9 us
    pallas_call x19 -> x20, Pallas kernels: 23.5 us -> 13.4 us  [the longest x9 5.32 us: local(): pl.pallas_call(functools.partial(history_kernel, slot, frames, holders, c...]
    unnamed x14 -> x2, local copies, waits for them, and re-layouts: 7.49 us -> 1 us
    ppermute x8, waiting for transfers between devices: 2.88 us -> 8.31 us  [local(): moving[slot] = lax.ppermute(out, 'segment', pairs)]
    ppermute x6, starting transfers between devices: 15.4 us -> 12.2 us  [local(): group.append(lax.ppermute(mine, MESH_AXES, pairs))]
    ppermute x6, waiting for transfers between devices: 0.02 us -> 1.25 us  [local(): group.append(lax.ppermute(mine, MESH_AXES, pairs))]
  transfers between devices with their start and end apart: 18 -> 18, of which waited for: 2 -> 4; matrix products, arithmetic and copies ran while one was open for 0% -> 0% of each run, Pallas kernels for 31% -> 21%
where the time goes in v2:
time: 63.7 us; the launch traced here: 63.3 us
  starting transfers between devices  25.9 us (41%)
  waiting for transfers between devices  21.8 us (34%)
  Pallas kernels  13.4 us (21%)
  local copies, waits for them, and re-layouts  1.12 us (2%)
  other arithmetic  0.66 us (1%)
    ppermute x4, waiting for transfers between devices, local(): landed.append((there, index, lax.ppermute(tails[index], MESH_AXES, pairs)))  12.3 us
    ppermute x6, starting transfers between devices, local(): group.append(lax.ppermute(mine, MESH_AXES, pairs))  12.2 us
    ppermute x8, starting transfers between devices, local(): moving[slot] = lax.ppermute(out, 'segment', pairs)  10.4 us
    ppermute x8, waiting for transfers between devices, local(): moving[slot] = lax.ppermute(out, 'segment', pairs)  8.31 us
    pallas_call x9, Pallas kernels, local(): pl.pallas_call(functools.partial(history_kernel, slot, frames, holders, c...  5.32 us
    pallas_call x10, Pallas kernels, local(): pl.pallas_call(functools.partial(frame_kernel, slot, frames, holders, len...  4.73 us
    pallas_call x1, Pallas kernels, local(): pl.pallas_call(loader_kernel, out_shape=[pltpu.VMEM(value.shape, value.dt...  3.29 us
    ppermute x4, starting transfers between devices, local(): landed.append((there, index, lax.ppermute(tails[index], MESH_AXES, pairs)))  3.28 us
  transfers between devices with their start and end apart: 18, of which 4 were waited for; matrix products, arithmetic and copies ran while one was open for 0% of the time, Pallas kernels for 21%

profile of v2, /device:TPU:18, one launch (start us, length us, event | category | flops | bytes accessed | tf_op | source)
XLA Modules:
  0.0 63.3 jit_solution(16195818246639166024)
XLA Ops:
  0.0 1.0 %copy-done = bf16[4,2,4,16,384]{4,3,2,1,0:T(8,128)(2,1)S(1)} copy-done((bf16[4,2,4,16,384]{4,3,2,1,0:T(8,128)(2,1)S(1)}, bf16[4,2,4,16,384]{4,3,2,1,0:T(8,128)(2,1)}, u32[]{:S(2)}) %copy-start) | copy-done | bytes 393240
  1.0 0.7 %collective-permute-start.5 = (bf16[2,64,384]{2,1,0:T(8,128)(2,1)S(1)}, bf16[2,64,384]{2,1,0:T(8,128)(2,1)S(1)}, u32[]{:S(2)}, u32[]{:S(2)}) collective-permute-start(bf16[2,64,384]{2,1,0:T(8,128)(2,1)S(1)} %bitcast.28), channel_id=1, source_target_pairs={{2,0},{3,2},{6,1},{7,3},{10,16},{11,18},{14,17},{15,19}} | collective-permute-start | bytes 294920 | tf_op jit(solution)/shard_map/ppermute | solution.py:166
  1.7 0.7 %collective-permute-start.4 = (bf16[2,64,384]{2,1,0:T(8,128)(2,1)S(1)}, bf16[2,64,384]{2,1,0:T(8,128)(2,1)S(1)}, u32[]{:S(2)}, u32[]{:S(2)}) collective-permute-start(bf16[2,64,384]{2,1,0:T(8,128)(2,1)S(1)} %bitcast.29), channel_id=1, source_target_pairs={{1,0},{2,2},{5,1},{6,3},{9,16},{10,18},{13,17},{14,19}} | collective-permute-start | bytes 294920 | tf_op jit(solution)/shard_map/ppermute | solution.py:166
  2.4 0.7 %collective-permute-start.3 = (bf16[2,64,384]{2,1,0:T(8,128)(2,1)S(1)}, bf16[2,64,384]{2,1,0:T(8,128)(2,1)S(1)}, u32[]{:S(2)}, u32[]{:S(2)}) collective-permute-start(bf16[2,64,384]{2,1,0:T(8,128)(2,1)S(1)} %bitcast.30), channel_id=1, source_target_pairs={{0,0},{1,2},{4,1},{5,3},{8,16},{9,18},{12,17},{13,19}} | collective-permute-start | bytes 294920 | tf_op jit(solution)/shard_map/ppermute | solution.py:166
  3.0 0.7 %collective-permute-start.2 = (bf16[2,64,384]{2,1,0:T(8,128)(2,1)S(1)}, bf16[2,64,384]{2,1,0:T(8,128)(2,1)S(1)}, u32[]{:S(2)}, u32[]{:S(2)}) collective-permute-start(bf16[2,64,384]{2,1,0:T(8,128)(2,1)S(1)} %bitcast.31), channel_id=1, source_target_pairs={{18,0},{19,2},{22,1},{23,3},{26,16},{27,18},{30,17},{31,19}} | collective-permute-start | bytes 294920 | tf_op jit(solution)/shard_map/ppermute | solution.py:166
  3.7 0.7 %collective-permute-start.1 = (bf16[2,64,384]{2,1,0:T(8,128)(2,1)S(1)}, bf16[2,64,384]{2,1,0:T(8,128)(2,1)S(1)}, u32[]{:S(2)}, u32[]{:S(2)}) collective-permute-start(bf16[2,64,384]{2,1,0:T(8,128)(2,1)S(1)} %bitcast.32), channel_id=1, source_target_pairs={{17,0},{18,2},{21,1},{22,3},{25,16},{26,18},{29,17},{30,19}} | collective-permute-start | bytes 294920 | tf_op jit(solution)/shard_map/ppermute | solution.py:166
  4.4 3.3 %loader.1 = (bf16[3,3,1152,384]{3,2,1,0:T(8,128)(2,1)S(1)}, f32[1,384]{1,0:T(1,128)S(1)}, f32[1,384]{1,0:T(1,128)S(1)}) custom-call(bf16[3,3,1152,384]{3,2,1,0:T(8,128)(2,1)} %bitcast.27, f32[1,384]{1,0:T(1,128)} %refs_1_.1, f32[1,384]{1,0:T(1,128)} %refs_2_.1), custom_call_target="tpu_custom_call" | custom-call | bytes 7962624 | tf_op jit(solution)/shard_map/loader/pallas_call | solution.py:142
  7.7 8.9 %collective-permute-start = (bf16[2,64,384]{2,1,0:T(8,128)(2,1)S(1)}, bf16[2,64,384]{2,1,0:T(8,128)(2,1)S(1)}, u32[]{:S(2)}, u32[]{:S(2)}) collective-permute-start(bf16[2,64,384]{2,1,0:T(8,128)(2,1)S(1)} %bitcast.33), channel_id=1, source_target_pairs={{16,0},{17,2},{20,1},{21,3},{24,16},{25,18},{28,17},{29,19}} | collective-permute-start | bytes 294920 | tf_op jit(solution)/shard_map/ppermute | solution.py:166
  16.7 0.7 %collective-permute-start.7 = (bf16[192,384]{1,0:T(8,128)(2,1)S(1)}, bf16[192,384]{1,0:T(8,128)(2,1)S(1)}, u32[]{:S(2)}, u32[]{:S(2)}) collective-permute-start(bf16[192,384]{1,0:T(8,128)(2,1)S(1)} %get-tuple-element.56), channel_id=1, source_target_pairs={{0,4},{1,5},{2,6},{3,7},{16,20},{17,21},{18,22},{19,23}} | collective-permute-start | bytes 442376 | tf_op jit(solution)/shard_map/ppermute | solution.py:222
  17.5 0.7 %collective-permute-start.6 = (bf16[192,384]{1,0:T(8,128)(2,1)S(1)}, bf16[192,384]{1,0:T(8,128)(2,1)S(1)}, u32[]{:S(2)}, u32[]{:S(2)}) collective-permute-start(bf16[192,384]{1,0:T(8,128)(2,1)S(1)} %get-tuple-element.55), channel_id=1, source_target_pairs={{0,4},{1,5},{2,6},{3,7},{16,20},{17,21},{18,22},{19,23}} | collective-permute-start | bytes 442376 | tf_op jit(solution)/shard_map/ppermute | solution.py:222
  18.2 1.2 %collective-permute-done = bf16[2,64,384]{2,1,0:T(8,128)(2,1)S(1)} collective-permute-done((bf16[2,64,384]{2,1,0:T(8,128)(2,1)S(1)}, bf16[2,64,384]{2,1,0:T(8,128)(2,1)S(1)}, u32[]{:S(2)}, u32[]{:S(2)}) %collective-permute-start) | collective-permute-done | bytes 98336 | tf_op jit(solution)/shard_map/ppermute | solution.py:166
  19.5 1.3 %collective-permute-start.9 = (bf16[192,384]{1,0:T(8,128)(2,1)S(1)}, bf16[192,384]{1,0:T(8,128)(2,1)S(1)}, u32[]{:S(2)}, u32[]{:S(2)}) collective-permute-start(bf16[192,384]{1,0:T(8,128)(2,1)S(1)} %get-tuple-element.64), channel_id=1, source_target_pairs={{0,4},{4,8},{1,5},{5,9},{2,6},{6,10},{3,7},{7,11},{16,20},{20,24},... | collective-permute-start | bytes 442376 | tf_op jit(solution)/shard_map/ppermute | solution.py:222
  20.9 1.3 %collective-permute-start.8 = (bf16[192,384]{1,0:T(8,128)(2,1)S(1)}, bf16[192,384]{1,0:T(8,128)(2,1)S(1)}, u32[]{:S(2)}, u32[]{:S(2)}) collective-permute-start(bf16[192,384]{1,0:T(8,128)(2,1)S(1)} %get-tuple-element.63), channel_id=1, source_target_pairs={{0,4},{4,8},{1,5},{5,9},{2,6},{6,10},{3,7},{7,11},{16,20},{20,24},... | collective-permute-start | bytes 442376 | tf_op jit(solution)/shard_map/ppermute | solution.py:222
  22.2 7.3 %collective-permute-done.9.refs_0_ = bf16[192,384]{1,0:T(8,128)(2,1)S(1)} collective-permute-done((bf16[192,384]{1,0:T(8,128)(2,1)S(1)}, bf16[192,384]{1,0:T(8,128)(2,1)S(1)}, u32[]{:S(2)}, u32[]{:S(2)}) %collective-permute-start.9) | collective-permute-done | bytes 147488 | tf_op jit(solution)/shard_map/ppermute | solution.py:222
  29.5 1.3 %frame.14 = (bf16[192,384]{1,0:T(8,128)(2,1)S(1)}, bf16[224,1152]{1,0:T(8,128)(2,1)S(1)}) custom-call(bf16[192,384]{1,0:T(8,128)(2,1)S(1)} %collective-permute-done.9.refs_0_, f32[192,384]{1,0:T(8,128)S(1)} %get-tuple-element.67.refs_1_.near, bf16[3,3,1152,384]{3,2,1,0:T(8,128)(2,1)S(1)} %get-tuple-element.50.refs_4_.weight.refs_5_.refs_2_, ...), custom_call_target="tpu_custom_call" | custom-call | flops 509607936 | bytes 884736 | tf_op jit(solution)/shard_map/frame/pallas_call | solution.py:204
  30.8 1.9 %collective-permute-start.11 = (bf16[192,384]{1,0:T(8,128)(2,1)S(1)}, bf16[192,384]{1,0:T(8,128)(2,1)S(1)}, u32[]{:S(2)}, u32[]{:S(2)}) collective-permute-start(bf16[192,384]{1,0:T(8,128)(2,1)S(1)} %get-tuple-element.72), channel_id=1, source_target_pairs={{4,8},{8,12},{5,9},{9,13},{6,10},{10,14},{7,11},{11,15},{20,24},{2... | collective-permute-start | bytes 442376 | tf_op jit(solution)/shard_map/ppermute | solution.py:222
  32.7 1.7 %history.13 = (f32[192,384]{1,0:T(8,128)S(1)}, f32[192,384]{1,0:T(8,128)S(1)}) custom-call(bf16[224,1152]{1,0:T(8,128)(2,1)S(1)} %get-tuple-element.68.spread, f32[192,384]{1,0:T(8,128)S(1)} %get-tuple-element.67.refs_1_.near, f32[192,384]{1,0:T(8,128)S(1)} %get-tuple-element.69.far, ...), custom_call_target="tpu_custom_call", output_to_operand_aliasing={{0}: (1, {}), {1}: (2, {})} | custom-call | flops 1019215872 | bytes 884736 | tf_op jit(solution)/shard_map/history/pallas_call | solution.py:233
  34.4 1.1 %frame.15 = (bf16[192,384]{1,0:T(8,128)(2,1)S(1)}, bf16[224,1152]{1,0:T(8,128)(2,1)S(1)}) custom-call(bf16[192,384]{1,0:T(8,128)(2,1)S(1)} %collective-permute-done.8.refs_0_, f32[192,384]{1,0:T(8,128)S(1)} %get-tuple-element.70.refs_1_.near, bf16[3,3,1152,384]{3,2,1,0:T(8,128)(2,1)S(1)} %get-tuple-element.50.refs_4_.weight.refs_5_.refs_2_, ...), custom_call_target="tpu_custom_call" | custom-call | flops 509607936 | bytes 884736 | tf_op jit(solution)/shard_map/frame/pallas_call | solution.py:204
  35.5 1.9 %collective-permute-start.10 = (bf16[192,384]{1,0:T(8,128)(2,1)S(1)}, bf16[192,384]{1,0:T(8,128)(2,1)S(1)}, u32[]{:S(2)}, u32[]{:S(2)}) collective-permute-start(bf16[192,384]{1,0:T(8,128)(2,1)S(1)} %get-tuple-element.71), channel_id=1, source_target_pairs={{4,8},{8,12},{5,9},{9,13},{6,10},{10,14},{7,11},{11,15},{20,24},{2... | collective-permute-start | bytes 442376 | tf_op jit(solution)/shard_map/ppermute | solution.py:222
  37.5 1.7 %history.14 = (f32[192,384]{1,0:T(8,128)S(1)}, f32[192,384]{1,0:T(8,128)S(1)}) custom-call(bf16[224,1152]{1,0:T(8,128)(2,1)S(1)} %get-tuple-element.73.spread, f32[192,384]{1,0:T(8,128)S(1)} %get-tuple-element.70.refs_1_.near, f32[192,384]{1,0:T(8,128)S(1)} %get-tuple-element.74.far, ...), custom_call_target="tpu_custom_call", output_to_operand_aliasing={{0}: (1, {}), {1}: (2, {})} | custom-call | flops 1019215872 | bytes 884736 | tf_op jit(solution)/shard_map/history/pallas_call | solution.py:233
  39.1 1.1 %frame.16 = (bf16[192,384]{1,0:T(8,128)(2,1)S(1)}, bf16[224,1152]{1,0:T(8,128)(2,1)S(1)}, bf16[2,64,384]{2,1,0:T(8,128)(2,1)S(1)}, bf16[2,64,384]{2,1,0:T(8,128)(2,1)S(1)}) custom-call(bf16[192,384]{1,0:T(8,128)(2,1)S(1)} %collective-permute-done.11.refs_0_, f32[192,384]{1,0:T(8,128)S(1)} %get-tuple-element.75.refs_1_.near, ...), custom_call_target="tpu_custom_call" | custom-call | flops 509607936 | bytes 884736 | tf_op jit(solution)/shard_map/frame/pallas_call | solution.py:204
  40.3 1.3 %collective-permute-start.13 = (bf16[192,384]{1,0:T(8,128)(2,1)S(1)}, bf16[192,384]{1,0:T(8,128)(2,1)S(1)}, u32[]{:S(2)}, u32[]{:S(2)}) collective-permute-start(bf16[192,384]{1,0:T(8,128)(2,1)S(1)} %get-tuple-element.82), channel_id=1, source_target_pairs={{8,12},{9,13},{10,14},{11,15},{24,28},{25,29},{26,30},{27,31}} | collective-permute-start | bytes 442376 | tf_op jit(solution)/shard_map/ppermute | solution.py:222
  41.6 1.7 %history.15 = (f32[192,384]{1,0:T(8,128)S(1)}, f32[192,384]{1,0:T(8,128)S(1)}) custom-call(bf16[224,1152]{1,0:T(8,128)(2,1)S(1)} %get-tuple-element.76.spread, f32[192,384]{1,0:T(8,128)S(1)} %get-tuple-element.75.refs_1_.near, f32[192,384]{1,0:T(8,128)S(1)} %get-tuple-element.77.far, ...), custom_call_target="tpu_custom_call", output_to_operand_aliasing={{0}: (1, {}), {1}: (2, {})} | custom-call | flops 1019215872 | bytes 884736 | tf_op jit(solution)/shard_map/history/pallas_call | solution.py:233
  43.3 1.1 %frame.17 = (bf16[192,384]{1,0:T(8,128)(2,1)S(1)}, bf16[224,1152]{1,0:T(8,128)(2,1)S(1)}, bf16[2,64,384]{2,1,0:T(8,128)(2,1)S(1)}, bf16[2,64,384]{2,1,0:T(8,128)(2,1)S(1)}) custom-call(bf16[192,384]{1,0:T(8,128)(2,1)S(1)} %collective-permute-done.10.refs_0_, ...), custom_call_target="tpu_custom_call", output_to_operand_aliasing={{2}: (5, {}), {3}: (6, {})} | custom-call | flops 509607936 | bytes 884736 | tf_op jit(solution)/shard_map/frame/pallas_call | solution.py:204
  44.4 1.3 %collective-permute-start.12 = (bf16[192,384]{1,0:T(8,128)(2,1)S(1)}, bf16[192,384]{1,0:T(8,128)(2,1)S(1)}, u32[]{:S(2)}, u32[]{:S(2)}) collective-permute-start(bf16[192,384]{1,0:T(8,128)(2,1)S(1)} %get-tuple-element.81), channel_id=1, source_target_pairs={{8,12},{9,13},{10,14},{11,15},{24,28},{25,29},{26,30},{27,31}} | collective-permute-start | bytes 442376 | tf_op jit(solution)/shard_map/ppermute | solution.py:222
  45.7 0.7 %collective-permute-start.16 = (bf16[2,64,384]{2,1,0:T(8,128)(2,1)S(1)}, bf16[2,64,384]{2,1,0:T(8,128)(2,1)S(1)}, u32[]{:S(2)}, u32[]{:S(2)}) collective-permute-start(bf16[2,64,384]{2,1,0:T(8,128)(2,1)S(1)} %get-tuple-element.93), channel_id=1, source_target_pairs={{12,1},{14,3},{13,5},{15,7},{28,9},{30,11},{29,13},{31,15}} | collective-permute-start | bytes 294920 | tf_op jit(solution)/shard_map/ppermute | solution.py:231
  46.4 0.7 %collective-permute-start.17 = (bf16[2,64,384]{2,1,0:T(8,128)(2,1)S(1)}, bf16[2,64,384]{2,1,0:T(8,128)(2,1)S(1)}, u32[]{:S(2)}, u32[]{:S(2)}) collective-permute-start(bf16[2,64,384]{2,1,0:T(8,128)(2,1)S(1)} %get-tuple-element.94), channel_id=1, source_target_pairs={{12,0},{14,2},{13,4},{15,6},{28,8},{30,10},{29,12},{31,14}} | collective-permute-start | bytes 294920 | tf_op jit(solution)/shard_map/ppermute | solution.py:231
  47.4 1.0 %collective-permute-done.12.refs_0_ = bf16[192,384]{1,0:T(8,128)(2,1)S(1)} collective-permute-done((bf16[192,384]{1,0:T(8,128)(2,1)S(1)}, bf16[192,384]{1,0:T(8,128)(2,1)S(1)}, u32[]{:S(2)}, u32[]{:S(2)}) %collective-permute-start.12) | collective-permute-done | bytes 147488 | tf_op jit(solution)/shard_map/ppermute | solution.py:222
  48.4 0.7 %collective-permute-start.14 = (bf16[2,64,384]{2,1,0:T(8,128)(2,1)S(1)}, bf16[2,64,384]{2,1,0:T(8,128)(2,1)S(1)}, u32[]{:S(2)}, u32[]{:S(2)}) collective-permute-start(bf16[2,64,384]{2,1,0:T(8,128)(2,1)S(1)} %get-tuple-element.91), channel_id=1, source_target_pairs={{12,17},{14,19},{13,21},{15,23},{28,25},{30,27},{29,29},{31,31}} | collective-permute-start | bytes 294920 | tf_op jit(solution)/shard_map/ppermute | solution.py:231
  49.0 1.3 %collective-permute-start.15 = (bf16[2,64,384]{2,1,0:T(8,128)(2,1)S(1)}, bf16[2,64,384]{2,1,0:T(8,128)(2,1)S(1)}, u32[]{:S(2)}, u32[]{:S(2)}) collective-permute-start(bf16[2,64,384]{2,1,0:T(8,128)(2,1)S(1)} %get-tuple-element.92), channel_id=1, source_target_pairs={{12,16},{14,18},{13,20},{15,22},{28,24},{30,26},{29,28},{31,30}} | collective-permute-start | bytes 294920 | tf_op jit(solution)/shard_map/ppermute | solution.py:231
  50.4 12.3 %collective-permute-done.15 = bf16[2,64,384]{2,1,0:T(8,128)(2,1)S(1)} collective-permute-done((bf16[2,64,384]{2,1,0:T(8,128)(2,1)S(1)}, bf16[2,64,384]{2,1,0:T(8,128)(2,1)S(1)}, u32[]{:S(2)}, u32[]{:S(2)}) %collective-permute-start.15) | collective-permute-done | bytes 98336 | tf_op jit(solution)/shard_map/ppermute | solution.py:231
  62.6 0.7 %select_select_fusion = bf16[2,64,384]{2,1,0:T(8,128)(2,1)} fusion(bf16[2,64,384]{2,1,0:T(8,128)(2,1)S(1)} %collective-permute-done.14, bf16[2,64,384]{2,1,0:T(8,128)(2,1)S(1)} %collective-permute-done.15, bf16[2,64,384]{2,1,0:T(8,128)(2,1)S(1)} %collective-permute-done.16, bf16[2,64,384]{2,1,0:T(8,128)(2,1)S(1)} %collective-permute-done.17, pred[]{:T(512)S(6)} %and.22, ...), kind=kLoop, calls=%fused_computation | loop fusion | flops 147456 | bytes 491523 | tf_op jit(solution)/shard_map/jit(_where)/select_n | solution.py:247
  (36 shorter events, 0.6 us)
Async XLA Ops:
  0.0 1.0 %copy-start = (bf16[4,2,4,16,384]{4,3,2,1,0:T(8,128)(2,1)S(1)}, bf16[4,2,4,16,384]{4,3,2,1,0:T(8,128)(2,1)}, u32[]{:S(2)}) copy-start(bf16[4,2,4,16,384]{4,3,2,1,0:T(8,128)(2,1)} %param.4) | copy-start | bytes 1179652
  1.0 6.7 %collective-permute-start.5 = (bf16[2,64,384]{2,1,0:T(8,128)(2,1)S(1)}, bf16[2,64,384]{2,1,0:T(8,128)(2,1)S(1)}, u32[]{:S(2)}, u32[]{:S(2)}) collective-permute-start(bf16[2,64,384]{2,1,0:T(8,128)(2,1)S(1)} %bitcast.28), channel_id=1, source_target_pairs={{2,0},{3,2},{6,1},{7,3},{10,16},{11,18},{14,17},{15,19}} | collective-permute-start | bytes 294920 | tf_op jit(solution)/shard_map/ppermute | solution.py:166
  1.7 14.9 %collective-permute-start.4 = (bf16[2,64,384]{2,1,0:T(8,128)(2,1)S(1)}, bf16[2,64,384]{2,1,0:T(8,128)(2,1)S(1)}, u32[]{:S(2)}, u32[]{:S(2)}) collective-permute-start(bf16[2,64,384]{2,1,0:T(8,128)(2,1)S(1)} %bitcast.29), channel_id=1, source_target_pairs={{1,0},{2,2},{5,1},{6,3},{9,16},{10,18},{13,17},{14,19}} | collective-permute-start | bytes 294920 | tf_op jit(solution)/shard_map/ppermute | solution.py:166
  2.4 14.3 %collective-permute-start.3 = (bf16[2,64,384]{2,1,0:T(8,128)(2,1)S(1)}, bf16[2,64,384]{2,1,0:T(8,128)(2,1)S(1)}, u32[]{:S(2)}, u32[]{:S(2)}) collective-permute-start(bf16[2,64,384]{2,1,0:T(8,128)(2,1)S(1)} %bitcast.30), channel_id=1, source_target_pairs={{0,0},{1,2},{4,1},{5,3},{8,16},{9,18},{12,17},{13,19}} | collective-permute-start | bytes 294920 | tf_op jit(solution)/shard_map/ppermute | solution.py:166
  3.0 15.1 %collective-permute-start.2 = (bf16[2,64,384]{2,1,0:T(8,128)(2,1)S(1)}, bf16[2,64,384]{2,1,0:T(8,128)(2,1)S(1)}, u32[]{:S(2)}, u32[]{:S(2)}) collective-permute-start(bf16[2,64,384]{2,1,0:T(8,128)(2,1)S(1)} %bitcast.31), channel_id=1, source_target_pairs={{18,0},{19,2},{22,1},{23,3},{26,16},{27,18},{30,17},{31,19}} | collective-permute-start | bytes 294920 | tf_op jit(solution)/shard_map/ppermute | solution.py:166
  3.7 14.5 %collective-permute-start.1 = (bf16[2,64,384]{2,1,0:T(8,128)(2,1)S(1)}, bf16[2,64,384]{2,1,0:T(8,128)(2,1)S(1)}, u32[]{:S(2)}, u32[]{:S(2)}) collective-permute-start(bf16[2,64,384]{2,1,0:T(8,128)(2,1)S(1)} %bitcast.32), channel_id=1, source_target_pairs={{17,0},{18,2},{21,1},{22,3},{25,16},{26,18},{29,17},{30,19}} | collective-permute-start | bytes 294920 | tf_op jit(solution)/shard_map/ppermute | solution.py:166
  7.7 11.8 %collective-permute-start = (bf16[2,64,384]{2,1,0:T(8,128)(2,1)S(1)}, bf16[2,64,384]{2,1,0:T(8,128)(2,1)S(1)}, u32[]{:S(2)}, u32[]{:S(2)}) collective-permute-start(bf16[2,64,384]{2,1,0:T(8,128)(2,1)S(1)} %bitcast.33), channel_id=1, source_target_pairs={{16,0},{17,2},{20,1},{21,3},{24,16},{25,18},{28,17},{29,19}} | collective-permute-start | bytes 294920 | tf_op jit(solution)/shard_map/ppermute | solution.py:166
  16.7 2.8 %collective-permute-start.7 = (bf16[192,384]{1,0:T(8,128)(2,1)S(1)}, bf16[192,384]{1,0:T(8,128)(2,1)S(1)}, u32[]{:S(2)}, u32[]{:S(2)}) collective-permute-start(bf16[192,384]{1,0:T(8,128)(2,1)S(1)} %get-tuple-element.56), channel_id=1, source_target_pairs={{0,4},{1,5},{2,6},{3,7},{16,20},{17,21},{18,22},{19,23}} | collective-permute-start | bytes 442376 | tf_op jit(solution)/shard_map/ppermute | solution.py:222
  17.5 3.4 %collective-permute-start.6 = (bf16[192,384]{1,0:T(8,128)(2,1)S(1)}, bf16[192,384]{1,0:T(8,128)(2,1)S(1)}, u32[]{:S(2)}, u32[]{:S(2)}) collective-permute-start(bf16[192,384]{1,0:T(8,128)(2,1)S(1)} %get-tuple-element.55), channel_id=1, source_target_pairs={{0,4},{1,5},{2,6},{3,7},{16,20},{17,21},{18,22},{19,23}} | collective-permute-start | bytes 442376 | tf_op jit(solution)/shard_map/ppermute | solution.py:222
  19.5 10.0 %collective-permute-start.9 = (bf16[192,384]{1,0:T(8,128)(2,1)S(1)}, bf16[192,384]{1,0:T(8,128)(2,1)S(1)}, u32[]{:S(2)}, u32[]{:S(2)}) collective-permute-start(bf16[192,384]{1,0:T(8,128)(2,1)S(1)} %get-tuple-element.64), channel_id=1, source_target_pairs={{0,4},{4,8},{1,5},{5,9},{2,6},{6,10},{3,7},{7,11},{16,20},{20,24},... | collective-permute-start | bytes 442376 | tf_op jit(solution)/shard_map/ppermute | solution.py:222
  20.9 13.5 %collective-permute-start.8 = (bf16[192,384]{1,0:T(8,128)(2,1)S(1)}, bf16[192,384]{1,0:T(8,128)(2,1)S(1)}, u32[]{:S(2)}, u32[]{:S(2)}) collective-permute-start(bf16[192,384]{1,0:T(8,128)(2,1)S(1)} %get-tuple-element.63), channel_id=1, source_target_pairs={{0,4},{4,8},{1,5},{5,9},{2,6},{6,10},{3,7},{7,11},{16,20},{20,24},... | collective-permute-start | bytes 442376 | tf_op jit(solution)/shard_map/ppermute | solution.py:222
  30.8 8.3 %collective-permute-start.11 = (bf16[192,384]{1,0:T(8,128)(2,1)S(1)}, bf16[192,384]{1,0:T(8,128)(2,1)S(1)}, u32[]{:S(2)}, u32[]{:S(2)}) collective-permute-start(bf16[192,384]{1,0:T(8,128)(2,1)S(1)} %get-tuple-element.72), channel_id=1, source_target_pairs={{4,8},{8,12},{5,9},{9,13},{6,10},{10,14},{7,11},{11,15},{20,24},{2... | collective-permute-start | bytes 442376 | tf_op jit(solution)/shard_map/ppermute | solution.py:222
  35.5 7.7 %collective-permute-start.10 = (bf16[192,384]{1,0:T(8,128)(2,1)S(1)}, bf16[192,384]{1,0:T(8,128)(2,1)S(1)}, u32[]{:S(2)}, u32[]{:S(2)}) collective-permute-start(bf16[192,384]{1,0:T(8,128)(2,1)S(1)} %get-tuple-element.71), channel_id=1, source_target_pairs={{4,8},{8,12},{5,9},{9,13},{6,10},{10,14},{7,11},{11,15},{20,24},{2... | collective-permute-start | bytes 442376 | tf_op jit(solution)/shard_map/ppermute | solution.py:222
  40.3 6.8 %collective-permute-start.13 = (bf16[192,384]{1,0:T(8,128)(2,1)S(1)}, bf16[192,384]{1,0:T(8,128)(2,1)S(1)}, u32[]{:S(2)}, u32[]{:S(2)}) collective-permute-start(bf16[192,384]{1,0:T(8,128)(2,1)S(1)} %get-tuple-element.82), channel_id=1, source_target_pairs={{8,12},{9,13},{10,14},{11,15},{24,28},{25,29},{26,30},{27,31}} | collective-permute-start | bytes 442376 | tf_op jit(solution)/shard_map/ppermute | solution.py:222
  44.4 4.0 %collective-permute-start.12 = (bf16[192,384]{1,0:T(8,128)(2,1)S(1)}, bf16[192,384]{1,0:T(8,128)(2,1)S(1)}, u32[]{:S(2)}, u32[]{:S(2)}) collective-permute-start(bf16[192,384]{1,0:T(8,128)(2,1)S(1)} %get-tuple-element.81), channel_id=1, source_target_pairs={{8,12},{9,13},{10,14},{11,15},{24,28},{25,29},{26,30},{27,31}} | collective-permute-start | bytes 442376 | tf_op jit(solution)/shard_map/ppermute | solution.py:222
  45.7 4.6 %collective-permute-start.16 = (bf16[2,64,384]{2,1,0:T(8,128)(2,1)S(1)}, bf16[2,64,384]{2,1,0:T(8,128)(2,1)S(1)}, u32[]{:S(2)}, u32[]{:S(2)}) collective-permute-start(bf16[2,64,384]{2,1,0:T(8,128)(2,1)S(1)} %get-tuple-element.93), channel_id=1, source_target_pairs={{12,1},{14,3},{13,5},{15,7},{28,9},{30,11},{29,13},{31,15}} | collective-permute-start | bytes 294920 | tf_op jit(solution)/shard_map/ppermute | solution.py:231
  46.4 4.0 %collective-permute-start.17 = (bf16[2,64,384]{2,1,0:T(8,128)(2,1)S(1)}, bf16[2,64,384]{2,1,0:T(8,128)(2,1)S(1)}, u32[]{:S(2)}, u32[]{:S(2)}) collective-permute-start(bf16[2,64,384]{2,1,0:T(8,128)(2,1)S(1)} %get-tuple-element.94), channel_id=1, source_target_pairs={{12,0},{14,2},{13,4},{15,6},{28,8},{30,10},{29,12},{31,14}} | collective-permute-start | bytes 294920 | tf_op jit(solution)/shard_map/ppermute | solution.py:231
  48.4 2.0 %collective-permute-start.14 = (bf16[2,64,384]{2,1,0:T(8,128)(2,1)S(1)}, bf16[2,64,384]{2,1,0:T(8,128)(2,1)S(1)}, u32[]{:S(2)}, u32[]{:S(2)}) collective-permute-start(bf16[2,64,384]{2,1,0:T(8,128)(2,1)S(1)} %get-tuple-element.91), channel_id=1, source_target_pairs={{12,17},{14,19},{13,21},{15,23},{28,25},{30,27},{29,29},{31,31}} | collective-permute-start | bytes 294920 | tf_op jit(solution)/shard_map/ppermute | solution.py:231
  49.0 13.6 %collective-permute-start.15 = (bf16[2,64,384]{2,1,0:T(8,128)(2,1)S(1)}, bf16[2,64,384]{2,1,0:T(8,128)(2,1)S(1)}, u32[]{:S(2)}, u32[]{:S(2)}) collective-permute-start(bf16[2,64,384]{2,1,0:T(8,128)(2,1)S(1)} %get-tuple-element.92), channel_id=1, source_target_pairs={{12,16},{14,18},{13,20},{15,22},{28,24},{30,26},{29,28},{31,30}} | collective-permute-start | bytes 294920 | tf_op jit(solution)/shard_map/ppermute | solution.py:231

commit v3 on v2

v3 whole, which is shorter than its diff:
```python
import functools

import jax
import jax.numpy as jnp
from jax import lax
from jax.experimental import pallas as pl
from jax.experimental.pallas import tpu as pltpu
from jax.sharding import PartitionSpec as P

HALVES = 2
LAG = 2
TAPS = 3
VMEM_LIMIT = 24 << 20
MESH_AXES = ("tm", "segment", "band")


def whole(space=pltpu.VMEM):
    return pl.BlockSpec(memory_space=space)


def resident(value):
    return pltpu.with_memory_space_constraint(value, pltpu.VMEM)


def working(slot, frames, segments):
    return [s for s in range(segments) if 0 <= slot - LAG * s < frames]


def on_unit(unit, holders):
    here = lax.axis_index("segment") == unit
    if holders < lax.axis_size("tm"):
        here = jnp.logical_and(here, lax.axis_index("tm") < holders)
    return here


def rows_at(start, count, cols):
    return pl.ds(pl.multiple_of(start * cols, cols), count * cols)


def loader_kernel(weight, bias, gain, now, past, bias_out, gain_out, sems):
    channels = weight.shape[-1]
    copies = [(bias, bias_out), (gain, gain_out), (weight.at[2], now)]
    for row in range(TAPS):
        for age in range(2):
            copies.append((weight.at[age, row], past.at[row, :, pl.ds(age * channels, channels)]))
    copies = [
        pltpu.make_async_copy(source, target, sems.at[number])
        for number, (source, target) in enumerate(copies)
    ]
    for copy in copies:
        copy.start()
    for copy in copies:
        copy.wait()


def frame_kernel(cfg, *refs):
    refs = list(refs)
    pieces = [refs.pop(0) for _ in cfg["places"]]
    received = refs.pop(0) if cfg["came"] is not None else None
    partial, weight, bias, gain = refs[:4]
    refs = refs[4:]
    if cfg["joins"]:
        refs = refs[cfg["finals"] :]
    out = refs.pop(0) if cfg["sends"] else None
    spread = refs.pop(0)
    tails = [refs.pop(0) for _ in range(cfg["finals"])]
    entry = refs.pop(0)
    cols, window, segments = cfg["cols"], cfg["window"], cfg["segments"]
    channels = entry.shape[-1]
    half = lax.axis_index("band") // cfg["per_half"]

    def run(unit):
        have = window - unit
        need = have - 1
        size = have * cols
        if unit == 0:
            step = entry.shape[0] // len(pieces)
            spot = lax.axis_index("tm") * cfg["bands"] + lax.axis_index("band")
            for piece, code in zip(pieces, cfg["places"]):
                number = (code >> (2 * spot)) & 3
                entry[pl.ds(pl.multiple_of(number * step, step), step), :] = piece[...]
            source, skip = entry, 0
        else:
            source, skip = received, half * (unit - 1 - cfg["came"])
        wide = source[rows_at(skip, have, cols), :].astype(jnp.float32)
        meansq = jnp.sum(wide * wide, axis=-1, keepdims=True) * (1.0 / channels)
        normed = wide * lax.rsqrt(meansq + 1e-06) * gain[...]
        ready = normed / (1.0 + jnp.exp(-normed))
        column = lax.broadcasted_iota(jnp.int32, ready.shape, 0) & (cols - 1)
        before = jnp.where(column == 0, 0.0, pltpu.roll(ready, 1, 0))
        after = jnp.where(column == cols - 1, 0.0, pltpu.roll(ready, size - 1, 0))
        edge = jnp.zeros((cols, TAPS * channels), jnp.bfloat16)
        spread[pl.ds(0, cols), :] = edge
        spread[pl.ds(size + cols, cols), :] = edge
        for number, value in enumerate((before, ready, after)):
            spread[pl.ds(cols, size), pl.ds(number * channels, channels)] = value.astype(jnp.bfloat16)
        kept = source[rows_at(skip + half, need, cols), :].astype(jnp.float32)
        total = partial[pl.ds(0, need * cols), :] + kept + bias[...]
        for row in range(TAPS):
            total += jnp.dot(
                spread[rows_at(half + row, need, cols), :], weight[row], preferred_element_type=jnp.float32
            )
        value = total.astype(jnp.bfloat16)
        if unit < segments - 1:
            out[rows_at(half * (unit - cfg["lowest"]), need, cols), :] = value
        else:
            length = value.shape[0] // len(tails)
            for number, tail in enumerate(tails):
                tail[cfg["tail_at"]] = value[number * length : (number + 1) * length]

    for unit in cfg["units"]:
        pl.when(on_unit(unit, cfg["holders"]))(functools.partial(run, unit))


def history_kernel(cfg, spread, near, far, weight, near_out, far_out):
    cols, window = cfg["cols"], cfg["window"]
    channels = near.shape[-1]
    half = lax.axis_index("band") // cfg["per_half"]

    def run(unit):
        need = window - unit - 1
        here = pl.ds(0, need * cols)
        total = jnp.zeros((need * cols, 2 * channels), jnp.float32)
        for row in range(TAPS):
            total += jnp.dot(
                spread[rows_at(half + row, need, cols), :], weight[row], preferred_element_type=jnp.float32
            )
        near_out[here, :] = far[here, :] + total[:, channels:]
        far_out[here, :] = total[:, :channels]

    for unit in cfg["later"]:
        pl.when(on_unit(unit, cfg["holders"]))(functools.partial(run, unit))


def entry_plan(times, segments, bands, clips, per_half):
    holders = clips // per_half

    def spot(t, s, b):
        return (t * segments + s) * bands + b

    pairs, places, clip_of = [], [], {}
    for t in range(times):
        near = t if t < holders else 0
        group = [[] for _ in range(TAPS)]
        codes = [0] * TAPS
        for x in range(holders):
            for h in range(HALVES):
                edge, inner, third = (0, 1, 2) if h == 0 else (3, 2, 1)
                for j in range(per_half):
                    own = 2 * h + j
                    other = 2 * h + 1 - j
                    if x == near:
                        steps = [(own, 0), (other, 0), (third, j)]
                    elif j == 0:
                        steps = [(third, 1), (inner, 1), (edge, 0)]
                    else:
                        steps = [(inner, 2), (edge, 1), (third, 2)]
                    there = h * per_half + j
                    for number, (source, segment) in enumerate(steps):
                        group[number].append((spot(t, segment, source), spot(x, 0, there)))
                        codes[number] |= (source - h) << (2 * (x * bands + there))
                        key = (near, number, segment, source)
                        assert clip_of.setdefault(key, x * per_half + j) == x * per_half + j
        for members in group:
            assert len({a for a, _ in members}) == len({b for _, b in members}) == len(members)
        pairs.append(group)
        places.append(codes)
    senders = [[0] * TAPS for _ in range(holders)]
    for (near, number, segment, source), clip in clip_of.items():
        senders[near][number] |= clip << (2 * (segment * bands + source))
    return pairs, places, senders


def local(features, conv_weight, conv_bias, norm_gain):
    times, segments, bands = (lax.axis_size(name) for name in MESH_AXES)
    time, position, band = (lax.axis_index(name) for name in MESH_AXES)
    clips, own_frames, own_rows, cols, channels = features.shape
    frames = own_frames * times
    per_half = bands // HALVES
    window = own_rows * bands // HALVES + segments
    holders = clips // per_half
    piece = own_rows * cols
    assert clips == segments == bands == 4 and holders == 2 <= times and window == TAPS * own_rows

    def stream(clip, half):
        return clip // per_half, half * per_half + clip % per_half

    def spot(t, s, b):
        return (t * segments + s) * bands + b

    pairs, places, senders = entry_plan(times, segments, bands, clips, per_half)
    sender = 2 * (position * bands + band)
    rounds = []
    for number in range(TAPS):
        first, second = (jnp.uint32(senders[near][number]) for near in range(holders))
        code = jnp.where(time == 1, second, first)
        clip = ((code >> sender.astype(jnp.uint32)) & 3).astype(jnp.int32)
        value = lax.dynamic_index_in_dim(features, clip, 0, keepdims=False)
        rounds.append(value.reshape(own_frames, piece, channels))
    entries = [
        [lax.ppermute(rounds[number], MESH_AXES, pairs[t][number]) for number in range(TAPS)]
        for t in range(times)
    ]

    stored = [conv_weight[0].reshape(TAPS, TAPS, TAPS * channels, channels), conv_bias, norm_gain]
    now, past, bias, gain = pl.pallas_call(
        loader_kernel,
        out_shape=[
            pltpu.VMEM((TAPS, TAPS * channels, channels), stored[0].dtype),
            pltpu.VMEM((TAPS, TAPS * channels, 2 * channels), stored[0].dtype),
            pltpu.VMEM(conv_bias.shape, conv_bias.dtype),
            pltpu.VMEM(norm_gain.shape, norm_gain.dtype),
        ],
        in_specs=[whole(pltpu.HBM)] * 3,
        out_specs=[whole()] * 4,
        scratch_shapes=[pltpu.SemaphoreType.DMA((9,))],
        compiler_params=pltpu.CompilerParams(vmem_limit_bytes=1 << 20),
        cost_estimate=pl.CostEstimate(flops=0, transcendentals=0, bytes_accessed=2 * stored[0].size),
        name="loader",
    )(*[pltpu.with_memory_space_constraint(value, pltpu.HBM) for value in stored])
    now, past, bias, gain = (resident(value) for value in (now, past, bias, gain))

    state = ((window - 1) * cols, channels)
    near = jnp.zeros(state, jnp.float32)
    far = jnp.zeros(state, jnp.float32)
    slots = frames + LAG * (segments - 1)
    moving = {}
    tails = []
    landed = []
    for slot in range(slots):
        units = working(slot, frames, segments)
        senders_now = [s for s in units if s < segments - 1]
        last = slot - LAG * (segments - 1)
        finals = per_half if last >= 0 else 0
        alone = last // own_frames == times - 1
        cfg = dict(
            units=units,
            later=[s for s in units if slot - LAG * s < frames - 1],
            sends=bool(senders_now),
            lowest=min(senders_now, default=0),
            places=places[slot // own_frames] if slot < frames else [],
            came=min(working(slot - LAG, frames, segments)) if slot >= LAG else None,
            finals=finals,
            tail_at=0 if alone else last % own_frames,
            joins=finals and not alone and last % own_frames > 0,
            cols=cols,
            window=window,
            segments=segments,
            bands=bands,
            per_half=per_half,
            holders=holders,
        )
        operands = []
        if slot < frames:
            operands += [resident(value[slot % own_frames]) for value in entries[slot // own_frames]]
        if slot >= LAG:
            operands.append(resident(moving.pop(slot - LAG)))
        operands += [resident(near), now, bias, gain]
        shapes = []
        if cfg["sends"]:
            shapes.append(pltpu.VMEM(((window - 1 - cfg["lowest"]) * cols, channels), jnp.bfloat16))
        shapes.append(pltpu.VMEM(((window + 2) * cols, TAPS * channels), jnp.bfloat16))
        aliases = {}
        if cfg["joins"]:
            for index, value in enumerate(tails):
                aliases[len(operands)] = len(shapes) + index
                operands.append(resident(value))
        shapes += [pltpu.VMEM((1 if alone else own_frames, piece, channels), jnp.bfloat16)] * finals
        results = list(
            pl.pallas_call(
                functools.partial(frame_kernel, cfg),
                out_shape=shapes,
                in_specs=[whole()] * len(operands),
                out_specs=[whole()] * len(shapes),
                scratch_shapes=[pltpu.VMEM((window * cols, channels), jnp.bfloat16)],
                input_output_aliases=aliases,
                compiler_params=pltpu.CompilerParams(vmem_limit_bytes=VMEM_LIMIT),
                cost_estimate=pl.CostEstimate(
                    flops=2 * state[0] * 9 * channels * channels,
                    transcendentals=state[0] * channels,
                    bytes_accessed=12 * state[0] * channels,
                ),
                name="frame",
            )(*operands)
        )
        out = results.pop(0) if cfg["sends"] else None
        spread = results.pop(0)
        tails = results
        if cfg["sends"]:
            moving[slot] = lax.ppermute(out, "segment", [(s, s + 1) for s in senders_now])
        if finals and (alone or last % own_frames == own_frames - 1):
            there = last // own_frames
            for index in range(per_half):
                routes = []
                for clip in range(clips):
                    for h in range(HALVES):
                        t, b = stream(clip, h)
                        routes.append((spot(t, segments - 1, b), spot(there, clip, h * per_half + index)))
                landed.append((there, index, lax.ppermute(tails[index], MESH_AXES, routes)))
        if cfg["later"]:
            near, far = pl.pallas_call(
                functools.partial(history_kernel, cfg),
                out_shape=[pltpu.VMEM(state, jnp.float32)] * 2,
                in_specs=[whole()] * 4,
                out_specs=[whole()] * 2,
                input_output_aliases={1: 0, 2: 1},
                compiler_params=pltpu.CompilerParams(vmem_limit_bytes=VMEM_LIMIT),
                cost_estimate=pl.CostEstimate(
                    flops=2 * state[0] * 18 * channels * channels,
                    transcendentals=0,
                    bytes_accessed=12 * state[0] * channels,
                ),
                name="history",
            )(resident(spread), resident(near), resident(far), past)

    result = None
    for t in range(times):
        for index in range(per_half):
            parts = [value for there, number, value in landed if (there, number) == (t, index)]
            value = parts[0] if len(parts) == 1 else jnp.concatenate(parts, axis=0)
            here = jnp.logical_and(time == t, band % per_half == index)
            result = value if result is None else jnp.where(here, value, result)
    return result.reshape(1, own_frames, own_rows, cols, channels)


def solution(mesh):
    return jax.shard_map(
        local,
        mesh=mesh,
        in_specs=(
            P(None, "tm", "band", None, None),
            P("segment", None, None, None),
            P("segment", None),
            P("segment", None),
        ),
        out_specs=P("segment", "tm", "band", None, None),
        check_vma=False,
    )
```

time: 63.7 us -> 66.3 us (1.041)
  waiting for transfers between devices: 21.8 us -> 27.1 us
  starting transfers between devices: 25.9 us -> 24.3 us
  Pallas kernels: 13.4 us -> 12.1 us
    ppermute x18 -> x20, waiting for transfers between devices: 21.8 us -> 27.1 us  [the longest x8 19.2 us: local(): lax.ppermute(out, 'segment', [(s, s + 1) for s in senders_now])]
    ppermute x18 -> x20, starting transfers between devices: 25.9 us -> 24.3 us  [the longest x8 15.1 us: local(): lax.ppermute(out, 'segment', [(s, s + 1) for s in senders_now])]
    pallas_call x20, Pallas kernels: 13.4 us -> 12.1 us  [the longest x10 5.16 us: local(): pl.pallas_call(functools.partial(frame_kernel, cfg), out_shape=shapes, in...]
    dynamic_slice x1, local copies, waits for them, and re-layouts: 0.01 us -> 1.07 us  [local(): value = lax.dynamic_index_in_dim(features, clip, 0, keepdims=False)]
    unnamed x2 -> x0, local copies, waits for them, and re-layouts: 1 us -> none
  transfers between devices with their start and end apart: 18 -> 20, of which waited for: 4 -> 6; matrix products, arithmetic and copies ran while one was open for 0% -> 0% of each run, Pallas kernels for 21% -> 18%
where the time goes in v3:
time: 66.3 us; the launch traced here: 65.8 us
  waiting for transfers between devices  27.1 us (41%)
  starting transfers between devices  24.3 us (37%)
  Pallas kernels  12.1 us (18%)
  local copies, waits for them, and re-layouts  1.18 us (2%)
  other arithmetic  0.67 us (1%)
    ppermute x8, waiting for transfers between devices, local(): lax.ppermute(out, 'segment', [(s, s + 1) for s in senders_now])  19.2 us
    ppermute x8, starting transfers between devices, local(): lax.ppermute(out, 'segment', [(s, s + 1) for s in senders_now])  15.1 us
    ppermute x6, waiting for transfers between devices, local(): landed.append((there, index, lax.ppermute(tails[index], MESH_AXES, routes)))  7.85 us
    ppermute x6, starting transfers between devices, local(): landed.append((there, index, lax.ppermute(tails[index], MESH_AXES, routes)))  5.23 us
    pallas_call x10, Pallas kernels, local(): pl.pallas_call(functools.partial(frame_kernel, cfg), out_shape=shapes, in...  5.16 us
    ppermute x6, starting transfers between devices, local(): lax.ppermute(rounds[number], MESH_AXES, pairs[t][number])  4 us
    pallas_call x9, Pallas kernels, local(): pl.pallas_call(functools.partial(history_kernel, cfg), out_shape=[pltpu.V...  3.59 us
    pallas_call x1, Pallas kernels, local(): pl.pallas_call(loader_kernel, out_shape=[pltpu.VMEM((TAPS, TAPS * channel...  3.38 us
  transfers between devices with their start and end apart: 20, of which 6 were waited for; matrix products, arithmetic and copies ran while one was open for 0% of the time, Pallas kernels for 18%

profile of v3, /device:TPU:18, one launch (start us, length us, event | category | flops | bytes accessed | tf_op | source)
XLA Modules:
  0.0 65.8 jit_solution(5279487352696117875)
XLA Ops:
  0.0 1.1 %constant_dynamic-slice_fusion = (bf16[1,2,4,16,384]{4,3,2,1,0:T(8,128)(2,1)S(1)}, bf16[1,2,4,16,384]{4,3,2,1,0:T(8,128)(2,1)S(1)}, bf16[1,2,4,16,384]{4,3,2,1,0:T(8,128)(2,1)S(1)}) fusion(bf16[4,2,4,16,384]{4,3,2,1,0:T(8,128)(2,1)} %param.4, s32[]{:T(128)S(6)} %select_n.60, s32[]{:T(128)S(6)} %select_n.56, s32[]{:T(128)S(6)} %select_n.58), kind=kLoop, calls=%fused_computation.14 | loop fusion | bytes 589836 | tf_op jit(solution)/shard_map/jit(dynamic_index_in_dim)/dynamic_slice | solution.py:198
  1.1 0.7 %collective-permute-start.3 = (bf16[2,64,384]{2,1,0:T(8,128)(2,1)S(1)}, bf16[2,64,384]{2,1,0:T(8,128)(2,1)S(1)}, u32[]{:S(2)}, u32[]{:S(2)}) collective-permute-start(bf16[2,64,384]{2,1,0:T(8,128)(2,1)S(1)} %bitcast.34), channel_id=1, source_target_pairs={{0,0},{1,1},{2,2},{3,3},{6,16},{9,17},{5,18},{10,19}} | collective-permute-start | bytes 294920 | tf_op jit(solution)/shard_map/ppermute | solution.py:201
  1.8 0.7 %collective-permute-start = (bf16[2,64,384]{2,1,0:T(8,128)(2,1)S(1)}, bf16[2,64,384]{2,1,0:T(8,128)(2,1)S(1)}, u32[]{:S(2)}, u32[]{:S(2)}) collective-permute-start(bf16[2,64,384]{2,1,0:T(8,128)(2,1)S(1)} %bitcast.35), channel_id=1, source_target_pairs={{22,0},{25,1},{21,2},{26,3},{16,16},{17,17},{18,18},{19,19}} | collective-permute-start | bytes 294920 | tf_op jit(solution)/shard_map/ppermute | solution.py:201
  2.4 0.7 %collective-permute-start.5 = (bf16[2,64,384]{2,1,0:T(8,128)(2,1)S(1)}, bf16[2,64,384]{2,1,0:T(8,128)(2,1)S(1)}, u32[]{:S(2)}, u32[]{:S(2)}) collective-permute-start(bf16[2,64,384]{2,1,0:T(8,128)(2,1)S(1)} %bitcast.32), channel_id=1, source_target_pairs={{2,0},{6,1},{1,2},{5,3},{0,16},{10,17},{3,18},{9,19}} | collective-permute-start | bytes 294920 | tf_op jit(solution)/shard_map/ppermute | solution.py:201
  3.1 0.7 %collective-permute-start.2 = (bf16[2,64,384]{2,1,0:T(8,128)(2,1)S(1)}, bf16[2,64,384]{2,1,0:T(8,128)(2,1)S(1)}, u32[]{:S(2)}, u32[]{:S(2)}) collective-permute-start(bf16[2,64,384]{2,1,0:T(8,128)(2,1)S(1)} %bitcast.33), channel_id=1, source_target_pairs={{16,0},{26,1},{19,2},{25,3},{18,16},{22,17},{17,18},{21,19}} | collective-permute-start | bytes 294920 | tf_op jit(solution)/shard_map/ppermute | solution.py:201
  3.8 0.7 %collective-permute-start.4 = (bf16[2,64,384]{2,1,0:T(8,128)(2,1)S(1)}, bf16[2,64,384]{2,1,0:T(8,128)(2,1)S(1)}, u32[]{:S(2)}, u32[]{:S(2)}) collective-permute-start(bf16[2,64,384]{2,1,0:T(8,128)(2,1)S(1)} %bitcast.30), channel_id=1, source_target_pairs={{1,0},{0,1},{3,2},{2,3},{5,16},{4,17},{6,18},{7,19}} | collective-permute-start | bytes 294920 | tf_op jit(solution)/shard_map/ppermute | solution.py:201
  4.4 3.4 %loader.1 = (bf16[3,1152,384]{2,1,0:T(8,128)(2,1)S(1)}, bf16[3,1152,768]{2,1,0:T(8,128)(2,1)S(1)}, f32[1,384]{1,0:T(1,128)S(1)}, f32[1,384]{1,0:T(1,128)S(1)}) custom-call(bf16[3,3,1152,384]{3,2,1,0:T(8,128)(2,1)} %bitcast.29, f32[1,384]{1,0:T(1,128)} %bias.1, f32[1,384]{1,0:T(1,128)} %gain.1), custom_call_target="tpu_custom_call" | custom-call | bytes 7962624 | tf_op jit(solution)/shard_map/loader/pallas_call | solution.py:206
  7.8 0.7 %collective-permute-start.1 = (bf16[2,64,384]{2,1,0:T(8,128)(2,1)S(1)}, bf16[2,64,384]{2,1,0:T(8,128)(2,1)S(1)}, u32[]{:S(2)}, u32[]{:S(2)}) collective-permute-start(bf16[2,64,384]{2,1,0:T(8,128)(2,1)S(1)} %bitcast.31), channel_id=1, source_target_pairs={{21,0},{20,1},{22,2},{23,3},{17,16},{16,17},{19,18},{18,19}} | collective-permute-start | bytes 294920 | tf_op jit(solution)/shard_map/ppermute | solution.py:201
  8.7 0.7 %collective-permute-start.6 = (bf16[176,384]{1,0:T(8,128)(2,1)S(1)}, bf16[176,384]{1,0:T(8,128)(2,1)S(1)}, u32[]{:S(2)}, u32[]{:S(2)}) collective-permute-start(bf16[176,384]{1,0:T(8,128)(2,1)S(1)} %get-tuple-element.54), channel_id=1, source_target_pairs={{0,4},{1,5},{2,6},{3,7},{16,20},{17,21},{18,22},{19,23}} | collective-permute-start | bytes 405512 | tf_op jit(solution)/shard_map/ppermute | solution.py:290
  9.4 0.7 %collective-permute-start.8 = (bf16[176,384]{1,0:T(8,128)(2,1)S(1)}, bf16[176,384]{1,0:T(8,128)(2,1)S(1)}, u32[]{:S(2)}, u32[]{:S(2)}) collective-permute-start(bf16[176,384]{1,0:T(8,128)(2,1)S(1)} %get-tuple-element.62), channel_id=1, source_target_pairs={{0,4},{1,5},{2,6},{3,7},{16,20},{17,21},{18,22},{19,23}} | collective-permute-start | bytes 405512 | tf_op jit(solution)/shard_map/ppermute | solution.py:290
  10.3 1.3 %collective-permute-start.7 = (bf16[176,384]{1,0:T(8,128)(2,1)S(1)}, bf16[176,384]{1,0:T(8,128)(2,1)S(1)}, u32[]{:S(2)}, u32[]{:S(2)}) collective-permute-start(bf16[176,384]{1,0:T(8,128)(2,1)S(1)} %get-tuple-element.61), channel_id=1, source_target_pairs={{0,4},{4,8},{1,5},{5,9},{2,6},{6,10},{3,7},{7,11},{16,20},{20,24},... | collective-permute-start | bytes 405512 | tf_op jit(solution)/shard_map/ppermute | solution.py:290
  11.6 1.3 %collective-permute-start.10 = (bf16[176,384]{1,0:T(8,128)(2,1)S(1)}, bf16[176,384]{1,0:T(8,128)(2,1)S(1)}, u32[]{:S(2)}, u32[]{:S(2)}) collective-permute-start(bf16[176,384]{1,0:T(8,128)(2,1)S(1)} %get-tuple-element.70), channel_id=1, source_target_pairs={{0,4},{4,8},{1,5},{5,9},{2,6},{6,10},{3,7},{7,11},{16,20},{20,24},... | collective-permute-start | bytes 405512 | tf_op jit(solution)/shard_map/ppermute | solution.py:290
  13.2 16.5 %collective-permute-done.7.refs_0_ = bf16[176,384]{1,0:T(8,128)(2,1)S(1)} collective-permute-done((bf16[176,384]{1,0:T(8,128)(2,1)S(1)}, bf16[176,384]{1,0:T(8,128)(2,1)S(1)}, u32[]{:S(2)}, u32[]{:S(2)}) %collective-permute-start.7) | collective-permute-done | bytes 135200 | tf_op jit(solution)/shard_map/ppermute | solution.py:290
  29.7 1.0 %frame.14 = (bf16[160,384]{1,0:T(8,128)(2,1)S(1)}, bf16[224,1152]{1,0:T(8,128)(2,1)S(1)}) custom-call(bf16[176,384]{1,0:T(8,128)(2,1)S(1)} %collective-permute-done.7.refs_0_, f32[176,384]{1,0:T(8,128)S(1)} %get-tuple-element.68.refs_1_.near, bf16[3,1152,384]{2,1,0:T(8,128)(2,1)S(1)} %get-tuple-element.51.refs_4_.refs_5_.refs_2_, ...), custom_call_target="tpu_custom_call" | custom-call | flops 467140608 | bytes 811008 | tf_op jit(solution)/shard_map/frame/pallas_call | solution.py:270
  30.7 1.9 %collective-permute-start.9 = (bf16[160,384]{1,0:T(8,128)(2,1)S(1)}, bf16[160,384]{1,0:T(8,128)(2,1)S(1)}, u32[]{:S(2)}, u32[]{:S(2)}) collective-permute-start(bf16[160,384]{1,0:T(8,128)(2,1)S(1)} %get-tuple-element.69), channel_id=1, source_target_pairs={{4,8},{8,12},{5,9},{9,13},{6,10},{10,14},{7,11},{11,15},{20,24},{2... | collective-permute-start | bytes 368648 | tf_op jit(solution)/shard_map/ppermute | solution.py:290
  32.6 1.1 %history.13 = (f32[176,384]{1,0:T(8,128)S(1)}, f32[176,384]{1,0:T(8,128)S(1)}) custom-call(bf16[224,1152]{1,0:T(8,128)(2,1)S(1)} %get-tuple-element.71.spread, f32[176,384]{1,0:T(8,128)S(1)} %get-tuple-element.68.refs_1_.near, f32[176,384]{1,0:T(8,128)S(1)} %get-tuple-element.72.far, ...), custom_call_target="tpu_custom_call", output_to_operand_aliasing={{0}: (1, {}), {1}: (2, {})} | custom-call | flops 934281216 | bytes 811008 | tf_op jit(solution)/shard_map/history/pallas_call | solution.py:301
  33.9 1.0 %frame.15 = (bf16[160,384]{1,0:T(8,128)(2,1)S(1)}, bf16[224,1152]{1,0:T(8,128)(2,1)S(1)}) custom-call(bf16[176,384]{1,0:T(8,128)(2,1)S(1)} %collective-permute-done.10.refs_0_, f32[176,384]{1,0:T(8,128)S(1)} %get-tuple-element.73.refs_1_.near, bf16[3,1152,384]{2,1,0:T(8,128)(2,1)S(1)} %get-tuple-element.51.refs_4_.refs_5_.refs_2_, ...), custom_call_target="tpu_custom_call" | custom-call | flops 467140608 | bytes 811008 | tf_op jit(solution)/shard_map/frame/pallas_call | solution.py:270
  34.9 1.9 %collective-permute-start.12 = (bf16[160,384]{1,0:T(8,128)(2,1)S(1)}, bf16[160,384]{1,0:T(8,128)(2,1)S(1)}, u32[]{:S(2)}, u32[]{:S(2)}) collective-permute-start(bf16[160,384]{1,0:T(8,128)(2,1)S(1)} %get-tuple-element.78), channel_id=1, source_target_pairs={{4,8},{8,12},{5,9},{9,13},{6,10},{10,14},{7,11},{11,15},{20,24},{2... | collective-permute-start | bytes 368648 | tf_op jit(solution)/shard_map/ppermute | solution.py:290
  36.8 1.1 %history.14 = (f32[176,384]{1,0:T(8,128)S(1)}, f32[176,384]{1,0:T(8,128)S(1)}) custom-call(bf16[224,1152]{1,0:T(8,128)(2,1)S(1)} %get-tuple-element.74.spread, f32[176,384]{1,0:T(8,128)S(1)} %get-tuple-element.73.refs_1_.near, f32[176,384]{1,0:T(8,128)S(1)} %get-tuple-element.75.far, ...), custom_call_target="tpu_custom_call", output_to_operand_aliasing={{0}: (1, {}), {1}: (2, {})} | custom-call | flops 934281216 | bytes 811008 | tf_op jit(solution)/shard_map/history/pallas_call | solution.py:301
  38.0 1.0 %frame.16 = (bf16[144,384]{1,0:T(8,128)(2,1)S(1)}, bf16[224,1152]{1,0:T(8,128)(2,1)S(1)}, bf16[2,64,384]{2,1,0:T(8,128)(2,1)S(1)}, bf16[2,64,384]{2,1,0:T(8,128)(2,1)S(1)}) custom-call(bf16[160,384]{1,0:T(8,128)(2,1)S(1)} %collective-permute-done.9.refs_0_, f32[176,384]{1,0:T(8,128)S(1)} %get-tuple-element.76.refs_1_.near, ...), custom_call_target="tpu_custom_call" | custom-call | flops 467140608 | bytes 811008 | tf_op jit(solution)/shard_map/frame/pallas_call | solution.py:270
  39.0 1.3 %collective-permute-start.11 = (bf16[144,384]{1,0:T(8,128)(2,1)S(1)}, bf16[144,384]{1,0:T(8,128)(2,1)S(1)}, u32[]{:S(2)}, u32[]{:S(2)}) collective-permute-start(bf16[144,384]{1,0:T(8,128)(2,1)S(1)} %get-tuple-element.77), channel_id=1, source_target_pairs={{8,12},{9,13},{10,14},{11,15},{24,28},{25,29},{26,30},{27,31}} | collective-permute-start | bytes 331784 | tf_op jit(solution)/shard_map/ppermute | solution.py:290
  40.3 1.1 %history.15 = (f32[176,384]{1,0:T(8,128)S(1)}, f32[176,384]{1,0:T(8,128)S(1)}) custom-call(bf16[224,1152]{1,0:T(8,128)(2,1)S(1)} %get-tuple-element.79.spread, f32[176,384]{1,0:T(8,128)S(1)} %get-tuple-element.76.refs_1_.near, f32[176,384]{1,0:T(8,128)S(1)} %get-tuple-element.80.far, ...), custom_call_target="tpu_custom_call", output_to_operand_aliasing={{0}: (1, {}), {1}: (2, {})} | custom-call | flops 934281216 | bytes 811008 | tf_op jit(solution)/shard_map/history/pallas_call | solution.py:301
  41.7 1.2 %frame.17 = (bf16[144,384]{1,0:T(8,128)(2,1)S(1)}, bf16[224,1152]{1,0:T(8,128)(2,1)S(1)}, bf16[2,64,384]{2,1,0:T(8,128)(2,1)S(1)}, bf16[2,64,384]{2,1,0:T(8,128)(2,1)S(1)}) custom-call(bf16[160,384]{1,0:T(8,128)(2,1)S(1)} %collective-permute-done.12.refs_0_, ...), custom_call_target="tpu_custom_call", output_to_operand_aliasing={{2}: (5, {}), {3}: (6, {})} | custom-call | flops 467140608 | bytes 811008 | tf_op jit(solution)/shard_map/frame/pallas_call | solution.py:270
  42.9 0.7 %collective-permute-start.18 = (bf16[2,64,384]{2,1,0:T(8,128)(2,1)S(1)}, bf16[2,64,384]{2,1,0:T(8,128)(2,1)S(1)}, u32[]{:S(2)}, u32[]{:S(2)}) collective-permute-start(bf16[2,64,384]{2,1,0:T(8,128)(2,1)S(1)} %get-tuple-element.95), channel_id=1, source_target_pairs={{12,1},{14,3},{13,5},{15,7},{28,9},{30,11},{29,13},{31,15}} | collective-permute-start | bytes 294920 | tf_op jit(solution)/shard_map/ppermute | solution.py:299
  44.3 6.0 %collective-permute-start.14 = (bf16[144,384]{1,0:T(8,128)(2,1)S(1)}, bf16[144,384]{1,0:T(8,128)(2,1)S(1)}, u32[]{:S(2)}, u32[]{:S(2)}) collective-permute-start(bf16[144,384]{1,0:T(8,128)(2,1)S(1)} %get-tuple-element.88), channel_id=1, source_target_pairs={{8,12},{9,13},{10,14},{11,15},{24,28},{25,29},{26,30},{27,31}} | collective-permute-start | bytes 331784 | tf_op jit(solution)/shard_map/ppermute | solution.py:290
  50.3 2.2 %collective-permute-done.14.refs_0_ = bf16[144,384]{1,0:T(8,128)(2,1)S(1)} collective-permute-done((bf16[144,384]{1,0:T(8,128)(2,1)S(1)}, bf16[144,384]{1,0:T(8,128)(2,1)S(1)}, u32[]{:S(2)}, u32[]{:S(2)}) %collective-permute-start.14) | collective-permute-done | bytes 110624 | tf_op jit(solution)/shard_map/ppermute | solution.py:290
  52.5 0.8 %frame.19 = (bf16[224,1152]{1,0:T(8,128)(2,1)}, bf16[1,64,384]{2,1,0:T(8,128)(2,1)S(1)}, bf16[1,64,384]{2,1,0:T(8,128)(2,1)S(1)}) custom-call(bf16[144,384]{1,0:T(8,128)(2,1)S(1)} %collective-permute-done.14.refs_0_, f32[176,384]{1,0:T(8,128)S(1)} %get-tuple-element.91.refs_1_, bf16[3,1152,384]{2,1,0:T(8,128)(2,1)S(1)} %get-tuple-element.51.refs_4_.refs_5_.refs_2_, ...), custom_call_target="tpu_custom_call" | custom-call | flops 467140608 | bytes 811008 | tf_op jit(solution)/shard_map/frame/pallas_call | solution.py:270
  54.0 1.3 %collective-permute-start.17 = (bf16[1,64,384]{2,1,0:T(8,128)(2,1)S(1)}, bf16[1,64,384]{2,1,0:T(8,128)(2,1)S(1)}, u32[]{:S(2)}, u32[]{:S(2)}) collective-permute-start(bf16[1,64,384]{2,1,0:T(8,128)(2,1)S(1)} %get-tuple-element.94), channel_id=1, source_target_pairs={{12,16},{14,18},{13,20},{15,22},{28,24},{30,26},{29,28},{31,30}} | collective-permute-start | bytes 147464 | tf_op jit(solution)/shard_map/ppermute | solution.py:299
  56.0 1.3 %collective-permute-start.16 = (bf16[1,64,384]{2,1,0:T(8,128)(2,1)S(1)}, bf16[1,64,384]{2,1,0:T(8,128)(2,1)S(1)}, u32[]{:S(2)}, u32[]{:S(2)}) collective-permute-start(bf16[1,64,384]{2,1,0:T(8,128)(2,1)S(1)} %get-tuple-element.93), channel_id=1, source_target_pairs={{12,16},{14,18},{13,20},{15,22},{28,24},{30,26},{29,28},{31,30}} | collective-permute-start | bytes 147464 | tf_op jit(solution)/shard_map/ppermute | solution.py:299
  57.3 4.6 %collective-permute-done.17 = bf16[1,64,384]{2,1,0:T(8,128)(2,1)S(1)} collective-permute-done((bf16[1,64,384]{2,1,0:T(8,128)(2,1)S(1)}, bf16[1,64,384]{2,1,0:T(8,128)(2,1)S(1)}, u32[]{:S(2)}, u32[]{:S(2)}) %collective-permute-start.17) | collective-permute-done | bytes 49184 | tf_op jit(solution)/shard_map/ppermute | solution.py:299
  61.9 3.2 %collective-permute-done.16 = bf16[1,64,384]{2,1,0:T(8,128)(2,1)S(1)} collective-permute-done((bf16[1,64,384]{2,1,0:T(8,128)(2,1)S(1)}, bf16[1,64,384]{2,1,0:T(8,128)(2,1)S(1)}, u32[]{:S(2)}, u32[]{:S(2)}) %collective-permute-start.16) | collective-permute-done | bytes 49184 | tf_op jit(solution)/shard_map/ppermute | solution.py:299
  65.2 0.7 %maximum_select_fusion = bf16[2,64,384]{2,1,0:T(8,128)(2,1)} fusion(bf16[1,64,384]{2,1,0:T(8,128)(2,1)S(1)} %collective-permute-done.15, bf16[1,64,384]{2,1,0:T(8,128)(2,1)S(1)} %collective-permute-done.13, bf16[1,64,384]{2,1,0:T(8,128)(2,1)S(1)} %collective-permute-done.17, bf16[1,64,384]{2,1,0:T(8,128)(2,1)S(1)} %collective-permute-done.16, ...), kind=kLoop, calls=%fused_computation | loop fusion | flops 245760 | bytes 491523 | tf_op jit(solution)/shard_map/jit(_where)/select_n | solution.py:322
  (38 shorter events, 3.0 us)
Async XLA Ops:
  1.1 6.8 %collective-permute-start.3 = (bf16[2,64,384]{2,1,0:T(8,128)(2,1)S(1)}, bf16[2,64,384]{2,1,0:T(8,128)(2,1)S(1)}, u32[]{:S(2)}, u32[]{:S(2)}) collective-permute-start(bf16[2,64,384]{2,1,0:T(8,128)(2,1)S(1)} %bitcast.34), channel_id=1, source_target_pairs={{0,0},{1,1},{2,2},{3,3},{6,16},{9,17},{5,18},{10,19}} | collective-permute-start | bytes 294920 | tf_op jit(solution)/shard_map/ppermute | solution.py:201
  1.8 8.4 %collective-permute-start = (bf16[2,64,384]{2,1,0:T(8,128)(2,1)S(1)}, bf16[2,64,384]{2,1,0:T(8,128)(2,1)S(1)}, u32[]{:S(2)}, u32[]{:S(2)}) collective-permute-start(bf16[2,64,384]{2,1,0:T(8,128)(2,1)S(1)} %bitcast.35), channel_id=1, source_target_pairs={{22,0},{25,1},{21,2},{26,3},{16,16},{17,17},{18,18},{19,19}} | collective-permute-start | bytes 294920 | tf_op jit(solution)/shard_map/ppermute | solution.py:201
  2.4 6.1 %collective-permute-start.5 = (bf16[2,64,384]{2,1,0:T(8,128)(2,1)S(1)}, bf16[2,64,384]{2,1,0:T(8,128)(2,1)S(1)}, u32[]{:S(2)}, u32[]{:S(2)}) collective-permute-start(bf16[2,64,384]{2,1,0:T(8,128)(2,1)S(1)} %bitcast.32), channel_id=1, source_target_pairs={{2,0},{6,1},{1,2},{5,3},{0,16},{10,17},{3,18},{9,19}} | collective-permute-start | bytes 294920 | tf_op jit(solution)/shard_map/ppermute | solution.py:201
  3.1 7.0 %collective-permute-start.2 = (bf16[2,64,384]{2,1,0:T(8,128)(2,1)S(1)}, bf16[2,64,384]{2,1,0:T(8,128)(2,1)S(1)}, u32[]{:S(2)}, u32[]{:S(2)}) collective-permute-start(bf16[2,64,384]{2,1,0:T(8,128)(2,1)S(1)} %bitcast.33), channel_id=1, source_target_pairs={{16,0},{26,1},{19,2},{25,3},{18,16},{22,17},{17,18},{21,19}} | collective-permute-start | bytes 294920 | tf_op jit(solution)/shard_map/ppermute | solution.py:201
  3.8 4.8 %collective-permute-start.4 = (bf16[2,64,384]{2,1,0:T(8,128)(2,1)S(1)}, bf16[2,64,384]{2,1,0:T(8,128)(2,1)S(1)}, u32[]{:S(2)}, u32[]{:S(2)}) collective-permute-start(bf16[2,64,384]{2,1,0:T(8,128)(2,1)S(1)} %bitcast.30), channel_id=1, source_target_pairs={{1,0},{0,1},{3,2},{2,3},{5,16},{4,17},{6,18},{7,19}} | collective-permute-start | bytes 294920 | tf_op jit(solution)/shard_map/ppermute | solution.py:201
  7.8 2.3 %collective-permute-start.1 = (bf16[2,64,384]{2,1,0:T(8,128)(2,1)S(1)}, bf16[2,64,384]{2,1,0:T(8,128)(2,1)S(1)}, u32[]{:S(2)}, u32[]{:S(2)}) collective-permute-start(bf16[2,64,384]{2,1,0:T(8,128)(2,1)S(1)} %bitcast.31), channel_id=1, source_target_pairs={{21,0},{20,1},{22,2},{23,3},{17,16},{16,17},{19,18},{18,19}} | collective-permute-start | bytes 294920 | tf_op jit(solution)/shard_map/ppermute | solution.py:201
  8.7 1.6 %collective-permute-start.6 = (bf16[176,384]{1,0:T(8,128)(2,1)S(1)}, bf16[176,384]{1,0:T(8,128)(2,1)S(1)}, u32[]{:S(2)}, u32[]{:S(2)}) collective-permute-start(bf16[176,384]{1,0:T(8,128)(2,1)S(1)} %get-tuple-element.54), channel_id=1, source_target_pairs={{0,4},{1,5},{2,6},{3,7},{16,20},{17,21},{18,22},{19,23}} | collective-permute-start | bytes 405512 | tf_op jit(solution)/shard_map/ppermute | solution.py:290
  9.4 2.2 %collective-permute-start.8 = (bf16[176,384]{1,0:T(8,128)(2,1)S(1)}, bf16[176,384]{1,0:T(8,128)(2,1)S(1)}, u32[]{:S(2)}, u32[]{:S(2)}) collective-permute-start(bf16[176,384]{1,0:T(8,128)(2,1)S(1)} %get-tuple-element.62), channel_id=1, source_target_pairs={{0,4},{1,5},{2,6},{3,7},{16,20},{17,21},{18,22},{19,23}} | collective-permute-start | bytes 405512 | tf_op jit(solution)/shard_map/ppermute | solution.py:290
  10.3 19.4 %collective-permute-start.7 = (bf16[176,384]{1,0:T(8,128)(2,1)S(1)}, bf16[176,384]{1,0:T(8,128)(2,1)S(1)}, u32[]{:S(2)}, u32[]{:S(2)}) collective-permute-start(bf16[176,384]{1,0:T(8,128)(2,1)S(1)} %get-tuple-element.61), channel_id=1, source_target_pairs={{0,4},{4,8},{1,5},{5,9},{2,6},{6,10},{3,7},{7,11},{16,20},{20,24},... | collective-permute-start | bytes 405512 | tf_op jit(solution)/shard_map/ppermute | solution.py:290
  11.6 22.3 %collective-permute-start.10 = (bf16[176,384]{1,0:T(8,128)(2,1)S(1)}, bf16[176,384]{1,0:T(8,128)(2,1)S(1)}, u32[]{:S(2)}, u32[]{:S(2)}) collective-permute-start(bf16[176,384]{1,0:T(8,128)(2,1)S(1)} %get-tuple-element.70), channel_id=1, source_target_pairs={{0,4},{4,8},{1,5},{5,9},{2,6},{6,10},{3,7},{7,11},{16,20},{20,24},... | collective-permute-start | bytes 405512 | tf_op jit(solution)/shard_map/ppermute | solution.py:290
  30.7 7.3 %collective-permute-start.9 = (bf16[160,384]{1,0:T(8,128)(2,1)S(1)}, bf16[160,384]{1,0:T(8,128)(2,1)S(1)}, u32[]{:S(2)}, u32[]{:S(2)}) collective-permute-start(bf16[160,384]{1,0:T(8,128)(2,1)S(1)} %get-tuple-element.69), channel_id=1, source_target_pairs={{4,8},{8,12},{5,9},{9,13},{6,10},{10,14},{7,11},{11,15},{20,24},{2... | collective-permute-start | bytes 368648 | tf_op jit(solution)/shard_map/ppermute | solution.py:290
  34.9 6.8 %collective-permute-start.12 = (bf16[160,384]{1,0:T(8,128)(2,1)S(1)}, bf16[160,384]{1,0:T(8,128)(2,1)S(1)}, u32[]{:S(2)}, u32[]{:S(2)}) collective-permute-start(bf16[160,384]{1,0:T(8,128)(2,1)S(1)} %get-tuple-element.78), channel_id=1, source_target_pairs={{4,8},{8,12},{5,9},{9,13},{6,10},{10,14},{7,11},{11,15},{20,24},{2... | collective-permute-start | bytes 368648 | tf_op jit(solution)/shard_map/ppermute | solution.py:290
  39.0 11.3 %collective-permute-start.11 = (bf16[144,384]{1,0:T(8,128)(2,1)S(1)}, bf16[144,384]{1,0:T(8,128)(2,1)S(1)}, u32[]{:S(2)}, u32[]{:S(2)}) collective-permute-start(bf16[144,384]{1,0:T(8,128)(2,1)S(1)} %get-tuple-element.77), channel_id=1, source_target_pairs={{8,12},{9,13},{10,14},{11,15},{24,28},{25,29},{26,30},{27,31}} | collective-permute-start | bytes 331784 | tf_op jit(solution)/shard_map/ppermute | solution.py:290
  42.9 13.1 %collective-permute-start.18 = (bf16[2,64,384]{2,1,0:T(8,128)(2,1)S(1)}, bf16[2,64,384]{2,1,0:T(8,128)(2,1)S(1)}, u32[]{:S(2)}, u32[]{:S(2)}) collective-permute-start(bf16[2,64,384]{2,1,0:T(8,128)(2,1)S(1)} %get-tuple-element.95), channel_id=1, source_target_pairs={{12,1},{14,3},{13,5},{15,7},{28,9},{30,11},{29,13},{31,15}} | collective-permute-start | bytes 294920 | tf_op jit(solution)/shard_map/ppermute | solution.py:299
  43.6 13.7 %collective-permute-start.19 = (bf16[2,64,384]{2,1,0:T(8,128)(2,1)S(1)}, bf16[2,64,384]{2,1,0:T(8,128)(2,1)S(1)}, u32[]{:S(2)}, u32[]{:S(2)}) collective-permute-start(bf16[2,64,384]{2,1,0:T(8,128)(2,1)S(1)} %get-tuple-element.96), channel_id=1, source_target_pairs={{12,0},{14,2},{13,4},{15,6},{28,8},{30,10},{29,12},{31,14}} | collective-permute-start | bytes 294920 | tf_op jit(solution)/shard_map/ppermute | solution.py:299
  44.3 8.3 %collective-permute-start.14 = (bf16[144,384]{1,0:T(8,128)(2,1)S(1)}, bf16[144,384]{1,0:T(8,128)(2,1)S(1)}, u32[]{:S(2)}, u32[]{:S(2)}) collective-permute-start(bf16[144,384]{1,0:T(8,128)(2,1)S(1)} %get-tuple-element.88), channel_id=1, source_target_pairs={{8,12},{9,13},{10,14},{11,15},{24,28},{25,29},{26,30},{27,31}} | collective-permute-start | bytes 331784 | tf_op jit(solution)/shard_map/ppermute | solution.py:290
  53.4 4.0 %collective-permute-start.15 = (bf16[1,64,384]{2,1,0:T(8,128)(2,1)S(1)}, bf16[1,64,384]{2,1,0:T(8,128)(2,1)S(1)}, u32[]{:S(2)}, u32[]{:S(2)}) collective-permute-start(bf16[1,64,384]{2,1,0:T(8,128)(2,1)S(1)} %get-tuple-element.92), channel_id=1, source_target_pairs={{12,17},{14,19},{13,21},{15,23},{28,25},{30,27},{29,29},{31,31}} | collective-permute-start | bytes 147464 | tf_op jit(solution)/shard_map/ppermute | solution.py:299
  54.0 7.9 %collective-permute-start.17 = (bf16[1,64,384]{2,1,0:T(8,128)(2,1)S(1)}, bf16[1,64,384]{2,1,0:T(8,128)(2,1)S(1)}, u32[]{:S(2)}, u32[]{:S(2)}) collective-permute-start(bf16[1,64,384]{2,1,0:T(8,128)(2,1)S(1)} %get-tuple-element.94), channel_id=1, source_target_pairs={{12,16},{14,18},{13,20},{15,22},{28,24},{30,26},{29,28},{31,30}} | collective-permute-start | bytes 147464 | tf_op jit(solution)/shard_map/ppermute | solution.py:299
  55.3 6.6 %collective-permute-start.13 = (bf16[1,64,384]{2,1,0:T(8,128)(2,1)S(1)}, bf16[1,64,384]{2,1,0:T(8,128)(2,1)S(1)}, u32[]{:S(2)}, u32[]{:S(2)}) collective-permute-start(bf16[1,64,384]{2,1,0:T(8,128)(2,1)S(1)} %get-tuple-element.87), channel_id=1, source_target_pairs={{12,17},{14,19},{13,21},{15,23},{28,25},{30,27},{29,29},{31,31}} | collective-permute-start | bytes 147464 | tf_op jit(solution)/shard_map/ppermute | solution.py:299
  56.0 9.2 %collective-permute-start.16 = (bf16[1,64,384]{2,1,0:T(8,128)(2,1)S(1)}, bf16[1,64,384]{2,1,0:T(8,128)(2,1)S(1)}, u32[]{:S(2)}, u32[]{:S(2)}) collective-permute-start(bf16[1,64,384]{2,1,0:T(8,128)(2,1)S(1)} %get-tuple-element.93), channel_id=1, source_target_pairs={{12,16},{14,18},{13,20},{15,22},{28,24},{30,26},{29,28},{31,30}} | collective-permute-start | bytes 147464 | tf_op jit(solution)/shard_map/ppermute | solution.py:299

commit v4 on v3

v4 whole, which is shorter than its diff:
```python
import functools

import jax
import jax.numpy as jnp
from jax import lax
from jax.experimental import pallas as pl
from jax.experimental.pallas import tpu as pltpu
from jax.sharding import PartitionSpec as P

HALVES = 2
DEPTH = 4
TAPS = 3
VMEM_LIMIT = 24 << 20
MESH_AXES = ("tm", "segment", "band")


def whole(space=pltpu.VMEM):
    return pl.BlockSpec(memory_space=space)


def resident(value):
    return pltpu.with_memory_space_constraint(value, pltpu.VMEM)


def working(slot, frames, segments, lag):
    return [s for s in range(segments) if 0 <= slot - lag * s < frames]


def on_unit(unit, holders):
    here = lax.axis_index("segment") == unit
    if holders < lax.axis_size("tm"):
        here = jnp.logical_and(here, lax.axis_index("tm") < holders)
    return here


def rows_at(start, count, cols):
    return pl.ds(pl.multiple_of(start * cols, cols), count * cols)


def pick_kernel(source, target, sem):
    copy = pltpu.make_async_copy(source.at[lax.axis_index("segment")], target, sem)
    copy.start()
    copy.wait()


def loader_kernel(weight, bias, gain, now, past, bias_out, gain_out, sems):
    channels = weight.shape[-1]
    copies = [(bias, bias_out), (gain, gain_out), (weight.at[2], now)]
    for row in range(TAPS):
        for age in range(2):
            copies.append((weight.at[age, row], past.at[row, :, pl.ds(age * channels, channels)]))
    copies = [
        pltpu.make_async_copy(source, target, sems.at[number])
        for number, (source, target) in enumerate(copies)
    ]
    for copy in copies:
        copy.start()
    for copy in copies:
        copy.wait()


def frame_kernel(cfg, *refs):
    refs = list(refs)
    pieces = [refs.pop(0) for _ in range(cfg["pieces"])]
    received = refs.pop(0) if cfg["came"] is not None else None
    partial, weight, bias, gain = refs[:4]
    refs = refs[4:]
    refs = refs[cfg["passing"] :]
    out = refs.pop(0) if cfg["sends"] else None
    spread = refs.pop(0) if cfg["later"] else refs.pop()
    tails = [refs.pop(0) for _ in range(cfg["finals"])]
    entry = refs.pop()
    cols, window, segments = cfg["cols"], cfg["window"], cfg["segments"]
    channels = entry.shape[-1]
    half = lax.axis_index("band") // cfg["per_half"]

    def run(unit):
        have = window - unit
        need = have - 1
        size = have * cols
        if unit == 0:
            step = entry.shape[0] // TAPS
            for number, piece in enumerate(pieces):
                entry[pl.ds(number * step, step), :] = piece[cfg["piece_at"]]
            source, skip = entry, 0
        else:
            source, skip = received, half * (unit - 1 - cfg["came"])
        wide = source[rows_at(skip, have, cols), :].astype(jnp.float32)
        meansq = jnp.sum(wide * wide, axis=-1, keepdims=True) * (1.0 / channels)
        normed = wide * lax.rsqrt(meansq + 1e-06) * gain[...]
        ready = normed / (1.0 + jnp.exp(-normed))
        column = lax.broadcasted_iota(jnp.int32, ready.shape, 0) & (cols - 1)
        before = jnp.where(column == 0, 0.0, pltpu.roll(ready, 1, 0))
        after = jnp.where(column == cols - 1, 0.0, pltpu.roll(ready, size - 1, 0))
        edge = jnp.zeros((cols, TAPS * channels), jnp.bfloat16)
        spread[pl.ds(0, cols), :] = edge
        spread[pl.ds(size + cols, cols), :] = edge
        for number, value in enumerate((before, ready, after)):
            spread[pl.ds(cols, size), pl.ds(number * channels, channels)] = value.astype(jnp.bfloat16)
        kept = source[rows_at(skip + half, need, cols), :].astype(jnp.float32)
        total = partial[pl.ds(0, need * cols), :] + kept + bias[...]
        for row in range(TAPS):
            total += jnp.dot(
                spread[rows_at(half + row, need, cols), :], weight[row], preferred_element_type=jnp.float32
            )
        value = total.astype(jnp.bfloat16)
        if unit < segments - 1:
            out[rows_at(half * (unit - cfg["lowest"]), need, cols), :] = value
        else:
            length = value.shape[0] // len(tails)
            for number, tail in enumerate(tails):
                tail[cfg["tail_at"]] = value[number * length : (number + 1) * length]

    for unit in cfg["units"]:
        pl.when(on_unit(unit, cfg["holders"]))(functools.partial(run, unit))


def history_kernel(cfg, spread, near, far, weight, near_out, far_out):
    cols, window = cfg["cols"], cfg["window"]
    channels = near.shape[-1]
    half = lax.axis_index("band") // cfg["per_half"]

    def run(unit):
        need = window - unit - 1
        here = pl.ds(0, need * cols)
        total = jnp.zeros((need * cols, 2 * channels), jnp.float32)
        for row in range(TAPS):
            total += jnp.dot(
                spread[rows_at(half + row, need, cols), :], weight[row], preferred_element_type=jnp.float32
            )
        near_out[here, :] = far[here, :] + total[:, channels:]
        far_out[here, :] = total[:, :channels]

    for unit in cfg["later"]:
        pl.when(on_unit(unit, cfg["holders"]))(functools.partial(run, unit))


def local(features, conv_weight, conv_bias, norm_gain):
    times, segments, bands = (lax.axis_size(name) for name in MESH_AXES)
    time, position, band = (lax.axis_index(name) for name in MESH_AXES)
    clips, own_frames, own_rows, cols, channels = features.shape
    frames = own_frames * times
    per_half = bands // HALVES
    window = own_rows * bands // HALVES + segments
    holders = clips // per_half
    piece = own_rows * cols
    assert clips == segments == bands == 4 and holders == 2 <= times and window == TAPS * own_rows

    def stream(clip, half):
        return clip // per_half, half * per_half + clip % per_half

    def spot(t, s, b):
        return (t * segments + s) * bands + b

    mine = pl.pallas_call(
        pick_kernel,
        out_shape=pltpu.VMEM((own_frames, piece, channels), features.dtype),
        in_specs=[whole(pltpu.HBM)],
        out_specs=whole(),
        scratch_shapes=[pltpu.SemaphoreType.DMA],
        compiler_params=pltpu.CompilerParams(vmem_limit_bytes=1 << 20),
        name="pick",
    )(pltpu.with_memory_space_constraint(features.reshape(clips, own_frames, piece, channels), pltpu.HBM))
    entries = []
    for t in range(times):
        group = []
        for number in range(TAPS):
            routes = []
            for clip in range(clips):
                for h in range(HALVES):
                    there, at = stream(clip, h)
                    routes.append((spot(t, clip, h + number), spot(there, 0, at)))
            group.append(lax.ppermute(mine, MESH_AXES, routes))
        entries.append(group)

    stored = [conv_weight[0].reshape(TAPS, TAPS, TAPS * channels, channels), conv_bias, norm_gain]
    now, past, bias, gain = pl.pallas_call(
        loader_kernel,
        out_shape=[
            pltpu.VMEM((TAPS, TAPS * channels, channels), stored[0].dtype),
            pltpu.VMEM((TAPS, TAPS * channels, 2 * channels), stored[0].dtype),
            pltpu.VMEM(conv_bias.shape, conv_bias.dtype),
            pltpu.VMEM(norm_gain.shape, norm_gain.dtype),
        ],
        in_specs=[whole(pltpu.HBM)] * 3,
        out_specs=[whole()] * 4,
        scratch_shapes=[pltpu.SemaphoreType.DMA((9,))],
        compiler_params=pltpu.CompilerParams(vmem_limit_bytes=1 << 20),
        name="loader",
    )(*[pltpu.with_memory_space_constraint(value, pltpu.HBM) for value in stored])
    now, past, bias, gain = (resident(value) for value in (now, past, bias, gain))

    state = ((window - 1) * cols, channels)
    near = jnp.zeros(state, jnp.float32)
    far = jnp.zeros(state, jnp.float32)
    lag = min(frames, DEPTH)
    slots = frames + lag * (segments - 1)
    moving = {}
    tails = []
    held = []
    landed = {}
    for slot in range(slots):
        units = working(slot, frames, segments, lag)
        senders_now = [s for s in units if s < segments - 1]
        last = slot - lag * (segments - 1)
        finals = per_half if last >= 0 else 0
        middle = finals and last % own_frames > 0
        cfg = dict(
            units=units,
            later=[s for s in units if slot - lag * s < frames - 1],
            sends=bool(senders_now),
            lowest=min(senders_now, default=0),
            pieces=TAPS if slot < frames else 0,
            piece_at=slot % own_frames,
            came=min(working(slot - lag, frames, segments, lag)) if slot >= lag else None,
            finals=finals,
            tail_at=last % own_frames,
            passing=(finals if middle else 0) + (len(landed) if slot + 1 == slots else len(held)),
            cols=cols,
            window=window,
            segments=segments,
                        per_half=per_half,
            holders=holders,
        )
        operands = []
        if slot < frames:
            operands += [resident(value) for value in entries[slot // own_frames]]
        if slot >= lag:
            operands.append(resident(moving.pop(slot - lag)))
        operands += [resident(near), now, bias, gain]
        shapes = []
        if cfg["sends"]:
            shapes.append(pltpu.VMEM(((window - 1 - cfg["lowest"]) * cols, channels), jnp.bfloat16))
        wide = pltpu.VMEM(((window + 2) * cols, TAPS * channels), jnp.bfloat16)
        if cfg["later"]:
            shapes.append(wide)
        shape = pltpu.VMEM((own_frames, piece, channels), jnp.bfloat16)
        aliases = {}
        if middle:
            for index, value in enumerate(tails):
                aliases[len(operands)] = len(shapes) + index
                operands.append(resident(value))
        shapes += [shape] * finals
        if slot + 1 == slots:
            held = [(*key, value) for key, value in landed.items()]
        for _, _, value in held:
            aliases[len(operands)] = len(shapes)
            operands.append(resident(value))
            shapes.append(shape)
        results = list(
            pl.pallas_call(
                functools.partial(frame_kernel, cfg),
                out_shape=shapes,
                in_specs=[whole()] * len(operands),
                out_specs=[whole()] * len(shapes),
                scratch_shapes=[pltpu.VMEM((window * cols, channels), jnp.bfloat16)] + ([] if cfg["later"] else [wide]),
                input_output_aliases=aliases,
                compiler_params=pltpu.CompilerParams(vmem_limit_bytes=VMEM_LIMIT),
                cost_estimate=pl.CostEstimate(flops=0, transcendentals=0, bytes_accessed=1 << 10),
                name="frame",
            )(*operands)
        )
        out = results.pop(0) if cfg["sends"] else None
        spread = results.pop(0) if cfg["later"] else None
        tails = results[:finals]
        leaving = [(there, index, value) for (there, index, _), value in zip(held, results[finals:])]
        if slot + 1 == slots:
            landed.update({(there, index): value for there, index, value in leaving})
            leaving = []
        held = []
        if cfg["sends"]:
            moving[slot] = lax.ppermute(out, "segment", [(s, s + 1) for s in senders_now])
        if finals and last % own_frames == own_frames - 1:
            there = last // own_frames
            ready = [(there, index, value) for index, value in enumerate(tails)]
            if there == times - 1:
                leaving += ready
            else:
                leaving.append(ready[0])
                held = ready[1:]
        for there, index, value in leaving:
            routes = []
            for clip in range(clips):
                for h in range(HALVES):
                    t, b = stream(clip, h)
                    routes.append((spot(t, segments - 1, b), spot(there, clip, h * per_half + index)))
            landed[there, index] = lax.ppermute(value, MESH_AXES, routes)
        if cfg["later"]:
            near, far = pl.pallas_call(
                functools.partial(history_kernel, cfg),
                out_shape=[pltpu.VMEM(state, jnp.float32)] * 2,
                in_specs=[whole()] * 4,
                out_specs=[whole()] * 2,
                input_output_aliases={1: 0, 2: 1},
                compiler_params=pltpu.CompilerParams(vmem_limit_bytes=VMEM_LIMIT),
                cost_estimate=pl.CostEstimate(flops=0, transcendentals=0, bytes_accessed=1 << 10),
                name="history",
            )(resident(spread), resident(near), resident(far), past)

    result = None
    for (t, index), value in landed.items():
        here = jnp.logical_and(time == t, band % per_half == index)
        result = value if result is None else jnp.where(here, value, result)
    return result.reshape(1, own_frames, own_rows, cols, channels)


def solution(mesh):
    return jax.shard_map(
        local,
        mesh=mesh,
        in_specs=(
            P(None, "tm", "band", None, None),
            P("segment", None, None, None),
            P("segment", None),
            P("segment", None),
        ),
        out_specs=P("segment", "tm", "band", None, None),
        check_vma=False,
    )
```

time: 66.3 us -> 61.5 us (0.928)
  the two profiles are of different devices: /device:TPU:18 before, /device:TPU:22 now
where the time goes in v4:
time: 61.5 us; the launch traced here: 61.1 us
  starting transfers between devices  30.8 us (50%)
  waiting for transfers between devices  16.7 us (27%)
  Pallas kernels  12.4 us (20%)
  other arithmetic  0.66 us (1%)
    ppermute x6, starting transfers between devices, local(): group.append(lax.ppermute(mine, MESH_AXES, routes))  14.5 us
    ppermute x12, starting transfers between devices, local(): lax.ppermute(out, 'segment', [(s, s + 1) for s in senders_now])  13 us
    ppermute x4, waiting for transfers between devices, local(): landed[there, index] = lax.ppermute(value, MESH_AXES, routes)  9.77 us
    ppermute x12, waiting for transfers between devices, local(): lax.ppermute(out, 'segment', [(s, s + 1) for s in senders_now])  6.91 us
    pallas_call x16, Pallas kernels, local(): pl.pallas_call(functools.partial(frame_kernel, cfg), out_shape=shapes, in...  4.24 us
    pallas_call x12, Pallas kernels, local(): pl.pallas_call(functools.partial(history_kernel, cfg), out_shape=[pltpu.V...  3.83 us
    pallas_call x1, Pallas kernels, local(): pl.pallas_call(loader_kernel, out_shape=[pltpu.VMEM((TAPS, TAPS * channel...  3.38 us
    ppermute x4, starting transfers between devices, local(): landed[there, index] = lax.ppermute(value, MESH_AXES, routes)  3.28 us
  transfers between devices with their start and end apart: 22, of which 5 were waited for; matrix products, arithmetic and copies ran while one was open for 0% of the time, Pallas kernels for 19%

profile of v4, /device:TPU:22, one launch (start us, length us, event | category | flops | bytes accessed | tf_op | source)
XLA Modules:
  0.0 61.1 jit_solution(9002882899913241351)
XLA Ops:
  0.0 0.9 %pick.1 = bf16[2,64,384]{2,1,0:T(8,128)(2,1)S(1)} custom-call(bf16[4,2,64,384]{3,2,1,0:T(8,128)(2,1)} %bitcast.4), custom_call_target="tpu_custom_call" | custom-call | tf_op jit(solution)/shard_map/pick/pallas_call | solution.py:155
  0.9 0.7 %collective-permute-start.3 = (bf16[2,64,384]{2,1,0:T(8,128)(2,1)S(1)}, bf16[2,64,384]{2,1,0:T(8,128)(2,1)S(1)}, u32[]{:S(2)}, u32[]{:S(2)}) collective-permute-start(bf16[2,64,384]{2,1,0:T(8,128)(2,1)S(1)} %pick.1), channel_id=1, source_target_pairs={{0,0},{1,2},{4,1},{5,3},{8,16},{9,18},{12,17},{13,19}} | collective-permute-start | bytes 294920 | tf_op jit(solution)/shard_map/ppermute | solution.py:173
  1.6 0.7 %collective-permute-start.4 = (bf16[2,64,384]{2,1,0:T(8,128)(2,1)S(1)}, bf16[2,64,384]{2,1,0:T(8,128)(2,1)S(1)}, u32[]{:S(2)}, u32[]{:S(2)}) collective-permute-start(bf16[2,64,384]{2,1,0:T(8,128)(2,1)S(1)} %pick.1), channel_id=1, source_target_pairs={{1,0},{2,2},{5,1},{6,3},{9,16},{10,18},{13,17},{14,19}} | collective-permute-start | bytes 294920 | tf_op jit(solution)/shard_map/ppermute | solution.py:173
  2.3 0.7 %collective-permute-start.5 = (bf16[2,64,384]{2,1,0:T(8,128)(2,1)S(1)}, bf16[2,64,384]{2,1,0:T(8,128)(2,1)S(1)}, u32[]{:S(2)}, u32[]{:S(2)}) collective-permute-start(bf16[2,64,384]{2,1,0:T(8,128)(2,1)S(1)} %pick.1), channel_id=1, source_target_pairs={{2,0},{3,2},{6,1},{7,3},{10,16},{11,18},{14,17},{15,19}} | collective-permute-start | bytes 294920 | tf_op jit(solution)/shard_map/ppermute | solution.py:173
  2.9 0.7 %collective-permute-start = (bf16[2,64,384]{2,1,0:T(8,128)(2,1)S(1)}, bf16[2,64,384]{2,1,0:T(8,128)(2,1)S(1)}, u32[]{:S(2)}, u32[]{:S(2)}) collective-permute-start(bf16[2,64,384]{2,1,0:T(8,128)(2,1)S(1)} %pick.1), channel_id=1, source_target_pairs={{16,0},{17,2},{20,1},{21,3},{24,16},{25,18},{28,17},{29,19}} | collective-permute-start | bytes 294920 | tf_op jit(solution)/shard_map/ppermute | solution.py:173
  3.6 4.7 %collective-permute-start.1 = (bf16[2,64,384]{2,1,0:T(8,128)(2,1)S(1)}, bf16[2,64,384]{2,1,0:T(8,128)(2,1)S(1)}, u32[]{:S(2)}, u32[]{:S(2)}) collective-permute-start(bf16[2,64,384]{2,1,0:T(8,128)(2,1)S(1)} %pick.1), channel_id=1, source_target_pairs={{17,0},{18,2},{21,1},{22,3},{25,16},{26,18},{29,17},{30,19}} | collective-permute-start | bytes 294920 | tf_op jit(solution)/shard_map/ppermute | solution.py:173
  8.4 7.0 %collective-permute-start.2 = (bf16[2,64,384]{2,1,0:T(8,128)(2,1)S(1)}, bf16[2,64,384]{2,1,0:T(8,128)(2,1)S(1)}, u32[]{:S(2)}, u32[]{:S(2)}) collective-permute-start(bf16[2,64,384]{2,1,0:T(8,128)(2,1)S(1)} %pick.1), channel_id=1, source_target_pairs={{18,0},{19,2},{22,1},{23,3},{26,16},{27,18},{30,17},{31,19}} | collective-permute-start | bytes 294920 | tf_op jit(solution)/shard_map/ppermute | solution.py:173
  15.4 3.4 %loader.1 = (bf16[3,1152,384]{2,1,0:T(8,128)(2,1)S(1)}, bf16[3,1152,768]{2,1,0:T(8,128)(2,1)S(1)}, f32[1,384]{1,0:T(1,128)S(1)}, f32[1,384]{1,0:T(1,128)S(1)}) custom-call(bf16[3,3,1152,384]{3,2,1,0:T(8,128)(2,1)} %bitcast.3, f32[1,384]{1,0:T(1,128)} %bias.1, f32[1,384]{1,0:T(1,128)} %gain.1), custom_call_target="tpu_custom_call" | custom-call | tf_op jit(solution)/shard_map/loader/pallas_call | solution.py:177
  18.9 0.7 %collective-permute-start.9 = (bf16[176,384]{1,0:T(8,128)(2,1)S(1)}, bf16[176,384]{1,0:T(8,128)(2,1)S(1)}, u32[]{:S(2)}, u32[]{:S(2)}) collective-permute-start(bf16[176,384]{1,0:T(8,128)(2,1)S(1)} %get-tuple-element.78), channel_id=1, source_target_pairs={{0,4},{1,5},{2,6},{3,7},{16,20},{17,21},{18,22},{19,23}} | collective-permute-start | bytes 405512 | tf_op jit(solution)/shard_map/ppermute | solution.py:272
  19.7 0.7 %collective-permute-start.8 = (bf16[176,384]{1,0:T(8,128)(2,1)S(1)}, bf16[176,384]{1,0:T(8,128)(2,1)S(1)}, u32[]{:S(2)}, u32[]{:S(2)}) collective-permute-start(bf16[176,384]{1,0:T(8,128)(2,1)S(1)} %get-tuple-element.77), channel_id=1, source_target_pairs={{0,4},{1,5},{2,6},{3,7},{16,20},{17,21},{18,22},{19,23}} | collective-permute-start | bytes 405512 | tf_op jit(solution)/shard_map/ppermute | solution.py:272
  20.4 0.7 %collective-permute-start.7 = (bf16[176,384]{1,0:T(8,128)(2,1)S(1)}, bf16[176,384]{1,0:T(8,128)(2,1)S(1)}, u32[]{:S(2)}, u32[]{:S(2)}) collective-permute-start(bf16[176,384]{1,0:T(8,128)(2,1)S(1)} %get-tuple-element.76), channel_id=1, source_target_pairs={{0,4},{1,5},{2,6},{3,7},{16,20},{17,21},{18,22},{19,23}} | collective-permute-start | bytes 405512 | tf_op jit(solution)/shard_map/ppermute | solution.py:272
  21.2 0.7 %collective-permute-start.6 = (bf16[176,384]{1,0:T(8,128)(2,1)S(1)}, bf16[176,384]{1,0:T(8,128)(2,1)S(1)}, u32[]{:S(2)}, u32[]{:S(2)}) collective-permute-start(bf16[176,384]{1,0:T(8,128)(2,1)S(1)} %frame.19), channel_id=1, source_target_pairs={{0,4},{1,5},{2,6},{3,7},{16,20},{17,21},{18,22},{19,23}} | collective-permute-start | bytes 405512 | tf_op jit(solution)/shard_map/ppermute | solution.py:272
  21.9 1.3 %collective-permute-start.13 = (bf16[160,384]{1,0:T(8,128)(2,1)S(1)}, bf16[160,384]{1,0:T(8,128)(2,1)S(1)}, u32[]{:S(2)}, u32[]{:S(2)}) collective-permute-start(bf16[160,384]{1,0:T(8,128)(2,1)S(1)} %get-tuple-element.90), channel_id=1, source_target_pairs={{4,8},{5,9},{6,10},{7,11},{20,24},{21,25},{22,26},{23,27}} | collective-permute-start | bytes 368648 | tf_op jit(solution)/shard_map/ppermute | solution.py:272
  23.2 1.3 %collective-permute-start.12 = (bf16[160,384]{1,0:T(8,128)(2,1)S(1)}, bf16[160,384]{1,0:T(8,128)(2,1)S(1)}, u32[]{:S(2)}, u32[]{:S(2)}) collective-permute-start(bf16[160,384]{1,0:T(8,128)(2,1)S(1)} %get-tuple-element.89), channel_id=1, source_target_pairs={{4,8},{5,9},{6,10},{7,11},{20,24},{21,25},{22,26},{23,27}} | collective-permute-start | bytes 368648 | tf_op jit(solution)/shard_map/ppermute | solution.py:272
  24.8 1.3 %collective-permute-start.11 = (bf16[160,384]{1,0:T(8,128)(2,1)S(1)}, bf16[160,384]{1,0:T(8,128)(2,1)S(1)}, u32[]{:S(2)}, u32[]{:S(2)}) collective-permute-start(bf16[160,384]{1,0:T(8,128)(2,1)S(1)} %get-tuple-element.88), channel_id=1, source_target_pairs={{4,8},{5,9},{6,10},{7,11},{20,24},{21,25},{22,26},{23,27}} | collective-permute-start | bytes 368648 | tf_op jit(solution)/shard_map/ppermute | solution.py:272
  26.2 1.3 %collective-permute-start.10 = (bf16[160,384]{1,0:T(8,128)(2,1)S(1)}, bf16[160,384]{1,0:T(8,128)(2,1)S(1)}, u32[]{:S(2)}, u32[]{:S(2)}) collective-permute-start(bf16[160,384]{1,0:T(8,128)(2,1)S(1)} %frame.23), channel_id=1, source_target_pairs={{4,8},{5,9},{6,10},{7,11},{20,24},{21,25},{22,26},{23,27}} | collective-permute-start | bytes 368648 | tf_op jit(solution)/shard_map/ppermute | solution.py:272
  27.5 5.8 %collective-permute-done.13.refs_0_ = bf16[160,384]{1,0:T(8,128)(2,1)S(1)} collective-permute-done((bf16[160,384]{1,0:T(8,128)(2,1)S(1)}, bf16[160,384]{1,0:T(8,128)(2,1)S(1)}, u32[]{:S(2)}, u32[]{:S(2)}) %collective-permute-start.13) | collective-permute-done | bytes 122912 | tf_op jit(solution)/shard_map/ppermute | solution.py:272
  33.2 1.0 %frame.24 = (bf16[144,384]{1,0:T(8,128)(2,1)S(1)}, bf16[224,1152]{1,0:T(8,128)(2,1)S(1)}) custom-call(bf16[160,384]{1,0:T(8,128)(2,1)S(1)} %collective-permute-done.13.refs_0_, f32[176,384]{1,0:T(8,128)S(1)} %get-tuple-element.87.refs_1_.near, bf16[3,1152,384]{2,1,0:T(8,128)(2,1)S(1)} %get-tuple-element.64.refs_4_.refs_2_, ...), custom_call_target="tpu_custom_call" | custom-call | bytes 1024 | tf_op jit(solution)/shard_map/frame/pallas_call | solution.py:251
  34.2 1.3 %collective-permute-start.17 = (bf16[144,384]{1,0:T(8,128)(2,1)S(1)}, bf16[144,384]{1,0:T(8,128)(2,1)S(1)}, u32[]{:S(2)}, u32[]{:S(2)}) collective-permute-start(bf16[144,384]{1,0:T(8,128)(2,1)S(1)} %get-tuple-element.102), channel_id=1, source_target_pairs={{8,12},{9,13},{10,14},{11,15},{24,28},{25,29},{26,30},{27,31}} | collective-permute-start | bytes 331784 | tf_op jit(solution)/shard_map/ppermute | solution.py:272
  35.5 1.1 %history.18 = (f32[176,384]{1,0:T(8,128)S(1)}, f32[176,384]{1,0:T(8,128)S(1)}) custom-call(bf16[224,1152]{1,0:T(8,128)(2,1)S(1)} %get-tuple-element.91.spread, f32[176,384]{1,0:T(8,128)S(1)} %get-tuple-element.87.refs_1_.near, f32[176,384]{1,0:T(8,128)S(1)} %get-tuple-element.92.far, ...), custom_call_target="tpu_custom_call", output_to_operand_aliasing={{0}: (1, {}), {1}: (2, {})} | custom-call | bytes 1024 | tf_op jit(solution)/shard_map/history/pallas_call | solution.py:289
  37.0 1.0 %frame.25 = (bf16[144,384]{1,0:T(8,128)(2,1)S(1)}, bf16[224,1152]{1,0:T(8,128)(2,1)S(1)}) custom-call(bf16[160,384]{1,0:T(8,128)(2,1)S(1)} %collective-permute-done.12.refs_0_, f32[176,384]{1,0:T(8,128)S(1)} %get-tuple-element.93.refs_1_.near, bf16[3,1152,384]{2,1,0:T(8,128)(2,1)S(1)} %get-tuple-element.64.refs_4_.refs_2_, ...), custom_call_target="tpu_custom_call" | custom-call | bytes 1024 | tf_op jit(solution)/shard_map/frame/pallas_call | solution.py:251
  38.0 1.3 %collective-permute-start.16 = (bf16[144,384]{1,0:T(8,128)(2,1)S(1)}, bf16[144,384]{1,0:T(8,128)(2,1)S(1)}, u32[]{:S(2)}, u32[]{:S(2)}) collective-permute-start(bf16[144,384]{1,0:T(8,128)(2,1)S(1)} %get-tuple-element.101), channel_id=1, source_target_pairs={{8,12},{9,13},{10,14},{11,15},{24,28},{25,29},{26,30},{27,31}} | collective-permute-start | bytes 331784 | tf_op jit(solution)/shard_map/ppermute | solution.py:272
  39.3 1.1 %history.19 = (f32[176,384]{1,0:T(8,128)S(1)}, f32[176,384]{1,0:T(8,128)S(1)}) custom-call(bf16[224,1152]{1,0:T(8,128)(2,1)S(1)} %get-tuple-element.94.spread, f32[176,384]{1,0:T(8,128)S(1)} %get-tuple-element.93.refs_1_.near, f32[176,384]{1,0:T(8,128)S(1)} %get-tuple-element.95.far, ...), custom_call_target="tpu_custom_call", output_to_operand_aliasing={{0}: (1, {}), {1}: (2, {})} | custom-call | bytes 1024 | tf_op jit(solution)/shard_map/history/pallas_call | solution.py:289
  40.6 1.0 %frame.26 = (bf16[144,384]{1,0:T(8,128)(2,1)S(1)}, bf16[224,1152]{1,0:T(8,128)(2,1)S(1)}) custom-call(bf16[160,384]{1,0:T(8,128)(2,1)S(1)} %collective-permute-done.11.refs_0_, f32[176,384]{1,0:T(8,128)S(1)} %get-tuple-element.96.refs_1_.near, bf16[3,1152,384]{2,1,0:T(8,128)(2,1)S(1)} %get-tuple-element.64.refs_4_.refs_2_, ...), custom_call_target="tpu_custom_call" | custom-call | bytes 1024 | tf_op jit(solution)/shard_map/frame/pallas_call | solution.py:251
  41.6 1.3 %collective-permute-start.15 = (bf16[144,384]{1,0:T(8,128)(2,1)S(1)}, bf16[144,384]{1,0:T(8,128)(2,1)S(1)}, u32[]{:S(2)}, u32[]{:S(2)}) collective-permute-start(bf16[144,384]{1,0:T(8,128)(2,1)S(1)} %get-tuple-element.100), channel_id=1, source_target_pairs={{8,12},{9,13},{10,14},{11,15},{24,28},{25,29},{26,30},{27,31}} | collective-permute-start | bytes 331784 | tf_op jit(solution)/shard_map/ppermute | solution.py:272
  42.9 1.1 %history.20 = (f32[176,384]{1,0:T(8,128)S(1)}, f32[176,384]{1,0:T(8,128)S(1)}) custom-call(bf16[224,1152]{1,0:T(8,128)(2,1)S(1)} %get-tuple-element.97.spread, f32[176,384]{1,0:T(8,128)S(1)} %get-tuple-element.96.refs_1_.near, f32[176,384]{1,0:T(8,128)S(1)} %get-tuple-element.98.far, ...), custom_call_target="tpu_custom_call", output_to_operand_aliasing={{0}: (1, {}), {1}: (2, {})} | custom-call | bytes 1024 | tf_op jit(solution)/shard_map/history/pallas_call | solution.py:289
  44.0 1.0 %frame.27 = bf16[144,384]{1,0:T(8,128)(2,1)S(1)} custom-call(bf16[160,384]{1,0:T(8,128)(2,1)S(1)} %collective-permute-done.10.refs_0_, f32[176,384]{1,0:T(8,128)S(1)} %get-tuple-element.99.refs_1_.near, bf16[3,1152,384]{2,1,0:T(8,128)(2,1)S(1)} %get-tuple-element.64.refs_4_.refs_2_, f32[1,384]{1,0:T(1,128)S(1)} %get-tuple-element.65.refs_5_.refs_3_, ...), custom_call_target="tpu_custom_call" | custom-call | bytes 1024 | tf_op jit(solution)/shard_map/frame/pallas_call | solution.py:251
  45.1 1.3 %collective-permute-start.14 = (bf16[144,384]{1,0:T(8,128)(2,1)S(1)}, bf16[144,384]{1,0:T(8,128)(2,1)S(1)}, u32[]{:S(2)}, u32[]{:S(2)}) collective-permute-start(bf16[144,384]{1,0:T(8,128)(2,1)S(1)} %frame.27), channel_id=1, source_target_pairs={{8,12},{9,13},{10,14},{11,15},{24,28},{25,29},{26,30},{27,31}} | collective-permute-start | bytes 331784 | tf_op jit(solution)/shard_map/ppermute | solution.py:272
  46.8 0.7 %collective-permute-start.19 = (bf16[2,64,384]{2,1,0:T(8,128)(2,1)S(1)}, bf16[2,64,384]{2,1,0:T(8,128)(2,1)S(1)}, u32[]{:S(2)}, u32[]{:S(2)}) collective-permute-start(bf16[2,64,384]{2,1,0:T(8,128)(2,1)S(1)} %get-tuple-element.118), channel_id=1, source_target_pairs={{12,1},{14,3},{13,5},{15,7},{28,9},{30,11},{29,13},{31,15}} | collective-permute-start | bytes 294920 | tf_op jit(solution)/shard_map/ppermute | solution.py:287
  47.4 0.7 %collective-permute-start.18 = (bf16[2,64,384]{2,1,0:T(8,128)(2,1)S(1)}, bf16[2,64,384]{2,1,0:T(8,128)(2,1)S(1)}, u32[]{:S(2)}, u32[]{:S(2)}) collective-permute-start(bf16[2,64,384]{2,1,0:T(8,128)(2,1)S(1)} %get-tuple-element.117), channel_id=1, source_target_pairs={{12,0},{14,2},{13,4},{15,6},{28,8},{30,10},{29,12},{31,14}} | collective-permute-start | bytes 294920 | tf_op jit(solution)/shard_map/ppermute | solution.py:287
  49.3 1.3 %collective-permute-start.21 = (bf16[2,64,384]{2,1,0:T(8,128)(2,1)S(1)}, bf16[2,64,384]{2,1,0:T(8,128)(2,1)S(1)}, u32[]{:S(2)}, u32[]{:S(2)}) collective-permute-start(bf16[2,64,384]{2,1,0:T(8,128)(2,1)S(1)} %get-tuple-element.120), channel_id=1, source_target_pairs={{12,16},{14,18},{13,20},{15,22},{28,24},{30,26},{29,28},{31,30}} | collective-permute-start | bytes 294920 | tf_op jit(solution)/shard_map/ppermute | solution.py:287
  50.7 9.8 %collective-permute-done.21 = bf16[2,64,384]{2,1,0:T(8,128)(2,1)S(1)} collective-permute-done((bf16[2,64,384]{2,1,0:T(8,128)(2,1)S(1)}, bf16[2,64,384]{2,1,0:T(8,128)(2,1)S(1)}, u32[]{:S(2)}, u32[]{:S(2)}) %collective-permute-start.21) | collective-permute-done | bytes 98336 | tf_op jit(solution)/shard_map/ppermute | solution.py:287
  (45 shorter events, 3.4 us)
Async XLA Ops:
  0.9 7.5 %collective-permute-start.3 = (bf16[2,64,384]{2,1,0:T(8,128)(2,1)S(1)}, bf16[2,64,384]{2,1,0:T(8,128)(2,1)S(1)}, u32[]{:S(2)}, u32[]{:S(2)}) collective-permute-start(bf16[2,64,384]{2,1,0:T(8,128)(2,1)S(1)} %pick.1), channel_id=1, source_target_pairs={{0,0},{1,2},{4,1},{5,3},{8,16},{9,18},{12,17},{13,19}} | collective-permute-start | bytes 294920 | tf_op jit(solution)/shard_map/ppermute | solution.py:173
  1.6 17.2 %collective-permute-start.4 = (bf16[2,64,384]{2,1,0:T(8,128)(2,1)S(1)}, bf16[2,64,384]{2,1,0:T(8,128)(2,1)S(1)}, u32[]{:S(2)}, u32[]{:S(2)}) collective-permute-start(bf16[2,64,384]{2,1,0:T(8,128)(2,1)S(1)} %pick.1), channel_id=1, source_target_pairs={{1,0},{2,2},{5,1},{6,3},{9,16},{10,18},{13,17},{14,19}} | collective-permute-start | bytes 294920 | tf_op jit(solution)/shard_map/ppermute | solution.py:173
  2.3 16.6 %collective-permute-start.5 = (bf16[2,64,384]{2,1,0:T(8,128)(2,1)S(1)}, bf16[2,64,384]{2,1,0:T(8,128)(2,1)S(1)}, u32[]{:S(2)}, u32[]{:S(2)}) collective-permute-start(bf16[2,64,384]{2,1,0:T(8,128)(2,1)S(1)} %pick.1), channel_id=1, source_target_pairs={{2,0},{3,2},{6,1},{7,3},{10,16},{11,18},{14,17},{15,19}} | collective-permute-start | bytes 294920 | tf_op jit(solution)/shard_map/ppermute | solution.py:173
  2.9 17.4 %collective-permute-start = (bf16[2,64,384]{2,1,0:T(8,128)(2,1)S(1)}, bf16[2,64,384]{2,1,0:T(8,128)(2,1)S(1)}, u32[]{:S(2)}, u32[]{:S(2)}) collective-permute-start(bf16[2,64,384]{2,1,0:T(8,128)(2,1)S(1)} %pick.1), channel_id=1, source_target_pairs={{16,0},{17,2},{20,1},{21,3},{24,16},{25,18},{28,17},{29,19}} | collective-permute-start | bytes 294920 | tf_op jit(solution)/shard_map/ppermute | solution.py:173
  3.6 16.8 %collective-permute-start.1 = (bf16[2,64,384]{2,1,0:T(8,128)(2,1)S(1)}, bf16[2,64,384]{2,1,0:T(8,128)(2,1)S(1)}, u32[]{:S(2)}, u32[]{:S(2)}) collective-permute-start(bf16[2,64,384]{2,1,0:T(8,128)(2,1)S(1)} %pick.1), channel_id=1, source_target_pairs={{17,0},{18,2},{21,1},{22,3},{25,16},{26,18},{29,17},{30,19}} | collective-permute-start | bytes 294920 | tf_op jit(solution)/shard_map/ppermute | solution.py:173
  8.4 12.0 %collective-permute-start.2 = (bf16[2,64,384]{2,1,0:T(8,128)(2,1)S(1)}, bf16[2,64,384]{2,1,0:T(8,128)(2,1)S(1)}, u32[]{:S(2)}, u32[]{:S(2)}) collective-permute-start(bf16[2,64,384]{2,1,0:T(8,128)(2,1)S(1)} %pick.1), channel_id=1, source_target_pairs={{18,0},{19,2},{22,1},{23,3},{26,16},{27,18},{30,17},{31,19}} | collective-permute-start | bytes 294920 | tf_op jit(solution)/shard_map/ppermute | solution.py:173
  18.9 2.9 %collective-permute-start.9 = (bf16[176,384]{1,0:T(8,128)(2,1)S(1)}, bf16[176,384]{1,0:T(8,128)(2,1)S(1)}, u32[]{:S(2)}, u32[]{:S(2)}) collective-permute-start(bf16[176,384]{1,0:T(8,128)(2,1)S(1)} %get-tuple-element.78), channel_id=1, source_target_pairs={{0,4},{1,5},{2,6},{3,7},{16,20},{17,21},{18,22},{19,23}} | collective-permute-start | bytes 405512 | tf_op jit(solution)/shard_map/ppermute | solution.py:272
  19.7 3.5 %collective-permute-start.8 = (bf16[176,384]{1,0:T(8,128)(2,1)S(1)}, bf16[176,384]{1,0:T(8,128)(2,1)S(1)}, u32[]{:S(2)}, u32[]{:S(2)}) collective-permute-start(bf16[176,384]{1,0:T(8,128)(2,1)S(1)} %get-tuple-element.77), channel_id=1, source_target_pairs={{0,4},{1,5},{2,6},{3,7},{16,20},{17,21},{18,22},{19,23}} | collective-permute-start | bytes 405512 | tf_op jit(solution)/shard_map/ppermute | solution.py:272
  20.4 4.3 %collective-permute-start.7 = (bf16[176,384]{1,0:T(8,128)(2,1)S(1)}, bf16[176,384]{1,0:T(8,128)(2,1)S(1)}, u32[]{:S(2)}, u32[]{:S(2)}) collective-permute-start(bf16[176,384]{1,0:T(8,128)(2,1)S(1)} %get-tuple-element.76), channel_id=1, source_target_pairs={{0,4},{1,5},{2,6},{3,7},{16,20},{17,21},{18,22},{19,23}} | collective-permute-start | bytes 405512 | tf_op jit(solution)/shard_map/ppermute | solution.py:272
  21.2 5.0 %collective-permute-start.6 = (bf16[176,384]{1,0:T(8,128)(2,1)S(1)}, bf16[176,384]{1,0:T(8,128)(2,1)S(1)}, u32[]{:S(2)}, u32[]{:S(2)}) collective-permute-start(bf16[176,384]{1,0:T(8,128)(2,1)S(1)} %frame.19), channel_id=1, source_target_pairs={{0,4},{1,5},{2,6},{3,7},{16,20},{17,21},{18,22},{19,23}} | collective-permute-start | bytes 405512 | tf_op jit(solution)/shard_map/ppermute | solution.py:272
  21.9 11.3 %collective-permute-start.13 = (bf16[160,384]{1,0:T(8,128)(2,1)S(1)}, bf16[160,384]{1,0:T(8,128)(2,1)S(1)}, u32[]{:S(2)}, u32[]{:S(2)}) collective-permute-start(bf16[160,384]{1,0:T(8,128)(2,1)S(1)} %get-tuple-element.90), channel_id=1, source_target_pairs={{4,8},{5,9},{6,10},{7,11},{20,24},{21,25},{22,26},{23,27}} | collective-permute-start | bytes 368648 | tf_op jit(solution)/shard_map/ppermute | solution.py:272
  23.2 13.8 %collective-permute-start.12 = (bf16[160,384]{1,0:T(8,128)(2,1)S(1)}, bf16[160,384]{1,0:T(8,128)(2,1)S(1)}, u32[]{:S(2)}, u32[]{:S(2)}) collective-permute-start(bf16[160,384]{1,0:T(8,128)(2,1)S(1)} %get-tuple-element.89), channel_id=1, source_target_pairs={{4,8},{5,9},{6,10},{7,11},{20,24},{21,25},{22,26},{23,27}} | collective-permute-start | bytes 368648 | tf_op jit(solution)/shard_map/ppermute | solution.py:272
  24.8 15.8 %collective-permute-start.11 = (bf16[160,384]{1,0:T(8,128)(2,1)S(1)}, bf16[160,384]{1,0:T(8,128)(2,1)S(1)}, u32[]{:S(2)}, u32[]{:S(2)}) collective-permute-start(bf16[160,384]{1,0:T(8,128)(2,1)S(1)} %get-tuple-element.88), channel_id=1, source_target_pairs={{4,8},{5,9},{6,10},{7,11},{20,24},{21,25},{22,26},{23,27}} | collective-permute-start | bytes 368648 | tf_op jit(solution)/shard_map/ppermute | solution.py:272
  26.2 17.9 %collective-permute-start.10 = (bf16[160,384]{1,0:T(8,128)(2,1)S(1)}, bf16[160,384]{1,0:T(8,128)(2,1)S(1)}, u32[]{:S(2)}, u32[]{:S(2)}) collective-permute-start(bf16[160,384]{1,0:T(8,128)(2,1)S(1)} %frame.23), channel_id=1, source_target_pairs={{4,8},{5,9},{6,10},{7,11},{20,24},{21,25},{22,26},{23,27}} | collective-permute-start | bytes 368648 | tf_op jit(solution)/shard_map/ppermute | solution.py:272
  34.2 12.1 %collective-permute-start.17 = (bf16[144,384]{1,0:T(8,128)(2,1)S(1)}, bf16[144,384]{1,0:T(8,128)(2,1)S(1)}, u32[]{:S(2)}, u32[]{:S(2)}) collective-permute-start(bf16[144,384]{1,0:T(8,128)(2,1)S(1)} %get-tuple-element.102), channel_id=1, source_target_pairs={{8,12},{9,13},{10,14},{11,15},{24,28},{25,29},{26,30},{27,31}} | collective-permute-start | bytes 331784 | tf_op jit(solution)/shard_map/ppermute | solution.py:272
  38.0 8.6 %collective-permute-start.16 = (bf16[144,384]{1,0:T(8,128)(2,1)S(1)}, bf16[144,384]{1,0:T(8,128)(2,1)S(1)}, u32[]{:S(2)}, u32[]{:S(2)}) collective-permute-start(bf16[144,384]{1,0:T(8,128)(2,1)S(1)} %get-tuple-element.101), channel_id=1, source_target_pairs={{8,12},{9,13},{10,14},{11,15},{24,28},{25,29},{26,30},{27,31}} | collective-permute-start | bytes 331784 | tf_op jit(solution)/shard_map/ppermute | solution.py:272
  41.6 5.1 %collective-permute-start.15 = (bf16[144,384]{1,0:T(8,128)(2,1)S(1)}, bf16[144,384]{1,0:T(8,128)(2,1)S(1)}, u32[]{:S(2)}, u32[]{:S(2)}) collective-permute-start(bf16[144,384]{1,0:T(8,128)(2,1)S(1)} %get-tuple-element.100), channel_id=1, source_target_pairs={{8,12},{9,13},{10,14},{11,15},{24,28},{25,29},{26,30},{27,31}} | collective-permute-start | bytes 331784 | tf_op jit(solution)/shard_map/ppermute | solution.py:272
  45.1 3.6 %collective-permute-start.14 = (bf16[144,384]{1,0:T(8,128)(2,1)S(1)}, bf16[144,384]{1,0:T(8,128)(2,1)S(1)}, u32[]{:S(2)}, u32[]{:S(2)}) collective-permute-start(bf16[144,384]{1,0:T(8,128)(2,1)S(1)} %frame.27), channel_id=1, source_target_pairs={{8,12},{9,13},{10,14},{11,15},{24,28},{25,29},{26,30},{27,31}} | collective-permute-start | bytes 331784 | tf_op jit(solution)/shard_map/ppermute | solution.py:272
  46.8 1.9 %collective-permute-start.19 = (bf16[2,64,384]{2,1,0:T(8,128)(2,1)S(1)}, bf16[2,64,384]{2,1,0:T(8,128)(2,1)S(1)}, u32[]{:S(2)}, u32[]{:S(2)}) collective-permute-start(bf16[2,64,384]{2,1,0:T(8,128)(2,1)S(1)} %get-tuple-element.118), channel_id=1, source_target_pairs={{12,1},{14,3},{13,5},{15,7},{28,9},{30,11},{29,13},{31,15}} | collective-permute-start | bytes 294920 | tf_op jit(solution)/shard_map/ppermute | solution.py:287
  47.4 1.2 %collective-permute-start.18 = (bf16[2,64,384]{2,1,0:T(8,128)(2,1)S(1)}, bf16[2,64,384]{2,1,0:T(8,128)(2,1)S(1)}, u32[]{:S(2)}, u32[]{:S(2)}) collective-permute-start(bf16[2,64,384]{2,1,0:T(8,128)(2,1)S(1)} %get-tuple-element.117), channel_id=1, source_target_pairs={{12,0},{14,2},{13,4},{15,6},{28,8},{30,10},{29,12},{31,14}} | collective-permute-start | bytes 294920 | tf_op jit(solution)/shard_map/ppermute | solution.py:287
  48.7 2.0 %collective-permute-start.20 = (bf16[2,64,384]{2,1,0:T(8,128)(2,1)S(1)}, bf16[2,64,384]{2,1,0:T(8,128)(2,1)S(1)}, u32[]{:S(2)}, u32[]{:S(2)}) collective-permute-start(bf16[2,64,384]{2,1,0:T(8,128)(2,1)S(1)} %get-tuple-element.119), channel_id=1, source_target_pairs={{12,17},{14,19},{13,21},{15,23},{28,25},{30,27},{29,29},{31,31}} | collective-permute-start | bytes 294920 | tf_op jit(solution)/shard_map/ppermute | solution.py:287
  49.3 11.1 %collective-permute-start.21 = (bf16[2,64,384]{2,1,0:T(8,128)(2,1)S(1)}, bf16[2,64,384]{2,1,0:T(8,128)(2,1)S(1)}, u32[]{:S(2)}, u32[]{:S(2)}) collective-permute-start(bf16[2,64,384]{2,1,0:T(8,128)(2,1)S(1)} %get-tuple-element.120), channel_id=1, source_target_pairs={{12,16},{14,18},{13,20},{15,22},{28,24},{30,26},{29,28},{31,30}} | collective-permute-start | bytes 294920 | tf_op jit(solution)/shard_map/ppermute | solution.py:287

commit v5 on v4

--- a/solution.py
+++ b/solution.py
@@ -37,10 +37,18 @@
     return pl.ds(pl.multiple_of(start * cols, cols), count * cols)
 
 
-def pick_kernel(source, target, sem):
-    copy = pltpu.make_async_copy(source.at[lax.axis_index("segment")], target, sem)
-    copy.start()
-    copy.wait()
+def pick_kernel(per_half, holders, source, mine, own, other, sems):
+    side = lax.axis_index("tm") & (holders - 1)
+    lane = lax.axis_index("band") & (per_half - 1)
+    clips = (lax.axis_index("segment"), side * per_half + lane, (holders - 1 - side) * per_half + lane)
+    copies = [
+        pltpu.make_async_copy(source.at[clip], target, sems.at[number])
+        for number, (clip, target) in enumerate(zip(clips, (mine, own, other)))
+    ]
+    for copy in copies:
+        copy.start()
+    for copy in copies:
+        copy.wait()
 
 
 def loader_kernel(weight, bias, gain, now, past, bias_out, gain_out, sems):
@@ -61,7 +69,7 @@
 
 def frame_kernel(cfg, *refs):
     refs = list(refs)
-    pieces = [refs.pop(0) for _ in range(cfg["pieces"])]
+    groups = [[refs.pop(0) for _ in range(TAPS)] for _ in range(cfg["groups"])]
     received = refs.pop(0) if cfg["came"] is not None else None
     partial, weight, bias, gain = refs[:4]
     refs = refs[4:]
@@ -80,8 +88,18 @@
         size = have * cols
         if unit == 0:
             step = entry.shape[0] // TAPS
-            for number, piece in enumerate(pieces):
-                entry[pl.ds(number * step, step), :] = piece[cfg["piece_at"]]
+
+            def place(group):
+                for piece, code in zip(group, cfg["places"]):
+                    number = (code >> (2 * lax.axis_index("band"))) & 3
+                    entry[pl.ds(pl.multiple_of(number * step, step), step), :] = piece[cfg["piece_at"]]
+
+            if len(groups) == 1:
+                place(groups[0])
+            else:
+                near = lax.axis_index("tm") == cfg["time"]
+                pl.when(near)(functools.partial(place, groups[0]))
+                pl.when(jnp.logical_not(near))(functools.partial(place, groups[1]))
             source, skip = entry, 0
         else:
             source, skip = received, half * (unit - 1 - cfg["came"])
@@ -152,26 +170,38 @@
     def spot(t, s, b):
         return (t * segments + s) * bands + b
 
-    mine = pl.pallas_call(
-        pick_kernel,
-        out_shape=pltpu.VMEM((own_frames, piece, channels), features.dtype),
+    mine, own, other = pl.pallas_call(
+        functools.partial(pick_kernel, per_half, holders),
+        out_shape=[pltpu.VMEM((own_frames, piece, channels), features.dtype)] * 3,
         in_specs=[whole(pltpu.HBM)],
-        out_specs=whole(),
-        scratch_shapes=[pltpu.SemaphoreType.DMA],
+        out_specs=[whole()] * 3,
+        scratch_shapes=[pltpu.SemaphoreType.DMA((3,))],
         compiler_params=pltpu.CompilerParams(vmem_limit_bytes=1 << 20),
         name="pick",
     )(pltpu.with_memory_space_constraint(features.reshape(clips, own_frames, piece, channels), pltpu.HBM))
-    entries = []
-    for t in range(times):
-        group = []
-        for number in range(TAPS):
-            routes = []
-            for clip in range(clips):
-                for h in range(HALVES):
-                    there, at = stream(clip, h)
-                    routes.append((spot(t, clip, h + number), spot(there, 0, at)))
-            group.append(lax.ppermute(mine, MESH_AXES, routes))
-        entries.append(group)
+    wanted = [[2 * h + j for h in range(HALVES) for j in range(per_half)], [1, 0, 3, 2], [2, 2, 1, 1]]
+    places = [sum((b - at // per_half) << (2 * at) for at, b in enumerate(row)) for row in wanted]
+
+    def gather(value, number, members):
+        routes = []
+        for t, clip in members:
+            for h in range(HALVES):
+                there, at = stream(clip, h)
+                segment = clip if value is mine else 0
+                routes.append((spot(t, segment, wanted[number][at]), spot(there, 0, at)))
+        assert len({a for a, _ in routes}) == len({b for _, b in routes}) == len(routes)
+        return lax.ppermute(value, MESH_AXES, routes)
+
+    sides = [(t, clip) for t in range(holders) for clip in range(clips)]
+    beside = [(t, clip) for t, clip in sides if clip // per_half == t]
+    across = [(t, clip) for t, clip in sides if clip // per_half != t]
+    far_group = [gather(mine, number, across) for number in (1, 2)]
+    near_group = [gather(mine, number, beside) for number in (1, 2)]
+    far_group = [gather(other, 0, across)] + far_group
+    near_group = [own] + near_group
+    entries = [[near_group, far_group]] * holders
+    for t in range(holders, times):
+        entries.append([[gather(mine, number, [(t, clip) for clip in range(clips)]) for number in range(TAPS)]])
 
     stored = [conv_weight[0].reshape(TAPS, TAPS, TAPS * channels, channels), conv_bias, norm_gain]
     now, past, bias, gain = pl.pallas_call(
@@ -210,8 +240,10 @@
             later=[s for s in units if slot - lag * s < frames - 1],
             sends=bool(senders_now),
             lowest=min(senders_now, default=0),
-            pieces=TAPS if slot < frames else 0,
+            groups=len(entries[slot // own_frames]) if slot < frames else 0,
+            places=places,
             piece_at=slot % own_frames,
+            time=slot // own_frames,
             came=min(working(slot - lag, frames, segments, lag)) if slot >= lag else None,
             finals=finals,
             tail_at=last % own_frames,
@@ -224,7 +256,7 @@
         )
         operands = []
         if slot < frames:
-            operands += [resident(value) for value in entries[slot // own_frames]]
+            operands += [resident(value) for group in entries[slot // own_frames] for value in group]
         if slot >= lag:
             operands.append(resident(moving.pop(slot - lag)))
         operands += [resident(near), now, bias, gain]
@@ -273,11 +305,7 @@
         if finals and last % own_frames == own_frames - 1:
             there = last // own_frames
             ready = [(there, index, value) for index, value in enumerate(tails)]
-            if there == times - 1:
-                leaving += ready
-            else:
-                leaving.append(ready[0])
-                held = ready[1:]
+            leaving += ready
         for there, index, value in leaving:
             routes = []
             for clip in range(clips):

time: 61.5 us -> 59 us (0.959)
  the two profiles are of different devices: /device:TPU:22 before, /device:TPU:18 now
where the time goes in v5:
time: 59 us; the launch traced here: 58.3 us
  waiting for transfers between devices  25 us (42%)
  starting transfers between devices  19.6 us (33%)
  Pallas kernels  12.4 us (21%)
  other arithmetic  0.66 us (1%)
    ppermute x12, waiting for transfers between devices, local(): lax.ppermute(out, 'segment', [(s, s + 1) for s in senders_now])  14.5 us
    ppermute x12, starting transfers between devices, local(): lax.ppermute(out, 'segment', [(s, s + 1) for s in senders_now])  13 us
    ppermute x4, waiting for transfers between devices, local(): landed[there, index] = lax.ppermute(value, MESH_AXES, routes)  10.5 us
    pallas_call x16, Pallas kernels, local(): pl.pallas_call(functools.partial(frame_kernel, cfg), out_shape=shapes, in...  4.22 us
    pallas_call x12, Pallas kernels, local(): pl.pallas_call(functools.partial(history_kernel, cfg), out_shape=[pltpu.V...  3.82 us
    pallas_call x1, Pallas kernels, local(): pl.pallas_call(loader_kernel, out_shape=[pltpu.VMEM((TAPS, TAPS * channel...  3.38 us
    ppermute x5, starting transfers between devices, gather(): return lax.ppermute(value, MESH_AXES, routes)  3.33 us
    ppermute x4, starting transfers between devices, local(): landed[there, index] = lax.ppermute(value, MESH_AXES, routes)  3.28 us
  transfers between devices with their start and end apart: 21, of which 6 were waited for; matrix products, arithmetic and copies ran while one was open for 0% of the time, Pallas kernels for 20%

profile of v5, /device:TPU:18, one launch (start us, length us, event | category | flops | bytes accessed | tf_op | source)
XLA Modules:
  0.0 58.3 jit_solution(3510463853433840296)
XLA Ops:
  0.0 1.0 %pick.1 = (bf16[2,64,384]{2,1,0:T(8,128)(2,1)S(1)}, bf16[2,64,384]{2,1,0:T(8,128)(2,1)S(1)}, bf16[2,64,384]{2,1,0:T(8,128)(2,1)S(1)}) custom-call(bf16[4,2,64,384]{3,2,1,0:T(8,128)(2,1)} %bitcast.4), custom_call_target="tpu_custom_call" | custom-call | tf_op jit(solution)/shard_map/pick/pallas_call | solution.py:173
  1.0 0.7 %collective-permute-start = (bf16[2,64,384]{2,1,0:T(8,128)(2,1)S(1)}, bf16[2,64,384]{2,1,0:T(8,128)(2,1)S(1)}, u32[]{:S(2)}, u32[]{:S(2)}) collective-permute-start(bf16[2,64,384]{2,1,0:T(8,128)(2,1)S(1)} %get-tuple-element.67), channel_id=1, source_target_pairs={{1,0},{3,2},{4,1},{6,3},{25,16},{27,18},{28,17},{30,19}} | collective-permute-start | bytes 294920 | tf_op jit(solution)/shard_map/ppermute | solution.py:193
  1.7 0.7 %collective-permute-start.1 = (bf16[2,64,384]{2,1,0:T(8,128)(2,1)S(1)}, bf16[2,64,384]{2,1,0:T(8,128)(2,1)S(1)}, u32[]{:S(2)}, u32[]{:S(2)}) collective-permute-start(bf16[2,64,384]{2,1,0:T(8,128)(2,1)S(1)} %get-tuple-element.67), channel_id=1, source_target_pairs={{2,0},{1,2},{6,1},{5,3},{26,16},{25,18},{30,17},{29,19}} | collective-permute-start | bytes 294920 | tf_op jit(solution)/shard_map/ppermute | solution.py:193
  2.4 0.7 %collective-permute-start.3 = (bf16[2,64,384]{2,1,0:T(8,128)(2,1)S(1)}, bf16[2,64,384]{2,1,0:T(8,128)(2,1)S(1)}, u32[]{:S(2)}, u32[]{:S(2)}) collective-permute-start(bf16[2,64,384]{2,1,0:T(8,128)(2,1)S(1)} %get-tuple-element.67), channel_id=1, source_target_pairs={{9,16},{11,18},{12,17},{14,19},{17,0},{19,2},{20,1},{22,3}} | collective-permute-start | bytes 294920 | tf_op jit(solution)/shard_map/ppermute | solution.py:193
  3.0 0.7 %collective-permute-start.4 = (bf16[2,64,384]{2,1,0:T(8,128)(2,1)S(1)}, bf16[2,64,384]{2,1,0:T(8,128)(2,1)S(1)}, u32[]{:S(2)}, u32[]{:S(2)}) collective-permute-start(bf16[2,64,384]{2,1,0:T(8,128)(2,1)S(1)} %get-tuple-element.67), channel_id=1, source_target_pairs={{10,16},{9,18},{14,17},{13,19},{18,0},{17,2},{22,1},{21,3}} | collective-permute-start | bytes 294920 | tf_op jit(solution)/shard_map/ppermute | solution.py:193
  3.7 0.7 %collective-permute-start.2 = (bf16[2,64,384]{2,1,0:T(8,128)(2,1)S(1)}, bf16[2,64,384]{2,1,0:T(8,128)(2,1)S(1)}, u32[]{:S(2)}, u32[]{:S(2)}) collective-permute-start(bf16[2,64,384]{2,1,0:T(8,128)(2,1)S(1)} %get-tuple-element.68), channel_id=1, source_target_pairs={{0,16},{2,18},{1,17},{3,19},{16,0},{18,2},{17,1},{19,3}} | collective-permute-start | bytes 294920 | tf_op jit(solution)/shard_map/ppermute | solution.py:193
  4.4 3.4 %loader.1 = (bf16[3,1152,384]{2,1,0:T(8,128)(2,1)S(1)}, bf16[3,1152,768]{2,1,0:T(8,128)(2,1)S(1)}, f32[1,384]{1,0:T(1,128)S(1)}, f32[1,384]{1,0:T(1,128)S(1)}) custom-call(bf16[3,3,1152,384]{3,2,1,0:T(8,128)(2,1)} %bitcast.3, f32[1,384]{1,0:T(1,128)} %bias.1, f32[1,384]{1,0:T(1,128)} %gain.1), custom_call_target="tpu_custom_call" | custom-call | tf_op jit(solution)/shard_map/loader/pallas_call | solution.py:207
  7.9 0.7 %collective-permute-start.8 = (bf16[176,384]{1,0:T(8,128)(2,1)S(1)}, bf16[176,384]{1,0:T(8,128)(2,1)S(1)}, u32[]{:S(2)}, u32[]{:S(2)}) collective-permute-start(bf16[176,384]{1,0:T(8,128)(2,1)S(1)} %get-tuple-element.83), channel_id=1, source_target_pairs={{0,4},{1,5},{2,6},{3,7},{16,20},{17,21},{18,22},{19,23}} | collective-permute-start | bytes 405512 | tf_op jit(solution)/shard_map/ppermute | solution.py:304
  8.7 0.7 %collective-permute-start.7 = (bf16[176,384]{1,0:T(8,128)(2,1)S(1)}, bf16[176,384]{1,0:T(8,128)(2,1)S(1)}, u32[]{:S(2)}, u32[]{:S(2)}) collective-permute-start(bf16[176,384]{1,0:T(8,128)(2,1)S(1)} %get-tuple-element.82), channel_id=1, source_target_pairs={{0,4},{1,5},{2,6},{3,7},{16,20},{17,21},{18,22},{19,23}} | collective-permute-start | bytes 405512 | tf_op jit(solution)/shard_map/ppermute | solution.py:304
  9.4 0.7 %collective-permute-start.6 = (bf16[176,384]{1,0:T(8,128)(2,1)S(1)}, bf16[176,384]{1,0:T(8,128)(2,1)S(1)}, u32[]{:S(2)}, u32[]{:S(2)}) collective-permute-start(bf16[176,384]{1,0:T(8,128)(2,1)S(1)} %get-tuple-element.81), channel_id=1, source_target_pairs={{0,4},{1,5},{2,6},{3,7},{16,20},{17,21},{18,22},{19,23}} | collective-permute-start | bytes 405512 | tf_op jit(solution)/shard_map/ppermute | solution.py:304
  10.1 0.7 %collective-permute-start.5 = (bf16[176,384]{1,0:T(8,128)(2,1)S(1)}, bf16[176,384]{1,0:T(8,128)(2,1)S(1)}, u32[]{:S(2)}, u32[]{:S(2)}) collective-permute-start(bf16[176,384]{1,0:T(8,128)(2,1)S(1)} %frame.19), channel_id=1, source_target_pairs={{0,4},{1,5},{2,6},{3,7},{16,20},{17,21},{18,22},{19,23}} | collective-permute-start | bytes 405512 | tf_op jit(solution)/shard_map/ppermute | solution.py:304
  10.8 1.3 %collective-permute-start.12 = (bf16[160,384]{1,0:T(8,128)(2,1)S(1)}, bf16[160,384]{1,0:T(8,128)(2,1)S(1)}, u32[]{:S(2)}, u32[]{:S(2)}) collective-permute-start(bf16[160,384]{1,0:T(8,128)(2,1)S(1)} %get-tuple-element.95), channel_id=1, source_target_pairs={{4,8},{5,9},{6,10},{7,11},{20,24},{21,25},{22,26},{23,27}} | collective-permute-start | bytes 368648 | tf_op jit(solution)/shard_map/ppermute | solution.py:304
  12.2 1.3 %collective-permute-start.11 = (bf16[160,384]{1,0:T(8,128)(2,1)S(1)}, bf16[160,384]{1,0:T(8,128)(2,1)S(1)}, u32[]{:S(2)}, u32[]{:S(2)}) collective-permute-start(bf16[160,384]{1,0:T(8,128)(2,1)S(1)} %get-tuple-element.94), channel_id=1, source_target_pairs={{4,8},{5,9},{6,10},{7,11},{20,24},{21,25},{22,26},{23,27}} | collective-permute-start | bytes 368648 | tf_op jit(solution)/shard_map/ppermute | solution.py:304
  13.8 1.3 %collective-permute-start.10 = (bf16[160,384]{1,0:T(8,128)(2,1)S(1)}, bf16[160,384]{1,0:T(8,128)(2,1)S(1)}, u32[]{:S(2)}, u32[]{:S(2)}) collective-permute-start(bf16[160,384]{1,0:T(8,128)(2,1)S(1)} %get-tuple-element.93), channel_id=1, source_target_pairs={{4,8},{5,9},{6,10},{7,11},{20,24},{21,25},{22,26},{23,27}} | collective-permute-start | bytes 368648 | tf_op jit(solution)/shard_map/ppermute | solution.py:304
  15.1 1.3 %collective-permute-start.9 = (bf16[160,384]{1,0:T(8,128)(2,1)S(1)}, bf16[160,384]{1,0:T(8,128)(2,1)S(1)}, u32[]{:S(2)}, u32[]{:S(2)}) collective-permute-start(bf16[160,384]{1,0:T(8,128)(2,1)S(1)} %frame.23), channel_id=1, source_target_pairs={{4,8},{5,9},{6,10},{7,11},{20,24},{21,25},{22,26},{23,27}} | collective-permute-start | bytes 368648 | tf_op jit(solution)/shard_map/ppermute | solution.py:304
  16.4 12.7 %collective-permute-done.12.refs_0_ = bf16[160,384]{1,0:T(8,128)(2,1)S(1)} collective-permute-done((bf16[160,384]{1,0:T(8,128)(2,1)S(1)}, bf16[160,384]{1,0:T(8,128)(2,1)S(1)}, u32[]{:S(2)}, u32[]{:S(2)}) %collective-permute-start.12) | collective-permute-done | bytes 122912 | tf_op jit(solution)/shard_map/ppermute | solution.py:304
  29.1 1.0 %frame.24 = (bf16[144,384]{1,0:T(8,128)(2,1)S(1)}, bf16[224,1152]{1,0:T(8,128)(2,1)S(1)}) custom-call(bf16[160,384]{1,0:T(8,128)(2,1)S(1)} %collective-permute-done.12.refs_0_, f32[176,384]{1,0:T(8,128)S(1)} %get-tuple-element.92.refs_1_.near, bf16[3,1152,384]{2,1,0:T(8,128)(2,1)S(1)} %get-tuple-element.69.refs_7_.refs_2_, ...), custom_call_target="tpu_custom_call" | custom-call | bytes 1024 | tf_op jit(solution)/shard_map/frame/pallas_call | solution.py:283
  30.1 1.3 %collective-permute-start.16 = (bf16[144,384]{1,0:T(8,128)(2,1)S(1)}, bf16[144,384]{1,0:T(8,128)(2,1)S(1)}, u32[]{:S(2)}, u32[]{:S(2)}) collective-permute-start(bf16[144,384]{1,0:T(8,128)(2,1)S(1)} %get-tuple-element.107), channel_id=1, source_target_pairs={{8,12},{9,13},{10,14},{11,15},{24,28},{25,29},{26,30},{27,31}} | collective-permute-start | bytes 331784 | tf_op jit(solution)/shard_map/ppermute | solution.py:304
  31.4 1.1 %history.18 = (f32[176,384]{1,0:T(8,128)S(1)}, f32[176,384]{1,0:T(8,128)S(1)}) custom-call(bf16[224,1152]{1,0:T(8,128)(2,1)S(1)} %get-tuple-element.96.spread, f32[176,384]{1,0:T(8,128)S(1)} %get-tuple-element.92.refs_1_.near, f32[176,384]{1,0:T(8,128)S(1)} %get-tuple-element.97.far, ...), custom_call_target="tpu_custom_call", output_to_operand_aliasing={{0}: (1, {}), {1}: (2, {})} | custom-call | bytes 1024 | tf_op jit(solution)/shard_map/history/pallas_call | solution.py:317
  32.9 1.0 %frame.25 = (bf16[144,384]{1,0:T(8,128)(2,1)S(1)}, bf16[224,1152]{1,0:T(8,128)(2,1)S(1)}) custom-call(bf16[160,384]{1,0:T(8,128)(2,1)S(1)} %collective-permute-done.11.refs_0_, f32[176,384]{1,0:T(8,128)S(1)} %get-tuple-element.98.refs_1_.near, bf16[3,1152,384]{2,1,0:T(8,128)(2,1)S(1)} %get-tuple-element.69.refs_7_.refs_2_, ...), custom_call_target="tpu_custom_call" | custom-call | bytes 1024 | tf_op jit(solution)/shard_map/frame/pallas_call | solution.py:283
  33.9 1.3 %collective-permute-start.15 = (bf16[144,384]{1,0:T(8,128)(2,1)S(1)}, bf16[144,384]{1,0:T(8,128)(2,1)S(1)}, u32[]{:S(2)}, u32[]{:S(2)}) collective-permute-start(bf16[144,384]{1,0:T(8,128)(2,1)S(1)} %get-tuple-element.106), channel_id=1, source_target_pairs={{8,12},{9,13},{10,14},{11,15},{24,28},{25,29},{26,30},{27,31}} | collective-permute-start | bytes 331784 | tf_op jit(solution)/shard_map/ppermute | solution.py:304
  35.2 1.1 %history.19 = (f32[176,384]{1,0:T(8,128)S(1)}, f32[176,384]{1,0:T(8,128)S(1)}) custom-call(bf16[224,1152]{1,0:T(8,128)(2,1)S(1)} %get-tuple-element.99.spread, f32[176,384]{1,0:T(8,128)S(1)} %get-tuple-element.98.refs_1_.near, f32[176,384]{1,0:T(8,128)S(1)} %get-tuple-element.100.far, ...), custom_call_target="tpu_custom_call", output_to_operand_aliasing={{0}: (1, {}), {1}: (2, {})} | custom-call | bytes 1024 | tf_op jit(solution)/shard_map/history/pallas_call | solution.py:317
  36.7 1.0 %frame.26 = (bf16[144,384]{1,0:T(8,128)(2,1)S(1)}, bf16[224,1152]{1,0:T(8,128)(2,1)S(1)}) custom-call(bf16[160,384]{1,0:T(8,128)(2,1)S(1)} %collective-permute-done.10.refs_0_, f32[176,384]{1,0:T(8,128)S(1)} %get-tuple-element.101.refs_1_.near, bf16[3,1152,384]{2,1,0:T(8,128)(2,1)S(1)} %get-tuple-element.69.refs_7_.refs_2_, ...), custom_call_target="tpu_custom_call" | custom-call | bytes 1024 | tf_op jit(solution)/shard_map/frame/pallas_call | solution.py:283
  37.7 1.3 %collective-permute-start.14 = (bf16[144,384]{1,0:T(8,128)(2,1)S(1)}, bf16[144,384]{1,0:T(8,128)(2,1)S(1)}, u32[]{:S(2)}, u32[]{:S(2)}) collective-permute-start(bf16[144,384]{1,0:T(8,128)(2,1)S(1)} %get-tuple-element.105), channel_id=1, source_target_pairs={{8,12},{9,13},{10,14},{11,15},{24,28},{25,29},{26,30},{27,31}} | collective-permute-start | bytes 331784 | tf_op jit(solution)/shard_map/ppermute | solution.py:304
  39.0 1.1 %history.20 = (f32[176,384]{1,0:T(8,128)S(1)}, f32[176,384]{1,0:T(8,128)S(1)}) custom-call(bf16[224,1152]{1,0:T(8,128)(2,1)S(1)} %get-tuple-element.102.spread, f32[176,384]{1,0:T(8,128)S(1)} %get-tuple-element.101.refs_1_.near, f32[176,384]{1,0:T(8,128)S(1)} %get-tuple-element.103.far, ...), custom_call_target="tpu_custom_call", output_to_operand_aliasing={{0}: (1, {}), {1}: (2, {})} | custom-call | bytes 1024 | tf_op jit(solution)/shard_map/history/pallas_call | solution.py:317
  40.5 1.0 %frame.27 = bf16[144,384]{1,0:T(8,128)(2,1)S(1)} custom-call(bf16[160,384]{1,0:T(8,128)(2,1)S(1)} %collective-permute-done.9.refs_0_, f32[176,384]{1,0:T(8,128)S(1)} %get-tuple-element.104.refs_1_.near, bf16[3,1152,384]{2,1,0:T(8,128)(2,1)S(1)} %get-tuple-element.69.refs_7_.refs_2_, f32[1,384]{1,0:T(1,128)S(1)} %get-tuple-element.70.refs_8_.refs_3_, ...), custom_call_target="tpu_custom_call" | custom-call | bytes 1024 | tf_op jit(solution)/shard_map/frame/pallas_call | solution.py:283
  41.5 1.3 %collective-permute-start.13 = (bf16[144,384]{1,0:T(8,128)(2,1)S(1)}, bf16[144,384]{1,0:T(8,128)(2,1)S(1)}, u32[]{:S(2)}, u32[]{:S(2)}) collective-permute-start(bf16[144,384]{1,0:T(8,128)(2,1)S(1)} %frame.27), channel_id=1, source_target_pairs={{8,12},{9,13},{10,14},{11,15},{24,28},{25,29},{26,30},{27,31}} | collective-permute-start | bytes 331784 | tf_op jit(solution)/shard_map/ppermute | solution.py:304
  43.2 0.7 %collective-permute-start.17 = (bf16[2,64,384]{2,1,0:T(8,128)(2,1)S(1)}, bf16[2,64,384]{2,1,0:T(8,128)(2,1)S(1)}, u32[]{:S(2)}, u32[]{:S(2)}) collective-permute-start(bf16[2,64,384]{2,1,0:T(8,128)(2,1)S(1)} %get-tuple-element.121), channel_id=1, source_target_pairs={{12,0},{14,2},{13,4},{15,6},{28,8},{30,10},{29,12},{31,14}} | collective-permute-start | bytes 294920 | tf_op jit(solution)/shard_map/ppermute | solution.py:315
  43.8 0.7 %collective-permute-start.18 = (bf16[2,64,384]{2,1,0:T(8,128)(2,1)S(1)}, bf16[2,64,384]{2,1,0:T(8,128)(2,1)S(1)}, u32[]{:S(2)}, u32[]{:S(2)}) collective-permute-start(bf16[2,64,384]{2,1,0:T(8,128)(2,1)S(1)} %get-tuple-element.122), channel_id=1, source_target_pairs={{12,1},{14,3},{13,5},{15,7},{28,9},{30,11},{29,13},{31,15}} | collective-permute-start | bytes 294920 | tf_op jit(solution)/shard_map/ppermute | solution.py:315
  45.8 1.3 %collective-permute-start.20 = (bf16[2,64,384]{2,1,0:T(8,128)(2,1)S(1)}, bf16[2,64,384]{2,1,0:T(8,128)(2,1)S(1)}, u32[]{:S(2)}, u32[]{:S(2)}) collective-permute-start(bf16[2,64,384]{2,1,0:T(8,128)(2,1)S(1)} %get-tuple-element.124), channel_id=1, source_target_pairs={{12,16},{14,18},{13,20},{15,22},{28,24},{30,26},{29,28},{31,30}} | collective-permute-start | bytes 294920 | tf_op jit(solution)/shard_map/ppermute | solution.py:315
  47.1 10.5 %collective-permute-done.20 = bf16[2,64,384]{2,1,0:T(8,128)(2,1)S(1)} collective-permute-done((bf16[2,64,384]{2,1,0:T(8,128)(2,1)S(1)}, bf16[2,64,384]{2,1,0:T(8,128)(2,1)S(1)}, u32[]{:S(2)}, u32[]{:S(2)}) %collective-permute-start.20) | collective-permute-done | bytes 98336 | tf_op jit(solution)/shard_map/ppermute | solution.py:315
  57.6 0.7 %select_select_fusion = bf16[2,64,384]{2,1,0:T(8,128)(2,1)} fusion(bf16[2,64,384]{2,1,0:T(8,128)(2,1)S(1)} %collective-permute-done.19, bf16[2,64,384]{2,1,0:T(8,128)(2,1)S(1)} %collective-permute-done.20, bf16[2,64,384]{2,1,0:T(8,128)(2,1)S(1)} %get-tuple-element.125, bf16[2,64,384]{2,1,0:T(8,128)(2,1)S(1)} %get-tuple-element.126, pred[]{:T(512)S(6)} %and.21, ...), kind=kLoop, calls=%fused_computation | loop fusion | flops 147456 | bytes 491523 | tf_op jit(solution)/shard_map/jit(_where)/select_n | solution.py:331
  (43 shorter events, 3.3 us)
Async XLA Ops:
  1.0 6.8 %collective-permute-start = (bf16[2,64,384]{2,1,0:T(8,128)(2,1)S(1)}, bf16[2,64,384]{2,1,0:T(8,128)(2,1)S(1)}, u32[]{:S(2)}, u32[]{:S(2)}) collective-permute-start(bf16[2,64,384]{2,1,0:T(8,128)(2,1)S(1)} %get-tuple-element.67), channel_id=1, source_target_pairs={{1,0},{3,2},{4,1},{6,3},{25,16},{27,18},{28,17},{30,19}} | collective-permute-start | bytes 294920 | tf_op jit(solution)/shard_map/ppermute | solution.py:193
  1.7 6.1 %collective-permute-start.1 = (bf16[2,64,384]{2,1,0:T(8,128)(2,1)S(1)}, bf16[2,64,384]{2,1,0:T(8,128)(2,1)S(1)}, u32[]{:S(2)}, u32[]{:S(2)}) collective-permute-start(bf16[2,64,384]{2,1,0:T(8,128)(2,1)S(1)} %get-tuple-element.67), channel_id=1, source_target_pairs={{2,0},{1,2},{6,1},{5,3},{26,16},{25,18},{30,17},{29,19}} | collective-permute-start | bytes 294920 | tf_op jit(solution)/shard_map/ppermute | solution.py:193
  2.4 5.4 %collective-permute-start.3 = (bf16[2,64,384]{2,1,0:T(8,128)(2,1)S(1)}, bf16[2,64,384]{2,1,0:T(8,128)(2,1)S(1)}, u32[]{:S(2)}, u32[]{:S(2)}) collective-permute-start(bf16[2,64,384]{2,1,0:T(8,128)(2,1)S(1)} %get-tuple-element.67), channel_id=1, source_target_pairs={{9,16},{11,18},{12,17},{14,19},{17,0},{19,2},{20,1},{22,3}} | collective-permute-start | bytes 294920 | tf_op jit(solution)/shard_map/ppermute | solution.py:193
  3.0 4.8 %collective-permute-start.4 = (bf16[2,64,384]{2,1,0:T(8,128)(2,1)S(1)}, bf16[2,64,384]{2,1,0:T(8,128)(2,1)S(1)}, u32[]{:S(2)}, u32[]{:S(2)}) collective-permute-start(bf16[2,64,384]{2,1,0:T(8,128)(2,1)S(1)} %get-tuple-element.67), channel_id=1, source_target_pairs={{10,16},{9,18},{14,17},{13,19},{18,0},{17,2},{22,1},{21,3}} | collective-permute-start | bytes 294920 | tf_op jit(solution)/shard_map/ppermute | solution.py:193
  3.7 4.1 %collective-permute-start.2 = (bf16[2,64,384]{2,1,0:T(8,128)(2,1)S(1)}, bf16[2,64,384]{2,1,0:T(8,128)(2,1)S(1)}, u32[]{:S(2)}, u32[]{:S(2)}) collective-permute-start(bf16[2,64,384]{2,1,0:T(8,128)(2,1)S(1)} %get-tuple-element.68), channel_id=1, source_target_pairs={{0,16},{2,18},{1,17},{3,19},{16,0},{18,2},{17,1},{19,3}} | collective-permute-start | bytes 294920 | tf_op jit(solution)/shard_map/ppermute | solution.py:193
  7.9 2.9 %collective-permute-start.8 = (bf16[176,384]{1,0:T(8,128)(2,1)S(1)}, bf16[176,384]{1,0:T(8,128)(2,1)S(1)}, u32[]{:S(2)}, u32[]{:S(2)}) collective-permute-start(bf16[176,384]{1,0:T(8,128)(2,1)S(1)} %get-tuple-element.83), channel_id=1, source_target_pairs={{0,4},{1,5},{2,6},{3,7},{16,20},{17,21},{18,22},{19,23}} | collective-permute-start | bytes 405512 | tf_op jit(solution)/shard_map/ppermute | solution.py:304
  8.7 3.5 %collective-permute-start.7 = (bf16[176,384]{1,0:T(8,128)(2,1)S(1)}, bf16[176,384]{1,0:T(8,128)(2,1)S(1)}, u32[]{:S(2)}, u32[]{:S(2)}) collective-permute-start(bf16[176,384]{1,0:T(8,128)(2,1)S(1)} %get-tuple-element.82), channel_id=1, source_target_pairs={{0,4},{1,5},{2,6},{3,7},{16,20},{17,21},{18,22},{19,23}} | collective-permute-start | bytes 405512 | tf_op jit(solution)/shard_map/ppermute | solution.py:304
  9.4 4.3 %collective-permute-start.6 = (bf16[176,384]{1,0:T(8,128)(2,1)S(1)}, bf16[176,384]{1,0:T(8,128)(2,1)S(1)}, u32[]{:S(2)}, u32[]{:S(2)}) collective-permute-start(bf16[176,384]{1,0:T(8,128)(2,1)S(1)} %get-tuple-element.81), channel_id=1, source_target_pairs={{0,4},{1,5},{2,6},{3,7},{16,20},{17,21},{18,22},{19,23}} | collective-permute-start | bytes 405512 | tf_op jit(solution)/shard_map/ppermute | solution.py:304
  10.1 5.0 %collective-permute-start.5 = (bf16[176,384]{1,0:T(8,128)(2,1)S(1)}, bf16[176,384]{1,0:T(8,128)(2,1)S(1)}, u32[]{:S(2)}, u32[]{:S(2)}) collective-permute-start(bf16[176,384]{1,0:T(8,128)(2,1)S(1)} %frame.19), channel_id=1, source_target_pairs={{0,4},{1,5},{2,6},{3,7},{16,20},{17,21},{18,22},{19,23}} | collective-permute-start | bytes 405512 | tf_op jit(solution)/shard_map/ppermute | solution.py:304
  10.8 18.3 %collective-permute-start.12 = (bf16[160,384]{1,0:T(8,128)(2,1)S(1)}, bf16[160,384]{1,0:T(8,128)(2,1)S(1)}, u32[]{:S(2)}, u32[]{:S(2)}) collective-permute-start(bf16[160,384]{1,0:T(8,128)(2,1)S(1)} %get-tuple-element.95), channel_id=1, source_target_pairs={{4,8},{5,9},{6,10},{7,11},{20,24},{21,25},{22,26},{23,27}} | collective-permute-start | bytes 368648 | tf_op jit(solution)/shard_map/ppermute | solution.py:304
  12.2 20.7 %collective-permute-start.11 = (bf16[160,384]{1,0:T(8,128)(2,1)S(1)}, bf16[160,384]{1,0:T(8,128)(2,1)S(1)}, u32[]{:S(2)}, u32[]{:S(2)}) collective-permute-start(bf16[160,384]{1,0:T(8,128)(2,1)S(1)} %get-tuple-element.94), channel_id=1, source_target_pairs={{4,8},{5,9},{6,10},{7,11},{20,24},{21,25},{22,26},{23,27}} | collective-permute-start | bytes 368648 | tf_op jit(solution)/shard_map/ppermute | solution.py:304
  13.8 23.0 %collective-permute-start.10 = (bf16[160,384]{1,0:T(8,128)(2,1)S(1)}, bf16[160,384]{1,0:T(8,128)(2,1)S(1)}, u32[]{:S(2)}, u32[]{:S(2)}) collective-permute-start(bf16[160,384]{1,0:T(8,128)(2,1)S(1)} %get-tuple-element.93), channel_id=1, source_target_pairs={{4,8},{5,9},{6,10},{7,11},{20,24},{21,25},{22,26},{23,27}} | collective-permute-start | bytes 368648 | tf_op jit(solution)/shard_map/ppermute | solution.py:304
  15.1 25.4 %collective-permute-start.9 = (bf16[160,384]{1,0:T(8,128)(2,1)S(1)}, bf16[160,384]{1,0:T(8,128)(2,1)S(1)}, u32[]{:S(2)}, u32[]{:S(2)}) collective-permute-start(bf16[160,384]{1,0:T(8,128)(2,1)S(1)} %frame.23), channel_id=1, source_target_pairs={{4,8},{5,9},{6,10},{7,11},{20,24},{21,25},{22,26},{23,27}} | collective-permute-start | bytes 368648 | tf_op jit(solution)/shard_map/ppermute | solution.py:304
  30.1 12.7 %collective-permute-start.16 = (bf16[144,384]{1,0:T(8,128)(2,1)S(1)}, bf16[144,384]{1,0:T(8,128)(2,1)S(1)}, u32[]{:S(2)}, u32[]{:S(2)}) collective-permute-start(bf16[144,384]{1,0:T(8,128)(2,1)S(1)} %get-tuple-element.107), channel_id=1, source_target_pairs={{8,12},{9,13},{10,14},{11,15},{24,28},{25,29},{26,30},{27,31}} | collective-permute-start | bytes 331784 | tf_op jit(solution)/shard_map/ppermute | solution.py:304
  33.9 9.2 %collective-permute-start.15 = (bf16[144,384]{1,0:T(8,128)(2,1)S(1)}, bf16[144,384]{1,0:T(8,128)(2,1)S(1)}, u32[]{:S(2)}, u32[]{:S(2)}) collective-permute-start(bf16[144,384]{1,0:T(8,128)(2,1)S(1)} %get-tuple-element.106), channel_id=1, source_target_pairs={{8,12},{9,13},{10,14},{11,15},{24,28},{25,29},{26,30},{27,31}} | collective-permute-start | bytes 331784 | tf_op jit(solution)/shard_map/ppermute | solution.py:304
  37.7 6.8 %collective-permute-start.14 = (bf16[144,384]{1,0:T(8,128)(2,1)S(1)}, bf16[144,384]{1,0:T(8,128)(2,1)S(1)}, u32[]{:S(2)}, u32[]{:S(2)}) collective-permute-start(bf16[144,384]{1,0:T(8,128)(2,1)S(1)} %get-tuple-element.105), channel_id=1, source_target_pairs={{8,12},{9,13},{10,14},{11,15},{24,28},{25,29},{26,30},{27,31}} | collective-permute-start | bytes 331784 | tf_op jit(solution)/shard_map/ppermute | solution.py:304
  41.5 3.6 %collective-permute-start.13 = (bf16[144,384]{1,0:T(8,128)(2,1)S(1)}, bf16[144,384]{1,0:T(8,128)(2,1)S(1)}, u32[]{:S(2)}, u32[]{:S(2)}) collective-permute-start(bf16[144,384]{1,0:T(8,128)(2,1)S(1)} %frame.27), channel_id=1, source_target_pairs={{8,12},{9,13},{10,14},{11,15},{24,28},{25,29},{26,30},{27,31}} | collective-permute-start | bytes 331784 | tf_op jit(solution)/shard_map/ppermute | solution.py:304
  43.2 2.0 %collective-permute-start.17 = (bf16[2,64,384]{2,1,0:T(8,128)(2,1)S(1)}, bf16[2,64,384]{2,1,0:T(8,128)(2,1)S(1)}, u32[]{:S(2)}, u32[]{:S(2)}) collective-permute-start(bf16[2,64,384]{2,1,0:T(8,128)(2,1)S(1)} %get-tuple-element.121), channel_id=1, source_target_pairs={{12,0},{14,2},{13,4},{15,6},{28,8},{30,10},{29,12},{31,14}} | collective-permute-start | bytes 294920 | tf_op jit(solution)/shard_map/ppermute | solution.py:315
  43.8 1.3 %collective-permute-start.18 = (bf16[2,64,384]{2,1,0:T(8,128)(2,1)S(1)}, bf16[2,64,384]{2,1,0:T(8,128)(2,1)S(1)}, u32[]{:S(2)}, u32[]{:S(2)}) collective-permute-start(bf16[2,64,384]{2,1,0:T(8,128)(2,1)S(1)} %get-tuple-element.122), channel_id=1, source_target_pairs={{12,1},{14,3},{13,5},{15,7},{28,9},{30,11},{29,13},{31,15}} | collective-permute-start | bytes 294920 | tf_op jit(solution)/shard_map/ppermute | solution.py:315
  45.1 2.0 %collective-permute-start.19 = (bf16[2,64,384]{2,1,0:T(8,128)(2,1)S(1)}, bf16[2,64,384]{2,1,0:T(8,128)(2,1)S(1)}, u32[]{:S(2)}, u32[]{:S(2)}) collective-permute-start(bf16[2,64,384]{2,1,0:T(8,128)(2,1)S(1)} %get-tuple-element.123), channel_id=1, source_target_pairs={{12,17},{14,19},{13,21},{15,23},{28,25},{30,27},{29,29},{31,31}} | collective-permute-start | bytes 294920 | tf_op jit(solution)/shard_map/ppermute | solution.py:315
  45.8 11.8 %collective-permute-start.20 = (bf16[2,64,384]{2,1,0:T(8,128)(2,1)S(1)}, bf16[2,64,384]{2,1,0:T(8,128)(2,1)S(1)}, u32[]{:S(2)}, u32[]{:S(2)}) collective-permute-start(bf16[2,64,384]{2,1,0:T(8,128)(2,1)S(1)} %get-tuple-element.124), channel_id=1, source_target_pairs={{12,16},{14,18},{13,20},{15,22},{28,24},{30,26},{29,28},{31,30}} | collective-permute-start | bytes 294920 | tf_op jit(solution)/shard_map/ppermute | solution.py:315

commit v6 on v5

--- a/solution.py
+++ b/solution.py
@@ -37,13 +37,13 @@
     return pl.ds(pl.multiple_of(start * cols, cols), count * cols)
 
 
-def pick_kernel(per_half, holders, source, mine, own, other, sems):
+def pick_kernel(per_half, holders, source, mine, own, sems):
     side = lax.axis_index("tm") & (holders - 1)
     lane = lax.axis_index("band") & (per_half - 1)
-    clips = (lax.axis_index("segment"), side * per_half + lane, (holders - 1 - side) * per_half + lane)
+    clips = (lax.axis_index("segment"), side * per_half + lane)
     copies = [
         pltpu.make_async_copy(source.at[clip], target, sems.at[number])
-        for number, (clip, target) in enumerate(zip(clips, (mine, own, other)))
+        for number, (clip, target) in enumerate(zip(clips, (mine, own)))
     ]
     for copy in copies:
         copy.start()
@@ -51,12 +51,15 @@
         copy.wait()
 
 
+def taps(spread, start, count, cols):
+    return jnp.concatenate([spread[rows_at(start + row, count, cols), :] for row in range(TAPS)], axis=1)
+
+
 def loader_kernel(weight, bias, gain, now, past, bias_out, gain_out, sems):
     channels = weight.shape[-1]
     copies = [(bias, bias_out), (gain, gain_out), (weight.at[2], now)]
-    for row in range(TAPS):
-        for age in range(2):
-            copies.append((weight.at[age, row], past.at[row, :, pl.ds(age * channels, channels)]))
+    for age in range(2):
+        copies.append((weight.at[age], past.at[:, pl.ds(age * channels, channels)]))
     copies = [
         pltpu.make_async_copy(source, target, sems.at[number])
         for number, (source, target) in enumerate(copies)
@@ -98,8 +101,8 @@
                 place(groups[0])
             else:
                 near = lax.axis_index("tm") == cfg["time"]
-                pl.when(near)(functools.partial(place, groups[0]))
-                pl.when(jnp.logical_not(near))(functools.partial(place, groups[1]))
+                pl.when(near)(functools.partial(place, groups[1]))
+                pl.when(jnp.logical_not(near))(functools.partial(place, groups[0]))
             source, skip = entry, 0
         else:
             source, skip = received, half * (unit - 1 - cfg["came"])
@@ -117,10 +120,7 @@
             spread[pl.ds(cols, size), pl.ds(number * channels, channels)] = value.astype(jnp.bfloat16)
         kept = source[rows_at(skip + half, need, cols), :].astype(jnp.float32)
         total = partial[pl.ds(0, need * cols), :] + kept + bias[...]
-        for row in range(TAPS):
-            total += jnp.dot(
-                spread[rows_at(half + row, need, cols), :], weight[row], preferred_element_type=jnp.float32
-            )
+        total += jnp.dot(taps(spread, half, need, cols), weight[...], preferred_element_type=jnp.float32)
         value = total.astype(jnp.bfloat16)
         if unit < segments - 1:
             out[rows_at(half * (unit - cfg["lowest"]), need, cols), :] = value
@@ -141,11 +141,7 @@
     def run(unit):
         need = window - unit - 1
         here = pl.ds(0, need * cols)
-        total = jnp.zeros((need * cols, 2 * channels), jnp.float32)
-        for row in range(TAPS):
-            total += jnp.dot(
-                spread[rows_at(half + row, need, cols), :], weight[row], preferred_element_type=jnp.float32
-            )
+        total = jnp.dot(taps(spread, half, need, cols), weight[...], preferred_element_type=jnp.float32)
         near_out[here, :] = far[here, :] + total[:, channels:]
         far_out[here, :] = total[:, :channels]
 
@@ -170,55 +166,60 @@
     def spot(t, s, b):
         return (t * segments + s) * bands + b
 
-    mine, own, other = pl.pallas_call(
+    mine, own = pl.pallas_call(
         functools.partial(pick_kernel, per_half, holders),
-        out_shape=[pltpu.VMEM((own_frames, piece, channels), features.dtype)] * 3,
+        out_shape=[pltpu.VMEM((own_frames, piece, channels), features.dtype)] * 2,
         in_specs=[whole(pltpu.HBM)],
-        out_specs=[whole()] * 3,
-        scratch_shapes=[pltpu.SemaphoreType.DMA((3,))],
+        out_specs=[whole()] * 2,
+        scratch_shapes=[pltpu.SemaphoreType.DMA((2,))],
         compiler_params=pltpu.CompilerParams(vmem_limit_bytes=1 << 20),
         name="pick",
     )(pltpu.with_memory_space_constraint(features.reshape(clips, own_frames, piece, channels), pltpu.HBM))
     wanted = [[2 * h + j for h in range(HALVES) for j in range(per_half)], [1, 0, 3, 2], [2, 2, 1, 1]]
     places = [sum((b - at // per_half) << (2 * at) for at, b in enumerate(row)) for row in wanted]
 
-    def gather(value, number, members):
+    def gather(number, members):
         routes = []
         for t, clip in members:
             for h in range(HALVES):
                 there, at = stream(clip, h)
-                segment = clip if value is mine else 0
-                routes.append((spot(t, segment, wanted[number][at]), spot(there, 0, at)))
+                routes.append((spot(t, clip, wanted[number][at]), spot(there, 0, at)))
         assert len({a for a, _ in routes}) == len({b for _, b in routes}) == len(routes)
-        return lax.ppermute(value, MESH_AXES, routes)
+        return lax.ppermute(mine, MESH_AXES, routes)
 
     sides = [(t, clip) for t in range(holders) for clip in range(clips)]
     beside = [(t, clip) for t, clip in sides if clip // per_half == t]
     across = [(t, clip) for t, clip in sides if clip // per_half != t]
-    far_group = [gather(mine, number, across) for number in (1, 2)]
-    near_group = [gather(mine, number, beside) for number in (1, 2)]
-    far_group = [gather(other, 0, across)] + far_group
-    near_group = [own] + near_group
-    entries = [[near_group, far_group]] * holders
+    far_group = [gather(number, across) for number in range(TAPS)]
+    near_group = [own] + [gather(number, beside) for number in (1, 2)]
+    entries = [[far_group, near_group]] * holders
     for t in range(holders, times):
-        entries.append([[gather(mine, number, [(t, clip) for clip in range(clips)]) for number in range(TAPS)]])
-
-    stored = [conv_weight[0].reshape(TAPS, TAPS, TAPS * channels, channels), conv_bias, norm_gain]
+        entries.append([[gather(number, [(t, clip) for clip in range(clips)]) for number in range(TAPS)]])
+
+    stored = [conv_weight[0].reshape(TAPS, TAPS * TAPS * channels, channels), conv_bias, norm_gain]
     now, past, bias, gain = pl.pallas_call(
         loader_kernel,
         out_shape=[
-            pltpu.VMEM((TAPS, TAPS * channels, channels), stored[0].dtype),
-            pltpu.VMEM((TAPS, TAPS * channels, 2 * channels), stored[0].dtype),
+            pltpu.VMEM((TAPS * TAPS * channels, channels), stored[0].dtype),
+            pltpu.VMEM((TAPS * TAPS * channels, 2 * channels), stored[0].dtype),
             pltpu.VMEM(conv_bias.shape, conv_bias.dtype),
             pltpu.VMEM(norm_gain.shape, norm_gain.dtype),
         ],
         in_specs=[whole(pltpu.HBM)] * 3,
         out_specs=[whole()] * 4,
-        scratch_shapes=[pltpu.SemaphoreType.DMA((9,))],
+        scratch_shapes=[pltpu.SemaphoreType.DMA((5,))],
         compiler_params=pltpu.CompilerParams(vmem_limit_bytes=1 << 20),
         name="loader",
     )(*[pltpu.with_memory_space_constraint(value, pltpu.HBM) for value in stored])
     now, past, bias, gain = (resident(value) for value in (now, past, bias, gain))
+
+    def leave(value, there, index, group):
+        routes = []
+        for clip in group:
+            for h in range(HALVES):
+                t, b = stream(clip, h)
+                routes.append((spot(t, segments - 1, b), spot(there, clip, h * per_half + index)))
+        return lax.ppermute(value, MESH_AXES, routes)
 
     state = ((window - 1) * cols, channels)
     near = jnp.zeros(state, jnp.float32)
@@ -227,7 +228,7 @@
     slots = frames + lag * (segments - 1)
     moving = {}
     tails = []
-    held = []
+    waiting = []
     landed = {}
     for slot in range(slots):
         units = working(slot, frames, segments, lag)
@@ -247,7 +248,7 @@
             came=min(working(slot - lag, frames, segments, lag)) if slot >= lag else None,
             finals=finals,
             tail_at=last % own_frames,
-            passing=(finals if middle else 0) + (len(landed) if slot + 1 == slots else len(held)),
+            passing=(finals if middle else 0) + (len(landed) + len(waiting) if slot + 1 == slots else 0),
             cols=cols,
             window=window,
             segments=segments,
@@ -273,9 +274,9 @@
                 aliases[len(operands)] = len(shapes) + index
                 operands.append(resident(value))
         shapes += [shape] * finals
-        if slot + 1 == slots:
-            held = [(*key, value) for key, value in landed.items()]
-        for _, _, value in held:
+        held = list(landed) if slot + 1 == slots else []
+        kept = [landed[key] for key in held] + ([value for _, _, value in waiting] if held else [])
+        for value in kept:
             aliases[len(operands)] = len(shapes)
             operands.append(resident(value))
             shapes.append(shape)
@@ -295,24 +296,21 @@
         out = results.pop(0) if cfg["sends"] else None
         spread = results.pop(0) if cfg["later"] else None
         tails = results[:finals]
-        leaving = [(there, index, value) for (there, index, _), value in zip(held, results[finals:])]
-        if slot + 1 == slots:
-            landed.update({(there, index): value for there, index, value in leaving})
-            leaving = []
-        held = []
         if cfg["sends"]:
             moving[slot] = lax.ppermute(out, "segment", [(s, s + 1) for s in senders_now])
+        if slot + 1 == slots:
+            kept = results[finals:]
+            landed.update(zip(held, kept))
+            waiting = [(there, index, value) for (there, index, _), value in zip(waiting, kept[len(held) :])]
         if finals and last % own_frames == own_frames - 1:
             there = last // own_frames
-            ready = [(there, index, value) for index, value in enumerate(tails)]
-            leaving += ready
-        for there, index, value in leaving:
-            routes = []
-            for clip in range(clips):
-                for h in range(HALVES):
-                    t, b = stream(clip, h)
-                    routes.append((spot(t, segments - 1, b), spot(there, clip, h * per_half + index)))
-            landed[there, index] = lax.ppermute(value, MESH_AXES, routes)
+            final = there == times - 1
+            for index, value in enumerate(tails):
+                landed[there, index, 0] = leave(value, there, index, range(clips if final else per_half))
+            waiting += [] if final else [(there, index, value) for index, value in enumerate(tails)]
+            if final:
+                for there, index, value in waiting:
+                    landed[there, index, 1] = leave(value, there, index, range(per_half, clips))
         if cfg["later"]:
             near, far = pl.pallas_call(
                 functools.partial(history_kernel, cfg),
@@ -326,8 +324,10 @@
             )(resident(spread), resident(near), resident(far), past)
 
     result = None
-    for (t, index), value in landed.items():
+    for (t, index, part), value in landed.items():
         here = jnp.logical_and(time == t, band % per_half == index)
+        if t < times - 1:
+            here = jnp.logical_and(here, (position >= per_half) == (part == 1))
         result = value if result is None else jnp.where(here, value, result)
     return result.reshape(1, own_frames, own_rows, cols, channels)
 

time: 59 us -> 59.9 us (1.015)
  the two profiles are of different devices: /device:TPU:18 before, /device:TPU:6 now
where the time goes in v6:
time: 59.9 us; the launch traced here: 59.5 us
  starting transfers between devices  23.4 us (39%)
  waiting for transfers between devices  21.2 us (35%)
  Pallas kernels  13.6 us (23%)
  other arithmetic  0.67 us (1%)
    ppermute x6, waiting for transfers between devices, leave(): return lax.ppermute(value, MESH_AXES, routes)  16.7 us
    ppermute x12, starting transfers between devices, local(): lax.ppermute(out, 'segment', [(s, s + 1) for s in senders_now])  10.5 us
    ppermute x5, starting transfers between devices, gather(): return lax.ppermute(mine, MESH_AXES, routes)  8.27 us
    pallas_call x16, Pallas kernels, local(): pl.pallas_call(functools.partial(frame_kernel, cfg), out_shape=shapes, in...  5.06 us
    ppermute x6, starting transfers between devices, leave(): return lax.ppermute(value, MESH_AXES, routes)  4.63 us
    ppermute x5, waiting for transfers between devices, gather(): return lax.ppermute(mine, MESH_AXES, routes)  4.37 us
    pallas_call x12, Pallas kernels, local(): pl.pallas_call(functools.partial(history_kernel, cfg), out_shape=[pltpu.V...  4.15 us
    pallas_call x1, Pallas kernels, local(): pl.pallas_call(loader_kernel, out_shape=[pltpu.VMEM((TAPS * TAPS * channe...  3.42 us
  transfers between devices with their start and end apart: 23, of which 6 were waited for; matrix products, arithmetic and copies ran while one was open for 0% of the time, Pallas kernels for 19%

profile of v6, /device:TPU:6, one launch (start us, length us, event | category | flops | bytes accessed | tf_op | source)
XLA Modules:
  0.0 59.5 jit_solution(4981096451669681899)
XLA Ops:
  0.0 1.0 %pick.1 = (bf16[2,64,384]{2,1,0:T(8,128)(2,1)S(1)}, bf16[2,64,384]{2,1,0:T(8,128)(2,1)S(1)}) custom-call(bf16[4,2,64,384]{3,2,1,0:T(8,128)(2,1)} %bitcast.4), custom_call_target="tpu_custom_call" | custom-call | tf_op jit(solution)/shard_map/pick/pallas_call | solution.py:169
  1.0 2.5 %collective-permute-start = (bf16[2,64,384]{2,1,0:T(8,128)(2,1)S(1)}, bf16[2,64,384]{2,1,0:T(8,128)(2,1)S(1)}, u32[]{:S(2)}, u32[]{:S(2)}) collective-permute-start(bf16[2,64,384]{2,1,0:T(8,128)(2,1)S(1)} %get-tuple-element.67), channel_id=1, source_target_pairs={{8,16},{10,18},{13,17},{15,19},{16,0},{18,2},{21,1},{23,3}} | collective-permute-start | bytes 294920 | tf_op jit(solution)/shard_map/ppermute | solution.py:188
  3.4 1.3 %collective-permute-start.1 = (bf16[2,64,384]{2,1,0:T(8,128)(2,1)S(1)}, bf16[2,64,384]{2,1,0:T(8,128)(2,1)S(1)}, u32[]{:S(2)}, u32[]{:S(2)}) collective-permute-start(bf16[2,64,384]{2,1,0:T(8,128)(2,1)S(1)} %get-tuple-element.67), channel_id=1, source_target_pairs={{9,16},{11,18},{12,17},{14,19},{17,0},{19,2},{20,1},{22,3}} | collective-permute-start | bytes 294920 | tf_op jit(solution)/shard_map/ppermute | solution.py:188
  4.7 1.9 %collective-permute-start.2 = (bf16[2,64,384]{2,1,0:T(8,128)(2,1)S(1)}, bf16[2,64,384]{2,1,0:T(8,128)(2,1)S(1)}, u32[]{:S(2)}, u32[]{:S(2)}) collective-permute-start(bf16[2,64,384]{2,1,0:T(8,128)(2,1)S(1)} %get-tuple-element.67), channel_id=1, source_target_pairs={{10,16},{9,18},{14,17},{13,19},{18,0},{17,2},{22,1},{21,3}} | collective-permute-start | bytes 294920 | tf_op jit(solution)/shard_map/ppermute | solution.py:188
  6.7 1.3 %collective-permute-start.3 = (bf16[2,64,384]{2,1,0:T(8,128)(2,1)S(1)}, bf16[2,64,384]{2,1,0:T(8,128)(2,1)S(1)}, u32[]{:S(2)}, u32[]{:S(2)}) collective-permute-start(bf16[2,64,384]{2,1,0:T(8,128)(2,1)S(1)} %get-tuple-element.67), channel_id=1, source_target_pairs={{1,0},{3,2},{4,1},{6,3},{25,16},{27,18},{28,17},{30,19}} | collective-permute-start | bytes 294920 | tf_op jit(solution)/shard_map/ppermute | solution.py:188
  8.0 1.3 %collective-permute-start.4 = (bf16[2,64,384]{2,1,0:T(8,128)(2,1)S(1)}, bf16[2,64,384]{2,1,0:T(8,128)(2,1)S(1)}, u32[]{:S(2)}, u32[]{:S(2)}) collective-permute-start(bf16[2,64,384]{2,1,0:T(8,128)(2,1)S(1)} %get-tuple-element.67), channel_id=1, source_target_pairs={{2,0},{1,2},{6,1},{5,3},{26,16},{25,18},{30,17},{29,19}} | collective-permute-start | bytes 294920 | tf_op jit(solution)/shard_map/ppermute | solution.py:188
  9.3 3.4 %loader.1 = (bf16[3456,384]{1,0:T(8,128)(2,1)S(1)}, bf16[3456,768]{1,0:T(8,128)(2,1)S(1)}, f32[1,384]{1,0:T(1,128)S(1)}, f32[1,384]{1,0:T(1,128)S(1)}) custom-call(bf16[3,3456,384]{2,1,0:T(8,128)(2,1)} %bitcast.3, f32[1,384]{1,0:T(1,128)} %bias.1, f32[1,384]{1,0:T(1,128)} %gain.1), custom_call_target="tpu_custom_call" | custom-call | tf_op jit(solution)/shard_map/loader/pallas_call | solution.py:200
  12.7 1.5 %collective-permute-done.1.refs_1_ = bf16[2,64,384]{2,1,0:T(8,128)(2,1)S(1)} collective-permute-done((bf16[2,64,384]{2,1,0:T(8,128)(2,1)S(1)}, bf16[2,64,384]{2,1,0:T(8,128)(2,1)S(1)}, u32[]{:S(2)}, u32[]{:S(2)}) %collective-permute-start.1) | collective-permute-done | bytes 98336 | tf_op jit(solution)/shard_map/ppermute | solution.py:188
  15.0 2.0 %collective-permute-done.4.refs_5_ = bf16[2,64,384]{2,1,0:T(8,128)(2,1)S(1)} collective-permute-done((bf16[2,64,384]{2,1,0:T(8,128)(2,1)S(1)}, bf16[2,64,384]{2,1,0:T(8,128)(2,1)S(1)}, u32[]{:S(2)}, u32[]{:S(2)}) %collective-permute-start.4) | collective-permute-done | bytes 98336 | tf_op jit(solution)/shard_map/ppermute | solution.py:188
  17.1 1.2 %frame.16 = (bf16[176,384]{1,0:T(8,128)(2,1)S(1)}, bf16[224,1152]{1,0:T(8,128)(2,1)S(1)}) custom-call(bf16[2,64,384]{2,1,0:T(8,128)(2,1)S(1)} %collective-permute-done.refs_0_, bf16[2,64,384]{2,1,0:T(8,128)(2,1)S(1)} %collective-permute-done.1.refs_1_, bf16[2,64,384]{2,1,0:T(8,128)(2,1)S(1)} %collective-permute-done.2.refs_2_, ...), custom_call_target="tpu_custom_call" | custom-call | bytes 1024 | tf_op jit(solution)/shard_map/frame/pallas_call | solution.py:284
  18.3 1.3 %collective-permute-start.8 = (bf16[176,384]{1,0:T(8,128)(2,1)S(1)}, bf16[176,384]{1,0:T(8,128)(2,1)S(1)}, u32[]{:S(2)}, u32[]{:S(2)}) collective-permute-start(bf16[176,384]{1,0:T(8,128)(2,1)S(1)} %get-tuple-element.83), channel_id=1, source_target_pairs={{0,4},{1,5},{2,6},{3,7},{16,20},{17,21},{18,22},{19,23}} | collective-permute-start | bytes 405512 | tf_op jit(solution)/shard_map/ppermute | solution.py:300
  19.6 1.2 %history.12 = (f32[176,384]{1,0:T(8,128)S(1)}, f32[176,384]{1,0:T(8,128)S(1)}) custom-call(bf16[224,1152]{1,0:T(8,128)(2,1)S(1)} %get-tuple-element.72.spread, f32[176,384]{1,0:T(8,128)S(1)} %broadcast_1_refs_6__near_far.2.refs_6_.near, f32[176,384]{1,0:T(8,128)S(1)} %broadcast_1_refs_6__near_far.2.clone.far, ...), custom_call_target="tpu_custom_call", output_to_operand_aliasing={{0}: (1, {}), {1}: (2, {})} | custom-call | bytes 1024 | tf_op jit(solution)/shard_map/history/pallas_call | solution.py:315
  20.8 1.2 %frame.17 = (bf16[176,384]{1,0:T(8,128)(2,1)S(1)}, bf16[224,1152]{1,0:T(8,128)(2,1)S(1)}) custom-call(bf16[2,64,384]{2,1,0:T(8,128)(2,1)S(1)} %collective-permute-done.refs_0_, bf16[2,64,384]{2,1,0:T(8,128)(2,1)S(1)} %collective-permute-done.1.refs_1_, bf16[2,64,384]{2,1,0:T(8,128)(2,1)S(1)} %collective-permute-done.2.refs_2_, ...), custom_call_target="tpu_custom_call" | custom-call | bytes 1024 | tf_op jit(solution)/shard_map/frame/pallas_call | solution.py:284
  22.0 1.3 %collective-permute-start.7 = (bf16[176,384]{1,0:T(8,128)(2,1)S(1)}, bf16[176,384]{1,0:T(8,128)(2,1)S(1)}, u32[]{:S(2)}, u32[]{:S(2)}) collective-permute-start(bf16[176,384]{1,0:T(8,128)(2,1)S(1)} %get-tuple-element.82), channel_id=1, source_target_pairs={{0,4},{1,5},{2,6},{3,7},{16,20},{17,21},{18,22},{19,23}} | collective-permute-start | bytes 405512 | tf_op jit(solution)/shard_map/ppermute | solution.py:300
  23.3 1.3 %history.13 = (f32[176,384]{1,0:T(8,128)S(1)}, f32[176,384]{1,0:T(8,128)S(1)}) custom-call(bf16[224,1152]{1,0:T(8,128)(2,1)S(1)} %get-tuple-element.75.spread, f32[176,384]{1,0:T(8,128)S(1)} %get-tuple-element.74.refs_6_.near, f32[176,384]{1,0:T(8,128)S(1)} %get-tuple-element.76.far, ...), custom_call_target="tpu_custom_call", output_to_operand_aliasing={{0}: (1, {}), {1}: (2, {})} | custom-call | bytes 1024 | tf_op jit(solution)/shard_map/history/pallas_call | solution.py:315
  24.6 1.2 %frame.18 = (bf16[176,384]{1,0:T(8,128)(2,1)S(1)}, bf16[224,1152]{1,0:T(8,128)(2,1)S(1)}) custom-call(bf16[2,64,384]{2,1,0:T(8,128)(2,1)S(1)} %collective-permute-done.refs_0_, bf16[2,64,384]{2,1,0:T(8,128)(2,1)S(1)} %collective-permute-done.1.refs_1_, bf16[2,64,384]{2,1,0:T(8,128)(2,1)S(1)} %collective-permute-done.2.refs_2_, ...), custom_call_target="tpu_custom_call" | custom-call | bytes 1024 | tf_op jit(solution)/shard_map/frame/pallas_call | solution.py:284
  25.7 1.3 %collective-permute-start.6 = (bf16[176,384]{1,0:T(8,128)(2,1)S(1)}, bf16[176,384]{1,0:T(8,128)(2,1)S(1)}, u32[]{:S(2)}, u32[]{:S(2)}) collective-permute-start(bf16[176,384]{1,0:T(8,128)(2,1)S(1)} %get-tuple-element.81), channel_id=1, source_target_pairs={{0,4},{1,5},{2,6},{3,7},{16,20},{17,21},{18,22},{19,23}} | collective-permute-start | bytes 405512 | tf_op jit(solution)/shard_map/ppermute | solution.py:300
  27.1 1.3 %history.14 = (f32[176,384]{1,0:T(8,128)S(1)}, f32[176,384]{1,0:T(8,128)S(1)}) custom-call(bf16[224,1152]{1,0:T(8,128)(2,1)S(1)} %get-tuple-element.78.spread, f32[176,384]{1,0:T(8,128)S(1)} %get-tuple-element.77.refs_6_.near, f32[176,384]{1,0:T(8,128)S(1)} %get-tuple-element.79.far, ...), custom_call_target="tpu_custom_call", output_to_operand_aliasing={{0}: (1, {}), {1}: (2, {})} | custom-call | bytes 1024 | tf_op jit(solution)/shard_map/history/pallas_call | solution.py:315
  28.3 1.2 %frame.19 = bf16[176,384]{1,0:T(8,128)(2,1)S(1)} custom-call(bf16[2,64,384]{2,1,0:T(8,128)(2,1)S(1)} %collective-permute-done.refs_0_, bf16[2,64,384]{2,1,0:T(8,128)(2,1)S(1)} %collective-permute-done.1.refs_1_, bf16[2,64,384]{2,1,0:T(8,128)(2,1)S(1)} %collective-permute-done.2.refs_2_, bf16[2,64,384]{2,1,0:T(8,128)(2,1)S(1)} %get-tuple-element.68.refs_3_, ...), custom_call_target="tpu_custom_call" | custom-call | bytes 1024 | tf_op jit(solution)/shard_map/frame/pallas_call | solution.py:284
  29.5 1.3 %collective-permute-start.5 = (bf16[176,384]{1,0:T(8,128)(2,1)S(1)}, bf16[176,384]{1,0:T(8,128)(2,1)S(1)}, u32[]{:S(2)}, u32[]{:S(2)}) collective-permute-start(bf16[176,384]{1,0:T(8,128)(2,1)S(1)} %frame.19), channel_id=1, source_target_pairs={{0,4},{1,5},{2,6},{3,7},{16,20},{17,21},{18,22},{19,23}} | collective-permute-start | bytes 405512 | tf_op jit(solution)/shard_map/ppermute | solution.py:300
  30.8 0.7 %collective-permute-start.12 = (bf16[160,384]{1,0:T(8,128)(2,1)S(1)}, bf16[160,384]{1,0:T(8,128)(2,1)S(1)}, u32[]{:S(2)}, u32[]{:S(2)}) collective-permute-start(bf16[160,384]{1,0:T(8,128)(2,1)S(1)} %get-tuple-element.95), channel_id=1, source_target_pairs={{4,8},{5,9},{6,10},{7,11},{20,24},{21,25},{22,26},{23,27}} | collective-permute-start | bytes 368648 | tf_op jit(solution)/shard_map/ppermute | solution.py:300
  31.6 0.7 %collective-permute-start.11 = (bf16[160,384]{1,0:T(8,128)(2,1)S(1)}, bf16[160,384]{1,0:T(8,128)(2,1)S(1)}, u32[]{:S(2)}, u32[]{:S(2)}) collective-permute-start(bf16[160,384]{1,0:T(8,128)(2,1)S(1)} %get-tuple-element.94), channel_id=1, source_target_pairs={{4,8},{5,9},{6,10},{7,11},{20,24},{21,25},{22,26},{23,27}} | collective-permute-start | bytes 368648 | tf_op jit(solution)/shard_map/ppermute | solution.py:300
  32.5 0.7 %collective-permute-start.10 = (bf16[160,384]{1,0:T(8,128)(2,1)S(1)}, bf16[160,384]{1,0:T(8,128)(2,1)S(1)}, u32[]{:S(2)}, u32[]{:S(2)}) collective-permute-start(bf16[160,384]{1,0:T(8,128)(2,1)S(1)} %get-tuple-element.93), channel_id=1, source_target_pairs={{4,8},{5,9},{6,10},{7,11},{20,24},{21,25},{22,26},{23,27}} | collective-permute-start | bytes 368648 | tf_op jit(solution)/shard_map/ppermute | solution.py:300
  34.0 0.7 %collective-permute-start.16 = (bf16[144,384]{1,0:T(8,128)(2,1)S(1)}, bf16[144,384]{1,0:T(8,128)(2,1)S(1)}, u32[]{:S(2)}, u32[]{:S(2)}) collective-permute-start(bf16[144,384]{1,0:T(8,128)(2,1)S(1)} %get-tuple-element.107), channel_id=1, source_target_pairs={{8,12},{9,13},{10,14},{11,15},{24,28},{25,29},{26,30},{27,31}} | collective-permute-start | bytes 331784 | tf_op jit(solution)/shard_map/ppermute | solution.py:300
  34.8 0.7 %collective-permute-start.15 = (bf16[144,384]{1,0:T(8,128)(2,1)S(1)}, bf16[144,384]{1,0:T(8,128)(2,1)S(1)}, u32[]{:S(2)}, u32[]{:S(2)}) collective-permute-start(bf16[144,384]{1,0:T(8,128)(2,1)S(1)} %get-tuple-element.106), channel_id=1, source_target_pairs={{8,12},{9,13},{10,14},{11,15},{24,28},{25,29},{26,30},{27,31}} | collective-permute-start | bytes 331784 | tf_op jit(solution)/shard_map/ppermute | solution.py:300
  35.5 0.7 %collective-permute-start.14 = (bf16[144,384]{1,0:T(8,128)(2,1)S(1)}, bf16[144,384]{1,0:T(8,128)(2,1)S(1)}, u32[]{:S(2)}, u32[]{:S(2)}) collective-permute-start(bf16[144,384]{1,0:T(8,128)(2,1)S(1)} %get-tuple-element.105), channel_id=1, source_target_pairs={{8,12},{9,13},{10,14},{11,15},{24,28},{25,29},{26,30},{27,31}} | collective-permute-start | bytes 331784 | tf_op jit(solution)/shard_map/ppermute | solution.py:300
  36.3 0.7 %collective-permute-start.13 = (bf16[144,384]{1,0:T(8,128)(2,1)S(1)}, bf16[144,384]{1,0:T(8,128)(2,1)S(1)}, u32[]{:S(2)}, u32[]{:S(2)}) collective-permute-start(bf16[144,384]{1,0:T(8,128)(2,1)S(1)} %frame.27), channel_id=1, source_target_pairs={{8,12},{9,13},{10,14},{11,15},{24,28},{25,29},{26,30},{27,31}} | collective-permute-start | bytes 331784 | tf_op jit(solution)/shard_map/ppermute | solution.py:300
  37.0 0.7 %collective-permute-start.17 = (bf16[2,64,384]{2,1,0:T(8,128)(2,1)S(1)}, bf16[2,64,384]{2,1,0:T(8,128)(2,1)S(1)}, u32[]{:S(2)}, u32[]{:S(2)}) collective-permute-start(bf16[2,64,384]{2,1,0:T(8,128)(2,1)S(1)} %get-tuple-element.121.refs_9_), channel_id=1, source_target_pairs={{12,0},{14,2},{13,4},{15,6}} | collective-permute-start | bytes 294920 | tf_op jit(solution)/shard_map/ppermute | solution.py:222
  40.1 0.7 %collective-permute-start.21 = (bf16[2,64,384]{2,1,0:T(8,128)(2,1)S(1)}, bf16[2,64,384]{2,1,0:T(8,128)(2,1)S(1)}, u32[]{:S(2)}, u32[]{:S(2)}) collective-permute-start(bf16[2,64,384]{2,1,0:T(8,128)(2,1)S(1)} %get-tuple-element.125), channel_id=1, source_target_pairs={{12,17},{14,19},{13,21},{15,23},{28,25},{30,27},{29,29},{31,31}} | collective-permute-start | bytes 294920 | tf_op jit(solution)/shard_map/ppermute | solution.py:222
  40.8 1.3 %collective-permute-start.22 = (bf16[2,64,384]{2,1,0:T(8,128)(2,1)S(1)}, bf16[2,64,384]{2,1,0:T(8,128)(2,1)S(1)}, u32[]{:S(2)}, u32[]{:S(2)}) collective-permute-start(bf16[2,64,384]{2,1,0:T(8,128)(2,1)S(1)} %get-tuple-element.126), channel_id=1, source_target_pairs={{12,16},{14,18},{13,20},{15,22},{28,24},{30,26},{29,28},{31,30}} | collective-permute-start | bytes 294920 | tf_op jit(solution)/shard_map/ppermute | solution.py:222
  42.2 16.6 %collective-permute-done.22 = bf16[2,64,384]{2,1,0:T(8,128)(2,1)S(1)} collective-permute-done((bf16[2,64,384]{2,1,0:T(8,128)(2,1)S(1)}, bf16[2,64,384]{2,1,0:T(8,128)(2,1)S(1)}, u32[]{:S(2)}, u32[]{:S(2)}) %collective-permute-start.22) | collective-permute-done | bytes 98336 | tf_op jit(solution)/shard_map/ppermute | solution.py:222
  58.8 0.7 %select_select_fusion = bf16[2,64,384]{2,1,0:T(8,128)(2,1)} fusion(bf16[2,64,384]{2,1,0:T(8,128)(2,1)S(1)} %collective-permute-done.19, bf16[2,64,384]{2,1,0:T(8,128)(2,1)S(1)} %collective-permute-done.20, bf16[2,64,384]{2,1,0:T(8,128)(2,1)S(1)} %collective-permute-done.21, bf16[2,64,384]{2,1,0:T(8,128)(2,1)S(1)} %collective-permute-done.22, ...), kind=kLoop, calls=%fused_computation | loop fusion | flops 245760 | bytes 688133 | tf_op jit(solution)/shard_map/jit(_where)/select_n | solution.py:331
  (47 shorter events, 4.6 us)
Async XLA Ops:
  1.0 11.7 %collective-permute-start = (bf16[2,64,384]{2,1,0:T(8,128)(2,1)S(1)}, bf16[2,64,384]{2,1,0:T(8,128)(2,1)S(1)}, u32[]{:S(2)}, u32[]{:S(2)}) collective-permute-start(bf16[2,64,384]{2,1,0:T(8,128)(2,1)S(1)} %get-tuple-element.67), channel_id=1, source_target_pairs={{8,16},{10,18},{13,17},{15,19},{16,0},{18,2},{21,1},{23,3}} | collective-permute-start | bytes 294920 | tf_op jit(solution)/shard_map/ppermute | solution.py:188
  3.4 10.7 %collective-permute-start.1 = (bf16[2,64,384]{2,1,0:T(8,128)(2,1)S(1)}, bf16[2,64,384]{2,1,0:T(8,128)(2,1)S(1)}, u32[]{:S(2)}, u32[]{:S(2)}) collective-permute-start(bf16[2,64,384]{2,1,0:T(8,128)(2,1)S(1)} %get-tuple-element.67), channel_id=1, source_target_pairs={{9,16},{11,18},{12,17},{14,19},{17,0},{19,2},{20,1},{22,3}} | collective-permute-start | bytes 294920 | tf_op jit(solution)/shard_map/ppermute | solution.py:188
  4.7 9.7 %collective-permute-start.2 = (bf16[2,64,384]{2,1,0:T(8,128)(2,1)S(1)}, bf16[2,64,384]{2,1,0:T(8,128)(2,1)S(1)}, u32[]{:S(2)}, u32[]{:S(2)}) collective-permute-start(bf16[2,64,384]{2,1,0:T(8,128)(2,1)S(1)} %get-tuple-element.67), channel_id=1, source_target_pairs={{10,16},{9,18},{14,17},{13,19},{18,0},{17,2},{22,1},{21,3}} | collective-permute-start | bytes 294920 | tf_op jit(solution)/shard_map/ppermute | solution.py:188
  6.7 8.4 %collective-permute-start.3 = (bf16[2,64,384]{2,1,0:T(8,128)(2,1)S(1)}, bf16[2,64,384]{2,1,0:T(8,128)(2,1)S(1)}, u32[]{:S(2)}, u32[]{:S(2)}) collective-permute-start(bf16[2,64,384]{2,1,0:T(8,128)(2,1)S(1)} %get-tuple-element.67), channel_id=1, source_target_pairs={{1,0},{3,2},{4,1},{6,3},{25,16},{27,18},{28,17},{30,19}} | collective-permute-start | bytes 294920 | tf_op jit(solution)/shard_map/ppermute | solution.py:188
  8.0 9.1 %collective-permute-start.4 = (bf16[2,64,384]{2,1,0:T(8,128)(2,1)S(1)}, bf16[2,64,384]{2,1,0:T(8,128)(2,1)S(1)}, u32[]{:S(2)}, u32[]{:S(2)}) collective-permute-start(bf16[2,64,384]{2,1,0:T(8,128)(2,1)S(1)} %get-tuple-element.67), channel_id=1, source_target_pairs={{2,0},{1,2},{6,1},{5,3},{26,16},{25,18},{30,17},{29,19}} | collective-permute-start | bytes 294920 | tf_op jit(solution)/shard_map/ppermute | solution.py:188
  18.3 12.5 %collective-permute-start.8 = (bf16[176,384]{1,0:T(8,128)(2,1)S(1)}, bf16[176,384]{1,0:T(8,128)(2,1)S(1)}, u32[]{:S(2)}, u32[]{:S(2)}) collective-permute-start(bf16[176,384]{1,0:T(8,128)(2,1)S(1)} %get-tuple-element.83), channel_id=1, source_target_pairs={{0,4},{1,5},{2,6},{3,7},{16,20},{17,21},{18,22},{19,23}} | collective-permute-start | bytes 405512 | tf_op jit(solution)/shard_map/ppermute | solution.py:300
  22.0 9.5 %collective-permute-start.7 = (bf16[176,384]{1,0:T(8,128)(2,1)S(1)}, bf16[176,384]{1,0:T(8,128)(2,1)S(1)}, u32[]{:S(2)}, u32[]{:S(2)}) collective-permute-start(bf16[176,384]{1,0:T(8,128)(2,1)S(1)} %get-tuple-element.82), channel_id=1, source_target_pairs={{0,4},{1,5},{2,6},{3,7},{16,20},{17,21},{18,22},{19,23}} | collective-permute-start | bytes 405512 | tf_op jit(solution)/shard_map/ppermute | solution.py:300
  25.7 6.5 %collective-permute-start.6 = (bf16[176,384]{1,0:T(8,128)(2,1)S(1)}, bf16[176,384]{1,0:T(8,128)(2,1)S(1)}, u32[]{:S(2)}, u32[]{:S(2)}) collective-permute-start(bf16[176,384]{1,0:T(8,128)(2,1)S(1)} %get-tuple-element.81), channel_id=1, source_target_pairs={{0,4},{1,5},{2,6},{3,7},{16,20},{17,21},{18,22},{19,23}} | collective-permute-start | bytes 405512 | tf_op jit(solution)/shard_map/ppermute | solution.py:300
  29.5 3.8 %collective-permute-start.5 = (bf16[176,384]{1,0:T(8,128)(2,1)S(1)}, bf16[176,384]{1,0:T(8,128)(2,1)S(1)}, u32[]{:S(2)}, u32[]{:S(2)}) collective-permute-start(bf16[176,384]{1,0:T(8,128)(2,1)S(1)} %frame.19), channel_id=1, source_target_pairs={{0,4},{1,5},{2,6},{3,7},{16,20},{17,21},{18,22},{19,23}} | collective-permute-start | bytes 405512 | tf_op jit(solution)/shard_map/ppermute | solution.py:300
  30.8 3.2 %collective-permute-start.12 = (bf16[160,384]{1,0:T(8,128)(2,1)S(1)}, bf16[160,384]{1,0:T(8,128)(2,1)S(1)}, u32[]{:S(2)}, u32[]{:S(2)}) collective-permute-start(bf16[160,384]{1,0:T(8,128)(2,1)S(1)} %get-tuple-element.95), channel_id=1, source_target_pairs={{4,8},{5,9},{6,10},{7,11},{20,24},{21,25},{22,26},{23,27}} | collective-permute-start | bytes 368648 | tf_op jit(solution)/shard_map/ppermute | solution.py:300
  31.6 3.2 %collective-permute-start.11 = (bf16[160,384]{1,0:T(8,128)(2,1)S(1)}, bf16[160,384]{1,0:T(8,128)(2,1)S(1)}, u32[]{:S(2)}, u32[]{:S(2)}) collective-permute-start(bf16[160,384]{1,0:T(8,128)(2,1)S(1)} %get-tuple-element.94), channel_id=1, source_target_pairs={{4,8},{5,9},{6,10},{7,11},{20,24},{21,25},{22,26},{23,27}} | collective-permute-start | bytes 368648 | tf_op jit(solution)/shard_map/ppermute | solution.py:300
  32.5 3.0 %collective-permute-start.10 = (bf16[160,384]{1,0:T(8,128)(2,1)S(1)}, bf16[160,384]{1,0:T(8,128)(2,1)S(1)}, u32[]{:S(2)}, u32[]{:S(2)}) collective-permute-start(bf16[160,384]{1,0:T(8,128)(2,1)S(1)} %get-tuple-element.93), channel_id=1, source_target_pairs={{4,8},{5,9},{6,10},{7,11},{20,24},{21,25},{22,26},{23,27}} | collective-permute-start | bytes 368648 | tf_op jit(solution)/shard_map/ppermute | solution.py:300
  33.3 2.9 %collective-permute-start.9 = (bf16[160,384]{1,0:T(8,128)(2,1)S(1)}, bf16[160,384]{1,0:T(8,128)(2,1)S(1)}, u32[]{:S(2)}, u32[]{:S(2)}) collective-permute-start(bf16[160,384]{1,0:T(8,128)(2,1)S(1)} %frame.23), channel_id=1, source_target_pairs={{4,8},{5,9},{6,10},{7,11},{20,24},{21,25},{22,26},{23,27}} | collective-permute-start | bytes 368648 | tf_op jit(solution)/shard_map/ppermute | solution.py:300
  34.0 2.9 %collective-permute-start.16 = (bf16[144,384]{1,0:T(8,128)(2,1)S(1)}, bf16[144,384]{1,0:T(8,128)(2,1)S(1)}, u32[]{:S(2)}, u32[]{:S(2)}) collective-permute-start(bf16[144,384]{1,0:T(8,128)(2,1)S(1)} %get-tuple-element.107), channel_id=1, source_target_pairs={{8,12},{9,13},{10,14},{11,15},{24,28},{25,29},{26,30},{27,31}} | collective-permute-start | bytes 331784 | tf_op jit(solution)/shard_map/ppermute | solution.py:300
  34.8 2.2 %collective-permute-start.15 = (bf16[144,384]{1,0:T(8,128)(2,1)S(1)}, bf16[144,384]{1,0:T(8,128)(2,1)S(1)}, u32[]{:S(2)}, u32[]{:S(2)}) collective-permute-start(bf16[144,384]{1,0:T(8,128)(2,1)S(1)} %get-tuple-element.106), channel_id=1, source_target_pairs={{8,12},{9,13},{10,14},{11,15},{24,28},{25,29},{26,30},{27,31}} | collective-permute-start | bytes 331784 | tf_op jit(solution)/shard_map/ppermute | solution.py:300
  35.5 3.1 %collective-permute-start.14 = (bf16[144,384]{1,0:T(8,128)(2,1)S(1)}, bf16[144,384]{1,0:T(8,128)(2,1)S(1)}, u32[]{:S(2)}, u32[]{:S(2)}) collective-permute-start(bf16[144,384]{1,0:T(8,128)(2,1)S(1)} %get-tuple-element.105), channel_id=1, source_target_pairs={{8,12},{9,13},{10,14},{11,15},{24,28},{25,29},{26,30},{27,31}} | collective-permute-start | bytes 331784 | tf_op jit(solution)/shard_map/ppermute | solution.py:300
  36.3 2.5 %collective-permute-start.13 = (bf16[144,384]{1,0:T(8,128)(2,1)S(1)}, bf16[144,384]{1,0:T(8,128)(2,1)S(1)}, u32[]{:S(2)}, u32[]{:S(2)}) collective-permute-start(bf16[144,384]{1,0:T(8,128)(2,1)S(1)} %frame.27), channel_id=1, source_target_pairs={{8,12},{9,13},{10,14},{11,15},{24,28},{25,29},{26,30},{27,31}} | collective-permute-start | bytes 331784 | tf_op jit(solution)/shard_map/ppermute | solution.py:300
  37.0 1.7 %collective-permute-start.17 = (bf16[2,64,384]{2,1,0:T(8,128)(2,1)S(1)}, bf16[2,64,384]{2,1,0:T(8,128)(2,1)S(1)}, u32[]{:S(2)}, u32[]{:S(2)}) collective-permute-start(bf16[2,64,384]{2,1,0:T(8,128)(2,1)S(1)} %get-tuple-element.121.refs_9_), channel_id=1, source_target_pairs={{12,0},{14,2},{13,4},{15,6}} | collective-permute-start | bytes 294920 | tf_op jit(solution)/shard_map/ppermute | solution.py:222
  37.7 1.0 %collective-permute-start.18 = (bf16[2,64,384]{2,1,0:T(8,128)(2,1)S(1)}, bf16[2,64,384]{2,1,0:T(8,128)(2,1)S(1)}, u32[]{:S(2)}, u32[]{:S(2)}) collective-permute-start(bf16[2,64,384]{2,1,0:T(8,128)(2,1)S(1)} %get-tuple-element.122.refs_10_), channel_id=1, source_target_pairs={{12,1},{14,3},{13,5},{15,7}} | collective-permute-start | bytes 294920 | tf_op jit(solution)/shard_map/ppermute | solution.py:222
  38.8 3.4 %collective-permute-start.19 = (bf16[2,64,384]{2,1,0:T(8,128)(2,1)S(1)}, bf16[2,64,384]{2,1,0:T(8,128)(2,1)S(1)}, u32[]{:S(2)}, u32[]{:S(2)}) collective-permute-start(bf16[2,64,384]{2,1,0:T(8,128)(2,1)S(1)} %get-tuple-element.123), channel_id=1, source_target_pairs={{28,9},{30,11},{29,13},{31,15}} | collective-permute-start | bytes 294920 | tf_op jit(solution)/shard_map/ppermute | solution.py:222
  39.4 2.7 %collective-permute-start.20 = (bf16[2,64,384]{2,1,0:T(8,128)(2,1)S(1)}, bf16[2,64,384]{2,1,0:T(8,128)(2,1)S(1)}, u32[]{:S(2)}, u32[]{:S(2)}) collective-permute-start(bf16[2,64,384]{2,1,0:T(8,128)(2,1)S(1)} %get-tuple-element.124), channel_id=1, source_target_pairs={{28,8},{30,10},{29,12},{31,14}} | collective-permute-start | bytes 294920 | tf_op jit(solution)/shard_map/ppermute | solution.py:222
  40.1 2.0 %collective-permute-start.21 = (bf16[2,64,384]{2,1,0:T(8,128)(2,1)S(1)}, bf16[2,64,384]{2,1,0:T(8,128)(2,1)S(1)}, u32[]{:S(2)}, u32[]{:S(2)}) collective-permute-start(bf16[2,64,384]{2,1,0:T(8,128)(2,1)S(1)} %get-tuple-element.125), channel_id=1, source_target_pairs={{12,17},{14,19},{13,21},{15,23},{28,25},{30,27},{29,29},{31,31}} | collective-permute-start | bytes 294920 | tf_op jit(solution)/shard_map/ppermute | solution.py:222
  40.8 18.0 %collective-permute-start.22 = (bf16[2,64,384]{2,1,0:T(8,128)(2,1)S(1)}, bf16[2,64,384]{2,1,0:T(8,128)(2,1)S(1)}, u32[]{:S(2)}, u32[]{:S(2)}) collective-permute-start(bf16[2,64,384]{2,1,0:T(8,128)(2,1)S(1)} %get-tuple-element.126), channel_id=1, source_target_pairs={{12,16},{14,18},{13,20},{15,22},{28,24},{30,26},{29,28},{31,30}} | collective-permute-start | bytes 294920 | tf_op jit(solution)/shard_map/ppermute | solution.py:222

commit v7 on v6

--- a/solution.py
+++ b/solution.py
@@ -72,15 +72,16 @@
 
 def frame_kernel(cfg, *refs):
     refs = list(refs)
-    groups = [[refs.pop(0) for _ in range(TAPS)] for _ in range(cfg["groups"])]
+    groups = [refs.pop(0) for _ in range(cfg["groups"])]
     received = refs.pop(0) if cfg["came"] is not None else None
     partial, weight, bias, gain = refs[:4]
     refs = refs[4:]
     refs = refs[cfg["passing"] :]
     out = refs.pop(0) if cfg["sends"] else None
-    spread = refs.pop(0) if cfg["later"] else refs.pop()
+    spread = refs.pop(0 if cfg["later"] else -1)
     tails = [refs.pop(0) for _ in range(cfg["finals"])]
-    entry = refs.pop()
+    merged = [refs.pop(0) for _ in range(cfg["keeps"])][cfg["merged"] :][: cfg["finals"]]
+    entry = refs.pop(0)
     cols, window, segments = cfg["cols"], cfg["window"], cfg["segments"]
     channels = entry.shape[-1]
     half = lax.axis_index("band") // cfg["per_half"]
@@ -92,17 +93,17 @@
         if unit == 0:
             step = entry.shape[0] // TAPS
 
-            def place(group):
-                for piece, code in zip(group, cfg["places"]):
-                    number = (code >> (2 * lax.axis_index("band"))) & 3
-                    entry[pl.ds(pl.multiple_of(number * step, step), step), :] = piece[cfg["piece_at"]]
-
-            if len(groups) == 1:
-                place(groups[0])
-            else:
+            def place(piece, code):
+                number = (code >> (2 * lax.axis_index("band"))) & 3
+                entry[pl.ds(pl.multiple_of(number * step, step), step), :] = piece[cfg["piece_at"]]
+
+            pieces, codes = list(groups), list(cfg["places"])
+            if len(pieces) > TAPS:
                 near = lax.axis_index("tm") == cfg["time"]
-                pl.when(near)(functools.partial(place, groups[1]))
-                pl.when(jnp.logical_not(near))(functools.partial(place, groups[0]))
+                pl.when(near)(functools.partial(place, pieces.pop(0), codes[0]))
+                pl.when(jnp.logical_not(near))(functools.partial(place, pieces.pop(0), codes.pop(0)))
+            for piece, code in zip(pieces, codes):
+                place(piece, code)
             source, skip = entry, 0
         else:
             source, skip = received, half * (unit - 1 - cfg["came"])
@@ -129,6 +130,11 @@
             for number, tail in enumerate(tails):
                 tail[cfg["tail_at"]] = value[number * length : (number + 1) * length]
 
+            @pl.when(lax.axis_index("tm") == 0)
+            def _():
+                for tail, ref in zip(tails, merged):
+                    ref[...] = tail[...]
+
     for unit in cfg["units"]:
         pl.when(on_unit(unit, cfg["holders"]))(functools.partial(run, unit))
 
@@ -187,14 +193,13 @@
         assert len({a for a, _ in routes}) == len({b for _, b in routes}) == len(routes)
         return lax.ppermute(mine, MESH_AXES, routes)
 
-    sides = [(t, clip) for t in range(holders) for clip in range(clips)]
-    beside = [(t, clip) for t, clip in sides if clip // per_half == t]
-    across = [(t, clip) for t, clip in sides if clip // per_half != t]
-    far_group = [gather(number, across) for number in range(TAPS)]
-    near_group = [own] + [gather(number, beside) for number in (1, 2)]
-    entries = [[far_group, near_group]] * holders
-    for t in range(holders, times):
-        entries.append([[gather(number, [(t, clip) for clip in range(clips)]) for number in range(TAPS)]])
+    across = [(t, clip) for t in range(holders) for clip in range(clips) if clip // per_half != t]
+    crossed = gather(0, across)
+    entries = []
+    for t in range(times):
+        members = [(t, clip) for clip in range(clips)]
+        first = [own, crossed] if t < holders else [gather(0, members)]
+        entries.append(first + [gather(number, members) for number in (1, 2)])
 
     stored = [conv_weight[0].reshape(TAPS, TAPS * TAPS * channels, channels), conv_bias, norm_gain]
     now, past, bias, gain = pl.pallas_call(
@@ -213,12 +218,13 @@
     )(*[pltpu.with_memory_space_constraint(value, pltpu.HBM) for value in stored])
     now, past, bias, gain = (resident(value) for value in (now, past, bias, gain))
 
-    def leave(value, there, index, group):
+    def leave(value, members):
         routes = []
-        for clip in group:
+        for there, index, clip in members:
             for h in range(HALVES):
                 t, b = stream(clip, h)
                 routes.append((spot(t, segments - 1, b), spot(there, clip, h * per_half + index)))
+        assert len({a for a, _ in routes}) == len({b for _, b in routes}) == len(routes)
         return lax.ppermute(value, MESH_AXES, routes)
 
     state = ((window - 1) * cols, channels)
@@ -236,6 +242,7 @@
         last = slot - lag * (segments - 1)
         finals = per_half if last >= 0 else 0
         middle = finals and last % own_frames > 0
+        keeps = len(landed) + len(waiting) if slot + 1 == slots else 0
         cfg = dict(
             units=units,
             later=[s for s in units if slot - lag * s < frames - 1],
@@ -248,7 +255,9 @@
             came=min(working(slot - lag, frames, segments, lag)) if slot >= lag else None,
             finals=finals,
             tail_at=last % own_frames,
-            passing=(finals if middle else 0) + (len(landed) + len(waiting) if slot + 1 == slots else 0),
+            passing=(finals if middle else 0) + keeps,
+            keeps=keeps,
+            merged=len(landed),
             cols=cols,
             window=window,
             segments=segments,
@@ -257,7 +266,7 @@
         )
         operands = []
         if slot < frames:
-            operands += [resident(value) for group in entries[slot // own_frames] for value in group]
+            operands += [resident(value) for value in entries[slot // own_frames]]
         if slot >= lag:
             operands.append(resident(moving.pop(slot - lag)))
         operands += [resident(near), now, bias, gain]
@@ -275,7 +284,7 @@
                 operands.append(resident(value))
         shapes += [shape] * finals
         held = list(landed) if slot + 1 == slots else []
-        kept = [landed[key] for key in held] + ([value for _, _, value in waiting] if held else [])
+        kept = [landed[key][0] for key in held] + ([value for _, _, value in waiting] if held else [])
         for value in kept:
             aliases[len(operands)] = len(shapes)
             operands.append(resident(value))
@@ -300,17 +309,27 @@
             moving[slot] = lax.ppermute(out, "segment", [(s, s + 1) for s in senders_now])
         if slot + 1 == slots:
             kept = results[finals:]
-            landed.update(zip(held, kept))
+            landed.update({key: [value] for key, value in zip(held, kept)})
             waiting = [(there, index, value) for (there, index, _), value in zip(waiting, kept[len(held) :])]
         if finals and last % own_frames == own_frames - 1:
             there = last // own_frames
             final = there == times - 1
-            for index, value in enumerate(tails):
-                landed[there, index, 0] = leave(value, there, index, range(clips if final else per_half))
-            waiting += [] if final else [(there, index, value) for index, value in enumerate(tails)]
-            if final:
-                for there, index, value in waiting:
-                    landed[there, index, 1] = leave(value, there, index, range(per_half, clips))
+            if not final:
+                for index, value in enumerate(tails):
+                    landed[there, index] = [leave(value, [(there, index, clip) for clip in range(per_half)])]
+                waiting += [(there, index, value) for index, value in enumerate(tails)]
+            else:
+                late = range(per_half, clips)
+                pairs_left = [((there, index, value), waiting.pop(0)) for index, value in enumerate(tails)]
+                for (_, index, _), (before, _, value) in pairs_left:
+                    both = [(there, index, clip) for clip in range(per_half)] + [(before, index, clip) for clip in late]
+                    sent = leave(value, both)
+                    landed[there, index] = [sent]
+                    landed[before, index].append(sent)
+                for before, index, value in waiting:
+                    landed[before, index].append(leave(value, [(before, index, clip) for clip in late]))
+                for (_, index, value), _ in pairs_left:
+                    landed[there, index].append(leave(value, [(there, index, clip) for clip in late]))
         if cfg["later"]:
             near, far = pl.pallas_call(
                 functools.partial(history_kernel, cfg),
@@ -324,10 +343,9 @@
             )(resident(spread), resident(near), resident(far), past)
 
     result = None
-    for (t, index, part), value in landed.items():
+    for (t, index), (early, late) in landed.items():
         here = jnp.logical_and(time == t, band % per_half == index)
-        if t < times - 1:
-            here = jnp.logical_and(here, (position >= per_half) == (part == 1))
+        value = jnp.where(position < per_half, early, late)
         result = value if result is None else jnp.where(here, value, result)
     return result.reshape(1, own_frames, own_rows, cols, channels)
 

time: 59.9 us -> 57.5 us (0.960)
  waiting for transfers between devices: 21.2 us -> 18.5 us
    ppermute x5, waiting for transfers between devices: 4.37 us -> 1.89 us  [gather(): return lax.ppermute(mine, MESH_AXES, routes)]
  transfers between devices with their start and end apart: 23 -> 23, of which waited for: 6 -> 4; matrix products, arithmetic and copies ran while one was open for 0% -> 0% of each run, Pallas kernels for 19% -> 22%
where the time goes in v7:
time: 57.5 us; the launch traced here: 57.1 us
  starting transfers between devices  23.7 us (41%)
  waiting for transfers between devices  18.5 us (32%)
  Pallas kernels  13.6 us (24%)
  other arithmetic  0.68 us (1%)
  between operations  0.59 us (1%)
    ppermute x6, waiting for transfers between devices, leave(): return lax.ppermute(value, MESH_AXES, routes)  16.5 us
    ppermute x12, starting transfers between devices, local(): lax.ppermute(out, 'segment', [(s, s + 1) for s in senders_now])  10.8 us
    ppermute x5, starting transfers between devices, gather(): return lax.ppermute(mine, MESH_AXES, routes)  8.27 us
    pallas_call x16, Pallas kernels, local(): pl.pallas_call(functools.partial(frame_kernel, cfg), out_shape=shapes, in...  5.05 us
    ppermute x6, starting transfers between devices, leave(): return lax.ppermute(value, MESH_AXES, routes)  4.63 us
    pallas_call x12, Pallas kernels, local(): pl.pallas_call(functools.partial(history_kernel, cfg), out_shape=[pltpu.V...  4.14 us
    pallas_call x1, Pallas kernels, local(): pl.pallas_call(loader_kernel, out_shape=[pltpu.VMEM((TAPS * TAPS * channe...  3.42 us
    ppermute x5, waiting for transfers between devices, gather(): return lax.ppermute(mine, MESH_AXES, routes)  1.89 us
  transfers between devices with their start and end apart: 23, of which 4 were waited for; matrix products, arithmetic and copies ran while one was open for 0% of the time, Pallas kernels for 22%

profile of v7, /device:TPU:6, one launch (start us, length us, event | category | flops | bytes accessed | tf_op | source)
XLA Modules:
  0.0 57.1 jit_solution(8751289866379049706)
XLA Ops:
  0.0 1.0 %pick.1 = (bf16[2,64,384]{2,1,0:T(8,128)(2,1)S(1)}, bf16[2,64,384]{2,1,0:T(8,128)(2,1)S(1)}) custom-call(bf16[4,2,64,384]{3,2,1,0:T(8,128)(2,1)} %bitcast.4), custom_call_target="tpu_custom_call" | custom-call | tf_op jit(solution)/shard_map/pick/pallas_call | solution.py:175
  1.0 2.5 %collective-permute-start = (bf16[2,64,384]{2,1,0:T(8,128)(2,1)S(1)}, bf16[2,64,384]{2,1,0:T(8,128)(2,1)S(1)}, u32[]{:S(2)}, u32[]{:S(2)}) collective-permute-start(bf16[2,64,384]{2,1,0:T(8,128)(2,1)S(1)} %get-tuple-element.68), channel_id=1, source_target_pairs={{8,16},{10,18},{13,17},{15,19},{16,0},{18,2},{21,1},{23,3}} | collective-permute-start | bytes 294920 | tf_op jit(solution)/shard_map/ppermute | solution.py:194
  3.4 1.3 %collective-permute-start.3 = (bf16[2,64,384]{2,1,0:T(8,128)(2,1)S(1)}, bf16[2,64,384]{2,1,0:T(8,128)(2,1)S(1)}, u32[]{:S(2)}, u32[]{:S(2)}) collective-permute-start(bf16[2,64,384]{2,1,0:T(8,128)(2,1)S(1)} %get-tuple-element.68), channel_id=1, source_target_pairs={{1,0},{3,2},{4,1},{6,3},{9,16},{11,18},{12,17},{14,19}} | collective-permute-start | bytes 294920 | tf_op jit(solution)/shard_map/ppermute | solution.py:194
  4.7 1.3 %collective-permute-start.4 = (bf16[2,64,384]{2,1,0:T(8,128)(2,1)S(1)}, bf16[2,64,384]{2,1,0:T(8,128)(2,1)S(1)}, u32[]{:S(2)}, u32[]{:S(2)}) collective-permute-start(bf16[2,64,384]{2,1,0:T(8,128)(2,1)S(1)} %get-tuple-element.68), channel_id=1, source_target_pairs={{2,0},{1,2},{6,1},{5,3},{10,16},{9,18},{14,17},{13,19}} | collective-permute-start | bytes 294920 | tf_op jit(solution)/shard_map/ppermute | solution.py:194
  6.0 1.3 %collective-permute-start.1 = (bf16[2,64,384]{2,1,0:T(8,128)(2,1)S(1)}, bf16[2,64,384]{2,1,0:T(8,128)(2,1)S(1)}, u32[]{:S(2)}, u32[]{:S(2)}) collective-permute-start(bf16[2,64,384]{2,1,0:T(8,128)(2,1)S(1)} %get-tuple-element.68), channel_id=1, source_target_pairs={{17,0},{19,2},{20,1},{22,3},{25,16},{27,18},{28,17},{30,19}} | collective-permute-start | bytes 294920 | tf_op jit(solution)/shard_map/ppermute | solution.py:194
  7.3 1.9 %collective-permute-start.2 = (bf16[2,64,384]{2,1,0:T(8,128)(2,1)S(1)}, bf16[2,64,384]{2,1,0:T(8,128)(2,1)S(1)}, u32[]{:S(2)}, u32[]{:S(2)}) collective-permute-start(bf16[2,64,384]{2,1,0:T(8,128)(2,1)S(1)} %get-tuple-element.68), channel_id=1, source_target_pairs={{18,0},{17,2},{22,1},{21,3},{26,16},{25,18},{30,17},{29,19}} | collective-permute-start | bytes 294920 | tf_op jit(solution)/shard_map/ppermute | solution.py:194
  9.3 3.4 %loader.1 = (bf16[3456,384]{1,0:T(8,128)(2,1)S(1)}, bf16[3456,768]{1,0:T(8,128)(2,1)S(1)}, f32[1,384]{1,0:T(1,128)S(1)}, f32[1,384]{1,0:T(1,128)S(1)}) custom-call(bf16[3,3456,384]{2,1,0:T(8,128)(2,1)} %bitcast.3, f32[1,384]{1,0:T(1,128)} %bias.1, f32[1,384]{1,0:T(1,128)} %gain.1), custom_call_target="tpu_custom_call" | custom-call | tf_op jit(solution)/shard_map/loader/pallas_call | solution.py:205
  12.7 1.6 %collective-permute-done.3.refs_2_ = bf16[2,64,384]{2,1,0:T(8,128)(2,1)S(1)} collective-permute-done((bf16[2,64,384]{2,1,0:T(8,128)(2,1)S(1)}, bf16[2,64,384]{2,1,0:T(8,128)(2,1)S(1)}, u32[]{:S(2)}, u32[]{:S(2)}) %collective-permute-start.3) | collective-permute-done | bytes 98336 | tf_op jit(solution)/shard_map/ppermute | solution.py:194
  14.6 1.2 %frame.16 = (bf16[176,384]{1,0:T(8,128)(2,1)S(1)}, bf16[224,1152]{1,0:T(8,128)(2,1)S(1)}) custom-call(bf16[2,64,384]{2,1,0:T(8,128)(2,1)S(1)} %get-tuple-element.67.refs_0_, bf16[2,64,384]{2,1,0:T(8,128)(2,1)S(1)} %collective-permute-done.refs_1_, bf16[2,64,384]{2,1,0:T(8,128)(2,1)S(1)} %collective-permute-done.3.refs_2_, ...), custom_call_target="tpu_custom_call" | custom-call | bytes 1024 | tf_op jit(solution)/shard_map/frame/pallas_call | solution.py:293
  15.8 1.6 %collective-permute-start.8 = (bf16[176,384]{1,0:T(8,128)(2,1)S(1)}, bf16[176,384]{1,0:T(8,128)(2,1)S(1)}, u32[]{:S(2)}, u32[]{:S(2)}) collective-permute-start(bf16[176,384]{1,0:T(8,128)(2,1)S(1)} %get-tuple-element.83), channel_id=1, source_target_pairs={{0,4},{1,5},{2,6},{3,7},{16,20},{17,21},{18,22},{19,23}} | collective-permute-start | bytes 405512 | tf_op jit(solution)/shard_map/ppermute | solution.py:309
  17.4 1.2 %history.12 = (f32[176,384]{1,0:T(8,128)S(1)}, f32[176,384]{1,0:T(8,128)S(1)}) custom-call(bf16[224,1152]{1,0:T(8,128)(2,1)S(1)} %get-tuple-element.72.spread, f32[176,384]{1,0:T(8,128)S(1)} %broadcast_1_refs_4__near_far.2.refs_4_.near, f32[176,384]{1,0:T(8,128)S(1)} %broadcast_1_refs_4__near_far.2.clone.far, ...), custom_call_target="tpu_custom_call", output_to_operand_aliasing={{0}: (1, {}), {1}: (2, {})} | custom-call | bytes 1024 | tf_op jit(solution)/shard_map/history/pallas_call | solution.py:334
  18.6 1.2 %frame.17 = (bf16[176,384]{1,0:T(8,128)(2,1)S(1)}, bf16[224,1152]{1,0:T(8,128)(2,1)S(1)}) custom-call(bf16[2,64,384]{2,1,0:T(8,128)(2,1)S(1)} %get-tuple-element.67.refs_0_, bf16[2,64,384]{2,1,0:T(8,128)(2,1)S(1)} %collective-permute-done.refs_1_, bf16[2,64,384]{2,1,0:T(8,128)(2,1)S(1)} %collective-permute-done.3.refs_2_, ...), custom_call_target="tpu_custom_call" | custom-call | bytes 1024 | tf_op jit(solution)/shard_map/frame/pallas_call | solution.py:293
  19.8 1.3 %collective-permute-start.7 = (bf16[176,384]{1,0:T(8,128)(2,1)S(1)}, bf16[176,384]{1,0:T(8,128)(2,1)S(1)}, u32[]{:S(2)}, u32[]{:S(2)}) collective-permute-start(bf16[176,384]{1,0:T(8,128)(2,1)S(1)} %get-tuple-element.82), channel_id=1, source_target_pairs={{0,4},{1,5},{2,6},{3,7},{16,20},{17,21},{18,22},{19,23}} | collective-permute-start | bytes 405512 | tf_op jit(solution)/shard_map/ppermute | solution.py:309
  21.1 1.2 %history.13 = (f32[176,384]{1,0:T(8,128)S(1)}, f32[176,384]{1,0:T(8,128)S(1)}) custom-call(bf16[224,1152]{1,0:T(8,128)(2,1)S(1)} %get-tuple-element.75.spread, f32[176,384]{1,0:T(8,128)S(1)} %get-tuple-element.74.refs_4_.near, f32[176,384]{1,0:T(8,128)S(1)} %get-tuple-element.76.far, ...), custom_call_target="tpu_custom_call", output_to_operand_aliasing={{0}: (1, {}), {1}: (2, {})} | custom-call | bytes 1024 | tf_op jit(solution)/shard_map/history/pallas_call | solution.py:334
  22.4 1.2 %frame.18 = (bf16[176,384]{1,0:T(8,128)(2,1)S(1)}, bf16[224,1152]{1,0:T(8,128)(2,1)S(1)}) custom-call(bf16[2,64,384]{2,1,0:T(8,128)(2,1)S(1)} %get-tuple-element.67.refs_0_, bf16[2,64,384]{2,1,0:T(8,128)(2,1)S(1)} %collective-permute-done.refs_1_, bf16[2,64,384]{2,1,0:T(8,128)(2,1)S(1)} %collective-permute-done.1.refs_2_, ...), custom_call_target="tpu_custom_call" | custom-call | bytes 1024 | tf_op jit(solution)/shard_map/frame/pallas_call | solution.py:293
  23.5 1.3 %collective-permute-start.6 = (bf16[176,384]{1,0:T(8,128)(2,1)S(1)}, bf16[176,384]{1,0:T(8,128)(2,1)S(1)}, u32[]{:S(2)}, u32[]{:S(2)}) collective-permute-start(bf16[176,384]{1,0:T(8,128)(2,1)S(1)} %get-tuple-element.81), channel_id=1, source_target_pairs={{0,4},{1,5},{2,6},{3,7},{16,20},{17,21},{18,22},{19,23}} | collective-permute-start | bytes 405512 | tf_op jit(solution)/shard_map/ppermute | solution.py:309
  24.8 1.3 %history.14 = (f32[176,384]{1,0:T(8,128)S(1)}, f32[176,384]{1,0:T(8,128)S(1)}) custom-call(bf16[224,1152]{1,0:T(8,128)(2,1)S(1)} %get-tuple-element.78.spread, f32[176,384]{1,0:T(8,128)S(1)} %get-tuple-element.77.refs_4_.near, f32[176,384]{1,0:T(8,128)S(1)} %get-tuple-element.79.far, ...), custom_call_target="tpu_custom_call", output_to_operand_aliasing={{0}: (1, {}), {1}: (2, {})} | custom-call | bytes 1024 | tf_op jit(solution)/shard_map/history/pallas_call | solution.py:334
  26.1 1.2 %frame.19 = bf16[176,384]{1,0:T(8,128)(2,1)S(1)} custom-call(bf16[2,64,384]{2,1,0:T(8,128)(2,1)S(1)} %get-tuple-element.67.refs_0_, bf16[2,64,384]{2,1,0:T(8,128)(2,1)S(1)} %collective-permute-done.refs_1_, bf16[2,64,384]{2,1,0:T(8,128)(2,1)S(1)} %collective-permute-done.1.refs_2_, bf16[2,64,384]{2,1,0:T(8,128)(2,1)S(1)} %collective-permute-done.2.refs_3_, ...), custom_call_target="tpu_custom_call" | custom-call | bytes 1024 | tf_op jit(solution)/shard_map/frame/pallas_call | solution.py:293
  27.3 1.3 %collective-permute-start.5 = (bf16[176,384]{1,0:T(8,128)(2,1)S(1)}, bf16[176,384]{1,0:T(8,128)(2,1)S(1)}, u32[]{:S(2)}, u32[]{:S(2)}) collective-permute-start(bf16[176,384]{1,0:T(8,128)(2,1)S(1)} %frame.19), channel_id=1, source_target_pairs={{0,4},{1,5},{2,6},{3,7},{16,20},{17,21},{18,22},{19,23}} | collective-permute-start | bytes 405512 | tf_op jit(solution)/shard_map/ppermute | solution.py:309
  28.6 0.7 %collective-permute-start.12 = (bf16[160,384]{1,0:T(8,128)(2,1)S(1)}, bf16[160,384]{1,0:T(8,128)(2,1)S(1)}, u32[]{:S(2)}, u32[]{:S(2)}) collective-permute-start(bf16[160,384]{1,0:T(8,128)(2,1)S(1)} %get-tuple-element.95), channel_id=1, source_target_pairs={{4,8},{5,9},{6,10},{7,11},{20,24},{21,25},{22,26},{23,27}} | collective-permute-start | bytes 368648 | tf_op jit(solution)/shard_map/ppermute | solution.py:309
  29.3 0.7 %collective-permute-start.11 = (bf16[160,384]{1,0:T(8,128)(2,1)S(1)}, bf16[160,384]{1,0:T(8,128)(2,1)S(1)}, u32[]{:S(2)}, u32[]{:S(2)}) collective-permute-start(bf16[160,384]{1,0:T(8,128)(2,1)S(1)} %get-tuple-element.94), channel_id=1, source_target_pairs={{4,8},{5,9},{6,10},{7,11},{20,24},{21,25},{22,26},{23,27}} | collective-permute-start | bytes 368648 | tf_op jit(solution)/shard_map/ppermute | solution.py:309
  30.3 0.7 %collective-permute-start.10 = (bf16[160,384]{1,0:T(8,128)(2,1)S(1)}, bf16[160,384]{1,0:T(8,128)(2,1)S(1)}, u32[]{:S(2)}, u32[]{:S(2)}) collective-permute-start(bf16[160,384]{1,0:T(8,128)(2,1)S(1)} %get-tuple-element.93), channel_id=1, source_target_pairs={{4,8},{5,9},{6,10},{7,11},{20,24},{21,25},{22,26},{23,27}} | collective-permute-start | bytes 368648 | tf_op jit(solution)/shard_map/ppermute | solution.py:309
  31.8 0.7 %collective-permute-start.16 = (bf16[144,384]{1,0:T(8,128)(2,1)S(1)}, bf16[144,384]{1,0:T(8,128)(2,1)S(1)}, u32[]{:S(2)}, u32[]{:S(2)}) collective-permute-start(bf16[144,384]{1,0:T(8,128)(2,1)S(1)} %get-tuple-element.107), channel_id=1, source_target_pairs={{8,12},{9,13},{10,14},{11,15},{24,28},{25,29},{26,30},{27,31}} | collective-permute-start | bytes 331784 | tf_op jit(solution)/shard_map/ppermute | solution.py:309
  32.5 0.7 %collective-permute-start.15 = (bf16[144,384]{1,0:T(8,128)(2,1)S(1)}, bf16[144,384]{1,0:T(8,128)(2,1)S(1)}, u32[]{:S(2)}, u32[]{:S(2)}) collective-permute-start(bf16[144,384]{1,0:T(8,128)(2,1)S(1)} %get-tuple-element.106), channel_id=1, source_target_pairs={{8,12},{9,13},{10,14},{11,15},{24,28},{25,29},{26,30},{27,31}} | collective-permute-start | bytes 331784 | tf_op jit(solution)/shard_map/ppermute | solution.py:309
  33.3 0.7 %collective-permute-start.14 = (bf16[144,384]{1,0:T(8,128)(2,1)S(1)}, bf16[144,384]{1,0:T(8,128)(2,1)S(1)}, u32[]{:S(2)}, u32[]{:S(2)}) collective-permute-start(bf16[144,384]{1,0:T(8,128)(2,1)S(1)} %get-tuple-element.105), channel_id=1, source_target_pairs={{8,12},{9,13},{10,14},{11,15},{24,28},{25,29},{26,30},{27,31}} | collective-permute-start | bytes 331784 | tf_op jit(solution)/shard_map/ppermute | solution.py:309
  34.0 0.7 %collective-permute-start.13 = (bf16[144,384]{1,0:T(8,128)(2,1)S(1)}, bf16[144,384]{1,0:T(8,128)(2,1)S(1)}, u32[]{:S(2)}, u32[]{:S(2)}) collective-permute-start(bf16[144,384]{1,0:T(8,128)(2,1)S(1)} %frame.27), channel_id=1, source_target_pairs={{8,12},{9,13},{10,14},{11,15},{24,28},{25,29},{26,30},{27,31}} | collective-permute-start | bytes 331784 | tf_op jit(solution)/shard_map/ppermute | solution.py:309
  34.8 0.7 %collective-permute-start.17 = (bf16[2,64,384]{2,1,0:T(8,128)(2,1)S(1)}, bf16[2,64,384]{2,1,0:T(8,128)(2,1)S(1)}, u32[]{:S(2)}, u32[]{:S(2)}) collective-permute-start(bf16[2,64,384]{2,1,0:T(8,128)(2,1)S(1)} %get-tuple-element.121.refs_9_), channel_id=1, source_target_pairs={{12,0},{14,2},{13,4},{15,6}} | collective-permute-start | bytes 294920 | tf_op jit(solution)/shard_map/ppermute | solution.py:228
  35.5 0.7 %collective-permute-start.18 = (bf16[2,64,384]{2,1,0:T(8,128)(2,1)S(1)}, bf16[2,64,384]{2,1,0:T(8,128)(2,1)S(1)}, u32[]{:S(2)}, u32[]{:S(2)}) collective-permute-start(bf16[2,64,384]{2,1,0:T(8,128)(2,1)S(1)} %get-tuple-element.122.refs_10_), channel_id=1, source_target_pairs={{12,1},{14,3},{13,5},{15,7}} | collective-permute-start | bytes 294920 | tf_op jit(solution)/shard_map/ppermute | solution.py:228
  36.5 0.7 %collective-permute-start.19 = (bf16[2,64,384]{2,1,0:T(8,128)(2,1)S(1)}, bf16[2,64,384]{2,1,0:T(8,128)(2,1)S(1)}, u32[]{:S(2)}, u32[]{:S(2)}) collective-permute-start(bf16[2,64,384]{2,1,0:T(8,128)(2,1)S(1)} %get-tuple-element.123), channel_id=1, source_target_pairs={{12,17},{14,19},{13,21},{15,23},{28,9},{30,11},{29,13},{31,15}} | collective-permute-start | bytes 294920 | tf_op jit(solution)/shard_map/ppermute | solution.py:228
  37.9 1.3 %collective-permute-start.21 = (bf16[2,64,384]{2,1,0:T(8,128)(2,1)S(1)}, bf16[2,64,384]{2,1,0:T(8,128)(2,1)S(1)}, u32[]{:S(2)}, u32[]{:S(2)}) collective-permute-start(bf16[2,64,384]{2,1,0:T(8,128)(2,1)S(1)} %get-tuple-element.125), channel_id=1, source_target_pairs={{12,16},{14,18},{13,20},{15,22},{28,8},{30,10},{29,12},{31,14}} | collective-permute-start | bytes 294920 | tf_op jit(solution)/shard_map/ppermute | solution.py:228
  39.9 16.5 %collective-permute-done.21 = bf16[2,64,384]{2,1,0:T(8,128)(2,1)S(1)} collective-permute-done((bf16[2,64,384]{2,1,0:T(8,128)(2,1)S(1)}, bf16[2,64,384]{2,1,0:T(8,128)(2,1)S(1)}, u32[]{:S(2)}, u32[]{:S(2)}) %collective-permute-start.21) | collective-permute-done | bytes 98336 | tf_op jit(solution)/shard_map/ppermute | solution.py:228
  56.4 0.7 %select_select_fusion = bf16[2,64,384]{2,1,0:T(8,128)(2,1)} fusion(bf16[2,64,384]{2,1,0:T(8,128)(2,1)S(1)} %get-tuple-element.128, bf16[2,64,384]{2,1,0:T(8,128)(2,1)S(1)} %collective-permute-done.21, bf16[2,64,384]{2,1,0:T(8,128)(2,1)S(1)} %get-tuple-element.127, bf16[2,64,384]{2,1,0:T(8,128)(2,1)S(1)} %collective-permute-done.19, ...), kind=kLoop, calls=%fused_computation | loop fusion | flops 344064 | bytes 688132 | tf_op jit(solution)/shard_map/jit(_where)/select_n | solution.py:349
  (47 shorter events, 3.3 us)
Async XLA Ops:
  1.0 11.7 %collective-permute-start = (bf16[2,64,384]{2,1,0:T(8,128)(2,1)S(1)}, bf16[2,64,384]{2,1,0:T(8,128)(2,1)S(1)}, u32[]{:S(2)}, u32[]{:S(2)}) collective-permute-start(bf16[2,64,384]{2,1,0:T(8,128)(2,1)S(1)} %get-tuple-element.68), channel_id=1, source_target_pairs={{8,16},{10,18},{13,17},{15,19},{16,0},{18,2},{21,1},{23,3}} | collective-permute-start | bytes 294920 | tf_op jit(solution)/shard_map/ppermute | solution.py:194
  3.4 10.8 %collective-permute-start.3 = (bf16[2,64,384]{2,1,0:T(8,128)(2,1)S(1)}, bf16[2,64,384]{2,1,0:T(8,128)(2,1)S(1)}, u32[]{:S(2)}, u32[]{:S(2)}) collective-permute-start(bf16[2,64,384]{2,1,0:T(8,128)(2,1)S(1)} %get-tuple-element.68), channel_id=1, source_target_pairs={{1,0},{3,2},{4,1},{6,3},{9,16},{11,18},{12,17},{14,19}} | collective-permute-start | bytes 294920 | tf_op jit(solution)/shard_map/ppermute | solution.py:194
  4.7 9.8 %collective-permute-start.4 = (bf16[2,64,384]{2,1,0:T(8,128)(2,1)S(1)}, bf16[2,64,384]{2,1,0:T(8,128)(2,1)S(1)}, u32[]{:S(2)}, u32[]{:S(2)}) collective-permute-start(bf16[2,64,384]{2,1,0:T(8,128)(2,1)S(1)} %get-tuple-element.68), channel_id=1, source_target_pairs={{2,0},{1,2},{6,1},{5,3},{10,16},{9,18},{14,17},{13,19}} | collective-permute-start | bytes 294920 | tf_op jit(solution)/shard_map/ppermute | solution.py:194
  6.0 16.3 %collective-permute-start.1 = (bf16[2,64,384]{2,1,0:T(8,128)(2,1)S(1)}, bf16[2,64,384]{2,1,0:T(8,128)(2,1)S(1)}, u32[]{:S(2)}, u32[]{:S(2)}) collective-permute-start(bf16[2,64,384]{2,1,0:T(8,128)(2,1)S(1)} %get-tuple-element.68), channel_id=1, source_target_pairs={{17,0},{19,2},{20,1},{22,3},{25,16},{27,18},{28,17},{30,19}} | collective-permute-start | bytes 294920 | tf_op jit(solution)/shard_map/ppermute | solution.py:194
  7.3 15.0 %collective-permute-start.2 = (bf16[2,64,384]{2,1,0:T(8,128)(2,1)S(1)}, bf16[2,64,384]{2,1,0:T(8,128)(2,1)S(1)}, u32[]{:S(2)}, u32[]{:S(2)}) collective-permute-start(bf16[2,64,384]{2,1,0:T(8,128)(2,1)S(1)} %get-tuple-element.68), channel_id=1, source_target_pairs={{18,0},{17,2},{22,1},{21,3},{26,16},{25,18},{30,17},{29,19}} | collective-permute-start | bytes 294920 | tf_op jit(solution)/shard_map/ppermute | solution.py:194
  15.8 12.8 %collective-permute-start.8 = (bf16[176,384]{1,0:T(8,128)(2,1)S(1)}, bf16[176,384]{1,0:T(8,128)(2,1)S(1)}, u32[]{:S(2)}, u32[]{:S(2)}) collective-permute-start(bf16[176,384]{1,0:T(8,128)(2,1)S(1)} %get-tuple-element.83), channel_id=1, source_target_pairs={{0,4},{1,5},{2,6},{3,7},{16,20},{17,21},{18,22},{19,23}} | collective-permute-start | bytes 405512 | tf_op jit(solution)/shard_map/ppermute | solution.py:309
  19.8 9.5 %collective-permute-start.7 = (bf16[176,384]{1,0:T(8,128)(2,1)S(1)}, bf16[176,384]{1,0:T(8,128)(2,1)S(1)}, u32[]{:S(2)}, u32[]{:S(2)}) collective-permute-start(bf16[176,384]{1,0:T(8,128)(2,1)S(1)} %get-tuple-element.82), channel_id=1, source_target_pairs={{0,4},{1,5},{2,6},{3,7},{16,20},{17,21},{18,22},{19,23}} | collective-permute-start | bytes 405512 | tf_op jit(solution)/shard_map/ppermute | solution.py:309
  23.5 6.5 %collective-permute-start.6 = (bf16[176,384]{1,0:T(8,128)(2,1)S(1)}, bf16[176,384]{1,0:T(8,128)(2,1)S(1)}, u32[]{:S(2)}, u32[]{:S(2)}) collective-permute-start(bf16[176,384]{1,0:T(8,128)(2,1)S(1)} %get-tuple-element.81), channel_id=1, source_target_pairs={{0,4},{1,5},{2,6},{3,7},{16,20},{17,21},{18,22},{19,23}} | collective-permute-start | bytes 405512 | tf_op jit(solution)/shard_map/ppermute | solution.py:309
  27.3 3.8 %collective-permute-start.5 = (bf16[176,384]{1,0:T(8,128)(2,1)S(1)}, bf16[176,384]{1,0:T(8,128)(2,1)S(1)}, u32[]{:S(2)}, u32[]{:S(2)}) collective-permute-start(bf16[176,384]{1,0:T(8,128)(2,1)S(1)} %frame.19), channel_id=1, source_target_pairs={{0,4},{1,5},{2,6},{3,7},{16,20},{17,21},{18,22},{19,23}} | collective-permute-start | bytes 405512 | tf_op jit(solution)/shard_map/ppermute | solution.py:309
  28.6 3.2 %collective-permute-start.12 = (bf16[160,384]{1,0:T(8,128)(2,1)S(1)}, bf16[160,384]{1,0:T(8,128)(2,1)S(1)}, u32[]{:S(2)}, u32[]{:S(2)}) collective-permute-start(bf16[160,384]{1,0:T(8,128)(2,1)S(1)} %get-tuple-element.95), channel_id=1, source_target_pairs={{4,8},{5,9},{6,10},{7,11},{20,24},{21,25},{22,26},{23,27}} | collective-permute-start | bytes 368648 | tf_op jit(solution)/shard_map/ppermute | solution.py:309
  29.3 3.2 %collective-permute-start.11 = (bf16[160,384]{1,0:T(8,128)(2,1)S(1)}, bf16[160,384]{1,0:T(8,128)(2,1)S(1)}, u32[]{:S(2)}, u32[]{:S(2)}) collective-permute-start(bf16[160,384]{1,0:T(8,128)(2,1)S(1)} %get-tuple-element.94), channel_id=1, source_target_pairs={{4,8},{5,9},{6,10},{7,11},{20,24},{21,25},{22,26},{23,27}} | collective-permute-start | bytes 368648 | tf_op jit(solution)/shard_map/ppermute | solution.py:309
  30.3 3.0 %collective-permute-start.10 = (bf16[160,384]{1,0:T(8,128)(2,1)S(1)}, bf16[160,384]{1,0:T(8,128)(2,1)S(1)}, u32[]{:S(2)}, u32[]{:S(2)}) collective-permute-start(bf16[160,384]{1,0:T(8,128)(2,1)S(1)} %get-tuple-element.93), channel_id=1, source_target_pairs={{4,8},{5,9},{6,10},{7,11},{20,24},{21,25},{22,26},{23,27}} | collective-permute-start | bytes 368648 | tf_op jit(solution)/shard_map/ppermute | solution.py:309
  31.1 2.9 %collective-permute-start.9 = (bf16[160,384]{1,0:T(8,128)(2,1)S(1)}, bf16[160,384]{1,0:T(8,128)(2,1)S(1)}, u32[]{:S(2)}, u32[]{:S(2)}) collective-permute-start(bf16[160,384]{1,0:T(8,128)(2,1)S(1)} %frame.23), channel_id=1, source_target_pairs={{4,8},{5,9},{6,10},{7,11},{20,24},{21,25},{22,26},{23,27}} | collective-permute-start | bytes 368648 | tf_op jit(solution)/shard_map/ppermute | solution.py:309
  31.8 2.9 %collective-permute-start.16 = (bf16[144,384]{1,0:T(8,128)(2,1)S(1)}, bf16[144,384]{1,0:T(8,128)(2,1)S(1)}, u32[]{:S(2)}, u32[]{:S(2)}) collective-permute-start(bf16[144,384]{1,0:T(8,128)(2,1)S(1)} %get-tuple-element.107), channel_id=1, source_target_pairs={{8,12},{9,13},{10,14},{11,15},{24,28},{25,29},{26,30},{27,31}} | collective-permute-start | bytes 331784 | tf_op jit(solution)/shard_map/ppermute | solution.py:309
  32.5 2.2 %collective-permute-start.15 = (bf16[144,384]{1,0:T(8,128)(2,1)S(1)}, bf16[144,384]{1,0:T(8,128)(2,1)S(1)}, u32[]{:S(2)}, u32[]{:S(2)}) collective-permute-start(bf16[144,384]{1,0:T(8,128)(2,1)S(1)} %get-tuple-element.106), channel_id=1, source_target_pairs={{8,12},{9,13},{10,14},{11,15},{24,28},{25,29},{26,30},{27,31}} | collective-permute-start | bytes 331784 | tf_op jit(solution)/shard_map/ppermute | solution.py:309
  33.3 3.1 %collective-permute-start.14 = (bf16[144,384]{1,0:T(8,128)(2,1)S(1)}, bf16[144,384]{1,0:T(8,128)(2,1)S(1)}, u32[]{:S(2)}, u32[]{:S(2)}) collective-permute-start(bf16[144,384]{1,0:T(8,128)(2,1)S(1)} %get-tuple-element.105), channel_id=1, source_target_pairs={{8,12},{9,13},{10,14},{11,15},{24,28},{25,29},{26,30},{27,31}} | collective-permute-start | bytes 331784 | tf_op jit(solution)/shard_map/ppermute | solution.py:309
  34.0 2.5 %collective-permute-start.13 = (bf16[144,384]{1,0:T(8,128)(2,1)S(1)}, bf16[144,384]{1,0:T(8,128)(2,1)S(1)}, u32[]{:S(2)}, u32[]{:S(2)}) collective-permute-start(bf16[144,384]{1,0:T(8,128)(2,1)S(1)} %frame.27), channel_id=1, source_target_pairs={{8,12},{9,13},{10,14},{11,15},{24,28},{25,29},{26,30},{27,31}} | collective-permute-start | bytes 331784 | tf_op jit(solution)/shard_map/ppermute | solution.py:309
  34.8 1.7 %collective-permute-start.17 = (bf16[2,64,384]{2,1,0:T(8,128)(2,1)S(1)}, bf16[2,64,384]{2,1,0:T(8,128)(2,1)S(1)}, u32[]{:S(2)}, u32[]{:S(2)}) collective-permute-start(bf16[2,64,384]{2,1,0:T(8,128)(2,1)S(1)} %get-tuple-element.121.refs_9_), channel_id=1, source_target_pairs={{12,0},{14,2},{13,4},{15,6}} | collective-permute-start | bytes 294920 | tf_op jit(solution)/shard_map/ppermute | solution.py:228
  35.5 1.0 %collective-permute-start.18 = (bf16[2,64,384]{2,1,0:T(8,128)(2,1)S(1)}, bf16[2,64,384]{2,1,0:T(8,128)(2,1)S(1)}, u32[]{:S(2)}, u32[]{:S(2)}) collective-permute-start(bf16[2,64,384]{2,1,0:T(8,128)(2,1)S(1)} %get-tuple-element.122.refs_10_), channel_id=1, source_target_pairs={{12,1},{14,3},{13,5},{15,7}} | collective-permute-start | bytes 294920 | tf_op jit(solution)/shard_map/ppermute | solution.py:228
  36.5 3.4 %collective-permute-start.19 = (bf16[2,64,384]{2,1,0:T(8,128)(2,1)S(1)}, bf16[2,64,384]{2,1,0:T(8,128)(2,1)S(1)}, u32[]{:S(2)}, u32[]{:S(2)}) collective-permute-start(bf16[2,64,384]{2,1,0:T(8,128)(2,1)S(1)} %get-tuple-element.123), channel_id=1, source_target_pairs={{12,17},{14,19},{13,21},{15,23},{28,9},{30,11},{29,13},{31,15}} | collective-permute-start | bytes 294920 | tf_op jit(solution)/shard_map/ppermute | solution.py:228
  37.2 2.7 %collective-permute-start.20 = (bf16[2,64,384]{2,1,0:T(8,128)(2,1)S(1)}, bf16[2,64,384]{2,1,0:T(8,128)(2,1)S(1)}, u32[]{:S(2)}, u32[]{:S(2)}) collective-permute-start(bf16[2,64,384]{2,1,0:T(8,128)(2,1)S(1)} %get-tuple-element.124), channel_id=1, source_target_pairs={{28,25},{30,27},{29,29},{31,31}} | collective-permute-start | bytes 294920 | tf_op jit(solution)/shard_map/ppermute | solution.py:228
  37.9 18.5 %collective-permute-start.21 = (bf16[2,64,384]{2,1,0:T(8,128)(2,1)S(1)}, bf16[2,64,384]{2,1,0:T(8,128)(2,1)S(1)}, u32[]{:S(2)}, u32[]{:S(2)}) collective-permute-start(bf16[2,64,384]{2,1,0:T(8,128)(2,1)S(1)} %get-tuple-element.125), channel_id=1, source_target_pairs={{12,16},{14,18},{13,20},{15,22},{28,8},{30,10},{29,12},{31,14}} | collective-permute-start | bytes 294920 | tf_op jit(solution)/shard_map/ppermute | solution.py:228
  39.2 17.2 %collective-permute-start.22 = (bf16[2,64,384]{2,1,0:T(8,128)(2,1)S(1)}, bf16[2,64,384]{2,1,0:T(8,128)(2,1)S(1)}, u32[]{:S(2)}, u32[]{:S(2)}) collective-permute-start(bf16[2,64,384]{2,1,0:T(8,128)(2,1)S(1)} %get-tuple-element.126), channel_id=1, source_target_pairs={{28,24},{30,26},{29,28},{31,30}} | collective-permute-start | bytes 294920 | tf_op jit(solution)/shard_map/ppermute | solution.py:228

commit v8 on v7

v8 whole, which is shorter than its diff:
```python
import functools

import jax
import jax.numpy as jnp
from jax import lax
from jax.experimental import pallas as pl
from jax.experimental.pallas import tpu as pltpu
from jax.sharding import PartitionSpec as P

HALVES = 2
DEPTH = 4
TAPS = 3
VMEM_LIMIT = 24 << 20
MESH_AXES = ("tm", "segment", "band")


def whole(space=pltpu.VMEM):
    return pl.BlockSpec(memory_space=space)


def resident(value):
    return pltpu.with_memory_space_constraint(value, pltpu.VMEM)


def in_hbm(value):
    return pltpu.with_memory_space_constraint(value, pltpu.HBM)


def working(slot, frames, segments, lag):
    return [s for s in range(segments) if 0 <= slot - lag * s < frames]


def on_unit(unit, holders):
    here = lax.axis_index("segment") == unit
    if holders < lax.axis_size("tm"):
        here = jnp.logical_and(here, lax.axis_index("tm") < holders)
    return here


def rows_at(start, count, cols):
    return pl.ds(pl.multiple_of(start * cols, cols), count * cols)


def run_copies(copies, sems):
    copies = [
        pltpu.make_async_copy(source, target, sems.at[number]) for number, (source, target) in enumerate(copies)
    ]
    for copy in copies:
        copy.start()
    return copies


def pick_kernel(per_half, holders, source, bias, gain, mine, own, bias_out, gain_out, *refs):
    singles, sems = refs[:-1], refs[-1]
    side = lax.axis_index("tm") & (holders - 1)
    lane = lax.axis_index("band") & (per_half - 1)
    clip = lax.axis_index("segment")
    copies = [(source.at[clip, number], single.at[0]) for number, single in enumerate(singles)]
    copies += [(source.at[clip], mine), (source.at[side * per_half + lane], own), (bias, bias_out), (gain, gain_out)]
    for copy in run_copies(copies, sems):
        copy.wait()


def taps_dot(spread, weight, start, count, cols, copies):
    rows = [spread[rows_at(start + row, count, cols), :] for row in range(TAPS)]
    if not copies:
        return jnp.dot(jnp.concatenate(rows, axis=1), weight[...], preferred_element_type=jnp.float32)
    depth = weight.shape[0] // TAPS
    total = None
    for number, row in enumerate(rows):
        for copy in copies[number :: TAPS]:
            copy.wait()
        part = jnp.dot(row, weight[pl.ds(number * depth, depth), :], preferred_element_type=jnp.float32)
        total = part if total is None else total + part
    return total


def frame_kernel(cfg, *refs):
    refs = list(refs)
    groups = [refs.pop(0) for _ in range(cfg["groups"])]
    received = refs.pop(0) if cfg["came"] is not None else None
    partial, weight, bias, gain = refs[:4]
    refs = refs[4:]
    refs = refs[cfg["passing"] :]
    copies = []
    if cfg["loads"]:
        source, weight, sems = weight, refs.pop(0), refs.pop()
        depth = weight.shape[0] // TAPS
        thirds = [pl.ds(number * depth, depth) for number in range(TAPS)]
        copies = run_copies([(source.at[2, third], weight.at[third]) for third in thirds], sems)
    out = refs.pop(0) if cfg["sends"] else None
    spread = refs.pop(0 if cfg["later"] else -1)
    tails = [refs.pop(0) for _ in range(cfg["finals"])]
    refs = refs[cfg["keeps"] :]
    entry = refs.pop(0)
    cols, window, segments = cfg["cols"], cfg["window"], cfg["segments"]
    channels = entry.shape[-1]
    half = lax.axis_index("band") // cfg["per_half"]

    def run(unit):
        have = window - unit
        need = have - 1
        size = have * cols
        if unit == 0:
            step = entry.shape[0] // TAPS

            def place(piece, code):
                number = (code >> (2 * lax.axis_index("band"))) & 3
                piece, at = piece
                entry[pl.ds(pl.multiple_of(number * step, step), step), :] = piece[at]

            pieces, codes = list(zip(groups, cfg["piece_at"])), list(cfg["places"])
            if len(pieces) > TAPS:
                near = lax.axis_index("tm") == cfg["time"]
                pl.when(near)(functools.partial(place, pieces.pop(0), codes[0]))
                pl.when(jnp.logical_not(near))(functools.partial(place, pieces.pop(0), codes.pop(0)))
            for piece, code in zip(pieces, codes):
                place(piece, code)
            source, skip = entry, 0
        else:
            source, skip = received, half * (unit - 1 - cfg["came"])
        wide = source[rows_at(skip, have, cols), :].astype(jnp.float32)
        meansq = jnp.sum(wide * wide, axis=-1, keepdims=True) * (1.0 / channels)
        normed = wide * lax.rsqrt(meansq + 1e-06) * gain[...]
        ready = normed / (1.0 + jnp.exp(-normed))
        column = lax.broadcasted_iota(jnp.int32, ready.shape, 0) & (cols - 1)
        before = jnp.where(column == 0, 0.0, pltpu.roll(ready, 1, 0))
        after = jnp.where(column == cols - 1, 0.0, pltpu.roll(ready, size - 1, 0))
        edge = jnp.zeros((cols, TAPS * channels), jnp.bfloat16)
        spread[pl.ds(0, cols), :] = edge
        spread[pl.ds(size + cols, cols), :] = edge
        for number, value in enumerate((before, ready, after)):
            spread[pl.ds(cols, size), pl.ds(number * channels, channels)] = value.astype(jnp.bfloat16)
        kept = source[rows_at(skip + half, need, cols), :].astype(jnp.float32)
        total = partial[pl.ds(0, need * cols), :] + kept + bias[...]
        total += taps_dot(spread, weight, half, need, cols, copies)
        value = total.astype(jnp.bfloat16)
        if unit < segments - 1:
            out[rows_at(half * (unit - cfg["lowest"]), need, cols), :] = value
        else:
            length = value.shape[0] // len(tails)
            for number, tail in enumerate(tails):
                tail[cfg["tail_at"]] = value[number * length : (number + 1) * length]

    run_units(cfg, cfg["units"], run, copies)


def run_units(cfg, units, run, copies):
    active = [on_unit(unit, cfg["holders"]) for unit in units]
    for unit, here in zip(units, active):
        pl.when(here)(functools.partial(run, unit))
    if copies:

        @pl.when(jnp.logical_not(functools.reduce(jnp.logical_or, active)))
        def _():
            for copy in copies:
                copy.wait()


def history_kernel(cfg, spread, near, far, weight, near_out, far_out, *refs):
    cols, window = cfg["cols"], cfg["window"]
    channels = near.shape[-1]
    half = lax.axis_index("band") // cfg["per_half"]
    copies = []
    if cfg["loads"]:
        source, (weight, sems) = weight, refs
        depth = weight.shape[0] // TAPS
        copies = run_copies(
            [
                (source.at[age, third], weight.at[third, pl.ds(age * channels, channels)])
                for age in range(2)
                for third in [pl.ds(number * depth, depth) for number in range(TAPS)]
            ],
            sems,
        )

    def run(unit):
        need = window - unit - 1
        here = pl.ds(0, need * cols)
        total = taps_dot(spread, weight, half, need, cols, copies)
        near_out[here, :] = far[here, :] + total[:, channels:]
        far_out[here, :] = total[:, :channels]

    run_units(cfg, cfg["later"], run, copies)


def local(features, conv_weight, conv_bias, norm_gain):
    times, segments, bands = (lax.axis_size(name) for name in MESH_AXES)
    time, position, band = (lax.axis_index(name) for name in MESH_AXES)
    clips, own_frames, own_rows, cols, channels = features.shape
    frames = own_frames * times
    per_half = bands // HALVES
    window = own_rows * bands // HALVES + segments
    holders = clips // per_half
    piece = own_rows * cols
    assert clips == segments == bands == 4 and holders == 2 <= times and window == TAPS * own_rows

    def stream(clip, half):
        return clip // per_half, half * per_half + clip % per_half

    def spot(t, s, b):
        return (t * segments + s) * bands + b

    shape = (own_frames, piece, channels)
    mine, own, bias, gain, *singles = pl.pallas_call(
        functools.partial(pick_kernel, per_half, holders),
        out_shape=[
            pltpu.VMEM(shape, features.dtype),
            pltpu.VMEM(shape, features.dtype),
            pltpu.VMEM(conv_bias.shape, conv_bias.dtype),
            pltpu.VMEM(norm_gain.shape, norm_gain.dtype),
        ]
        + [pltpu.VMEM((1, piece, channels), features.dtype)] * own_frames,
        in_specs=[whole(pltpu.HBM)] * 3,
        out_specs=[whole()] * (4 + own_frames),
        scratch_shapes=[pltpu.SemaphoreType.DMA((4 + own_frames,))],
        compiler_params=pltpu.CompilerParams(vmem_limit_bytes=1 << 20),
        name="pick",
    )(*[in_hbm(value) for value in (features.reshape(clips, *shape), conv_bias, norm_gain)])
    bias, gain = resident(bias), resident(gain)
    weight = in_hbm(conv_weight[0].reshape(TAPS, TAPS * TAPS * channels, channels))
    wanted = [[2 * h + j for h in range(HALVES) for j in range(per_half)], [1, 0, 3, 2], [2, 2, 1, 1]]
    places = [sum((b - at // per_half) << (2 * at) for at, b in enumerate(row)) for row in wanted]

    def gather(value, number, members):
        routes = []
        for t, clip in members:
            for h in range(HALVES):
                there, at = stream(clip, h)
                routes.append((spot(t, clip, wanted[number][at]), spot(there, 0, at)))
        assert len({a for a, _ in routes}) == len({b for _, b in routes}) == len(routes)
        return lax.ppermute(value, MESH_AXES, routes)

    across = [(t, clip) for t in range(holders) for clip in range(clips) if clip // per_half != t]
    entries = []
    crossed = gather(mine, 0, across)
    for t in range(times):
        members = [(t, clip) for clip in range(clips)]
        if t == 0:
            for number, single in enumerate(singles):
                others = [gather(single, part, members) for part in (1, 2)]
                entries.append(([own, crossed, *others], [number, number, 0, 0]))
            continue
        others = [gather(mine, part, members) for part in (1, 2)]
        whole_own = [] if t < holders else [gather(mine, 0, members)]
        for number in range(own_frames):
            if t < holders:
                entries.append(([own, crossed, *others], [number] * 4))
            else:
                entries.append((whole_own + others, [number] * TAPS))

    def leave(value, there, index):
        routes = []
        for clip in range(clips):
            for h in range(HALVES):
                t, b = stream(clip, h)
                routes.append((spot(t, segments - 1, b), spot(there, clip, h * per_half + index)))
        return lax.ppermute(value, MESH_AXES, routes)

    state = ((window - 1) * cols, channels)
    near = jnp.zeros(state, jnp.float32)
    far = jnp.zeros(state, jnp.float32)
    lag = min(frames, DEPTH)
    slots = frames + lag * (segments - 1)
    moving = {}
    tails = []
    landed = {}
    for slot in range(slots):
        units = working(slot, frames, segments, lag)
        senders_now = [s for s in units if s < segments - 1]
        last = slot - lag * (segments - 1)
        finals = per_half if last >= 0 else 0
        middle = finals and last % own_frames > 0
        keeps = len(landed) if slot + 1 == slots else 0
        cfg = dict(
            units=units,
            later=[s for s in units if slot - lag * s < frames - 1],
            sends=bool(senders_now),
            lowest=min(senders_now, default=0),
            groups=len(entries[slot][0]) if slot < frames else 0,
            loads=slot == 0,
            places=places,
            piece_at=entries[slot][1] if slot < frames else [],
            time=slot // own_frames,
            came=min(working(slot - lag, frames, segments, lag)) if slot >= lag else None,
            finals=finals,
            tail_at=last % own_frames,
            passing=(finals if middle else 0) + keeps,
            keeps=keeps,
            cols=cols,
            window=window,
            segments=segments,
                        per_half=per_half,
            holders=holders,
        )
        operands = []
        if slot < frames:
            operands += [resident(value) for value in entries[slot][0]]
        if slot >= lag:
            operands.append(resident(moving.pop(slot - lag)))
        operands += [resident(near), weight if slot == 0 else now, bias, gain]
        shapes = [pltpu.VMEM((TAPS * TAPS * channels, channels), weight.dtype)] if cfg["loads"] else []
        if cfg["sends"]:
            shapes.append(pltpu.VMEM(((window - 1 - cfg["lowest"]) * cols, channels), jnp.bfloat16))
        wide = pltpu.VMEM(((window + 2) * cols, TAPS * channels), jnp.bfloat16)
        if cfg["later"]:
            shapes.append(wide)
        shape = pltpu.VMEM((own_frames, piece, channels), jnp.bfloat16)
        aliases = {}
        if middle:
            for index, value in enumerate(tails):
                aliases[len(operands)] = len(shapes) + index
                operands.append(resident(value))
        shapes += [shape] * finals
        held = list(landed) if keeps else []
        for value in [landed[key] for key in held]:
            aliases[len(operands)] = len(shapes)
            operands.append(resident(value))
            shapes.append(shape)
        results = list(
            pl.pallas_call(
                functools.partial(frame_kernel, cfg),
                out_shape=shapes,
                in_specs=[whole(pltpu.HBM if value is weight else pltpu.VMEM) for value in operands],
                out_specs=[whole()] * len(shapes),
                scratch_shapes=[pltpu.VMEM((window * cols, channels), jnp.bfloat16)]
                + ([] if cfg["later"] else [wide])
                + ([pltpu.SemaphoreType.DMA((TAPS,))] if cfg["loads"] else []),
                input_output_aliases=aliases,
                compiler_params=pltpu.CompilerParams(vmem_limit_bytes=VMEM_LIMIT),
                cost_estimate=pl.CostEstimate(flops=0, transcendentals=0, bytes_accessed=1 << 10),
                name="frame",
            )(*operands)
        )
        if cfg["loads"]:
            now = resident(results.pop(0))
        out = results.pop(0) if cfg["sends"] else None
        spread = results.pop(0) if cfg["later"] else None
        tails = results[:finals]
        if cfg["sends"]:
            moving[slot] = lax.ppermute(out, "segment", [(s, s + 1) for s in senders_now])
        landed.update(zip(held, results[finals:]))
        if finals and last % own_frames == own_frames - 1:
            there = last // own_frames
            for index, value in enumerate(tails):
                landed[there, index] = leave(value, there, index)
        if cfg["later"]:
            loading = [pltpu.VMEM((TAPS * TAPS * channels, 2 * channels), weight.dtype)] if cfg["loads"] else []
            near, far, *loaded = pl.pallas_call(
                functools.partial(history_kernel, cfg),
                out_shape=[pltpu.VMEM(state, jnp.float32)] * 2 + loading,
                in_specs=[whole()] * 3 + [whole(pltpu.HBM if loading else pltpu.VMEM)],
                out_specs=[whole()] * (2 + len(loading)),
                scratch_shapes=[pltpu.SemaphoreType.DMA((2 * TAPS,))] if loading else [],
                input_output_aliases={1: 0, 2: 1},
                compiler_params=pltpu.CompilerParams(vmem_limit_bytes=VMEM_LIMIT),
                cost_estimate=pl.CostEstimate(flops=0, transcendentals=0, bytes_accessed=1 << 10),
                name="history",
            )(resident(spread), resident(near), resident(far), weight if loading else past)
            past = resident(loaded[0]) if loading else past

    result = None
    for (t, index), value in landed.items():
        here = jnp.logical_and(time == t, band % per_half == index)
        result = value if result is None else jnp.where(here, value, result)
    return result.reshape(1, own_frames, own_rows, cols, channels)


def solution(mesh):
    return jax.shard_map(
        local,
        mesh=mesh,
        in_specs=(
            P(None, "tm", "band", None, None),
            P("segment", None, None, None),
            P("segment", None),
            P("segment", None),
        ),
        out_specs=P("segment", "tm", "band", None, None),
        check_vma=False,
    )
```

time: 57.5 us -> 61.8 us (1.075)
  the two profiles are of different devices: /device:TPU:6 before, /device:TPU:18 now
where the time goes in v8:
time: 61.8 us; the launch traced here: 61.3 us
  waiting for transfers between devices  25.8 us (42%)
  starting transfers between devices  21 us (34%)
  Pallas kernels  13.2 us (21%)
  other arithmetic  0.66 us (1%)
    ppermute x12, waiting for transfers between devices, local(): lax.ppermute(out, 'segment', [(s, s + 1) for s in senders_now])  15.6 us
    ppermute x12, starting transfers between devices, local(): lax.ppermute(out, 'segment', [(s, s + 1) for s in senders_now])  13 us
    ppermute x4, waiting for transfers between devices, leave(): return lax.ppermute(value, MESH_AXES, routes)  10.2 us
    pallas_call x12, Pallas kernels, local(): pl.pallas_call(functools.partial(history_kernel, cfg), out_shape=[pltpu.V...  6.13 us
    pallas_call x16, Pallas kernels, local(): pl.pallas_call(functools.partial(frame_kernel, cfg), out_shape=shapes, in...  6 us
    ppermute x7, starting transfers between devices, gather(): return lax.ppermute(value, MESH_AXES, routes)  4.66 us
    ppermute x4, starting transfers between devices, leave(): return lax.ppermute(value, MESH_AXES, routes)  3.28 us
  transfers between devices with their start and end apart: 23, of which 6 were waited for; matrix products, arithmetic and copies ran while one was open for 0% of the time, Pallas kernels for 20%

profile of v8, /device:TPU:18, one launch (start us, length us, event | category | flops | bytes accessed | tf_op | source)
XLA Modules:
  0.0 61.3 jit_solution(10268995062648778198)
XLA Ops:
  0.0 1.1 %pick.1 = (bf16[2,64,384]{2,1,0:T(8,128)(2,1)S(1)}, bf16[2,64,384]{2,1,0:T(8,128)(2,1)S(1)}, f32[1,384]{1,0:T(1,128)S(1)}, f32[1,384]{1,0:T(1,128)S(1)}, bf16[1,...) custom-call(bf16[4,2,64,384]{3,2,1,0:T(8,128)(2,1)} %bitcast.5, f32[1,384]{1,0:T(1,128)} %bias.1, f32[1,384]{1,0:T(1,128)} %gain.1), custom_call_target="tpu_custom_call" | custom-call | tf_op jit(solution)/shard_map/pick/pallas_call | solution.py:205
  1.1 0.7 %collective-permute-start = (bf16[2,64,384]{2,1,0:T(8,128)(2,1)S(1)}, bf16[2,64,384]{2,1,0:T(8,128)(2,1)S(1)}, u32[]{:S(2)}, u32[]{:S(2)}) collective-permute-start(bf16[2,64,384]{2,1,0:T(8,128)(2,1)S(1)} %get-tuple-element.68), channel_id=1, source_target_pairs={{8,16},{10,18},{13,17},{15,19},{16,0},{18,2},{21,1},{23,3}} | collective-permute-start | bytes 294920 | tf_op jit(solution)/shard_map/ppermute | solution.py:232
  1.8 0.7 %collective-permute-start.5 = (bf16[1,64,384]{2,1,0:T(8,128)(2,1)S(1)}, bf16[1,64,384]{2,1,0:T(8,128)(2,1)S(1)}, u32[]{:S(2)}, u32[]{:S(2)}) collective-permute-start(bf16[1,64,384]{2,1,0:T(8,128)(2,1)S(1)} %get-tuple-element.70), channel_id=1, source_target_pairs={{1,0},{3,2},{4,1},{6,3},{9,16},{11,18},{12,17},{14,19}} | collective-permute-start | bytes 147464 | tf_op jit(solution)/shard_map/ppermute | solution.py:232
  4.5 0.7 %collective-permute-start.1 = (bf16[2,64,384]{2,1,0:T(8,128)(2,1)S(1)}, bf16[2,64,384]{2,1,0:T(8,128)(2,1)S(1)}, u32[]{:S(2)}, u32[]{:S(2)}) collective-permute-start(bf16[2,64,384]{2,1,0:T(8,128)(2,1)S(1)} %get-tuple-element.68), channel_id=1, source_target_pairs={{17,0},{19,2},{20,1},{22,3},{25,16},{27,18},{28,17},{30,19}} | collective-permute-start | bytes 294920 | tf_op jit(solution)/shard_map/ppermute | solution.py:232
  5.2 0.7 %collective-permute-start.2 = (bf16[2,64,384]{2,1,0:T(8,128)(2,1)S(1)}, bf16[2,64,384]{2,1,0:T(8,128)(2,1)S(1)}, u32[]{:S(2)}, u32[]{:S(2)}) collective-permute-start(bf16[2,64,384]{2,1,0:T(8,128)(2,1)S(1)} %get-tuple-element.68), channel_id=1, source_target_pairs={{18,0},{17,2},{22,1},{21,3},{26,16},{25,18},{30,17},{29,19}} | collective-permute-start | bytes 294920 | tf_op jit(solution)/shard_map/ppermute | solution.py:232
  5.9 1.7 %frame.16 = (bf16[3456,384]{1,0:T(8,128)(2,1)S(1)}, bf16[176,384]{1,0:T(8,128)(2,1)S(1)}, bf16[224,1152]{1,0:T(8,128)(2,1)S(1)}) custom-call(bf16[2,64,384]{2,1,0:T(8,128)(2,1)S(1)} %get-tuple-element.67.refs_0_, bf16[2,64,384]{2,1,0:T(8,128)(2,1)S(1)} %collective-permute-done.refs_1_, bf16[1,64,384]{2,1,0:T(8,128)(2,1)S(1)} %collective-permute-done.5.refs_2_, ...), custom_call_target="tpu_custom_call" | custom-call | bytes 1024 | tf_op jit(solution)/shard_map/frame/pallas_call | solution.py:321
  7.6 0.7 %collective-permute-start.10 = (bf16[176,384]{1,0:T(8,128)(2,1)S(1)}, bf16[176,384]{1,0:T(8,128)(2,1)S(1)}, u32[]{:S(2)}, u32[]{:S(2)}) collective-permute-start(bf16[176,384]{1,0:T(8,128)(2,1)S(1)} %get-tuple-element.85), channel_id=1, source_target_pairs={{0,4},{1,5},{2,6},{3,7},{16,20},{17,21},{18,22},{19,23}} | collective-permute-start | bytes 405512 | tf_op jit(solution)/shard_map/ppermute | solution.py:341
  8.3 2.6 %history.12 = (f32[176,384]{1,0:T(8,128)S(1)}, f32[176,384]{1,0:T(8,128)S(1)}, bf16[3456,768]{1,0:T(8,128)(2,1)S(1)}) custom-call(bf16[224,1152]{1,0:T(8,128)(2,1)S(1)} %get-tuple-element.73.spread, f32[176,384]{1,0:T(8,128)S(1)} %broadcast_1_refs_4__near_far.2.refs_4_.near, ...), custom_call_target="tpu_custom_call", output_to_operand_aliasing={{0}: (1, {}), {1}: (2, {})} | custom-call | bytes 1024 | tf_op jit(solution)/shard_map/history/pallas_call | solution.py:349
  10.9 0.7 %collective-permute-start.9 = (bf16[176,384]{1,0:T(8,128)(2,1)S(1)}, bf16[176,384]{1,0:T(8,128)(2,1)S(1)}, u32[]{:S(2)}, u32[]{:S(2)}) collective-permute-start(bf16[176,384]{1,0:T(8,128)(2,1)S(1)} %get-tuple-element.84), channel_id=1, source_target_pairs={{0,4},{1,5},{2,6},{3,7},{16,20},{17,21},{18,22},{19,23}} | collective-permute-start | bytes 405512 | tf_op jit(solution)/shard_map/ppermute | solution.py:341
  11.7 0.7 %collective-permute-start.8 = (bf16[176,384]{1,0:T(8,128)(2,1)S(1)}, bf16[176,384]{1,0:T(8,128)(2,1)S(1)}, u32[]{:S(2)}, u32[]{:S(2)}) collective-permute-start(bf16[176,384]{1,0:T(8,128)(2,1)S(1)} %get-tuple-element.83), channel_id=1, source_target_pairs={{0,4},{1,5},{2,6},{3,7},{16,20},{17,21},{18,22},{19,23}} | collective-permute-start | bytes 405512 | tf_op jit(solution)/shard_map/ppermute | solution.py:341
  12.4 0.7 %collective-permute-start.7 = (bf16[176,384]{1,0:T(8,128)(2,1)S(1)}, bf16[176,384]{1,0:T(8,128)(2,1)S(1)}, u32[]{:S(2)}, u32[]{:S(2)}) collective-permute-start(bf16[176,384]{1,0:T(8,128)(2,1)S(1)} %frame.19), channel_id=1, source_target_pairs={{0,4},{1,5},{2,6},{3,7},{16,20},{17,21},{18,22},{19,23}} | collective-permute-start | bytes 405512 | tf_op jit(solution)/shard_map/ppermute | solution.py:341
  13.2 1.3 %collective-permute-start.14 = (bf16[160,384]{1,0:T(8,128)(2,1)S(1)}, bf16[160,384]{1,0:T(8,128)(2,1)S(1)}, u32[]{:S(2)}, u32[]{:S(2)}) collective-permute-start(bf16[160,384]{1,0:T(8,128)(2,1)S(1)} %get-tuple-element.97), channel_id=1, source_target_pairs={{4,8},{5,9},{6,10},{7,11},{20,24},{21,25},{22,26},{23,27}} | collective-permute-start | bytes 368648 | tf_op jit(solution)/shard_map/ppermute | solution.py:341
  14.5 1.3 %collective-permute-start.13 = (bf16[160,384]{1,0:T(8,128)(2,1)S(1)}, bf16[160,384]{1,0:T(8,128)(2,1)S(1)}, u32[]{:S(2)}, u32[]{:S(2)}) collective-permute-start(bf16[160,384]{1,0:T(8,128)(2,1)S(1)} %get-tuple-element.96), channel_id=1, source_target_pairs={{4,8},{5,9},{6,10},{7,11},{20,24},{21,25},{22,26},{23,27}} | collective-permute-start | bytes 368648 | tf_op jit(solution)/shard_map/ppermute | solution.py:341
  16.1 1.3 %collective-permute-start.12 = (bf16[160,384]{1,0:T(8,128)(2,1)S(1)}, bf16[160,384]{1,0:T(8,128)(2,1)S(1)}, u32[]{:S(2)}, u32[]{:S(2)}) collective-permute-start(bf16[160,384]{1,0:T(8,128)(2,1)S(1)} %get-tuple-element.95), channel_id=1, source_target_pairs={{4,8},{5,9},{6,10},{7,11},{20,24},{21,25},{22,26},{23,27}} | collective-permute-start | bytes 368648 | tf_op jit(solution)/shard_map/ppermute | solution.py:341
  17.4 1.3 %collective-permute-start.11 = (bf16[160,384]{1,0:T(8,128)(2,1)S(1)}, bf16[160,384]{1,0:T(8,128)(2,1)S(1)}, u32[]{:S(2)}, u32[]{:S(2)}) collective-permute-start(bf16[160,384]{1,0:T(8,128)(2,1)S(1)} %frame.23), channel_id=1, source_target_pairs={{4,8},{5,9},{6,10},{7,11},{20,24},{21,25},{22,26},{23,27}} | collective-permute-start | bytes 368648 | tf_op jit(solution)/shard_map/ppermute | solution.py:341
  18.7 11.1 %collective-permute-done.14.refs_0_ = bf16[160,384]{1,0:T(8,128)(2,1)S(1)} collective-permute-done((bf16[160,384]{1,0:T(8,128)(2,1)S(1)}, bf16[160,384]{1,0:T(8,128)(2,1)S(1)}, u32[]{:S(2)}, u32[]{:S(2)}) %collective-permute-start.14) | collective-permute-done | bytes 122912 | tf_op jit(solution)/shard_map/ppermute | solution.py:341
  29.9 1.0 %frame.24 = (bf16[144,384]{1,0:T(8,128)(2,1)S(1)}, bf16[224,1152]{1,0:T(8,128)(2,1)S(1)}) custom-call(bf16[160,384]{1,0:T(8,128)(2,1)S(1)} %collective-permute-done.14.refs_0_, f32[176,384]{1,0:T(8,128)S(1)} %get-tuple-element.94.refs_1_.near, bf16[3456,384]{1,0:T(8,128)(2,1)S(1)} %get-tuple-element.75.refs_5_.refs_2_, ...), custom_call_target="tpu_custom_call" | custom-call | bytes 1024 | tf_op jit(solution)/shard_map/frame/pallas_call | solution.py:321
  30.8 1.3 %collective-permute-start.18 = (bf16[144,384]{1,0:T(8,128)(2,1)S(1)}, bf16[144,384]{1,0:T(8,128)(2,1)S(1)}, u32[]{:S(2)}, u32[]{:S(2)}) collective-permute-start(bf16[144,384]{1,0:T(8,128)(2,1)S(1)} %get-tuple-element.109), channel_id=1, source_target_pairs={{8,12},{9,13},{10,14},{11,15},{24,28},{25,29},{26,30},{27,31}} | collective-permute-start | bytes 331784 | tf_op jit(solution)/shard_map/ppermute | solution.py:341
  32.1 1.1 %history.18 = (f32[176,384]{1,0:T(8,128)S(1)}, f32[176,384]{1,0:T(8,128)S(1)}) custom-call(bf16[224,1152]{1,0:T(8,128)(2,1)S(1)} %get-tuple-element.98.spread, f32[176,384]{1,0:T(8,128)S(1)} %get-tuple-element.94.refs_1_.near, f32[176,384]{1,0:T(8,128)S(1)} %get-tuple-element.99.far, ...), custom_call_target="tpu_custom_call", output_to_operand_aliasing={{0}: (1, {}), {1}: (2, {})} | custom-call | bytes 1024 | tf_op jit(solution)/shard_map/history/pallas_call | solution.py:349
  33.2 3.1 %collective-permute-done.13.refs_0_ = bf16[160,384]{1,0:T(8,128)(2,1)S(1)} collective-permute-done((bf16[160,384]{1,0:T(8,128)(2,1)S(1)}, bf16[160,384]{1,0:T(8,128)(2,1)S(1)}, u32[]{:S(2)}, u32[]{:S(2)}) %collective-permute-start.13) | collective-permute-done | bytes 122912 | tf_op jit(solution)/shard_map/ppermute | solution.py:341
  36.4 1.0 %frame.25 = (bf16[144,384]{1,0:T(8,128)(2,1)S(1)}, bf16[224,1152]{1,0:T(8,128)(2,1)S(1)}) custom-call(bf16[160,384]{1,0:T(8,128)(2,1)S(1)} %collective-permute-done.13.refs_0_, f32[176,384]{1,0:T(8,128)S(1)} %get-tuple-element.100.refs_1_.near, bf16[3456,384]{1,0:T(8,128)(2,1)S(1)} %get-tuple-element.75.refs_5_.refs_2_, ...), custom_call_target="tpu_custom_call" | custom-call | bytes 1024 | tf_op jit(solution)/shard_map/frame/pallas_call | solution.py:321
  37.3 1.3 %collective-permute-start.17 = (bf16[144,384]{1,0:T(8,128)(2,1)S(1)}, bf16[144,384]{1,0:T(8,128)(2,1)S(1)}, u32[]{:S(2)}, u32[]{:S(2)}) collective-permute-start(bf16[144,384]{1,0:T(8,128)(2,1)S(1)} %get-tuple-element.108), channel_id=1, source_target_pairs={{8,12},{9,13},{10,14},{11,15},{24,28},{25,29},{26,30},{27,31}} | collective-permute-start | bytes 331784 | tf_op jit(solution)/shard_map/ppermute | solution.py:341
  38.6 1.1 %history.19 = (f32[176,384]{1,0:T(8,128)S(1)}, f32[176,384]{1,0:T(8,128)S(1)}) custom-call(bf16[224,1152]{1,0:T(8,128)(2,1)S(1)} %get-tuple-element.101.spread, f32[176,384]{1,0:T(8,128)S(1)} %get-tuple-element.100.refs_1_.near, f32[176,384]{1,0:T(8,128)S(1)} %get-tuple-element.102.far, ...), custom_call_target="tpu_custom_call", output_to_operand_aliasing={{0}: (1, {}), {1}: (2, {})} | custom-call | bytes 1024 | tf_op jit(solution)/shard_map/history/pallas_call | solution.py:349
  40.1 1.0 %frame.26 = (bf16[144,384]{1,0:T(8,128)(2,1)S(1)}, bf16[224,1152]{1,0:T(8,128)(2,1)S(1)}) custom-call(bf16[160,384]{1,0:T(8,128)(2,1)S(1)} %collective-permute-done.12.refs_0_, f32[176,384]{1,0:T(8,128)S(1)} %get-tuple-element.103.refs_1_.near, bf16[3456,384]{1,0:T(8,128)(2,1)S(1)} %get-tuple-element.75.refs_5_.refs_2_, ...), custom_call_target="tpu_custom_call" | custom-call | bytes 1024 | tf_op jit(solution)/shard_map/frame/pallas_call | solution.py:321
  41.0 1.3 %collective-permute-start.16 = (bf16[144,384]{1,0:T(8,128)(2,1)S(1)}, bf16[144,384]{1,0:T(8,128)(2,1)S(1)}, u32[]{:S(2)}, u32[]{:S(2)}) collective-permute-start(bf16[144,384]{1,0:T(8,128)(2,1)S(1)} %get-tuple-element.107), channel_id=1, source_target_pairs={{8,12},{9,13},{10,14},{11,15},{24,28},{25,29},{26,30},{27,31}} | collective-permute-start | bytes 331784 | tf_op jit(solution)/shard_map/ppermute | solution.py:341
  42.3 1.1 %history.20 = (f32[176,384]{1,0:T(8,128)S(1)}, f32[176,384]{1,0:T(8,128)S(1)}) custom-call(bf16[224,1152]{1,0:T(8,128)(2,1)S(1)} %get-tuple-element.104.spread, f32[176,384]{1,0:T(8,128)S(1)} %get-tuple-element.103.refs_1_.near, f32[176,384]{1,0:T(8,128)S(1)} %get-tuple-element.105.far, ...), custom_call_target="tpu_custom_call", output_to_operand_aliasing={{0}: (1, {}), {1}: (2, {})} | custom-call | bytes 1024 | tf_op jit(solution)/shard_map/history/pallas_call | solution.py:349
  43.8 1.0 %frame.27 = bf16[144,384]{1,0:T(8,128)(2,1)S(1)} custom-call(bf16[160,384]{1,0:T(8,128)(2,1)S(1)} %collective-permute-done.11.refs_0_, f32[176,384]{1,0:T(8,128)S(1)} %get-tuple-element.106.refs_1_.near, bf16[3456,384]{1,0:T(8,128)(2,1)S(1)} %get-tuple-element.75.refs_5_.refs_2_, f32[1,384]{1,0:T(1,128)S(1)} %get-tuple-element.71.refs_6_.refs_3_, ...), custom_call_target="tpu_custom_call" | custom-call | bytes 1024 | tf_op jit(solution)/shard_map/frame/pallas_call | solution.py:321
  44.8 1.3 %collective-permute-start.15 = (bf16[144,384]{1,0:T(8,128)(2,1)S(1)}, bf16[144,384]{1,0:T(8,128)(2,1)S(1)}, u32[]{:S(2)}, u32[]{:S(2)}) collective-permute-start(bf16[144,384]{1,0:T(8,128)(2,1)S(1)} %frame.27), channel_id=1, source_target_pairs={{8,12},{9,13},{10,14},{11,15},{24,28},{25,29},{26,30},{27,31}} | collective-permute-start | bytes 331784 | tf_op jit(solution)/shard_map/ppermute | solution.py:341
  46.4 0.7 %collective-permute-start.19 = (bf16[2,64,384]{2,1,0:T(8,128)(2,1)S(1)}, bf16[2,64,384]{2,1,0:T(8,128)(2,1)S(1)}, u32[]{:S(2)}, u32[]{:S(2)}) collective-permute-start(bf16[2,64,384]{2,1,0:T(8,128)(2,1)S(1)} %get-tuple-element.123), channel_id=1, source_target_pairs={{12,0},{14,2},{13,4},{15,6},{28,8},{30,10},{29,12},{31,14}} | collective-permute-start | bytes 294920 | tf_op jit(solution)/shard_map/ppermute | solution.py:258
  47.1 0.7 %collective-permute-start.20 = (bf16[2,64,384]{2,1,0:T(8,128)(2,1)S(1)}, bf16[2,64,384]{2,1,0:T(8,128)(2,1)S(1)}, u32[]{:S(2)}, u32[]{:S(2)}) collective-permute-start(bf16[2,64,384]{2,1,0:T(8,128)(2,1)S(1)} %get-tuple-element.124), channel_id=1, source_target_pairs={{12,1},{14,3},{13,5},{15,7},{28,9},{30,11},{29,13},{31,15}} | collective-permute-start | bytes 294920 | tf_op jit(solution)/shard_map/ppermute | solution.py:258
  49.1 1.3 %collective-permute-start.22 = (bf16[2,64,384]{2,1,0:T(8,128)(2,1)S(1)}, bf16[2,64,384]{2,1,0:T(8,128)(2,1)S(1)}, u32[]{:S(2)}, u32[]{:S(2)}) collective-permute-start(bf16[2,64,384]{2,1,0:T(8,128)(2,1)S(1)} %get-tuple-element.126), channel_id=1, source_target_pairs={{12,16},{14,18},{13,20},{15,22},{28,24},{30,26},{29,28},{31,30}} | collective-permute-start | bytes 294920 | tf_op jit(solution)/shard_map/ppermute | solution.py:258
  50.4 10.2 %collective-permute-done.22 = bf16[2,64,384]{2,1,0:T(8,128)(2,1)S(1)} collective-permute-done((bf16[2,64,384]{2,1,0:T(8,128)(2,1)S(1)}, bf16[2,64,384]{2,1,0:T(8,128)(2,1)S(1)}, u32[]{:S(2)}, u32[]{:S(2)}) %collective-permute-start.22) | collective-permute-done | bytes 98336 | tf_op jit(solution)/shard_map/ppermute | solution.py:258
  (46 shorter events, 5.5 us)
Async XLA Ops:
  1.1 4.7 %collective-permute-start = (bf16[2,64,384]{2,1,0:T(8,128)(2,1)S(1)}, bf16[2,64,384]{2,1,0:T(8,128)(2,1)S(1)}, u32[]{:S(2)}, u32[]{:S(2)}) collective-permute-start(bf16[2,64,384]{2,1,0:T(8,128)(2,1)S(1)} %get-tuple-element.68), channel_id=1, source_target_pairs={{8,16},{10,18},{13,17},{15,19},{16,0},{18,2},{21,1},{23,3}} | collective-permute-start | bytes 294920 | tf_op jit(solution)/shard_map/ppermute | solution.py:232
  1.8 2.7 %collective-permute-start.5 = (bf16[1,64,384]{2,1,0:T(8,128)(2,1)S(1)}, bf16[1,64,384]{2,1,0:T(8,128)(2,1)S(1)}, u32[]{:S(2)}, u32[]{:S(2)}) collective-permute-start(bf16[1,64,384]{2,1,0:T(8,128)(2,1)S(1)} %get-tuple-element.70), channel_id=1, source_target_pairs={{1,0},{3,2},{4,1},{6,3},{9,16},{11,18},{12,17},{14,19}} | collective-permute-start | bytes 147464 | tf_op jit(solution)/shard_map/ppermute | solution.py:232
  2.5 2.7 %collective-permute-start.6 = (bf16[1,64,384]{2,1,0:T(8,128)(2,1)S(1)}, bf16[1,64,384]{2,1,0:T(8,128)(2,1)S(1)}, u32[]{:S(2)}, u32[]{:S(2)}) collective-permute-start(bf16[1,64,384]{2,1,0:T(8,128)(2,1)S(1)} %get-tuple-element.70), channel_id=1, source_target_pairs={{2,0},{1,2},{6,1},{5,3},{10,16},{9,18},{14,17},{13,19}} | collective-permute-start | bytes 147464 | tf_op jit(solution)/shard_map/ppermute | solution.py:232
  3.1 7.8 %collective-permute-start.3 = (bf16[1,64,384]{2,1,0:T(8,128)(2,1)S(1)}, bf16[1,64,384]{2,1,0:T(8,128)(2,1)S(1)}, u32[]{:S(2)}, u32[]{:S(2)}) collective-permute-start(bf16[1,64,384]{2,1,0:T(8,128)(2,1)S(1)} %get-tuple-element.69), channel_id=1, source_target_pairs={{1,0},{3,2},{4,1},{6,3},{9,16},{11,18},{12,17},{14,19}} | collective-permute-start | bytes 147464 | tf_op jit(solution)/shard_map/ppermute | solution.py:232
  3.8 7.1 %collective-permute-start.4 = (bf16[1,64,384]{2,1,0:T(8,128)(2,1)S(1)}, bf16[1,64,384]{2,1,0:T(8,128)(2,1)S(1)}, u32[]{:S(2)}, u32[]{:S(2)}) collective-permute-start(bf16[1,64,384]{2,1,0:T(8,128)(2,1)S(1)} %get-tuple-element.69), channel_id=1, source_target_pairs={{2,0},{1,2},{6,1},{5,3},{10,16},{9,18},{14,17},{13,19}} | collective-permute-start | bytes 147464 | tf_op jit(solution)/shard_map/ppermute | solution.py:232
  4.5 7.2 %collective-permute-start.1 = (bf16[2,64,384]{2,1,0:T(8,128)(2,1)S(1)}, bf16[2,64,384]{2,1,0:T(8,128)(2,1)S(1)}, u32[]{:S(2)}, u32[]{:S(2)}) collective-permute-start(bf16[2,64,384]{2,1,0:T(8,128)(2,1)S(1)} %get-tuple-element.68), channel_id=1, source_target_pairs={{17,0},{19,2},{20,1},{22,3},{25,16},{27,18},{28,17},{30,19}} | collective-permute-start | bytes 294920 | tf_op jit(solution)/shard_map/ppermute | solution.py:232
  5.2 6.5 %collective-permute-start.2 = (bf16[2,64,384]{2,1,0:T(8,128)(2,1)S(1)}, bf16[2,64,384]{2,1,0:T(8,128)(2,1)S(1)}, u32[]{:S(2)}, u32[]{:S(2)}) collective-permute-start(bf16[2,64,384]{2,1,0:T(8,128)(2,1)S(1)} %get-tuple-element.68), channel_id=1, source_target_pairs={{18,0},{17,2},{22,1},{21,3},{26,16},{25,18},{30,17},{29,19}} | collective-permute-start | bytes 294920 | tf_op jit(solution)/shard_map/ppermute | solution.py:232
  7.6 5.5 %collective-permute-start.10 = (bf16[176,384]{1,0:T(8,128)(2,1)S(1)}, bf16[176,384]{1,0:T(8,128)(2,1)S(1)}, u32[]{:S(2)}, u32[]{:S(2)}) collective-permute-start(bf16[176,384]{1,0:T(8,128)(2,1)S(1)} %get-tuple-element.85), channel_id=1, source_target_pairs={{0,4},{1,5},{2,6},{3,7},{16,20},{17,21},{18,22},{19,23}} | collective-permute-start | bytes 405512 | tf_op jit(solution)/shard_map/ppermute | solution.py:341
  10.9 3.5 %collective-permute-start.9 = (bf16[176,384]{1,0:T(8,128)(2,1)S(1)}, bf16[176,384]{1,0:T(8,128)(2,1)S(1)}, u32[]{:S(2)}, u32[]{:S(2)}) collective-permute-start(bf16[176,384]{1,0:T(8,128)(2,1)S(1)} %get-tuple-element.84), channel_id=1, source_target_pairs={{0,4},{1,5},{2,6},{3,7},{16,20},{17,21},{18,22},{19,23}} | collective-permute-start | bytes 405512 | tf_op jit(solution)/shard_map/ppermute | solution.py:341
  11.7 4.3 %collective-permute-start.8 = (bf16[176,384]{1,0:T(8,128)(2,1)S(1)}, bf16[176,384]{1,0:T(8,128)(2,1)S(1)}, u32[]{:S(2)}, u32[]{:S(2)}) collective-permute-start(bf16[176,384]{1,0:T(8,128)(2,1)S(1)} %get-tuple-element.83), channel_id=1, source_target_pairs={{0,4},{1,5},{2,6},{3,7},{16,20},{17,21},{18,22},{19,23}} | collective-permute-start | bytes 405512 | tf_op jit(solution)/shard_map/ppermute | solution.py:341
  12.4 5.0 %collective-permute-start.7 = (bf16[176,384]{1,0:T(8,128)(2,1)S(1)}, bf16[176,384]{1,0:T(8,128)(2,1)S(1)}, u32[]{:S(2)}, u32[]{:S(2)}) collective-permute-start(bf16[176,384]{1,0:T(8,128)(2,1)S(1)} %frame.19), channel_id=1, source_target_pairs={{0,4},{1,5},{2,6},{3,7},{16,20},{17,21},{18,22},{19,23}} | collective-permute-start | bytes 405512 | tf_op jit(solution)/shard_map/ppermute | solution.py:341
  13.2 16.7 %collective-permute-start.14 = (bf16[160,384]{1,0:T(8,128)(2,1)S(1)}, bf16[160,384]{1,0:T(8,128)(2,1)S(1)}, u32[]{:S(2)}, u32[]{:S(2)}) collective-permute-start(bf16[160,384]{1,0:T(8,128)(2,1)S(1)} %get-tuple-element.97), channel_id=1, source_target_pairs={{4,8},{5,9},{6,10},{7,11},{20,24},{21,25},{22,26},{23,27}} | collective-permute-start | bytes 368648 | tf_op jit(solution)/shard_map/ppermute | solution.py:341
  14.5 21.8 %collective-permute-start.13 = (bf16[160,384]{1,0:T(8,128)(2,1)S(1)}, bf16[160,384]{1,0:T(8,128)(2,1)S(1)}, u32[]{:S(2)}, u32[]{:S(2)}) collective-permute-start(bf16[160,384]{1,0:T(8,128)(2,1)S(1)} %get-tuple-element.96), channel_id=1, source_target_pairs={{4,8},{5,9},{6,10},{7,11},{20,24},{21,25},{22,26},{23,27}} | collective-permute-start | bytes 368648 | tf_op jit(solution)/shard_map/ppermute | solution.py:341
  16.1 24.0 %collective-permute-start.12 = (bf16[160,384]{1,0:T(8,128)(2,1)S(1)}, bf16[160,384]{1,0:T(8,128)(2,1)S(1)}, u32[]{:S(2)}, u32[]{:S(2)}) collective-permute-start(bf16[160,384]{1,0:T(8,128)(2,1)S(1)} %get-tuple-element.95), channel_id=1, source_target_pairs={{4,8},{5,9},{6,10},{7,11},{20,24},{21,25},{22,26},{23,27}} | collective-permute-start | bytes 368648 | tf_op jit(solution)/shard_map/ppermute | solution.py:341
  17.4 26.4 %collective-permute-start.11 = (bf16[160,384]{1,0:T(8,128)(2,1)S(1)}, bf16[160,384]{1,0:T(8,128)(2,1)S(1)}, u32[]{:S(2)}, u32[]{:S(2)}) collective-permute-start(bf16[160,384]{1,0:T(8,128)(2,1)S(1)} %frame.23), channel_id=1, source_target_pairs={{4,8},{5,9},{6,10},{7,11},{20,24},{21,25},{22,26},{23,27}} | collective-permute-start | bytes 368648 | tf_op jit(solution)/shard_map/ppermute | solution.py:341
  30.8 15.2 %collective-permute-start.18 = (bf16[144,384]{1,0:T(8,128)(2,1)S(1)}, bf16[144,384]{1,0:T(8,128)(2,1)S(1)}, u32[]{:S(2)}, u32[]{:S(2)}) collective-permute-start(bf16[144,384]{1,0:T(8,128)(2,1)S(1)} %get-tuple-element.109), channel_id=1, source_target_pairs={{8,12},{9,13},{10,14},{11,15},{24,28},{25,29},{26,30},{27,31}} | collective-permute-start | bytes 331784 | tf_op jit(solution)/shard_map/ppermute | solution.py:341
  37.3 8.8 %collective-permute-start.17 = (bf16[144,384]{1,0:T(8,128)(2,1)S(1)}, bf16[144,384]{1,0:T(8,128)(2,1)S(1)}, u32[]{:S(2)}, u32[]{:S(2)}) collective-permute-start(bf16[144,384]{1,0:T(8,128)(2,1)S(1)} %get-tuple-element.108), channel_id=1, source_target_pairs={{8,12},{9,13},{10,14},{11,15},{24,28},{25,29},{26,30},{27,31}} | collective-permute-start | bytes 331784 | tf_op jit(solution)/shard_map/ppermute | solution.py:341
  41.0 6.7 %collective-permute-start.16 = (bf16[144,384]{1,0:T(8,128)(2,1)S(1)}, bf16[144,384]{1,0:T(8,128)(2,1)S(1)}, u32[]{:S(2)}, u32[]{:S(2)}) collective-permute-start(bf16[144,384]{1,0:T(8,128)(2,1)S(1)} %get-tuple-element.107), channel_id=1, source_target_pairs={{8,12},{9,13},{10,14},{11,15},{24,28},{25,29},{26,30},{27,31}} | collective-permute-start | bytes 331784 | tf_op jit(solution)/shard_map/ppermute | solution.py:341
  44.8 3.6 %collective-permute-start.15 = (bf16[144,384]{1,0:T(8,128)(2,1)S(1)}, bf16[144,384]{1,0:T(8,128)(2,1)S(1)}, u32[]{:S(2)}, u32[]{:S(2)}) collective-permute-start(bf16[144,384]{1,0:T(8,128)(2,1)S(1)} %frame.27), channel_id=1, source_target_pairs={{8,12},{9,13},{10,14},{11,15},{24,28},{25,29},{26,30},{27,31}} | collective-permute-start | bytes 331784 | tf_op jit(solution)/shard_map/ppermute | solution.py:341
  46.4 2.0 %collective-permute-start.19 = (bf16[2,64,384]{2,1,0:T(8,128)(2,1)S(1)}, bf16[2,64,384]{2,1,0:T(8,128)(2,1)S(1)}, u32[]{:S(2)}, u32[]{:S(2)}) collective-permute-start(bf16[2,64,384]{2,1,0:T(8,128)(2,1)S(1)} %get-tuple-element.123), channel_id=1, source_target_pairs={{12,0},{14,2},{13,4},{15,6},{28,8},{30,10},{29,12},{31,14}} | collective-permute-start | bytes 294920 | tf_op jit(solution)/shard_map/ppermute | solution.py:258
  47.1 1.3 %collective-permute-start.20 = (bf16[2,64,384]{2,1,0:T(8,128)(2,1)S(1)}, bf16[2,64,384]{2,1,0:T(8,128)(2,1)S(1)}, u32[]{:S(2)}, u32[]{:S(2)}) collective-permute-start(bf16[2,64,384]{2,1,0:T(8,128)(2,1)S(1)} %get-tuple-element.124), channel_id=1, source_target_pairs={{12,1},{14,3},{13,5},{15,7},{28,9},{30,11},{29,13},{31,15}} | collective-permute-start | bytes 294920 | tf_op jit(solution)/shard_map/ppermute | solution.py:258
  48.4 2.0 %collective-permute-start.21 = (bf16[2,64,384]{2,1,0:T(8,128)(2,1)S(1)}, bf16[2,64,384]{2,1,0:T(8,128)(2,1)S(1)}, u32[]{:S(2)}, u32[]{:S(2)}) collective-permute-start(bf16[2,64,384]{2,1,0:T(8,128)(2,1)S(1)} %get-tuple-element.125), channel_id=1, source_target_pairs={{12,17},{14,19},{13,21},{15,23},{28,25},{30,27},{29,29},{31,31}} | collective-permute-start | bytes 294920 | tf_op jit(solution)/shard_map/ppermute | solution.py:258
  49.1 11.5 %collective-permute-start.22 = (bf16[2,64,384]{2,1,0:T(8,128)(2,1)S(1)}, bf16[2,64,384]{2,1,0:T(8,128)(2,1)S(1)}, u32[]{:S(2)}, u32[]{:S(2)}) collective-permute-start(bf16[2,64,384]{2,1,0:T(8,128)(2,1)S(1)} %get-tuple-element.126), channel_id=1, source_target_pairs={{12,16},{14,18},{13,20},{15,22},{28,24},{30,26},{29,28},{31,30}} | collective-permute-start | bytes 294920 | tf_op jit(solution)/shard_map/ppermute | solution.py:258

commit v9 on v7

--- a/solution.py
+++ b/solution.py
@@ -37,13 +37,24 @@
     return pl.ds(pl.multiple_of(start * cols, cols), count * cols)
 
 
-def pick_kernel(per_half, holders, source, mine, own, sems):
-    side = lax.axis_index("tm") & (holders - 1)
-    lane = lax.axis_index("band") & (per_half - 1)
-    clips = (lax.axis_index("segment"), side * per_half + lane)
+def sent_clips(side, lane, segment, choose):
+    near, far = 2 * side, 2 - 2 * side
+    behind = far + ((segment - 1) & 1)
+    return (
+        far + lane,
+        choose(segment == 0, near + 1, choose(segment == 3, near, behind)),
+        choose(segment == 0, near, choose(segment == 3, near + 1, behind)),
+    )
+
+
+def pick_kernel(holders, source, own, across, second, third, sems):
+    time = lax.axis_index("tm")
+    side = jnp.where(time < holders, time, 0)
+    lane = lax.axis_index("band") & 1
+    clips = (2 * side + lane, *sent_clips(side, lane, lax.axis_index("segment"), jnp.where))
     copies = [
         pltpu.make_async_copy(source.at[clip], target, sems.at[number])
-        for number, (clip, target) in enumerate(zip(clips, (mine, own)))
+        for number, (clip, target) in enumerate(zip(clips, (own, across, second, third)))
     ]
     for copy in copies:
         copy.start()
@@ -97,12 +108,12 @@
                 number = (code >> (2 * lax.axis_index("band"))) & 3
                 entry[pl.ds(pl.multiple_of(number * step, step), step), :] = piece[cfg["piece_at"]]
 
-            pieces, codes = list(groups), list(cfg["places"])
-            if len(pieces) > TAPS:
-                near = lax.axis_index("tm") == cfg["time"]
-                pl.when(near)(functools.partial(place, pieces.pop(0), codes[0]))
-                pl.when(jnp.logical_not(near))(functools.partial(place, pieces.pop(0), codes.pop(0)))
-            for piece, code in zip(pieces, codes):
+            *others, own, crossed = groups
+            first, *rest = cfg["places"]
+            near = lax.axis_index("tm") == cfg["near"]
+            pl.when(near)(functools.partial(place, own, first))
+            pl.when(jnp.logical_not(near))(functools.partial(place, crossed, first))
+            for piece, code in zip(others, rest):
                 place(piece, code)
             source, skip = entry, 0
         else:
@@ -164,7 +175,7 @@
     window = own_rows * bands // HALVES + segments
     holders = clips // per_half
     piece = own_rows * cols
-    assert clips == segments == bands == 4 and holders == 2 <= times and window == TAPS * own_rows
+    assert clips == segments == bands == 4 == 2 * per_half and holders == 2 <= times and window == TAPS * own_rows
 
     def stream(clip, half):
         return clip // per_half, half * per_half + clip % per_half
@@ -172,34 +183,49 @@
     def spot(t, s, b):
         return (t * segments + s) * bands + b
 
-    mine, own = pl.pallas_call(
-        functools.partial(pick_kernel, per_half, holders),
-        out_shape=[pltpu.VMEM((own_frames, piece, channels), features.dtype)] * 2,
+    own, *sources = pl.pallas_call(
+        functools.partial(pick_kernel, holders),
+        out_shape=[pltpu.VMEM((own_frames, piece, channels), features.dtype)] * 4,
         in_specs=[whole(pltpu.HBM)],
-        out_specs=[whole()] * 2,
-        scratch_shapes=[pltpu.SemaphoreType.DMA((2,))],
+        out_specs=[whole()] * 4,
+        scratch_shapes=[pltpu.SemaphoreType.DMA((4,))],
         compiler_params=pltpu.CompilerParams(vmem_limit_bytes=1 << 20),
         name="pick",
     )(pltpu.with_memory_space_constraint(features.reshape(clips, own_frames, piece, channels), pltpu.HBM))
-    wanted = [[2 * h + j for h in range(HALVES) for j in range(per_half)], [1, 0, 3, 2], [2, 2, 1, 1]]
+    wanted = [[2 * h + j for h in range(HALVES) for j in range(per_half)], [2, 0, 1, 2], [1, 2, 3, 1]]
     places = [sum((b - at // per_half) << (2 * at) for at, b in enumerate(row)) for row in wanted]
 
     def gather(number, members):
         routes = []
         for t, clip in members:
+            side, (there, lane) = t if t < holders else 0, divmod(clip, per_half)
+            if number == 0:
+                segment = t if t < holders else 1
+            elif there == side:
+                segment = 3 if lane == number - 1 else 0
+            else:
+                segment = 1 + lane
             for h in range(HALVES):
-                there, at = stream(clip, h)
-                routes.append((spot(t, clip, wanted[number][at]), spot(there, 0, at)))
+                at = stream(clip, h)[1]
+                source = wanted[number][at]
+                assert clip == sent_clips(side, source & 1, segment, lambda a, b, c: b if a else c)[number]
+                routes.append((spot(t, segment, source), spot(there, 0, at)))
         assert len({a for a, _ in routes}) == len({b for _, b in routes}) == len(routes)
-        return lax.ppermute(mine, MESH_AXES, routes)
-
-    across = [(t, clip) for t in range(holders) for clip in range(clips) if clip // per_half != t]
-    crossed = gather(0, across)
+        return lax.ppermute(sources[number], MESH_AXES, routes)
+
+    def far_side(t):
+        return [(t, clip) for clip in range(clips) if clip // per_half != (t if t < holders else 0)]
+
     entries = []
     for t in range(times):
-        members = [(t, clip) for clip in range(clips)]
-        first = [own, crossed] if t < holders else [gather(0, members)]
-        entries.append(first + [gather(number, members) for number in (1, 2)])
+        others = [gather(number, [(t, clip) for clip in range(clips)]) for number in (1, 2)]
+        if t == 0:
+            crossed = gather(0, [member for side in range(holders) for member in far_side(side)])
+        if t < holders:
+            entries.append(others + [own, crossed])
+        else:
+            routes = [(spot(t, 0, b), spot(0, 0, b)) for b in range(bands)]
+            entries.append(others + [lax.ppermute(own, MESH_AXES, routes), gather(0, far_side(t))])
 
     stored = [conv_weight[0].reshape(TAPS, TAPS * TAPS * channels, channels), conv_bias, norm_gain]
     now, past, bias, gain = pl.pallas_call(
@@ -251,7 +277,7 @@
             groups=len(entries[slot // own_frames]) if slot < frames else 0,
             places=places,
             piece_at=slot % own_frames,
-            time=slot // own_frames,
+            near=slot // own_frames if slot // own_frames < holders else 0,
             came=min(working(slot - lag, frames, segments, lag)) if slot >= lag else None,
             finals=finals,
             tail_at=last % own_frames,

time: 57.5 us -> 58 us (level)
  the two profiles are of different devices: /device:TPU:6 before, /device:TPU:18 now
where the time goes in v9:
time: 58 us; the launch traced here: 57.5 us
  starting transfers between devices  27.9 us (48%)
  waiting for transfers between devices  16 us (28%)
  Pallas kernels  12.4 us (21%)
  other arithmetic  0.68 us (1%)
    ppermute x12, starting transfers between devices, local(): lax.ppermute(out, 'segment', [(s, s + 1) for s in senders_now])  13 us
    ppermute x5, starting transfers between devices, gather(): return lax.ppermute(sources[number], MESH_AXES, routes)  10.2 us
    ppermute x6, waiting for transfers between devices, leave(): return lax.ppermute(value, MESH_AXES, routes)  8.43 us
    ppermute x12, waiting for transfers between devices, local(): lax.ppermute(out, 'segment', [(s, s + 1) for s in senders_now])  7.52 us
    ppermute x6, starting transfers between devices, leave(): return lax.ppermute(value, MESH_AXES, routes)  4.62 us
    pallas_call x16, Pallas kernels, local(): pl.pallas_call(functools.partial(frame_kernel, cfg), out_shape=shapes, in...  4.25 us
    pallas_call x12, Pallas kernels, local(): pl.pallas_call(functools.partial(history_kernel, cfg), out_shape=[pltpu.V...  3.63 us
    pallas_call x1, Pallas kernels, local(): pl.pallas_call(loader_kernel, out_shape=[pltpu.VMEM((TAPS * TAPS * channe...  3.42 us
  transfers between devices with their start and end apart: 23, of which 6 were waited for; matrix products, arithmetic and copies ran while one was open for 0% of the time, Pallas kernels for 20%

profile of v9, /device:TPU:18, one launch (start us, length us, event | category | flops | bytes accessed | tf_op | source)
XLA Modules:
  0.0 57.5 jit_solution(5399893748370959027)
XLA Ops:
  0.0 1.1 %pick.1 = (bf16[2,64,384]{2,1,0:T(8,128)(2,1)S(1)}, bf16[2,64,384]{2,1,0:T(8,128)(2,1)S(1)}, bf16[2,64,384]{2,1,0:T(8,128)(2,1)S(1)}, bf16[2,64,384]{2,1,0:T(8,128)(2,1)S(1)}) custom-call(bf16[4,2,64,384]{3,2,1,0:T(8,128)(2,1)} %bitcast.4), custom_call_target="tpu_custom_call" | custom-call | tf_op jit(solution)/shard_map/pick/pallas_call | solution.py:186
  1.1 0.7 %collective-permute-start.2 = (bf16[2,64,384]{2,1,0:T(8,128)(2,1)S(1)}, bf16[2,64,384]{2,1,0:T(8,128)(2,1)S(1)}, u32[]{:S(2)}, u32[]{:S(2)}) collective-permute-start(bf16[2,64,384]{2,1,0:T(8,128)(2,1)S(1)} %get-tuple-element.72), channel_id=1, source_target_pairs={{0,16},{2,18},{1,17},{3,19},{20,0},{22,2},{21,1},{23,3}} | collective-permute-start | bytes 294920 | tf_op jit(solution)/shard_map/ppermute | solution.py:214
  1.8 0.7 %collective-permute-start.3 = (bf16[2,64,384]{2,1,0:T(8,128)(2,1)S(1)}, bf16[2,64,384]{2,1,0:T(8,128)(2,1)S(1)}, u32[]{:S(2)}, u32[]{:S(2)}) collective-permute-start(bf16[2,64,384]{2,1,0:T(8,128)(2,1)S(1)} %get-tuple-element.69), channel_id=1, source_target_pairs={{14,0},{13,2},{0,1},{2,3},{6,16},{5,18},{8,17},{10,19}} | collective-permute-start | bytes 294920 | tf_op jit(solution)/shard_map/ppermute | solution.py:214
  2.4 0.7 %collective-permute-start.4 = (bf16[2,64,384]{2,1,0:T(8,128)(2,1)S(1)}, bf16[2,64,384]{2,1,0:T(8,128)(2,1)S(1)}, u32[]{:S(2)}, u32[]{:S(2)}) collective-permute-start(bf16[2,64,384]{2,1,0:T(8,128)(2,1)S(1)} %get-tuple-element.70), channel_id=1, source_target_pairs={{1,0},{3,2},{14,1},{13,3},{5,16},{7,18},{10,17},{9,19}} | collective-permute-start | bytes 294920 | tf_op jit(solution)/shard_map/ppermute | solution.py:214
  3.1 7.6 %collective-permute-start = (bf16[2,64,384]{2,1,0:T(8,128)(2,1)S(1)}, bf16[2,64,384]{2,1,0:T(8,128)(2,1)S(1)}, u32[]{:S(2)}, u32[]{:S(2)}) collective-permute-start(bf16[2,64,384]{2,1,0:T(8,128)(2,1)S(1)} %get-tuple-element.69), channel_id=1, source_target_pairs={{22,0},{21,2},{24,1},{26,3},{30,16},{29,18},{16,17},{18,19}} | collective-permute-start | bytes 294920 | tf_op jit(solution)/shard_map/ppermute | solution.py:214
  10.7 0.7 %collective-permute-start.1 = (bf16[2,64,384]{2,1,0:T(8,128)(2,1)S(1)}, bf16[2,64,384]{2,1,0:T(8,128)(2,1)S(1)}, u32[]{:S(2)}, u32[]{:S(2)}) collective-permute-start(bf16[2,64,384]{2,1,0:T(8,128)(2,1)S(1)} %get-tuple-element.70), channel_id=1, source_target_pairs={{21,0},{23,2},{26,1},{25,3},{17,16},{19,18},{30,17},{29,19}} | collective-permute-start | bytes 294920 | tf_op jit(solution)/shard_map/ppermute | solution.py:214
  11.3 3.4 %loader.1 = (bf16[3456,384]{1,0:T(8,128)(2,1)S(1)}, bf16[3456,768]{1,0:T(8,128)(2,1)S(1)}, f32[1,384]{1,0:T(1,128)S(1)}, f32[1,384]{1,0:T(1,128)S(1)}) custom-call(bf16[3,3456,384]{2,1,0:T(8,128)(2,1)} %bitcast.3, f32[1,384]{1,0:T(1,128)} %bias.1, f32[1,384]{1,0:T(1,128)} %gain.1), custom_call_target="tpu_custom_call" | custom-call | tf_op jit(solution)/shard_map/loader/pallas_call | solution.py:231
  14.9 0.7 %collective-permute-start.8 = (bf16[176,384]{1,0:T(8,128)(2,1)S(1)}, bf16[176,384]{1,0:T(8,128)(2,1)S(1)}, u32[]{:S(2)}, u32[]{:S(2)}) collective-permute-start(bf16[176,384]{1,0:T(8,128)(2,1)S(1)} %get-tuple-element.87), channel_id=1, source_target_pairs={{0,4},{1,5},{2,6},{3,7},{16,20},{17,21},{18,22},{19,23}} | collective-permute-start | bytes 405512 | tf_op jit(solution)/shard_map/ppermute | solution.py:335
  15.6 0.7 %collective-permute-start.7 = (bf16[176,384]{1,0:T(8,128)(2,1)S(1)}, bf16[176,384]{1,0:T(8,128)(2,1)S(1)}, u32[]{:S(2)}, u32[]{:S(2)}) collective-permute-start(bf16[176,384]{1,0:T(8,128)(2,1)S(1)} %get-tuple-element.86), channel_id=1, source_target_pairs={{0,4},{1,5},{2,6},{3,7},{16,20},{17,21},{18,22},{19,23}} | collective-permute-start | bytes 405512 | tf_op jit(solution)/shard_map/ppermute | solution.py:335
  16.4 0.7 %collective-permute-start.6 = (bf16[176,384]{1,0:T(8,128)(2,1)S(1)}, bf16[176,384]{1,0:T(8,128)(2,1)S(1)}, u32[]{:S(2)}, u32[]{:S(2)}) collective-permute-start(bf16[176,384]{1,0:T(8,128)(2,1)S(1)} %get-tuple-element.85), channel_id=1, source_target_pairs={{0,4},{1,5},{2,6},{3,7},{16,20},{17,21},{18,22},{19,23}} | collective-permute-start | bytes 405512 | tf_op jit(solution)/shard_map/ppermute | solution.py:335
  17.1 0.7 %collective-permute-start.5 = (bf16[176,384]{1,0:T(8,128)(2,1)S(1)}, bf16[176,384]{1,0:T(8,128)(2,1)S(1)}, u32[]{:S(2)}, u32[]{:S(2)}) collective-permute-start(bf16[176,384]{1,0:T(8,128)(2,1)S(1)} %frame.19), channel_id=1, source_target_pairs={{0,4},{1,5},{2,6},{3,7},{16,20},{17,21},{18,22},{19,23}} | collective-permute-start | bytes 405512 | tf_op jit(solution)/shard_map/ppermute | solution.py:335
  17.8 1.3 %collective-permute-start.12 = (bf16[160,384]{1,0:T(8,128)(2,1)S(1)}, bf16[160,384]{1,0:T(8,128)(2,1)S(1)}, u32[]{:S(2)}, u32[]{:S(2)}) collective-permute-start(bf16[160,384]{1,0:T(8,128)(2,1)S(1)} %get-tuple-element.99), channel_id=1, source_target_pairs={{4,8},{5,9},{6,10},{7,11},{20,24},{21,25},{22,26},{23,27}} | collective-permute-start | bytes 368648 | tf_op jit(solution)/shard_map/ppermute | solution.py:335
  19.2 1.3 %collective-permute-start.11 = (bf16[160,384]{1,0:T(8,128)(2,1)S(1)}, bf16[160,384]{1,0:T(8,128)(2,1)S(1)}, u32[]{:S(2)}, u32[]{:S(2)}) collective-permute-start(bf16[160,384]{1,0:T(8,128)(2,1)S(1)} %get-tuple-element.98), channel_id=1, source_target_pairs={{4,8},{5,9},{6,10},{7,11},{20,24},{21,25},{22,26},{23,27}} | collective-permute-start | bytes 368648 | tf_op jit(solution)/shard_map/ppermute | solution.py:335
  20.7 1.3 %collective-permute-start.10 = (bf16[160,384]{1,0:T(8,128)(2,1)S(1)}, bf16[160,384]{1,0:T(8,128)(2,1)S(1)}, u32[]{:S(2)}, u32[]{:S(2)}) collective-permute-start(bf16[160,384]{1,0:T(8,128)(2,1)S(1)} %get-tuple-element.97), channel_id=1, source_target_pairs={{4,8},{5,9},{6,10},{7,11},{20,24},{21,25},{22,26},{23,27}} | collective-permute-start | bytes 368648 | tf_op jit(solution)/shard_map/ppermute | solution.py:335
  22.1 1.3 %collective-permute-start.9 = (bf16[160,384]{1,0:T(8,128)(2,1)S(1)}, bf16[160,384]{1,0:T(8,128)(2,1)S(1)}, u32[]{:S(2)}, u32[]{:S(2)}) collective-permute-start(bf16[160,384]{1,0:T(8,128)(2,1)S(1)} %frame.23), channel_id=1, source_target_pairs={{4,8},{5,9},{6,10},{7,11},{20,24},{21,25},{22,26},{23,27}} | collective-permute-start | bytes 368648 | tf_op jit(solution)/shard_map/ppermute | solution.py:335
  23.4 5.8 %collective-permute-done.12.refs_0_ = bf16[160,384]{1,0:T(8,128)(2,1)S(1)} collective-permute-done((bf16[160,384]{1,0:T(8,128)(2,1)S(1)}, bf16[160,384]{1,0:T(8,128)(2,1)S(1)}, u32[]{:S(2)}, u32[]{:S(2)}) %collective-permute-start.12) | collective-permute-done | bytes 122912 | tf_op jit(solution)/shard_map/ppermute | solution.py:335
  29.2 1.0 %frame.24 = (bf16[144,384]{1,0:T(8,128)(2,1)S(1)}, bf16[224,1152]{1,0:T(8,128)(2,1)S(1)}) custom-call(bf16[160,384]{1,0:T(8,128)(2,1)S(1)} %collective-permute-done.12.refs_0_, f32[176,384]{1,0:T(8,128)S(1)} %get-tuple-element.96.refs_1_.near, bf16[3456,384]{1,0:T(8,128)(2,1)S(1)} %get-tuple-element.73.refs_5_.refs_2_, ...), custom_call_target="tpu_custom_call" | custom-call | bytes 1024 | tf_op jit(solution)/shard_map/frame/pallas_call | solution.py:319
  30.2 1.3 %collective-permute-start.16 = (bf16[144,384]{1,0:T(8,128)(2,1)S(1)}, bf16[144,384]{1,0:T(8,128)(2,1)S(1)}, u32[]{:S(2)}, u32[]{:S(2)}) collective-permute-start(bf16[144,384]{1,0:T(8,128)(2,1)S(1)} %get-tuple-element.111), channel_id=1, source_target_pairs={{8,12},{9,13},{10,14},{11,15},{24,28},{25,29},{26,30},{27,31}} | collective-permute-start | bytes 331784 | tf_op jit(solution)/shard_map/ppermute | solution.py:335
  31.5 1.1 %history.18 = (f32[176,384]{1,0:T(8,128)S(1)}, f32[176,384]{1,0:T(8,128)S(1)}) custom-call(bf16[224,1152]{1,0:T(8,128)(2,1)S(1)} %get-tuple-element.100.spread, f32[176,384]{1,0:T(8,128)S(1)} %get-tuple-element.96.refs_1_.near, f32[176,384]{1,0:T(8,128)S(1)} %get-tuple-element.101.far, ...), custom_call_target="tpu_custom_call", output_to_operand_aliasing={{0}: (1, {}), {1}: (2, {})} | custom-call | bytes 1024 | tf_op jit(solution)/shard_map/history/pallas_call | solution.py:360
  33.0 1.0 %frame.25 = (bf16[144,384]{1,0:T(8,128)(2,1)S(1)}, bf16[224,1152]{1,0:T(8,128)(2,1)S(1)}) custom-call(bf16[160,384]{1,0:T(8,128)(2,1)S(1)} %collective-permute-done.11.refs_0_, f32[176,384]{1,0:T(8,128)S(1)} %get-tuple-element.102.refs_1_.near, bf16[3456,384]{1,0:T(8,128)(2,1)S(1)} %get-tuple-element.73.refs_5_.refs_2_, ...), custom_call_target="tpu_custom_call" | custom-call | bytes 1024 | tf_op jit(solution)/shard_map/frame/pallas_call | solution.py:319
  33.9 1.3 %collective-permute-start.15 = (bf16[144,384]{1,0:T(8,128)(2,1)S(1)}, bf16[144,384]{1,0:T(8,128)(2,1)S(1)}, u32[]{:S(2)}, u32[]{:S(2)}) collective-permute-start(bf16[144,384]{1,0:T(8,128)(2,1)S(1)} %get-tuple-element.110), channel_id=1, source_target_pairs={{8,12},{9,13},{10,14},{11,15},{24,28},{25,29},{26,30},{27,31}} | collective-permute-start | bytes 331784 | tf_op jit(solution)/shard_map/ppermute | solution.py:335
  35.2 1.1 %history.19 = (f32[176,384]{1,0:T(8,128)S(1)}, f32[176,384]{1,0:T(8,128)S(1)}) custom-call(bf16[224,1152]{1,0:T(8,128)(2,1)S(1)} %get-tuple-element.103.spread, f32[176,384]{1,0:T(8,128)S(1)} %get-tuple-element.102.refs_1_.near, f32[176,384]{1,0:T(8,128)S(1)} %get-tuple-element.104.far, ...), custom_call_target="tpu_custom_call", output_to_operand_aliasing={{0}: (1, {}), {1}: (2, {})} | custom-call | bytes 1024 | tf_op jit(solution)/shard_map/history/pallas_call | solution.py:360
  36.7 1.0 %frame.26 = (bf16[144,384]{1,0:T(8,128)(2,1)S(1)}, bf16[224,1152]{1,0:T(8,128)(2,1)S(1)}) custom-call(bf16[160,384]{1,0:T(8,128)(2,1)S(1)} %collective-permute-done.10.refs_0_, f32[176,384]{1,0:T(8,128)S(1)} %get-tuple-element.105.refs_1_.near, bf16[3456,384]{1,0:T(8,128)(2,1)S(1)} %get-tuple-element.73.refs_5_.refs_2_, ...), custom_call_target="tpu_custom_call" | custom-call | bytes 1024 | tf_op jit(solution)/shard_map/frame/pallas_call | solution.py:319
  37.7 1.3 %collective-permute-start.14 = (bf16[144,384]{1,0:T(8,128)(2,1)S(1)}, bf16[144,384]{1,0:T(8,128)(2,1)S(1)}, u32[]{:S(2)}, u32[]{:S(2)}) collective-permute-start(bf16[144,384]{1,0:T(8,128)(2,1)S(1)} %get-tuple-element.109), channel_id=1, source_target_pairs={{8,12},{9,13},{10,14},{11,15},{24,28},{25,29},{26,30},{27,31}} | collective-permute-start | bytes 331784 | tf_op jit(solution)/shard_map/ppermute | solution.py:335
  39.0 1.1 %history.20 = (f32[176,384]{1,0:T(8,128)S(1)}, f32[176,384]{1,0:T(8,128)S(1)}) custom-call(bf16[224,1152]{1,0:T(8,128)(2,1)S(1)} %get-tuple-element.106.spread, f32[176,384]{1,0:T(8,128)S(1)} %get-tuple-element.105.refs_1_.near, f32[176,384]{1,0:T(8,128)S(1)} %get-tuple-element.107.far, ...), custom_call_target="tpu_custom_call", output_to_operand_aliasing={{0}: (1, {}), {1}: (2, {})} | custom-call | bytes 1024 | tf_op jit(solution)/shard_map/history/pallas_call | solution.py:360
  40.4 1.0 %frame.27 = bf16[144,384]{1,0:T(8,128)(2,1)S(1)} custom-call(bf16[160,384]{1,0:T(8,128)(2,1)S(1)} %collective-permute-done.9.refs_0_, f32[176,384]{1,0:T(8,128)S(1)} %get-tuple-element.108.refs_1_.near, bf16[3456,384]{1,0:T(8,128)(2,1)S(1)} %get-tuple-element.73.refs_5_.refs_2_, f32[1,384]{1,0:T(1,128)S(1)} %get-tuple-element.74.refs_6_.refs_3_, ...), custom_call_target="tpu_custom_call" | custom-call | bytes 1024 | tf_op jit(solution)/shard_map/frame/pallas_call | solution.py:319
  41.4 1.3 %collective-permute-start.13 = (bf16[144,384]{1,0:T(8,128)(2,1)S(1)}, bf16[144,384]{1,0:T(8,128)(2,1)S(1)}, u32[]{:S(2)}, u32[]{:S(2)}) collective-permute-start(bf16[144,384]{1,0:T(8,128)(2,1)S(1)} %frame.27), channel_id=1, source_target_pairs={{8,12},{9,13},{10,14},{11,15},{24,28},{25,29},{26,30},{27,31}} | collective-permute-start | bytes 331784 | tf_op jit(solution)/shard_map/ppermute | solution.py:335
  42.8 0.7 %collective-permute-start.17 = (bf16[2,64,384]{2,1,0:T(8,128)(2,1)S(1)}, bf16[2,64,384]{2,1,0:T(8,128)(2,1)S(1)}, u32[]{:S(2)}, u32[]{:S(2)}) collective-permute-start(bf16[2,64,384]{2,1,0:T(8,128)(2,1)S(1)} %get-tuple-element.125.refs_9_), channel_id=1, source_target_pairs={{12,0},{14,2},{13,4},{15,6}} | collective-permute-start | bytes 294920 | tf_op jit(solution)/shard_map/ppermute | solution.py:254
  43.5 0.7 %collective-permute-start.18 = (bf16[2,64,384]{2,1,0:T(8,128)(2,1)S(1)}, bf16[2,64,384]{2,1,0:T(8,128)(2,1)S(1)}, u32[]{:S(2)}, u32[]{:S(2)}) collective-permute-start(bf16[2,64,384]{2,1,0:T(8,128)(2,1)S(1)} %get-tuple-element.126.refs_10_), channel_id=1, source_target_pairs={{12,1},{14,3},{13,5},{15,7}} | collective-permute-start | bytes 294920 | tf_op jit(solution)/shard_map/ppermute | solution.py:254
  47.0 1.3 %collective-permute-start.22 = (bf16[2,64,384]{2,1,0:T(8,128)(2,1)S(1)}, bf16[2,64,384]{2,1,0:T(8,128)(2,1)S(1)}, u32[]{:S(2)}, u32[]{:S(2)}) collective-permute-start(bf16[2,64,384]{2,1,0:T(8,128)(2,1)S(1)} %get-tuple-element.130), channel_id=1, source_target_pairs={{28,24},{30,26},{29,28},{31,30}} | collective-permute-start | bytes 294920 | tf_op jit(solution)/shard_map/ppermute | solution.py:254
  48.4 8.4 %collective-permute-done.22 = bf16[2,64,384]{2,1,0:T(8,128)(2,1)S(1)} collective-permute-done((bf16[2,64,384]{2,1,0:T(8,128)(2,1)S(1)}, bf16[2,64,384]{2,1,0:T(8,128)(2,1)S(1)}, u32[]{:S(2)}, u32[]{:S(2)}) %collective-permute-start.22) | collective-permute-done | bytes 98336 | tf_op jit(solution)/shard_map/ppermute | solution.py:254
  56.8 0.7 %select_select_fusion = bf16[2,64,384]{2,1,0:T(8,128)(2,1)} fusion(bf16[2,64,384]{2,1,0:T(8,128)(2,1)S(1)} %get-tuple-element.132, bf16[2,64,384]{2,1,0:T(8,128)(2,1)S(1)} %collective-permute-done.21, bf16[2,64,384]{2,1,0:T(8,128)(2,1)S(1)} %get-tuple-element.131, bf16[2,64,384]{2,1,0:T(8,128)(2,1)S(1)} %collective-permute-done.19, ...), kind=kLoop, calls=%fused_computation | loop fusion | flops 344064 | bytes 688132 | tf_op jit(solution)/shard_map/jit(_where)/select_n | solution.py:375
  (47 shorter events, 4.6 us)
Async XLA Ops:
  1.1 13.7 %collective-permute-start.2 = (bf16[2,64,384]{2,1,0:T(8,128)(2,1)S(1)}, bf16[2,64,384]{2,1,0:T(8,128)(2,1)S(1)}, u32[]{:S(2)}, u32[]{:S(2)}) collective-permute-start(bf16[2,64,384]{2,1,0:T(8,128)(2,1)S(1)} %get-tuple-element.72), channel_id=1, source_target_pairs={{0,16},{2,18},{1,17},{3,19},{20,0},{22,2},{21,1},{23,3}} | collective-permute-start | bytes 294920 | tf_op jit(solution)/shard_map/ppermute | solution.py:214
  1.8 13.0 %collective-permute-start.3 = (bf16[2,64,384]{2,1,0:T(8,128)(2,1)S(1)}, bf16[2,64,384]{2,1,0:T(8,128)(2,1)S(1)}, u32[]{:S(2)}, u32[]{:S(2)}) collective-permute-start(bf16[2,64,384]{2,1,0:T(8,128)(2,1)S(1)} %get-tuple-element.69), channel_id=1, source_target_pairs={{14,0},{13,2},{0,1},{2,3},{6,16},{5,18},{8,17},{10,19}} | collective-permute-start | bytes 294920 | tf_op jit(solution)/shard_map/ppermute | solution.py:214
  2.4 12.4 %collective-permute-start.4 = (bf16[2,64,384]{2,1,0:T(8,128)(2,1)S(1)}, bf16[2,64,384]{2,1,0:T(8,128)(2,1)S(1)}, u32[]{:S(2)}, u32[]{:S(2)}) collective-permute-start(bf16[2,64,384]{2,1,0:T(8,128)(2,1)S(1)} %get-tuple-element.70), channel_id=1, source_target_pairs={{1,0},{3,2},{14,1},{13,3},{5,16},{7,18},{10,17},{9,19}} | collective-permute-start | bytes 294920 | tf_op jit(solution)/shard_map/ppermute | solution.py:214
  3.1 13.2 %collective-permute-start = (bf16[2,64,384]{2,1,0:T(8,128)(2,1)S(1)}, bf16[2,64,384]{2,1,0:T(8,128)(2,1)S(1)}, u32[]{:S(2)}, u32[]{:S(2)}) collective-permute-start(bf16[2,64,384]{2,1,0:T(8,128)(2,1)S(1)} %get-tuple-element.69), channel_id=1, source_target_pairs={{22,0},{21,2},{24,1},{26,3},{30,16},{29,18},{16,17},{18,19}} | collective-permute-start | bytes 294920 | tf_op jit(solution)/shard_map/ppermute | solution.py:214
  10.7 5.7 %collective-permute-start.1 = (bf16[2,64,384]{2,1,0:T(8,128)(2,1)S(1)}, bf16[2,64,384]{2,1,0:T(8,128)(2,1)S(1)}, u32[]{:S(2)}, u32[]{:S(2)}) collective-permute-start(bf16[2,64,384]{2,1,0:T(8,128)(2,1)S(1)} %get-tuple-element.70), channel_id=1, source_target_pairs={{21,0},{23,2},{26,1},{25,3},{17,16},{19,18},{30,17},{29,19}} | collective-permute-start | bytes 294920 | tf_op jit(solution)/shard_map/ppermute | solution.py:214
  14.9 2.9 %collective-permute-start.8 = (bf16[176,384]{1,0:T(8,128)(2,1)S(1)}, bf16[176,384]{1,0:T(8,128)(2,1)S(1)}, u32[]{:S(2)}, u32[]{:S(2)}) collective-permute-start(bf16[176,384]{1,0:T(8,128)(2,1)S(1)} %get-tuple-element.87), channel_id=1, source_target_pairs={{0,4},{1,5},{2,6},{3,7},{16,20},{17,21},{18,22},{19,23}} | collective-permute-start | bytes 405512 | tf_op jit(solution)/shard_map/ppermute | solution.py:335
  15.6 3.5 %collective-permute-start.7 = (bf16[176,384]{1,0:T(8,128)(2,1)S(1)}, bf16[176,384]{1,0:T(8,128)(2,1)S(1)}, u32[]{:S(2)}, u32[]{:S(2)}) collective-permute-start(bf16[176,384]{1,0:T(8,128)(2,1)S(1)} %get-tuple-element.86), channel_id=1, source_target_pairs={{0,4},{1,5},{2,6},{3,7},{16,20},{17,21},{18,22},{19,23}} | collective-permute-start | bytes 405512 | tf_op jit(solution)/shard_map/ppermute | solution.py:335
  16.4 4.2 %collective-permute-start.6 = (bf16[176,384]{1,0:T(8,128)(2,1)S(1)}, bf16[176,384]{1,0:T(8,128)(2,1)S(1)}, u32[]{:S(2)}, u32[]{:S(2)}) collective-permute-start(bf16[176,384]{1,0:T(8,128)(2,1)S(1)} %get-tuple-element.85), channel_id=1, source_target_pairs={{0,4},{1,5},{2,6},{3,7},{16,20},{17,21},{18,22},{19,23}} | collective-permute-start | bytes 405512 | tf_op jit(solution)/shard_map/ppermute | solution.py:335
  17.1 5.0 %collective-permute-start.5 = (bf16[176,384]{1,0:T(8,128)(2,1)S(1)}, bf16[176,384]{1,0:T(8,128)(2,1)S(1)}, u32[]{:S(2)}, u32[]{:S(2)}) collective-permute-start(bf16[176,384]{1,0:T(8,128)(2,1)S(1)} %frame.19), channel_id=1, source_target_pairs={{0,4},{1,5},{2,6},{3,7},{16,20},{17,21},{18,22},{19,23}} | collective-permute-start | bytes 405512 | tf_op jit(solution)/shard_map/ppermute | solution.py:335
  17.8 11.4 %collective-permute-start.12 = (bf16[160,384]{1,0:T(8,128)(2,1)S(1)}, bf16[160,384]{1,0:T(8,128)(2,1)S(1)}, u32[]{:S(2)}, u32[]{:S(2)}) collective-permute-start(bf16[160,384]{1,0:T(8,128)(2,1)S(1)} %get-tuple-element.99), channel_id=1, source_target_pairs={{4,8},{5,9},{6,10},{7,11},{20,24},{21,25},{22,26},{23,27}} | collective-permute-start | bytes 368648 | tf_op jit(solution)/shard_map/ppermute | solution.py:335
  19.2 13.8 %collective-permute-start.11 = (bf16[160,384]{1,0:T(8,128)(2,1)S(1)}, bf16[160,384]{1,0:T(8,128)(2,1)S(1)}, u32[]{:S(2)}, u32[]{:S(2)}) collective-permute-start(bf16[160,384]{1,0:T(8,128)(2,1)S(1)} %get-tuple-element.98), channel_id=1, source_target_pairs={{4,8},{5,9},{6,10},{7,11},{20,24},{21,25},{22,26},{23,27}} | collective-permute-start | bytes 368648 | tf_op jit(solution)/shard_map/ppermute | solution.py:335
  20.7 16.0 %collective-permute-start.10 = (bf16[160,384]{1,0:T(8,128)(2,1)S(1)}, bf16[160,384]{1,0:T(8,128)(2,1)S(1)}, u32[]{:S(2)}, u32[]{:S(2)}) collective-permute-start(bf16[160,384]{1,0:T(8,128)(2,1)S(1)} %get-tuple-element.97), channel_id=1, source_target_pairs={{4,8},{5,9},{6,10},{7,11},{20,24},{21,25},{22,26},{23,27}} | collective-permute-start | bytes 368648 | tf_op jit(solution)/shard_map/ppermute | solution.py:335
  22.1 18.3 %collective-permute-start.9 = (bf16[160,384]{1,0:T(8,128)(2,1)S(1)}, bf16[160,384]{1,0:T(8,128)(2,1)S(1)}, u32[]{:S(2)}, u32[]{:S(2)}) collective-permute-start(bf16[160,384]{1,0:T(8,128)(2,1)S(1)} %frame.23), channel_id=1, source_target_pairs={{4,8},{5,9},{6,10},{7,11},{20,24},{21,25},{22,26},{23,27}} | collective-permute-start | bytes 368648 | tf_op jit(solution)/shard_map/ppermute | solution.py:335
  30.2 12.5 %collective-permute-start.16 = (bf16[144,384]{1,0:T(8,128)(2,1)S(1)}, bf16[144,384]{1,0:T(8,128)(2,1)S(1)}, u32[]{:S(2)}, u32[]{:S(2)}) collective-permute-start(bf16[144,384]{1,0:T(8,128)(2,1)S(1)} %get-tuple-element.111), channel_id=1, source_target_pairs={{8,12},{9,13},{10,14},{11,15},{24,28},{25,29},{26,30},{27,31}} | collective-permute-start | bytes 331784 | tf_op jit(solution)/shard_map/ppermute | solution.py:335
  33.9 8.8 %collective-permute-start.15 = (bf16[144,384]{1,0:T(8,128)(2,1)S(1)}, bf16[144,384]{1,0:T(8,128)(2,1)S(1)}, u32[]{:S(2)}, u32[]{:S(2)}) collective-permute-start(bf16[144,384]{1,0:T(8,128)(2,1)S(1)} %get-tuple-element.110), channel_id=1, source_target_pairs={{8,12},{9,13},{10,14},{11,15},{24,28},{25,29},{26,30},{27,31}} | collective-permute-start | bytes 331784 | tf_op jit(solution)/shard_map/ppermute | solution.py:335
  37.7 6.7 %collective-permute-start.14 = (bf16[144,384]{1,0:T(8,128)(2,1)S(1)}, bf16[144,384]{1,0:T(8,128)(2,1)S(1)}, u32[]{:S(2)}, u32[]{:S(2)}) collective-permute-start(bf16[144,384]{1,0:T(8,128)(2,1)S(1)} %get-tuple-element.109), channel_id=1, source_target_pairs={{8,12},{9,13},{10,14},{11,15},{24,28},{25,29},{26,30},{27,31}} | collective-permute-start | bytes 331784 | tf_op jit(solution)/shard_map/ppermute | solution.py:335
  41.4 3.6 %collective-permute-start.13 = (bf16[144,384]{1,0:T(8,128)(2,1)S(1)}, bf16[144,384]{1,0:T(8,128)(2,1)S(1)}, u32[]{:S(2)}, u32[]{:S(2)}) collective-permute-start(bf16[144,384]{1,0:T(8,128)(2,1)S(1)} %frame.27), channel_id=1, source_target_pairs={{8,12},{9,13},{10,14},{11,15},{24,28},{25,29},{26,30},{27,31}} | collective-permute-start | bytes 331784 | tf_op jit(solution)/shard_map/ppermute | solution.py:335
  42.8 2.2 %collective-permute-start.17 = (bf16[2,64,384]{2,1,0:T(8,128)(2,1)S(1)}, bf16[2,64,384]{2,1,0:T(8,128)(2,1)S(1)}, u32[]{:S(2)}, u32[]{:S(2)}) collective-permute-start(bf16[2,64,384]{2,1,0:T(8,128)(2,1)S(1)} %get-tuple-element.125.refs_9_), channel_id=1, source_target_pairs={{12,0},{14,2},{13,4},{15,6}} | collective-permute-start | bytes 294920 | tf_op jit(solution)/shard_map/ppermute | solution.py:254
  43.5 1.6 %collective-permute-start.18 = (bf16[2,64,384]{2,1,0:T(8,128)(2,1)S(1)}, bf16[2,64,384]{2,1,0:T(8,128)(2,1)S(1)}, u32[]{:S(2)}, u32[]{:S(2)}) collective-permute-start(bf16[2,64,384]{2,1,0:T(8,128)(2,1)S(1)} %get-tuple-element.126.refs_10_), channel_id=1, source_target_pairs={{12,1},{14,3},{13,5},{15,7}} | collective-permute-start | bytes 294920 | tf_op jit(solution)/shard_map/ppermute | solution.py:254
  45.0 3.3 %collective-permute-start.19 = (bf16[2,64,384]{2,1,0:T(8,128)(2,1)S(1)}, bf16[2,64,384]{2,1,0:T(8,128)(2,1)S(1)}, u32[]{:S(2)}, u32[]{:S(2)}) collective-permute-start(bf16[2,64,384]{2,1,0:T(8,128)(2,1)S(1)} %get-tuple-element.127), channel_id=1, source_target_pairs={{12,17},{14,19},{13,21},{15,23},{28,9},{30,11},{29,13},{31,15}} | collective-permute-start | bytes 294920 | tf_op jit(solution)/shard_map/ppermute | solution.py:254
  45.7 2.7 %collective-permute-start.20 = (bf16[2,64,384]{2,1,0:T(8,128)(2,1)S(1)}, bf16[2,64,384]{2,1,0:T(8,128)(2,1)S(1)}, u32[]{:S(2)}, u32[]{:S(2)}) collective-permute-start(bf16[2,64,384]{2,1,0:T(8,128)(2,1)S(1)} %get-tuple-element.128), channel_id=1, source_target_pairs={{28,25},{30,27},{29,29},{31,31}} | collective-permute-start | bytes 294920 | tf_op jit(solution)/shard_map/ppermute | solution.py:254
  46.4 2.0 %collective-permute-start.21 = (bf16[2,64,384]{2,1,0:T(8,128)(2,1)S(1)}, bf16[2,64,384]{2,1,0:T(8,128)(2,1)S(1)}, u32[]{:S(2)}, u32[]{:S(2)}) collective-permute-start(bf16[2,64,384]{2,1,0:T(8,128)(2,1)S(1)} %get-tuple-element.129), channel_id=1, source_target_pairs={{12,16},{14,18},{13,20},{15,22},{28,8},{30,10},{29,12},{31,14}} | collective-permute-start | bytes 294920 | tf_op jit(solution)/shard_map/ppermute | solution.py:254
  47.0 9.8 %collective-permute-start.22 = (bf16[2,64,384]{2,1,0:T(8,128)(2,1)S(1)}, bf16[2,64,384]{2,1,0:T(8,128)(2,1)S(1)}, u32[]{:S(2)}, u32[]{:S(2)}) collective-permute-start(bf16[2,64,384]{2,1,0:T(8,128)(2,1)S(1)} %get-tuple-element.130), channel_id=1, source_target_pairs={{28,24},{30,26},{29,28},{31,30}} | collective-permute-start | bytes 294920 | tf_op jit(solution)/shard_map/ppermute | solution.py:254

commit v10 on v9

--- a/solution.py
+++ b/solution.py
@@ -108,7 +108,7 @@
                 number = (code >> (2 * lax.axis_index("band"))) & 3
                 entry[pl.ds(pl.multiple_of(number * step, step), step), :] = piece[cfg["piece_at"]]
 
-            *others, own, crossed = groups
+            *others, own, crossed = groups[:4]
             first, *rest = cfg["places"]
             near = lax.axis_index("tm") == cfg["near"]
             pl.when(near)(functools.partial(place, own, first))
@@ -158,9 +158,14 @@
     def run(unit):
         need = window - unit - 1
         here = pl.ds(0, need * cols)
-        total = jnp.dot(taps(spread, half, need, cols), weight[...], preferred_element_type=jnp.float32)
-        near_out[here, :] = far[here, :] + total[:, channels:]
-        far_out[here, :] = total[:, :channels]
+        ready = taps(spread, half, need, cols)
+        if unit in cfg["ending"]:
+            total = jnp.dot(ready, weight[:, channels:], preferred_element_type=jnp.float32)
+            near_out[here, :] = far[here, :] + total
+        else:
+            total = jnp.dot(ready, weight[...], preferred_element_type=jnp.float32)
+            near_out[here, :] = far[here, :] + total[:, channels:]
+            far_out[here, :] = total[:, :channels]
 
     for unit in cfg["later"]:
         pl.when(on_unit(unit, cfg["holders"]))(functools.partial(run, unit))
@@ -222,7 +227,7 @@
         if t == 0:
             crossed = gather(0, [member for side in range(holders) for member in far_side(side)])
         if t < holders:
-            entries.append(others + [own, crossed])
+            entries.append(others + [own, crossed] + (entries[0][:2] if t else []))
         else:
             routes = [(spot(t, 0, b), spot(0, 0, b)) for b in range(bands)]
             entries.append(others + [lax.ppermute(own, MESH_AXES, routes), gather(0, far_side(t))])
@@ -272,6 +277,7 @@
         cfg = dict(
             units=units,
             later=[s for s in units if slot - lag * s < frames - 1],
+            ending=[s for s in units if slot - lag * s == frames - 2],
             sends=bool(senders_now),
             lowest=min(senders_now, default=0),
             groups=len(entries[slot // own_frames]) if slot < frames else 0,
@@ -368,11 +374,21 @@
                 name="history",
             )(resident(spread), resident(near), resident(far), past)
 
-    result = None
-    for (t, index), (early, late) in landed.items():
-        here = jnp.logical_and(time == t, band % per_half == index)
-        value = jnp.where(position < per_half, early, late)
-        result = value if result is None else jnp.where(here, value, result)
+    chosen = []
+    for (t, index), parts in landed.items():
+        for late, value in enumerate(parts):
+            here = jnp.logical_and(time == t, band % per_half == index)
+            here = jnp.logical_and(here, (position >= per_half) == bool(late))
+            same = [number for number, (_, other) in enumerate(chosen) if other is value]
+            if same:
+                chosen[same[0]] = (jnp.logical_or(here, chosen[same[0]][0]), value)
+            else:
+                chosen.append((here, value))
+    shared = [value for parts in landed.values() for value in parts]
+    chosen.sort(key=lambda pair: sum(value is pair[1] for value in shared))
+    result = chosen[0][1]
+    for here, value in chosen[1:]:
+        result = jnp.where(here, value, result)
     return result.reshape(1, own_frames, own_rows, cols, channels)
 
 

time: 58 us -> 56.8 us (0.979)
  starting transfers between devices: 27.9 us -> 25.7 us
  waiting for transfers between devices: 16 us -> 17.3 us
    ppermute x5, starting transfers between devices: 10.2 us -> 8.03 us  [gather(): return lax.ppermute(sources[number], MESH_AXES, routes)]
    ppermute x12, waiting for transfers between devices: 7.52 us -> 8.86 us  [local(): lax.ppermute(out, 'segment', [(s, s + 1) for s in senders_now])]
  transfers between devices with their start and end apart: 23 -> 23, of which waited for: 6 -> 6; matrix products, arithmetic and copies ran while one was open for 0% -> 0% of each run, Pallas kernels for 20% -> 19%
where the time goes in v10:
time: 56.8 us; the launch traced here: 56.3 us
  starting transfers between devices  25.7 us (45%)
  waiting for transfers between devices  17.3 us (30%)
  Pallas kernels  12 us (21%)
  other arithmetic  0.67 us (1%)
  between operations  0.59 us (1%)
    ppermute x12, starting transfers between devices, local(): lax.ppermute(out, 'segment', [(s, s + 1) for s in senders_now])  13 us
    ppermute x12, waiting for transfers between devices, local(): lax.ppermute(out, 'segment', [(s, s + 1) for s in senders_now])  8.86 us
    ppermute x6, waiting for transfers between devices, leave(): return lax.ppermute(value, MESH_AXES, routes)  8.41 us
    ppermute x5, starting transfers between devices, gather(): return lax.ppermute(sources[number], MESH_AXES, routes)  8.03 us
    ppermute x6, starting transfers between devices, leave(): return lax.ppermute(value, MESH_AXES, routes)  4.62 us
    pallas_call x16, Pallas kernels, local(): pl.pallas_call(functools.partial(frame_kernel, cfg), out_shape=shapes, in...  4.25 us
    pallas_call x1, Pallas kernels, local(): pl.pallas_call(loader_kernel, out_shape=[pltpu.VMEM((TAPS * TAPS * channe...  3.42 us
    pallas_call x12, Pallas kernels, local(): pl.pallas_call(functools.partial(history_kernel, cfg), out_shape=[pltpu.V...  3.27 us
  transfers between devices with their start and end apart: 23, of which 6 were waited for; matrix products, arithmetic and copies ran while one was open for 0% of the time, Pallas kernels for 19%

profile of v10, /device:TPU:18, one launch (start us, length us, event | category | flops | bytes accessed | tf_op | source)
XLA Modules:
  0.0 56.3 jit_solution(3478119214130887381)
XLA Ops:
  0.0 1.1 %pick.1 = (bf16[2,64,384]{2,1,0:T(8,128)(2,1)S(1)}, bf16[2,64,384]{2,1,0:T(8,128)(2,1)S(1)}, bf16[2,64,384]{2,1,0:T(8,128)(2,1)S(1)}, bf16[2,64,384]{2,1,0:T(8,128)(2,1)S(1)}) custom-call(bf16[4,2,64,384]{3,2,1,0:T(8,128)(2,1)} %bitcast.4), custom_call_target="tpu_custom_call" | custom-call | tf_op jit(solution)/shard_map/pick/pallas_call | solution.py:191
  1.1 0.7 %collective-permute-start.3 = (bf16[2,64,384]{2,1,0:T(8,128)(2,1)S(1)}, bf16[2,64,384]{2,1,0:T(8,128)(2,1)S(1)}, u32[]{:S(2)}, u32[]{:S(2)}) collective-permute-start(bf16[2,64,384]{2,1,0:T(8,128)(2,1)S(1)} %get-tuple-element.69), channel_id=1, source_target_pairs={{14,0},{13,2},{0,1},{2,3},{6,16},{5,18},{8,17},{10,19}} | collective-permute-start | bytes 294920 | tf_op jit(solution)/shard_map/ppermute | solution.py:219
  1.8 0.7 %collective-permute-start.4 = (bf16[2,64,384]{2,1,0:T(8,128)(2,1)S(1)}, bf16[2,64,384]{2,1,0:T(8,128)(2,1)S(1)}, u32[]{:S(2)}, u32[]{:S(2)}) collective-permute-start(bf16[2,64,384]{2,1,0:T(8,128)(2,1)S(1)} %get-tuple-element.70), channel_id=1, source_target_pairs={{1,0},{3,2},{14,1},{13,3},{5,16},{7,18},{10,17},{9,19}} | collective-permute-start | bytes 294920 | tf_op jit(solution)/shard_map/ppermute | solution.py:219
  2.4 0.7 %collective-permute-start.2 = (bf16[2,64,384]{2,1,0:T(8,128)(2,1)S(1)}, bf16[2,64,384]{2,1,0:T(8,128)(2,1)S(1)}, u32[]{:S(2)}, u32[]{:S(2)}) collective-permute-start(bf16[2,64,384]{2,1,0:T(8,128)(2,1)S(1)} %get-tuple-element.72), channel_id=1, source_target_pairs={{0,16},{2,18},{1,17},{3,19},{20,0},{22,2},{21,1},{23,3}} | collective-permute-start | bytes 294920 | tf_op jit(solution)/shard_map/ppermute | solution.py:219
  3.1 5.4 %collective-permute-start = (bf16[2,64,384]{2,1,0:T(8,128)(2,1)S(1)}, bf16[2,64,384]{2,1,0:T(8,128)(2,1)S(1)}, u32[]{:S(2)}, u32[]{:S(2)}) collective-permute-start(bf16[2,64,384]{2,1,0:T(8,128)(2,1)S(1)} %get-tuple-element.69), channel_id=1, source_target_pairs={{22,0},{21,2},{24,1},{26,3},{30,16},{29,18},{16,17},{18,19}} | collective-permute-start | bytes 294920 | tf_op jit(solution)/shard_map/ppermute | solution.py:219
  8.5 0.7 %collective-permute-start.1 = (bf16[2,64,384]{2,1,0:T(8,128)(2,1)S(1)}, bf16[2,64,384]{2,1,0:T(8,128)(2,1)S(1)}, u32[]{:S(2)}, u32[]{:S(2)}) collective-permute-start(bf16[2,64,384]{2,1,0:T(8,128)(2,1)S(1)} %get-tuple-element.70), channel_id=1, source_target_pairs={{21,0},{23,2},{26,1},{25,3},{17,16},{19,18},{30,17},{29,19}} | collective-permute-start | bytes 294920 | tf_op jit(solution)/shard_map/ppermute | solution.py:219
  9.1 3.4 %loader.1 = (bf16[3456,384]{1,0:T(8,128)(2,1)S(1)}, bf16[3456,768]{1,0:T(8,128)(2,1)S(1)}, f32[1,384]{1,0:T(1,128)S(1)}, f32[1,384]{1,0:T(1,128)S(1)}) custom-call(bf16[3,3456,384]{2,1,0:T(8,128)(2,1)} %bitcast.3, f32[1,384]{1,0:T(1,128)} %bias.1, f32[1,384]{1,0:T(1,128)} %gain.1), custom_call_target="tpu_custom_call" | custom-call | tf_op jit(solution)/shard_map/loader/pallas_call | solution.py:236
  12.7 0.7 %collective-permute-start.8 = (bf16[176,384]{1,0:T(8,128)(2,1)S(1)}, bf16[176,384]{1,0:T(8,128)(2,1)S(1)}, u32[]{:S(2)}, u32[]{:S(2)}) collective-permute-start(bf16[176,384]{1,0:T(8,128)(2,1)S(1)} %get-tuple-element.87), channel_id=1, source_target_pairs={{0,4},{1,5},{2,6},{3,7},{16,20},{17,21},{18,22},{19,23}} | collective-permute-start | bytes 405512 | tf_op jit(solution)/shard_map/ppermute | solution.py:341
  13.4 0.7 %collective-permute-start.7 = (bf16[176,384]{1,0:T(8,128)(2,1)S(1)}, bf16[176,384]{1,0:T(8,128)(2,1)S(1)}, u32[]{:S(2)}, u32[]{:S(2)}) collective-permute-start(bf16[176,384]{1,0:T(8,128)(2,1)S(1)} %get-tuple-element.86), channel_id=1, source_target_pairs={{0,4},{1,5},{2,6},{3,7},{16,20},{17,21},{18,22},{19,23}} | collective-permute-start | bytes 405512 | tf_op jit(solution)/shard_map/ppermute | solution.py:341
  14.2 0.7 %collective-permute-start.6 = (bf16[176,384]{1,0:T(8,128)(2,1)S(1)}, bf16[176,384]{1,0:T(8,128)(2,1)S(1)}, u32[]{:S(2)}, u32[]{:S(2)}) collective-permute-start(bf16[176,384]{1,0:T(8,128)(2,1)S(1)} %get-tuple-element.85), channel_id=1, source_target_pairs={{0,4},{1,5},{2,6},{3,7},{16,20},{17,21},{18,22},{19,23}} | collective-permute-start | bytes 405512 | tf_op jit(solution)/shard_map/ppermute | solution.py:341
  14.9 0.7 %collective-permute-start.5 = (bf16[176,384]{1,0:T(8,128)(2,1)S(1)}, bf16[176,384]{1,0:T(8,128)(2,1)S(1)}, u32[]{:S(2)}, u32[]{:S(2)}) collective-permute-start(bf16[176,384]{1,0:T(8,128)(2,1)S(1)} %frame.19), channel_id=1, source_target_pairs={{0,4},{1,5},{2,6},{3,7},{16,20},{17,21},{18,22},{19,23}} | collective-permute-start | bytes 405512 | tf_op jit(solution)/shard_map/ppermute | solution.py:341
  15.6 1.3 %collective-permute-start.12 = (bf16[160,384]{1,0:T(8,128)(2,1)S(1)}, bf16[160,384]{1,0:T(8,128)(2,1)S(1)}, u32[]{:S(2)}, u32[]{:S(2)}) collective-permute-start(bf16[160,384]{1,0:T(8,128)(2,1)S(1)} %get-tuple-element.99), channel_id=1, source_target_pairs={{4,8},{5,9},{6,10},{7,11},{20,24},{21,25},{22,26},{23,27}} | collective-permute-start | bytes 368648 | tf_op jit(solution)/shard_map/ppermute | solution.py:341
  17.0 1.3 %collective-permute-start.11 = (bf16[160,384]{1,0:T(8,128)(2,1)S(1)}, bf16[160,384]{1,0:T(8,128)(2,1)S(1)}, u32[]{:S(2)}, u32[]{:S(2)}) collective-permute-start(bf16[160,384]{1,0:T(8,128)(2,1)S(1)} %get-tuple-element.98), channel_id=1, source_target_pairs={{4,8},{5,9},{6,10},{7,11},{20,24},{21,25},{22,26},{23,27}} | collective-permute-start | bytes 368648 | tf_op jit(solution)/shard_map/ppermute | solution.py:341
  18.5 1.3 %collective-permute-start.10 = (bf16[160,384]{1,0:T(8,128)(2,1)S(1)}, bf16[160,384]{1,0:T(8,128)(2,1)S(1)}, u32[]{:S(2)}, u32[]{:S(2)}) collective-permute-start(bf16[160,384]{1,0:T(8,128)(2,1)S(1)} %get-tuple-element.97), channel_id=1, source_target_pairs={{4,8},{5,9},{6,10},{7,11},{20,24},{21,25},{22,26},{23,27}} | collective-permute-start | bytes 368648 | tf_op jit(solution)/shard_map/ppermute | solution.py:341
  19.9 1.3 %collective-permute-start.9 = (bf16[160,384]{1,0:T(8,128)(2,1)S(1)}, bf16[160,384]{1,0:T(8,128)(2,1)S(1)}, u32[]{:S(2)}, u32[]{:S(2)}) collective-permute-start(bf16[160,384]{1,0:T(8,128)(2,1)S(1)} %frame.23), channel_id=1, source_target_pairs={{4,8},{5,9},{6,10},{7,11},{20,24},{21,25},{22,26},{23,27}} | collective-permute-start | bytes 368648 | tf_op jit(solution)/shard_map/ppermute | solution.py:341
  21.2 7.1 %collective-permute-done.12.refs_0_ = bf16[160,384]{1,0:T(8,128)(2,1)S(1)} collective-permute-done((bf16[160,384]{1,0:T(8,128)(2,1)S(1)}, bf16[160,384]{1,0:T(8,128)(2,1)S(1)}, u32[]{:S(2)}, u32[]{:S(2)}) %collective-permute-start.12) | collective-permute-done | bytes 122912 | tf_op jit(solution)/shard_map/ppermute | solution.py:341
  28.3 1.0 %frame.24 = (bf16[144,384]{1,0:T(8,128)(2,1)S(1)}, bf16[224,1152]{1,0:T(8,128)(2,1)S(1)}) custom-call(bf16[160,384]{1,0:T(8,128)(2,1)S(1)} %collective-permute-done.12.refs_0_, f32[176,384]{1,0:T(8,128)S(1)} %get-tuple-element.96.refs_1_.near, bf16[3456,384]{1,0:T(8,128)(2,1)S(1)} %get-tuple-element.73.refs_5_.refs_7_.refs_2_, ...), custom_call_target="tpu_custom_call" | custom-call | bytes 1024 | tf_op jit(solution)/shard_map/frame/pallas_call | solution.py:325
  29.3 1.3 %collective-permute-start.16 = (bf16[144,384]{1,0:T(8,128)(2,1)S(1)}, bf16[144,384]{1,0:T(8,128)(2,1)S(1)}, u32[]{:S(2)}, u32[]{:S(2)}) collective-permute-start(bf16[144,384]{1,0:T(8,128)(2,1)S(1)} %get-tuple-element.111), channel_id=1, source_target_pairs={{8,12},{9,13},{10,14},{11,15},{24,28},{25,29},{26,30},{27,31}} | collective-permute-start | bytes 331784 | tf_op jit(solution)/shard_map/ppermute | solution.py:341
  30.6 1.1 %history.18 = (f32[176,384]{1,0:T(8,128)S(1)}, f32[176,384]{1,0:T(8,128)S(1)}) custom-call(bf16[224,1152]{1,0:T(8,128)(2,1)S(1)} %get-tuple-element.100.spread, f32[176,384]{1,0:T(8,128)S(1)} %get-tuple-element.96.refs_1_.near, f32[176,384]{1,0:T(8,128)S(1)} %get-tuple-element.101.far, ...), custom_call_target="tpu_custom_call", output_to_operand_aliasing={{0}: (1, {}), {1}: (2, {})} | custom-call | bytes 1024 | tf_op jit(solution)/shard_map/history/pallas_call | solution.py:366
  32.1 1.0 %frame.25 = (bf16[144,384]{1,0:T(8,128)(2,1)S(1)}, bf16[224,1152]{1,0:T(8,128)(2,1)S(1)}) custom-call(bf16[160,384]{1,0:T(8,128)(2,1)S(1)} %collective-permute-done.11.refs_0_, f32[176,384]{1,0:T(8,128)S(1)} %get-tuple-element.102.refs_1_.near, bf16[3456,384]{1,0:T(8,128)(2,1)S(1)} %get-tuple-element.73.refs_5_.refs_7_.refs_2_, ...), custom_call_target="tpu_custom_call" | custom-call | bytes 1024 | tf_op jit(solution)/shard_map/frame/pallas_call | solution.py:325
  33.1 1.3 %collective-permute-start.15 = (bf16[144,384]{1,0:T(8,128)(2,1)S(1)}, bf16[144,384]{1,0:T(8,128)(2,1)S(1)}, u32[]{:S(2)}, u32[]{:S(2)}) collective-permute-start(bf16[144,384]{1,0:T(8,128)(2,1)S(1)} %get-tuple-element.110), channel_id=1, source_target_pairs={{8,12},{9,13},{10,14},{11,15},{24,28},{25,29},{26,30},{27,31}} | collective-permute-start | bytes 331784 | tf_op jit(solution)/shard_map/ppermute | solution.py:341
  34.4 1.1 %history.19 = (f32[176,384]{1,0:T(8,128)S(1)}, f32[176,384]{1,0:T(8,128)S(1)}) custom-call(bf16[224,1152]{1,0:T(8,128)(2,1)S(1)} %get-tuple-element.103.spread, f32[176,384]{1,0:T(8,128)S(1)} %get-tuple-element.102.refs_1_.near, f32[176,384]{1,0:T(8,128)S(1)} %get-tuple-element.104.far, ...), custom_call_target="tpu_custom_call", output_to_operand_aliasing={{0}: (1, {}), {1}: (2, {})} | custom-call | bytes 1024 | tf_op jit(solution)/shard_map/history/pallas_call | solution.py:366
  35.8 1.0 %frame.26 = (bf16[144,384]{1,0:T(8,128)(2,1)S(1)}, bf16[224,1152]{1,0:T(8,128)(2,1)S(1)}) custom-call(bf16[160,384]{1,0:T(8,128)(2,1)S(1)} %collective-permute-done.10.refs_0_, f32[176,384]{1,0:T(8,128)S(1)} %get-tuple-element.105.refs_1_.near, bf16[3456,384]{1,0:T(8,128)(2,1)S(1)} %get-tuple-element.73.refs_5_.refs_7_.refs_2_, ...), custom_call_target="tpu_custom_call" | custom-call | bytes 1024 | tf_op jit(solution)/shard_map/frame/pallas_call | solution.py:325
  36.8 1.3 %collective-permute-start.14 = (bf16[144,384]{1,0:T(8,128)(2,1)S(1)}, bf16[144,384]{1,0:T(8,128)(2,1)S(1)}, u32[]{:S(2)}, u32[]{:S(2)}) collective-permute-start(bf16[144,384]{1,0:T(8,128)(2,1)S(1)} %get-tuple-element.109), channel_id=1, source_target_pairs={{8,12},{9,13},{10,14},{11,15},{24,28},{25,29},{26,30},{27,31}} | collective-permute-start | bytes 331784 | tf_op jit(solution)/shard_map/ppermute | solution.py:341
  38.1 0.7 %history.20 = (f32[176,384]{1,0:T(8,128)S(1)}, f32[176,384]{1,0:T(8,128)S(1)}) custom-call(bf16[224,1152]{1,0:T(8,128)(2,1)S(1)} %get-tuple-element.106.spread, f32[176,384]{1,0:T(8,128)S(1)} %get-tuple-element.105.refs_1_.near, f32[176,384]{1,0:T(8,128)S(1)} %get-tuple-element.107.far, ...), custom_call_target="tpu_custom_call", output_to_operand_aliasing={{0}: (1, {}), {1}: (2, {})} | custom-call | bytes 1024 | tf_op jit(solution)/shard_map/history/pallas_call | solution.py:366
  39.2 1.0 %frame.27 = bf16[144,384]{1,0:T(8,128)(2,1)S(1)} custom-call(bf16[160,384]{1,0:T(8,128)(2,1)S(1)} %collective-permute-done.9.refs_0_, f32[176,384]{1,0:T(8,128)S(1)} %get-tuple-element.108.refs_1_.near, bf16[3456,384]{1,0:T(8,128)(2,1)S(1)} %get-tuple-element.73.refs_5_.refs_7_.refs_2_, f32[1,384]{1,0:T(1,128)S(1)} %get-tuple-element.74.refs_6_.refs_8_.refs_3_, ...), custom_call_target="tpu_custom_call" | custom-call | bytes 1024 | tf_op jit(solution)/shard_map/frame/pallas_call | solution.py:325
  40.1 1.3 %collective-permute-start.13 = (bf16[144,384]{1,0:T(8,128)(2,1)S(1)}, bf16[144,384]{1,0:T(8,128)(2,1)S(1)}, u32[]{:S(2)}, u32[]{:S(2)}) collective-permute-start(bf16[144,384]{1,0:T(8,128)(2,1)S(1)} %frame.27), channel_id=1, source_target_pairs={{8,12},{9,13},{10,14},{11,15},{24,28},{25,29},{26,30},{27,31}} | collective-permute-start | bytes 331784 | tf_op jit(solution)/shard_map/ppermute | solution.py:341
  41.5 0.7 %collective-permute-start.17 = (bf16[2,64,384]{2,1,0:T(8,128)(2,1)S(1)}, bf16[2,64,384]{2,1,0:T(8,128)(2,1)S(1)}, u32[]{:S(2)}, u32[]{:S(2)}) collective-permute-start(bf16[2,64,384]{2,1,0:T(8,128)(2,1)S(1)} %get-tuple-element.125.refs_9_), channel_id=1, source_target_pairs={{12,0},{14,2},{13,4},{15,6}} | collective-permute-start | bytes 294920 | tf_op jit(solution)/shard_map/ppermute | solution.py:259
  42.2 0.7 %collective-permute-start.18 = (bf16[2,64,384]{2,1,0:T(8,128)(2,1)S(1)}, bf16[2,64,384]{2,1,0:T(8,128)(2,1)S(1)}, u32[]{:S(2)}, u32[]{:S(2)}) collective-permute-start(bf16[2,64,384]{2,1,0:T(8,128)(2,1)S(1)} %get-tuple-element.126.refs_10_), channel_id=1, source_target_pairs={{12,1},{14,3},{13,5},{15,7}} | collective-permute-start | bytes 294920 | tf_op jit(solution)/shard_map/ppermute | solution.py:259
  45.8 1.3 %collective-permute-start.22 = (bf16[2,64,384]{2,1,0:T(8,128)(2,1)S(1)}, bf16[2,64,384]{2,1,0:T(8,128)(2,1)S(1)}, u32[]{:S(2)}, u32[]{:S(2)}) collective-permute-start(bf16[2,64,384]{2,1,0:T(8,128)(2,1)S(1)} %get-tuple-element.130), channel_id=1, source_target_pairs={{28,24},{30,26},{29,28},{31,30}} | collective-permute-start | bytes 294920 | tf_op jit(solution)/shard_map/ppermute | solution.py:259
  47.2 8.4 %collective-permute-done.22 = bf16[2,64,384]{2,1,0:T(8,128)(2,1)S(1)} collective-permute-done((bf16[2,64,384]{2,1,0:T(8,128)(2,1)S(1)}, bf16[2,64,384]{2,1,0:T(8,128)(2,1)S(1)}, u32[]{:S(2)}, u32[]{:S(2)}) %collective-permute-start.22) | collective-permute-done | bytes 98336 | tf_op jit(solution)/shard_map/ppermute | solution.py:259
  55.6 0.7 %select_select_fusion = bf16[2,64,384]{2,1,0:T(8,128)(2,1)} fusion(bf16[2,64,384]{2,1,0:T(8,128)(2,1)S(1)} %collective-permute-done.19, bf16[2,64,384]{2,1,0:T(8,128)(2,1)S(1)} %collective-permute-done.20, bf16[2,64,384]{2,1,0:T(8,128)(2,1)S(1)} %collective-permute-done.21, bf16[2,64,384]{2,1,0:T(8,128)(2,1)S(1)} %collective-permute-done.22, ...), kind=kLoop, calls=%fused_computation | loop fusion | flops 245760 | bytes 688133 | tf_op jit(solution)/shard_map/jit(_where)/select_n | solution.py:391
  (47 shorter events, 4.6 us)
Async XLA Ops:
  1.1 11.5 %collective-permute-start.3 = (bf16[2,64,384]{2,1,0:T(8,128)(2,1)S(1)}, bf16[2,64,384]{2,1,0:T(8,128)(2,1)S(1)}, u32[]{:S(2)}, u32[]{:S(2)}) collective-permute-start(bf16[2,64,384]{2,1,0:T(8,128)(2,1)S(1)} %get-tuple-element.69), channel_id=1, source_target_pairs={{14,0},{13,2},{0,1},{2,3},{6,16},{5,18},{8,17},{10,19}} | collective-permute-start | bytes 294920 | tf_op jit(solution)/shard_map/ppermute | solution.py:219
  1.8 10.8 %collective-permute-start.4 = (bf16[2,64,384]{2,1,0:T(8,128)(2,1)S(1)}, bf16[2,64,384]{2,1,0:T(8,128)(2,1)S(1)}, u32[]{:S(2)}, u32[]{:S(2)}) collective-permute-start(bf16[2,64,384]{2,1,0:T(8,128)(2,1)S(1)} %get-tuple-element.70), channel_id=1, source_target_pairs={{1,0},{3,2},{14,1},{13,3},{5,16},{7,18},{10,17},{9,19}} | collective-permute-start | bytes 294920 | tf_op jit(solution)/shard_map/ppermute | solution.py:219
  2.4 10.2 %collective-permute-start.2 = (bf16[2,64,384]{2,1,0:T(8,128)(2,1)S(1)}, bf16[2,64,384]{2,1,0:T(8,128)(2,1)S(1)}, u32[]{:S(2)}, u32[]{:S(2)}) collective-permute-start(bf16[2,64,384]{2,1,0:T(8,128)(2,1)S(1)} %get-tuple-element.72), channel_id=1, source_target_pairs={{0,16},{2,18},{1,17},{3,19},{20,0},{22,2},{21,1},{23,3}} | collective-permute-start | bytes 294920 | tf_op jit(solution)/shard_map/ppermute | solution.py:219
  3.1 11.0 %collective-permute-start = (bf16[2,64,384]{2,1,0:T(8,128)(2,1)S(1)}, bf16[2,64,384]{2,1,0:T(8,128)(2,1)S(1)}, u32[]{:S(2)}, u32[]{:S(2)}) collective-permute-start(bf16[2,64,384]{2,1,0:T(8,128)(2,1)S(1)} %get-tuple-element.69), channel_id=1, source_target_pairs={{22,0},{21,2},{24,1},{26,3},{30,16},{29,18},{16,17},{18,19}} | collective-permute-start | bytes 294920 | tf_op jit(solution)/shard_map/ppermute | solution.py:219
  8.5 5.7 %collective-permute-start.1 = (bf16[2,64,384]{2,1,0:T(8,128)(2,1)S(1)}, bf16[2,64,384]{2,1,0:T(8,128)(2,1)S(1)}, u32[]{:S(2)}, u32[]{:S(2)}) collective-permute-start(bf16[2,64,384]{2,1,0:T(8,128)(2,1)S(1)} %get-tuple-element.70), channel_id=1, source_target_pairs={{21,0},{23,2},{26,1},{25,3},{17,16},{19,18},{30,17},{29,19}} | collective-permute-start | bytes 294920 | tf_op jit(solution)/shard_map/ppermute | solution.py:219
  12.7 2.9 %collective-permute-start.8 = (bf16[176,384]{1,0:T(8,128)(2,1)S(1)}, bf16[176,384]{1,0:T(8,128)(2,1)S(1)}, u32[]{:S(2)}, u32[]{:S(2)}) collective-permute-start(bf16[176,384]{1,0:T(8,128)(2,1)S(1)} %get-tuple-element.87), channel_id=1, source_target_pairs={{0,4},{1,5},{2,6},{3,7},{16,20},{17,21},{18,22},{19,23}} | collective-permute-start | bytes 405512 | tf_op jit(solution)/shard_map/ppermute | solution.py:341
  13.4 3.5 %collective-permute-start.7 = (bf16[176,384]{1,0:T(8,128)(2,1)S(1)}, bf16[176,384]{1,0:T(8,128)(2,1)S(1)}, u32[]{:S(2)}, u32[]{:S(2)}) collective-permute-start(bf16[176,384]{1,0:T(8,128)(2,1)S(1)} %get-tuple-element.86), channel_id=1, source_target_pairs={{0,4},{1,5},{2,6},{3,7},{16,20},{17,21},{18,22},{19,23}} | collective-permute-start | bytes 405512 | tf_op jit(solution)/shard_map/ppermute | solution.py:341
  14.2 4.2 %collective-permute-start.6 = (bf16[176,384]{1,0:T(8,128)(2,1)S(1)}, bf16[176,384]{1,0:T(8,128)(2,1)S(1)}, u32[]{:S(2)}, u32[]{:S(2)}) collective-permute-start(bf16[176,384]{1,0:T(8,128)(2,1)S(1)} %get-tuple-element.85), channel_id=1, source_target_pairs={{0,4},{1,5},{2,6},{3,7},{16,20},{17,21},{18,22},{19,23}} | collective-permute-start | bytes 405512 | tf_op jit(solution)/shard_map/ppermute | solution.py:341
  14.9 5.0 %collective-permute-start.5 = (bf16[176,384]{1,0:T(8,128)(2,1)S(1)}, bf16[176,384]{1,0:T(8,128)(2,1)S(1)}, u32[]{:S(2)}, u32[]{:S(2)}) collective-permute-start(bf16[176,384]{1,0:T(8,128)(2,1)S(1)} %frame.19), channel_id=1, source_target_pairs={{0,4},{1,5},{2,6},{3,7},{16,20},{17,21},{18,22},{19,23}} | collective-permute-start | bytes 405512 | tf_op jit(solution)/shard_map/ppermute | solution.py:341
  15.6 12.7 %collective-permute-start.12 = (bf16[160,384]{1,0:T(8,128)(2,1)S(1)}, bf16[160,384]{1,0:T(8,128)(2,1)S(1)}, u32[]{:S(2)}, u32[]{:S(2)}) collective-permute-start(bf16[160,384]{1,0:T(8,128)(2,1)S(1)} %get-tuple-element.99), channel_id=1, source_target_pairs={{4,8},{5,9},{6,10},{7,11},{20,24},{21,25},{22,26},{23,27}} | collective-permute-start | bytes 368648 | tf_op jit(solution)/shard_map/ppermute | solution.py:341
  17.0 15.1 %collective-permute-start.11 = (bf16[160,384]{1,0:T(8,128)(2,1)S(1)}, bf16[160,384]{1,0:T(8,128)(2,1)S(1)}, u32[]{:S(2)}, u32[]{:S(2)}) collective-permute-start(bf16[160,384]{1,0:T(8,128)(2,1)S(1)} %get-tuple-element.98), channel_id=1, source_target_pairs={{4,8},{5,9},{6,10},{7,11},{20,24},{21,25},{22,26},{23,27}} | collective-permute-start | bytes 368648 | tf_op jit(solution)/shard_map/ppermute | solution.py:341
  18.5 17.3 %collective-permute-start.10 = (bf16[160,384]{1,0:T(8,128)(2,1)S(1)}, bf16[160,384]{1,0:T(8,128)(2,1)S(1)}, u32[]{:S(2)}, u32[]{:S(2)}) collective-permute-start(bf16[160,384]{1,0:T(8,128)(2,1)S(1)} %get-tuple-element.97), channel_id=1, source_target_pairs={{4,8},{5,9},{6,10},{7,11},{20,24},{21,25},{22,26},{23,27}} | collective-permute-start | bytes 368648 | tf_op jit(solution)/shard_map/ppermute | solution.py:341
  19.9 19.3 %collective-permute-start.9 = (bf16[160,384]{1,0:T(8,128)(2,1)S(1)}, bf16[160,384]{1,0:T(8,128)(2,1)S(1)}, u32[]{:S(2)}, u32[]{:S(2)}) collective-permute-start(bf16[160,384]{1,0:T(8,128)(2,1)S(1)} %frame.23), channel_id=1, source_target_pairs={{4,8},{5,9},{6,10},{7,11},{20,24},{21,25},{22,26},{23,27}} | collective-permute-start | bytes 368648 | tf_op jit(solution)/shard_map/ppermute | solution.py:341
  29.3 12.1 %collective-permute-start.16 = (bf16[144,384]{1,0:T(8,128)(2,1)S(1)}, bf16[144,384]{1,0:T(8,128)(2,1)S(1)}, u32[]{:S(2)}, u32[]{:S(2)}) collective-permute-start(bf16[144,384]{1,0:T(8,128)(2,1)S(1)} %get-tuple-element.111), channel_id=1, source_target_pairs={{8,12},{9,13},{10,14},{11,15},{24,28},{25,29},{26,30},{27,31}} | collective-permute-start | bytes 331784 | tf_op jit(solution)/shard_map/ppermute | solution.py:341
  33.1 8.4 %collective-permute-start.15 = (bf16[144,384]{1,0:T(8,128)(2,1)S(1)}, bf16[144,384]{1,0:T(8,128)(2,1)S(1)}, u32[]{:S(2)}, u32[]{:S(2)}) collective-permute-start(bf16[144,384]{1,0:T(8,128)(2,1)S(1)} %get-tuple-element.110), channel_id=1, source_target_pairs={{8,12},{9,13},{10,14},{11,15},{24,28},{25,29},{26,30},{27,31}} | collective-permute-start | bytes 331784 | tf_op jit(solution)/shard_map/ppermute | solution.py:341
  36.8 6.3 %collective-permute-start.14 = (bf16[144,384]{1,0:T(8,128)(2,1)S(1)}, bf16[144,384]{1,0:T(8,128)(2,1)S(1)}, u32[]{:S(2)}, u32[]{:S(2)}) collective-permute-start(bf16[144,384]{1,0:T(8,128)(2,1)S(1)} %get-tuple-element.109), channel_id=1, source_target_pairs={{8,12},{9,13},{10,14},{11,15},{24,28},{25,29},{26,30},{27,31}} | collective-permute-start | bytes 331784 | tf_op jit(solution)/shard_map/ppermute | solution.py:341
  40.1 3.7 %collective-permute-start.13 = (bf16[144,384]{1,0:T(8,128)(2,1)S(1)}, bf16[144,384]{1,0:T(8,128)(2,1)S(1)}, u32[]{:S(2)}, u32[]{:S(2)}) collective-permute-start(bf16[144,384]{1,0:T(8,128)(2,1)S(1)} %frame.27), channel_id=1, source_target_pairs={{8,12},{9,13},{10,14},{11,15},{24,28},{25,29},{26,30},{27,31}} | collective-permute-start | bytes 331784 | tf_op jit(solution)/shard_map/ppermute | solution.py:341
  41.5 2.3 %collective-permute-start.17 = (bf16[2,64,384]{2,1,0:T(8,128)(2,1)S(1)}, bf16[2,64,384]{2,1,0:T(8,128)(2,1)S(1)}, u32[]{:S(2)}, u32[]{:S(2)}) collective-permute-start(bf16[2,64,384]{2,1,0:T(8,128)(2,1)S(1)} %get-tuple-element.125.refs_9_), channel_id=1, source_target_pairs={{12,0},{14,2},{13,4},{15,6}} | collective-permute-start | bytes 294920 | tf_op jit(solution)/shard_map/ppermute | solution.py:259
  42.2 1.6 %collective-permute-start.18 = (bf16[2,64,384]{2,1,0:T(8,128)(2,1)S(1)}, bf16[2,64,384]{2,1,0:T(8,128)(2,1)S(1)}, u32[]{:S(2)}, u32[]{:S(2)}) collective-permute-start(bf16[2,64,384]{2,1,0:T(8,128)(2,1)S(1)} %get-tuple-element.126.refs_10_), channel_id=1, source_target_pairs={{12,1},{14,3},{13,5},{15,7}} | collective-permute-start | bytes 294920 | tf_op jit(solution)/shard_map/ppermute | solution.py:259
  43.8 3.4 %collective-permute-start.19 = (bf16[2,64,384]{2,1,0:T(8,128)(2,1)S(1)}, bf16[2,64,384]{2,1,0:T(8,128)(2,1)S(1)}, u32[]{:S(2)}, u32[]{:S(2)}) collective-permute-start(bf16[2,64,384]{2,1,0:T(8,128)(2,1)S(1)} %get-tuple-element.127), channel_id=1, source_target_pairs={{12,17},{14,19},{13,21},{15,23},{28,9},{30,11},{29,13},{31,15}} | collective-permute-start | bytes 294920 | tf_op jit(solution)/shard_map/ppermute | solution.py:259
  44.5 2.7 %collective-permute-start.20 = (bf16[2,64,384]{2,1,0:T(8,128)(2,1)S(1)}, bf16[2,64,384]{2,1,0:T(8,128)(2,1)S(1)}, u32[]{:S(2)}, u32[]{:S(2)}) collective-permute-start(bf16[2,64,384]{2,1,0:T(8,128)(2,1)S(1)} %get-tuple-element.128), channel_id=1, source_target_pairs={{12,16},{14,18},{13,20},{15,22},{28,8},{30,10},{29,12},{31,14}} | collective-permute-start | bytes 294920 | tf_op jit(solution)/shard_map/ppermute | solution.py:259
  45.1 2.0 %collective-permute-start.21 = (bf16[2,64,384]{2,1,0:T(8,128)(2,1)S(1)}, bf16[2,64,384]{2,1,0:T(8,128)(2,1)S(1)}, u32[]{:S(2)}, u32[]{:S(2)}) collective-permute-start(bf16[2,64,384]{2,1,0:T(8,128)(2,1)S(1)} %get-tuple-element.129), channel_id=1, source_target_pairs={{28,25},{30,27},{29,29},{31,31}} | collective-permute-start | bytes 294920 | tf_op jit(solution)/shard_map/ppermute | solution.py:259
  45.8 9.8 %collective-permute-start.22 = (bf16[2,64,384]{2,1,0:T(8,128)(2,1)S(1)}, bf16[2,64,384]{2,1,0:T(8,128)(2,1)S(1)}, u32[]{:S(2)}, u32[]{:S(2)}) collective-permute-start(bf16[2,64,384]{2,1,0:T(8,128)(2,1)S(1)} %get-tuple-element.130), channel_id=1, source_target_pairs={{28,24},{30,26},{29,28},{31,30}} | collective-permute-start | bytes 294920 | tf_op jit(solution)/shard_map/ppermute | solution.py:259

commit v11 on v10

--- a/solution.py
+++ b/solution.py
@@ -91,7 +91,8 @@
     out = refs.pop(0) if cfg["sends"] else None
     spread = refs.pop(0 if cfg["later"] else -1)
     tails = [refs.pop(0) for _ in range(cfg["finals"])]
-    merged = [refs.pop(0) for _ in range(cfg["keeps"])][cfg["merged"] :][: cfg["finals"]]
+    refs = refs[cfg["keeps"] :]
+    doubles = [refs.pop(0) for _ in range(cfg["doubles"])]
     entry = refs.pop(0)
     cols, window, segments = cfg["cols"], cfg["window"], cfg["segments"]
     channels = entry.shape[-1]
@@ -140,11 +141,8 @@
             length = value.shape[0] // len(tails)
             for number, tail in enumerate(tails):
                 tail[cfg["tail_at"]] = value[number * length : (number + 1) * length]
-
-            @pl.when(lax.axis_index("tm") == 0)
-            def _():
-                for tail, ref in zip(tails, merged):
-                    ref[...] = tail[...]
+            for double, tail in zip(doubles, tails):
+                double[...] = tail[...]
 
     for unit in cfg["units"]:
         pl.when(on_unit(unit, cfg["holders"]))(functools.partial(run, unit))
@@ -249,13 +247,12 @@
     )(*[pltpu.with_memory_space_constraint(value, pltpu.HBM) for value in stored])
     now, past, bias, gain = (resident(value) for value in (now, past, bias, gain))
 
-    def leave(value, members):
+    def leave(value, there, index, group):
         routes = []
-        for there, index, clip in members:
+        for clip in group:
             for h in range(HALVES):
                 t, b = stream(clip, h)
                 routes.append((spot(t, segments - 1, b), spot(there, clip, h * per_half + index)))
-        assert len({a for a, _ in routes}) == len({b for _, b in routes}) == len(routes)
         return lax.ppermute(value, MESH_AXES, routes)
 
     state = ((window - 1) * cols, channels)
@@ -273,7 +270,10 @@
         last = slot - lag * (segments - 1)
         finals = per_half if last >= 0 else 0
         middle = finals and last % own_frames > 0
-        keeps = len(landed) + len(waiting) if slot + 1 == slots else 0
+        closing = slot + 1 == slots
+        old = [key for key, (_, since) in landed.items() if closing and since < slot - 1]
+        keeps = len(old) + len(waiting)
+        doubles = finals if finals and not closing and last % own_frames == own_frames - 1 else 0
         cfg = dict(
             units=units,
             later=[s for s in units if slot - lag * s < frames - 1],
@@ -289,7 +289,7 @@
             tail_at=last % own_frames,
             passing=(finals if middle else 0) + keeps,
             keeps=keeps,
-            merged=len(landed),
+            doubles=doubles,
             cols=cols,
             window=window,
             segments=segments,
@@ -315,12 +315,11 @@
                 aliases[len(operands)] = len(shapes) + index
                 operands.append(resident(value))
         shapes += [shape] * finals
-        held = list(landed) if slot + 1 == slots else []
-        kept = [landed[key][0] for key in held] + ([value for _, _, value in waiting] if held else [])
-        for value in kept:
+        for value in [landed[key][0] for key in old] + [value for _, _, value in waiting]:
             aliases[len(operands)] = len(shapes)
             operands.append(resident(value))
             shapes.append(shape)
+        shapes += [shape] * doubles
         results = list(
             pl.pallas_call(
                 functools.partial(frame_kernel, cfg),
@@ -339,29 +338,19 @@
         tails = results[:finals]
         if cfg["sends"]:
             moving[slot] = lax.ppermute(out, "segment", [(s, s + 1) for s in senders_now])
-        if slot + 1 == slots:
-            kept = results[finals:]
-            landed.update({key: [value] for key, value in zip(held, kept)})
-            waiting = [(there, index, value) for (there, index, _), value in zip(waiting, kept[len(held) :])]
+        kept = results[finals:]
+        for key, value in zip(old, kept):
+            landed[key] = (value, slot)
+        for (there, index, _), value in zip(waiting, kept[len(old) :]):
+            landed[there, index, 1] = (leave(value, there, index, range(per_half, clips)), slot)
+        waiting = []
         if finals and last % own_frames == own_frames - 1:
             there = last // own_frames
-            final = there == times - 1
-            if not final:
-                for index, value in enumerate(tails):
-                    landed[there, index] = [leave(value, [(there, index, clip) for clip in range(per_half)])]
-                waiting += [(there, index, value) for index, value in enumerate(tails)]
-            else:
-                late = range(per_half, clips)
-                pairs_left = [((there, index, value), waiting.pop(0)) for index, value in enumerate(tails)]
-                for (_, index, _), (before, _, value) in pairs_left:
-                    both = [(there, index, clip) for clip in range(per_half)] + [(before, index, clip) for clip in late]
-                    sent = leave(value, both)
-                    landed[there, index] = [sent]
-                    landed[before, index].append(sent)
-                for before, index, value in waiting:
-                    landed[before, index].append(leave(value, [(before, index, clip) for clip in late]))
-                for (_, index, value), _ in pairs_left:
-                    landed[there, index].append(leave(value, [(there, index, clip) for clip in late]))
+            if not closing:
+                waiting = [(there, index, value) for index, value in enumerate(kept[keeps:])]
+            for index, value in enumerate(tails):
+                group = range(clips if closing else per_half)
+                landed[there, index, 0] = (leave(value, there, index, group), slot)
         if cfg["later"]:
             near, far = pl.pallas_call(
                 functools.partial(history_kernel, cfg),
@@ -374,21 +363,12 @@
                 name="history",
             )(resident(spread), resident(near), resident(far), past)
 
-    chosen = []
-    for (t, index), parts in landed.items():
-        for late, value in enumerate(parts):
-            here = jnp.logical_and(time == t, band % per_half == index)
+    result = None
+    for (t, index, late), (value, _) in landed.items():
+        here = jnp.logical_and(time == t, band % per_half == index)
+        if t < times - 1:
             here = jnp.logical_and(here, (position >= per_half) == bool(late))
-            same = [number for number, (_, other) in enumerate(chosen) if other is value]
-            if same:
-                chosen[same[0]] = (jnp.logical_or(here, chosen[same[0]][0]), value)
-            else:
-                chosen.append((here, value))
-    shared = [value for parts in landed.values() for value in parts]
-    chosen.sort(key=lambda pair: sum(value is pair[1] for value in shared))
-    result = chosen[0][1]
-    for here, value in chosen[1:]:
-        result = jnp.where(here, value, result)
+        result = value if result is None else jnp.where(here, value, result)
     return result.reshape(1, own_frames, own_rows, cols, channels)
 
 

time: 56.8 us -> 55.1 us (0.970)
  waiting for transfers between devices: 17.3 us -> 15.5 us
    ppermute x6, waiting for transfers between devices: 8.41 us -> 7.22 us  [leave(): return lax.ppermute(value, MESH_AXES, routes)]
    ppermute x12, waiting for transfers between devices: 8.86 us -> 8.28 us  [local(): lax.ppermute(out, 'segment', [(s, s + 1) for s in senders_now])]
  transfers between devices with their start and end apart: 23 -> 23, of which waited for: 6 -> 5; matrix products, arithmetic and copies ran while one was open for 0% -> 0% of each run, Pallas kernels for 19% -> 20%
where the time goes in v11:
time: 55.1 us; the launch traced here: 54.5 us
  starting transfers between devices  25.7 us (47%)
  waiting for transfers between devices  15.5 us (28%)
  Pallas kernels  12 us (22%)
  other arithmetic  0.67 us (1%)
  between operations  0.61 us (1%)
    ppermute x12, starting transfers between devices, local(): lax.ppermute(out, 'segment', [(s, s + 1) for s in senders_now])  13 us
    ppermute x12, waiting for transfers between devices, local(): lax.ppermute(out, 'segment', [(s, s + 1) for s in senders_now])  8.28 us
    ppermute x5, starting transfers between devices, gather(): return lax.ppermute(sources[number], MESH_AXES, routes)  8.03 us
    ppermute x6, waiting for transfers between devices, leave(): return lax.ppermute(value, MESH_AXES, routes)  7.22 us
    ppermute x6, starting transfers between devices, leave(): return lax.ppermute(value, MESH_AXES, routes)  4.63 us
    pallas_call x16, Pallas kernels, local(): pl.pallas_call(functools.partial(frame_kernel, cfg), out_shape=shapes, in...  4.27 us
    pallas_call x1, Pallas kernels, local(): pl.pallas_call(loader_kernel, out_shape=[pltpu.VMEM((TAPS * TAPS * channe...  3.42 us
    pallas_call x12, Pallas kernels, local(): pl.pallas_call(functools.partial(history_kernel, cfg), out_shape=[pltpu.V...  3.27 us
  transfers between devices with their start and end apart: 23, of which 5 were waited for; matrix products, arithmetic and copies ran while one was open for 0% of the time, Pallas kernels for 20%

profile of v11, /device:TPU:18, one launch (start us, length us, event | category | flops | bytes accessed | tf_op | source)
XLA Modules:
  0.0 54.5 jit_solution(9569227267718852220)
XLA Ops:
  0.0 1.1 %pick.1 = (bf16[2,64,384]{2,1,0:T(8,128)(2,1)S(1)}, bf16[2,64,384]{2,1,0:T(8,128)(2,1)S(1)}, bf16[2,64,384]{2,1,0:T(8,128)(2,1)S(1)}, bf16[2,64,384]{2,1,0:T(8,128)(2,1)S(1)}) custom-call(bf16[4,2,64,384]{3,2,1,0:T(8,128)(2,1)} %bitcast.4), custom_call_target="tpu_custom_call" | custom-call | tf_op jit(solution)/shard_map/pick/pallas_call | solution.py:189
  1.1 0.7 %collective-permute-start.3 = (bf16[2,64,384]{2,1,0:T(8,128)(2,1)S(1)}, bf16[2,64,384]{2,1,0:T(8,128)(2,1)S(1)}, u32[]{:S(2)}, u32[]{:S(2)}) collective-permute-start(bf16[2,64,384]{2,1,0:T(8,128)(2,1)S(1)} %get-tuple-element.71), channel_id=1, source_target_pairs={{14,0},{13,2},{0,1},{2,3},{6,16},{5,18},{8,17},{10,19}} | collective-permute-start | bytes 294920 | tf_op jit(solution)/shard_map/ppermute | solution.py:217
  1.8 0.7 %collective-permute-start.4 = (bf16[2,64,384]{2,1,0:T(8,128)(2,1)S(1)}, bf16[2,64,384]{2,1,0:T(8,128)(2,1)S(1)}, u32[]{:S(2)}, u32[]{:S(2)}) collective-permute-start(bf16[2,64,384]{2,1,0:T(8,128)(2,1)S(1)} %get-tuple-element.72), channel_id=1, source_target_pairs={{1,0},{3,2},{14,1},{13,3},{5,16},{7,18},{10,17},{9,19}} | collective-permute-start | bytes 294920 | tf_op jit(solution)/shard_map/ppermute | solution.py:217
  2.4 0.7 %collective-permute-start.2 = (bf16[2,64,384]{2,1,0:T(8,128)(2,1)S(1)}, bf16[2,64,384]{2,1,0:T(8,128)(2,1)S(1)}, u32[]{:S(2)}, u32[]{:S(2)}) collective-permute-start(bf16[2,64,384]{2,1,0:T(8,128)(2,1)S(1)} %get-tuple-element.74), channel_id=1, source_target_pairs={{0,16},{2,18},{1,17},{3,19},{20,0},{22,2},{21,1},{23,3}} | collective-permute-start | bytes 294920 | tf_op jit(solution)/shard_map/ppermute | solution.py:217
  3.1 5.4 %collective-permute-start = (bf16[2,64,384]{2,1,0:T(8,128)(2,1)S(1)}, bf16[2,64,384]{2,1,0:T(8,128)(2,1)S(1)}, u32[]{:S(2)}, u32[]{:S(2)}) collective-permute-start(bf16[2,64,384]{2,1,0:T(8,128)(2,1)S(1)} %get-tuple-element.71), channel_id=1, source_target_pairs={{22,0},{21,2},{24,1},{26,3},{30,16},{29,18},{16,17},{18,19}} | collective-permute-start | bytes 294920 | tf_op jit(solution)/shard_map/ppermute | solution.py:217
  8.5 0.7 %collective-permute-start.1 = (bf16[2,64,384]{2,1,0:T(8,128)(2,1)S(1)}, bf16[2,64,384]{2,1,0:T(8,128)(2,1)S(1)}, u32[]{:S(2)}, u32[]{:S(2)}) collective-permute-start(bf16[2,64,384]{2,1,0:T(8,128)(2,1)S(1)} %get-tuple-element.72), channel_id=1, source_target_pairs={{21,0},{23,2},{26,1},{25,3},{17,16},{19,18},{30,17},{29,19}} | collective-permute-start | bytes 294920 | tf_op jit(solution)/shard_map/ppermute | solution.py:217
  9.1 3.4 %loader.1 = (bf16[3456,384]{1,0:T(8,128)(2,1)S(1)}, bf16[3456,768]{1,0:T(8,128)(2,1)S(1)}, f32[1,384]{1,0:T(1,128)S(1)}, f32[1,384]{1,0:T(1,128)S(1)}) custom-call(bf16[3,3456,384]{2,1,0:T(8,128)(2,1)} %bitcast.3, f32[1,384]{1,0:T(1,128)} %bias.1, f32[1,384]{1,0:T(1,128)} %gain.1), custom_call_target="tpu_custom_call" | custom-call | tf_op jit(solution)/shard_map/loader/pallas_call | solution.py:234
  12.7 0.7 %collective-permute-start.8 = (bf16[176,384]{1,0:T(8,128)(2,1)S(1)}, bf16[176,384]{1,0:T(8,128)(2,1)S(1)}, u32[]{:S(2)}, u32[]{:S(2)}) collective-permute-start(bf16[176,384]{1,0:T(8,128)(2,1)S(1)} %get-tuple-element.89), channel_id=1, source_target_pairs={{0,4},{1,5},{2,6},{3,7},{16,20},{17,21},{18,22},{19,23}} | collective-permute-start | bytes 405512 | tf_op jit(solution)/shard_map/ppermute | solution.py:340
  13.4 0.7 %collective-permute-start.7 = (bf16[176,384]{1,0:T(8,128)(2,1)S(1)}, bf16[176,384]{1,0:T(8,128)(2,1)S(1)}, u32[]{:S(2)}, u32[]{:S(2)}) collective-permute-start(bf16[176,384]{1,0:T(8,128)(2,1)S(1)} %get-tuple-element.88), channel_id=1, source_target_pairs={{0,4},{1,5},{2,6},{3,7},{16,20},{17,21},{18,22},{19,23}} | collective-permute-start | bytes 405512 | tf_op jit(solution)/shard_map/ppermute | solution.py:340
  14.2 0.7 %collective-permute-start.6 = (bf16[176,384]{1,0:T(8,128)(2,1)S(1)}, bf16[176,384]{1,0:T(8,128)(2,1)S(1)}, u32[]{:S(2)}, u32[]{:S(2)}) collective-permute-start(bf16[176,384]{1,0:T(8,128)(2,1)S(1)} %get-tuple-element.87), channel_id=1, source_target_pairs={{0,4},{1,5},{2,6},{3,7},{16,20},{17,21},{18,22},{19,23}} | collective-permute-start | bytes 405512 | tf_op jit(solution)/shard_map/ppermute | solution.py:340
  14.9 0.7 %collective-permute-start.5 = (bf16[176,384]{1,0:T(8,128)(2,1)S(1)}, bf16[176,384]{1,0:T(8,128)(2,1)S(1)}, u32[]{:S(2)}, u32[]{:S(2)}) collective-permute-start(bf16[176,384]{1,0:T(8,128)(2,1)S(1)} %frame.19), channel_id=1, source_target_pairs={{0,4},{1,5},{2,6},{3,7},{16,20},{17,21},{18,22},{19,23}} | collective-permute-start | bytes 405512 | tf_op jit(solution)/shard_map/ppermute | solution.py:340
  15.6 1.3 %collective-permute-start.12 = (bf16[160,384]{1,0:T(8,128)(2,1)S(1)}, bf16[160,384]{1,0:T(8,128)(2,1)S(1)}, u32[]{:S(2)}, u32[]{:S(2)}) collective-permute-start(bf16[160,384]{1,0:T(8,128)(2,1)S(1)} %get-tuple-element.101), channel_id=1, source_target_pairs={{4,8},{5,9},{6,10},{7,11},{20,24},{21,25},{22,26},{23,27}} | collective-permute-start | bytes 368648 | tf_op jit(solution)/shard_map/ppermute | solution.py:340
  17.0 1.3 %collective-permute-start.11 = (bf16[160,384]{1,0:T(8,128)(2,1)S(1)}, bf16[160,384]{1,0:T(8,128)(2,1)S(1)}, u32[]{:S(2)}, u32[]{:S(2)}) collective-permute-start(bf16[160,384]{1,0:T(8,128)(2,1)S(1)} %get-tuple-element.100), channel_id=1, source_target_pairs={{4,8},{5,9},{6,10},{7,11},{20,24},{21,25},{22,26},{23,27}} | collective-permute-start | bytes 368648 | tf_op jit(solution)/shard_map/ppermute | solution.py:340
  18.5 1.3 %collective-permute-start.10 = (bf16[160,384]{1,0:T(8,128)(2,1)S(1)}, bf16[160,384]{1,0:T(8,128)(2,1)S(1)}, u32[]{:S(2)}, u32[]{:S(2)}) collective-permute-start(bf16[160,384]{1,0:T(8,128)(2,1)S(1)} %get-tuple-element.99), channel_id=1, source_target_pairs={{4,8},{5,9},{6,10},{7,11},{20,24},{21,25},{22,26},{23,27}} | collective-permute-start | bytes 368648 | tf_op jit(solution)/shard_map/ppermute | solution.py:340
  19.9 1.3 %collective-permute-start.9 = (bf16[160,384]{1,0:T(8,128)(2,1)S(1)}, bf16[160,384]{1,0:T(8,128)(2,1)S(1)}, u32[]{:S(2)}, u32[]{:S(2)}) collective-permute-start(bf16[160,384]{1,0:T(8,128)(2,1)S(1)} %frame.23), channel_id=1, source_target_pairs={{4,8},{5,9},{6,10},{7,11},{20,24},{21,25},{22,26},{23,27}} | collective-permute-start | bytes 368648 | tf_op jit(solution)/shard_map/ppermute | solution.py:340
  21.2 7.1 %collective-permute-done.12.refs_0_ = bf16[160,384]{1,0:T(8,128)(2,1)S(1)} collective-permute-done((bf16[160,384]{1,0:T(8,128)(2,1)S(1)}, bf16[160,384]{1,0:T(8,128)(2,1)S(1)}, u32[]{:S(2)}, u32[]{:S(2)}) %collective-permute-start.12) | collective-permute-done | bytes 122912 | tf_op jit(solution)/shard_map/ppermute | solution.py:340
  28.3 1.0 %frame.24 = (bf16[144,384]{1,0:T(8,128)(2,1)S(1)}, bf16[224,1152]{1,0:T(8,128)(2,1)S(1)}) custom-call(bf16[160,384]{1,0:T(8,128)(2,1)S(1)} %collective-permute-done.12.refs_0_, f32[176,384]{1,0:T(8,128)S(1)} %get-tuple-element.98.refs_1_.near, bf16[3456,384]{1,0:T(8,128)(2,1)S(1)} %get-tuple-element.75.refs_5_.refs_7_.refs_2_, ...), custom_call_target="tpu_custom_call" | custom-call | bytes 1024 | tf_op jit(solution)/shard_map/frame/pallas_call | solution.py:324
  29.3 1.3 %collective-permute-start.16 = (bf16[144,384]{1,0:T(8,128)(2,1)S(1)}, bf16[144,384]{1,0:T(8,128)(2,1)S(1)}, u32[]{:S(2)}, u32[]{:S(2)}) collective-permute-start(bf16[144,384]{1,0:T(8,128)(2,1)S(1)} %get-tuple-element.113), channel_id=1, source_target_pairs={{8,12},{9,13},{10,14},{11,15},{24,28},{25,29},{26,30},{27,31}} | collective-permute-start | bytes 331784 | tf_op jit(solution)/shard_map/ppermute | solution.py:340
  30.6 1.1 %history.18 = (f32[176,384]{1,0:T(8,128)S(1)}, f32[176,384]{1,0:T(8,128)S(1)}) custom-call(bf16[224,1152]{1,0:T(8,128)(2,1)S(1)} %get-tuple-element.102.spread, f32[176,384]{1,0:T(8,128)S(1)} %get-tuple-element.98.refs_1_.near, f32[176,384]{1,0:T(8,128)S(1)} %get-tuple-element.103.far, ...), custom_call_target="tpu_custom_call", output_to_operand_aliasing={{0}: (1, {}), {1}: (2, {})} | custom-call | bytes 1024 | tf_op jit(solution)/shard_map/history/pallas_call | solution.py:355
  32.1 1.0 %frame.25 = (bf16[144,384]{1,0:T(8,128)(2,1)S(1)}, bf16[224,1152]{1,0:T(8,128)(2,1)S(1)}) custom-call(bf16[160,384]{1,0:T(8,128)(2,1)S(1)} %collective-permute-done.11.refs_0_, f32[176,384]{1,0:T(8,128)S(1)} %get-tuple-element.104.refs_1_.near, bf16[3456,384]{1,0:T(8,128)(2,1)S(1)} %get-tuple-element.75.refs_5_.refs_7_.refs_2_, ...), custom_call_target="tpu_custom_call" | custom-call | bytes 1024 | tf_op jit(solution)/shard_map/frame/pallas_call | solution.py:324
  33.1 1.3 %collective-permute-start.15 = (bf16[144,384]{1,0:T(8,128)(2,1)S(1)}, bf16[144,384]{1,0:T(8,128)(2,1)S(1)}, u32[]{:S(2)}, u32[]{:S(2)}) collective-permute-start(bf16[144,384]{1,0:T(8,128)(2,1)S(1)} %get-tuple-element.112), channel_id=1, source_target_pairs={{8,12},{9,13},{10,14},{11,15},{24,28},{25,29},{26,30},{27,31}} | collective-permute-start | bytes 331784 | tf_op jit(solution)/shard_map/ppermute | solution.py:340
  34.4 1.1 %history.19 = (f32[176,384]{1,0:T(8,128)S(1)}, f32[176,384]{1,0:T(8,128)S(1)}) custom-call(bf16[224,1152]{1,0:T(8,128)(2,1)S(1)} %get-tuple-element.105.spread, f32[176,384]{1,0:T(8,128)S(1)} %get-tuple-element.104.refs_1_.near, f32[176,384]{1,0:T(8,128)S(1)} %get-tuple-element.106.far, ...), custom_call_target="tpu_custom_call", output_to_operand_aliasing={{0}: (1, {}), {1}: (2, {})} | custom-call | bytes 1024 | tf_op jit(solution)/shard_map/history/pallas_call | solution.py:355
  35.8 1.0 %frame.26 = (bf16[144,384]{1,0:T(8,128)(2,1)S(1)}, bf16[224,1152]{1,0:T(8,128)(2,1)S(1)}) custom-call(bf16[160,384]{1,0:T(8,128)(2,1)S(1)} %collective-permute-done.10.refs_0_, f32[176,384]{1,0:T(8,128)S(1)} %get-tuple-element.107.refs_1_.near, bf16[3456,384]{1,0:T(8,128)(2,1)S(1)} %get-tuple-element.75.refs_5_.refs_7_.refs_2_, ...), custom_call_target="tpu_custom_call" | custom-call | bytes 1024 | tf_op jit(solution)/shard_map/frame/pallas_call | solution.py:324
  36.8 1.3 %collective-permute-start.14 = (bf16[144,384]{1,0:T(8,128)(2,1)S(1)}, bf16[144,384]{1,0:T(8,128)(2,1)S(1)}, u32[]{:S(2)}, u32[]{:S(2)}) collective-permute-start(bf16[144,384]{1,0:T(8,128)(2,1)S(1)} %get-tuple-element.111), channel_id=1, source_target_pairs={{8,12},{9,13},{10,14},{11,15},{24,28},{25,29},{26,30},{27,31}} | collective-permute-start | bytes 331784 | tf_op jit(solution)/shard_map/ppermute | solution.py:340
  38.1 0.7 %history.20 = (f32[176,384]{1,0:T(8,128)S(1)}, f32[176,384]{1,0:T(8,128)S(1)}) custom-call(bf16[224,1152]{1,0:T(8,128)(2,1)S(1)} %get-tuple-element.108.spread, f32[176,384]{1,0:T(8,128)S(1)} %get-tuple-element.107.refs_1_.near, f32[176,384]{1,0:T(8,128)S(1)} %get-tuple-element.109.far, ...), custom_call_target="tpu_custom_call", output_to_operand_aliasing={{0}: (1, {}), {1}: (2, {})} | custom-call | bytes 1024 | tf_op jit(solution)/shard_map/history/pallas_call | solution.py:355
  39.2 1.0 %frame.27 = bf16[144,384]{1,0:T(8,128)(2,1)S(1)} custom-call(bf16[160,384]{1,0:T(8,128)(2,1)S(1)} %collective-permute-done.9.refs_0_, f32[176,384]{1,0:T(8,128)S(1)} %get-tuple-element.110.refs_1_.near, bf16[3456,384]{1,0:T(8,128)(2,1)S(1)} %get-tuple-element.75.refs_5_.refs_7_.refs_2_, f32[1,384]{1,0:T(1,128)S(1)} %get-tuple-element.76.refs_6_.refs_8_.refs_3_, ...), custom_call_target="tpu_custom_call" | custom-call | bytes 1024 | tf_op jit(solution)/shard_map/frame/pallas_call | solution.py:324
  40.1 1.3 %collective-permute-start.13 = (bf16[144,384]{1,0:T(8,128)(2,1)S(1)}, bf16[144,384]{1,0:T(8,128)(2,1)S(1)}, u32[]{:S(2)}, u32[]{:S(2)}) collective-permute-start(bf16[144,384]{1,0:T(8,128)(2,1)S(1)} %frame.27), channel_id=1, source_target_pairs={{8,12},{9,13},{10,14},{11,15},{24,28},{25,29},{26,30},{27,31}} | collective-permute-start | bytes 331784 | tf_op jit(solution)/shard_map/ppermute | solution.py:340
  41.5 0.7 %collective-permute-start.17 = (bf16[2,64,384]{2,1,0:T(8,128)(2,1)S(1)}, bf16[2,64,384]{2,1,0:T(8,128)(2,1)S(1)}, u32[]{:S(2)}, u32[]{:S(2)}) collective-permute-start(bf16[2,64,384]{2,1,0:T(8,128)(2,1)S(1)} %get-tuple-element.129), channel_id=1, source_target_pairs={{12,0},{14,2},{13,4},{15,6}} | collective-permute-start | bytes 294920 | tf_op jit(solution)/shard_map/ppermute | solution.py:256
  42.2 0.7 %collective-permute-start.18 = (bf16[2,64,384]{2,1,0:T(8,128)(2,1)S(1)}, bf16[2,64,384]{2,1,0:T(8,128)(2,1)S(1)}, u32[]{:S(2)}, u32[]{:S(2)}) collective-permute-start(bf16[2,64,384]{2,1,0:T(8,128)(2,1)S(1)} %get-tuple-element.130), channel_id=1, source_target_pairs={{12,1},{14,3},{13,5},{15,7}} | collective-permute-start | bytes 294920 | tf_op jit(solution)/shard_map/ppermute | solution.py:256
  45.3 1.3 %collective-permute-start.20 = (bf16[2,64,384]{2,1,0:T(8,128)(2,1)S(1)}, bf16[2,64,384]{2,1,0:T(8,128)(2,1)S(1)}, u32[]{:S(2)}, u32[]{:S(2)}) collective-permute-start(bf16[2,64,384]{2,1,0:T(8,128)(2,1)S(1)} %get-tuple-element.132), channel_id=1, source_target_pairs={{12,16},{14,18},{13,20},{15,22},{28,24},{30,26},{29,28},{31,30}} | collective-permute-start | bytes 294920 | tf_op jit(solution)/shard_map/ppermute | solution.py:256
  46.7 7.2 %collective-permute-done.20 = bf16[2,64,384]{2,1,0:T(8,128)(2,1)S(1)} collective-permute-done((bf16[2,64,384]{2,1,0:T(8,128)(2,1)S(1)}, bf16[2,64,384]{2,1,0:T(8,128)(2,1)S(1)}, u32[]{:S(2)}, u32[]{:S(2)}) %collective-permute-start.20) | collective-permute-done | bytes 98336 | tf_op jit(solution)/shard_map/ppermute | solution.py:256
  53.9 0.7 %select_select_fusion = bf16[2,64,384]{2,1,0:T(8,128)(2,1)} fusion(bf16[2,64,384]{2,1,0:T(8,128)(2,1)S(1)} %collective-permute-done.19, bf16[2,64,384]{2,1,0:T(8,128)(2,1)S(1)} %collective-permute-done.20, bf16[2,64,384]{2,1,0:T(8,128)(2,1)S(1)} %collective-permute-done.21, bf16[2,64,384]{2,1,0:T(8,128)(2,1)S(1)} %collective-permute-done.22, ...), kind=kLoop, calls=%fused_computation | loop fusion | flops 245760 | bytes 688133 | tf_op jit(solution)/shard_map/jit(_where)/select_n | solution.py:371
  (47 shorter events, 4.1 us)
Async XLA Ops:
  1.1 11.5 %collective-permute-start.3 = (bf16[2,64,384]{2,1,0:T(8,128)(2,1)S(1)}, bf16[2,64,384]{2,1,0:T(8,128)(2,1)S(1)}, u32[]{:S(2)}, u32[]{:S(2)}) collective-permute-start(bf16[2,64,384]{2,1,0:T(8,128)(2,1)S(1)} %get-tuple-element.71), channel_id=1, source_target_pairs={{14,0},{13,2},{0,1},{2,3},{6,16},{5,18},{8,17},{10,19}} | collective-permute-start | bytes 294920 | tf_op jit(solution)/shard_map/ppermute | solution.py:217
  1.8 10.8 %collective-permute-start.4 = (bf16[2,64,384]{2,1,0:T(8,128)(2,1)S(1)}, bf16[2,64,384]{2,1,0:T(8,128)(2,1)S(1)}, u32[]{:S(2)}, u32[]{:S(2)}) collective-permute-start(bf16[2,64,384]{2,1,0:T(8,128)(2,1)S(1)} %get-tuple-element.72), channel_id=1, source_target_pairs={{1,0},{3,2},{14,1},{13,3},{5,16},{7,18},{10,17},{9,19}} | collective-permute-start | bytes 294920 | tf_op jit(solution)/shard_map/ppermute | solution.py:217
  2.4 10.2 %collective-permute-start.2 = (bf16[2,64,384]{2,1,0:T(8,128)(2,1)S(1)}, bf16[2,64,384]{2,1,0:T(8,128)(2,1)S(1)}, u32[]{:S(2)}, u32[]{:S(2)}) collective-permute-start(bf16[2,64,384]{2,1,0:T(8,128)(2,1)S(1)} %get-tuple-element.74), channel_id=1, source_target_pairs={{0,16},{2,18},{1,17},{3,19},{20,0},{22,2},{21,1},{23,3}} | collective-permute-start | bytes 294920 | tf_op jit(solution)/shard_map/ppermute | solution.py:217
  3.1 11.0 %collective-permute-start = (bf16[2,64,384]{2,1,0:T(8,128)(2,1)S(1)}, bf16[2,64,384]{2,1,0:T(8,128)(2,1)S(1)}, u32[]{:S(2)}, u32[]{:S(2)}) collective-permute-start(bf16[2,64,384]{2,1,0:T(8,128)(2,1)S(1)} %get-tuple-element.71), channel_id=1, source_target_pairs={{22,0},{21,2},{24,1},{26,3},{30,16},{29,18},{16,17},{18,19}} | collective-permute-start | bytes 294920 | tf_op jit(solution)/shard_map/ppermute | solution.py:217
  8.5 5.7 %collective-permute-start.1 = (bf16[2,64,384]{2,1,0:T(8,128)(2,1)S(1)}, bf16[2,64,384]{2,1,0:T(8,128)(2,1)S(1)}, u32[]{:S(2)}, u32[]{:S(2)}) collective-permute-start(bf16[2,64,384]{2,1,0:T(8,128)(2,1)S(1)} %get-tuple-element.72), channel_id=1, source_target_pairs={{21,0},{23,2},{26,1},{25,3},{17,16},{19,18},{30,17},{29,19}} | collective-permute-start | bytes 294920 | tf_op jit(solution)/shard_map/ppermute | solution.py:217
  12.7 2.9 %collective-permute-start.8 = (bf16[176,384]{1,0:T(8,128)(2,1)S(1)}, bf16[176,384]{1,0:T(8,128)(2,1)S(1)}, u32[]{:S(2)}, u32[]{:S(2)}) collective-permute-start(bf16[176,384]{1,0:T(8,128)(2,1)S(1)} %get-tuple-element.89), channel_id=1, source_target_pairs={{0,4},{1,5},{2,6},{3,7},{16,20},{17,21},{18,22},{19,23}} | collective-permute-start | bytes 405512 | tf_op jit(solution)/shard_map/ppermute | solution.py:340
  13.4 3.5 %collective-permute-start.7 = (bf16[176,384]{1,0:T(8,128)(2,1)S(1)}, bf16[176,384]{1,0:T(8,128)(2,1)S(1)}, u32[]{:S(2)}, u32[]{:S(2)}) collective-permute-start(bf16[176,384]{1,0:T(8,128)(2,1)S(1)} %get-tuple-element.88), channel_id=1, source_target_pairs={{0,4},{1,5},{2,6},{3,7},{16,20},{17,21},{18,22},{19,23}} | collective-permute-start | bytes 405512 | tf_op jit(solution)/shard_map/ppermute | solution.py:340
  14.2 4.2 %collective-permute-start.6 = (bf16[176,384]{1,0:T(8,128)(2,1)S(1)}, bf16[176,384]{1,0:T(8,128)(2,1)S(1)}, u32[]{:S(2)}, u32[]{:S(2)}) collective-permute-start(bf16[176,384]{1,0:T(8,128)(2,1)S(1)} %get-tuple-element.87), channel_id=1, source_target_pairs={{0,4},{1,5},{2,6},{3,7},{16,20},{17,21},{18,22},{19,23}} | collective-permute-start | bytes 405512 | tf_op jit(solution)/shard_map/ppermute | solution.py:340
  14.9 5.0 %collective-permute-start.5 = (bf16[176,384]{1,0:T(8,128)(2,1)S(1)}, bf16[176,384]{1,0:T(8,128)(2,1)S(1)}, u32[]{:S(2)}, u32[]{:S(2)}) collective-permute-start(bf16[176,384]{1,0:T(8,128)(2,1)S(1)} %frame.19), channel_id=1, source_target_pairs={{0,4},{1,5},{2,6},{3,7},{16,20},{17,21},{18,22},{19,23}} | collective-permute-start | bytes 405512 | tf_op jit(solution)/shard_map/ppermute | solution.py:340
  15.6 12.7 %collective-permute-start.12 = (bf16[160,384]{1,0:T(8,128)(2,1)S(1)}, bf16[160,384]{1,0:T(8,128)(2,1)S(1)}, u32[]{:S(2)}, u32[]{:S(2)}) collective-permute-start(bf16[160,384]{1,0:T(8,128)(2,1)S(1)} %get-tuple-element.101), channel_id=1, source_target_pairs={{4,8},{5,9},{6,10},{7,11},{20,24},{21,25},{22,26},{23,27}} | collective-permute-start | bytes 368648 | tf_op jit(solution)/shard_map/ppermute | solution.py:340
  17.0 15.1 %collective-permute-start.11 = (bf16[160,384]{1,0:T(8,128)(2,1)S(1)}, bf16[160,384]{1,0:T(8,128)(2,1)S(1)}, u32[]{:S(2)}, u32[]{:S(2)}) collective-permute-start(bf16[160,384]{1,0:T(8,128)(2,1)S(1)} %get-tuple-element.100), channel_id=1, source_target_pairs={{4,8},{5,9},{6,10},{7,11},{20,24},{21,25},{22,26},{23,27}} | collective-permute-start | bytes 368648 | tf_op jit(solution)/shard_map/ppermute | solution.py:340
  18.5 17.3 %collective-permute-start.10 = (bf16[160,384]{1,0:T(8,128)(2,1)S(1)}, bf16[160,384]{1,0:T(8,128)(2,1)S(1)}, u32[]{:S(2)}, u32[]{:S(2)}) collective-permute-start(bf16[160,384]{1,0:T(8,128)(2,1)S(1)} %get-tuple-element.99), channel_id=1, source_target_pairs={{4,8},{5,9},{6,10},{7,11},{20,24},{21,25},{22,26},{23,27}} | collective-permute-start | bytes 368648 | tf_op jit(solution)/shard_map/ppermute | solution.py:340
  19.9 19.3 %collective-permute-start.9 = (bf16[160,384]{1,0:T(8,128)(2,1)S(1)}, bf16[160,384]{1,0:T(8,128)(2,1)S(1)}, u32[]{:S(2)}, u32[]{:S(2)}) collective-permute-start(bf16[160,384]{1,0:T(8,128)(2,1)S(1)} %frame.23), channel_id=1, source_target_pairs={{4,8},{5,9},{6,10},{7,11},{20,24},{21,25},{22,26},{23,27}} | collective-permute-start | bytes 368648 | tf_op jit(solution)/shard_map/ppermute | solution.py:340
  29.3 12.1 %collective-permute-start.16 = (bf16[144,384]{1,0:T(8,128)(2,1)S(1)}, bf16[144,384]{1,0:T(8,128)(2,1)S(1)}, u32[]{:S(2)}, u32[]{:S(2)}) collective-permute-start(bf16[144,384]{1,0:T(8,128)(2,1)S(1)} %get-tuple-element.113), channel_id=1, source_target_pairs={{8,12},{9,13},{10,14},{11,15},{24,28},{25,29},{26,30},{27,31}} | collective-permute-start | bytes 331784 | tf_op jit(solution)/shard_map/ppermute | solution.py:340
  33.1 8.4 %collective-permute-start.15 = (bf16[144,384]{1,0:T(8,128)(2,1)S(1)}, bf16[144,384]{1,0:T(8,128)(2,1)S(1)}, u32[]{:S(2)}, u32[]{:S(2)}) collective-permute-start(bf16[144,384]{1,0:T(8,128)(2,1)S(1)} %get-tuple-element.112), channel_id=1, source_target_pairs={{8,12},{9,13},{10,14},{11,15},{24,28},{25,29},{26,30},{27,31}} | collective-permute-start | bytes 331784 | tf_op jit(solution)/shard_map/ppermute | solution.py:340
  36.8 6.3 %collective-permute-start.14 = (bf16[144,384]{1,0:T(8,128)(2,1)S(1)}, bf16[144,384]{1,0:T(8,128)(2,1)S(1)}, u32[]{:S(2)}, u32[]{:S(2)}) collective-permute-start(bf16[144,384]{1,0:T(8,128)(2,1)S(1)} %get-tuple-element.111), channel_id=1, source_target_pairs={{8,12},{9,13},{10,14},{11,15},{24,28},{25,29},{26,30},{27,31}} | collective-permute-start | bytes 331784 | tf_op jit(solution)/shard_map/ppermute | solution.py:340
  40.1 4.4 %collective-permute-start.13 = (bf16[144,384]{1,0:T(8,128)(2,1)S(1)}, bf16[144,384]{1,0:T(8,128)(2,1)S(1)}, u32[]{:S(2)}, u32[]{:S(2)}) collective-permute-start(bf16[144,384]{1,0:T(8,128)(2,1)S(1)} %frame.27), channel_id=1, source_target_pairs={{8,12},{9,13},{10,14},{11,15},{24,28},{25,29},{26,30},{27,31}} | collective-permute-start | bytes 331784 | tf_op jit(solution)/shard_map/ppermute | solution.py:340
  41.5 3.0 %collective-permute-start.17 = (bf16[2,64,384]{2,1,0:T(8,128)(2,1)S(1)}, bf16[2,64,384]{2,1,0:T(8,128)(2,1)S(1)}, u32[]{:S(2)}, u32[]{:S(2)}) collective-permute-start(bf16[2,64,384]{2,1,0:T(8,128)(2,1)S(1)} %get-tuple-element.129), channel_id=1, source_target_pairs={{12,0},{14,2},{13,4},{15,6}} | collective-permute-start | bytes 294920 | tf_op jit(solution)/shard_map/ppermute | solution.py:256
  42.2 2.4 %collective-permute-start.18 = (bf16[2,64,384]{2,1,0:T(8,128)(2,1)S(1)}, bf16[2,64,384]{2,1,0:T(8,128)(2,1)S(1)}, u32[]{:S(2)}, u32[]{:S(2)}) collective-permute-start(bf16[2,64,384]{2,1,0:T(8,128)(2,1)S(1)} %get-tuple-element.130), channel_id=1, source_target_pairs={{12,1},{14,3},{13,5},{15,7}} | collective-permute-start | bytes 294920 | tf_op jit(solution)/shard_map/ppermute | solution.py:256
  43.2 3.5 %collective-permute-start.21 = (bf16[2,64,384]{2,1,0:T(8,128)(2,1)S(1)}, bf16[2,64,384]{2,1,0:T(8,128)(2,1)S(1)}, u32[]{:S(2)}, u32[]{:S(2)}) collective-permute-start(bf16[2,64,384]{2,1,0:T(8,128)(2,1)S(1)} %get-tuple-element.133), channel_id=1, source_target_pairs={{28,9},{30,11},{29,13},{31,15}} | collective-permute-start | bytes 294920 | tf_op jit(solution)/shard_map/ppermute | solution.py:256
  43.9 2.8 %collective-permute-start.22 = (bf16[2,64,384]{2,1,0:T(8,128)(2,1)S(1)}, bf16[2,64,384]{2,1,0:T(8,128)(2,1)S(1)}, u32[]{:S(2)}, u32[]{:S(2)}) collective-permute-start(bf16[2,64,384]{2,1,0:T(8,128)(2,1)S(1)} %get-tuple-element.134), channel_id=1, source_target_pairs={{28,8},{30,10},{29,12},{31,14}} | collective-permute-start | bytes 294920 | tf_op jit(solution)/shard_map/ppermute | solution.py:256
  44.6 2.0 %collective-permute-start.19 = (bf16[2,64,384]{2,1,0:T(8,128)(2,1)S(1)}, bf16[2,64,384]{2,1,0:T(8,128)(2,1)S(1)}, u32[]{:S(2)}, u32[]{:S(2)}) collective-permute-start(bf16[2,64,384]{2,1,0:T(8,128)(2,1)S(1)} %get-tuple-element.131), channel_id=1, source_target_pairs={{12,17},{14,19},{13,21},{15,23},{28,25},{30,27},{29,29},{31,31}} | collective-permute-start | bytes 294920 | tf_op jit(solution)/shard_map/ppermute | solution.py:256
  45.3 8.6 %collective-permute-start.20 = (bf16[2,64,384]{2,1,0:T(8,128)(2,1)S(1)}, bf16[2,64,384]{2,1,0:T(8,128)(2,1)S(1)}, u32[]{:S(2)}, u32[]{:S(2)}) collective-permute-start(bf16[2,64,384]{2,1,0:T(8,128)(2,1)S(1)} %get-tuple-element.132), channel_id=1, source_target_pairs={{12,16},{14,18},{13,20},{15,22},{28,24},{30,26},{29,28},{31,30}} | collective-permute-start | bytes 294920 | tf_op jit(solution)/shard_map/ppermute | solution.py:256

commit v12 on v11

--- a/solution.py
+++ b/solution.py
@@ -41,20 +41,23 @@
     near, far = 2 * side, 2 - 2 * side
     behind = far + ((segment - 1) & 1)
     return (
+        choose(segment == 0, near, far) + 1 - lane,
+        choose(side == 0, behind, far + 1 - lane),
         far + lane,
-        choose(segment == 0, near + 1, choose(segment == 3, near, behind)),
-        choose(segment == 0, near, choose(segment == 3, near + 1, behind)),
+        choose(segment == 3, near, near + 1),
+        choose(segment == 0, near + 1 - lane, behind),
     )
 
 
-def pick_kernel(holders, source, own, across, second, third, sems):
+def pick_kernel(holders, source, *refs):
+    targets, sems = refs[:-1], refs[-1]
     time = lax.axis_index("tm")
     side = jnp.where(time < holders, time, 0)
     lane = lax.axis_index("band") & 1
-    clips = (2 * side + lane, *sent_clips(side, lane, lax.axis_index("segment"), jnp.where))
+    clips = (*sent_clips(side, lane, lax.axis_index("segment"), jnp.where), 2 * side + lane)
     copies = [
         pltpu.make_async_copy(source.at[clip], target, sems.at[number])
-        for number, (clip, target) in enumerate(zip(clips, (own, across, second, third)))
+        for number, (clip, target) in enumerate(zip(clips, targets))
     ]
     for copy in copies:
         copy.start()
@@ -109,13 +112,14 @@
                 number = (code >> (2 * lax.axis_index("band"))) & 3
                 entry[pl.ds(pl.multiple_of(number * step, step), step), :] = piece[cfg["piece_at"]]
 
-            *others, own, crossed = groups[:4]
-            first, *rest = cfg["places"]
             near = lax.axis_index("tm") == cfg["near"]
-            pl.when(near)(functools.partial(place, own, first))
-            pl.when(jnp.logical_not(near))(functools.partial(place, crossed, first))
-            for piece, code in zip(others, rest):
-                place(piece, code)
+            for here, chosen in zip((near, jnp.logical_not(near)), cfg["chosen"]):
+
+                @pl.when(here)
+                def _():
+                    for number, code in zip(chosen, cfg["places"]):
+                        place(groups[number], code)
+
             source, skip = entry, 0
         else:
             source, skip = received, half * (unit - 1 - cfg["came"])
@@ -186,49 +190,45 @@
     def spot(t, s, b):
         return (t * segments + s) * bands + b
 
-    own, *sources = pl.pallas_call(
+    *sources, own = pl.pallas_call(
         functools.partial(pick_kernel, holders),
-        out_shape=[pltpu.VMEM((own_frames, piece, channels), features.dtype)] * 4,
+        out_shape=[pltpu.VMEM((own_frames, piece, channels), features.dtype)] * 6,
         in_specs=[whole(pltpu.HBM)],
-        out_specs=[whole()] * 4,
-        scratch_shapes=[pltpu.SemaphoreType.DMA((4,))],
+        out_specs=[whole()] * 6,
+        scratch_shapes=[pltpu.SemaphoreType.DMA((6,))],
         compiler_params=pltpu.CompilerParams(vmem_limit_bytes=1 << 20),
         name="pick",
     )(pltpu.with_memory_space_constraint(features.reshape(clips, own_frames, piece, channels), pltpu.HBM))
-    wanted = [[2 * h + j for h in range(HALVES) for j in range(per_half)], [2, 0, 1, 2], [1, 2, 3, 1]]
+    wanted = [[0, 1, 2, 3], [1, 0, 3, 2], [2, 2, 1, 1]]
     places = [sum((b - at // per_half) << (2 * at) for at, b in enumerate(row)) for row in wanted]
 
-    def gather(number, members):
+    def gather(number, *members):
         routes = []
-        for t, clip in members:
-            side, (there, lane) = t if t < holders else 0, divmod(clip, per_half)
-            if number == 0:
-                segment = t if t < holders else 1
-            elif there == side:
-                segment = 3 if lane == number - 1 else 0
-            else:
-                segment = 1 + lane
-            for h in range(HALVES):
-                at = stream(clip, h)[1]
-                source = wanted[number][at]
-                assert clip == sent_clips(side, source & 1, segment, lambda a, b, c: b if a else c)[number]
-                routes.append((spot(t, segment, source), spot(there, 0, at)))
+        for t, side, kind, froms in members:
+            for lane in range(per_half):
+                clip = side * per_half + lane
+                for h in range(HALVES):
+                    at = stream(clip, h)[1]
+                    source, segment = wanted[kind][at], froms[lane]
+                    sent = sent_clips(t if t < holders else 0, source & 1, segment, lambda a, b, c: b if a else c)
+                    assert sent[number] == clip
+                    routes.append((spot(t, segment, source), spot(side, 0, at)))
         assert len({a for a, _ in routes}) == len({b for _, b in routes}) == len(routes)
         return lax.ppermute(sources[number], MESH_AXES, routes)
 
-    def far_side(t):
-        return [(t, clip) for clip in range(clips) if clip // per_half != (t if t < holders else 0)]
-
-    entries = []
-    for t in range(times):
-        others = [gather(number, [(t, clip) for clip in range(clips)]) for number in (1, 2)]
-        if t == 0:
-            crossed = gather(0, [member for side in range(holders) for member in far_side(side)])
-        if t < holders:
-            entries.append(others + [own, crossed] + (entries[0][:2] if t else []))
-        else:
-            routes = [(spot(t, 0, b), spot(0, 0, b)) for b in range(bands)]
-            entries.append(others + [lax.ppermute(own, MESH_AXES, routes), gather(0, far_side(t))])
+    siblings = gather(0, (0, 0, 1, (0, 0)), (0, 1, 1, (1, 1)))
+    thirds = gather(1, (0, 1, 2, (1, 2)), (1, 0, 1, (1, 1)))
+    crossed = gather(2, (0, 1, 0, (0, 0)), (1, 0, 0, (1, 1)))
+    nearest = gather(3, (0, 0, 2, (3, 2)), (1, 1, 2, (3, 2)))
+    latest = gather(4, (1, 0, 2, (1, 2)), (1, 1, 1, (0, 0)))
+    early = [siblings, thirds, crossed, nearest, own]
+    entries = [(early, ((4, 0, 3), (2, 0, 1))), (early + [latest], ((4, 5, 3), (2, 1, 5)))]
+    for t in range(holders, times):
+        routes = [(spot(t, 0, b), spot(0, 0, b)) for b in range(bands)]
+        group = [lax.ppermute(own, MESH_AXES, routes), gather(2, (t, 1, 0, (1, 1)))]
+        group += [gather(0, (t, 0, 1, (0, 0)), (t, 1, 1, (1, 1)))]
+        group += [gather(3, (t, 0, 2, (3, 2))), gather(1, (t, 1, 2, (1, 2)))]
+        entries.append((group, ((0, 2, 3), (1, 2, 4))))
 
     stored = [conv_weight[0].reshape(TAPS, TAPS * TAPS * channels, channels), conv_bias, norm_gain]
     now, past, bias, gain = pl.pallas_call(
@@ -280,7 +280,8 @@
             ending=[s for s in units if slot - lag * s == frames - 2],
             sends=bool(senders_now),
             lowest=min(senders_now, default=0),
-            groups=len(entries[slot // own_frames]) if slot < frames else 0,
+            groups=len(entries[slot // own_frames][0]) if slot < frames else 0,
+            chosen=entries[slot // own_frames][1] if slot < frames else (),
             places=places,
             piece_at=slot % own_frames,
             near=slot // own_frames if slot // own_frames < holders else 0,
@@ -298,7 +299,7 @@
         )
         operands = []
         if slot < frames:
-            operands += [resident(value) for value in entries[slot // own_frames]]
+            operands += [resident(value) for value in entries[slot // own_frames][0]]
         if slot >= lag:
             operands.append(resident(moving.pop(slot - lag)))
         operands += [resident(near), now, bias, gain]

time: 55.1 us -> 60.7 us (1.10)
  the two profiles are of different devices: /device:TPU:18 before, /device:TPU:2 now
where the time goes in v12:
time: 60.7 us; the launch traced here: 60.2 us
  waiting for transfers between devices  23.3 us (38%)
  starting transfers between devices  22.2 us (37%)
  Pallas kernels  13.3 us (22%)
  other arithmetic  0.67 us (1%)
    ppermute x6, waiting for transfers between devices, leave(): return lax.ppermute(value, MESH_AXES, routes)  20.3 us
    ppermute x12, starting transfers between devices, local(): lax.ppermute(out, 'segment', [(s, s + 1) for s in senders_now])  10.5 us
    ppermute x5, starting transfers between devices, gather(): return lax.ppermute(sources[number], MESH_AXES, routes)  7.09 us
    pallas_call x16, Pallas kernels, local(): pl.pallas_call(functools.partial(frame_kernel, cfg), out_shape=shapes, in...  5.02 us
    ppermute x6, starting transfers between devices, leave(): return lax.ppermute(value, MESH_AXES, routes)  4.63 us
    pallas_call x12, Pallas kernels, local(): pl.pallas_call(functools.partial(history_kernel, cfg), out_shape=[pltpu.V...  3.73 us
    pallas_call x1, Pallas kernels, local(): pl.pallas_call(loader_kernel, out_shape=[pltpu.VMEM((TAPS * TAPS * channe...  3.42 us
    ppermute x5, waiting for transfers between devices, gather(): return lax.ppermute(sources[number], MESH_AXES, routes)  2.6 us
  transfers between devices with their start and end apart: 23, of which 5 were waited for; matrix products, arithmetic and copies ran while one was open for 0% of the time, Pallas kernels for 20%

profile of v12, /device:TPU:2, one launch (start us, length us, event | category | flops | bytes accessed | tf_op | source)
XLA Modules:
  0.0 60.2 jit_solution(1622289131573189823)
XLA Ops:
  0.0 1.2 %pick.1 = (bf16[2,64,384]{2,1,0:T(8,128)(2,1)S(1)}, bf16[2,64,384]{2,1,0:T(8,128)(2,1)S(1)}, bf16[2,64,384]{2,1,0:T(8,128)(2,1)S(1)}, bf16[2,64,384]{2,1,0:T(8,1...) custom-call(bf16[4,2,64,384]{3,2,1,0:T(8,128)(2,1)} %bitcast.4), custom_call_target="tpu_custom_call" | custom-call | tf_op jit(solution)/shard_map/pick/pallas_call | solution.py:193
  1.2 1.3 %collective-permute-start = (bf16[2,64,384]{2,1,0:T(8,128)(2,1)S(1)}, bf16[2,64,384]{2,1,0:T(8,128)(2,1)S(1)}, u32[]{:S(2)}, u32[]{:S(2)}) collective-permute-start(bf16[2,64,384]{2,1,0:T(8,128)(2,1)S(1)} %get-tuple-element.73), channel_id=1, source_target_pairs={{1,0},{3,2},{0,1},{2,3},{5,16},{7,18},{4,17},{6,19}} | collective-permute-start | bytes 294920 | tf_op jit(solution)/shard_map/ppermute | solution.py:217
  2.5 1.3 %collective-permute-start.1 = (bf16[2,64,384]{2,1,0:T(8,128)(2,1)S(1)}, bf16[2,64,384]{2,1,0:T(8,128)(2,1)S(1)}, u32[]{:S(2)}, u32[]{:S(2)}) collective-permute-start(bf16[2,64,384]{2,1,0:T(8,128)(2,1)S(1)} %get-tuple-element.74), channel_id=1, source_target_pairs={{6,16},{5,18},{10,17},{9,19},{21,0},{23,2},{20,1},{22,3}} | collective-permute-start | bytes 294920 | tf_op jit(solution)/shard_map/ppermute | solution.py:217
  3.8 1.3 %collective-permute-start.2 = (bf16[2,64,384]{2,1,0:T(8,128)(2,1)S(1)}, bf16[2,64,384]{2,1,0:T(8,128)(2,1)S(1)}, u32[]{:S(2)}, u32[]{:S(2)}) collective-permute-start(bf16[2,64,384]{2,1,0:T(8,128)(2,1)S(1)} %get-tuple-element.75), channel_id=1, source_target_pairs={{0,16},{2,18},{1,17},{3,19},{20,0},{22,2},{21,1},{23,3}} | collective-permute-start | bytes 294920 | tf_op jit(solution)/shard_map/ppermute | solution.py:217
  5.1 1.3 %collective-permute-start.3 = (bf16[2,64,384]{2,1,0:T(8,128)(2,1)S(1)}, bf16[2,64,384]{2,1,0:T(8,128)(2,1)S(1)}, u32[]{:S(2)}, u32[]{:S(2)}) collective-permute-start(bf16[2,64,384]{2,1,0:T(8,128)(2,1)S(1)} %get-tuple-element.76), channel_id=1, source_target_pairs={{14,0},{13,2},{10,1},{9,3},{30,16},{29,18},{26,17},{25,19}} | collective-permute-start | bytes 294920 | tf_op jit(solution)/shard_map/ppermute | solution.py:217
  6.4 1.9 %collective-permute-start.4 = (bf16[2,64,384]{2,1,0:T(8,128)(2,1)S(1)}, bf16[2,64,384]{2,1,0:T(8,128)(2,1)S(1)}, u32[]{:S(2)}, u32[]{:S(2)}) collective-permute-start(bf16[2,64,384]{2,1,0:T(8,128)(2,1)S(1)} %get-tuple-element.78), channel_id=1, source_target_pairs={{22,0},{21,2},{26,1},{25,3},{17,16},{19,18},{16,17},{18,19}} | collective-permute-start | bytes 294920 | tf_op jit(solution)/shard_map/ppermute | solution.py:217
  8.3 3.4 %loader.1 = (bf16[3456,384]{1,0:T(8,128)(2,1)S(1)}, bf16[3456,768]{1,0:T(8,128)(2,1)S(1)}, f32[1,384]{1,0:T(1,128)S(1)}, f32[1,384]{1,0:T(1,128)S(1)}) custom-call(bf16[3,3456,384]{2,1,0:T(8,128)(2,1)} %bitcast.3, f32[1,384]{1,0:T(1,128)} %bias.1, f32[1,384]{1,0:T(1,128)} %gain.1), custom_call_target="tpu_custom_call" | custom-call | tf_op jit(solution)/shard_map/loader/pallas_call | solution.py:234
  11.8 0.9 %collective-permute-done.1.refs_1_ = bf16[2,64,384]{2,1,0:T(8,128)(2,1)S(1)} collective-permute-done((bf16[2,64,384]{2,1,0:T(8,128)(2,1)S(1)}, bf16[2,64,384]{2,1,0:T(8,128)(2,1)S(1)}, u32[]{:S(2)}, u32[]{:S(2)}) %collective-permute-start.1) | collective-permute-done | bytes 98336 | tf_op jit(solution)/shard_map/ppermute | solution.py:217
  12.6 0.7 %collective-permute-done.2.refs_2_ = bf16[2,64,384]{2,1,0:T(8,128)(2,1)S(1)} collective-permute-done((bf16[2,64,384]{2,1,0:T(8,128)(2,1)S(1)}, bf16[2,64,384]{2,1,0:T(8,128)(2,1)S(1)}, u32[]{:S(2)}, u32[]{:S(2)}) %collective-permute-start.2) | collective-permute-done | bytes 98336 | tf_op jit(solution)/shard_map/ppermute | solution.py:217
  13.3 1.1 %collective-permute-done.3.refs_3_ = bf16[2,64,384]{2,1,0:T(8,128)(2,1)S(1)} collective-permute-done((bf16[2,64,384]{2,1,0:T(8,128)(2,1)S(1)}, bf16[2,64,384]{2,1,0:T(8,128)(2,1)S(1)}, u32[]{:S(2)}, u32[]{:S(2)}) %collective-permute-start.3) | collective-permute-done | bytes 98336 | tf_op jit(solution)/shard_map/ppermute | solution.py:217
  14.4 1.2 %frame.16 = (bf16[176,384]{1,0:T(8,128)(2,1)S(1)}, bf16[224,1152]{1,0:T(8,128)(2,1)S(1)}) custom-call(bf16[2,64,384]{2,1,0:T(8,128)(2,1)S(1)} %collective-permute-done.refs_0_, bf16[2,64,384]{2,1,0:T(8,128)(2,1)S(1)} %collective-permute-done.1.refs_1_, bf16[2,64,384]{2,1,0:T(8,128)(2,1)S(1)} %collective-permute-done.2.refs_2_, ...), custom_call_target="tpu_custom_call" | custom-call | bytes 1024 | tf_op jit(solution)/shard_map/frame/pallas_call | solution.py:325
  15.5 1.3 %collective-permute-start.8 = (bf16[176,384]{1,0:T(8,128)(2,1)S(1)}, bf16[176,384]{1,0:T(8,128)(2,1)S(1)}, u32[]{:S(2)}, u32[]{:S(2)}) collective-permute-start(bf16[176,384]{1,0:T(8,128)(2,1)S(1)} %get-tuple-element.93), channel_id=1, source_target_pairs={{0,4},{1,5},{2,6},{3,7},{16,20},{17,21},{18,22},{19,23}} | collective-permute-start | bytes 405512 | tf_op jit(solution)/shard_map/ppermute | solution.py:341
  16.9 1.2 %history.12 = (f32[176,384]{1,0:T(8,128)S(1)}, f32[176,384]{1,0:T(8,128)S(1)}) custom-call(bf16[224,1152]{1,0:T(8,128)(2,1)S(1)} %get-tuple-element.82.spread, f32[176,384]{1,0:T(8,128)S(1)} %broadcast_1_refs_5__near_far.2.refs_5_.near, f32[176,384]{1,0:T(8,128)S(1)} %broadcast_1_refs_5__near_far.2.clone.far, ...), custom_call_target="tpu_custom_call", output_to_operand_aliasing={{0}: (1, {}), {1}: (2, {})} | custom-call | bytes 1024 | tf_op jit(solution)/shard_map/history/pallas_call | solution.py:356
  18.1 1.2 %frame.17 = (bf16[176,384]{1,0:T(8,128)(2,1)S(1)}, bf16[224,1152]{1,0:T(8,128)(2,1)S(1)}) custom-call(bf16[2,64,384]{2,1,0:T(8,128)(2,1)S(1)} %collective-permute-done.refs_0_, bf16[2,64,384]{2,1,0:T(8,128)(2,1)S(1)} %collective-permute-done.1.refs_1_, bf16[2,64,384]{2,1,0:T(8,128)(2,1)S(1)} %collective-permute-done.2.refs_2_, ...), custom_call_target="tpu_custom_call" | custom-call | bytes 1024 | tf_op jit(solution)/shard_map/frame/pallas_call | solution.py:325
  19.3 1.3 %collective-permute-start.7 = (bf16[176,384]{1,0:T(8,128)(2,1)S(1)}, bf16[176,384]{1,0:T(8,128)(2,1)S(1)}, u32[]{:S(2)}, u32[]{:S(2)}) collective-permute-start(bf16[176,384]{1,0:T(8,128)(2,1)S(1)} %get-tuple-element.92), channel_id=1, source_target_pairs={{0,4},{1,5},{2,6},{3,7},{16,20},{17,21},{18,22},{19,23}} | collective-permute-start | bytes 405512 | tf_op jit(solution)/shard_map/ppermute | solution.py:341
  20.6 1.2 %history.13 = (f32[176,384]{1,0:T(8,128)S(1)}, f32[176,384]{1,0:T(8,128)S(1)}) custom-call(bf16[224,1152]{1,0:T(8,128)(2,1)S(1)} %get-tuple-element.85.spread, f32[176,384]{1,0:T(8,128)S(1)} %get-tuple-element.84.refs_5_.near, f32[176,384]{1,0:T(8,128)S(1)} %get-tuple-element.86.far, ...), custom_call_target="tpu_custom_call", output_to_operand_aliasing={{0}: (1, {}), {1}: (2, {})} | custom-call | bytes 1024 | tf_op jit(solution)/shard_map/history/pallas_call | solution.py:356
  21.8 1.2 %frame.18 = (bf16[176,384]{1,0:T(8,128)(2,1)S(1)}, bf16[224,1152]{1,0:T(8,128)(2,1)S(1)}) custom-call(bf16[2,64,384]{2,1,0:T(8,128)(2,1)S(1)} %collective-permute-done.refs_0_, bf16[2,64,384]{2,1,0:T(8,128)(2,1)S(1)} %collective-permute-done.1.refs_1_, bf16[2,64,384]{2,1,0:T(8,128)(2,1)S(1)} %collective-permute-done.2.refs_2_, ...), custom_call_target="tpu_custom_call" | custom-call | bytes 1024 | tf_op jit(solution)/shard_map/frame/pallas_call | solution.py:325
  23.0 1.3 %collective-permute-start.6 = (bf16[176,384]{1,0:T(8,128)(2,1)S(1)}, bf16[176,384]{1,0:T(8,128)(2,1)S(1)}, u32[]{:S(2)}, u32[]{:S(2)}) collective-permute-start(bf16[176,384]{1,0:T(8,128)(2,1)S(1)} %get-tuple-element.91), channel_id=1, source_target_pairs={{0,4},{1,5},{2,6},{3,7},{16,20},{17,21},{18,22},{19,23}} | collective-permute-start | bytes 405512 | tf_op jit(solution)/shard_map/ppermute | solution.py:341
  24.3 0.8 %history.14 = (f32[176,384]{1,0:T(8,128)S(1)}, f32[176,384]{1,0:T(8,128)S(1)}) custom-call(bf16[224,1152]{1,0:T(8,128)(2,1)S(1)} %get-tuple-element.88.spread, f32[176,384]{1,0:T(8,128)S(1)} %get-tuple-element.87.refs_6_.near, f32[176,384]{1,0:T(8,128)S(1)} %get-tuple-element.89.far, ...), custom_call_target="tpu_custom_call", output_to_operand_aliasing={{0}: (1, {}), {1}: (2, {})} | custom-call | bytes 1024 | tf_op jit(solution)/shard_map/history/pallas_call | solution.py:356
  25.1 1.1 %frame.19 = bf16[176,384]{1,0:T(8,128)(2,1)S(1)} custom-call(bf16[2,64,384]{2,1,0:T(8,128)(2,1)S(1)} %collective-permute-done.refs_0_, bf16[2,64,384]{2,1,0:T(8,128)(2,1)S(1)} %collective-permute-done.1.refs_1_, bf16[2,64,384]{2,1,0:T(8,128)(2,1)S(1)} %collective-permute-done.2.refs_2_, bf16[2,64,384]{2,1,0:T(8,128)(2,1)S(1)} %collective-permute-done.3.refs_3_, ...), custom_call_target="tpu_custom_call" | custom-call | bytes 1024 | tf_op jit(solution)/shard_map/frame/pallas_call | solution.py:325
  26.3 1.3 %collective-permute-start.5 = (bf16[176,384]{1,0:T(8,128)(2,1)S(1)}, bf16[176,384]{1,0:T(8,128)(2,1)S(1)}, u32[]{:S(2)}, u32[]{:S(2)}) collective-permute-start(bf16[176,384]{1,0:T(8,128)(2,1)S(1)} %frame.19), channel_id=1, source_target_pairs={{0,4},{1,5},{2,6},{3,7},{16,20},{17,21},{18,22},{19,23}} | collective-permute-start | bytes 405512 | tf_op jit(solution)/shard_map/ppermute | solution.py:341
  27.6 0.7 %collective-permute-start.12 = (bf16[160,384]{1,0:T(8,128)(2,1)S(1)}, bf16[160,384]{1,0:T(8,128)(2,1)S(1)}, u32[]{:S(2)}, u32[]{:S(2)}) collective-permute-start(bf16[160,384]{1,0:T(8,128)(2,1)S(1)} %get-tuple-element.105), channel_id=1, source_target_pairs={{4,8},{5,9},{6,10},{7,11},{20,24},{21,25},{22,26},{23,27}} | collective-permute-start | bytes 368648 | tf_op jit(solution)/shard_map/ppermute | solution.py:341
  28.4 0.7 %collective-permute-start.11 = (bf16[160,384]{1,0:T(8,128)(2,1)S(1)}, bf16[160,384]{1,0:T(8,128)(2,1)S(1)}, u32[]{:S(2)}, u32[]{:S(2)}) collective-permute-start(bf16[160,384]{1,0:T(8,128)(2,1)S(1)} %get-tuple-element.104), channel_id=1, source_target_pairs={{4,8},{5,9},{6,10},{7,11},{20,24},{21,25},{22,26},{23,27}} | collective-permute-start | bytes 368648 | tf_op jit(solution)/shard_map/ppermute | solution.py:341
  29.3 0.7 %collective-permute-start.10 = (bf16[160,384]{1,0:T(8,128)(2,1)S(1)}, bf16[160,384]{1,0:T(8,128)(2,1)S(1)}, u32[]{:S(2)}, u32[]{:S(2)}) collective-permute-start(bf16[160,384]{1,0:T(8,128)(2,1)S(1)} %get-tuple-element.103), channel_id=1, source_target_pairs={{4,8},{5,9},{6,10},{7,11},{20,24},{21,25},{22,26},{23,27}} | collective-permute-start | bytes 368648 | tf_op jit(solution)/shard_map/ppermute | solution.py:341
  31.1 0.7 %collective-permute-start.16 = (bf16[144,384]{1,0:T(8,128)(2,1)S(1)}, bf16[144,384]{1,0:T(8,128)(2,1)S(1)}, u32[]{:S(2)}, u32[]{:S(2)}) collective-permute-start(bf16[144,384]{1,0:T(8,128)(2,1)S(1)} %get-tuple-element.117), channel_id=1, source_target_pairs={{8,12},{9,13},{10,14},{11,15},{24,28},{25,29},{26,30},{27,31}} | collective-permute-start | bytes 331784 | tf_op jit(solution)/shard_map/ppermute | solution.py:341
  31.8 0.7 %collective-permute-start.15 = (bf16[144,384]{1,0:T(8,128)(2,1)S(1)}, bf16[144,384]{1,0:T(8,128)(2,1)S(1)}, u32[]{:S(2)}, u32[]{:S(2)}) collective-permute-start(bf16[144,384]{1,0:T(8,128)(2,1)S(1)} %get-tuple-element.116), channel_id=1, source_target_pairs={{8,12},{9,13},{10,14},{11,15},{24,28},{25,29},{26,30},{27,31}} | collective-permute-start | bytes 331784 | tf_op jit(solution)/shard_map/ppermute | solution.py:341
  32.6 0.7 %collective-permute-start.14 = (bf16[144,384]{1,0:T(8,128)(2,1)S(1)}, bf16[144,384]{1,0:T(8,128)(2,1)S(1)}, u32[]{:S(2)}, u32[]{:S(2)}) collective-permute-start(bf16[144,384]{1,0:T(8,128)(2,1)S(1)} %get-tuple-element.115), channel_id=1, source_target_pairs={{8,12},{9,13},{10,14},{11,15},{24,28},{25,29},{26,30},{27,31}} | collective-permute-start | bytes 331784 | tf_op jit(solution)/shard_map/ppermute | solution.py:341
  33.3 0.7 %collective-permute-start.13 = (bf16[144,384]{1,0:T(8,128)(2,1)S(1)}, bf16[144,384]{1,0:T(8,128)(2,1)S(1)}, u32[]{:S(2)}, u32[]{:S(2)}) collective-permute-start(bf16[144,384]{1,0:T(8,128)(2,1)S(1)} %frame.27), channel_id=1, source_target_pairs={{8,12},{9,13},{10,14},{11,15},{24,28},{25,29},{26,30},{27,31}} | collective-permute-start | bytes 331784 | tf_op jit(solution)/shard_map/ppermute | solution.py:341
  36.4 0.7 %collective-permute-start.22 = (bf16[2,64,384]{2,1,0:T(8,128)(2,1)S(1)}, bf16[2,64,384]{2,1,0:T(8,128)(2,1)S(1)}, u32[]{:S(2)}, u32[]{:S(2)}) collective-permute-start(bf16[2,64,384]{2,1,0:T(8,128)(2,1)S(1)} %get-tuple-element.138), channel_id=1, source_target_pairs={{28,8},{30,10},{29,12},{31,14}} | collective-permute-start | bytes 294920 | tf_op jit(solution)/shard_map/ppermute | solution.py:256
  37.9 1.3 %collective-permute-start.20 = (bf16[2,64,384]{2,1,0:T(8,128)(2,1)S(1)}, bf16[2,64,384]{2,1,0:T(8,128)(2,1)S(1)}, u32[]{:S(2)}, u32[]{:S(2)}) collective-permute-start(bf16[2,64,384]{2,1,0:T(8,128)(2,1)S(1)} %get-tuple-element.136), channel_id=1, source_target_pairs={{12,16},{14,18},{13,20},{15,22},{28,24},{30,26},{29,28},{31,30}} | collective-permute-start | bytes 294920 | tf_op jit(solution)/shard_map/ppermute | solution.py:256
  39.2 20.3 %collective-permute-done.20 = bf16[2,64,384]{2,1,0:T(8,128)(2,1)S(1)} collective-permute-done((bf16[2,64,384]{2,1,0:T(8,128)(2,1)S(1)}, bf16[2,64,384]{2,1,0:T(8,128)(2,1)S(1)}, u32[]{:S(2)}, u32[]{:S(2)}) %collective-permute-start.20) | collective-permute-done | bytes 98336 | tf_op jit(solution)/shard_map/ppermute | solution.py:256
  59.5 0.7 %select_select_fusion = bf16[2,64,384]{2,1,0:T(8,128)(2,1)} fusion(bf16[2,64,384]{2,1,0:T(8,128)(2,1)S(1)} %collective-permute-done.19, bf16[2,64,384]{2,1,0:T(8,128)(2,1)S(1)} %collective-permute-done.20, bf16[2,64,384]{2,1,0:T(8,128)(2,1)S(1)} %collective-permute-done.21, bf16[2,64,384]{2,1,0:T(8,128)(2,1)S(1)} %collective-permute-done.22, ...), kind=kLoop, calls=%fused_computation | loop fusion | flops 245760 | bytes 688133 | tf_op jit(solution)/shard_map/jit(_where)/select_n | solution.py:372
  (47 shorter events, 4.6 us)
Async XLA Ops:
  1.2 10.6 %collective-permute-start = (bf16[2,64,384]{2,1,0:T(8,128)(2,1)S(1)}, bf16[2,64,384]{2,1,0:T(8,128)(2,1)S(1)}, u32[]{:S(2)}, u32[]{:S(2)}) collective-permute-start(bf16[2,64,384]{2,1,0:T(8,128)(2,1)S(1)} %get-tuple-element.73), channel_id=1, source_target_pairs={{1,0},{3,2},{0,1},{2,3},{5,16},{7,18},{4,17},{6,19}} | collective-permute-start | bytes 294920 | tf_op jit(solution)/shard_map/ppermute | solution.py:217
  2.5 10.1 %collective-permute-start.1 = (bf16[2,64,384]{2,1,0:T(8,128)(2,1)S(1)}, bf16[2,64,384]{2,1,0:T(8,128)(2,1)S(1)}, u32[]{:S(2)}, u32[]{:S(2)}) collective-permute-start(bf16[2,64,384]{2,1,0:T(8,128)(2,1)S(1)} %get-tuple-element.74), channel_id=1, source_target_pairs={{6,16},{5,18},{10,17},{9,19},{21,0},{23,2},{20,1},{22,3}} | collective-permute-start | bytes 294920 | tf_op jit(solution)/shard_map/ppermute | solution.py:217
  3.8 9.5 %collective-permute-start.2 = (bf16[2,64,384]{2,1,0:T(8,128)(2,1)S(1)}, bf16[2,64,384]{2,1,0:T(8,128)(2,1)S(1)}, u32[]{:S(2)}, u32[]{:S(2)}) collective-permute-start(bf16[2,64,384]{2,1,0:T(8,128)(2,1)S(1)} %get-tuple-element.75), channel_id=1, source_target_pairs={{0,16},{2,18},{1,17},{3,19},{20,0},{22,2},{21,1},{23,3}} | collective-permute-start | bytes 294920 | tf_op jit(solution)/shard_map/ppermute | solution.py:217
  5.1 9.3 %collective-permute-start.3 = (bf16[2,64,384]{2,1,0:T(8,128)(2,1)S(1)}, bf16[2,64,384]{2,1,0:T(8,128)(2,1)S(1)}, u32[]{:S(2)}, u32[]{:S(2)}) collective-permute-start(bf16[2,64,384]{2,1,0:T(8,128)(2,1)S(1)} %get-tuple-element.76), channel_id=1, source_target_pairs={{14,0},{13,2},{10,1},{9,3},{30,16},{29,18},{26,17},{25,19}} | collective-permute-start | bytes 294920 | tf_op jit(solution)/shard_map/ppermute | solution.py:217
  6.4 15.4 %collective-permute-start.4 = (bf16[2,64,384]{2,1,0:T(8,128)(2,1)S(1)}, bf16[2,64,384]{2,1,0:T(8,128)(2,1)S(1)}, u32[]{:S(2)}, u32[]{:S(2)}) collective-permute-start(bf16[2,64,384]{2,1,0:T(8,128)(2,1)S(1)} %get-tuple-element.78), channel_id=1, source_target_pairs={{22,0},{21,2},{26,1},{25,3},{17,16},{19,18},{16,17},{18,19}} | collective-permute-start | bytes 294920 | tf_op jit(solution)/shard_map/ppermute | solution.py:217
  15.5 12.1 %collective-permute-start.8 = (bf16[176,384]{1,0:T(8,128)(2,1)S(1)}, bf16[176,384]{1,0:T(8,128)(2,1)S(1)}, u32[]{:S(2)}, u32[]{:S(2)}) collective-permute-start(bf16[176,384]{1,0:T(8,128)(2,1)S(1)} %get-tuple-element.93), channel_id=1, source_target_pairs={{0,4},{1,5},{2,6},{3,7},{16,20},{17,21},{18,22},{19,23}} | collective-permute-start | bytes 405512 | tf_op jit(solution)/shard_map/ppermute | solution.py:341
  19.3 9.1 %collective-permute-start.7 = (bf16[176,384]{1,0:T(8,128)(2,1)S(1)}, bf16[176,384]{1,0:T(8,128)(2,1)S(1)}, u32[]{:S(2)}, u32[]{:S(2)}) collective-permute-start(bf16[176,384]{1,0:T(8,128)(2,1)S(1)} %get-tuple-element.92), channel_id=1, source_target_pairs={{0,4},{1,5},{2,6},{3,7},{16,20},{17,21},{18,22},{19,23}} | collective-permute-start | bytes 405512 | tf_op jit(solution)/shard_map/ppermute | solution.py:341
  23.0 6.1 %collective-permute-start.6 = (bf16[176,384]{1,0:T(8,128)(2,1)S(1)}, bf16[176,384]{1,0:T(8,128)(2,1)S(1)}, u32[]{:S(2)}, u32[]{:S(2)}) collective-permute-start(bf16[176,384]{1,0:T(8,128)(2,1)S(1)} %get-tuple-element.91), channel_id=1, source_target_pairs={{0,4},{1,5},{2,6},{3,7},{16,20},{17,21},{18,22},{19,23}} | collective-permute-start | bytes 405512 | tf_op jit(solution)/shard_map/ppermute | solution.py:341
  26.3 4.1 %collective-permute-start.5 = (bf16[176,384]{1,0:T(8,128)(2,1)S(1)}, bf16[176,384]{1,0:T(8,128)(2,1)S(1)}, u32[]{:S(2)}, u32[]{:S(2)}) collective-permute-start(bf16[176,384]{1,0:T(8,128)(2,1)S(1)} %frame.19), channel_id=1, source_target_pairs={{0,4},{1,5},{2,6},{3,7},{16,20},{17,21},{18,22},{19,23}} | collective-permute-start | bytes 405512 | tf_op jit(solution)/shard_map/ppermute | solution.py:341
  27.6 3.4 %collective-permute-start.12 = (bf16[160,384]{1,0:T(8,128)(2,1)S(1)}, bf16[160,384]{1,0:T(8,128)(2,1)S(1)}, u32[]{:S(2)}, u32[]{:S(2)}) collective-permute-start(bf16[160,384]{1,0:T(8,128)(2,1)S(1)} %get-tuple-element.105), channel_id=1, source_target_pairs={{4,8},{5,9},{6,10},{7,11},{20,24},{21,25},{22,26},{23,27}} | collective-permute-start | bytes 368648 | tf_op jit(solution)/shard_map/ppermute | solution.py:341
  28.4 3.4 %collective-permute-start.11 = (bf16[160,384]{1,0:T(8,128)(2,1)S(1)}, bf16[160,384]{1,0:T(8,128)(2,1)S(1)}, u32[]{:S(2)}, u32[]{:S(2)}) collective-permute-start(bf16[160,384]{1,0:T(8,128)(2,1)S(1)} %get-tuple-element.104), channel_id=1, source_target_pairs={{4,8},{5,9},{6,10},{7,11},{20,24},{21,25},{22,26},{23,27}} | collective-permute-start | bytes 368648 | tf_op jit(solution)/shard_map/ppermute | solution.py:341
  29.3 3.2 %collective-permute-start.10 = (bf16[160,384]{1,0:T(8,128)(2,1)S(1)}, bf16[160,384]{1,0:T(8,128)(2,1)S(1)}, u32[]{:S(2)}, u32[]{:S(2)}) collective-permute-start(bf16[160,384]{1,0:T(8,128)(2,1)S(1)} %get-tuple-element.103), channel_id=1, source_target_pairs={{4,8},{5,9},{6,10},{7,11},{20,24},{21,25},{22,26},{23,27}} | collective-permute-start | bytes 368648 | tf_op jit(solution)/shard_map/ppermute | solution.py:341
  30.4 2.9 %collective-permute-start.9 = (bf16[160,384]{1,0:T(8,128)(2,1)S(1)}, bf16[160,384]{1,0:T(8,128)(2,1)S(1)}, u32[]{:S(2)}, u32[]{:S(2)}) collective-permute-start(bf16[160,384]{1,0:T(8,128)(2,1)S(1)} %frame.23), channel_id=1, source_target_pairs={{4,8},{5,9},{6,10},{7,11},{20,24},{21,25},{22,26},{23,27}} | collective-permute-start | bytes 368648 | tf_op jit(solution)/shard_map/ppermute | solution.py:341
  31.1 2.9 %collective-permute-start.16 = (bf16[144,384]{1,0:T(8,128)(2,1)S(1)}, bf16[144,384]{1,0:T(8,128)(2,1)S(1)}, u32[]{:S(2)}, u32[]{:S(2)}) collective-permute-start(bf16[144,384]{1,0:T(8,128)(2,1)S(1)} %get-tuple-element.117), channel_id=1, source_target_pairs={{8,12},{9,13},{10,14},{11,15},{24,28},{25,29},{26,30},{27,31}} | collective-permute-start | bytes 331784 | tf_op jit(solution)/shard_map/ppermute | solution.py:341
  31.8 2.2 %collective-permute-start.15 = (bf16[144,384]{1,0:T(8,128)(2,1)S(1)}, bf16[144,384]{1,0:T(8,128)(2,1)S(1)}, u32[]{:S(2)}, u32[]{:S(2)}) collective-permute-start(bf16[144,384]{1,0:T(8,128)(2,1)S(1)} %get-tuple-element.116), channel_id=1, source_target_pairs={{8,12},{9,13},{10,14},{11,15},{24,28},{25,29},{26,30},{27,31}} | collective-permute-start | bytes 331784 | tf_op jit(solution)/shard_map/ppermute | solution.py:341
  32.6 3.1 %collective-permute-start.14 = (bf16[144,384]{1,0:T(8,128)(2,1)S(1)}, bf16[144,384]{1,0:T(8,128)(2,1)S(1)}, u32[]{:S(2)}, u32[]{:S(2)}) collective-permute-start(bf16[144,384]{1,0:T(8,128)(2,1)S(1)} %get-tuple-element.115), channel_id=1, source_target_pairs={{8,12},{9,13},{10,14},{11,15},{24,28},{25,29},{26,30},{27,31}} | collective-permute-start | bytes 331784 | tf_op jit(solution)/shard_map/ppermute | solution.py:341
  33.3 3.8 %collective-permute-start.13 = (bf16[144,384]{1,0:T(8,128)(2,1)S(1)}, bf16[144,384]{1,0:T(8,128)(2,1)S(1)}, u32[]{:S(2)}, u32[]{:S(2)}) collective-permute-start(bf16[144,384]{1,0:T(8,128)(2,1)S(1)} %frame.27), channel_id=1, source_target_pairs={{8,12},{9,13},{10,14},{11,15},{24,28},{25,29},{26,30},{27,31}} | collective-permute-start | bytes 331784 | tf_op jit(solution)/shard_map/ppermute | solution.py:341
  34.1 3.0 %collective-permute-start.17 = (bf16[2,64,384]{2,1,0:T(8,128)(2,1)S(1)}, bf16[2,64,384]{2,1,0:T(8,128)(2,1)S(1)}, u32[]{:S(2)}, u32[]{:S(2)}) collective-permute-start(bf16[2,64,384]{2,1,0:T(8,128)(2,1)S(1)} %get-tuple-element.133), channel_id=1, source_target_pairs={{12,0},{14,2},{13,4},{15,6}} | collective-permute-start | bytes 294920 | tf_op jit(solution)/shard_map/ppermute | solution.py:256
  34.8 2.4 %collective-permute-start.18 = (bf16[2,64,384]{2,1,0:T(8,128)(2,1)S(1)}, bf16[2,64,384]{2,1,0:T(8,128)(2,1)S(1)}, u32[]{:S(2)}, u32[]{:S(2)}) collective-permute-start(bf16[2,64,384]{2,1,0:T(8,128)(2,1)S(1)} %get-tuple-element.134), channel_id=1, source_target_pairs={{12,1},{14,3},{13,5},{15,7}} | collective-permute-start | bytes 294920 | tf_op jit(solution)/shard_map/ppermute | solution.py:256
  35.8 3.5 %collective-permute-start.21 = (bf16[2,64,384]{2,1,0:T(8,128)(2,1)S(1)}, bf16[2,64,384]{2,1,0:T(8,128)(2,1)S(1)}, u32[]{:S(2)}, u32[]{:S(2)}) collective-permute-start(bf16[2,64,384]{2,1,0:T(8,128)(2,1)S(1)} %get-tuple-element.137), channel_id=1, source_target_pairs={{28,9},{30,11},{29,13},{31,15}} | collective-permute-start | bytes 294920 | tf_op jit(solution)/shard_map/ppermute | solution.py:256
  36.4 2.8 %collective-permute-start.22 = (bf16[2,64,384]{2,1,0:T(8,128)(2,1)S(1)}, bf16[2,64,384]{2,1,0:T(8,128)(2,1)S(1)}, u32[]{:S(2)}, u32[]{:S(2)}) collective-permute-start(bf16[2,64,384]{2,1,0:T(8,128)(2,1)S(1)} %get-tuple-element.138), channel_id=1, source_target_pairs={{28,8},{30,10},{29,12},{31,14}} | collective-permute-start | bytes 294920 | tf_op jit(solution)/shard_map/ppermute | solution.py:256
  37.2 2.0 %collective-permute-start.19 = (bf16[2,64,384]{2,1,0:T(8,128)(2,1)S(1)}, bf16[2,64,384]{2,1,0:T(8,128)(2,1)S(1)}, u32[]{:S(2)}, u32[]{:S(2)}) collective-permute-start(bf16[2,64,384]{2,1,0:T(8,128)(2,1)S(1)} %get-tuple-element.135), channel_id=1, source_target_pairs={{12,17},{14,19},{13,21},{15,23},{28,25},{30,27},{29,29},{31,31}} | collective-permute-start | bytes 294920 | tf_op jit(solution)/shard_map/ppermute | solution.py:256
  37.9 21.7 %collective-permute-start.20 = (bf16[2,64,384]{2,1,0:T(8,128)(2,1)S(1)}, bf16[2,64,384]{2,1,0:T(8,128)(2,1)S(1)}, u32[]{:S(2)}, u32[]{:S(2)}) collective-permute-start(bf16[2,64,384]{2,1,0:T(8,128)(2,1)S(1)} %get-tuple-element.136), channel_id=1, source_target_pairs={{12,16},{14,18},{13,20},{15,22},{28,24},{30,26},{29,28},{31,30}} | collective-permute-start | bytes 294920 | tf_op jit(solution)/shard_map/ppermute | solution.py:256

commit v13 on v11

--- a/solution.py
+++ b/solution.py
@@ -122,7 +122,8 @@
         wide = source[rows_at(skip, have, cols), :].astype(jnp.float32)
         meansq = jnp.sum(wide * wide, axis=-1, keepdims=True) * (1.0 / channels)
         normed = wide * lax.rsqrt(meansq + 1e-06) * gain[...]
-        ready = normed / (1.0 + jnp.exp(-normed))
+        half_normed = 0.5 * normed
+        ready = half_normed + half_normed * jnp.tanh(half_normed)
         column = lax.broadcasted_iota(jnp.int32, ready.shape, 0) & (cols - 1)
         before = jnp.where(column == 0, 0.0, pltpu.roll(ready, 1, 0))
         after = jnp.where(column == cols - 1, 0.0, pltpu.roll(ready, size - 1, 0))

time: 55.1 us -> 55 us (level)
  no operation moved by 1% of the time
where the time goes in v13:
time: 55 us; the launch traced here: 54.5 us
  starting transfers between devices  25.7 us (47%)
  waiting for transfers between devices  15.5 us (28%)
  Pallas kernels  12 us (22%)
  other arithmetic  0.67 us (1%)
  between operations  0.61 us (1%)
    ppermute x12, starting transfers between devices, local(): lax.ppermute(out, 'segment', [(s, s + 1) for s in senders_now])  13 us
    ppermute x12, waiting for transfers between devices, local(): lax.ppermute(out, 'segment', [(s, s + 1) for s in senders_now])  8.24 us
    ppermute x5, starting transfers between devices, gather(): return lax.ppermute(sources[number], MESH_AXES, routes)  8.03 us
    ppermute x6, waiting for transfers between devices, leave(): return lax.ppermute(value, MESH_AXES, routes)  7.24 us
    ppermute x6, starting transfers between devices, leave(): return lax.ppermute(value, MESH_AXES, routes)  4.63 us
    pallas_call x16, Pallas kernels, local(): pl.pallas_call(functools.partial(frame_kernel, cfg), out_shape=shapes, in...  4.26 us
    pallas_call x1, Pallas kernels, local(): pl.pallas_call(loader_kernel, out_shape=[pltpu.VMEM((TAPS * TAPS * channe...  3.42 us
    pallas_call x12, Pallas kernels, local(): pl.pallas_call(functools.partial(history_kernel, cfg), out_shape=[pltpu.V...  3.26 us
  transfers between devices with their start and end apart: 23, of which 5 were waited for; matrix products, arithmetic and copies ran while one was open for 0% of the time, Pallas kernels for 20%

profile of v13, /device:TPU:18, one launch (start us, length us, event | category | flops | bytes accessed | tf_op | source)
XLA Modules:
  0.0 54.5 jit_solution(8311315941186919696)
XLA Ops:
  0.0 1.1 %pick.1 = (bf16[2,64,384]{2,1,0:T(8,128)(2,1)S(1)}, bf16[2,64,384]{2,1,0:T(8,128)(2,1)S(1)}, bf16[2,64,384]{2,1,0:T(8,128)(2,1)S(1)}, bf16[2,64,384]{2,1,0:T(8,128)(2,1)S(1)}) custom-call(bf16[4,2,64,384]{3,2,1,0:T(8,128)(2,1)} %bitcast.4), custom_call_target="tpu_custom_call" | custom-call | tf_op jit(solution)/shard_map/pick/pallas_call | solution.py:190
  1.1 0.7 %collective-permute-start.3 = (bf16[2,64,384]{2,1,0:T(8,128)(2,1)S(1)}, bf16[2,64,384]{2,1,0:T(8,128)(2,1)S(1)}, u32[]{:S(2)}, u32[]{:S(2)}) collective-permute-start(bf16[2,64,384]{2,1,0:T(8,128)(2,1)S(1)} %get-tuple-element.71), channel_id=1, source_target_pairs={{14,0},{13,2},{0,1},{2,3},{6,16},{5,18},{8,17},{10,19}} | collective-permute-start | bytes 294920 | tf_op jit(solution)/shard_map/ppermute | solution.py:218
  1.8 0.7 %collective-permute-start.4 = (bf16[2,64,384]{2,1,0:T(8,128)(2,1)S(1)}, bf16[2,64,384]{2,1,0:T(8,128)(2,1)S(1)}, u32[]{:S(2)}, u32[]{:S(2)}) collective-permute-start(bf16[2,64,384]{2,1,0:T(8,128)(2,1)S(1)} %get-tuple-element.72), channel_id=1, source_target_pairs={{1,0},{3,2},{14,1},{13,3},{5,16},{7,18},{10,17},{9,19}} | collective-permute-start | bytes 294920 | tf_op jit(solution)/shard_map/ppermute | solution.py:218
  2.4 0.7 %collective-permute-start.2 = (bf16[2,64,384]{2,1,0:T(8,128)(2,1)S(1)}, bf16[2,64,384]{2,1,0:T(8,128)(2,1)S(1)}, u32[]{:S(2)}, u32[]{:S(2)}) collective-permute-start(bf16[2,64,384]{2,1,0:T(8,128)(2,1)S(1)} %get-tuple-element.74), channel_id=1, source_target_pairs={{0,16},{2,18},{1,17},{3,19},{20,0},{22,2},{21,1},{23,3}} | collective-permute-start | bytes 294920 | tf_op jit(solution)/shard_map/ppermute | solution.py:218
  3.1 5.4 %collective-permute-start = (bf16[2,64,384]{2,1,0:T(8,128)(2,1)S(1)}, bf16[2,64,384]{2,1,0:T(8,128)(2,1)S(1)}, u32[]{:S(2)}, u32[]{:S(2)}) collective-permute-start(bf16[2,64,384]{2,1,0:T(8,128)(2,1)S(1)} %get-tuple-element.71), channel_id=1, source_target_pairs={{22,0},{21,2},{24,1},{26,3},{30,16},{29,18},{16,17},{18,19}} | collective-permute-start | bytes 294920 | tf_op jit(solution)/shard_map/ppermute | solution.py:218
  8.5 0.7 %collective-permute-start.1 = (bf16[2,64,384]{2,1,0:T(8,128)(2,1)S(1)}, bf16[2,64,384]{2,1,0:T(8,128)(2,1)S(1)}, u32[]{:S(2)}, u32[]{:S(2)}) collective-permute-start(bf16[2,64,384]{2,1,0:T(8,128)(2,1)S(1)} %get-tuple-element.72), channel_id=1, source_target_pairs={{21,0},{23,2},{26,1},{25,3},{17,16},{19,18},{30,17},{29,19}} | collective-permute-start | bytes 294920 | tf_op jit(solution)/shard_map/ppermute | solution.py:218
  9.1 3.4 %loader.1 = (bf16[3456,384]{1,0:T(8,128)(2,1)S(1)}, bf16[3456,768]{1,0:T(8,128)(2,1)S(1)}, f32[1,384]{1,0:T(1,128)S(1)}, f32[1,384]{1,0:T(1,128)S(1)}) custom-call(bf16[3,3456,384]{2,1,0:T(8,128)(2,1)} %bitcast.3, f32[1,384]{1,0:T(1,128)} %bias.1, f32[1,384]{1,0:T(1,128)} %gain.1), custom_call_target="tpu_custom_call" | custom-call | tf_op jit(solution)/shard_map/loader/pallas_call | solution.py:235
  12.7 0.7 %collective-permute-start.8 = (bf16[176,384]{1,0:T(8,128)(2,1)S(1)}, bf16[176,384]{1,0:T(8,128)(2,1)S(1)}, u32[]{:S(2)}, u32[]{:S(2)}) collective-permute-start(bf16[176,384]{1,0:T(8,128)(2,1)S(1)} %get-tuple-element.89), channel_id=1, source_target_pairs={{0,4},{1,5},{2,6},{3,7},{16,20},{17,21},{18,22},{19,23}} | collective-permute-start | bytes 405512 | tf_op jit(solution)/shard_map/ppermute | solution.py:341
  13.4 0.7 %collective-permute-start.7 = (bf16[176,384]{1,0:T(8,128)(2,1)S(1)}, bf16[176,384]{1,0:T(8,128)(2,1)S(1)}, u32[]{:S(2)}, u32[]{:S(2)}) collective-permute-start(bf16[176,384]{1,0:T(8,128)(2,1)S(1)} %get-tuple-element.88), channel_id=1, source_target_pairs={{0,4},{1,5},{2,6},{3,7},{16,20},{17,21},{18,22},{19,23}} | collective-permute-start | bytes 405512 | tf_op jit(solution)/shard_map/ppermute | solution.py:341
  14.2 0.7 %collective-permute-start.6 = (bf16[176,384]{1,0:T(8,128)(2,1)S(1)}, bf16[176,384]{1,0:T(8,128)(2,1)S(1)}, u32[]{:S(2)}, u32[]{:S(2)}) collective-permute-start(bf16[176,384]{1,0:T(8,128)(2,1)S(1)} %get-tuple-element.87), channel_id=1, source_target_pairs={{0,4},{1,5},{2,6},{3,7},{16,20},{17,21},{18,22},{19,23}} | collective-permute-start | bytes 405512 | tf_op jit(solution)/shard_map/ppermute | solution.py:341
  14.9 0.7 %collective-permute-start.5 = (bf16[176,384]{1,0:T(8,128)(2,1)S(1)}, bf16[176,384]{1,0:T(8,128)(2,1)S(1)}, u32[]{:S(2)}, u32[]{:S(2)}) collective-permute-start(bf16[176,384]{1,0:T(8,128)(2,1)S(1)} %frame.19), channel_id=1, source_target_pairs={{0,4},{1,5},{2,6},{3,7},{16,20},{17,21},{18,22},{19,23}} | collective-permute-start | bytes 405512 | tf_op jit(solution)/shard_map/ppermute | solution.py:341
  15.6 1.3 %collective-permute-start.12 = (bf16[160,384]{1,0:T(8,128)(2,1)S(1)}, bf16[160,384]{1,0:T(8,128)(2,1)S(1)}, u32[]{:S(2)}, u32[]{:S(2)}) collective-permute-start(bf16[160,384]{1,0:T(8,128)(2,1)S(1)} %get-tuple-element.101), channel_id=1, source_target_pairs={{4,8},{5,9},{6,10},{7,11},{20,24},{21,25},{22,26},{23,27}} | collective-permute-start | bytes 368648 | tf_op jit(solution)/shard_map/ppermute | solution.py:341
  17.0 1.3 %collective-permute-start.11 = (bf16[160,384]{1,0:T(8,128)(2,1)S(1)}, bf16[160,384]{1,0:T(8,128)(2,1)S(1)}, u32[]{:S(2)}, u32[]{:S(2)}) collective-permute-start(bf16[160,384]{1,0:T(8,128)(2,1)S(1)} %get-tuple-element.100), channel_id=1, source_target_pairs={{4,8},{5,9},{6,10},{7,11},{20,24},{21,25},{22,26},{23,27}} | collective-permute-start | bytes 368648 | tf_op jit(solution)/shard_map/ppermute | solution.py:341
  18.5 1.3 %collective-permute-start.10 = (bf16[160,384]{1,0:T(8,128)(2,1)S(1)}, bf16[160,384]{1,0:T(8,128)(2,1)S(1)}, u32[]{:S(2)}, u32[]{:S(2)}) collective-permute-start(bf16[160,384]{1,0:T(8,128)(2,1)S(1)} %get-tuple-element.99), channel_id=1, source_target_pairs={{4,8},{5,9},{6,10},{7,11},{20,24},{21,25},{22,26},{23,27}} | collective-permute-start | bytes 368648 | tf_op jit(solution)/shard_map/ppermute | solution.py:341
  19.9 1.3 %collective-permute-start.9 = (bf16[160,384]{1,0:T(8,128)(2,1)S(1)}, bf16[160,384]{1,0:T(8,128)(2,1)S(1)}, u32[]{:S(2)}, u32[]{:S(2)}) collective-permute-start(bf16[160,384]{1,0:T(8,128)(2,1)S(1)} %frame.23), channel_id=1, source_target_pairs={{4,8},{5,9},{6,10},{7,11},{20,24},{21,25},{22,26},{23,27}} | collective-permute-start | bytes 368648 | tf_op jit(solution)/shard_map/ppermute | solution.py:341
  21.2 7.1 %collective-permute-done.12.refs_0_ = bf16[160,384]{1,0:T(8,128)(2,1)S(1)} collective-permute-done((bf16[160,384]{1,0:T(8,128)(2,1)S(1)}, bf16[160,384]{1,0:T(8,128)(2,1)S(1)}, u32[]{:S(2)}, u32[]{:S(2)}) %collective-permute-start.12) | collective-permute-done | bytes 122912 | tf_op jit(solution)/shard_map/ppermute | solution.py:341
  28.3 1.0 %frame.24 = (bf16[144,384]{1,0:T(8,128)(2,1)S(1)}, bf16[224,1152]{1,0:T(8,128)(2,1)S(1)}) custom-call(bf16[160,384]{1,0:T(8,128)(2,1)S(1)} %collective-permute-done.12.refs_0_, f32[176,384]{1,0:T(8,128)S(1)} %get-tuple-element.98.refs_1_.near, bf16[3456,384]{1,0:T(8,128)(2,1)S(1)} %get-tuple-element.75.refs_5_.refs_7_.refs_2_, ...), custom_call_target="tpu_custom_call" | custom-call | bytes 1024 | tf_op jit(solution)/shard_map/frame/pallas_call | solution.py:325
  29.3 1.3 %collective-permute-start.16 = (bf16[144,384]{1,0:T(8,128)(2,1)S(1)}, bf16[144,384]{1,0:T(8,128)(2,1)S(1)}, u32[]{:S(2)}, u32[]{:S(2)}) collective-permute-start(bf16[144,384]{1,0:T(8,128)(2,1)S(1)} %get-tuple-element.113), channel_id=1, source_target_pairs={{8,12},{9,13},{10,14},{11,15},{24,28},{25,29},{26,30},{27,31}} | collective-permute-start | bytes 331784 | tf_op jit(solution)/shard_map/ppermute | solution.py:341
  30.6 1.1 %history.18 = (f32[176,384]{1,0:T(8,128)S(1)}, f32[176,384]{1,0:T(8,128)S(1)}) custom-call(bf16[224,1152]{1,0:T(8,128)(2,1)S(1)} %get-tuple-element.102.spread, f32[176,384]{1,0:T(8,128)S(1)} %get-tuple-element.98.refs_1_.near, f32[176,384]{1,0:T(8,128)S(1)} %get-tuple-element.103.far, ...), custom_call_target="tpu_custom_call", output_to_operand_aliasing={{0}: (1, {}), {1}: (2, {})} | custom-call | bytes 1024 | tf_op jit(solution)/shard_map/history/pallas_call | solution.py:356
  32.1 1.0 %frame.25 = (bf16[144,384]{1,0:T(8,128)(2,1)S(1)}, bf16[224,1152]{1,0:T(8,128)(2,1)S(1)}) custom-call(bf16[160,384]{1,0:T(8,128)(2,1)S(1)} %collective-permute-done.11.refs_0_, f32[176,384]{1,0:T(8,128)S(1)} %get-tuple-element.104.refs_1_.near, bf16[3456,384]{1,0:T(8,128)(2,1)S(1)} %get-tuple-element.75.refs_5_.refs_7_.refs_2_, ...), custom_call_target="tpu_custom_call" | custom-call | bytes 1024 | tf_op jit(solution)/shard_map/frame/pallas_call | solution.py:325
  33.0 1.3 %collective-permute-start.15 = (bf16[144,384]{1,0:T(8,128)(2,1)S(1)}, bf16[144,384]{1,0:T(8,128)(2,1)S(1)}, u32[]{:S(2)}, u32[]{:S(2)}) collective-permute-start(bf16[144,384]{1,0:T(8,128)(2,1)S(1)} %get-tuple-element.112), channel_id=1, source_target_pairs={{8,12},{9,13},{10,14},{11,15},{24,28},{25,29},{26,30},{27,31}} | collective-permute-start | bytes 331784 | tf_op jit(solution)/shard_map/ppermute | solution.py:341
  34.3 1.1 %history.19 = (f32[176,384]{1,0:T(8,128)S(1)}, f32[176,384]{1,0:T(8,128)S(1)}) custom-call(bf16[224,1152]{1,0:T(8,128)(2,1)S(1)} %get-tuple-element.105.spread, f32[176,384]{1,0:T(8,128)S(1)} %get-tuple-element.104.refs_1_.near, f32[176,384]{1,0:T(8,128)S(1)} %get-tuple-element.106.far, ...), custom_call_target="tpu_custom_call", output_to_operand_aliasing={{0}: (1, {}), {1}: (2, {})} | custom-call | bytes 1024 | tf_op jit(solution)/shard_map/history/pallas_call | solution.py:356
  35.8 1.0 %frame.26 = (bf16[144,384]{1,0:T(8,128)(2,1)S(1)}, bf16[224,1152]{1,0:T(8,128)(2,1)S(1)}) custom-call(bf16[160,384]{1,0:T(8,128)(2,1)S(1)} %collective-permute-done.10.refs_0_, f32[176,384]{1,0:T(8,128)S(1)} %get-tuple-element.107.refs_1_.near, bf16[3456,384]{1,0:T(8,128)(2,1)S(1)} %get-tuple-element.75.refs_5_.refs_7_.refs_2_, ...), custom_call_target="tpu_custom_call" | custom-call | bytes 1024 | tf_op jit(solution)/shard_map/frame/pallas_call | solution.py:325
  36.8 1.3 %collective-permute-start.14 = (bf16[144,384]{1,0:T(8,128)(2,1)S(1)}, bf16[144,384]{1,0:T(8,128)(2,1)S(1)}, u32[]{:S(2)}, u32[]{:S(2)}) collective-permute-start(bf16[144,384]{1,0:T(8,128)(2,1)S(1)} %get-tuple-element.111), channel_id=1, source_target_pairs={{8,12},{9,13},{10,14},{11,15},{24,28},{25,29},{26,30},{27,31}} | collective-permute-start | bytes 331784 | tf_op jit(solution)/shard_map/ppermute | solution.py:341
  38.1 0.7 %history.20 = (f32[176,384]{1,0:T(8,128)S(1)}, f32[176,384]{1,0:T(8,128)S(1)}) custom-call(bf16[224,1152]{1,0:T(8,128)(2,1)S(1)} %get-tuple-element.108.spread, f32[176,384]{1,0:T(8,128)S(1)} %get-tuple-element.107.refs_1_.near, f32[176,384]{1,0:T(8,128)S(1)} %get-tuple-element.109.far, ...), custom_call_target="tpu_custom_call", output_to_operand_aliasing={{0}: (1, {}), {1}: (2, {})} | custom-call | bytes 1024 | tf_op jit(solution)/shard_map/history/pallas_call | solution.py:356
  39.1 1.0 %frame.27 = bf16[144,384]{1,0:T(8,128)(2,1)S(1)} custom-call(bf16[160,384]{1,0:T(8,128)(2,1)S(1)} %collective-permute-done.9.refs_0_, f32[176,384]{1,0:T(8,128)S(1)} %get-tuple-element.110.refs_1_.near, bf16[3456,384]{1,0:T(8,128)(2,1)S(1)} %get-tuple-element.75.refs_5_.refs_7_.refs_2_, f32[1,384]{1,0:T(1,128)S(1)} %get-tuple-element.76.refs_6_.refs_8_.refs_3_, ...), custom_call_target="tpu_custom_call" | custom-call | bytes 1024 | tf_op jit(solution)/shard_map/frame/pallas_call | solution.py:325
  40.1 1.3 %collective-permute-start.13 = (bf16[144,384]{1,0:T(8,128)(2,1)S(1)}, bf16[144,384]{1,0:T(8,128)(2,1)S(1)}, u32[]{:S(2)}, u32[]{:S(2)}) collective-permute-start(bf16[144,384]{1,0:T(8,128)(2,1)S(1)} %frame.27), channel_id=1, source_target_pairs={{8,12},{9,13},{10,14},{11,15},{24,28},{25,29},{26,30},{27,31}} | collective-permute-start | bytes 331784 | tf_op jit(solution)/shard_map/ppermute | solution.py:341
  41.5 0.7 %collective-permute-start.17 = (bf16[2,64,384]{2,1,0:T(8,128)(2,1)S(1)}, bf16[2,64,384]{2,1,0:T(8,128)(2,1)S(1)}, u32[]{:S(2)}, u32[]{:S(2)}) collective-permute-start(bf16[2,64,384]{2,1,0:T(8,128)(2,1)S(1)} %get-tuple-element.129), channel_id=1, source_target_pairs={{12,0},{14,2},{13,4},{15,6}} | collective-permute-start | bytes 294920 | tf_op jit(solution)/shard_map/ppermute | solution.py:257
  42.2 0.7 %collective-permute-start.18 = (bf16[2,64,384]{2,1,0:T(8,128)(2,1)S(1)}, bf16[2,64,384]{2,1,0:T(8,128)(2,1)S(1)}, u32[]{:S(2)}, u32[]{:S(2)}) collective-permute-start(bf16[2,64,384]{2,1,0:T(8,128)(2,1)S(1)} %get-tuple-element.130), channel_id=1, source_target_pairs={{12,1},{14,3},{13,5},{15,7}} | collective-permute-start | bytes 294920 | tf_op jit(solution)/shard_map/ppermute | solution.py:257
  45.2 1.3 %collective-permute-start.20 = (bf16[2,64,384]{2,1,0:T(8,128)(2,1)S(1)}, bf16[2,64,384]{2,1,0:T(8,128)(2,1)S(1)}, u32[]{:S(2)}, u32[]{:S(2)}) collective-permute-start(bf16[2,64,384]{2,1,0:T(8,128)(2,1)S(1)} %get-tuple-element.132), channel_id=1, source_target_pairs={{12,16},{14,18},{13,20},{15,22},{28,24},{30,26},{29,28},{31,30}} | collective-permute-start | bytes 294920 | tf_op jit(solution)/shard_map/ppermute | solution.py:257
  46.6 7.2 %collective-permute-done.20 = bf16[2,64,384]{2,1,0:T(8,128)(2,1)S(1)} collective-permute-done((bf16[2,64,384]{2,1,0:T(8,128)(2,1)S(1)}, bf16[2,64,384]{2,1,0:T(8,128)(2,1)S(1)}, u32[]{:S(2)}, u32[]{:S(2)}) %collective-permute-start.20) | collective-permute-done | bytes 98336 | tf_op jit(solution)/shard_map/ppermute | solution.py:257
  53.8 0.7 %select_select_fusion = bf16[2,64,384]{2,1,0:T(8,128)(2,1)} fusion(bf16[2,64,384]{2,1,0:T(8,128)(2,1)S(1)} %collective-permute-done.19, bf16[2,64,384]{2,1,0:T(8,128)(2,1)S(1)} %collective-permute-done.20, bf16[2,64,384]{2,1,0:T(8,128)(2,1)S(1)} %collective-permute-done.21, bf16[2,64,384]{2,1,0:T(8,128)(2,1)S(1)} %collective-permute-done.22, ...), kind=kLoop, calls=%fused_computation | loop fusion | flops 245760 | bytes 688133 | tf_op jit(solution)/shard_map/jit(_where)/select_n | solution.py:372
  (47 shorter events, 4.0 us)
Async XLA Ops:
  1.1 11.5 %collective-permute-start.3 = (bf16[2,64,384]{2,1,0:T(8,128)(2,1)S(1)}, bf16[2,64,384]{2,1,0:T(8,128)(2,1)S(1)}, u32[]{:S(2)}, u32[]{:S(2)}) collective-permute-start(bf16[2,64,384]{2,1,0:T(8,128)(2,1)S(1)} %get-tuple-element.71), channel_id=1, source_target_pairs={{14,0},{13,2},{0,1},{2,3},{6,16},{5,18},{8,17},{10,19}} | collective-permute-start | bytes 294920 | tf_op jit(solution)/shard_map/ppermute | solution.py:218
  1.8 10.8 %collective-permute-start.4 = (bf16[2,64,384]{2,1,0:T(8,128)(2,1)S(1)}, bf16[2,64,384]{2,1,0:T(8,128)(2,1)S(1)}, u32[]{:S(2)}, u32[]{:S(2)}) collective-permute-start(bf16[2,64,384]{2,1,0:T(8,128)(2,1)S(1)} %get-tuple-element.72), channel_id=1, source_target_pairs={{1,0},{3,2},{14,1},{13,3},{5,16},{7,18},{10,17},{9,19}} | collective-permute-start | bytes 294920 | tf_op jit(solution)/shard_map/ppermute | solution.py:218
  2.4 10.2 %collective-permute-start.2 = (bf16[2,64,384]{2,1,0:T(8,128)(2,1)S(1)}, bf16[2,64,384]{2,1,0:T(8,128)(2,1)S(1)}, u32[]{:S(2)}, u32[]{:S(2)}) collective-permute-start(bf16[2,64,384]{2,1,0:T(8,128)(2,1)S(1)} %get-tuple-element.74), channel_id=1, source_target_pairs={{0,16},{2,18},{1,17},{3,19},{20,0},{22,2},{21,1},{23,3}} | collective-permute-start | bytes 294920 | tf_op jit(solution)/shard_map/ppermute | solution.py:218
  3.1 11.0 %collective-permute-start = (bf16[2,64,384]{2,1,0:T(8,128)(2,1)S(1)}, bf16[2,64,384]{2,1,0:T(8,128)(2,1)S(1)}, u32[]{:S(2)}, u32[]{:S(2)}) collective-permute-start(bf16[2,64,384]{2,1,0:T(8,128)(2,1)S(1)} %get-tuple-element.71), channel_id=1, source_target_pairs={{22,0},{21,2},{24,1},{26,3},{30,16},{29,18},{16,17},{18,19}} | collective-permute-start | bytes 294920 | tf_op jit(solution)/shard_map/ppermute | solution.py:218
  8.5 5.7 %collective-permute-start.1 = (bf16[2,64,384]{2,1,0:T(8,128)(2,1)S(1)}, bf16[2,64,384]{2,1,0:T(8,128)(2,1)S(1)}, u32[]{:S(2)}, u32[]{:S(2)}) collective-permute-start(bf16[2,64,384]{2,1,0:T(8,128)(2,1)S(1)} %get-tuple-element.72), channel_id=1, source_target_pairs={{21,0},{23,2},{26,1},{25,3},{17,16},{19,18},{30,17},{29,19}} | collective-permute-start | bytes 294920 | tf_op jit(solution)/shard_map/ppermute | solution.py:218
  12.7 2.9 %collective-permute-start.8 = (bf16[176,384]{1,0:T(8,128)(2,1)S(1)}, bf16[176,384]{1,0:T(8,128)(2,1)S(1)}, u32[]{:S(2)}, u32[]{:S(2)}) collective-permute-start(bf16[176,384]{1,0:T(8,128)(2,1)S(1)} %get-tuple-element.89), channel_id=1, source_target_pairs={{0,4},{1,5},{2,6},{3,7},{16,20},{17,21},{18,22},{19,23}} | collective-permute-start | bytes 405512 | tf_op jit(solution)/shard_map/ppermute | solution.py:341
  13.4 3.5 %collective-permute-start.7 = (bf16[176,384]{1,0:T(8,128)(2,1)S(1)}, bf16[176,384]{1,0:T(8,128)(2,1)S(1)}, u32[]{:S(2)}, u32[]{:S(2)}) collective-permute-start(bf16[176,384]{1,0:T(8,128)(2,1)S(1)} %get-tuple-element.88), channel_id=1, source_target_pairs={{0,4},{1,5},{2,6},{3,7},{16,20},{17,21},{18,22},{19,23}} | collective-permute-start | bytes 405512 | tf_op jit(solution)/shard_map/ppermute | solution.py:341
  14.2 4.2 %collective-permute-start.6 = (bf16[176,384]{1,0:T(8,128)(2,1)S(1)}, bf16[176,384]{1,0:T(8,128)(2,1)S(1)}, u32[]{:S(2)}, u32[]{:S(2)}) collective-permute-start(bf16[176,384]{1,0:T(8,128)(2,1)S(1)} %get-tuple-element.87), channel_id=1, source_target_pairs={{0,4},{1,5},{2,6},{3,7},{16,20},{17,21},{18,22},{19,23}} | collective-permute-start | bytes 405512 | tf_op jit(solution)/shard_map/ppermute | solution.py:341
  14.9 5.0 %collective-permute-start.5 = (bf16[176,384]{1,0:T(8,128)(2,1)S(1)}, bf16[176,384]{1,0:T(8,128)(2,1)S(1)}, u32[]{:S(2)}, u32[]{:S(2)}) collective-permute-start(bf16[176,384]{1,0:T(8,128)(2,1)S(1)} %frame.19), channel_id=1, source_target_pairs={{0,4},{1,5},{2,6},{3,7},{16,20},{17,21},{18,22},{19,23}} | collective-permute-start | bytes 405512 | tf_op jit(solution)/shard_map/ppermute | solution.py:341
  15.6 12.7 %collective-permute-start.12 = (bf16[160,384]{1,0:T(8,128)(2,1)S(1)}, bf16[160,384]{1,0:T(8,128)(2,1)S(1)}, u32[]{:S(2)}, u32[]{:S(2)}) collective-permute-start(bf16[160,384]{1,0:T(8,128)(2,1)S(1)} %get-tuple-element.101), channel_id=1, source_target_pairs={{4,8},{5,9},{6,10},{7,11},{20,24},{21,25},{22,26},{23,27}} | collective-permute-start | bytes 368648 | tf_op jit(solution)/shard_map/ppermute | solution.py:341
  17.0 15.1 %collective-permute-start.11 = (bf16[160,384]{1,0:T(8,128)(2,1)S(1)}, bf16[160,384]{1,0:T(8,128)(2,1)S(1)}, u32[]{:S(2)}, u32[]{:S(2)}) collective-permute-start(bf16[160,384]{1,0:T(8,128)(2,1)S(1)} %get-tuple-element.100), channel_id=1, source_target_pairs={{4,8},{5,9},{6,10},{7,11},{20,24},{21,25},{22,26},{23,27}} | collective-permute-start | bytes 368648 | tf_op jit(solution)/shard_map/ppermute | solution.py:341
  18.5 17.3 %collective-permute-start.10 = (bf16[160,384]{1,0:T(8,128)(2,1)S(1)}, bf16[160,384]{1,0:T(8,128)(2,1)S(1)}, u32[]{:S(2)}, u32[]{:S(2)}) collective-permute-start(bf16[160,384]{1,0:T(8,128)(2,1)S(1)} %get-tuple-element.99), channel_id=1, source_target_pairs={{4,8},{5,9},{6,10},{7,11},{20,24},{21,25},{22,26},{23,27}} | collective-permute-start | bytes 368648 | tf_op jit(solution)/shard_map/ppermute | solution.py:341
  19.9 19.2 %collective-permute-start.9 = (bf16[160,384]{1,0:T(8,128)(2,1)S(1)}, bf16[160,384]{1,0:T(8,128)(2,1)S(1)}, u32[]{:S(2)}, u32[]{:S(2)}) collective-permute-start(bf16[160,384]{1,0:T(8,128)(2,1)S(1)} %frame.23), channel_id=1, source_target_pairs={{4,8},{5,9},{6,10},{7,11},{20,24},{21,25},{22,26},{23,27}} | collective-permute-start | bytes 368648 | tf_op jit(solution)/shard_map/ppermute | solution.py:341
  29.3 12.1 %collective-permute-start.16 = (bf16[144,384]{1,0:T(8,128)(2,1)S(1)}, bf16[144,384]{1,0:T(8,128)(2,1)S(1)}, u32[]{:S(2)}, u32[]{:S(2)}) collective-permute-start(bf16[144,384]{1,0:T(8,128)(2,1)S(1)} %get-tuple-element.113), channel_id=1, source_target_pairs={{8,12},{9,13},{10,14},{11,15},{24,28},{25,29},{26,30},{27,31}} | collective-permute-start | bytes 331784 | tf_op jit(solution)/shard_map/ppermute | solution.py:341
  33.0 8.4 %collective-permute-start.15 = (bf16[144,384]{1,0:T(8,128)(2,1)S(1)}, bf16[144,384]{1,0:T(8,128)(2,1)S(1)}, u32[]{:S(2)}, u32[]{:S(2)}) collective-permute-start(bf16[144,384]{1,0:T(8,128)(2,1)S(1)} %get-tuple-element.112), channel_id=1, source_target_pairs={{8,12},{9,13},{10,14},{11,15},{24,28},{25,29},{26,30},{27,31}} | collective-permute-start | bytes 331784 | tf_op jit(solution)/shard_map/ppermute | solution.py:341
  36.8 6.3 %collective-permute-start.14 = (bf16[144,384]{1,0:T(8,128)(2,1)S(1)}, bf16[144,384]{1,0:T(8,128)(2,1)S(1)}, u32[]{:S(2)}, u32[]{:S(2)}) collective-permute-start(bf16[144,384]{1,0:T(8,128)(2,1)S(1)} %get-tuple-element.111), channel_id=1, source_target_pairs={{8,12},{9,13},{10,14},{11,15},{24,28},{25,29},{26,30},{27,31}} | collective-permute-start | bytes 331784 | tf_op jit(solution)/shard_map/ppermute | solution.py:341
  40.1 4.4 %collective-permute-start.13 = (bf16[144,384]{1,0:T(8,128)(2,1)S(1)}, bf16[144,384]{1,0:T(8,128)(2,1)S(1)}, u32[]{:S(2)}, u32[]{:S(2)}) collective-permute-start(bf16[144,384]{1,0:T(8,128)(2,1)S(1)} %frame.27), channel_id=1, source_target_pairs={{8,12},{9,13},{10,14},{11,15},{24,28},{25,29},{26,30},{27,31}} | collective-permute-start | bytes 331784 | tf_op jit(solution)/shard_map/ppermute | solution.py:341
  41.5 3.0 %collective-permute-start.17 = (bf16[2,64,384]{2,1,0:T(8,128)(2,1)S(1)}, bf16[2,64,384]{2,1,0:T(8,128)(2,1)S(1)}, u32[]{:S(2)}, u32[]{:S(2)}) collective-permute-start(bf16[2,64,384]{2,1,0:T(8,128)(2,1)S(1)} %get-tuple-element.129), channel_id=1, source_target_pairs={{12,0},{14,2},{13,4},{15,6}} | collective-permute-start | bytes 294920 | tf_op jit(solution)/shard_map/ppermute | solution.py:257
  42.2 2.4 %collective-permute-start.18 = (bf16[2,64,384]{2,1,0:T(8,128)(2,1)S(1)}, bf16[2,64,384]{2,1,0:T(8,128)(2,1)S(1)}, u32[]{:S(2)}, u32[]{:S(2)}) collective-permute-start(bf16[2,64,384]{2,1,0:T(8,128)(2,1)S(1)} %get-tuple-element.130), channel_id=1, source_target_pairs={{12,1},{14,3},{13,5},{15,7}} | collective-permute-start | bytes 294920 | tf_op jit(solution)/shard_map/ppermute | solution.py:257
  43.1 3.5 %collective-permute-start.21 = (bf16[2,64,384]{2,1,0:T(8,128)(2,1)S(1)}, bf16[2,64,384]{2,1,0:T(8,128)(2,1)S(1)}, u32[]{:S(2)}, u32[]{:S(2)}) collective-permute-start(bf16[2,64,384]{2,1,0:T(8,128)(2,1)S(1)} %get-tuple-element.133), channel_id=1, source_target_pairs={{28,9},{30,11},{29,13},{31,15}} | collective-permute-start | bytes 294920 | tf_op jit(solution)/shard_map/ppermute | solution.py:257
  43.8 2.8 %collective-permute-start.22 = (bf16[2,64,384]{2,1,0:T(8,128)(2,1)S(1)}, bf16[2,64,384]{2,1,0:T(8,128)(2,1)S(1)}, u32[]{:S(2)}, u32[]{:S(2)}) collective-permute-start(bf16[2,64,384]{2,1,0:T(8,128)(2,1)S(1)} %get-tuple-element.134), channel_id=1, source_target_pairs={{28,8},{30,10},{29,12},{31,14}} | collective-permute-start | bytes 294920 | tf_op jit(solution)/shard_map/ppermute | solution.py:257
  44.6 2.0 %collective-permute-start.19 = (bf16[2,64,384]{2,1,0:T(8,128)(2,1)S(1)}, bf16[2,64,384]{2,1,0:T(8,128)(2,1)S(1)}, u32[]{:S(2)}, u32[]{:S(2)}) collective-permute-start(bf16[2,64,384]{2,1,0:T(8,128)(2,1)S(1)} %get-tuple-element.131), channel_id=1, source_target_pairs={{12,17},{14,19},{13,21},{15,23},{28,25},{30,27},{29,29},{31,31}} | collective-permute-start | bytes 294920 | tf_op jit(solution)/shard_map/ppermute | solution.py:257
  45.2 8.6 %collective-permute-start.20 = (bf16[2,64,384]{2,1,0:T(8,128)(2,1)S(1)}, bf16[2,64,384]{2,1,0:T(8,128)(2,1)S(1)}, u32[]{:S(2)}, u32[]{:S(2)}) collective-permute-start(bf16[2,64,384]{2,1,0:T(8,128)(2,1)S(1)} %get-tuple-element.132), channel_id=1, source_target_pairs={{12,16},{14,18},{13,20},{15,22},{28,24},{30,26},{29,28},{31,30}} | collective-permute-start | bytes 294920 | tf_op jit(solution)/shard_map/ppermute | solution.py:257

commit v14 on v12

--- a/solution.py
+++ b/solution.py
@@ -126,7 +126,8 @@
         wide = source[rows_at(skip, have, cols), :].astype(jnp.float32)
         meansq = jnp.sum(wide * wide, axis=-1, keepdims=True) * (1.0 / channels)
         normed = wide * lax.rsqrt(meansq + 1e-06) * gain[...]
-        ready = normed / (1.0 + jnp.exp(-normed))
+        half_normed = 0.5 * normed
+        ready = half_normed + half_normed * jnp.tanh(half_normed)
         column = lax.broadcasted_iota(jnp.int32, ready.shape, 0) & (cols - 1)
         before = jnp.where(column == 0, 0.0, pltpu.roll(ready, 1, 0))
         after = jnp.where(column == cols - 1, 0.0, pltpu.roll(ready, size - 1, 0))
@@ -221,8 +222,8 @@
     crossed = gather(2, (0, 1, 0, (0, 0)), (1, 0, 0, (1, 1)))
     nearest = gather(3, (0, 0, 2, (3, 2)), (1, 1, 2, (3, 2)))
     latest = gather(4, (1, 0, 2, (1, 2)), (1, 1, 1, (0, 0)))
-    early = [siblings, thirds, crossed, nearest, own]
-    entries = [(early, ((4, 0, 3), (2, 0, 1))), (early + [latest], ((4, 5, 3), (2, 1, 5)))]
+    early = [siblings, nearest, thirds, crossed, own]
+    entries = [(early, ((4, 0, 1), (3, 0, 2))), (early + [latest], ((4, 5, 1), (3, 2, 5)))]
     for t in range(holders, times):
         routes = [(spot(t, 0, b), spot(0, 0, b)) for b in range(bands)]
         group = [lax.ppermute(own, MESH_AXES, routes), gather(2, (t, 1, 0, (1, 1)))]

time: 60.7 us -> 59.6 us (0.982)
  waiting for transfers between devices: 23.3 us -> 22.2 us
    ppermute x6, waiting for transfers between devices: 20.3 us -> 19 us  [leave(): return lax.ppermute(value, MESH_AXES, routes)]
  transfers between devices with their start and end apart: 23 -> 23, of which waited for: 5 -> 4; matrix products, arithmetic and copies ran while one was open for 0% -> 0% of each run, Pallas kernels for 20% -> 21%
where the time goes in v14:
time: 59.6 us; the launch traced here: 59.1 us
  starting transfers between devices  22.2 us (37%)
  waiting for transfers between devices  22.2 us (37%)
  Pallas kernels  13.4 us (22%)
  other arithmetic  0.67 us (1%)
  between operations  0.6 us (1%)
    ppermute x6, waiting for transfers between devices, leave(): return lax.ppermute(value, MESH_AXES, routes)  19 us
    ppermute x12, starting transfers between devices, local(): lax.ppermute(out, 'segment', [(s, s + 1) for s in senders_now])  10.5 us
    ppermute x5, starting transfers between devices, gather(): return lax.ppermute(sources[number], MESH_AXES, routes)  7.09 us
    pallas_call x16, Pallas kernels, local(): pl.pallas_call(functools.partial(frame_kernel, cfg), out_shape=shapes, in...  5.07 us
    ppermute x6, starting transfers between devices, leave(): return lax.ppermute(value, MESH_AXES, routes)  4.63 us
    pallas_call x12, Pallas kernels, local(): pl.pallas_call(functools.partial(history_kernel, cfg), out_shape=[pltpu.V...  3.73 us
    pallas_call x1, Pallas kernels, local(): pl.pallas_call(loader_kernel, out_shape=[pltpu.VMEM((TAPS * TAPS * channe...  3.42 us
    ppermute x5, waiting for transfers between devices, gather(): return lax.ppermute(sources[number], MESH_AXES, routes)  2.65 us
  transfers between devices with their start and end apart: 23, of which 4 were waited for; matrix products, arithmetic and copies ran while one was open for 0% of the time, Pallas kernels for 21%

profile of v14, /device:TPU:2, one launch (start us, length us, event | category | flops | bytes accessed | tf_op | source)
XLA Modules:
  0.0 59.1 jit_solution(16504803545032380415)
XLA Ops:
  0.0 1.2 %pick.1 = (bf16[2,64,384]{2,1,0:T(8,128)(2,1)S(1)}, bf16[2,64,384]{2,1,0:T(8,128)(2,1)S(1)}, bf16[2,64,384]{2,1,0:T(8,128)(2,1)S(1)}, bf16[2,64,384]{2,1,0:T(8,1...) custom-call(bf16[4,2,64,384]{3,2,1,0:T(8,128)(2,1)} %bitcast.4), custom_call_target="tpu_custom_call" | custom-call | tf_op jit(solution)/shard_map/pick/pallas_call | solution.py:194
  1.2 1.3 %collective-permute-start = (bf16[2,64,384]{2,1,0:T(8,128)(2,1)S(1)}, bf16[2,64,384]{2,1,0:T(8,128)(2,1)S(1)}, u32[]{:S(2)}, u32[]{:S(2)}) collective-permute-start(bf16[2,64,384]{2,1,0:T(8,128)(2,1)S(1)} %get-tuple-element.73), channel_id=1, source_target_pairs={{1,0},{3,2},{0,1},{2,3},{5,16},{7,18},{4,17},{6,19}} | collective-permute-start | bytes 294920 | tf_op jit(solution)/shard_map/ppermute | solution.py:218
  2.5 1.3 %collective-permute-start.1 = (bf16[2,64,384]{2,1,0:T(8,128)(2,1)S(1)}, bf16[2,64,384]{2,1,0:T(8,128)(2,1)S(1)}, u32[]{:S(2)}, u32[]{:S(2)}) collective-permute-start(bf16[2,64,384]{2,1,0:T(8,128)(2,1)S(1)} %get-tuple-element.74), channel_id=1, source_target_pairs={{14,0},{13,2},{10,1},{9,3},{30,16},{29,18},{26,17},{25,19}} | collective-permute-start | bytes 294920 | tf_op jit(solution)/shard_map/ppermute | solution.py:218
  3.8 1.3 %collective-permute-start.2 = (bf16[2,64,384]{2,1,0:T(8,128)(2,1)S(1)}, bf16[2,64,384]{2,1,0:T(8,128)(2,1)S(1)}, u32[]{:S(2)}, u32[]{:S(2)}) collective-permute-start(bf16[2,64,384]{2,1,0:T(8,128)(2,1)S(1)} %get-tuple-element.75), channel_id=1, source_target_pairs={{6,16},{5,18},{10,17},{9,19},{21,0},{23,2},{20,1},{22,3}} | collective-permute-start | bytes 294920 | tf_op jit(solution)/shard_map/ppermute | solution.py:218
  5.1 1.3 %collective-permute-start.3 = (bf16[2,64,384]{2,1,0:T(8,128)(2,1)S(1)}, bf16[2,64,384]{2,1,0:T(8,128)(2,1)S(1)}, u32[]{:S(2)}, u32[]{:S(2)}) collective-permute-start(bf16[2,64,384]{2,1,0:T(8,128)(2,1)S(1)} %get-tuple-element.76), channel_id=1, source_target_pairs={{0,16},{2,18},{1,17},{3,19},{20,0},{22,2},{21,1},{23,3}} | collective-permute-start | bytes 294920 | tf_op jit(solution)/shard_map/ppermute | solution.py:218
  6.4 1.9 %collective-permute-start.4 = (bf16[2,64,384]{2,1,0:T(8,128)(2,1)S(1)}, bf16[2,64,384]{2,1,0:T(8,128)(2,1)S(1)}, u32[]{:S(2)}, u32[]{:S(2)}) collective-permute-start(bf16[2,64,384]{2,1,0:T(8,128)(2,1)S(1)} %get-tuple-element.78), channel_id=1, source_target_pairs={{22,0},{21,2},{26,1},{25,3},{17,16},{19,18},{16,17},{18,19}} | collective-permute-start | bytes 294920 | tf_op jit(solution)/shard_map/ppermute | solution.py:218
  8.3 3.4 %loader.1 = (bf16[3456,384]{1,0:T(8,128)(2,1)S(1)}, bf16[3456,768]{1,0:T(8,128)(2,1)S(1)}, f32[1,384]{1,0:T(1,128)S(1)}, f32[1,384]{1,0:T(1,128)S(1)}) custom-call(bf16[3,3456,384]{2,1,0:T(8,128)(2,1)} %bitcast.3, f32[1,384]{1,0:T(1,128)} %bias.1, f32[1,384]{1,0:T(1,128)} %gain.1), custom_call_target="tpu_custom_call" | custom-call | tf_op jit(solution)/shard_map/loader/pallas_call | solution.py:235
  12.1 2.3 %collective-permute-done.2.refs_2_ = bf16[2,64,384]{2,1,0:T(8,128)(2,1)S(1)} collective-permute-done((bf16[2,64,384]{2,1,0:T(8,128)(2,1)S(1)}, bf16[2,64,384]{2,1,0:T(8,128)(2,1)S(1)}, u32[]{:S(2)}, u32[]{:S(2)}) %collective-permute-start.2) | collective-permute-done | bytes 98336 | tf_op jit(solution)/shard_map/ppermute | solution.py:218
  14.4 1.2 %frame.16 = (bf16[176,384]{1,0:T(8,128)(2,1)S(1)}, bf16[224,1152]{1,0:T(8,128)(2,1)S(1)}) custom-call(bf16[2,64,384]{2,1,0:T(8,128)(2,1)S(1)} %collective-permute-done.refs_0_, bf16[2,64,384]{2,1,0:T(8,128)(2,1)S(1)} %collective-permute-done.1.refs_1_, bf16[2,64,384]{2,1,0:T(8,128)(2,1)S(1)} %collective-permute-done.2.refs_2_, ...), custom_call_target="tpu_custom_call" | custom-call | bytes 1024 | tf_op jit(solution)/shard_map/frame/pallas_call | solution.py:326
  15.6 1.3 %collective-permute-start.8 = (bf16[176,384]{1,0:T(8,128)(2,1)S(1)}, bf16[176,384]{1,0:T(8,128)(2,1)S(1)}, u32[]{:S(2)}, u32[]{:S(2)}) collective-permute-start(bf16[176,384]{1,0:T(8,128)(2,1)S(1)} %get-tuple-element.93), channel_id=1, source_target_pairs={{0,4},{1,5},{2,6},{3,7},{16,20},{17,21},{18,22},{19,23}} | collective-permute-start | bytes 405512 | tf_op jit(solution)/shard_map/ppermute | solution.py:342
  16.9 1.2 %history.12 = (f32[176,384]{1,0:T(8,128)S(1)}, f32[176,384]{1,0:T(8,128)S(1)}) custom-call(bf16[224,1152]{1,0:T(8,128)(2,1)S(1)} %get-tuple-element.82.spread, f32[176,384]{1,0:T(8,128)S(1)} %broadcast_1_refs_5__near_far.2.refs_5_.near, f32[176,384]{1,0:T(8,128)S(1)} %broadcast_1_refs_5__near_far.2.clone.far, ...), custom_call_target="tpu_custom_call", output_to_operand_aliasing={{0}: (1, {}), {1}: (2, {})} | custom-call | bytes 1024 | tf_op jit(solution)/shard_map/history/pallas_call | solution.py:357
  18.2 1.2 %frame.17 = (bf16[176,384]{1,0:T(8,128)(2,1)S(1)}, bf16[224,1152]{1,0:T(8,128)(2,1)S(1)}) custom-call(bf16[2,64,384]{2,1,0:T(8,128)(2,1)S(1)} %collective-permute-done.refs_0_, bf16[2,64,384]{2,1,0:T(8,128)(2,1)S(1)} %collective-permute-done.1.refs_1_, bf16[2,64,384]{2,1,0:T(8,128)(2,1)S(1)} %collective-permute-done.2.refs_2_, ...), custom_call_target="tpu_custom_call" | custom-call | bytes 1024 | tf_op jit(solution)/shard_map/frame/pallas_call | solution.py:326
  19.4 1.3 %collective-permute-start.7 = (bf16[176,384]{1,0:T(8,128)(2,1)S(1)}, bf16[176,384]{1,0:T(8,128)(2,1)S(1)}, u32[]{:S(2)}, u32[]{:S(2)}) collective-permute-start(bf16[176,384]{1,0:T(8,128)(2,1)S(1)} %get-tuple-element.92), channel_id=1, source_target_pairs={{0,4},{1,5},{2,6},{3,7},{16,20},{17,21},{18,22},{19,23}} | collective-permute-start | bytes 405512 | tf_op jit(solution)/shard_map/ppermute | solution.py:342
  20.7 1.2 %history.13 = (f32[176,384]{1,0:T(8,128)S(1)}, f32[176,384]{1,0:T(8,128)S(1)}) custom-call(bf16[224,1152]{1,0:T(8,128)(2,1)S(1)} %get-tuple-element.85.spread, f32[176,384]{1,0:T(8,128)S(1)} %get-tuple-element.84.refs_5_.near, f32[176,384]{1,0:T(8,128)S(1)} %get-tuple-element.86.far, ...), custom_call_target="tpu_custom_call", output_to_operand_aliasing={{0}: (1, {}), {1}: (2, {})} | custom-call | bytes 1024 | tf_op jit(solution)/shard_map/history/pallas_call | solution.py:357
  21.9 1.2 %frame.18 = (bf16[176,384]{1,0:T(8,128)(2,1)S(1)}, bf16[224,1152]{1,0:T(8,128)(2,1)S(1)}) custom-call(bf16[2,64,384]{2,1,0:T(8,128)(2,1)S(1)} %collective-permute-done.refs_0_, bf16[2,64,384]{2,1,0:T(8,128)(2,1)S(1)} %collective-permute-done.1.refs_1_, bf16[2,64,384]{2,1,0:T(8,128)(2,1)S(1)} %collective-permute-done.2.refs_2_, ...), custom_call_target="tpu_custom_call" | custom-call | bytes 1024 | tf_op jit(solution)/shard_map/frame/pallas_call | solution.py:326
  23.1 1.3 %collective-permute-start.6 = (bf16[176,384]{1,0:T(8,128)(2,1)S(1)}, bf16[176,384]{1,0:T(8,128)(2,1)S(1)}, u32[]{:S(2)}, u32[]{:S(2)}) collective-permute-start(bf16[176,384]{1,0:T(8,128)(2,1)S(1)} %get-tuple-element.91), channel_id=1, source_target_pairs={{0,4},{1,5},{2,6},{3,7},{16,20},{17,21},{18,22},{19,23}} | collective-permute-start | bytes 405512 | tf_op jit(solution)/shard_map/ppermute | solution.py:342
  24.4 0.8 %history.14 = (f32[176,384]{1,0:T(8,128)S(1)}, f32[176,384]{1,0:T(8,128)S(1)}) custom-call(bf16[224,1152]{1,0:T(8,128)(2,1)S(1)} %get-tuple-element.88.spread, f32[176,384]{1,0:T(8,128)S(1)} %get-tuple-element.87.refs_6_.near, f32[176,384]{1,0:T(8,128)S(1)} %get-tuple-element.89.far, ...), custom_call_target="tpu_custom_call", output_to_operand_aliasing={{0}: (1, {}), {1}: (2, {})} | custom-call | bytes 1024 | tf_op jit(solution)/shard_map/history/pallas_call | solution.py:357
  25.3 1.1 %frame.19 = bf16[176,384]{1,0:T(8,128)(2,1)S(1)} custom-call(bf16[2,64,384]{2,1,0:T(8,128)(2,1)S(1)} %collective-permute-done.refs_0_, bf16[2,64,384]{2,1,0:T(8,128)(2,1)S(1)} %collective-permute-done.1.refs_1_, bf16[2,64,384]{2,1,0:T(8,128)(2,1)S(1)} %collective-permute-done.2.refs_2_, bf16[2,64,384]{2,1,0:T(8,128)(2,1)S(1)} %collective-permute-done.3.refs_3_, ...), custom_call_target="tpu_custom_call" | custom-call | bytes 1024 | tf_op jit(solution)/shard_map/frame/pallas_call | solution.py:326
  26.4 1.3 %collective-permute-start.5 = (bf16[176,384]{1,0:T(8,128)(2,1)S(1)}, bf16[176,384]{1,0:T(8,128)(2,1)S(1)}, u32[]{:S(2)}, u32[]{:S(2)}) collective-permute-start(bf16[176,384]{1,0:T(8,128)(2,1)S(1)} %frame.19), channel_id=1, source_target_pairs={{0,4},{1,5},{2,6},{3,7},{16,20},{17,21},{18,22},{19,23}} | collective-permute-start | bytes 405512 | tf_op jit(solution)/shard_map/ppermute | solution.py:342
  27.8 0.7 %collective-permute-start.12 = (bf16[160,384]{1,0:T(8,128)(2,1)S(1)}, bf16[160,384]{1,0:T(8,128)(2,1)S(1)}, u32[]{:S(2)}, u32[]{:S(2)}) collective-permute-start(bf16[160,384]{1,0:T(8,128)(2,1)S(1)} %get-tuple-element.105), channel_id=1, source_target_pairs={{4,8},{5,9},{6,10},{7,11},{20,24},{21,25},{22,26},{23,27}} | collective-permute-start | bytes 368648 | tf_op jit(solution)/shard_map/ppermute | solution.py:342
  28.5 0.7 %collective-permute-start.11 = (bf16[160,384]{1,0:T(8,128)(2,1)S(1)}, bf16[160,384]{1,0:T(8,128)(2,1)S(1)}, u32[]{:S(2)}, u32[]{:S(2)}) collective-permute-start(bf16[160,384]{1,0:T(8,128)(2,1)S(1)} %get-tuple-element.104), channel_id=1, source_target_pairs={{4,8},{5,9},{6,10},{7,11},{20,24},{21,25},{22,26},{23,27}} | collective-permute-start | bytes 368648 | tf_op jit(solution)/shard_map/ppermute | solution.py:342
  29.4 0.7 %collective-permute-start.10 = (bf16[160,384]{1,0:T(8,128)(2,1)S(1)}, bf16[160,384]{1,0:T(8,128)(2,1)S(1)}, u32[]{:S(2)}, u32[]{:S(2)}) collective-permute-start(bf16[160,384]{1,0:T(8,128)(2,1)S(1)} %get-tuple-element.103), channel_id=1, source_target_pairs={{4,8},{5,9},{6,10},{7,11},{20,24},{21,25},{22,26},{23,27}} | collective-permute-start | bytes 368648 | tf_op jit(solution)/shard_map/ppermute | solution.py:342
  31.3 0.7 %collective-permute-start.16 = (bf16[144,384]{1,0:T(8,128)(2,1)S(1)}, bf16[144,384]{1,0:T(8,128)(2,1)S(1)}, u32[]{:S(2)}, u32[]{:S(2)}) collective-permute-start(bf16[144,384]{1,0:T(8,128)(2,1)S(1)} %get-tuple-element.117), channel_id=1, source_target_pairs={{8,12},{9,13},{10,14},{11,15},{24,28},{25,29},{26,30},{27,31}} | collective-permute-start | bytes 331784 | tf_op jit(solution)/shard_map/ppermute | solution.py:342
  32.1 0.7 %collective-permute-start.15 = (bf16[144,384]{1,0:T(8,128)(2,1)S(1)}, bf16[144,384]{1,0:T(8,128)(2,1)S(1)}, u32[]{:S(2)}, u32[]{:S(2)}) collective-permute-start(bf16[144,384]{1,0:T(8,128)(2,1)S(1)} %get-tuple-element.116), channel_id=1, source_target_pairs={{8,12},{9,13},{10,14},{11,15},{24,28},{25,29},{26,30},{27,31}} | collective-permute-start | bytes 331784 | tf_op jit(solution)/shard_map/ppermute | solution.py:342
  32.8 0.7 %collective-permute-start.14 = (bf16[144,384]{1,0:T(8,128)(2,1)S(1)}, bf16[144,384]{1,0:T(8,128)(2,1)S(1)}, u32[]{:S(2)}, u32[]{:S(2)}) collective-permute-start(bf16[144,384]{1,0:T(8,128)(2,1)S(1)} %get-tuple-element.115), channel_id=1, source_target_pairs={{8,12},{9,13},{10,14},{11,15},{24,28},{25,29},{26,30},{27,31}} | collective-permute-start | bytes 331784 | tf_op jit(solution)/shard_map/ppermute | solution.py:342
  33.6 0.7 %collective-permute-start.13 = (bf16[144,384]{1,0:T(8,128)(2,1)S(1)}, bf16[144,384]{1,0:T(8,128)(2,1)S(1)}, u32[]{:S(2)}, u32[]{:S(2)}) collective-permute-start(bf16[144,384]{1,0:T(8,128)(2,1)S(1)} %frame.27), channel_id=1, source_target_pairs={{8,12},{9,13},{10,14},{11,15},{24,28},{25,29},{26,30},{27,31}} | collective-permute-start | bytes 331784 | tf_op jit(solution)/shard_map/ppermute | solution.py:342
  34.4 0.7 %collective-permute-start.17 = (bf16[2,64,384]{2,1,0:T(8,128)(2,1)S(1)}, bf16[2,64,384]{2,1,0:T(8,128)(2,1)S(1)}, u32[]{:S(2)}, u32[]{:S(2)}) collective-permute-start(bf16[2,64,384]{2,1,0:T(8,128)(2,1)S(1)} %get-tuple-element.133), channel_id=1, source_target_pairs={{12,0},{14,2},{13,4},{15,6}} | collective-permute-start | bytes 294920 | tf_op jit(solution)/shard_map/ppermute | solution.py:257
  35.0 0.7 %collective-permute-start.18 = (bf16[2,64,384]{2,1,0:T(8,128)(2,1)S(1)}, bf16[2,64,384]{2,1,0:T(8,128)(2,1)S(1)}, u32[]{:S(2)}, u32[]{:S(2)}) collective-permute-start(bf16[2,64,384]{2,1,0:T(8,128)(2,1)S(1)} %get-tuple-element.134), channel_id=1, source_target_pairs={{12,1},{14,3},{13,5},{15,7}} | collective-permute-start | bytes 294920 | tf_op jit(solution)/shard_map/ppermute | solution.py:257
  36.0 0.7 %collective-permute-start.21 = (bf16[2,64,384]{2,1,0:T(8,128)(2,1)S(1)}, bf16[2,64,384]{2,1,0:T(8,128)(2,1)S(1)}, u32[]{:S(2)}, u32[]{:S(2)}) collective-permute-start(bf16[2,64,384]{2,1,0:T(8,128)(2,1)S(1)} %get-tuple-element.137), channel_id=1, source_target_pairs={{28,9},{30,11},{29,13},{31,15}} | collective-permute-start | bytes 294920 | tf_op jit(solution)/shard_map/ppermute | solution.py:257
  38.1 1.3 %collective-permute-start.20 = (bf16[2,64,384]{2,1,0:T(8,128)(2,1)S(1)}, bf16[2,64,384]{2,1,0:T(8,128)(2,1)S(1)}, u32[]{:S(2)}, u32[]{:S(2)}) collective-permute-start(bf16[2,64,384]{2,1,0:T(8,128)(2,1)S(1)} %get-tuple-element.136), channel_id=1, source_target_pairs={{12,16},{14,18},{13,20},{15,22},{28,24},{30,26},{29,28},{31,30}} | collective-permute-start | bytes 294920 | tf_op jit(solution)/shard_map/ppermute | solution.py:257
  39.5 19.0 %collective-permute-done.20 = bf16[2,64,384]{2,1,0:T(8,128)(2,1)S(1)} collective-permute-done((bf16[2,64,384]{2,1,0:T(8,128)(2,1)S(1)}, bf16[2,64,384]{2,1,0:T(8,128)(2,1)S(1)}, u32[]{:S(2)}, u32[]{:S(2)}) %collective-permute-start.20) | collective-permute-done | bytes 98336 | tf_op jit(solution)/shard_map/ppermute | solution.py:257
  58.5 0.7 %select_select_fusion = bf16[2,64,384]{2,1,0:T(8,128)(2,1)} fusion(bf16[2,64,384]{2,1,0:T(8,128)(2,1)S(1)} %collective-permute-done.19, bf16[2,64,384]{2,1,0:T(8,128)(2,1)S(1)} %collective-permute-done.20, bf16[2,64,384]{2,1,0:T(8,128)(2,1)S(1)} %collective-permute-done.21, bf16[2,64,384]{2,1,0:T(8,128)(2,1)S(1)} %collective-permute-done.22, ...), kind=kLoop, calls=%fused_computation | loop fusion | flops 245760 | bytes 688133 | tf_op jit(solution)/shard_map/jit(_where)/select_n | solution.py:373
  (47 shorter events, 3.7 us)
Async XLA Ops:
  1.2 10.6 %collective-permute-start = (bf16[2,64,384]{2,1,0:T(8,128)(2,1)S(1)}, bf16[2,64,384]{2,1,0:T(8,128)(2,1)S(1)}, u32[]{:S(2)}, u32[]{:S(2)}) collective-permute-start(bf16[2,64,384]{2,1,0:T(8,128)(2,1)S(1)} %get-tuple-element.73), channel_id=1, source_target_pairs={{1,0},{3,2},{0,1},{2,3},{5,16},{7,18},{4,17},{6,19}} | collective-permute-start | bytes 294920 | tf_op jit(solution)/shard_map/ppermute | solution.py:218
  2.5 9.6 %collective-permute-start.1 = (bf16[2,64,384]{2,1,0:T(8,128)(2,1)S(1)}, bf16[2,64,384]{2,1,0:T(8,128)(2,1)S(1)}, u32[]{:S(2)}, u32[]{:S(2)}) collective-permute-start(bf16[2,64,384]{2,1,0:T(8,128)(2,1)S(1)} %get-tuple-element.74), channel_id=1, source_target_pairs={{14,0},{13,2},{10,1},{9,3},{30,16},{29,18},{26,17},{25,19}} | collective-permute-start | bytes 294920 | tf_op jit(solution)/shard_map/ppermute | solution.py:218
  3.8 10.6 %collective-permute-start.2 = (bf16[2,64,384]{2,1,0:T(8,128)(2,1)S(1)}, bf16[2,64,384]{2,1,0:T(8,128)(2,1)S(1)}, u32[]{:S(2)}, u32[]{:S(2)}) collective-permute-start(bf16[2,64,384]{2,1,0:T(8,128)(2,1)S(1)} %get-tuple-element.75), channel_id=1, source_target_pairs={{6,16},{5,18},{10,17},{9,19},{21,0},{23,2},{20,1},{22,3}} | collective-permute-start | bytes 294920 | tf_op jit(solution)/shard_map/ppermute | solution.py:218
  5.1 9.3 %collective-permute-start.3 = (bf16[2,64,384]{2,1,0:T(8,128)(2,1)S(1)}, bf16[2,64,384]{2,1,0:T(8,128)(2,1)S(1)}, u32[]{:S(2)}, u32[]{:S(2)}) collective-permute-start(bf16[2,64,384]{2,1,0:T(8,128)(2,1)S(1)} %get-tuple-element.76), channel_id=1, source_target_pairs={{0,16},{2,18},{1,17},{3,19},{20,0},{22,2},{21,1},{23,3}} | collective-permute-start | bytes 294920 | tf_op jit(solution)/shard_map/ppermute | solution.py:218
  6.4 15.5 %collective-permute-start.4 = (bf16[2,64,384]{2,1,0:T(8,128)(2,1)S(1)}, bf16[2,64,384]{2,1,0:T(8,128)(2,1)S(1)}, u32[]{:S(2)}, u32[]{:S(2)}) collective-permute-start(bf16[2,64,384]{2,1,0:T(8,128)(2,1)S(1)} %get-tuple-element.78), channel_id=1, source_target_pairs={{22,0},{21,2},{26,1},{25,3},{17,16},{19,18},{16,17},{18,19}} | collective-permute-start | bytes 294920 | tf_op jit(solution)/shard_map/ppermute | solution.py:218
  15.6 12.1 %collective-permute-start.8 = (bf16[176,384]{1,0:T(8,128)(2,1)S(1)}, bf16[176,384]{1,0:T(8,128)(2,1)S(1)}, u32[]{:S(2)}, u32[]{:S(2)}) collective-permute-start(bf16[176,384]{1,0:T(8,128)(2,1)S(1)} %get-tuple-element.93), channel_id=1, source_target_pairs={{0,4},{1,5},{2,6},{3,7},{16,20},{17,21},{18,22},{19,23}} | collective-permute-start | bytes 405512 | tf_op jit(solution)/shard_map/ppermute | solution.py:342
  19.4 9.1 %collective-permute-start.7 = (bf16[176,384]{1,0:T(8,128)(2,1)S(1)}, bf16[176,384]{1,0:T(8,128)(2,1)S(1)}, u32[]{:S(2)}, u32[]{:S(2)}) collective-permute-start(bf16[176,384]{1,0:T(8,128)(2,1)S(1)} %get-tuple-element.92), channel_id=1, source_target_pairs={{0,4},{1,5},{2,6},{3,7},{16,20},{17,21},{18,22},{19,23}} | collective-permute-start | bytes 405512 | tf_op jit(solution)/shard_map/ppermute | solution.py:342
  23.1 6.1 %collective-permute-start.6 = (bf16[176,384]{1,0:T(8,128)(2,1)S(1)}, bf16[176,384]{1,0:T(8,128)(2,1)S(1)}, u32[]{:S(2)}, u32[]{:S(2)}) collective-permute-start(bf16[176,384]{1,0:T(8,128)(2,1)S(1)} %get-tuple-element.91), channel_id=1, source_target_pairs={{0,4},{1,5},{2,6},{3,7},{16,20},{17,21},{18,22},{19,23}} | collective-permute-start | bytes 405512 | tf_op jit(solution)/shard_map/ppermute | solution.py:342
  26.4 4.2 %collective-permute-start.5 = (bf16[176,384]{1,0:T(8,128)(2,1)S(1)}, bf16[176,384]{1,0:T(8,128)(2,1)S(1)}, u32[]{:S(2)}, u32[]{:S(2)}) collective-permute-start(bf16[176,384]{1,0:T(8,128)(2,1)S(1)} %frame.19), channel_id=1, source_target_pairs={{0,4},{1,5},{2,6},{3,7},{16,20},{17,21},{18,22},{19,23}} | collective-permute-start | bytes 405512 | tf_op jit(solution)/shard_map/ppermute | solution.py:342
  27.8 3.5 %collective-permute-start.12 = (bf16[160,384]{1,0:T(8,128)(2,1)S(1)}, bf16[160,384]{1,0:T(8,128)(2,1)S(1)}, u32[]{:S(2)}, u32[]{:S(2)}) collective-permute-start(bf16[160,384]{1,0:T(8,128)(2,1)S(1)} %get-tuple-element.105), channel_id=1, source_target_pairs={{4,8},{5,9},{6,10},{7,11},{20,24},{21,25},{22,26},{23,27}} | collective-permute-start | bytes 368648 | tf_op jit(solution)/shard_map/ppermute | solution.py:342
  28.5 3.5 %collective-permute-start.11 = (bf16[160,384]{1,0:T(8,128)(2,1)S(1)}, bf16[160,384]{1,0:T(8,128)(2,1)S(1)}, u32[]{:S(2)}, u32[]{:S(2)}) collective-permute-start(bf16[160,384]{1,0:T(8,128)(2,1)S(1)} %get-tuple-element.104), channel_id=1, source_target_pairs={{4,8},{5,9},{6,10},{7,11},{20,24},{21,25},{22,26},{23,27}} | collective-permute-start | bytes 368648 | tf_op jit(solution)/shard_map/ppermute | solution.py:342
  29.4 3.4 %collective-permute-start.10 = (bf16[160,384]{1,0:T(8,128)(2,1)S(1)}, bf16[160,384]{1,0:T(8,128)(2,1)S(1)}, u32[]{:S(2)}, u32[]{:S(2)}) collective-permute-start(bf16[160,384]{1,0:T(8,128)(2,1)S(1)} %get-tuple-element.103), channel_id=1, source_target_pairs={{4,8},{5,9},{6,10},{7,11},{20,24},{21,25},{22,26},{23,27}} | collective-permute-start | bytes 368648 | tf_op jit(solution)/shard_map/ppermute | solution.py:342
  30.6 2.9 %collective-permute-start.9 = (bf16[160,384]{1,0:T(8,128)(2,1)S(1)}, bf16[160,384]{1,0:T(8,128)(2,1)S(1)}, u32[]{:S(2)}, u32[]{:S(2)}) collective-permute-start(bf16[160,384]{1,0:T(8,128)(2,1)S(1)} %frame.23), channel_id=1, source_target_pairs={{4,8},{5,9},{6,10},{7,11},{20,24},{21,25},{22,26},{23,27}} | collective-permute-start | bytes 368648 | tf_op jit(solution)/shard_map/ppermute | solution.py:342
  31.3 2.9 %collective-permute-start.16 = (bf16[144,384]{1,0:T(8,128)(2,1)S(1)}, bf16[144,384]{1,0:T(8,128)(2,1)S(1)}, u32[]{:S(2)}, u32[]{:S(2)}) collective-permute-start(bf16[144,384]{1,0:T(8,128)(2,1)S(1)} %get-tuple-element.117), channel_id=1, source_target_pairs={{8,12},{9,13},{10,14},{11,15},{24,28},{25,29},{26,30},{27,31}} | collective-permute-start | bytes 331784 | tf_op jit(solution)/shard_map/ppermute | solution.py:342
  32.1 2.2 %collective-permute-start.15 = (bf16[144,384]{1,0:T(8,128)(2,1)S(1)}, bf16[144,384]{1,0:T(8,128)(2,1)S(1)}, u32[]{:S(2)}, u32[]{:S(2)}) collective-permute-start(bf16[144,384]{1,0:T(8,128)(2,1)S(1)} %get-tuple-element.116), channel_id=1, source_target_pairs={{8,12},{9,13},{10,14},{11,15},{24,28},{25,29},{26,30},{27,31}} | collective-permute-start | bytes 331784 | tf_op jit(solution)/shard_map/ppermute | solution.py:342
  32.8 3.1 %collective-permute-start.14 = (bf16[144,384]{1,0:T(8,128)(2,1)S(1)}, bf16[144,384]{1,0:T(8,128)(2,1)S(1)}, u32[]{:S(2)}, u32[]{:S(2)}) collective-permute-start(bf16[144,384]{1,0:T(8,128)(2,1)S(1)} %get-tuple-element.115), channel_id=1, source_target_pairs={{8,12},{9,13},{10,14},{11,15},{24,28},{25,29},{26,30},{27,31}} | collective-permute-start | bytes 331784 | tf_op jit(solution)/shard_map/ppermute | solution.py:342
  33.6 3.8 %collective-permute-start.13 = (bf16[144,384]{1,0:T(8,128)(2,1)S(1)}, bf16[144,384]{1,0:T(8,128)(2,1)S(1)}, u32[]{:S(2)}, u32[]{:S(2)}) collective-permute-start(bf16[144,384]{1,0:T(8,128)(2,1)S(1)} %frame.27), channel_id=1, source_target_pairs={{8,12},{9,13},{10,14},{11,15},{24,28},{25,29},{26,30},{27,31}} | collective-permute-start | bytes 331784 | tf_op jit(solution)/shard_map/ppermute | solution.py:342
  34.4 3.0 %collective-permute-start.17 = (bf16[2,64,384]{2,1,0:T(8,128)(2,1)S(1)}, bf16[2,64,384]{2,1,0:T(8,128)(2,1)S(1)}, u32[]{:S(2)}, u32[]{:S(2)}) collective-permute-start(bf16[2,64,384]{2,1,0:T(8,128)(2,1)S(1)} %get-tuple-element.133), channel_id=1, source_target_pairs={{12,0},{14,2},{13,4},{15,6}} | collective-permute-start | bytes 294920 | tf_op jit(solution)/shard_map/ppermute | solution.py:257
  35.0 2.4 %collective-permute-start.18 = (bf16[2,64,384]{2,1,0:T(8,128)(2,1)S(1)}, bf16[2,64,384]{2,1,0:T(8,128)(2,1)S(1)}, u32[]{:S(2)}, u32[]{:S(2)}) collective-permute-start(bf16[2,64,384]{2,1,0:T(8,128)(2,1)S(1)} %get-tuple-element.134), channel_id=1, source_target_pairs={{12,1},{14,3},{13,5},{15,7}} | collective-permute-start | bytes 294920 | tf_op jit(solution)/shard_map/ppermute | solution.py:257
  36.0 3.5 %collective-permute-start.21 = (bf16[2,64,384]{2,1,0:T(8,128)(2,1)S(1)}, bf16[2,64,384]{2,1,0:T(8,128)(2,1)S(1)}, u32[]{:S(2)}, u32[]{:S(2)}) collective-permute-start(bf16[2,64,384]{2,1,0:T(8,128)(2,1)S(1)} %get-tuple-element.137), channel_id=1, source_target_pairs={{28,9},{30,11},{29,13},{31,15}} | collective-permute-start | bytes 294920 | tf_op jit(solution)/shard_map/ppermute | solution.py:257
  36.7 2.8 %collective-permute-start.22 = (bf16[2,64,384]{2,1,0:T(8,128)(2,1)S(1)}, bf16[2,64,384]{2,1,0:T(8,128)(2,1)S(1)}, u32[]{:S(2)}, u32[]{:S(2)}) collective-permute-start(bf16[2,64,384]{2,1,0:T(8,128)(2,1)S(1)} %get-tuple-element.138), channel_id=1, source_target_pairs={{28,8},{30,10},{29,12},{31,14}} | collective-permute-start | bytes 294920 | tf_op jit(solution)/shard_map/ppermute | solution.py:257
  37.4 2.0 %collective-permute-start.19 = (bf16[2,64,384]{2,1,0:T(8,128)(2,1)S(1)}, bf16[2,64,384]{2,1,0:T(8,128)(2,1)S(1)}, u32[]{:S(2)}, u32[]{:S(2)}) collective-permute-start(bf16[2,64,384]{2,1,0:T(8,128)(2,1)S(1)} %get-tuple-element.135), channel_id=1, source_target_pairs={{12,17},{14,19},{13,21},{15,23},{28,25},{30,27},{29,29},{31,31}} | collective-permute-start | bytes 294920 | tf_op jit(solution)/shard_map/ppermute | solution.py:257
  38.1 20.4 %collective-permute-start.20 = (bf16[2,64,384]{2,1,0:T(8,128)(2,1)S(1)}, bf16[2,64,384]{2,1,0:T(8,128)(2,1)S(1)}, u32[]{:S(2)}, u32[]{:S(2)}) collective-permute-start(bf16[2,64,384]{2,1,0:T(8,128)(2,1)S(1)} %get-tuple-element.136), channel_id=1, source_target_pairs={{12,16},{14,18},{13,20},{15,22},{28,24},{30,26},{29,28},{31,30}} | collective-permute-start | bytes 294920 | tf_op jit(solution)/shard_map/ppermute | solution.py:257

commit v15 on v13

--- a/solution.py
+++ b/solution.py
@@ -10,6 +10,7 @@
 HALVES = 2
 DEPTH = 4
 TAPS = 3
+SUBLANES = 8
 VMEM_LIMIT = 24 << 20
 MESH_AXES = ("tm", "segment", "band")
 
@@ -93,7 +94,7 @@
     tails = [refs.pop(0) for _ in range(cfg["finals"])]
     refs = refs[cfg["keeps"] :]
     doubles = [refs.pop(0) for _ in range(cfg["doubles"])]
-    entry = refs.pop(0)
+    entry, shifting = refs
     cols, window, segments = cfg["cols"], cfg["window"], cfg["segments"]
     channels = entry.shape[-1]
     half = lax.axis_index("band") // cfg["per_half"]
@@ -125,8 +126,9 @@
         half_normed = 0.5 * normed
         ready = half_normed + half_normed * jnp.tanh(half_normed)
         column = lax.broadcasted_iota(jnp.int32, ready.shape, 0) & (cols - 1)
-        before = jnp.where(column == 0, 0.0, pltpu.roll(ready, 1, 0))
-        after = jnp.where(column == cols - 1, 0.0, pltpu.roll(ready, size - 1, 0))
+        shifting[pl.ds(SUBLANES, size), :] = ready
+        before = jnp.where(column == 0, 0.0, shifting[pl.ds(SUBLANES - 1, size), :])
+        after = jnp.where(column == cols - 1, 0.0, shifting[pl.ds(SUBLANES + 1, size), :])
         edge = jnp.zeros((cols, TAPS * channels), jnp.bfloat16)
         spread[pl.ds(0, cols), :] = edge
         spread[pl.ds(size + cols, cols), :] = edge
@@ -327,7 +329,11 @@
                 out_shape=shapes,
                 in_specs=[whole()] * len(operands),
                 out_specs=[whole()] * len(shapes),
-                scratch_shapes=[pltpu.VMEM((window * cols, channels), jnp.bfloat16)] + ([] if cfg["later"] else [wide]),
+                scratch_shapes=[
+                    pltpu.VMEM((window * cols, channels), jnp.bfloat16),
+                    pltpu.VMEM((window * cols + 2 * SUBLANES, channels), jnp.float32),
+                ]
+                + ([] if cfg["later"] else [wide]),
                 input_output_aliases=aliases,
                 compiler_params=pltpu.CompilerParams(vmem_limit_bytes=VMEM_LIMIT),
                 cost_estimate=pl.CostEstimate(flops=0, transcendentals=0, bytes_accessed=1 << 10),

time: 55 us -> 54.9 us (level)
  no operation moved by 1% of the time
where the time goes in v15:
time: 54.9 us; the launch traced here: 54.4 us
  starting transfers between devices  25.7 us (47%)
  waiting for transfers between devices  15.4 us (28%)
  Pallas kernels  11.9 us (22%)
  other arithmetic  0.67 us (1%)
  between operations  0.61 us (1%)
    ppermute x12, starting transfers between devices, local(): lax.ppermute(out, 'segment', [(s, s + 1) for s in senders_now])  13 us
    ppermute x12, waiting for transfers between devices, local(): lax.ppermute(out, 'segment', [(s, s + 1) for s in senders_now])  8.15 us
    ppermute x5, starting transfers between devices, gather(): return lax.ppermute(sources[number], MESH_AXES, routes)  8.03 us
    ppermute x6, waiting for transfers between devices, leave(): return lax.ppermute(value, MESH_AXES, routes)  7.27 us
    ppermute x6, starting transfers between devices, leave(): return lax.ppermute(value, MESH_AXES, routes)  4.63 us
    pallas_call x16, Pallas kernels, local(): pl.pallas_call(functools.partial(frame_kernel, cfg), out_shape=shapes, in...  4.17 us
    pallas_call x1, Pallas kernels, local(): pl.pallas_call(loader_kernel, out_shape=[pltpu.VMEM((TAPS * TAPS * channe...  3.42 us
    pallas_call x12, Pallas kernels, local(): pl.pallas_call(functools.partial(history_kernel, cfg), out_shape=[pltpu.V...  3.27 us
  transfers between devices with their start and end apart: 23, of which 5 were waited for; matrix products, arithmetic and copies ran while one was open for 0% of the time, Pallas kernels for 20%

profile of v15, /device:TPU:18, one launch (start us, length us, event | category | flops | bytes accessed | tf_op | source)
XLA Modules:
  0.0 54.4 jit_solution(11668374573742620117)
XLA Ops:
  0.0 1.1 %pick.1 = (bf16[2,64,384]{2,1,0:T(8,128)(2,1)S(1)}, bf16[2,64,384]{2,1,0:T(8,128)(2,1)S(1)}, bf16[2,64,384]{2,1,0:T(8,128)(2,1)S(1)}, bf16[2,64,384]{2,1,0:T(8,128)(2,1)S(1)}) custom-call(bf16[4,2,64,384]{3,2,1,0:T(8,128)(2,1)} %bitcast.4), custom_call_target="tpu_custom_call" | custom-call | tf_op jit(solution)/shard_map/pick/pallas_call | solution.py:192
  1.1 0.7 %collective-permute-start.3 = (bf16[2,64,384]{2,1,0:T(8,128)(2,1)S(1)}, bf16[2,64,384]{2,1,0:T(8,128)(2,1)S(1)}, u32[]{:S(2)}, u32[]{:S(2)}) collective-permute-start(bf16[2,64,384]{2,1,0:T(8,128)(2,1)S(1)} %get-tuple-element.71), channel_id=1, source_target_pairs={{14,0},{13,2},{0,1},{2,3},{6,16},{5,18},{8,17},{10,19}} | collective-permute-start | bytes 294920 | tf_op jit(solution)/shard_map/ppermute | solution.py:220
  1.8 0.7 %collective-permute-start.4 = (bf16[2,64,384]{2,1,0:T(8,128)(2,1)S(1)}, bf16[2,64,384]{2,1,0:T(8,128)(2,1)S(1)}, u32[]{:S(2)}, u32[]{:S(2)}) collective-permute-start(bf16[2,64,384]{2,1,0:T(8,128)(2,1)S(1)} %get-tuple-element.72), channel_id=1, source_target_pairs={{1,0},{3,2},{14,1},{13,3},{5,16},{7,18},{10,17},{9,19}} | collective-permute-start | bytes 294920 | tf_op jit(solution)/shard_map/ppermute | solution.py:220
  2.4 0.7 %collective-permute-start.2 = (bf16[2,64,384]{2,1,0:T(8,128)(2,1)S(1)}, bf16[2,64,384]{2,1,0:T(8,128)(2,1)S(1)}, u32[]{:S(2)}, u32[]{:S(2)}) collective-permute-start(bf16[2,64,384]{2,1,0:T(8,128)(2,1)S(1)} %get-tuple-element.74), channel_id=1, source_target_pairs={{0,16},{2,18},{1,17},{3,19},{20,0},{22,2},{21,1},{23,3}} | collective-permute-start | bytes 294920 | tf_op jit(solution)/shard_map/ppermute | solution.py:220
  3.1 5.4 %collective-permute-start = (bf16[2,64,384]{2,1,0:T(8,128)(2,1)S(1)}, bf16[2,64,384]{2,1,0:T(8,128)(2,1)S(1)}, u32[]{:S(2)}, u32[]{:S(2)}) collective-permute-start(bf16[2,64,384]{2,1,0:T(8,128)(2,1)S(1)} %get-tuple-element.71), channel_id=1, source_target_pairs={{22,0},{21,2},{24,1},{26,3},{30,16},{29,18},{16,17},{18,19}} | collective-permute-start | bytes 294920 | tf_op jit(solution)/shard_map/ppermute | solution.py:220
  8.5 0.7 %collective-permute-start.1 = (bf16[2,64,384]{2,1,0:T(8,128)(2,1)S(1)}, bf16[2,64,384]{2,1,0:T(8,128)(2,1)S(1)}, u32[]{:S(2)}, u32[]{:S(2)}) collective-permute-start(bf16[2,64,384]{2,1,0:T(8,128)(2,1)S(1)} %get-tuple-element.72), channel_id=1, source_target_pairs={{21,0},{23,2},{26,1},{25,3},{17,16},{19,18},{30,17},{29,19}} | collective-permute-start | bytes 294920 | tf_op jit(solution)/shard_map/ppermute | solution.py:220
  9.1 3.4 %loader.1 = (bf16[3456,384]{1,0:T(8,128)(2,1)S(1)}, bf16[3456,768]{1,0:T(8,128)(2,1)S(1)}, f32[1,384]{1,0:T(1,128)S(1)}, f32[1,384]{1,0:T(1,128)S(1)}) custom-call(bf16[3,3456,384]{2,1,0:T(8,128)(2,1)} %bitcast.3, f32[1,384]{1,0:T(1,128)} %bias.1, f32[1,384]{1,0:T(1,128)} %gain.1), custom_call_target="tpu_custom_call" | custom-call | tf_op jit(solution)/shard_map/loader/pallas_call | solution.py:237
  12.7 0.7 %collective-permute-start.8 = (bf16[176,384]{1,0:T(8,128)(2,1)S(1)}, bf16[176,384]{1,0:T(8,128)(2,1)S(1)}, u32[]{:S(2)}, u32[]{:S(2)}) collective-permute-start(bf16[176,384]{1,0:T(8,128)(2,1)S(1)} %get-tuple-element.89), channel_id=1, source_target_pairs={{0,4},{1,5},{2,6},{3,7},{16,20},{17,21},{18,22},{19,23}} | collective-permute-start | bytes 405512 | tf_op jit(solution)/shard_map/ppermute | solution.py:347
  13.4 0.7 %collective-permute-start.7 = (bf16[176,384]{1,0:T(8,128)(2,1)S(1)}, bf16[176,384]{1,0:T(8,128)(2,1)S(1)}, u32[]{:S(2)}, u32[]{:S(2)}) collective-permute-start(bf16[176,384]{1,0:T(8,128)(2,1)S(1)} %get-tuple-element.88), channel_id=1, source_target_pairs={{0,4},{1,5},{2,6},{3,7},{16,20},{17,21},{18,22},{19,23}} | collective-permute-start | bytes 405512 | tf_op jit(solution)/shard_map/ppermute | solution.py:347
  14.2 0.7 %collective-permute-start.6 = (bf16[176,384]{1,0:T(8,128)(2,1)S(1)}, bf16[176,384]{1,0:T(8,128)(2,1)S(1)}, u32[]{:S(2)}, u32[]{:S(2)}) collective-permute-start(bf16[176,384]{1,0:T(8,128)(2,1)S(1)} %get-tuple-element.87), channel_id=1, source_target_pairs={{0,4},{1,5},{2,6},{3,7},{16,20},{17,21},{18,22},{19,23}} | collective-permute-start | bytes 405512 | tf_op jit(solution)/shard_map/ppermute | solution.py:347
  14.9 0.7 %collective-permute-start.5 = (bf16[176,384]{1,0:T(8,128)(2,1)S(1)}, bf16[176,384]{1,0:T(8,128)(2,1)S(1)}, u32[]{:S(2)}, u32[]{:S(2)}) collective-permute-start(bf16[176,384]{1,0:T(8,128)(2,1)S(1)} %frame.19), channel_id=1, source_target_pairs={{0,4},{1,5},{2,6},{3,7},{16,20},{17,21},{18,22},{19,23}} | collective-permute-start | bytes 405512 | tf_op jit(solution)/shard_map/ppermute | solution.py:347
  15.6 1.3 %collective-permute-start.12 = (bf16[160,384]{1,0:T(8,128)(2,1)S(1)}, bf16[160,384]{1,0:T(8,128)(2,1)S(1)}, u32[]{:S(2)}, u32[]{:S(2)}) collective-permute-start(bf16[160,384]{1,0:T(8,128)(2,1)S(1)} %get-tuple-element.101), channel_id=1, source_target_pairs={{4,8},{5,9},{6,10},{7,11},{20,24},{21,25},{22,26},{23,27}} | collective-permute-start | bytes 368648 | tf_op jit(solution)/shard_map/ppermute | solution.py:347
  17.0 1.3 %collective-permute-start.11 = (bf16[160,384]{1,0:T(8,128)(2,1)S(1)}, bf16[160,384]{1,0:T(8,128)(2,1)S(1)}, u32[]{:S(2)}, u32[]{:S(2)}) collective-permute-start(bf16[160,384]{1,0:T(8,128)(2,1)S(1)} %get-tuple-element.100), channel_id=1, source_target_pairs={{4,8},{5,9},{6,10},{7,11},{20,24},{21,25},{22,26},{23,27}} | collective-permute-start | bytes 368648 | tf_op jit(solution)/shard_map/ppermute | solution.py:347
  18.5 1.3 %collective-permute-start.10 = (bf16[160,384]{1,0:T(8,128)(2,1)S(1)}, bf16[160,384]{1,0:T(8,128)(2,1)S(1)}, u32[]{:S(2)}, u32[]{:S(2)}) collective-permute-start(bf16[160,384]{1,0:T(8,128)(2,1)S(1)} %get-tuple-element.99), channel_id=1, source_target_pairs={{4,8},{5,9},{6,10},{7,11},{20,24},{21,25},{22,26},{23,27}} | collective-permute-start | bytes 368648 | tf_op jit(solution)/shard_map/ppermute | solution.py:347
  19.9 1.3 %collective-permute-start.9 = (bf16[160,384]{1,0:T(8,128)(2,1)S(1)}, bf16[160,384]{1,0:T(8,128)(2,1)S(1)}, u32[]{:S(2)}, u32[]{:S(2)}) collective-permute-start(bf16[160,384]{1,0:T(8,128)(2,1)S(1)} %frame.23), channel_id=1, source_target_pairs={{4,8},{5,9},{6,10},{7,11},{20,24},{21,25},{22,26},{23,27}} | collective-permute-start | bytes 368648 | tf_op jit(solution)/shard_map/ppermute | solution.py:347
  21.2 7.1 %collective-permute-done.12.refs_0_ = bf16[160,384]{1,0:T(8,128)(2,1)S(1)} collective-permute-done((bf16[160,384]{1,0:T(8,128)(2,1)S(1)}, bf16[160,384]{1,0:T(8,128)(2,1)S(1)}, u32[]{:S(2)}, u32[]{:S(2)}) %collective-permute-start.12) | collective-permute-done | bytes 122912 | tf_op jit(solution)/shard_map/ppermute | solution.py:347
  28.3 0.9 %frame.24 = (bf16[144,384]{1,0:T(8,128)(2,1)S(1)}, bf16[224,1152]{1,0:T(8,128)(2,1)S(1)}) custom-call(bf16[160,384]{1,0:T(8,128)(2,1)S(1)} %collective-permute-done.12.refs_0_, f32[176,384]{1,0:T(8,128)S(1)} %get-tuple-element.98.refs_1_.near, bf16[3456,384]{1,0:T(8,128)(2,1)S(1)} %get-tuple-element.75.refs_5_.refs_7_.refs_2_, ...), custom_call_target="tpu_custom_call" | custom-call | bytes 1024 | tf_op jit(solution)/shard_map/frame/pallas_call | solution.py:327
  29.2 1.3 %collective-permute-start.16 = (bf16[144,384]{1,0:T(8,128)(2,1)S(1)}, bf16[144,384]{1,0:T(8,128)(2,1)S(1)}, u32[]{:S(2)}, u32[]{:S(2)}) collective-permute-start(bf16[144,384]{1,0:T(8,128)(2,1)S(1)} %get-tuple-element.113), channel_id=1, source_target_pairs={{8,12},{9,13},{10,14},{11,15},{24,28},{25,29},{26,30},{27,31}} | collective-permute-start | bytes 331784 | tf_op jit(solution)/shard_map/ppermute | solution.py:347
  30.5 1.1 %history.18 = (f32[176,384]{1,0:T(8,128)S(1)}, f32[176,384]{1,0:T(8,128)S(1)}) custom-call(bf16[224,1152]{1,0:T(8,128)(2,1)S(1)} %get-tuple-element.102.spread, f32[176,384]{1,0:T(8,128)S(1)} %get-tuple-element.98.refs_1_.near, f32[176,384]{1,0:T(8,128)S(1)} %get-tuple-element.103.far, ...), custom_call_target="tpu_custom_call", output_to_operand_aliasing={{0}: (1, {}), {1}: (2, {})} | custom-call | bytes 1024 | tf_op jit(solution)/shard_map/history/pallas_call | solution.py:362
  32.0 0.9 %frame.25 = (bf16[144,384]{1,0:T(8,128)(2,1)S(1)}, bf16[224,1152]{1,0:T(8,128)(2,1)S(1)}) custom-call(bf16[160,384]{1,0:T(8,128)(2,1)S(1)} %collective-permute-done.11.refs_0_, f32[176,384]{1,0:T(8,128)S(1)} %get-tuple-element.104.refs_1_.near, bf16[3456,384]{1,0:T(8,128)(2,1)S(1)} %get-tuple-element.75.refs_5_.refs_7_.refs_2_, ...), custom_call_target="tpu_custom_call" | custom-call | bytes 1024 | tf_op jit(solution)/shard_map/frame/pallas_call | solution.py:327
  32.9 1.3 %collective-permute-start.15 = (bf16[144,384]{1,0:T(8,128)(2,1)S(1)}, bf16[144,384]{1,0:T(8,128)(2,1)S(1)}, u32[]{:S(2)}, u32[]{:S(2)}) collective-permute-start(bf16[144,384]{1,0:T(8,128)(2,1)S(1)} %get-tuple-element.112), channel_id=1, source_target_pairs={{8,12},{9,13},{10,14},{11,15},{24,28},{25,29},{26,30},{27,31}} | collective-permute-start | bytes 331784 | tf_op jit(solution)/shard_map/ppermute | solution.py:347
  34.2 1.1 %history.19 = (f32[176,384]{1,0:T(8,128)S(1)}, f32[176,384]{1,0:T(8,128)S(1)}) custom-call(bf16[224,1152]{1,0:T(8,128)(2,1)S(1)} %get-tuple-element.105.spread, f32[176,384]{1,0:T(8,128)S(1)} %get-tuple-element.104.refs_1_.near, f32[176,384]{1,0:T(8,128)S(1)} %get-tuple-element.106.far, ...), custom_call_target="tpu_custom_call", output_to_operand_aliasing={{0}: (1, {}), {1}: (2, {})} | custom-call | bytes 1024 | tf_op jit(solution)/shard_map/history/pallas_call | solution.py:362
  35.7 0.9 %frame.26 = (bf16[144,384]{1,0:T(8,128)(2,1)S(1)}, bf16[224,1152]{1,0:T(8,128)(2,1)S(1)}) custom-call(bf16[160,384]{1,0:T(8,128)(2,1)S(1)} %collective-permute-done.10.refs_0_, f32[176,384]{1,0:T(8,128)S(1)} %get-tuple-element.107.refs_1_.near, bf16[3456,384]{1,0:T(8,128)(2,1)S(1)} %get-tuple-element.75.refs_5_.refs_7_.refs_2_, ...), custom_call_target="tpu_custom_call" | custom-call | bytes 1024 | tf_op jit(solution)/shard_map/frame/pallas_call | solution.py:327
  36.6 1.3 %collective-permute-start.14 = (bf16[144,384]{1,0:T(8,128)(2,1)S(1)}, bf16[144,384]{1,0:T(8,128)(2,1)S(1)}, u32[]{:S(2)}, u32[]{:S(2)}) collective-permute-start(bf16[144,384]{1,0:T(8,128)(2,1)S(1)} %get-tuple-element.111), channel_id=1, source_target_pairs={{8,12},{9,13},{10,14},{11,15},{24,28},{25,29},{26,30},{27,31}} | collective-permute-start | bytes 331784 | tf_op jit(solution)/shard_map/ppermute | solution.py:347
  37.9 0.7 %history.20 = (f32[176,384]{1,0:T(8,128)S(1)}, f32[176,384]{1,0:T(8,128)S(1)}) custom-call(bf16[224,1152]{1,0:T(8,128)(2,1)S(1)} %get-tuple-element.108.spread, f32[176,384]{1,0:T(8,128)S(1)} %get-tuple-element.107.refs_1_.near, f32[176,384]{1,0:T(8,128)S(1)} %get-tuple-element.109.far, ...), custom_call_target="tpu_custom_call", output_to_operand_aliasing={{0}: (1, {}), {1}: (2, {})} | custom-call | bytes 1024 | tf_op jit(solution)/shard_map/history/pallas_call | solution.py:362
  39.0 0.9 %frame.27 = bf16[144,384]{1,0:T(8,128)(2,1)S(1)} custom-call(bf16[160,384]{1,0:T(8,128)(2,1)S(1)} %collective-permute-done.9.refs_0_, f32[176,384]{1,0:T(8,128)S(1)} %get-tuple-element.110.refs_1_.near, bf16[3456,384]{1,0:T(8,128)(2,1)S(1)} %get-tuple-element.75.refs_5_.refs_7_.refs_2_, f32[1,384]{1,0:T(1,128)S(1)} %get-tuple-element.76.refs_6_.refs_8_.refs_3_, ...), custom_call_target="tpu_custom_call" | custom-call | bytes 1024 | tf_op jit(solution)/shard_map/frame/pallas_call | solution.py:327
  39.9 1.3 %collective-permute-start.13 = (bf16[144,384]{1,0:T(8,128)(2,1)S(1)}, bf16[144,384]{1,0:T(8,128)(2,1)S(1)}, u32[]{:S(2)}, u32[]{:S(2)}) collective-permute-start(bf16[144,384]{1,0:T(8,128)(2,1)S(1)} %frame.27), channel_id=1, source_target_pairs={{8,12},{9,13},{10,14},{11,15},{24,28},{25,29},{26,30},{27,31}} | collective-permute-start | bytes 331784 | tf_op jit(solution)/shard_map/ppermute | solution.py:347
  41.3 0.7 %collective-permute-start.17 = (bf16[2,64,384]{2,1,0:T(8,128)(2,1)S(1)}, bf16[2,64,384]{2,1,0:T(8,128)(2,1)S(1)}, u32[]{:S(2)}, u32[]{:S(2)}) collective-permute-start(bf16[2,64,384]{2,1,0:T(8,128)(2,1)S(1)} %get-tuple-element.129), channel_id=1, source_target_pairs={{12,0},{14,2},{13,4},{15,6}} | collective-permute-start | bytes 294920 | tf_op jit(solution)/shard_map/ppermute | solution.py:259
  42.0 0.7 %collective-permute-start.18 = (bf16[2,64,384]{2,1,0:T(8,128)(2,1)S(1)}, bf16[2,64,384]{2,1,0:T(8,128)(2,1)S(1)}, u32[]{:S(2)}, u32[]{:S(2)}) collective-permute-start(bf16[2,64,384]{2,1,0:T(8,128)(2,1)S(1)} %get-tuple-element.130), channel_id=1, source_target_pairs={{12,1},{14,3},{13,5},{15,7}} | collective-permute-start | bytes 294920 | tf_op jit(solution)/shard_map/ppermute | solution.py:259
  45.1 1.3 %collective-permute-start.20 = (bf16[2,64,384]{2,1,0:T(8,128)(2,1)S(1)}, bf16[2,64,384]{2,1,0:T(8,128)(2,1)S(1)}, u32[]{:S(2)}, u32[]{:S(2)}) collective-permute-start(bf16[2,64,384]{2,1,0:T(8,128)(2,1)S(1)} %get-tuple-element.132), channel_id=1, source_target_pairs={{12,16},{14,18},{13,20},{15,22},{28,24},{30,26},{29,28},{31,30}} | collective-permute-start | bytes 294920 | tf_op jit(solution)/shard_map/ppermute | solution.py:259
  46.4 7.3 %collective-permute-done.20 = bf16[2,64,384]{2,1,0:T(8,128)(2,1)S(1)} collective-permute-done((bf16[2,64,384]{2,1,0:T(8,128)(2,1)S(1)}, bf16[2,64,384]{2,1,0:T(8,128)(2,1)S(1)}, u32[]{:S(2)}, u32[]{:S(2)}) %collective-permute-start.20) | collective-permute-done | bytes 98336 | tf_op jit(solution)/shard_map/ppermute | solution.py:259
  53.7 0.7 %select_select_fusion = bf16[2,64,384]{2,1,0:T(8,128)(2,1)} fusion(bf16[2,64,384]{2,1,0:T(8,128)(2,1)S(1)} %collective-permute-done.19, bf16[2,64,384]{2,1,0:T(8,128)(2,1)S(1)} %collective-permute-done.20, bf16[2,64,384]{2,1,0:T(8,128)(2,1)S(1)} %collective-permute-done.21, bf16[2,64,384]{2,1,0:T(8,128)(2,1)S(1)} %collective-permute-done.22, ...), kind=kLoop, calls=%fused_computation | loop fusion | flops 245760 | bytes 688133 | tf_op jit(solution)/shard_map/jit(_where)/select_n | solution.py:378
  (47 shorter events, 4.0 us)
Async XLA Ops:
  1.1 11.5 %collective-permute-start.3 = (bf16[2,64,384]{2,1,0:T(8,128)(2,1)S(1)}, bf16[2,64,384]{2,1,0:T(8,128)(2,1)S(1)}, u32[]{:S(2)}, u32[]{:S(2)}) collective-permute-start(bf16[2,64,384]{2,1,0:T(8,128)(2,1)S(1)} %get-tuple-element.71), channel_id=1, source_target_pairs={{14,0},{13,2},{0,1},{2,3},{6,16},{5,18},{8,17},{10,19}} | collective-permute-start | bytes 294920 | tf_op jit(solution)/shard_map/ppermute | solution.py:220
  1.8 10.8 %collective-permute-start.4 = (bf16[2,64,384]{2,1,0:T(8,128)(2,1)S(1)}, bf16[2,64,384]{2,1,0:T(8,128)(2,1)S(1)}, u32[]{:S(2)}, u32[]{:S(2)}) collective-permute-start(bf16[2,64,384]{2,1,0:T(8,128)(2,1)S(1)} %get-tuple-element.72), channel_id=1, source_target_pairs={{1,0},{3,2},{14,1},{13,3},{5,16},{7,18},{10,17},{9,19}} | collective-permute-start | bytes 294920 | tf_op jit(solution)/shard_map/ppermute | solution.py:220
  2.4 10.2 %collective-permute-start.2 = (bf16[2,64,384]{2,1,0:T(8,128)(2,1)S(1)}, bf16[2,64,384]{2,1,0:T(8,128)(2,1)S(1)}, u32[]{:S(2)}, u32[]{:S(2)}) collective-permute-start(bf16[2,64,384]{2,1,0:T(8,128)(2,1)S(1)} %get-tuple-element.74), channel_id=1, source_target_pairs={{0,16},{2,18},{1,17},{3,19},{20,0},{22,2},{21,1},{23,3}} | collective-permute-start | bytes 294920 | tf_op jit(solution)/shard_map/ppermute | solution.py:220
  3.1 11.0 %collective-permute-start = (bf16[2,64,384]{2,1,0:T(8,128)(2,1)S(1)}, bf16[2,64,384]{2,1,0:T(8,128)(2,1)S(1)}, u32[]{:S(2)}, u32[]{:S(2)}) collective-permute-start(bf16[2,64,384]{2,1,0:T(8,128)(2,1)S(1)} %get-tuple-element.71), channel_id=1, source_target_pairs={{22,0},{21,2},{24,1},{26,3},{30,16},{29,18},{16,17},{18,19}} | collective-permute-start | bytes 294920 | tf_op jit(solution)/shard_map/ppermute | solution.py:220
  8.5 5.7 %collective-permute-start.1 = (bf16[2,64,384]{2,1,0:T(8,128)(2,1)S(1)}, bf16[2,64,384]{2,1,0:T(8,128)(2,1)S(1)}, u32[]{:S(2)}, u32[]{:S(2)}) collective-permute-start(bf16[2,64,384]{2,1,0:T(8,128)(2,1)S(1)} %get-tuple-element.72), channel_id=1, source_target_pairs={{21,0},{23,2},{26,1},{25,3},{17,16},{19,18},{30,17},{29,19}} | collective-permute-start | bytes 294920 | tf_op jit(solution)/shard_map/ppermute | solution.py:220
  12.7 2.9 %collective-permute-start.8 = (bf16[176,384]{1,0:T(8,128)(2,1)S(1)}, bf16[176,384]{1,0:T(8,128)(2,1)S(1)}, u32[]{:S(2)}, u32[]{:S(2)}) collective-permute-start(bf16[176,384]{1,0:T(8,128)(2,1)S(1)} %get-tuple-element.89), channel_id=1, source_target_pairs={{0,4},{1,5},{2,6},{3,7},{16,20},{17,21},{18,22},{19,23}} | collective-permute-start | bytes 405512 | tf_op jit(solution)/shard_map/ppermute | solution.py:347
  13.4 3.5 %collective-permute-start.7 = (bf16[176,384]{1,0:T(8,128)(2,1)S(1)}, bf16[176,384]{1,0:T(8,128)(2,1)S(1)}, u32[]{:S(2)}, u32[]{:S(2)}) collective-permute-start(bf16[176,384]{1,0:T(8,128)(2,1)S(1)} %get-tuple-element.88), channel_id=1, source_target_pairs={{0,4},{1,5},{2,6},{3,7},{16,20},{17,21},{18,22},{19,23}} | collective-permute-start | bytes 405512 | tf_op jit(solution)/shard_map/ppermute | solution.py:347
  14.2 4.2 %collective-permute-start.6 = (bf16[176,384]{1,0:T(8,128)(2,1)S(1)}, bf16[176,384]{1,0:T(8,128)(2,1)S(1)}, u32[]{:S(2)}, u32[]{:S(2)}) collective-permute-start(bf16[176,384]{1,0:T(8,128)(2,1)S(1)} %get-tuple-element.87), channel_id=1, source_target_pairs={{0,4},{1,5},{2,6},{3,7},{16,20},{17,21},{18,22},{19,23}} | collective-permute-start | bytes 405512 | tf_op jit(solution)/shard_map/ppermute | solution.py:347
  14.9 5.0 %collective-permute-start.5 = (bf16[176,384]{1,0:T(8,128)(2,1)S(1)}, bf16[176,384]{1,0:T(8,128)(2,1)S(1)}, u32[]{:S(2)}, u32[]{:S(2)}) collective-permute-start(bf16[176,384]{1,0:T(8,128)(2,1)S(1)} %frame.19), channel_id=1, source_target_pairs={{0,4},{1,5},{2,6},{3,7},{16,20},{17,21},{18,22},{19,23}} | collective-permute-start | bytes 405512 | tf_op jit(solution)/shard_map/ppermute | solution.py:347
  15.6 12.6 %collective-permute-start.12 = (bf16[160,384]{1,0:T(8,128)(2,1)S(1)}, bf16[160,384]{1,0:T(8,128)(2,1)S(1)}, u32[]{:S(2)}, u32[]{:S(2)}) collective-permute-start(bf16[160,384]{1,0:T(8,128)(2,1)S(1)} %get-tuple-element.101), channel_id=1, source_target_pairs={{4,8},{5,9},{6,10},{7,11},{20,24},{21,25},{22,26},{23,27}} | collective-permute-start | bytes 368648 | tf_op jit(solution)/shard_map/ppermute | solution.py:347
  17.0 15.0 %collective-permute-start.11 = (bf16[160,384]{1,0:T(8,128)(2,1)S(1)}, bf16[160,384]{1,0:T(8,128)(2,1)S(1)}, u32[]{:S(2)}, u32[]{:S(2)}) collective-permute-start(bf16[160,384]{1,0:T(8,128)(2,1)S(1)} %get-tuple-element.100), channel_id=1, source_target_pairs={{4,8},{5,9},{6,10},{7,11},{20,24},{21,25},{22,26},{23,27}} | collective-permute-start | bytes 368648 | tf_op jit(solution)/shard_map/ppermute | solution.py:347
  18.5 17.1 %collective-permute-start.10 = (bf16[160,384]{1,0:T(8,128)(2,1)S(1)}, bf16[160,384]{1,0:T(8,128)(2,1)S(1)}, u32[]{:S(2)}, u32[]{:S(2)}) collective-permute-start(bf16[160,384]{1,0:T(8,128)(2,1)S(1)} %get-tuple-element.99), channel_id=1, source_target_pairs={{4,8},{5,9},{6,10},{7,11},{20,24},{21,25},{22,26},{23,27}} | collective-permute-start | bytes 368648 | tf_op jit(solution)/shard_map/ppermute | solution.py:347
  19.9 19.0 %collective-permute-start.9 = (bf16[160,384]{1,0:T(8,128)(2,1)S(1)}, bf16[160,384]{1,0:T(8,128)(2,1)S(1)}, u32[]{:S(2)}, u32[]{:S(2)}) collective-permute-start(bf16[160,384]{1,0:T(8,128)(2,1)S(1)} %frame.23), channel_id=1, source_target_pairs={{4,8},{5,9},{6,10},{7,11},{20,24},{21,25},{22,26},{23,27}} | collective-permute-start | bytes 368648 | tf_op jit(solution)/shard_map/ppermute | solution.py:347
  29.2 12.0 %collective-permute-start.16 = (bf16[144,384]{1,0:T(8,128)(2,1)S(1)}, bf16[144,384]{1,0:T(8,128)(2,1)S(1)}, u32[]{:S(2)}, u32[]{:S(2)}) collective-permute-start(bf16[144,384]{1,0:T(8,128)(2,1)S(1)} %get-tuple-element.113), channel_id=1, source_target_pairs={{8,12},{9,13},{10,14},{11,15},{24,28},{25,29},{26,30},{27,31}} | collective-permute-start | bytes 331784 | tf_op jit(solution)/shard_map/ppermute | solution.py:347
  32.9 8.4 %collective-permute-start.15 = (bf16[144,384]{1,0:T(8,128)(2,1)S(1)}, bf16[144,384]{1,0:T(8,128)(2,1)S(1)}, u32[]{:S(2)}, u32[]{:S(2)}) collective-permute-start(bf16[144,384]{1,0:T(8,128)(2,1)S(1)} %get-tuple-element.112), channel_id=1, source_target_pairs={{8,12},{9,13},{10,14},{11,15},{24,28},{25,29},{26,30},{27,31}} | collective-permute-start | bytes 331784 | tf_op jit(solution)/shard_map/ppermute | solution.py:347
  36.6 6.3 %collective-permute-start.14 = (bf16[144,384]{1,0:T(8,128)(2,1)S(1)}, bf16[144,384]{1,0:T(8,128)(2,1)S(1)}, u32[]{:S(2)}, u32[]{:S(2)}) collective-permute-start(bf16[144,384]{1,0:T(8,128)(2,1)S(1)} %get-tuple-element.111), channel_id=1, source_target_pairs={{8,12},{9,13},{10,14},{11,15},{24,28},{25,29},{26,30},{27,31}} | collective-permute-start | bytes 331784 | tf_op jit(solution)/shard_map/ppermute | solution.py:347
  39.9 4.4 %collective-permute-start.13 = (bf16[144,384]{1,0:T(8,128)(2,1)S(1)}, bf16[144,384]{1,0:T(8,128)(2,1)S(1)}, u32[]{:S(2)}, u32[]{:S(2)}) collective-permute-start(bf16[144,384]{1,0:T(8,128)(2,1)S(1)} %frame.27), channel_id=1, source_target_pairs={{8,12},{9,13},{10,14},{11,15},{24,28},{25,29},{26,30},{27,31}} | collective-permute-start | bytes 331784 | tf_op jit(solution)/shard_map/ppermute | solution.py:347
  41.3 3.0 %collective-permute-start.17 = (bf16[2,64,384]{2,1,0:T(8,128)(2,1)S(1)}, bf16[2,64,384]{2,1,0:T(8,128)(2,1)S(1)}, u32[]{:S(2)}, u32[]{:S(2)}) collective-permute-start(bf16[2,64,384]{2,1,0:T(8,128)(2,1)S(1)} %get-tuple-element.129), channel_id=1, source_target_pairs={{12,0},{14,2},{13,4},{15,6}} | collective-permute-start | bytes 294920 | tf_op jit(solution)/shard_map/ppermute | solution.py:259
  42.0 2.4 %collective-permute-start.18 = (bf16[2,64,384]{2,1,0:T(8,128)(2,1)S(1)}, bf16[2,64,384]{2,1,0:T(8,128)(2,1)S(1)}, u32[]{:S(2)}, u32[]{:S(2)}) collective-permute-start(bf16[2,64,384]{2,1,0:T(8,128)(2,1)S(1)} %get-tuple-element.130), channel_id=1, source_target_pairs={{12,1},{14,3},{13,5},{15,7}} | collective-permute-start | bytes 294920 | tf_op jit(solution)/shard_map/ppermute | solution.py:259
  43.0 3.5 %collective-permute-start.21 = (bf16[2,64,384]{2,1,0:T(8,128)(2,1)S(1)}, bf16[2,64,384]{2,1,0:T(8,128)(2,1)S(1)}, u32[]{:S(2)}, u32[]{:S(2)}) collective-permute-start(bf16[2,64,384]{2,1,0:T(8,128)(2,1)S(1)} %get-tuple-element.133), channel_id=1, source_target_pairs={{28,9},{30,11},{29,13},{31,15}} | collective-permute-start | bytes 294920 | tf_op jit(solution)/shard_map/ppermute | solution.py:259
  43.6 2.8 %collective-permute-start.22 = (bf16[2,64,384]{2,1,0:T(8,128)(2,1)S(1)}, bf16[2,64,384]{2,1,0:T(8,128)(2,1)S(1)}, u32[]{:S(2)}, u32[]{:S(2)}) collective-permute-start(bf16[2,64,384]{2,1,0:T(8,128)(2,1)S(1)} %get-tuple-element.134), channel_id=1, source_target_pairs={{28,8},{30,10},{29,12},{31,14}} | collective-permute-start | bytes 294920 | tf_op jit(solution)/shard_map/ppermute | solution.py:259
  44.4 2.0 %collective-permute-start.19 = (bf16[2,64,384]{2,1,0:T(8,128)(2,1)S(1)}, bf16[2,64,384]{2,1,0:T(8,128)(2,1)S(1)}, u32[]{:S(2)}, u32[]{:S(2)}) collective-permute-start(bf16[2,64,384]{2,1,0:T(8,128)(2,1)S(1)} %get-tuple-element.131), channel_id=1, source_target_pairs={{12,17},{14,19},{13,21},{15,23},{28,25},{30,27},{29,29},{31,31}} | collective-permute-start | bytes 294920 | tf_op jit(solution)/shard_map/ppermute | solution.py:259
  45.1 8.6 %collective-permute-start.20 = (bf16[2,64,384]{2,1,0:T(8,128)(2,1)S(1)}, bf16[2,64,384]{2,1,0:T(8,128)(2,1)S(1)}, u32[]{:S(2)}, u32[]{:S(2)}) collective-permute-start(bf16[2,64,384]{2,1,0:T(8,128)(2,1)S(1)} %get-tuple-element.132), channel_id=1, source_target_pairs={{12,16},{14,18},{13,20},{15,22},{28,24},{30,26},{29,28},{31,30}} | collective-permute-start | bytes 294920 | tf_op jit(solution)/shard_map/ppermute | solution.py:259

commit v16 on v13

--- a/solution.py
+++ b/solution.py
@@ -142,8 +142,11 @@
             length = value.shape[0] // len(tails)
             for number, tail in enumerate(tails):
                 tail[cfg["tail_at"]] = value[number * length : (number + 1) * length]
-            for double, tail in zip(doubles, tails):
-                double[...] = tail[...]
+            if doubles:
+                leads = lax.axis_index("tm") == 0
+                for number, double in enumerate(doubles):
+                    turned = tails[(number + 1) % len(tails)] if number == 0 else tails[number]
+                    double[...] = jnp.where(leads, turned[...], tails[number][...])
 
     for unit in cfg["units"]:
         pl.when(on_unit(unit, cfg["holders"]))(functools.partial(run, unit))
@@ -248,12 +251,14 @@
     )(*[pltpu.with_memory_space_constraint(value, pltpu.HBM) for value in stored])
     now, past, bias, gain = (resident(value) for value in (now, past, bias, gain))
 
-    def leave(value, there, index, group):
+    def leave(value, there, *members):
         routes = []
-        for clip in group:
-            for h in range(HALVES):
-                t, b = stream(clip, h)
-                routes.append((spot(t, segments - 1, b), spot(there, clip, h * per_half + index)))
+        for index, group in members:
+            for clip in group:
+                for h in range(HALVES):
+                    t, b = stream(clip, h)
+                    routes.append((spot(t, segments - 1, b), spot(there, clip, h * per_half + index)))
+        assert len({a for a, _ in routes}) == len({b for _, b in routes}) == len(routes)
         return lax.ppermute(value, MESH_AXES, routes)
 
     state = ((window - 1) * cols, channels)
@@ -342,16 +347,21 @@
         kept = results[finals:]
         for key, value in zip(old, kept):
             landed[key] = (value, slot)
-        for (there, index, _), value in zip(waiting, kept[len(old) :]):
-            landed[there, index, 1] = (leave(value, there, index, range(per_half, clips)), slot)
+        ahead, behind = range(per_half), range(per_half, clips)
+        if waiting:
+            there, (shared, alone) = waiting[0][0], kept[len(old) : len(old) + per_half]
+            both = leave(shared, there, (1, ahead), (0, behind))
+            landed[there, 1, 0] = landed[there, 0, 1] = (both, slot)
+            landed[there, 1, 1] = (leave(alone, there, (1, behind)), slot)
         waiting = []
         if finals and last % own_frames == own_frames - 1:
             there = last // own_frames
-            if not closing:
+            if closing:
+                for index, value in enumerate(tails):
+                    landed[there, index, 0] = (leave(value, there, (index, range(clips))), slot)
+            else:
                 waiting = [(there, index, value) for index, value in enumerate(kept[keeps:])]
-            for index, value in enumerate(tails):
-                group = range(clips if closing else per_half)
-                landed[there, index, 0] = (leave(value, there, index, group), slot)
+                landed[there, 0, 0] = (leave(tails[0], there, (0, ahead)), slot)
         if cfg["later"]:
             near, far = pl.pallas_call(
                 functools.partial(history_kernel, cfg),

time: 55 us -> 55.5 us (level)
  starting transfers between devices: 25.7 us -> 25 us
  waiting for transfers between devices: 15.5 us -> 16.2 us
    ppermute x6 -> x5, waiting for transfers between devices: 7.24 us -> 7.92 us  [leave(): return lax.ppermute(value, MESH_AXES, routes)]
    ppermute x6 -> x5, starting transfers between devices: 4.63 us -> 3.96 us  [leave(): return lax.ppermute(value, MESH_AXES, routes)]
  transfers between devices with their start and end apart: 23 -> 22, of which waited for: 5 -> 5; matrix products, arithmetic and copies ran while one was open for 0% -> 0% of each run, Pallas kernels for 20% -> 20%
where the time goes in v16:
time: 55.5 us; the launch traced here: 54.5 us
  starting transfers between devices  25 us (45%)
  waiting for transfers between devices  16.2 us (29%)
  Pallas kernels  12 us (22%)
  other arithmetic  0.67 us (1%)
  between operations  0.6 us (1%)
    ppermute x12, starting transfers between devices, local(): lax.ppermute(out, 'segment', [(s, s + 1) for s in senders_now])  13 us
    ppermute x12, waiting for transfers between devices, local(): lax.ppermute(out, 'segment', [(s, s + 1) for s in senders_now])  8.24 us
    ppermute x5, starting transfers between devices, gather(): return lax.ppermute(sources[number], MESH_AXES, routes)  8.03 us
    ppermute x5, waiting for transfers between devices, leave(): return lax.ppermute(value, MESH_AXES, routes)  7.92 us
    pallas_call x16, Pallas kernels, local(): pl.pallas_call(functools.partial(frame_kernel, cfg), out_shape=shapes, in...  4.26 us
    ppermute x5, starting transfers between devices, leave(): return lax.ppermute(value, MESH_AXES, routes)  3.96 us
    pallas_call x1, Pallas kernels, local(): pl.pallas_call(loader_kernel, out_shape=[pltpu.VMEM((TAPS * TAPS * channe...  3.42 us
    pallas_call x12, Pallas kernels, local(): pl.pallas_call(functools.partial(history_kernel, cfg), out_shape=[pltpu.V...  3.26 us
  transfers between devices with their start and end apart: 22, of which 5 were waited for; matrix products, arithmetic and copies ran while one was open for 0% of the time, Pallas kernels for 20%

profile of v16, /device:TPU:18, one launch (start us, length us, event | category | flops | bytes accessed | tf_op | source)
XLA Modules:
  0.0 54.5 jit_solution(3195989528824938664)
XLA Ops:
  0.0 1.1 %pick.1 = (bf16[2,64,384]{2,1,0:T(8,128)(2,1)S(1)}, bf16[2,64,384]{2,1,0:T(8,128)(2,1)S(1)}, bf16[2,64,384]{2,1,0:T(8,128)(2,1)S(1)}, bf16[2,64,384]{2,1,0:T(8,128)(2,1)S(1)}) custom-call(bf16[4,2,64,384]{3,2,1,0:T(8,128)(2,1)} %bitcast.4), custom_call_target="tpu_custom_call" | custom-call | tf_op jit(solution)/shard_map/pick/pallas_call | solution.py:193
  1.1 0.7 %collective-permute-start.3 = (bf16[2,64,384]{2,1,0:T(8,128)(2,1)S(1)}, bf16[2,64,384]{2,1,0:T(8,128)(2,1)S(1)}, u32[]{:S(2)}, u32[]{:S(2)}) collective-permute-start(bf16[2,64,384]{2,1,0:T(8,128)(2,1)S(1)} %get-tuple-element.69), channel_id=1, source_target_pairs={{14,0},{13,2},{0,1},{2,3},{6,16},{5,18},{8,17},{10,19}} | collective-permute-start | bytes 294920 | tf_op jit(solution)/shard_map/ppermute | solution.py:221
  1.8 0.7 %collective-permute-start.4 = (bf16[2,64,384]{2,1,0:T(8,128)(2,1)S(1)}, bf16[2,64,384]{2,1,0:T(8,128)(2,1)S(1)}, u32[]{:S(2)}, u32[]{:S(2)}) collective-permute-start(bf16[2,64,384]{2,1,0:T(8,128)(2,1)S(1)} %get-tuple-element.70), channel_id=1, source_target_pairs={{1,0},{3,2},{14,1},{13,3},{5,16},{7,18},{10,17},{9,19}} | collective-permute-start | bytes 294920 | tf_op jit(solution)/shard_map/ppermute | solution.py:221
  2.4 0.7 %collective-permute-start.2 = (bf16[2,64,384]{2,1,0:T(8,128)(2,1)S(1)}, bf16[2,64,384]{2,1,0:T(8,128)(2,1)S(1)}, u32[]{:S(2)}, u32[]{:S(2)}) collective-permute-start(bf16[2,64,384]{2,1,0:T(8,128)(2,1)S(1)} %get-tuple-element.72), channel_id=1, source_target_pairs={{0,16},{2,18},{1,17},{3,19},{20,0},{22,2},{21,1},{23,3}} | collective-permute-start | bytes 294920 | tf_op jit(solution)/shard_map/ppermute | solution.py:221
  3.1 5.4 %collective-permute-start = (bf16[2,64,384]{2,1,0:T(8,128)(2,1)S(1)}, bf16[2,64,384]{2,1,0:T(8,128)(2,1)S(1)}, u32[]{:S(2)}, u32[]{:S(2)}) collective-permute-start(bf16[2,64,384]{2,1,0:T(8,128)(2,1)S(1)} %get-tuple-element.69), channel_id=1, source_target_pairs={{22,0},{21,2},{24,1},{26,3},{30,16},{29,18},{16,17},{18,19}} | collective-permute-start | bytes 294920 | tf_op jit(solution)/shard_map/ppermute | solution.py:221
  8.5 0.7 %collective-permute-start.1 = (bf16[2,64,384]{2,1,0:T(8,128)(2,1)S(1)}, bf16[2,64,384]{2,1,0:T(8,128)(2,1)S(1)}, u32[]{:S(2)}, u32[]{:S(2)}) collective-permute-start(bf16[2,64,384]{2,1,0:T(8,128)(2,1)S(1)} %get-tuple-element.70), channel_id=1, source_target_pairs={{21,0},{23,2},{26,1},{25,3},{17,16},{19,18},{30,17},{29,19}} | collective-permute-start | bytes 294920 | tf_op jit(solution)/shard_map/ppermute | solution.py:221
  9.1 3.4 %loader.1 = (bf16[3456,384]{1,0:T(8,128)(2,1)S(1)}, bf16[3456,768]{1,0:T(8,128)(2,1)S(1)}, f32[1,384]{1,0:T(1,128)S(1)}, f32[1,384]{1,0:T(1,128)S(1)}) custom-call(bf16[3,3456,384]{2,1,0:T(8,128)(2,1)} %bitcast.3, f32[1,384]{1,0:T(1,128)} %bias.1, f32[1,384]{1,0:T(1,128)} %gain.1), custom_call_target="tpu_custom_call" | custom-call | tf_op jit(solution)/shard_map/loader/pallas_call | solution.py:238
  12.7 0.7 %collective-permute-start.8 = (bf16[176,384]{1,0:T(8,128)(2,1)S(1)}, bf16[176,384]{1,0:T(8,128)(2,1)S(1)}, u32[]{:S(2)}, u32[]{:S(2)}) collective-permute-start(bf16[176,384]{1,0:T(8,128)(2,1)S(1)} %get-tuple-element.87), channel_id=1, source_target_pairs={{0,4},{1,5},{2,6},{3,7},{16,20},{17,21},{18,22},{19,23}} | collective-permute-start | bytes 405512 | tf_op jit(solution)/shard_map/ppermute | solution.py:346
  13.4 0.7 %collective-permute-start.7 = (bf16[176,384]{1,0:T(8,128)(2,1)S(1)}, bf16[176,384]{1,0:T(8,128)(2,1)S(1)}, u32[]{:S(2)}, u32[]{:S(2)}) collective-permute-start(bf16[176,384]{1,0:T(8,128)(2,1)S(1)} %get-tuple-element.86), channel_id=1, source_target_pairs={{0,4},{1,5},{2,6},{3,7},{16,20},{17,21},{18,22},{19,23}} | collective-permute-start | bytes 405512 | tf_op jit(solution)/shard_map/ppermute | solution.py:346
  14.2 0.7 %collective-permute-start.6 = (bf16[176,384]{1,0:T(8,128)(2,1)S(1)}, bf16[176,384]{1,0:T(8,128)(2,1)S(1)}, u32[]{:S(2)}, u32[]{:S(2)}) collective-permute-start(bf16[176,384]{1,0:T(8,128)(2,1)S(1)} %get-tuple-element.85), channel_id=1, source_target_pairs={{0,4},{1,5},{2,6},{3,7},{16,20},{17,21},{18,22},{19,23}} | collective-permute-start | bytes 405512 | tf_op jit(solution)/shard_map/ppermute | solution.py:346
  14.9 0.7 %collective-permute-start.5 = (bf16[176,384]{1,0:T(8,128)(2,1)S(1)}, bf16[176,384]{1,0:T(8,128)(2,1)S(1)}, u32[]{:S(2)}, u32[]{:S(2)}) collective-permute-start(bf16[176,384]{1,0:T(8,128)(2,1)S(1)} %frame.19), channel_id=1, source_target_pairs={{0,4},{1,5},{2,6},{3,7},{16,20},{17,21},{18,22},{19,23}} | collective-permute-start | bytes 405512 | tf_op jit(solution)/shard_map/ppermute | solution.py:346
  15.6 1.3 %collective-permute-start.12 = (bf16[160,384]{1,0:T(8,128)(2,1)S(1)}, bf16[160,384]{1,0:T(8,128)(2,1)S(1)}, u32[]{:S(2)}, u32[]{:S(2)}) collective-permute-start(bf16[160,384]{1,0:T(8,128)(2,1)S(1)} %get-tuple-element.99), channel_id=1, source_target_pairs={{4,8},{5,9},{6,10},{7,11},{20,24},{21,25},{22,26},{23,27}} | collective-permute-start | bytes 368648 | tf_op jit(solution)/shard_map/ppermute | solution.py:346
  17.0 1.3 %collective-permute-start.11 = (bf16[160,384]{1,0:T(8,128)(2,1)S(1)}, bf16[160,384]{1,0:T(8,128)(2,1)S(1)}, u32[]{:S(2)}, u32[]{:S(2)}) collective-permute-start(bf16[160,384]{1,0:T(8,128)(2,1)S(1)} %get-tuple-element.98), channel_id=1, source_target_pairs={{4,8},{5,9},{6,10},{7,11},{20,24},{21,25},{22,26},{23,27}} | collective-permute-start | bytes 368648 | tf_op jit(solution)/shard_map/ppermute | solution.py:346
  18.5 1.3 %collective-permute-start.10 = (bf16[160,384]{1,0:T(8,128)(2,1)S(1)}, bf16[160,384]{1,0:T(8,128)(2,1)S(1)}, u32[]{:S(2)}, u32[]{:S(2)}) collective-permute-start(bf16[160,384]{1,0:T(8,128)(2,1)S(1)} %get-tuple-element.97), channel_id=1, source_target_pairs={{4,8},{5,9},{6,10},{7,11},{20,24},{21,25},{22,26},{23,27}} | collective-permute-start | bytes 368648 | tf_op jit(solution)/shard_map/ppermute | solution.py:346
  19.9 1.3 %collective-permute-start.9 = (bf16[160,384]{1,0:T(8,128)(2,1)S(1)}, bf16[160,384]{1,0:T(8,128)(2,1)S(1)}, u32[]{:S(2)}, u32[]{:S(2)}) collective-permute-start(bf16[160,384]{1,0:T(8,128)(2,1)S(1)} %frame.23), channel_id=1, source_target_pairs={{4,8},{5,9},{6,10},{7,11},{20,24},{21,25},{22,26},{23,27}} | collective-permute-start | bytes 368648 | tf_op jit(solution)/shard_map/ppermute | solution.py:346
  21.2 7.1 %collective-permute-done.12.refs_0_ = bf16[160,384]{1,0:T(8,128)(2,1)S(1)} collective-permute-done((bf16[160,384]{1,0:T(8,128)(2,1)S(1)}, bf16[160,384]{1,0:T(8,128)(2,1)S(1)}, u32[]{:S(2)}, u32[]{:S(2)}) %collective-permute-start.12) | collective-permute-done | bytes 122912 | tf_op jit(solution)/shard_map/ppermute | solution.py:346
  28.3 1.0 %frame.24 = (bf16[144,384]{1,0:T(8,128)(2,1)S(1)}, bf16[224,1152]{1,0:T(8,128)(2,1)S(1)}) custom-call(bf16[160,384]{1,0:T(8,128)(2,1)S(1)} %collective-permute-done.12.refs_0_, f32[176,384]{1,0:T(8,128)S(1)} %get-tuple-element.96.refs_1_.near, bf16[3456,384]{1,0:T(8,128)(2,1)S(1)} %get-tuple-element.73.refs_5_.refs_7_.refs_2_, ...), custom_call_target="tpu_custom_call" | custom-call | bytes 1024 | tf_op jit(solution)/shard_map/frame/pallas_call | solution.py:330
  29.3 1.3 %collective-permute-start.16 = (bf16[144,384]{1,0:T(8,128)(2,1)S(1)}, bf16[144,384]{1,0:T(8,128)(2,1)S(1)}, u32[]{:S(2)}, u32[]{:S(2)}) collective-permute-start(bf16[144,384]{1,0:T(8,128)(2,1)S(1)} %get-tuple-element.111), channel_id=1, source_target_pairs={{8,12},{9,13},{10,14},{11,15},{24,28},{25,29},{26,30},{27,31}} | collective-permute-start | bytes 331784 | tf_op jit(solution)/shard_map/ppermute | solution.py:346
  30.6 1.1 %history.18 = (f32[176,384]{1,0:T(8,128)S(1)}, f32[176,384]{1,0:T(8,128)S(1)}) custom-call(bf16[224,1152]{1,0:T(8,128)(2,1)S(1)} %get-tuple-element.100.spread, f32[176,384]{1,0:T(8,128)S(1)} %get-tuple-element.96.refs_1_.near, f32[176,384]{1,0:T(8,128)S(1)} %get-tuple-element.101.far, ...), custom_call_target="tpu_custom_call", output_to_operand_aliasing={{0}: (1, {}), {1}: (2, {})} | custom-call | bytes 1024 | tf_op jit(solution)/shard_map/history/pallas_call | solution.py:366
  32.1 1.0 %frame.25 = (bf16[144,384]{1,0:T(8,128)(2,1)S(1)}, bf16[224,1152]{1,0:T(8,128)(2,1)S(1)}) custom-call(bf16[160,384]{1,0:T(8,128)(2,1)S(1)} %collective-permute-done.11.refs_0_, f32[176,384]{1,0:T(8,128)S(1)} %get-tuple-element.102.refs_1_.near, bf16[3456,384]{1,0:T(8,128)(2,1)S(1)} %get-tuple-element.73.refs_5_.refs_7_.refs_2_, ...), custom_call_target="tpu_custom_call" | custom-call | bytes 1024 | tf_op jit(solution)/shard_map/frame/pallas_call | solution.py:330
  33.0 1.3 %collective-permute-start.15 = (bf16[144,384]{1,0:T(8,128)(2,1)S(1)}, bf16[144,384]{1,0:T(8,128)(2,1)S(1)}, u32[]{:S(2)}, u32[]{:S(2)}) collective-permute-start(bf16[144,384]{1,0:T(8,128)(2,1)S(1)} %get-tuple-element.110), channel_id=1, source_target_pairs={{8,12},{9,13},{10,14},{11,15},{24,28},{25,29},{26,30},{27,31}} | collective-permute-start | bytes 331784 | tf_op jit(solution)/shard_map/ppermute | solution.py:346
  34.3 1.1 %history.19 = (f32[176,384]{1,0:T(8,128)S(1)}, f32[176,384]{1,0:T(8,128)S(1)}) custom-call(bf16[224,1152]{1,0:T(8,128)(2,1)S(1)} %get-tuple-element.103.spread, f32[176,384]{1,0:T(8,128)S(1)} %get-tuple-element.102.refs_1_.near, f32[176,384]{1,0:T(8,128)S(1)} %get-tuple-element.104.far, ...), custom_call_target="tpu_custom_call", output_to_operand_aliasing={{0}: (1, {}), {1}: (2, {})} | custom-call | bytes 1024 | tf_op jit(solution)/shard_map/history/pallas_call | solution.py:366
  35.8 1.0 %frame.26 = (bf16[144,384]{1,0:T(8,128)(2,1)S(1)}, bf16[224,1152]{1,0:T(8,128)(2,1)S(1)}) custom-call(bf16[160,384]{1,0:T(8,128)(2,1)S(1)} %collective-permute-done.10.refs_0_, f32[176,384]{1,0:T(8,128)S(1)} %get-tuple-element.105.refs_1_.near, bf16[3456,384]{1,0:T(8,128)(2,1)S(1)} %get-tuple-element.73.refs_5_.refs_7_.refs_2_, ...), custom_call_target="tpu_custom_call" | custom-call | bytes 1024 | tf_op jit(solution)/shard_map/frame/pallas_call | solution.py:330
  36.8 1.3 %collective-permute-start.14 = (bf16[144,384]{1,0:T(8,128)(2,1)S(1)}, bf16[144,384]{1,0:T(8,128)(2,1)S(1)}, u32[]{:S(2)}, u32[]{:S(2)}) collective-permute-start(bf16[144,384]{1,0:T(8,128)(2,1)S(1)} %get-tuple-element.109), channel_id=1, source_target_pairs={{8,12},{9,13},{10,14},{11,15},{24,28},{25,29},{26,30},{27,31}} | collective-permute-start | bytes 331784 | tf_op jit(solution)/shard_map/ppermute | solution.py:346
  38.1 0.7 %history.20 = (f32[176,384]{1,0:T(8,128)S(1)}, f32[176,384]{1,0:T(8,128)S(1)}) custom-call(bf16[224,1152]{1,0:T(8,128)(2,1)S(1)} %get-tuple-element.106.spread, f32[176,384]{1,0:T(8,128)S(1)} %get-tuple-element.105.refs_1_.near, f32[176,384]{1,0:T(8,128)S(1)} %get-tuple-element.107.far, ...), custom_call_target="tpu_custom_call", output_to_operand_aliasing={{0}: (1, {}), {1}: (2, {})} | custom-call | bytes 1024 | tf_op jit(solution)/shard_map/history/pallas_call | solution.py:366
  39.1 1.0 %frame.27 = bf16[144,384]{1,0:T(8,128)(2,1)S(1)} custom-call(bf16[160,384]{1,0:T(8,128)(2,1)S(1)} %collective-permute-done.9.refs_0_, f32[176,384]{1,0:T(8,128)S(1)} %get-tuple-element.108.refs_1_.near, bf16[3456,384]{1,0:T(8,128)(2,1)S(1)} %get-tuple-element.73.refs_5_.refs_7_.refs_2_, f32[1,384]{1,0:T(1,128)S(1)} %get-tuple-element.74.refs_6_.refs_8_.refs_3_, ...), custom_call_target="tpu_custom_call" | custom-call | bytes 1024 | tf_op jit(solution)/shard_map/frame/pallas_call | solution.py:330
  40.1 1.3 %collective-permute-start.13 = (bf16[144,384]{1,0:T(8,128)(2,1)S(1)}, bf16[144,384]{1,0:T(8,128)(2,1)S(1)}, u32[]{:S(2)}, u32[]{:S(2)}) collective-permute-start(bf16[144,384]{1,0:T(8,128)(2,1)S(1)} %frame.27), channel_id=1, source_target_pairs={{8,12},{9,13},{10,14},{11,15},{24,28},{25,29},{26,30},{27,31}} | collective-permute-start | bytes 331784 | tf_op jit(solution)/shard_map/ppermute | solution.py:346
  41.5 0.7 %collective-permute-start.17 = (bf16[2,64,384]{2,1,0:T(8,128)(2,1)S(1)}, bf16[2,64,384]{2,1,0:T(8,128)(2,1)S(1)}, u32[]{:S(2)}, u32[]{:S(2)}) collective-permute-start(bf16[2,64,384]{2,1,0:T(8,128)(2,1)S(1)} %get-tuple-element.127), channel_id=1, source_target_pairs={{12,0},{14,2},{13,4},{15,6}} | collective-permute-start | bytes 294920 | tf_op jit(solution)/shard_map/ppermute | solution.py:262
  42.4 0.7 %collective-permute-start.20 = (bf16[2,64,384]{2,1,0:T(8,128)(2,1)S(1)}, bf16[2,64,384]{2,1,0:T(8,128)(2,1)S(1)}, u32[]{:S(2)}, u32[]{:S(2)}) collective-permute-start(bf16[2,64,384]{2,1,0:T(8,128)(2,1)S(1)} %get-tuple-element.130), channel_id=1, source_target_pairs={{28,9},{30,11},{29,13},{31,15}} | collective-permute-start | bytes 294920 | tf_op jit(solution)/shard_map/ppermute | solution.py:262
  44.6 1.3 %collective-permute-start.19 = (bf16[2,64,384]{2,1,0:T(8,128)(2,1)S(1)}, bf16[2,64,384]{2,1,0:T(8,128)(2,1)S(1)}, u32[]{:S(2)}, u32[]{:S(2)}) collective-permute-start(bf16[2,64,384]{2,1,0:T(8,128)(2,1)S(1)} %get-tuple-element.129), channel_id=1, source_target_pairs={{12,16},{14,18},{13,20},{15,22},{28,24},{30,26},{29,28},{31,30}} | collective-permute-start | bytes 294920 | tf_op jit(solution)/shard_map/ppermute | solution.py:262
  45.9 7.9 %collective-permute-done.19 = bf16[2,64,384]{2,1,0:T(8,128)(2,1)S(1)} collective-permute-done((bf16[2,64,384]{2,1,0:T(8,128)(2,1)S(1)}, bf16[2,64,384]{2,1,0:T(8,128)(2,1)S(1)}, u32[]{:S(2)}, u32[]{:S(2)}) %collective-permute-start.19) | collective-permute-done | bytes 98336 | tf_op jit(solution)/shard_map/ppermute | solution.py:262
  53.8 0.7 %fusion.2 = bf16[2,64,384]{2,1,0:T(8,128)(2,1)} fusion(bf16[2,64,384]{2,1,0:T(8,128)(2,1)S(1)} %collective-permute-done.18, bf16[2,64,384]{2,1,0:T(8,128)(2,1)S(1)} %collective-permute-done.19, bf16[2,64,384]{2,1,0:T(8,128)(2,1)S(1)} %collective-permute-done.20, bf16[2,64,384]{2,1,0:T(8,128)(2,1)S(1)} %collective-permute-done.21, ...), kind=kLoop, calls=%fused_computation.3 | loop fusion | flops 245760 | bytes 589829 | tf_op jit(solution)/shard_map/jit(_where)/select_n | solution.py:382
  (45 shorter events, 3.3 us)
Async XLA Ops:
  1.1 11.5 %collective-permute-start.3 = (bf16[2,64,384]{2,1,0:T(8,128)(2,1)S(1)}, bf16[2,64,384]{2,1,0:T(8,128)(2,1)S(1)}, u32[]{:S(2)}, u32[]{:S(2)}) collective-permute-start(bf16[2,64,384]{2,1,0:T(8,128)(2,1)S(1)} %get-tuple-element.69), channel_id=1, source_target_pairs={{14,0},{13,2},{0,1},{2,3},{6,16},{5,18},{8,17},{10,19}} | collective-permute-start | bytes 294920 | tf_op jit(solution)/shard_map/ppermute | solution.py:221
  1.8 10.8 %collective-permute-start.4 = (bf16[2,64,384]{2,1,0:T(8,128)(2,1)S(1)}, bf16[2,64,384]{2,1,0:T(8,128)(2,1)S(1)}, u32[]{:S(2)}, u32[]{:S(2)}) collective-permute-start(bf16[2,64,384]{2,1,0:T(8,128)(2,1)S(1)} %get-tuple-element.70), channel_id=1, source_target_pairs={{1,0},{3,2},{14,1},{13,3},{5,16},{7,18},{10,17},{9,19}} | collective-permute-start | bytes 294920 | tf_op jit(solution)/shard_map/ppermute | solution.py:221
  2.4 10.2 %collective-permute-start.2 = (bf16[2,64,384]{2,1,0:T(8,128)(2,1)S(1)}, bf16[2,64,384]{2,1,0:T(8,128)(2,1)S(1)}, u32[]{:S(2)}, u32[]{:S(2)}) collective-permute-start(bf16[2,64,384]{2,1,0:T(8,128)(2,1)S(1)} %get-tuple-element.72), channel_id=1, source_target_pairs={{0,16},{2,18},{1,17},{3,19},{20,0},{22,2},{21,1},{23,3}} | collective-permute-start | bytes 294920 | tf_op jit(solution)/shard_map/ppermute | solution.py:221
  3.1 11.0 %collective-permute-start = (bf16[2,64,384]{2,1,0:T(8,128)(2,1)S(1)}, bf16[2,64,384]{2,1,0:T(8,128)(2,1)S(1)}, u32[]{:S(2)}, u32[]{:S(2)}) collective-permute-start(bf16[2,64,384]{2,1,0:T(8,128)(2,1)S(1)} %get-tuple-element.69), channel_id=1, source_target_pairs={{22,0},{21,2},{24,1},{26,3},{30,16},{29,18},{16,17},{18,19}} | collective-permute-start | bytes 294920 | tf_op jit(solution)/shard_map/ppermute | solution.py:221
  8.5 5.7 %collective-permute-start.1 = (bf16[2,64,384]{2,1,0:T(8,128)(2,1)S(1)}, bf16[2,64,384]{2,1,0:T(8,128)(2,1)S(1)}, u32[]{:S(2)}, u32[]{:S(2)}) collective-permute-start(bf16[2,64,384]{2,1,0:T(8,128)(2,1)S(1)} %get-tuple-element.70), channel_id=1, source_target_pairs={{21,0},{23,2},{26,1},{25,3},{17,16},{19,18},{30,17},{29,19}} | collective-permute-start | bytes 294920 | tf_op jit(solution)/shard_map/ppermute | solution.py:221
  12.7 2.9 %collective-permute-start.8 = (bf16[176,384]{1,0:T(8,128)(2,1)S(1)}, bf16[176,384]{1,0:T(8,128)(2,1)S(1)}, u32[]{:S(2)}, u32[]{:S(2)}) collective-permute-start(bf16[176,384]{1,0:T(8,128)(2,1)S(1)} %get-tuple-element.87), channel_id=1, source_target_pairs={{0,4},{1,5},{2,6},{3,7},{16,20},{17,21},{18,22},{19,23}} | collective-permute-start | bytes 405512 | tf_op jit(solution)/shard_map/ppermute | solution.py:346
  13.4 3.5 %collective-permute-start.7 = (bf16[176,384]{1,0:T(8,128)(2,1)S(1)}, bf16[176,384]{1,0:T(8,128)(2,1)S(1)}, u32[]{:S(2)}, u32[]{:S(2)}) collective-permute-start(bf16[176,384]{1,0:T(8,128)(2,1)S(1)} %get-tuple-element.86), channel_id=1, source_target_pairs={{0,4},{1,5},{2,6},{3,7},{16,20},{17,21},{18,22},{19,23}} | collective-permute-start | bytes 405512 | tf_op jit(solution)/shard_map/ppermute | solution.py:346
  14.2 4.2 %collective-permute-start.6 = (bf16[176,384]{1,0:T(8,128)(2,1)S(1)}, bf16[176,384]{1,0:T(8,128)(2,1)S(1)}, u32[]{:S(2)}, u32[]{:S(2)}) collective-permute-start(bf16[176,384]{1,0:T(8,128)(2,1)S(1)} %get-tuple-element.85), channel_id=1, source_target_pairs={{0,4},{1,5},{2,6},{3,7},{16,20},{17,21},{18,22},{19,23}} | collective-permute-start | bytes 405512 | tf_op jit(solution)/shard_map/ppermute | solution.py:346
  14.9 5.0 %collective-permute-start.5 = (bf16[176,384]{1,0:T(8,128)(2,1)S(1)}, bf16[176,384]{1,0:T(8,128)(2,1)S(1)}, u32[]{:S(2)}, u32[]{:S(2)}) collective-permute-start(bf16[176,384]{1,0:T(8,128)(2,1)S(1)} %frame.19), channel_id=1, source_target_pairs={{0,4},{1,5},{2,6},{3,7},{16,20},{17,21},{18,22},{19,23}} | collective-permute-start | bytes 405512 | tf_op jit(solution)/shard_map/ppermute | solution.py:346
  15.6 12.7 %collective-permute-start.12 = (bf16[160,384]{1,0:T(8,128)(2,1)S(1)}, bf16[160,384]{1,0:T(8,128)(2,1)S(1)}, u32[]{:S(2)}, u32[]{:S(2)}) collective-permute-start(bf16[160,384]{1,0:T(8,128)(2,1)S(1)} %get-tuple-element.99), channel_id=1, source_target_pairs={{4,8},{5,9},{6,10},{7,11},{20,24},{21,25},{22,26},{23,27}} | collective-permute-start | bytes 368648 | tf_op jit(solution)/shard_map/ppermute | solution.py:346
  17.0 15.1 %collective-permute-start.11 = (bf16[160,384]{1,0:T(8,128)(2,1)S(1)}, bf16[160,384]{1,0:T(8,128)(2,1)S(1)}, u32[]{:S(2)}, u32[]{:S(2)}) collective-permute-start(bf16[160,384]{1,0:T(8,128)(2,1)S(1)} %get-tuple-element.98), channel_id=1, source_target_pairs={{4,8},{5,9},{6,10},{7,11},{20,24},{21,25},{22,26},{23,27}} | collective-permute-start | bytes 368648 | tf_op jit(solution)/shard_map/ppermute | solution.py:346
  18.5 17.3 %collective-permute-start.10 = (bf16[160,384]{1,0:T(8,128)(2,1)S(1)}, bf16[160,384]{1,0:T(8,128)(2,1)S(1)}, u32[]{:S(2)}, u32[]{:S(2)}) collective-permute-start(bf16[160,384]{1,0:T(8,128)(2,1)S(1)} %get-tuple-element.97), channel_id=1, source_target_pairs={{4,8},{5,9},{6,10},{7,11},{20,24},{21,25},{22,26},{23,27}} | collective-permute-start | bytes 368648 | tf_op jit(solution)/shard_map/ppermute | solution.py:346
  19.9 19.2 %collective-permute-start.9 = (bf16[160,384]{1,0:T(8,128)(2,1)S(1)}, bf16[160,384]{1,0:T(8,128)(2,1)S(1)}, u32[]{:S(2)}, u32[]{:S(2)}) collective-permute-start(bf16[160,384]{1,0:T(8,128)(2,1)S(1)} %frame.23), channel_id=1, source_target_pairs={{4,8},{5,9},{6,10},{7,11},{20,24},{21,25},{22,26},{23,27}} | collective-permute-start | bytes 368648 | tf_op jit(solution)/shard_map/ppermute | solution.py:346
  29.3 12.1 %collective-permute-start.16 = (bf16[144,384]{1,0:T(8,128)(2,1)S(1)}, bf16[144,384]{1,0:T(8,128)(2,1)S(1)}, u32[]{:S(2)}, u32[]{:S(2)}) collective-permute-start(bf16[144,384]{1,0:T(8,128)(2,1)S(1)} %get-tuple-element.111), channel_id=1, source_target_pairs={{8,12},{9,13},{10,14},{11,15},{24,28},{25,29},{26,30},{27,31}} | collective-permute-start | bytes 331784 | tf_op jit(solution)/shard_map/ppermute | solution.py:346
  33.0 8.4 %collective-permute-start.15 = (bf16[144,384]{1,0:T(8,128)(2,1)S(1)}, bf16[144,384]{1,0:T(8,128)(2,1)S(1)}, u32[]{:S(2)}, u32[]{:S(2)}) collective-permute-start(bf16[144,384]{1,0:T(8,128)(2,1)S(1)} %get-tuple-element.110), channel_id=1, source_target_pairs={{8,12},{9,13},{10,14},{11,15},{24,28},{25,29},{26,30},{27,31}} | collective-permute-start | bytes 331784 | tf_op jit(solution)/shard_map/ppermute | solution.py:346
  36.8 5.6 %collective-permute-start.14 = (bf16[144,384]{1,0:T(8,128)(2,1)S(1)}, bf16[144,384]{1,0:T(8,128)(2,1)S(1)}, u32[]{:S(2)}, u32[]{:S(2)}) collective-permute-start(bf16[144,384]{1,0:T(8,128)(2,1)S(1)} %get-tuple-element.109), channel_id=1, source_target_pairs={{8,12},{9,13},{10,14},{11,15},{24,28},{25,29},{26,30},{27,31}} | collective-permute-start | bytes 331784 | tf_op jit(solution)/shard_map/ppermute | solution.py:346
  40.1 3.8 %collective-permute-start.13 = (bf16[144,384]{1,0:T(8,128)(2,1)S(1)}, bf16[144,384]{1,0:T(8,128)(2,1)S(1)}, u32[]{:S(2)}, u32[]{:S(2)}) collective-permute-start(bf16[144,384]{1,0:T(8,128)(2,1)S(1)} %frame.27), channel_id=1, source_target_pairs={{8,12},{9,13},{10,14},{11,15},{24,28},{25,29},{26,30},{27,31}} | collective-permute-start | bytes 331784 | tf_op jit(solution)/shard_map/ppermute | solution.py:346
  41.5 2.4 %collective-permute-start.17 = (bf16[2,64,384]{2,1,0:T(8,128)(2,1)S(1)}, bf16[2,64,384]{2,1,0:T(8,128)(2,1)S(1)}, u32[]{:S(2)}, u32[]{:S(2)}) collective-permute-start(bf16[2,64,384]{2,1,0:T(8,128)(2,1)S(1)} %get-tuple-element.127), channel_id=1, source_target_pairs={{12,0},{14,2},{13,4},{15,6}} | collective-permute-start | bytes 294920 | tf_op jit(solution)/shard_map/ppermute | solution.py:262
  42.4 3.4 %collective-permute-start.20 = (bf16[2,64,384]{2,1,0:T(8,128)(2,1)S(1)}, bf16[2,64,384]{2,1,0:T(8,128)(2,1)S(1)}, u32[]{:S(2)}, u32[]{:S(2)}) collective-permute-start(bf16[2,64,384]{2,1,0:T(8,128)(2,1)S(1)} %get-tuple-element.130), channel_id=1, source_target_pairs={{28,9},{30,11},{29,13},{31,15}} | collective-permute-start | bytes 294920 | tf_op jit(solution)/shard_map/ppermute | solution.py:262
  43.1 2.8 %collective-permute-start.21 = (bf16[2,64,384]{2,1,0:T(8,128)(2,1)S(1)}, bf16[2,64,384]{2,1,0:T(8,128)(2,1)S(1)}, u32[]{:S(2)}, u32[]{:S(2)}) collective-permute-start(bf16[2,64,384]{2,1,0:T(8,128)(2,1)S(1)} %get-tuple-element.131), channel_id=1, source_target_pairs={{12,1},{14,3},{13,5},{15,7},{28,8},{30,10},{29,12},{31,14}} | collective-permute-start | bytes 294920 | tf_op jit(solution)/shard_map/ppermute | solution.py:262
  43.9 2.0 %collective-permute-start.18 = (bf16[2,64,384]{2,1,0:T(8,128)(2,1)S(1)}, bf16[2,64,384]{2,1,0:T(8,128)(2,1)S(1)}, u32[]{:S(2)}, u32[]{:S(2)}) collective-permute-start(bf16[2,64,384]{2,1,0:T(8,128)(2,1)S(1)} %get-tuple-element.128), channel_id=1, source_target_pairs={{12,17},{14,19},{13,21},{15,23},{28,25},{30,27},{29,29},{31,31}} | collective-permute-start | bytes 294920 | tf_op jit(solution)/shard_map/ppermute | solution.py:262
  44.6 9.3 %collective-permute-start.19 = (bf16[2,64,384]{2,1,0:T(8,128)(2,1)S(1)}, bf16[2,64,384]{2,1,0:T(8,128)(2,1)S(1)}, u32[]{:S(2)}, u32[]{:S(2)}) collective-permute-start(bf16[2,64,384]{2,1,0:T(8,128)(2,1)S(1)} %get-tuple-element.129), channel_id=1, source_target_pairs={{12,16},{14,18},{13,20},{15,22},{28,24},{30,26},{29,28},{31,30}} | collective-permute-start | bytes 294920 | tf_op jit(solution)/shard_map/ppermute | solution.py:262

commit v17 on v11

--- a/solution.py
+++ b/solution.py
@@ -146,6 +146,21 @@
 
     for unit in cfg["units"]:
         pl.when(on_unit(unit, cfg["holders"]))(functools.partial(run, unit))
+
+
+def keep_kernel(keys, times, per_half, *refs):
+    arrived, out, sem = refs[:-2], refs[-2], refs[-1]
+    band, position = lax.axis_index("band"), lax.axis_index("segment")
+    for (time, index, late), value in zip(keys, arrived):
+        here = jnp.logical_and(lax.axis_index("tm") == time, band % per_half == index)
+        if time < times - 1:
+            here = jnp.logical_and(here, position >= per_half if late else position < per_half)
+
+        @pl.when(here)
+        def _():
+            copy = pltpu.make_async_copy(value, out, sem)
+            copy.start()
+            copy.wait()
 
 
 def history_kernel(cfg, spread, near, far, weight, near_out, far_out):
@@ -363,12 +378,16 @@
                 name="history",
             )(resident(spread), resident(near), resident(far), past)
 
-    result = None
-    for (t, index, late), (value, _) in landed.items():
-        here = jnp.logical_and(time == t, band % per_half == index)
-        if t < times - 1:
-            here = jnp.logical_and(here, (position >= per_half) == bool(late))
-        result = value if result is None else jnp.where(here, value, result)
+    result = pl.pallas_call(
+        functools.partial(keep_kernel, list(landed), times, per_half),
+        out_shape=jax.ShapeDtypeStruct((own_frames, piece, channels), features.dtype),
+        in_specs=[whole()] * len(landed),
+        out_specs=whole(pltpu.HBM),
+        scratch_shapes=[pltpu.SemaphoreType.DMA],
+        compiler_params=pltpu.CompilerParams(vmem_limit_bytes=1 << 20),
+        cost_estimate=pl.CostEstimate(flops=0, transcendentals=0, bytes_accessed=1 << 10),
+        name="keep",
+    )(*[resident(value) for value, _ in landed.values()])
     return result.reshape(1, own_frames, own_rows, cols, channels)
 
 

time: 55.1 us -> 56.8 us (1.031)
  the two profiles are of different devices: /device:TPU:18 before, /device:TPU:3 now
where the time goes in v17:
time: 56.8 us; the launch traced here: 56.4 us
  starting transfers between devices  27.4 us (48%)
  waiting for transfers between devices  14.2 us (25%)
  Pallas kernels  13.9 us (24%)
  between operations  0.78 us (1%)
    ppermute x12, starting transfers between devices, local(): lax.ppermute(out, 'segment', [(s, s + 1) for s in senders_now])  14.4 us
    ppermute x6, waiting for transfers between devices, leave(): return lax.ppermute(value, MESH_AXES, routes)  13.4 us
    ppermute x5, starting transfers between devices, gather(): return lax.ppermute(sources[number], MESH_AXES, routes)  8.38 us
    pallas_call x16, Pallas kernels, local(): pl.pallas_call(functools.partial(frame_kernel, cfg), out_shape=shapes, in...  5.04 us
    ppermute x6, starting transfers between devices, leave(): return lax.ppermute(value, MESH_AXES, routes)  4.63 us
    pallas_call x12, Pallas kernels, local(): pl.pallas_call(functools.partial(history_kernel, cfg), out_shape=[pltpu.V...  3.73 us
    pallas_call x1, Pallas kernels, local(): pl.pallas_call(loader_kernel, out_shape=[pltpu.VMEM((TAPS * TAPS * channe...  3.42 us
  transfers between devices with their start and end apart: 23, of which 2 were waited for; matrix products, arithmetic and copies ran while one was open for 0% of the time, Pallas kernels for 22%

profile of v17, /device:TPU:3, one launch (start us, length us, event | category | flops | bytes accessed | tf_op | source)
XLA Modules:
  0.0 56.4 jit_solution(8155486020454510035)
XLA Ops:
  0.0 1.1 %pick.1 = (bf16[2,64,384]{2,1,0:T(8,128)(2,1)S(1)}, bf16[2,64,384]{2,1,0:T(8,128)(2,1)S(1)}, bf16[2,64,384]{2,1,0:T(8,128)(2,1)S(1)}, bf16[2,64,384]{2,1,0:T(8,128)(2,1)S(1)}) custom-call(bf16[4,2,64,384]{3,2,1,0:T(8,128)(2,1)} %bitcast.4), custom_call_target="tpu_custom_call" | custom-call | tf_op jit(solution)/shard_map/pick/pallas_call | solution.py:204
  1.1 1.3 %collective-permute-start.2 = (bf16[2,64,384]{2,1,0:T(8,128)(2,1)S(1)}, bf16[2,64,384]{2,1,0:T(8,128)(2,1)S(1)}, u32[]{:S(2)}, u32[]{:S(2)}) collective-permute-start(bf16[2,64,384]{2,1,0:T(8,128)(2,1)S(1)} %get-tuple-element.74), channel_id=1, source_target_pairs={{0,16},{2,18},{1,17},{3,19},{20,0},{22,2},{21,1},{23,3}} | collective-permute-start | bytes 294920 | tf_op jit(solution)/shard_map/ppermute | solution.py:232
  2.4 1.3 %collective-permute-start.3 = (bf16[2,64,384]{2,1,0:T(8,128)(2,1)S(1)}, bf16[2,64,384]{2,1,0:T(8,128)(2,1)S(1)}, u32[]{:S(2)}, u32[]{:S(2)}) collective-permute-start(bf16[2,64,384]{2,1,0:T(8,128)(2,1)S(1)} %get-tuple-element.71), channel_id=1, source_target_pairs={{14,0},{13,2},{0,1},{2,3},{6,16},{5,18},{8,17},{10,19}} | collective-permute-start | bytes 294920 | tf_op jit(solution)/shard_map/ppermute | solution.py:232
  3.7 1.3 %collective-permute-start.4 = (bf16[2,64,384]{2,1,0:T(8,128)(2,1)S(1)}, bf16[2,64,384]{2,1,0:T(8,128)(2,1)S(1)}, u32[]{:S(2)}, u32[]{:S(2)}) collective-permute-start(bf16[2,64,384]{2,1,0:T(8,128)(2,1)S(1)} %get-tuple-element.72), channel_id=1, source_target_pairs={{1,0},{3,2},{14,1},{13,3},{5,16},{7,18},{10,17},{9,19}} | collective-permute-start | bytes 294920 | tf_op jit(solution)/shard_map/ppermute | solution.py:232
  5.0 1.3 %collective-permute-start = (bf16[2,64,384]{2,1,0:T(8,128)(2,1)S(1)}, bf16[2,64,384]{2,1,0:T(8,128)(2,1)S(1)}, u32[]{:S(2)}, u32[]{:S(2)}) collective-permute-start(bf16[2,64,384]{2,1,0:T(8,128)(2,1)S(1)} %get-tuple-element.71), channel_id=1, source_target_pairs={{22,0},{21,2},{24,1},{26,3},{30,16},{29,18},{16,17},{18,19}} | collective-permute-start | bytes 294920 | tf_op jit(solution)/shard_map/ppermute | solution.py:232
  6.3 3.2 %collective-permute-start.1 = (bf16[2,64,384]{2,1,0:T(8,128)(2,1)S(1)}, bf16[2,64,384]{2,1,0:T(8,128)(2,1)S(1)}, u32[]{:S(2)}, u32[]{:S(2)}) collective-permute-start(bf16[2,64,384]{2,1,0:T(8,128)(2,1)S(1)} %get-tuple-element.72), channel_id=1, source_target_pairs={{21,0},{23,2},{26,1},{25,3},{17,16},{19,18},{30,17},{29,19}} | collective-permute-start | bytes 294920 | tf_op jit(solution)/shard_map/ppermute | solution.py:232
  9.5 3.4 %loader.1 = (bf16[3456,384]{1,0:T(8,128)(2,1)S(1)}, bf16[3456,768]{1,0:T(8,128)(2,1)S(1)}, f32[1,384]{1,0:T(1,128)S(1)}, f32[1,384]{1,0:T(1,128)S(1)}) custom-call(bf16[3,3456,384]{2,1,0:T(8,128)(2,1)} %bitcast.3, f32[1,384]{1,0:T(1,128)} %bias.1, f32[1,384]{1,0:T(1,128)} %gain.1), custom_call_target="tpu_custom_call" | custom-call | tf_op jit(solution)/shard_map/loader/pallas_call | solution.py:249
  13.0 1.2 %frame.16 = (bf16[176,384]{1,0:T(8,128)(2,1)S(1)}, bf16[224,1152]{1,0:T(8,128)(2,1)S(1)}) custom-call(bf16[2,64,384]{2,1,0:T(8,128)(2,1)S(1)} %collective-permute-done.3.refs_0_.refs_4_, bf16[2,64,384]{2,1,0:T(8,128)(2,1)S(1)} %collective-permute-done.4.refs_1_.refs_5_, bf16[2,64,384]{2,1,0:T(8,128)(2,1)S(1)} %get-tuple-element.73.refs_2_, ...), custom_call_target="tpu_custom_call" | custom-call | bytes 1024 | tf_op jit(solution)/shard_map/frame/pallas_call | solution.py:339
  14.1 5.2 %collective-permute-start.8 = (bf16[176,384]{1,0:T(8,128)(2,1)S(1)}, bf16[176,384]{1,0:T(8,128)(2,1)S(1)}, u32[]{:S(2)}, u32[]{:S(2)}) collective-permute-start(bf16[176,384]{1,0:T(8,128)(2,1)S(1)} %get-tuple-element.89), channel_id=1, source_target_pairs={{0,4},{1,5},{2,6},{3,7},{16,20},{17,21},{18,22},{19,23}} | collective-permute-start | bytes 405512 | tf_op jit(solution)/shard_map/ppermute | solution.py:355
  19.3 1.2 %history.12 = (f32[176,384]{1,0:T(8,128)S(1)}, f32[176,384]{1,0:T(8,128)S(1)}) custom-call(bf16[224,1152]{1,0:T(8,128)(2,1)S(1)} %get-tuple-element.78.spread, f32[176,384]{1,0:T(8,128)S(1)} %broadcast_1_refs_4__near_far.2.refs_4_.near, f32[176,384]{1,0:T(8,128)S(1)} %broadcast_1_refs_4__near_far.2.clone.far, ...), custom_call_target="tpu_custom_call", output_to_operand_aliasing={{0}: (1, {}), {1}: (2, {})} | custom-call | bytes 1024 | tf_op jit(solution)/shard_map/history/pallas_call | solution.py:370
  20.6 1.2 %frame.17 = (bf16[176,384]{1,0:T(8,128)(2,1)S(1)}, bf16[224,1152]{1,0:T(8,128)(2,1)S(1)}) custom-call(bf16[2,64,384]{2,1,0:T(8,128)(2,1)S(1)} %collective-permute-done.3.refs_0_.refs_4_, bf16[2,64,384]{2,1,0:T(8,128)(2,1)S(1)} %collective-permute-done.4.refs_1_.refs_5_, bf16[2,64,384]{2,1,0:T(8,128)(2,1)S(1)} %get-tuple-element.73.refs_2_, ...), custom_call_target="tpu_custom_call" | custom-call | bytes 1024 | tf_op jit(solution)/shard_map/frame/pallas_call | solution.py:339
  21.8 1.3 %collective-permute-start.7 = (bf16[176,384]{1,0:T(8,128)(2,1)S(1)}, bf16[176,384]{1,0:T(8,128)(2,1)S(1)}, u32[]{:S(2)}, u32[]{:S(2)}) collective-permute-start(bf16[176,384]{1,0:T(8,128)(2,1)S(1)} %get-tuple-element.88), channel_id=1, source_target_pairs={{0,4},{1,5},{2,6},{3,7},{16,20},{17,21},{18,22},{19,23}} | collective-permute-start | bytes 405512 | tf_op jit(solution)/shard_map/ppermute | solution.py:355
  23.1 1.2 %history.13 = (f32[176,384]{1,0:T(8,128)S(1)}, f32[176,384]{1,0:T(8,128)S(1)}) custom-call(bf16[224,1152]{1,0:T(8,128)(2,1)S(1)} %get-tuple-element.81.spread, f32[176,384]{1,0:T(8,128)S(1)} %get-tuple-element.80.refs_4_.near, f32[176,384]{1,0:T(8,128)S(1)} %get-tuple-element.82.far, ...), custom_call_target="tpu_custom_call", output_to_operand_aliasing={{0}: (1, {}), {1}: (2, {})} | custom-call | bytes 1024 | tf_op jit(solution)/shard_map/history/pallas_call | solution.py:370
  24.3 1.2 %frame.18 = (bf16[176,384]{1,0:T(8,128)(2,1)S(1)}, bf16[224,1152]{1,0:T(8,128)(2,1)S(1)}) custom-call(bf16[2,64,384]{2,1,0:T(8,128)(2,1)S(1)} %collective-permute-done.refs_0_, bf16[2,64,384]{2,1,0:T(8,128)(2,1)S(1)} %collective-permute-done.1.refs_1_, bf16[2,64,384]{2,1,0:T(8,128)(2,1)S(1)} %get-tuple-element.73.refs_2_, ...), custom_call_target="tpu_custom_call" | custom-call | bytes 1024 | tf_op jit(solution)/shard_map/frame/pallas_call | solution.py:339
  25.5 1.3 %collective-permute-start.6 = (bf16[176,384]{1,0:T(8,128)(2,1)S(1)}, bf16[176,384]{1,0:T(8,128)(2,1)S(1)}, u32[]{:S(2)}, u32[]{:S(2)}) collective-permute-start(bf16[176,384]{1,0:T(8,128)(2,1)S(1)} %get-tuple-element.87), channel_id=1, source_target_pairs={{0,4},{1,5},{2,6},{3,7},{16,20},{17,21},{18,22},{19,23}} | collective-permute-start | bytes 405512 | tf_op jit(solution)/shard_map/ppermute | solution.py:355
  26.8 0.8 %history.14 = (f32[176,384]{1,0:T(8,128)S(1)}, f32[176,384]{1,0:T(8,128)S(1)}) custom-call(bf16[224,1152]{1,0:T(8,128)(2,1)S(1)} %get-tuple-element.84.spread, f32[176,384]{1,0:T(8,128)S(1)} %get-tuple-element.83.refs_6_.near, f32[176,384]{1,0:T(8,128)S(1)} %get-tuple-element.85.far, ...), custom_call_target="tpu_custom_call", output_to_operand_aliasing={{0}: (1, {}), {1}: (2, {})} | custom-call | bytes 1024 | tf_op jit(solution)/shard_map/history/pallas_call | solution.py:370
  27.6 1.2 %frame.19 = bf16[176,384]{1,0:T(8,128)(2,1)S(1)} custom-call(bf16[2,64,384]{2,1,0:T(8,128)(2,1)S(1)} %collective-permute-done.refs_0_, bf16[2,64,384]{2,1,0:T(8,128)(2,1)S(1)} %collective-permute-done.1.refs_1_, bf16[2,64,384]{2,1,0:T(8,128)(2,1)S(1)} %get-tuple-element.73.refs_2_, bf16[2,64,384]{2,1,0:T(8,128)(2,1)S(1)} %collective-permute-done.2.refs_3_, ...), custom_call_target="tpu_custom_call" | custom-call | bytes 1024 | tf_op jit(solution)/shard_map/frame/pallas_call | solution.py:339
  28.8 1.3 %collective-permute-start.5 = (bf16[176,384]{1,0:T(8,128)(2,1)S(1)}, bf16[176,384]{1,0:T(8,128)(2,1)S(1)}, u32[]{:S(2)}, u32[]{:S(2)}) collective-permute-start(bf16[176,384]{1,0:T(8,128)(2,1)S(1)} %frame.19), channel_id=1, source_target_pairs={{0,4},{1,5},{2,6},{3,7},{16,20},{17,21},{18,22},{19,23}} | collective-permute-start | bytes 405512 | tf_op jit(solution)/shard_map/ppermute | solution.py:355
  30.2 0.7 %collective-permute-start.12 = (bf16[160,384]{1,0:T(8,128)(2,1)S(1)}, bf16[160,384]{1,0:T(8,128)(2,1)S(1)}, u32[]{:S(2)}, u32[]{:S(2)}) collective-permute-start(bf16[160,384]{1,0:T(8,128)(2,1)S(1)} %get-tuple-element.101), channel_id=1, source_target_pairs={{4,8},{5,9},{6,10},{7,11},{20,24},{21,25},{22,26},{23,27}} | collective-permute-start | bytes 368648 | tf_op jit(solution)/shard_map/ppermute | solution.py:355
  30.9 0.7 %collective-permute-start.11 = (bf16[160,384]{1,0:T(8,128)(2,1)S(1)}, bf16[160,384]{1,0:T(8,128)(2,1)S(1)}, u32[]{:S(2)}, u32[]{:S(2)}) collective-permute-start(bf16[160,384]{1,0:T(8,128)(2,1)S(1)} %get-tuple-element.100), channel_id=1, source_target_pairs={{4,8},{5,9},{6,10},{7,11},{20,24},{21,25},{22,26},{23,27}} | collective-permute-start | bytes 368648 | tf_op jit(solution)/shard_map/ppermute | solution.py:355
  31.8 0.7 %collective-permute-start.10 = (bf16[160,384]{1,0:T(8,128)(2,1)S(1)}, bf16[160,384]{1,0:T(8,128)(2,1)S(1)}, u32[]{:S(2)}, u32[]{:S(2)}) collective-permute-start(bf16[160,384]{1,0:T(8,128)(2,1)S(1)} %get-tuple-element.99), channel_id=1, source_target_pairs={{4,8},{5,9},{6,10},{7,11},{20,24},{21,25},{22,26},{23,27}} | collective-permute-start | bytes 368648 | tf_op jit(solution)/shard_map/ppermute | solution.py:355
  32.5 0.7 %collective-permute-done.5.refs_0_ = bf16[176,384]{1,0:T(8,128)(2,1)S(1)} collective-permute-done((bf16[176,384]{1,0:T(8,128)(2,1)S(1)}, bf16[176,384]{1,0:T(8,128)(2,1)S(1)}, u32[]{:S(2)}, u32[]{:S(2)}) %collective-permute-start.5) | collective-permute-done | bytes 135200 | tf_op jit(solution)/shard_map/ppermute | solution.py:355
  34.0 0.7 %collective-permute-start.16 = (bf16[144,384]{1,0:T(8,128)(2,1)S(1)}, bf16[144,384]{1,0:T(8,128)(2,1)S(1)}, u32[]{:S(2)}, u32[]{:S(2)}) collective-permute-start(bf16[144,384]{1,0:T(8,128)(2,1)S(1)} %get-tuple-element.113), channel_id=1, source_target_pairs={{8,12},{9,13},{10,14},{11,15},{24,28},{25,29},{26,30},{27,31}} | collective-permute-start | bytes 331784 | tf_op jit(solution)/shard_map/ppermute | solution.py:355
  34.7 0.7 %collective-permute-start.15 = (bf16[144,384]{1,0:T(8,128)(2,1)S(1)}, bf16[144,384]{1,0:T(8,128)(2,1)S(1)}, u32[]{:S(2)}, u32[]{:S(2)}) collective-permute-start(bf16[144,384]{1,0:T(8,128)(2,1)S(1)} %get-tuple-element.112), channel_id=1, source_target_pairs={{8,12},{9,13},{10,14},{11,15},{24,28},{25,29},{26,30},{27,31}} | collective-permute-start | bytes 331784 | tf_op jit(solution)/shard_map/ppermute | solution.py:355
  35.5 0.7 %collective-permute-start.14 = (bf16[144,384]{1,0:T(8,128)(2,1)S(1)}, bf16[144,384]{1,0:T(8,128)(2,1)S(1)}, u32[]{:S(2)}, u32[]{:S(2)}) collective-permute-start(bf16[144,384]{1,0:T(8,128)(2,1)S(1)} %get-tuple-element.111), channel_id=1, source_target_pairs={{8,12},{9,13},{10,14},{11,15},{24,28},{25,29},{26,30},{27,31}} | collective-permute-start | bytes 331784 | tf_op jit(solution)/shard_map/ppermute | solution.py:355
  36.2 0.7 %collective-permute-start.13 = (bf16[144,384]{1,0:T(8,128)(2,1)S(1)}, bf16[144,384]{1,0:T(8,128)(2,1)S(1)}, u32[]{:S(2)}, u32[]{:S(2)}) collective-permute-start(bf16[144,384]{1,0:T(8,128)(2,1)S(1)} %frame.27), channel_id=1, source_target_pairs={{8,12},{9,13},{10,14},{11,15},{24,28},{25,29},{26,30},{27,31}} | collective-permute-start | bytes 331784 | tf_op jit(solution)/shard_map/ppermute | solution.py:355
  37.0 0.7 %collective-permute-start.17 = (bf16[2,64,384]{2,1,0:T(8,128)(2,1)S(1)}, bf16[2,64,384]{2,1,0:T(8,128)(2,1)S(1)}, u32[]{:S(2)}, u32[]{:S(2)}) collective-permute-start(bf16[2,64,384]{2,1,0:T(8,128)(2,1)S(1)} %get-tuple-element.129), channel_id=1, source_target_pairs={{12,0},{14,2},{13,4},{15,6}} | collective-permute-start | bytes 294920 | tf_op jit(solution)/shard_map/ppermute | solution.py:271
  37.7 0.7 %collective-permute-start.18 = (bf16[2,64,384]{2,1,0:T(8,128)(2,1)S(1)}, bf16[2,64,384]{2,1,0:T(8,128)(2,1)S(1)}, u32[]{:S(2)}, u32[]{:S(2)}) collective-permute-start(bf16[2,64,384]{2,1,0:T(8,128)(2,1)S(1)} %get-tuple-element.130), channel_id=1, source_target_pairs={{12,1},{14,3},{13,5},{15,7}} | collective-permute-start | bytes 294920 | tf_op jit(solution)/shard_map/ppermute | solution.py:271
  38.6 0.7 %collective-permute-start.19 = (bf16[2,64,384]{2,1,0:T(8,128)(2,1)S(1)}, bf16[2,64,384]{2,1,0:T(8,128)(2,1)S(1)}, u32[]{:S(2)}, u32[]{:S(2)}) collective-permute-start(bf16[2,64,384]{2,1,0:T(8,128)(2,1)S(1)} %get-tuple-element.133), channel_id=1, source_target_pairs={{28,8},{30,10},{29,12},{31,14}} | collective-permute-start | bytes 294920 | tf_op jit(solution)/shard_map/ppermute | solution.py:271
  39.3 0.7 %collective-permute-start.20 = (bf16[2,64,384]{2,1,0:T(8,128)(2,1)S(1)}, bf16[2,64,384]{2,1,0:T(8,128)(2,1)S(1)}, u32[]{:S(2)}, u32[]{:S(2)}) collective-permute-start(bf16[2,64,384]{2,1,0:T(8,128)(2,1)S(1)} %get-tuple-element.134), channel_id=1, source_target_pairs={{28,9},{30,11},{29,13},{31,15}} | collective-permute-start | bytes 294920 | tf_op jit(solution)/shard_map/ppermute | solution.py:271
  40.8 1.3 %collective-permute-start.22 = (bf16[2,64,384]{2,1,0:T(8,128)(2,1)S(1)}, bf16[2,64,384]{2,1,0:T(8,128)(2,1)S(1)}, u32[]{:S(2)}, u32[]{:S(2)}) collective-permute-start(bf16[2,64,384]{2,1,0:T(8,128)(2,1)S(1)} %get-tuple-element.136), channel_id=1, source_target_pairs={{12,17},{14,19},{13,21},{15,23},{28,25},{30,27},{29,29},{31,31}} | collective-permute-start | bytes 294920 | tf_op jit(solution)/shard_map/ppermute | solution.py:271
  42.1 13.4 %collective-permute-done.22.refs_5_ = bf16[2,64,384]{2,1,0:T(8,128)(2,1)S(1)} collective-permute-done((bf16[2,64,384]{2,1,0:T(8,128)(2,1)S(1)}, bf16[2,64,384]{2,1,0:T(8,128)(2,1)S(1)}, u32[]{:S(2)}, u32[]{:S(2)}) %collective-permute-start.22) | collective-permute-done | bytes 98336 | tf_op jit(solution)/shard_map/ppermute | solution.py:271
  (47 shorter events, 2.9 us)
Async XLA Ops:
  1.1 11.8 %collective-permute-start.2 = (bf16[2,64,384]{2,1,0:T(8,128)(2,1)S(1)}, bf16[2,64,384]{2,1,0:T(8,128)(2,1)S(1)}, u32[]{:S(2)}, u32[]{:S(2)}) collective-permute-start(bf16[2,64,384]{2,1,0:T(8,128)(2,1)S(1)} %get-tuple-element.74), channel_id=1, source_target_pairs={{0,16},{2,18},{1,17},{3,19},{20,0},{22,2},{21,1},{23,3}} | collective-permute-start | bytes 294920 | tf_op jit(solution)/shard_map/ppermute | solution.py:232
  2.4 10.6 %collective-permute-start.3 = (bf16[2,64,384]{2,1,0:T(8,128)(2,1)S(1)}, bf16[2,64,384]{2,1,0:T(8,128)(2,1)S(1)}, u32[]{:S(2)}, u32[]{:S(2)}) collective-permute-start(bf16[2,64,384]{2,1,0:T(8,128)(2,1)S(1)} %get-tuple-element.71), channel_id=1, source_target_pairs={{14,0},{13,2},{0,1},{2,3},{6,16},{5,18},{8,17},{10,19}} | collective-permute-start | bytes 294920 | tf_op jit(solution)/shard_map/ppermute | solution.py:232
  3.7 9.3 %collective-permute-start.4 = (bf16[2,64,384]{2,1,0:T(8,128)(2,1)S(1)}, bf16[2,64,384]{2,1,0:T(8,128)(2,1)S(1)}, u32[]{:S(2)}, u32[]{:S(2)}) collective-permute-start(bf16[2,64,384]{2,1,0:T(8,128)(2,1)S(1)} %get-tuple-element.72), channel_id=1, source_target_pairs={{1,0},{3,2},{14,1},{13,3},{5,16},{7,18},{10,17},{9,19}} | collective-permute-start | bytes 294920 | tf_op jit(solution)/shard_map/ppermute | solution.py:232
  5.0 19.3 %collective-permute-start = (bf16[2,64,384]{2,1,0:T(8,128)(2,1)S(1)}, bf16[2,64,384]{2,1,0:T(8,128)(2,1)S(1)}, u32[]{:S(2)}, u32[]{:S(2)}) collective-permute-start(bf16[2,64,384]{2,1,0:T(8,128)(2,1)S(1)} %get-tuple-element.71), channel_id=1, source_target_pairs={{22,0},{21,2},{24,1},{26,3},{30,16},{29,18},{16,17},{18,19}} | collective-permute-start | bytes 294920 | tf_op jit(solution)/shard_map/ppermute | solution.py:232
  6.3 18.0 %collective-permute-start.1 = (bf16[2,64,384]{2,1,0:T(8,128)(2,1)S(1)}, bf16[2,64,384]{2,1,0:T(8,128)(2,1)S(1)}, u32[]{:S(2)}, u32[]{:S(2)}) collective-permute-start(bf16[2,64,384]{2,1,0:T(8,128)(2,1)S(1)} %get-tuple-element.72), channel_id=1, source_target_pairs={{21,0},{23,2},{26,1},{25,3},{17,16},{19,18},{30,17},{29,19}} | collective-permute-start | bytes 294920 | tf_op jit(solution)/shard_map/ppermute | solution.py:232
  14.1 16.0 %collective-permute-start.8 = (bf16[176,384]{1,0:T(8,128)(2,1)S(1)}, bf16[176,384]{1,0:T(8,128)(2,1)S(1)}, u32[]{:S(2)}, u32[]{:S(2)}) collective-permute-start(bf16[176,384]{1,0:T(8,128)(2,1)S(1)} %get-tuple-element.89), channel_id=1, source_target_pairs={{0,4},{1,5},{2,6},{3,7},{16,20},{17,21},{18,22},{19,23}} | collective-permute-start | bytes 405512 | tf_op jit(solution)/shard_map/ppermute | solution.py:355
  21.8 9.1 %collective-permute-start.7 = (bf16[176,384]{1,0:T(8,128)(2,1)S(1)}, bf16[176,384]{1,0:T(8,128)(2,1)S(1)}, u32[]{:S(2)}, u32[]{:S(2)}) collective-permute-start(bf16[176,384]{1,0:T(8,128)(2,1)S(1)} %get-tuple-element.88), channel_id=1, source_target_pairs={{0,4},{1,5},{2,6},{3,7},{16,20},{17,21},{18,22},{19,23}} | collective-permute-start | bytes 405512 | tf_op jit(solution)/shard_map/ppermute | solution.py:355
  25.5 6.1 %collective-permute-start.6 = (bf16[176,384]{1,0:T(8,128)(2,1)S(1)}, bf16[176,384]{1,0:T(8,128)(2,1)S(1)}, u32[]{:S(2)}, u32[]{:S(2)}) collective-permute-start(bf16[176,384]{1,0:T(8,128)(2,1)S(1)} %get-tuple-element.87), channel_id=1, source_target_pairs={{0,4},{1,5},{2,6},{3,7},{16,20},{17,21},{18,22},{19,23}} | collective-permute-start | bytes 405512 | tf_op jit(solution)/shard_map/ppermute | solution.py:355
  28.8 4.5 %collective-permute-start.5 = (bf16[176,384]{1,0:T(8,128)(2,1)S(1)}, bf16[176,384]{1,0:T(8,128)(2,1)S(1)}, u32[]{:S(2)}, u32[]{:S(2)}) collective-permute-start(bf16[176,384]{1,0:T(8,128)(2,1)S(1)} %frame.19), channel_id=1, source_target_pairs={{0,4},{1,5},{2,6},{3,7},{16,20},{17,21},{18,22},{19,23}} | collective-permute-start | bytes 405512 | tf_op jit(solution)/shard_map/ppermute | solution.py:355
  30.2 3.8 %collective-permute-start.12 = (bf16[160,384]{1,0:T(8,128)(2,1)S(1)}, bf16[160,384]{1,0:T(8,128)(2,1)S(1)}, u32[]{:S(2)}, u32[]{:S(2)}) collective-permute-start(bf16[160,384]{1,0:T(8,128)(2,1)S(1)} %get-tuple-element.101), channel_id=1, source_target_pairs={{4,8},{5,9},{6,10},{7,11},{20,24},{21,25},{22,26},{23,27}} | collective-permute-start | bytes 368648 | tf_op jit(solution)/shard_map/ppermute | solution.py:355
  30.9 3.8 %collective-permute-start.11 = (bf16[160,384]{1,0:T(8,128)(2,1)S(1)}, bf16[160,384]{1,0:T(8,128)(2,1)S(1)}, u32[]{:S(2)}, u32[]{:S(2)}) collective-permute-start(bf16[160,384]{1,0:T(8,128)(2,1)S(1)} %get-tuple-element.100), channel_id=1, source_target_pairs={{4,8},{5,9},{6,10},{7,11},{20,24},{21,25},{22,26},{23,27}} | collective-permute-start | bytes 368648 | tf_op jit(solution)/shard_map/ppermute | solution.py:355
  31.8 3.6 %collective-permute-start.10 = (bf16[160,384]{1,0:T(8,128)(2,1)S(1)}, bf16[160,384]{1,0:T(8,128)(2,1)S(1)}, u32[]{:S(2)}, u32[]{:S(2)}) collective-permute-start(bf16[160,384]{1,0:T(8,128)(2,1)S(1)} %get-tuple-element.99), channel_id=1, source_target_pairs={{4,8},{5,9},{6,10},{7,11},{20,24},{21,25},{22,26},{23,27}} | collective-permute-start | bytes 368648 | tf_op jit(solution)/shard_map/ppermute | solution.py:355
  33.3 2.9 %collective-permute-start.9 = (bf16[160,384]{1,0:T(8,128)(2,1)S(1)}, bf16[160,384]{1,0:T(8,128)(2,1)S(1)}, u32[]{:S(2)}, u32[]{:S(2)}) collective-permute-start(bf16[160,384]{1,0:T(8,128)(2,1)S(1)} %frame.23), channel_id=1, source_target_pairs={{4,8},{5,9},{6,10},{7,11},{20,24},{21,25},{22,26},{23,27}} | collective-permute-start | bytes 368648 | tf_op jit(solution)/shard_map/ppermute | solution.py:355
  34.0 2.9 %collective-permute-start.16 = (bf16[144,384]{1,0:T(8,128)(2,1)S(1)}, bf16[144,384]{1,0:T(8,128)(2,1)S(1)}, u32[]{:S(2)}, u32[]{:S(2)}) collective-permute-start(bf16[144,384]{1,0:T(8,128)(2,1)S(1)} %get-tuple-element.113), channel_id=1, source_target_pairs={{8,12},{9,13},{10,14},{11,15},{24,28},{25,29},{26,30},{27,31}} | collective-permute-start | bytes 331784 | tf_op jit(solution)/shard_map/ppermute | solution.py:355
  34.7 2.2 %collective-permute-start.15 = (bf16[144,384]{1,0:T(8,128)(2,1)S(1)}, bf16[144,384]{1,0:T(8,128)(2,1)S(1)}, u32[]{:S(2)}, u32[]{:S(2)}) collective-permute-start(bf16[144,384]{1,0:T(8,128)(2,1)S(1)} %get-tuple-element.112), channel_id=1, source_target_pairs={{8,12},{9,13},{10,14},{11,15},{24,28},{25,29},{26,30},{27,31}} | collective-permute-start | bytes 331784 | tf_op jit(solution)/shard_map/ppermute | solution.py:355
  35.5 3.1 %collective-permute-start.14 = (bf16[144,384]{1,0:T(8,128)(2,1)S(1)}, bf16[144,384]{1,0:T(8,128)(2,1)S(1)}, u32[]{:S(2)}, u32[]{:S(2)}) collective-permute-start(bf16[144,384]{1,0:T(8,128)(2,1)S(1)} %get-tuple-element.111), channel_id=1, source_target_pairs={{8,12},{9,13},{10,14},{11,15},{24,28},{25,29},{26,30},{27,31}} | collective-permute-start | bytes 331784 | tf_op jit(solution)/shard_map/ppermute | solution.py:355
  36.2 3.8 %collective-permute-start.13 = (bf16[144,384]{1,0:T(8,128)(2,1)S(1)}, bf16[144,384]{1,0:T(8,128)(2,1)S(1)}, u32[]{:S(2)}, u32[]{:S(2)}) collective-permute-start(bf16[144,384]{1,0:T(8,128)(2,1)S(1)} %frame.27), channel_id=1, source_target_pairs={{8,12},{9,13},{10,14},{11,15},{24,28},{25,29},{26,30},{27,31}} | collective-permute-start | bytes 331784 | tf_op jit(solution)/shard_map/ppermute | solution.py:355
  37.0 3.0 %collective-permute-start.17 = (bf16[2,64,384]{2,1,0:T(8,128)(2,1)S(1)}, bf16[2,64,384]{2,1,0:T(8,128)(2,1)S(1)}, u32[]{:S(2)}, u32[]{:S(2)}) collective-permute-start(bf16[2,64,384]{2,1,0:T(8,128)(2,1)S(1)} %get-tuple-element.129), channel_id=1, source_target_pairs={{12,0},{14,2},{13,4},{15,6}} | collective-permute-start | bytes 294920 | tf_op jit(solution)/shard_map/ppermute | solution.py:271
  37.7 2.4 %collective-permute-start.18 = (bf16[2,64,384]{2,1,0:T(8,128)(2,1)S(1)}, bf16[2,64,384]{2,1,0:T(8,128)(2,1)S(1)}, u32[]{:S(2)}, u32[]{:S(2)}) collective-permute-start(bf16[2,64,384]{2,1,0:T(8,128)(2,1)S(1)} %get-tuple-element.130), channel_id=1, source_target_pairs={{12,1},{14,3},{13,5},{15,7}} | collective-permute-start | bytes 294920 | tf_op jit(solution)/shard_map/ppermute | solution.py:271
  38.6 3.4 %collective-permute-start.19 = (bf16[2,64,384]{2,1,0:T(8,128)(2,1)S(1)}, bf16[2,64,384]{2,1,0:T(8,128)(2,1)S(1)}, u32[]{:S(2)}, u32[]{:S(2)}) collective-permute-start(bf16[2,64,384]{2,1,0:T(8,128)(2,1)S(1)} %get-tuple-element.133), channel_id=1, source_target_pairs={{28,8},{30,10},{29,12},{31,14}} | collective-permute-start | bytes 294920 | tf_op jit(solution)/shard_map/ppermute | solution.py:271
  39.3 2.8 %collective-permute-start.20 = (bf16[2,64,384]{2,1,0:T(8,128)(2,1)S(1)}, bf16[2,64,384]{2,1,0:T(8,128)(2,1)S(1)}, u32[]{:S(2)}, u32[]{:S(2)}) collective-permute-start(bf16[2,64,384]{2,1,0:T(8,128)(2,1)S(1)} %get-tuple-element.134), channel_id=1, source_target_pairs={{28,9},{30,11},{29,13},{31,15}} | collective-permute-start | bytes 294920 | tf_op jit(solution)/shard_map/ppermute | solution.py:271
  40.1 2.0 %collective-permute-start.21 = (bf16[2,64,384]{2,1,0:T(8,128)(2,1)S(1)}, bf16[2,64,384]{2,1,0:T(8,128)(2,1)S(1)}, u32[]{:S(2)}, u32[]{:S(2)}) collective-permute-start(bf16[2,64,384]{2,1,0:T(8,128)(2,1)S(1)} %get-tuple-element.135), channel_id=1, source_target_pairs={{12,16},{14,18},{13,20},{15,22},{28,24},{30,26},{29,28},{31,30}} | collective-permute-start | bytes 294920 | tf_op jit(solution)/shard_map/ppermute | solution.py:271
  40.8 14.8 %collective-permute-start.22 = (bf16[2,64,384]{2,1,0:T(8,128)(2,1)S(1)}, bf16[2,64,384]{2,1,0:T(8,128)(2,1)S(1)}, u32[]{:S(2)}, u32[]{:S(2)}) collective-permute-start(bf16[2,64,384]{2,1,0:T(8,128)(2,1)S(1)} %get-tuple-element.136), channel_id=1, source_target_pairs={{12,17},{14,19},{13,21},{15,23},{28,25},{30,27},{29,29},{31,31}} | collective-permute-start | bytes 294920 | tf_op jit(solution)/shard_map/ppermute | solution.py:271

commit v18 on v11

--- a/solution.py
+++ b/solution.py
@@ -39,11 +39,11 @@
 
 def sent_clips(side, lane, segment, choose):
     near, far = 2 * side, 2 - 2 * side
-    behind = far + ((segment - 1) & 1)
+    behind = far + (segment & 1)
     return (
         far + lane,
-        choose(segment == 0, near + 1, choose(segment == 3, near, behind)),
-        choose(segment == 0, near, choose(segment == 3, near + 1, behind)),
+        choose(segment == 0, near + 1, choose(segment == 1, near, behind)),
+        choose(segment == 0, near, choose(segment == 1, near + 1, behind)),
     )
 
 
@@ -205,9 +205,9 @@
             if number == 0:
                 segment = t if t < holders else 1
             elif there == side:
-                segment = 3 if lane == number - 1 else 0
+                segment = 1 if lane == number - 1 else 0
             else:
-                segment = 1 + lane
+                segment = 2 + lane
             for h in range(HALVES):
                 at = stream(clip, h)[1]
                 source = wanted[number][at]

time: 55.1 us -> 55.4 us (level)
  the two profiles are of different devices: /device:TPU:18 before, /device:TPU:6 now
where the time goes in v18:
time: 55.4 us; the launch traced here: 54.9 us
  starting transfers between devices  22.2 us (40%)
  waiting for transfers between devices  18.1 us (33%)
  Pallas kernels  13.3 us (24%)
  other arithmetic  0.67 us (1%)
  between operations  0.6 us (1%)
    ppermute x6, waiting for transfers between devices, leave(): return lax.ppermute(value, MESH_AXES, routes)  14.2 us
    ppermute x12, starting transfers between devices, local(): lax.ppermute(out, 'segment', [(s, s + 1) for s in senders_now])  10.5 us
    ppermute x5, starting transfers between devices, gather(): return lax.ppermute(sources[number], MESH_AXES, routes)  7.09 us
    pallas_call x16, Pallas kernels, local(): pl.pallas_call(functools.partial(frame_kernel, cfg), out_shape=shapes, in...  5.05 us
    ppermute x6, starting transfers between devices, leave(): return lax.ppermute(value, MESH_AXES, routes)  4.63 us
    pallas_call x12, Pallas kernels, local(): pl.pallas_call(functools.partial(history_kernel, cfg), out_shape=[pltpu.V...  3.74 us
    pallas_call x1, Pallas kernels, local(): pl.pallas_call(loader_kernel, out_shape=[pltpu.VMEM((TAPS * TAPS * channe...  3.42 us
    ppermute x5, waiting for transfers between devices, gather(): return lax.ppermute(sources[number], MESH_AXES, routes)  2.97 us
  transfers between devices with their start and end apart: 23, of which 4 were waited for; matrix products, arithmetic and copies ran while one was open for 0% of the time, Pallas kernels for 22%

profile of v18, /device:TPU:6, one launch (start us, length us, event | category | flops | bytes accessed | tf_op | source)
XLA Modules:
  0.0 54.9 jit_solution(9661692048761191051)
XLA Ops:
  0.0 1.1 %pick.1 = (bf16[2,64,384]{2,1,0:T(8,128)(2,1)S(1)}, bf16[2,64,384]{2,1,0:T(8,128)(2,1)S(1)}, bf16[2,64,384]{2,1,0:T(8,128)(2,1)S(1)}, bf16[2,64,384]{2,1,0:T(8,128)(2,1)S(1)}) custom-call(bf16[4,2,64,384]{3,2,1,0:T(8,128)(2,1)} %bitcast.4), custom_call_target="tpu_custom_call" | custom-call | tf_op jit(solution)/shard_map/pick/pallas_call | solution.py:189
  1.1 1.3 %collective-permute-start.3 = (bf16[2,64,384]{2,1,0:T(8,128)(2,1)S(1)}, bf16[2,64,384]{2,1,0:T(8,128)(2,1)S(1)}, u32[]{:S(2)}, u32[]{:S(2)}) collective-permute-start(bf16[2,64,384]{2,1,0:T(8,128)(2,1)S(1)} %get-tuple-element.71), channel_id=1, source_target_pairs={{6,0},{5,2},{0,1},{2,3},{10,16},{9,18},{12,17},{14,19}} | collective-permute-start | bytes 294920 | tf_op jit(solution)/shard_map/ppermute | solution.py:217
  2.4 1.3 %collective-permute-start.4 = (bf16[2,64,384]{2,1,0:T(8,128)(2,1)S(1)}, bf16[2,64,384]{2,1,0:T(8,128)(2,1)S(1)}, u32[]{:S(2)}, u32[]{:S(2)}) collective-permute-start(bf16[2,64,384]{2,1,0:T(8,128)(2,1)S(1)} %get-tuple-element.72), channel_id=1, source_target_pairs={{1,0},{3,2},{6,1},{5,3},{9,16},{11,18},{14,17},{13,19}} | collective-permute-start | bytes 294920 | tf_op jit(solution)/shard_map/ppermute | solution.py:217
  3.7 1.3 %collective-permute-start.2 = (bf16[2,64,384]{2,1,0:T(8,128)(2,1)S(1)}, bf16[2,64,384]{2,1,0:T(8,128)(2,1)S(1)}, u32[]{:S(2)}, u32[]{:S(2)}) collective-permute-start(bf16[2,64,384]{2,1,0:T(8,128)(2,1)S(1)} %get-tuple-element.74), channel_id=1, source_target_pairs={{0,16},{2,18},{1,17},{3,19},{20,0},{22,2},{21,1},{23,3}} | collective-permute-start | bytes 294920 | tf_op jit(solution)/shard_map/ppermute | solution.py:217
  5.0 1.9 %collective-permute-start = (bf16[2,64,384]{2,1,0:T(8,128)(2,1)S(1)}, bf16[2,64,384]{2,1,0:T(8,128)(2,1)S(1)}, u32[]{:S(2)}, u32[]{:S(2)}) collective-permute-start(bf16[2,64,384]{2,1,0:T(8,128)(2,1)S(1)} %get-tuple-element.71), channel_id=1, source_target_pairs={{26,0},{25,2},{28,1},{30,3},{22,16},{21,18},{16,17},{18,19}} | collective-permute-start | bytes 294920 | tf_op jit(solution)/shard_map/ppermute | solution.py:217
  6.9 1.3 %collective-permute-start.1 = (bf16[2,64,384]{2,1,0:T(8,128)(2,1)S(1)}, bf16[2,64,384]{2,1,0:T(8,128)(2,1)S(1)}, u32[]{:S(2)}, u32[]{:S(2)}) collective-permute-start(bf16[2,64,384]{2,1,0:T(8,128)(2,1)S(1)} %get-tuple-element.72), channel_id=1, source_target_pairs={{25,0},{27,2},{30,1},{29,3},{17,16},{19,18},{22,17},{21,19}} | collective-permute-start | bytes 294920 | tf_op jit(solution)/shard_map/ppermute | solution.py:217
  8.2 3.4 %loader.1 = (bf16[3456,384]{1,0:T(8,128)(2,1)S(1)}, bf16[3456,768]{1,0:T(8,128)(2,1)S(1)}, f32[1,384]{1,0:T(1,128)S(1)}, f32[1,384]{1,0:T(1,128)S(1)}) custom-call(bf16[3,3456,384]{2,1,0:T(8,128)(2,1)} %bitcast.3, f32[1,384]{1,0:T(1,128)} %bias.1, f32[1,384]{1,0:T(1,128)} %gain.1), custom_call_target="tpu_custom_call" | custom-call | tf_op jit(solution)/shard_map/loader/pallas_call | solution.py:234
  11.6 1.3 %collective-permute-done.3.refs_0_.refs_4_ = bf16[2,64,384]{2,1,0:T(8,128)(2,1)S(1)} collective-permute-done((bf16[2,64,384]{2,1,0:T(8,128)(2,1)S(1)}, bf16[2,64,384]{2,1,0:T(8,128)(2,1)S(1)}, u32[]{:S(2)}, u32[]{:S(2)}) %collective-permute-start.3) | collective-permute-done | bytes 98336 | tf_op jit(solution)/shard_map/ppermute | solution.py:217
  12.9 1.7 %collective-permute-done.2.refs_3_ = bf16[2,64,384]{2,1,0:T(8,128)(2,1)S(1)} collective-permute-done((bf16[2,64,384]{2,1,0:T(8,128)(2,1)S(1)}, bf16[2,64,384]{2,1,0:T(8,128)(2,1)S(1)}, u32[]{:S(2)}, u32[]{:S(2)}) %collective-permute-start.2) | collective-permute-done | bytes 98336 | tf_op jit(solution)/shard_map/ppermute | solution.py:217
  14.6 1.2 %frame.16 = (bf16[176,384]{1,0:T(8,128)(2,1)S(1)}, bf16[224,1152]{1,0:T(8,128)(2,1)S(1)}) custom-call(bf16[2,64,384]{2,1,0:T(8,128)(2,1)S(1)} %collective-permute-done.3.refs_0_.refs_4_, bf16[2,64,384]{2,1,0:T(8,128)(2,1)S(1)} %collective-permute-done.4.refs_1_.refs_5_, bf16[2,64,384]{2,1,0:T(8,128)(2,1)S(1)} %get-tuple-element.73.refs_2_, ...), custom_call_target="tpu_custom_call" | custom-call | bytes 1024 | tf_op jit(solution)/shard_map/frame/pallas_call | solution.py:324
  15.8 1.3 %collective-permute-start.8 = (bf16[176,384]{1,0:T(8,128)(2,1)S(1)}, bf16[176,384]{1,0:T(8,128)(2,1)S(1)}, u32[]{:S(2)}, u32[]{:S(2)}) collective-permute-start(bf16[176,384]{1,0:T(8,128)(2,1)S(1)} %get-tuple-element.89), channel_id=1, source_target_pairs={{0,4},{1,5},{2,6},{3,7},{16,20},{17,21},{18,22},{19,23}} | collective-permute-start | bytes 405512 | tf_op jit(solution)/shard_map/ppermute | solution.py:340
  17.1 1.2 %history.12 = (f32[176,384]{1,0:T(8,128)S(1)}, f32[176,384]{1,0:T(8,128)S(1)}) custom-call(bf16[224,1152]{1,0:T(8,128)(2,1)S(1)} %get-tuple-element.78.spread, f32[176,384]{1,0:T(8,128)S(1)} %broadcast_1_refs_4__near_far.2.refs_4_.near, f32[176,384]{1,0:T(8,128)S(1)} %broadcast_1_refs_4__near_far.2.clone.far, ...), custom_call_target="tpu_custom_call", output_to_operand_aliasing={{0}: (1, {}), {1}: (2, {})} | custom-call | bytes 1024 | tf_op jit(solution)/shard_map/history/pallas_call | solution.py:355
  18.4 1.2 %frame.17 = (bf16[176,384]{1,0:T(8,128)(2,1)S(1)}, bf16[224,1152]{1,0:T(8,128)(2,1)S(1)}) custom-call(bf16[2,64,384]{2,1,0:T(8,128)(2,1)S(1)} %collective-permute-done.3.refs_0_.refs_4_, bf16[2,64,384]{2,1,0:T(8,128)(2,1)S(1)} %collective-permute-done.4.refs_1_.refs_5_, bf16[2,64,384]{2,1,0:T(8,128)(2,1)S(1)} %get-tuple-element.73.refs_2_, ...), custom_call_target="tpu_custom_call" | custom-call | bytes 1024 | tf_op jit(solution)/shard_map/frame/pallas_call | solution.py:324
  19.5 1.3 %collective-permute-start.7 = (bf16[176,384]{1,0:T(8,128)(2,1)S(1)}, bf16[176,384]{1,0:T(8,128)(2,1)S(1)}, u32[]{:S(2)}, u32[]{:S(2)}) collective-permute-start(bf16[176,384]{1,0:T(8,128)(2,1)S(1)} %get-tuple-element.88), channel_id=1, source_target_pairs={{0,4},{1,5},{2,6},{3,7},{16,20},{17,21},{18,22},{19,23}} | collective-permute-start | bytes 405512 | tf_op jit(solution)/shard_map/ppermute | solution.py:340
  20.8 1.2 %history.13 = (f32[176,384]{1,0:T(8,128)S(1)}, f32[176,384]{1,0:T(8,128)S(1)}) custom-call(bf16[224,1152]{1,0:T(8,128)(2,1)S(1)} %get-tuple-element.81.spread, f32[176,384]{1,0:T(8,128)S(1)} %get-tuple-element.80.refs_4_.near, f32[176,384]{1,0:T(8,128)S(1)} %get-tuple-element.82.far, ...), custom_call_target="tpu_custom_call", output_to_operand_aliasing={{0}: (1, {}), {1}: (2, {})} | custom-call | bytes 1024 | tf_op jit(solution)/shard_map/history/pallas_call | solution.py:355
  22.1 1.2 %frame.18 = (bf16[176,384]{1,0:T(8,128)(2,1)S(1)}, bf16[224,1152]{1,0:T(8,128)(2,1)S(1)}) custom-call(bf16[2,64,384]{2,1,0:T(8,128)(2,1)S(1)} %collective-permute-done.refs_0_, bf16[2,64,384]{2,1,0:T(8,128)(2,1)S(1)} %collective-permute-done.1.refs_1_, bf16[2,64,384]{2,1,0:T(8,128)(2,1)S(1)} %get-tuple-element.73.refs_2_, ...), custom_call_target="tpu_custom_call" | custom-call | bytes 1024 | tf_op jit(solution)/shard_map/frame/pallas_call | solution.py:324
  23.3 1.3 %collective-permute-start.6 = (bf16[176,384]{1,0:T(8,128)(2,1)S(1)}, bf16[176,384]{1,0:T(8,128)(2,1)S(1)}, u32[]{:S(2)}, u32[]{:S(2)}) collective-permute-start(bf16[176,384]{1,0:T(8,128)(2,1)S(1)} %get-tuple-element.87), channel_id=1, source_target_pairs={{0,4},{1,5},{2,6},{3,7},{16,20},{17,21},{18,22},{19,23}} | collective-permute-start | bytes 405512 | tf_op jit(solution)/shard_map/ppermute | solution.py:340
  24.6 0.8 %history.14 = (f32[176,384]{1,0:T(8,128)S(1)}, f32[176,384]{1,0:T(8,128)S(1)}) custom-call(bf16[224,1152]{1,0:T(8,128)(2,1)S(1)} %get-tuple-element.84.spread, f32[176,384]{1,0:T(8,128)S(1)} %get-tuple-element.83.refs_6_.near, f32[176,384]{1,0:T(8,128)S(1)} %get-tuple-element.85.far, ...), custom_call_target="tpu_custom_call", output_to_operand_aliasing={{0}: (1, {}), {1}: (2, {})} | custom-call | bytes 1024 | tf_op jit(solution)/shard_map/history/pallas_call | solution.py:355
  25.4 1.2 %frame.19 = bf16[176,384]{1,0:T(8,128)(2,1)S(1)} custom-call(bf16[2,64,384]{2,1,0:T(8,128)(2,1)S(1)} %collective-permute-done.refs_0_, bf16[2,64,384]{2,1,0:T(8,128)(2,1)S(1)} %collective-permute-done.1.refs_1_, bf16[2,64,384]{2,1,0:T(8,128)(2,1)S(1)} %get-tuple-element.73.refs_2_, bf16[2,64,384]{2,1,0:T(8,128)(2,1)S(1)} %collective-permute-done.2.refs_3_, ...), custom_call_target="tpu_custom_call" | custom-call | bytes 1024 | tf_op jit(solution)/shard_map/frame/pallas_call | solution.py:324
  26.6 1.3 %collective-permute-start.5 = (bf16[176,384]{1,0:T(8,128)(2,1)S(1)}, bf16[176,384]{1,0:T(8,128)(2,1)S(1)}, u32[]{:S(2)}, u32[]{:S(2)}) collective-permute-start(bf16[176,384]{1,0:T(8,128)(2,1)S(1)} %frame.19), channel_id=1, source_target_pairs={{0,4},{1,5},{2,6},{3,7},{16,20},{17,21},{18,22},{19,23}} | collective-permute-start | bytes 405512 | tf_op jit(solution)/shard_map/ppermute | solution.py:340
  27.9 0.7 %collective-permute-start.12 = (bf16[160,384]{1,0:T(8,128)(2,1)S(1)}, bf16[160,384]{1,0:T(8,128)(2,1)S(1)}, u32[]{:S(2)}, u32[]{:S(2)}) collective-permute-start(bf16[160,384]{1,0:T(8,128)(2,1)S(1)} %get-tuple-element.101), channel_id=1, source_target_pairs={{4,8},{5,9},{6,10},{7,11},{20,24},{21,25},{22,26},{23,27}} | collective-permute-start | bytes 368648 | tf_op jit(solution)/shard_map/ppermute | solution.py:340
  28.7 0.7 %collective-permute-start.11 = (bf16[160,384]{1,0:T(8,128)(2,1)S(1)}, bf16[160,384]{1,0:T(8,128)(2,1)S(1)}, u32[]{:S(2)}, u32[]{:S(2)}) collective-permute-start(bf16[160,384]{1,0:T(8,128)(2,1)S(1)} %get-tuple-element.100), channel_id=1, source_target_pairs={{4,8},{5,9},{6,10},{7,11},{20,24},{21,25},{22,26},{23,27}} | collective-permute-start | bytes 368648 | tf_op jit(solution)/shard_map/ppermute | solution.py:340
  29.6 0.7 %collective-permute-start.10 = (bf16[160,384]{1,0:T(8,128)(2,1)S(1)}, bf16[160,384]{1,0:T(8,128)(2,1)S(1)}, u32[]{:S(2)}, u32[]{:S(2)}) collective-permute-start(bf16[160,384]{1,0:T(8,128)(2,1)S(1)} %get-tuple-element.99), channel_id=1, source_target_pairs={{4,8},{5,9},{6,10},{7,11},{20,24},{21,25},{22,26},{23,27}} | collective-permute-start | bytes 368648 | tf_op jit(solution)/shard_map/ppermute | solution.py:340
  30.3 0.9 %collective-permute-done.5.refs_0_ = bf16[176,384]{1,0:T(8,128)(2,1)S(1)} collective-permute-done((bf16[176,384]{1,0:T(8,128)(2,1)S(1)}, bf16[176,384]{1,0:T(8,128)(2,1)S(1)}, u32[]{:S(2)}, u32[]{:S(2)}) %collective-permute-start.5) | collective-permute-done | bytes 135200 | tf_op jit(solution)/shard_map/ppermute | solution.py:340
  32.0 0.7 %collective-permute-start.16 = (bf16[144,384]{1,0:T(8,128)(2,1)S(1)}, bf16[144,384]{1,0:T(8,128)(2,1)S(1)}, u32[]{:S(2)}, u32[]{:S(2)}) collective-permute-start(bf16[144,384]{1,0:T(8,128)(2,1)S(1)} %get-tuple-element.113), channel_id=1, source_target_pairs={{8,12},{9,13},{10,14},{11,15},{24,28},{25,29},{26,30},{27,31}} | collective-permute-start | bytes 331784 | tf_op jit(solution)/shard_map/ppermute | solution.py:340
  32.7 0.7 %collective-permute-start.15 = (bf16[144,384]{1,0:T(8,128)(2,1)S(1)}, bf16[144,384]{1,0:T(8,128)(2,1)S(1)}, u32[]{:S(2)}, u32[]{:S(2)}) collective-permute-start(bf16[144,384]{1,0:T(8,128)(2,1)S(1)} %get-tuple-element.112), channel_id=1, source_target_pairs={{8,12},{9,13},{10,14},{11,15},{24,28},{25,29},{26,30},{27,31}} | collective-permute-start | bytes 331784 | tf_op jit(solution)/shard_map/ppermute | solution.py:340
  33.5 0.7 %collective-permute-start.14 = (bf16[144,384]{1,0:T(8,128)(2,1)S(1)}, bf16[144,384]{1,0:T(8,128)(2,1)S(1)}, u32[]{:S(2)}, u32[]{:S(2)}) collective-permute-start(bf16[144,384]{1,0:T(8,128)(2,1)S(1)} %get-tuple-element.111), channel_id=1, source_target_pairs={{8,12},{9,13},{10,14},{11,15},{24,28},{25,29},{26,30},{27,31}} | collective-permute-start | bytes 331784 | tf_op jit(solution)/shard_map/ppermute | solution.py:340
  34.2 0.7 %collective-permute-start.13 = (bf16[144,384]{1,0:T(8,128)(2,1)S(1)}, bf16[144,384]{1,0:T(8,128)(2,1)S(1)}, u32[]{:S(2)}, u32[]{:S(2)}) collective-permute-start(bf16[144,384]{1,0:T(8,128)(2,1)S(1)} %frame.27), channel_id=1, source_target_pairs={{8,12},{9,13},{10,14},{11,15},{24,28},{25,29},{26,30},{27,31}} | collective-permute-start | bytes 331784 | tf_op jit(solution)/shard_map/ppermute | solution.py:340
  38.1 0.7 %collective-permute-start.19 = (bf16[2,64,384]{2,1,0:T(8,128)(2,1)S(1)}, bf16[2,64,384]{2,1,0:T(8,128)(2,1)S(1)}, u32[]{:S(2)}, u32[]{:S(2)}) collective-permute-start(bf16[2,64,384]{2,1,0:T(8,128)(2,1)S(1)} %get-tuple-element.131), channel_id=1, source_target_pairs={{12,17},{14,19},{13,21},{15,23},{28,25},{30,27},{29,29},{31,31}} | collective-permute-start | bytes 294920 | tf_op jit(solution)/shard_map/ppermute | solution.py:256
  38.7 1.3 %collective-permute-start.20 = (bf16[2,64,384]{2,1,0:T(8,128)(2,1)S(1)}, bf16[2,64,384]{2,1,0:T(8,128)(2,1)S(1)}, u32[]{:S(2)}, u32[]{:S(2)}) collective-permute-start(bf16[2,64,384]{2,1,0:T(8,128)(2,1)S(1)} %get-tuple-element.132), channel_id=1, source_target_pairs={{12,16},{14,18},{13,20},{15,22},{28,24},{30,26},{29,28},{31,30}} | collective-permute-start | bytes 294920 | tf_op jit(solution)/shard_map/ppermute | solution.py:256
  40.1 14.2 %collective-permute-done.20 = bf16[2,64,384]{2,1,0:T(8,128)(2,1)S(1)} collective-permute-done((bf16[2,64,384]{2,1,0:T(8,128)(2,1)S(1)}, bf16[2,64,384]{2,1,0:T(8,128)(2,1)S(1)}, u32[]{:S(2)}, u32[]{:S(2)}) %collective-permute-start.20) | collective-permute-done | bytes 98336 | tf_op jit(solution)/shard_map/ppermute | solution.py:256
  54.3 0.7 %select_select_fusion = bf16[2,64,384]{2,1,0:T(8,128)(2,1)} fusion(bf16[2,64,384]{2,1,0:T(8,128)(2,1)S(1)} %collective-permute-done.19, bf16[2,64,384]{2,1,0:T(8,128)(2,1)S(1)} %collective-permute-done.20, bf16[2,64,384]{2,1,0:T(8,128)(2,1)S(1)} %collective-permute-done.21, bf16[2,64,384]{2,1,0:T(8,128)(2,1)S(1)} %collective-permute-done.22, ...), kind=kLoop, calls=%fused_computation | loop fusion | flops 245760 | bytes 688133 | tf_op jit(solution)/shard_map/jit(_where)/select_n | solution.py:371
  (47 shorter events, 4.2 us)
Async XLA Ops:
  1.1 11.9 %collective-permute-start.3 = (bf16[2,64,384]{2,1,0:T(8,128)(2,1)S(1)}, bf16[2,64,384]{2,1,0:T(8,128)(2,1)S(1)}, u32[]{:S(2)}, u32[]{:S(2)}) collective-permute-start(bf16[2,64,384]{2,1,0:T(8,128)(2,1)S(1)} %get-tuple-element.71), channel_id=1, source_target_pairs={{6,0},{5,2},{0,1},{2,3},{10,16},{9,18},{12,17},{14,19}} | collective-permute-start | bytes 294920 | tf_op jit(solution)/shard_map/ppermute | solution.py:217
  2.4 10.6 %collective-permute-start.4 = (bf16[2,64,384]{2,1,0:T(8,128)(2,1)S(1)}, bf16[2,64,384]{2,1,0:T(8,128)(2,1)S(1)}, u32[]{:S(2)}, u32[]{:S(2)}) collective-permute-start(bf16[2,64,384]{2,1,0:T(8,128)(2,1)S(1)} %get-tuple-element.72), channel_id=1, source_target_pairs={{1,0},{3,2},{6,1},{5,3},{9,16},{11,18},{14,17},{13,19}} | collective-permute-start | bytes 294920 | tf_op jit(solution)/shard_map/ppermute | solution.py:217
  3.7 10.9 %collective-permute-start.2 = (bf16[2,64,384]{2,1,0:T(8,128)(2,1)S(1)}, bf16[2,64,384]{2,1,0:T(8,128)(2,1)S(1)}, u32[]{:S(2)}, u32[]{:S(2)}) collective-permute-start(bf16[2,64,384]{2,1,0:T(8,128)(2,1)S(1)} %get-tuple-element.74), channel_id=1, source_target_pairs={{0,16},{2,18},{1,17},{3,19},{20,0},{22,2},{21,1},{23,3}} | collective-permute-start | bytes 294920 | tf_op jit(solution)/shard_map/ppermute | solution.py:217
  5.0 17.1 %collective-permute-start = (bf16[2,64,384]{2,1,0:T(8,128)(2,1)S(1)}, bf16[2,64,384]{2,1,0:T(8,128)(2,1)S(1)}, u32[]{:S(2)}, u32[]{:S(2)}) collective-permute-start(bf16[2,64,384]{2,1,0:T(8,128)(2,1)S(1)} %get-tuple-element.71), channel_id=1, source_target_pairs={{26,0},{25,2},{28,1},{30,3},{22,16},{21,18},{16,17},{18,19}} | collective-permute-start | bytes 294920 | tf_op jit(solution)/shard_map/ppermute | solution.py:217
  6.9 15.2 %collective-permute-start.1 = (bf16[2,64,384]{2,1,0:T(8,128)(2,1)S(1)}, bf16[2,64,384]{2,1,0:T(8,128)(2,1)S(1)}, u32[]{:S(2)}, u32[]{:S(2)}) collective-permute-start(bf16[2,64,384]{2,1,0:T(8,128)(2,1)S(1)} %get-tuple-element.72), channel_id=1, source_target_pairs={{25,0},{27,2},{30,1},{29,3},{17,16},{19,18},{22,17},{21,19}} | collective-permute-start | bytes 294920 | tf_op jit(solution)/shard_map/ppermute | solution.py:217
  15.8 12.1 %collective-permute-start.8 = (bf16[176,384]{1,0:T(8,128)(2,1)S(1)}, bf16[176,384]{1,0:T(8,128)(2,1)S(1)}, u32[]{:S(2)}, u32[]{:S(2)}) collective-permute-start(bf16[176,384]{1,0:T(8,128)(2,1)S(1)} %get-tuple-element.89), channel_id=1, source_target_pairs={{0,4},{1,5},{2,6},{3,7},{16,20},{17,21},{18,22},{19,23}} | collective-permute-start | bytes 405512 | tf_op jit(solution)/shard_map/ppermute | solution.py:340
  19.5 9.1 %collective-permute-start.7 = (bf16[176,384]{1,0:T(8,128)(2,1)S(1)}, bf16[176,384]{1,0:T(8,128)(2,1)S(1)}, u32[]{:S(2)}, u32[]{:S(2)}) collective-permute-start(bf16[176,384]{1,0:T(8,128)(2,1)S(1)} %get-tuple-element.88), channel_id=1, source_target_pairs={{0,4},{1,5},{2,6},{3,7},{16,20},{17,21},{18,22},{19,23}} | collective-permute-start | bytes 405512 | tf_op jit(solution)/shard_map/ppermute | solution.py:340
  23.3 6.1 %collective-permute-start.6 = (bf16[176,384]{1,0:T(8,128)(2,1)S(1)}, bf16[176,384]{1,0:T(8,128)(2,1)S(1)}, u32[]{:S(2)}, u32[]{:S(2)}) collective-permute-start(bf16[176,384]{1,0:T(8,128)(2,1)S(1)} %get-tuple-element.87), channel_id=1, source_target_pairs={{0,4},{1,5},{2,6},{3,7},{16,20},{17,21},{18,22},{19,23}} | collective-permute-start | bytes 405512 | tf_op jit(solution)/shard_map/ppermute | solution.py:340
  26.6 4.7 %collective-permute-start.5 = (bf16[176,384]{1,0:T(8,128)(2,1)S(1)}, bf16[176,384]{1,0:T(8,128)(2,1)S(1)}, u32[]{:S(2)}, u32[]{:S(2)}) collective-permute-start(bf16[176,384]{1,0:T(8,128)(2,1)S(1)} %frame.19), channel_id=1, source_target_pairs={{0,4},{1,5},{2,6},{3,7},{16,20},{17,21},{18,22},{19,23}} | collective-permute-start | bytes 405512 | tf_op jit(solution)/shard_map/ppermute | solution.py:340
  27.9 4.0 %collective-permute-start.12 = (bf16[160,384]{1,0:T(8,128)(2,1)S(1)}, bf16[160,384]{1,0:T(8,128)(2,1)S(1)}, u32[]{:S(2)}, u32[]{:S(2)}) collective-permute-start(bf16[160,384]{1,0:T(8,128)(2,1)S(1)} %get-tuple-element.101), channel_id=1, source_target_pairs={{4,8},{5,9},{6,10},{7,11},{20,24},{21,25},{22,26},{23,27}} | collective-permute-start | bytes 368648 | tf_op jit(solution)/shard_map/ppermute | solution.py:340
  28.7 4.0 %collective-permute-start.11 = (bf16[160,384]{1,0:T(8,128)(2,1)S(1)}, bf16[160,384]{1,0:T(8,128)(2,1)S(1)}, u32[]{:S(2)}, u32[]{:S(2)}) collective-permute-start(bf16[160,384]{1,0:T(8,128)(2,1)S(1)} %get-tuple-element.100), channel_id=1, source_target_pairs={{4,8},{5,9},{6,10},{7,11},{20,24},{21,25},{22,26},{23,27}} | collective-permute-start | bytes 368648 | tf_op jit(solution)/shard_map/ppermute | solution.py:340
  29.6 3.8 %collective-permute-start.10 = (bf16[160,384]{1,0:T(8,128)(2,1)S(1)}, bf16[160,384]{1,0:T(8,128)(2,1)S(1)}, u32[]{:S(2)}, u32[]{:S(2)}) collective-permute-start(bf16[160,384]{1,0:T(8,128)(2,1)S(1)} %get-tuple-element.99), channel_id=1, source_target_pairs={{4,8},{5,9},{6,10},{7,11},{20,24},{21,25},{22,26},{23,27}} | collective-permute-start | bytes 368648 | tf_op jit(solution)/shard_map/ppermute | solution.py:340
  31.3 2.9 %collective-permute-start.9 = (bf16[160,384]{1,0:T(8,128)(2,1)S(1)}, bf16[160,384]{1,0:T(8,128)(2,1)S(1)}, u32[]{:S(2)}, u32[]{:S(2)}) collective-permute-start(bf16[160,384]{1,0:T(8,128)(2,1)S(1)} %frame.23), channel_id=1, source_target_pairs={{4,8},{5,9},{6,10},{7,11},{20,24},{21,25},{22,26},{23,27}} | collective-permute-start | bytes 368648 | tf_op jit(solution)/shard_map/ppermute | solution.py:340
  32.0 2.9 %collective-permute-start.16 = (bf16[144,384]{1,0:T(8,128)(2,1)S(1)}, bf16[144,384]{1,0:T(8,128)(2,1)S(1)}, u32[]{:S(2)}, u32[]{:S(2)}) collective-permute-start(bf16[144,384]{1,0:T(8,128)(2,1)S(1)} %get-tuple-element.113), channel_id=1, source_target_pairs={{8,12},{9,13},{10,14},{11,15},{24,28},{25,29},{26,30},{27,31}} | collective-permute-start | bytes 331784 | tf_op jit(solution)/shard_map/ppermute | solution.py:340
  32.7 2.2 %collective-permute-start.15 = (bf16[144,384]{1,0:T(8,128)(2,1)S(1)}, bf16[144,384]{1,0:T(8,128)(2,1)S(1)}, u32[]{:S(2)}, u32[]{:S(2)}) collective-permute-start(bf16[144,384]{1,0:T(8,128)(2,1)S(1)} %get-tuple-element.112), channel_id=1, source_target_pairs={{8,12},{9,13},{10,14},{11,15},{24,28},{25,29},{26,30},{27,31}} | collective-permute-start | bytes 331784 | tf_op jit(solution)/shard_map/ppermute | solution.py:340
  33.5 3.1 %collective-permute-start.14 = (bf16[144,384]{1,0:T(8,128)(2,1)S(1)}, bf16[144,384]{1,0:T(8,128)(2,1)S(1)}, u32[]{:S(2)}, u32[]{:S(2)}) collective-permute-start(bf16[144,384]{1,0:T(8,128)(2,1)S(1)} %get-tuple-element.111), channel_id=1, source_target_pairs={{8,12},{9,13},{10,14},{11,15},{24,28},{25,29},{26,30},{27,31}} | collective-permute-start | bytes 331784 | tf_op jit(solution)/shard_map/ppermute | solution.py:340
  34.2 3.8 %collective-permute-start.13 = (bf16[144,384]{1,0:T(8,128)(2,1)S(1)}, bf16[144,384]{1,0:T(8,128)(2,1)S(1)}, u32[]{:S(2)}, u32[]{:S(2)}) collective-permute-start(bf16[144,384]{1,0:T(8,128)(2,1)S(1)} %frame.27), channel_id=1, source_target_pairs={{8,12},{9,13},{10,14},{11,15},{24,28},{25,29},{26,30},{27,31}} | collective-permute-start | bytes 331784 | tf_op jit(solution)/shard_map/ppermute | solution.py:340
  35.0 3.0 %collective-permute-start.17 = (bf16[2,64,384]{2,1,0:T(8,128)(2,1)S(1)}, bf16[2,64,384]{2,1,0:T(8,128)(2,1)S(1)}, u32[]{:S(2)}, u32[]{:S(2)}) collective-permute-start(bf16[2,64,384]{2,1,0:T(8,128)(2,1)S(1)} %get-tuple-element.129), channel_id=1, source_target_pairs={{12,0},{14,2},{13,4},{15,6}} | collective-permute-start | bytes 294920 | tf_op jit(solution)/shard_map/ppermute | solution.py:256
  35.7 2.4 %collective-permute-start.18 = (bf16[2,64,384]{2,1,0:T(8,128)(2,1)S(1)}, bf16[2,64,384]{2,1,0:T(8,128)(2,1)S(1)}, u32[]{:S(2)}, u32[]{:S(2)}) collective-permute-start(bf16[2,64,384]{2,1,0:T(8,128)(2,1)S(1)} %get-tuple-element.130), channel_id=1, source_target_pairs={{12,1},{14,3},{13,5},{15,7}} | collective-permute-start | bytes 294920 | tf_op jit(solution)/shard_map/ppermute | solution.py:256
  36.6 3.5 %collective-permute-start.21 = (bf16[2,64,384]{2,1,0:T(8,128)(2,1)S(1)}, bf16[2,64,384]{2,1,0:T(8,128)(2,1)S(1)}, u32[]{:S(2)}, u32[]{:S(2)}) collective-permute-start(bf16[2,64,384]{2,1,0:T(8,128)(2,1)S(1)} %get-tuple-element.133), channel_id=1, source_target_pairs={{28,9},{30,11},{29,13},{31,15}} | collective-permute-start | bytes 294920 | tf_op jit(solution)/shard_map/ppermute | solution.py:256
  37.3 2.8 %collective-permute-start.22 = (bf16[2,64,384]{2,1,0:T(8,128)(2,1)S(1)}, bf16[2,64,384]{2,1,0:T(8,128)(2,1)S(1)}, u32[]{:S(2)}, u32[]{:S(2)}) collective-permute-start(bf16[2,64,384]{2,1,0:T(8,128)(2,1)S(1)} %get-tuple-element.134), channel_id=1, source_target_pairs={{28,8},{30,10},{29,12},{31,14}} | collective-permute-start | bytes 294920 | tf_op jit(solution)/shard_map/ppermute | solution.py:256
  38.1 2.0 %collective-permute-start.19 = (bf16[2,64,384]{2,1,0:T(8,128)(2,1)S(1)}, bf16[2,64,384]{2,1,0:T(8,128)(2,1)S(1)}, u32[]{:S(2)}, u32[]{:S(2)}) collective-permute-start(bf16[2,64,384]{2,1,0:T(8,128)(2,1)S(1)} %get-tuple-element.131), channel_id=1, source_target_pairs={{12,17},{14,19},{13,21},{15,23},{28,25},{30,27},{29,29},{31,31}} | collective-permute-start | bytes 294920 | tf_op jit(solution)/shard_map/ppermute | solution.py:256
  38.7 15.5 %collective-permute-start.20 = (bf16[2,64,384]{2,1,0:T(8,128)(2,1)S(1)}, bf16[2,64,384]{2,1,0:T(8,128)(2,1)S(1)}, u32[]{:S(2)}, u32[]{:S(2)}) collective-permute-start(bf16[2,64,384]{2,1,0:T(8,128)(2,1)S(1)} %get-tuple-element.132), channel_id=1, source_target_pairs={{12,16},{14,18},{13,20},{15,22},{28,24},{30,26},{29,28},{31,30}} | collective-permute-start | bytes 294920 | tf_op jit(solution)/shard_map/ppermute | solution.py:256
